TPU v7x, 32 devices: a whole 2x2x4 slice. The times are simulated.
32 devices in a mesh: dp: 8 (over y, x, core), tensor: 4 (over z).
Axes of the slice: x: 2, y: 2, z: 4, core: 2. Of those that a mesh axis runs over, the one named last changes fastest.
Arguments:
- inputs: bfloat16 [8, 2048, 768], P('dp', 'tensor'), may hold values from -6 to 6
- segment_ids: int32 [8, 2048], P('dp'), may hold values from 0 to 7, never falling along the last dimension, each value on 1 to 1024 neighbouring positions
- valid_mask: int32 [8, 2048], P('dp', 'tensor'), may hold values from 0 to 1
- teacher: bfloat16 [8, 2048, 768], P('dp', 'tensor'), may hold values from -5 to 5
- cotangent: bfloat16 [8, 2048, 768], P('dp', 'tensor'), may hold values from -6 to 6
- w_query: bfloat16 [768, 768], P('dp', 'tensor'), may hold values from -0.3125 to 0.3125
- w_key: bfloat16 [768, 768], P('dp', 'tensor'), may hold values from -0.21875 to 0.21875
- w_value: bfloat16 [768, 768], P('dp', 'tensor'), may hold values from -0.21875 to 0.21875
- w_output: bfloat16 [768, 768], P('tensor', 'dp'), may hold values from -0.875 to 0.875
- w_inner: bfloat16 [768, 3072], P('dp', 'tensor'), may hold values from -0.21875 to 0.21875
- w_outer: bfloat16 [3072, 768], P('tensor', 'dp'), may hold values from -0.15625 to 0.15625
- query_bias: bfloat16 [768], replicated, may hold values from -3 to 3
- value_bias: bfloat16 [768], replicated, may hold values from -3 to 3
- output_bias: bfloat16 [768], replicated, may hold values from -3 to 3
- inner_bias: bfloat16 [3072], replicated, may hold values from -3 to 3
- outer_bias: bfloat16 [768], replicated, may hold values from -3 to 3
- gain_attn: bfloat16 [768], replicated, may hold values from 0.5 to 1.5
- shift_attn: bfloat16 [768], replicated, may hold values from -3 to 3
- gain_ffn: bfloat16 [768], replicated, may hold values from 0.5 to 1.5
- shift_ffn: bfloat16 [768], replicated, may hold values from -3 to 3
Outputs:
- layer_out: bfloat16 [8, 2048, 768], P('dp', 'tensor')
- mse_loss: float32 [], replicated
- input_grad: float32 [8, 2048, 768], P('dp', 'tensor')
- query_weight_grad: float32 [768, 768], P('dp', 'tensor')
- key_weight_grad: float32 [768, 768], P('dp', 'tensor')
- value_weight_grad: float32 [768, 768], P('dp', 'tensor')
- output_weight_grad: float32 [768, 768], P('tensor', 'dp')
- inner_weight_grad: float32 [768, 3072], P('dp', 'tensor')
- outer_weight_grad: float32 [3072, 768], P('tensor', 'dp')
- query_bias_grad: float32 [768], replicated
- value_bias_grad: float32 [768], replicated
- output_bias_grad: float32 [768], replicated
- inner_bias_grad: float32 [3072], replicated
- outer_bias_grad: float32 [768], replicated
- gain_attn_grad: float32 [768], replicated
- shift_attn_grad: float32 [768], replicated
- gain_ffn_grad: float32 [768], replicated
- shift_ffn_grad: float32 [768], replicated
All inputs are finite; a program needn't handle non-finite values.
Results may differ from a plain program's by a relative error of at most 0.017.
Values may be sent and summed in bfloat16 or wider, within the bound.
No kernel may reach another device: no remote copies, remote signals or barrier semaphores. Data moves between devices by JAX's collectives and lax.ppermute only.
A program may use at most 128 MiB of HBM per device.

v0:
```python
import jax
import jax.numpy as jnp
from jax import lax
from jax.sharding import PartitionSpec as P

DH = 64
QBLOCK = 512


EPSILON = 1e-12
ROOT_HALF = 0.7071067811865476
INV_ROOT_TAU = 0.3989422804014327


def norm_forward(summed, gain_vec, shift_vec):
    average = jnp.mean(summed, axis=-1, keepdims=True)
    centered = summed - average
    variance = jnp.mean(centered * centered, axis=-1, keepdims=True)
    inverse = lax.rsqrt(variance + EPSILON)
    normed = centered * inverse
    return (normed * gain_vec + shift_vec, normed, inverse)


def norm_backward(upstream, normed, inverse, gain_vec):
    scaled = upstream * gain_vec
    first_mean = jnp.mean(scaled, axis=-1, keepdims=True)
    second_mean = jnp.mean(scaled * normed, axis=-1, keepdims=True)
    back_grad = inverse * (scaled - first_mean - normed * second_mean)
    return (back_grad, jnp.sum(upstream * normed, axis=0), jnp.sum(upstream, axis=0))


def gelu_value(hidden):
    return 0.5 * hidden * (1.0 + lax.erf(hidden * ROOT_HALF))


def gelu_slope(hidden):
    return 0.5 * (1.0 + lax.erf(hidden * ROOT_HALF)) + hidden * INV_ROOT_TAU * jnp.exp(
        -0.5 * hidden * hidden
    )


def block_scores(query_block, key_seq, segment_block, segment_row, score_scale):
    scores = (
        jnp.einsum("qhd,khd->hqk", query_block, key_seq, preferred_element_type=jnp.float32)
        * score_scale
    )
    allowed = segment_block[None, :, None] == segment_row[None, None, :]
    return jnp.where(allowed, scores, -1e30)


def attention_forward(queries, keys_all, values_all, segment_ids, score_scale):

    def per_sequence(sequence_item):
        query_seq, key_seq, value_seq, segment_row = sequence_item

        def per_block(block_index):
            row_start = block_index * QBLOCK
            query_block = lax.dynamic_slice_in_dim(query_seq, row_start, QBLOCK, 0)
            segment_block = lax.dynamic_slice_in_dim(segment_row, row_start, QBLOCK, 0)
            masked = block_scores(query_block, key_seq, segment_block, segment_row, score_scale)
            highest = jnp.max(masked, axis=-1, keepdims=True)
            raised = jnp.exp(masked - highest)
            summed = jnp.sum(raised, axis=-1, keepdims=True)
            rounded = (raised / summed).astype(jnp.bfloat16)
            context = jnp.einsum(
                "hqk,khd->qhd", rounded, value_seq, preferred_element_type=jnp.float32
            )
            return (context.astype(jnp.bfloat16), (highest + jnp.log(summed))[:, :, 0])

        blocks = query_seq.shape[0] // QBLOCK
        return lax.map(per_block, jnp.arange(blocks, dtype=jnp.int32))

    return lax.map(per_sequence, (queries, keys_all, values_all, segment_ids))


def attention_backward(
    queries, keys_all, values_all, segment_ids, log_sums, context_grad, score_scale
):

    def per_sequence(sequence_item):
        query_seq, key_seq, value_seq, segment_row, lse_seq, grad_seq = sequence_item

        def per_block(running, block_index):
            key_acc, value_acc = running
            row_start = block_index * QBLOCK
            query_block = lax.dynamic_slice_in_dim(query_seq, row_start, QBLOCK, 0)
            grad_block = lax.dynamic_slice_in_dim(grad_seq, row_start, QBLOCK, 0)
            segment_block = lax.dynamic_slice_in_dim(segment_row, row_start, QBLOCK, 0)
            lse_block = lax.dynamic_index_in_dim(lse_seq, block_index, 0, keepdims=False)
            masked = block_scores(query_block, key_seq, segment_block, segment_row, score_scale)
            probs_block = jnp.exp(masked - lse_block[:, :, None])
            rounded = probs_block.astype(jnp.bfloat16)
            value_acc = value_acc + jnp.einsum(
                "hqk,qhd->khd", rounded, grad_block, preferred_element_type=jnp.float32
            )
            probs_grad = jnp.einsum(
                "qhd,khd->hqk", grad_block, value_seq, preferred_element_type=jnp.float32
            )
            row_dot = jnp.sum(probs_grad * probs_block, axis=-1, keepdims=True)
            score_grad = (probs_block * (probs_grad - row_dot)).astype(jnp.bfloat16)
            query_grad = (
                jnp.einsum("hqk,khd->qhd", score_grad, key_seq, preferred_element_type=jnp.float32)
                * score_scale
            )
            key_acc = (
                key_acc
                + jnp.einsum(
                    "hqk,qhd->khd", score_grad, query_block, preferred_element_type=jnp.float32
                )
                * score_scale
            )
            return ((key_acc, value_acc), query_grad.astype(jnp.bfloat16))

        blocks = query_seq.shape[0] // QBLOCK
        zeroed = jnp.zeros(key_seq.shape, jnp.float32)
        (key_acc, value_acc), query_grads = lax.scan(
            per_block, (zeroed, zeroed), jnp.arange(blocks, dtype=jnp.int32)
        )
        return (query_grads, key_acc.astype(jnp.bfloat16), value_acc.astype(jnp.bfloat16))

    return lax.map(
        per_sequence, (queries, keys_all, values_all, segment_ids, log_sums, context_grad)
    )


def place_slice(local_grad, full_size, offset):
    return lax.dynamic_update_slice_in_dim(
        jnp.zeros((full_size,), jnp.float32), local_grad, offset, 0
    )


def local(
    inputs,
    segment_ids,
    valid_mask,
    teacher,
    cotangent,
    w_query,
    w_key,
    w_value,
    w_output,
    w_inner,
    w_outer,
    query_bias,
    value_bias,
    output_bias,
    inner_bias,
    outer_bias,
    gain_attn,
    shift_attn,
    gain_ffn,
    shift_ffn,
):
    groups, part_len, model_width = inputs.shape
    tensor_rank = lax.axis_index("tensor")
    seq_len = part_len * lax.axis_size("tensor")
    all_rows = groups * seq_len
    local_rows = groups * part_len
    total_tokens = all_rows * lax.axis_size("dp")
    score_scale = DH ** (-0.5)
    matrices = (
        lax.all_gather(w_query, "dp", axis=0, tiled=True),
        lax.all_gather(w_key, "dp", axis=0, tiled=True),
        lax.all_gather(w_value, "dp", axis=0, tiled=True),
        lax.all_gather(w_output, "dp", axis=1, tiled=True),
        lax.all_gather(w_inner, "dp", axis=0, tiled=True),
        lax.all_gather(w_outer, "dp", axis=1, tiled=True),
    )
    query_full, key_full, value_full, output_full, inner_full, outer_full = matrices
    head_cols = query_full.shape[1]
    hidden_cols = inner_full.shape[1]
    heads_here = head_cols // DH
    head_shape = (groups, seq_len, heads_here, DH)
    joined = jnp.concatenate((query_full, key_full, value_full), axis=1)
    query_shift = lax.dynamic_slice_in_dim(query_bias, tensor_rank * head_cols, head_cols).astype(
        jnp.float32
    )
    value_shift = lax.dynamic_slice_in_dim(value_bias, tensor_rank * head_cols, head_cols).astype(
        jnp.float32
    )
    inner_shift = lax.dynamic_slice_in_dim(
        inner_bias, tensor_rank * hidden_cols, hidden_cols
    ).astype(jnp.float32)
    valid_rows = valid_mask.astype(jnp.float32).reshape(local_rows, 1)
    counted = lax.psum(jnp.sum(valid_rows), ("dp", "tensor"))
    gathered = lax.all_gather(inputs, "tensor", axis=1, tiled=True)
    flat_in = gathered.reshape(all_rows, model_width)
    projected = jnp.dot(flat_in, joined, preferred_element_type=jnp.float32)
    queries = (projected[:, :head_cols] + query_shift).astype(jnp.bfloat16).reshape(head_shape)
    keys_all = projected[:, head_cols : 2 * head_cols].astype(jnp.bfloat16).reshape(head_shape)
    values_all = (
        (projected[:, 2 * head_cols :] + value_shift).astype(jnp.bfloat16).reshape(head_shape)
    )
    context, log_sums = attention_forward(queries, keys_all, values_all, segment_ids, score_scale)
    context_rows = context.reshape(all_rows, head_cols)
    attn_partial = jnp.dot(context_rows, output_full, preferred_element_type=jnp.float32).reshape(
        groups, seq_len, model_width
    )
    attention = lax.psum_scatter(attn_partial, "tensor", scatter_dimension=1, tiled=True).reshape(
        local_rows, model_width
    )
    first_sum = (
        inputs.reshape(local_rows, model_width).astype(jnp.float32)
        + attention
        + output_bias.astype(jnp.float32)
    )
    gain_one = gain_attn.astype(jnp.float32)
    first_exact, normed_one, inverse_one = norm_forward(
        first_sum, gain_one, shift_attn.astype(jnp.float32)
    )
    first = first_exact.astype(jnp.bfloat16)
    ffn_in = lax.all_gather(
        first.reshape(groups, part_len, model_width), "tensor", axis=1, tiled=True
    ).reshape(all_rows, model_width)
    hidden = jnp.dot(ffn_in, inner_full, preferred_element_type=jnp.float32) + inner_shift
    activated = gelu_value(hidden).astype(jnp.bfloat16)
    branch_partial = jnp.dot(activated, outer_full, preferred_element_type=jnp.float32).reshape(
        groups, seq_len, model_width
    )
    branch = lax.psum_scatter(branch_partial, "tensor", scatter_dimension=1, tiled=True).reshape(
        local_rows, model_width
    )
    second_sum = first.astype(jnp.float32) + branch + outer_bias.astype(jnp.float32)
    gain_two = gain_ffn.astype(jnp.float32)
    layer_rows, normed_two, inverse_two = norm_forward(
        second_sum, gain_two, shift_ffn.astype(jnp.float32)
    )
    misfit = layer_rows - teacher.reshape(local_rows, model_width).astype(jnp.float32)
    squared = jnp.sum(valid_rows * misfit * misfit)
    out_grad = cotangent.reshape(local_rows, model_width).astype(
        jnp.float32
    ) + valid_rows * misfit * (total_tokens / counted)
    query_back, key_back, value_back, output_back, inner_back, outer_back = matrices
    joined_back = jnp.concatenate((query_back, key_back, value_back), axis=1)
    second_grad, gain_ffn_grad, shift_ffn_grad = norm_backward(
        out_grad, normed_two, inverse_two, gain_two
    )
    branch_grad = second_grad.astype(jnp.bfloat16)
    outer_bias_grad = jnp.sum(branch_grad.astype(jnp.float32), axis=0)
    branch_grad_all = lax.all_gather(
        branch_grad.reshape(groups, part_len, model_width), "tensor", axis=1, tiled=True
    ).reshape(all_rows, model_width)
    outer_weight_grad = jnp.einsum(
        "rh,rd->hd", activated, branch_grad_all, preferred_element_type=jnp.float32
    )
    active_grad = jnp.einsum(
        "rd,hd->rh", branch_grad_all, outer_back, preferred_element_type=jnp.float32
    )
    hidden_grad = (active_grad * gelu_slope(hidden)).astype(jnp.bfloat16)
    inner_bias_local = jnp.sum(hidden_grad.astype(jnp.float32), axis=0)
    inner_weight_grad = jnp.einsum(
        "rd,rh->dh", ffn_in, hidden_grad, preferred_element_type=jnp.float32
    )
    ffn_back_partial = jnp.einsum(
        "rh,dh->rd", hidden_grad, inner_back, preferred_element_type=jnp.float32
    ).reshape(groups, seq_len, model_width)
    ffn_back = lax.psum_scatter(
        ffn_back_partial, "tensor", scatter_dimension=1, tiled=True
    ).reshape(local_rows, model_width)
    first_grad, gain_attn_grad, shift_attn_grad = norm_backward(
        second_grad + ffn_back, normed_one, inverse_one, gain_one
    )
    attn_grad = first_grad.astype(jnp.bfloat16)
    output_bias_grad = jnp.sum(attn_grad.astype(jnp.float32), axis=0)
    attn_grad_all = lax.all_gather(
        attn_grad.reshape(groups, part_len, model_width), "tensor", axis=1, tiled=True
    ).reshape(all_rows, model_width)
    output_weight_grad = jnp.einsum(
        "rc,rd->cd", context_rows, attn_grad_all, preferred_element_type=jnp.float32
    )
    context_grad = jnp.einsum(
        "rd,cd->rc", attn_grad_all, output_back, preferred_element_type=jnp.float32
    ).astype(jnp.bfloat16)
    query_grad, key_grad, value_grad = attention_backward(
        queries,
        keys_all,
        values_all,
        segment_ids,
        log_sums,
        context_grad.reshape(head_shape),
        score_scale,
    )
    joined_grad = jnp.concatenate(
        (
            query_grad.reshape(all_rows, head_cols),
            key_grad.reshape(all_rows, head_cols),
            value_grad.reshape(all_rows, head_cols),
        ),
        axis=1,
    )
    projection_grad = jnp.einsum(
        "rd,rc->dc", flat_in, joined_grad, preferred_element_type=jnp.float32
    )
    attn_back_partial = jnp.einsum(
        "rc,dc->rd", joined_grad, joined_back, preferred_element_type=jnp.float32
    ).reshape(groups, seq_len, model_width)
    attn_back = (
        lax.psum_scatter(
            attn_back_partial.astype(jnp.bfloat16), "tensor", scatter_dimension=1, tiled=True
        )
        .astype(jnp.float32)
        .reshape(local_rows, model_width)
    )
    input_grad = first_grad + attn_back
    column_sums = jnp.sum(joined_grad.astype(jnp.float32), axis=0)
    query_bias_pad = place_slice(column_sums[:head_cols], model_width, tensor_rank * head_cols)
    value_bias_pad = place_slice(column_sums[2 * head_cols :], model_width, tensor_rank * head_cols)
    inner_bias_pad = place_slice(inner_bias_local, inner_bias.shape[0], tensor_rank * hidden_cols)
    scattered = (
        lax.psum_scatter(projection_grad[:, :head_cols], "dp", scatter_dimension=0, tiled=True),
        lax.psum_scatter(
            projection_grad[:, head_cols : 2 * head_cols], "dp", scatter_dimension=0, tiled=True
        ),
        lax.psum_scatter(
            projection_grad[:, 2 * head_cols :], "dp", scatter_dimension=0, tiled=True
        ),
        lax.psum_scatter(output_weight_grad, "dp", scatter_dimension=1, tiled=True),
        lax.psum_scatter(inner_weight_grad, "dp", scatter_dimension=0, tiled=True),
        lax.psum_scatter(outer_weight_grad, "dp", scatter_dimension=1, tiled=True),
    )
    totals = lax.psum(
        (
            squared,
            query_bias_pad,
            value_bias_pad,
            output_bias_grad,
            inner_bias_pad,
            outer_bias_grad,
            gain_attn_grad,
            shift_attn_grad,
            gain_ffn_grad,
            shift_ffn_grad,
        ),
        ("dp", "tensor"),
    )
    mse_loss = totals[0] / (counted * model_width)
    layer_out = layer_rows.astype(jnp.bfloat16).reshape(groups, part_len, model_width)
    return (
        layer_out,
        mse_loss,
        input_grad.reshape(groups, part_len, model_width),
        scattered[0],
        scattered[1],
        scattered[2],
        scattered[3],
        scattered[4],
        scattered[5],
        totals[1],
        totals[2],
        totals[3],
        totals[4],
        totals[5],
        totals[6],
        totals[7],
        totals[8],
        totals[9],
    )


def solution(mesh):
    in_specs = (
        P("dp", "tensor", None),
        P("dp", None),
        P("dp", "tensor"),
        P("dp", "tensor", None),
        P("dp", "tensor", None),
        P("dp", "tensor"),
        P("dp", "tensor"),
        P("dp", "tensor"),
        P("tensor", "dp"),
        P("dp", "tensor"),
        P("tensor", "dp"),
        P(),
        P(),
        P(),
        P(),
        P(),
        P(),
        P(),
        P(),
        P(),
    )
    out_specs = (
        P("dp", "tensor", None),
        P(),
        P("dp", "tensor", None),
        P("dp", "tensor"),
        P("dp", "tensor"),
        P("dp", "tensor"),
        P("tensor", "dp"),
        P("dp", "tensor"),
        P("tensor", "dp"),
        P(),
        P(),
        P(),
        P(),
        P(),
        P(),
        P(),
        P(),
        P(),
    )
    return jax.shard_map(local, mesh=mesh, in_specs=in_specs, out_specs=out_specs, check_vma=False)
```

profile of v0, /device:TPU:0, one launch (start us, length us, event | category | flops | bytes accessed | tf_op | source)
XLA Modules:
  0.0 1200.4 jit_solution(10365290391935206340)
XLA Ops:
  9.7 11.0 all_gather.34
  20.8 9.5 all_gather.30
  30.3 8.9 all_gather.31
  39.2 9.5 all_gather.32
  49.5 27.2 %all-gather.7.cloned.1.call-done = bf16[1,2048,768]{2,1,0:T(8,128)(2,1)} async-done(((bf16[1,512,768]{2,1,0:T(8,128)(2,1)}), bf16[1,2048,768]{2,1,0:T(8,128)(2,1)}) %all-gather.7.cloned.1.call-update) | async-done | bytes 3145744 | tf_op jit(solution)/shard_map/all_gather | solution.py:186
  81.9 88.0 %while.47 = (s32[]{:T(128)}, bf16[4,512,3,64]{1,3,2,0:T(8,128)(2,1)S(1)}, f32[4,3,512]{2,1,0:T(4,128)}, s32[4]{0:T(128)S(1)}, s32[2048]{0:T(1024)S(1)}, /*index=...) while((s32[]{:T(128)}, ...), condition=%wide.region_3.4_spmd, body=%wide.region_0.3_spmd.sunk | while | flops 844200448 | bytes 43978948 | solution.py:71
  83.9 5.9 fusion.132
  89.8 6.8 fusion.133
  96.6 6.7 fusion.134
  105.9 6.0 fusion.132
  111.9 6.8 fusion.133
  118.6 6.7 fusion.134
  127.9 5.9 fusion.132
  133.9 6.8 fusion.133
  140.6 6.7 fusion.134
  149.9 6.0 fusion.132
  155.9 6.8 fusion.133
  162.6 6.7 fusion.134
  177.0 108.3 %reduce-scatter.19.cloned.1.call-done = f32[1,512,768]{2,1,0:T(8,128)} async-done(((f32[1,2048,768]{2,1,0:T(8,128)}), f32[1,512,768]{2,1,0:T(8,128)}) %reduce-scatter.19.cloned.1.call-update) | async-done | bytes 1572880 | tf_op jit(solution)/shard_map/reduce_scatter | solution.py:199
  292.1 61.6 %all-gather.9.cloned.1.call-done = bf16[1,2048,768]{2,1,0:T(8,128)(2,1)} async-done(((bf16[1,512,768]{2,1,0:T(8,128)(2,1)}), bf16[1,2048,768]{2,1,0:T(8,128)(2,1)}) %all-gather.9.cloned.1.call-update) | async-done | bytes 3145744 | tf_op jit(solution)/shard_map/all_gather | solution.py:212
  353.6 7.0 multiply_convert_fusion.1
  360.7 17.3 %all-gather.13.cloned.1.call-done = bf16[768,768]{0,1:T(8,128)(2,1)} async-done(((bf16[768,96]{0,1:T(8,128)(2,1)}), bf16[768,768]{0,1:T(8,128)(2,1)}) %all-gather.13.cloned.1.call-update) | async-done | bytes 1179664 | tf_op jit(solution)/shard_map/all_gather | solution.py:167
  378.0 7.5 convolution_bitcast_fusion.2
  386.8 46.4 %psum.78 = f32[]{:T(128)} all-reduce(f32[]{:T(128)} %convert_reduce_fusion.4), channel_id=1, replica_groups=mesh['dp'=8,'tensor'=4] {'dp','tensor'}, use_global_device_ids=true, to_apply=%region_13.14 | all-reduce | flops 1 | bytes 8 | tf_op jit(solution)/shard_map/psum | solution.py:185
  439.0 58.3 %reduce-scatter.21.cloned.1.call-done = f32[1,512,768]{2,1,0:T(8,128)} async-done(((f32[1,2048,768]{2,1,0:T(8,128)}), f32[1,512,768]{2,1,0:T(8,128)}) %reduce-scatter.21.cloned.1.call-update) | async-done | bytes 1572880 | tf_op jit(solution)/shard_map/reduce_scatter | solution.py:220
  507.0 64.1 %all-gather.15.cloned.1.call-done = bf16[1,2048,768]{2,1,0:T(8,128)(2,1)} async-done(((bf16[1,512,768]{2,1,0:T(8,128)(2,1)}), bf16[1,2048,768]{2,1,0:T(8,128)(2,1)}) %all-gather.15.cloned.1.call-update) | async-done | bytes 3145744 | tf_op jit(solution)/shard_map/all_gather | solution.py:240
  571.1 7.6 convert_reduce_fusion
  589.2 105.2 %reduce-scatter.23.cloned.1.call-done = f32[1,512,768]{2,1,0:T(8,128)} async-done(((f32[1,2048,768]{2,1,0:T(8,128)}), f32[1,512,768]{2,1,0:T(8,128)}) %reduce-scatter.23.cloned.1.call-update) | async-done | bytes 1572880 | tf_op jit(solution)/shard_map/reduce_scatter | solution.py:257
  701.2 64.1 %all-gather.17.cloned.1.call-done = bf16[1,2048,768]{2,1,0:T(8,128)(2,1)} async-done(((bf16[1,512,768]{2,1,0:T(8,128)(2,1)}), bf16[1,2048,768]{2,1,0:T(8,128)(2,1)}) %all-gather.17.cloned.1.call-update) | async-done | bytes 3145744 | tf_op jit(solution)/shard_map/all_gather | solution.py:265
  773.8 140.8 %while.48 = (s32[]{:T(128)}, f32[2048,3,64]{0,2,1:T(8,128)}, f32[2048,3,64]{0,2,1:T(8,128)}, bf16[4,512,3,64]{1,3,2,0:T(8,128)(2,1)}, s32[4]{0:T(128)S(1)}, /*in...) while((s32[]{:T(128)}, f32[2048,3,64]{0,2,1:T(8,128)}, ...), condition=%wide.region_21.22_spmd.clone, body=%wide.region_19.21_spmd.clone.sunk | while | flops 2063661568 | bytes 150202832 | solution.py:116
  792.2 6.1 multiply_convert_fusion.4
  798.3 5.8 fusion.147
  815.4 6.1 fusion.146
  827.3 6.1 multiply_convert_fusion.4
  851.0 6.1 fusion.146
  862.9 6.1 multiply_convert_fusion.4
  869.0 5.8 fusion.147
  886.6 6.1 fusion.146
  898.5 6.1 multiply_convert_fusion.4
  904.6 5.8 fusion.147
  923.4 6.9 fusion.50
  930.4 6.9 fusion.47
  953.6 42.0 %all-reduce = (f32[]{:T(128)}, f32[768]{0:T(1024)}, f32[768]{0:T(1024)}, f32[768]{0:T(1024)}, f32[3072]{0:T(1024)}, /*index=5*/f32[768]{0:T(1024)}, f32[768]{0:T...) all-reduce(f32[]{:T(128)} %get-tuple-element.270, ...), channel_id=1, replica_groups=mesh['dp'=8,'tensor'=4] {'dp','tensor'}, use_global_device_ids=true, to_apply=%region_11.12 | all-reduce | flops 9217 | bytes 73736 | tf_op jit(solution)/shard_map/psum | solution.py:321
  1000.5 28.9 %reduce-scatter.27.cloned.1.call-done = f32[96,768]{1,0:T(8,128)} async-done(((f32[768,768]{1,0:T(8,128)}), f32[96,768]{1,0:T(8,128)}) %reduce-scatter.27.cloned.1.call-update) | async-done | bytes 294928 | tf_op jit(solution)/shard_map/reduce_scatter | solution.py:318
  1029.4 46.5 %reduce-scatter.29.cloned.1.call-done = f32[768,96]{0,1:T(8,128)} async-done(((f32[768,768]{0,1:T(8,128)}), f32[768,96]{0,1:T(8,128)}) %reduce-scatter.29.cloned.1.call-update) | async-done | bytes 294928 | tf_op jit(solution)/shard_map/reduce_scatter | solution.py:319
  1075.9 38.7 %reduce-scatter.35.cloned.1.call-done = f32[96,192]{1,0:T(8,128)} async-done(((f32[768,192]{1,0:T(8,128)}), f32[96,192]{1,0:T(8,128)}) %reduce-scatter.35.cloned.1.call-update) | async-done | bytes 73744
  1114.6 38.6 %reduce-scatter.33.cloned.1.call-done = f32[96,192]{1,0:T(8,128)} async-done(((f32[768,192]{1,0:T(8,128)}), f32[96,192]{1,0:T(8,128)}) %reduce-scatter.33.cloned.1.call-update) | async-done | bytes 73744
  1153.2 38.7 %reduce-scatter.31.cloned.1.call-done = f32[96,192]{1,0:T(8,128)} async-done(((f32[768,192]{1,0:T(8,128)}), f32[96,192]{1,0:T(8,128)}) %reduce-scatter.31.cloned.1.call-update) | async-done | bytes 73744
  (316 shorter events, 168.8 us)
Async XLA Ops:
  8.0 22.3 %copy-start.44 = (bf16[96,192]{1,0:T(8,128)(2,1)S(1)}, bf16[96,192]{1,0:T(8,128)(2,1)}, u32[]{:S(2)}) copy-start(bf16[96,192]{1,0:T(8,128)(2,1)} %param.30) | copy-start | bytes 110596
  8.0 31.2 %copy-start.45 = (bf16[96,192]{1,0:T(8,128)(2,1)S(1)}, bf16[96,192]{1,0:T(8,128)(2,1)}, u32[]{:S(2)}) copy-start(bf16[96,192]{1,0:T(8,128)(2,1)} %param.31) | copy-start | bytes 110596
  8.0 68.6 %all-gather.7.cloned.1.call-start = ((), (), s32[]{:S(2)}) async-start(), calls=%async_computation.10 | async-start | bytes 3932160 | tf_op jit(solution)/shard_map/all_gather | solution.py:186
  8.8 276.5 %reduce-scatter.19.cloned.1.call-start = ((), (), s32[]{:S(2)}) async-start(), calls=%async_computation.11 | async-start | bytes 7864320 | tf_op jit(solution)/shard_map/reduce_scatter | solution.py:199
  30.3 46.4 %copy-start.26 = (bf16[768,192]{1,0:T(8,128)(2,1)}, bf16[768,192]{1,0:T(8,128)(2,1)S(1)}, u32[]{:S(2)}) copy-start(bf16[768,192]{1,0:T(8,128)(2,1)S(1)} %all_gather.30) | copy-start | bytes 884740
  39.2 37.5 %copy-start.28 = (bf16[768,192]{1,0:T(8,128)(2,1)}, bf16[768,192]{1,0:T(8,128)(2,1)S(1)}, u32[]{:S(2)}) copy-start(bf16[768,192]{1,0:T(8,128)(2,1)S(1)} %all_gather.31) | copy-start | bytes 884740
  48.7 32.4 %copy-start.30 = (bf16[768,192]{1,0:T(8,128)(2,1)}, bf16[768,192]{1,0:T(8,128)(2,1)S(1)}, u32[]{:S(2)}) copy-start(bf16[768,192]{1,0:T(8,128)(2,1)S(1)} %all_gather.32) | copy-start | bytes 884740
  175.7 109.6 %copy-start.7 = (bf16[1,512,768]{2,1,0:T(8,128)(2,1)S(1)}, bf16[1,512,768]{2,1,0:T(8,128)(2,1)}, u32[]{:S(2)}) copy-start(bf16[1,512,768]{2,1,0:T(8,128)(2,1)} %param.24) | copy-start | bytes 2359300
  175.7 116.3 %all-gather.11.cloned.1.call-start = ((), (), s32[]{:S(2)}) async-start(), calls=%async_computation.13 | async-start | bytes 1327104 | tf_op jit(solution)/shard_map/all_gather | solution.py:166
  176.3 177.3 %all-gather.9.cloned.1.call-start = ((), (), s32[]{:S(2)}) async-start(), calls=%async_computation.12 | async-start | bytes 3932160 | tf_op jit(solution)/shard_map/all_gather | solution.py:212
  176.4 522.5 %copy-start.32 = (f32[768]{0:T(1024)}, f32[768]{0:T(1024)S(1)}, u32[]{:S(2)}) copy-start(f32[768]{0:T(1024)S(1)} %convert_element_type.167) | copy-start | bytes 9220
  176.4 522.5 %copy-start.34 = (f32[768]{0:T(1024)}, f32[768]{0:T(1024)S(1)}, u32[]{:S(2)}) copy-start(f32[768]{0:T(1024)S(1)} %convert_element_type.168) | copy-start | bytes 9220
  289.7 88.3 %all-gather.13.cloned.1.call-start = ((), (), s32[]{:S(2)}) async-start(), calls=%async_computation.14 | async-start | bytes 1327104 | tf_op jit(solution)/shard_map/all_gather | solution.py:167
  290.2 207.1 %reduce-scatter.21.cloned.1.call-start = ((), (), s32[]{:S(2)}) async-start(), calls=%async_computation.15 | async-start | bytes 7864320 | tf_op jit(solution)/shard_map/reduce_scatter | solution.py:220
  385.5 185.6 %all-gather.15.cloned.1.call-start = ((), (), s32[]{:S(2)}) async-start(), calls=%async_computation.16 | async-start | bytes 3932160 | tf_op jit(solution)/shard_map/all_gather | solution.py:240
  499.4 5.1 copy-start.10
  499.5 5.0 copy-start.43
  499.8 4.7 copy-start.49
  507.0 187.4 %reduce-scatter.23.cloned.1.call-start = ((), (), s32[]{:S(2)}) async-start(), calls=%async_computation.17 | async-start | bytes 7864320 | tf_op jit(solution)/shard_map/reduce_scatter | solution.py:257
  571.1 9.3 copy-start.65
  585.0 180.4 %all-gather.17.cloned.1.call-start = ((), (), s32[]{:S(2)}) async-start(), calls=%async_computation.18 | async-start | bytes 3932160 | tf_op jit(solution)/shard_map/all_gather | solution.py:265
  694.4 4.6 copy-start.15
  694.4 4.6 copy-start.16
  694.4 4.6 copy-start.37
  694.4 4.6 copy-start.40
  701.2 295.2 %reduce-scatter.37.cloned.1.call-start = ((), (), s32[]{:S(2)}) async-start(), calls=%async_computation.25 | async-start | bytes 884736
  769.7 228.3 %reduce-scatter.25.cloned.1.call-start = ((), (), s32[]{:S(2)}) async-start(), calls=%async_computation.19 | async-start | bytes 3932160 | tf_op jit(solution)/shard_map/reduce_scatter | solution.py:298
  774.0 7.8 copy-start.2
  774.0 7.8 copy-start.18
  798.3 5.8 copy-start
  807.6 7.7 copy-start.2
  807.6 7.7 copy-start.18
  833.4 5.8 copy-start
  843.2 7.7 copy-start.2
  843.2 7.7 copy-start.18
  869.0 5.8 copy-start
  874.8 4.1 copy-start.19
  878.8 7.7 copy-start.2
  878.8 7.7 copy-start.18
  904.6 5.8 copy-start
  916.8 20.6 %copy-start.22 = (bf16[2048,3,64]{0,2,1:T(8,128)(2,1)}, bf16[2048,3,64]{0,2,1:T(8,128)(2,1)S(1)}, u32[]{:S(2)}) copy-start(bf16[2048,3,64]{0,2,1:T(8,128)(2,1)S(1)} %convert_element_type.191) | copy-start | bytes 2359300
  918.7 18.8 %copy-start.24 = (bf16[2048,3,64]{0,2,1:T(8,128)(2,1)}, bf16[2048,3,64]{0,2,1:T(8,128)(2,1)S(1)}, u32[]{:S(2)}) copy-start(bf16[2048,3,64]{0,2,1:T(8,128)(2,1)S(1)} %convert_element_type.192) | copy-start | bytes 2359300
  923.4 106.0 %reduce-scatter.27.cloned.1.call-start = ((), (), s32[]{:S(2)}) async-start(), calls=%async_computation.20 | async-start | bytes 2654208 | tf_op jit(solution)/shard_map/reduce_scatter | solution.py:318
  930.4 145.5 %reduce-scatter.29.cloned.1.call-start = ((), (), s32[]{:S(2)}) async-start(), calls=%async_computation.21 | async-start | bytes 2654208 | tf_op jit(solution)/shard_map/reduce_scatter | solution.py:319
  937.4 177.3 %reduce-scatter.35.cloned.1.call-start = ((), (), s32[]{:S(2)}) async-start(), calls=%async_computation.24 | async-start | bytes 884736
  943.7 209.5 %reduce-scatter.33.cloned.1.call-start = ((), (), s32[]{:S(2)}) async-start(), calls=%async_computation.23 | async-start | bytes 884736
  946.2 245.8 %reduce-scatter.31.cloned.1.call-start = ((), (), s32[]{:S(2)}) async-start(), calls=%async_computation.22 | async-start | bytes 884736
  951.7 46.3 %copy-start.13 = (f32[1,512,768]{2,1,0:T(8,128)S(1)}, f32[1,512,768]{2,1,0:T(8,128)}, u32[]{:S(2)}) copy-start(f32[1,512,768]{2,1,0:T(8,128)} %get-tuple-element.327) | copy-start | bytes 4718596
  (53 other events, 129.0 us)
Sparse Core Ops, SparseCore 0:
  10.4 66.1 all-gather.6
  175.9 109.3 reduce-scatter.18
  507.1 63.9 all-gather.14
  701.3 63.9 all-gather.16
Sparse Core Ops, SparseCore 1:
  178.1 22.5 all-gather.10
  289.7 63.8 all-gather.8
  355.4 22.5 all-gather.12
  385.6 111.7 reduce-scatter.20
  585.0 109.3 reduce-scatter.22
  769.8 33.6 reduce-scatter.36
  923.4 59.6 reduce-scatter.24
  986.9 42.5 reduce-scatter.26
  1033.6 42.3 reduce-scatter.28
  1079.7 34.9 reduce-scatter.34
  1118.2 34.9 reduce-scatter.32
  1156.9 34.9 reduce-scatter.30
where the time goes:
time: 1200 us
  waiting for transfers between devices  699 us (58%)
  matrix products  212 us (18%)
  blocking collectives  127 us (11%)
  other arithmetic  98.9 us (8%)
  local copies, waits for them, and re-layouts  28.6 us (2%)
  between operations  19.5 us (2%)
  loops' own time  13.7 us (1%)
    unnamed x20, waiting for transfers between devices  118 us
    reduce_scatter x1, waiting for transfers between devices, local(): lax.psum_scatter(attn_partial, 'tensor', scatter_dimension=1, tiled=True)  108 us
    reduce_scatter x1, waiting for transfers between devices, local(): lax.psum_scatter(ffn_back_partial, 'tensor', scatter_dimension=1, tiled=T...  105 us
    all_gather x1, waiting for transfers between devices, local(): lax.all_gather(attn_grad.reshape(groups, part_len, model_width), 'tensor'...  64.1 us
    all_gather x1, waiting for transfers between devices, local(): lax.all_gather(branch_grad.reshape(groups, part_len, model_width), 'tenso...  64.1 us
    all_gather x1, waiting for transfers between devices, local(): lax.all_gather(first.reshape(groups, part_len, model_width), 'tensor', ax...  61.6 us
    reduce_scatter x1, waiting for transfers between devices, local(): lax.psum_scatter(branch_partial, 'tensor', scatter_dimension=1, tiled=True)  58.3 us
    reduce_scatter x1, waiting for transfers between devices, local(): lax.psum_scatter(outer_weight_grad, 'dp', scatter_dimension=1, tiled=True)  46.5 us
  transfers between devices with their start and end apart: 16, of which 13 were waited for; matrix products, arithmetic and copies ran while one was open for 17% of the time, Pallas kernels for 0%

commit v1 on v0

v1 whole, which is shorter than its diff:
```python
import functools

import jax
import jax.numpy as jnp
from jax import lax
from jax.experimental import pallas as pl
from jax.experimental.pallas import tpu as pltpu
from jax.sharding import PartitionSpec as P

DH = 64
BLOCK = 256
SLAB = 4 * DH
EPSILON = 1e-12
ROOT_HALF = 0.7071067811865476
INV_ROOT_TAU = 0.3989422804014327
LOG2E = 1.4426950408889634
LN2 = 0.6931471805599453
SCALE = DH ** (-0.5)
MASKED = -1e30

BF16 = jnp.bfloat16
F32 = jnp.float32
NN = (((1,), (0,)), ((), ()))
NT = (((1,), (1,)), ((), ()))
TN = (((0,), (0,)), ((), ()))


def dot(left_side, right_side, dims=NN):
    return lax.dot_general(left_side, right_side, dims, preferred_element_type=F32)


def norm_forward(summed, gain_vec, shift_vec):
    average = jnp.mean(summed, axis=-1, keepdims=True)
    centered = summed - average
    variance = jnp.mean(centered * centered, axis=-1, keepdims=True)
    inverse = lax.rsqrt(variance + EPSILON)
    normed = centered * inverse
    return (normed * gain_vec + shift_vec, normed, inverse)


def norm_backward(upstream, normed, inverse, gain_vec):
    scaled = upstream * gain_vec
    first_mean = jnp.mean(scaled, axis=-1, keepdims=True)
    second_mean = jnp.mean(scaled * normed, axis=-1, keepdims=True)
    back_grad = inverse * (scaled - first_mean - normed * second_mean)
    return (back_grad, jnp.sum(upstream * normed, axis=0), jnp.sum(upstream, axis=0))


def lane_is_right(rows):
    return lax.broadcasted_iota(jnp.int32, (rows, 2 * DH), 1) >= DH


def attend_forward(low_ref, high_ref, qkv_ref, seg_col_ref, seg_row_ref, ctx_ref, lse_ref, held, outs):
    head = pl.program_id(0)
    blocks = qkv_ref.shape[0] // BLOCK
    for qb in range(blocks):
        rows = pl.ds(qb * BLOCK, BLOCK)
        query = qkv_ref[rows, : 2 * DH] * jnp.asarray(SCALE, BF16)
        seg_q = seg_col_ref[rows, :]
        low, high = low_ref[qb], high_ref[qb]

        def score(kb, peak):
            keys = pl.ds(pl.multiple_of(kb * BLOCK, BLOCK), BLOCK)
            scores = dot(query, qkv_ref[keys, 2 * DH :], NT)
            scores = jnp.where(seg_q == seg_row_ref[:, keys], scores, MASKED)
            held[kb] = scores
            return jnp.maximum(peak, jnp.maximum(scores[:, :128], scores[:, 128:]))

        peak = lax.fori_loop(low, high, score, jnp.full((BLOCK, 128), MASKED, F32))
        highest = jnp.max(peak, axis=-1, keepdims=True)

        def weigh(kb, carry):
            total, acc = carry
            keys = pl.ds(pl.multiple_of(kb * BLOCK, BLOCK), BLOCK)
            raised = jnp.exp2((held[kb] - highest) * LOG2E)
            total = total + (raised[:, :128] + raised[:, 128:])
            return (total, acc + dot(raised.astype(BF16), qkv_ref[keys, 2 * DH :]))

        zero = jnp.zeros((BLOCK, 128), F32)
        total, acc = lax.fori_loop(low, high, weigh, (zero, zero))
        summed = jnp.sum(total, axis=-1, keepdims=True)
        outs[rows, :] = (acc / summed).astype(BF16)
        lse_ref[0, :, rows] = jnp.transpose(highest + jnp.log(summed))
    value = outs[...]
    right = lane_is_right(value.shape[0])

    @pl.when(head == 0)
    def _():
        ctx_ref[:, :128] = jnp.where(right, jnp.zeros_like(value), pltpu.roll(value, DH, 1))

    @pl.when(head == 1)
    def _():
        ctx_ref[:, :128] = jnp.where(right, value, ctx_ref[:, :128])

    @pl.when(head == 2)
    def _():
        ctx_ref[:, 128:] = pltpu.roll(value, DH, 1)[:, :DH]


def attend_backward(
    low_ref, high_ref, qkv_ref, seg_col_ref, seg_row_ref, ctx_ref, grad_ref, lse_ref,
    out_ref, sums_ref, grads, dkv, deltas
):
    head = pl.program_id(0)
    seq_len = qkv_ref.shape[0]
    blocks = seq_len // BLOCK
    right = lane_is_right(seq_len)

    def place(value, both):
        moved = pltpu.roll(value, DH, 1) if both else value
        grads[...] = jnp.where(right, moved, jnp.zeros_like(moved))

    def widen(ref):
        tail = ref[:, 128:]
        return jnp.concatenate([tail, jnp.zeros_like(tail)], axis=1)

    def delta_of(low_lanes, first_tile):
        if first_tile:
            product = grad_ref[:, :128].astype(F32) * ctx_ref[:, :128].astype(F32)
            keep = jnp.logical_not(right) if low_lanes else right
            product = jnp.where(keep, product, 0.0)
        else:
            product = grad_ref[:, 128:].astype(F32) * ctx_ref[:, 128:].astype(F32)
        return jnp.sum(product, axis=-1, keepdims=True)

    @pl.when(head == 0)
    def _():
        place(grad_ref[:, :128], True)
        deltas[...] = jnp.transpose(delta_of(True, True))

    @pl.when(head == 1)
    def _():
        place(grad_ref[:, :128], False)
        deltas[...] = jnp.transpose(delta_of(False, True))

    @pl.when(head == 2)
    def _():
        place(widen(grad_ref), True)
        deltas[...] = jnp.transpose(delta_of(True, False))

    dkv[...] = jnp.zeros_like(dkv)
    right_block = lane_is_right(BLOCK)
    query_total = jnp.zeros((1, 128), F32)
    for qb in range(blocks):
        rows = pl.ds(qb * BLOCK, BLOCK)
        query = qkv_ref[rows, : 2 * DH] * jnp.asarray(SCALE, BF16)
        grad = grads[rows, :]
        paired = jnp.concatenate([query, grad], axis=0)
        seg_q = seg_row_ref[:, rows]
        lse = lse_ref[0, :, rows]
        delta = deltas[:, rows]
        low, high = low_ref[qb], high_ref[qb]

        def step(kb, acc):
            keys = pl.ds(pl.multiple_of(kb * BLOCK, BLOCK), BLOCK)
            pair = qkv_ref[keys, 2 * DH :]
            scores = dot(pair, query, NT)
            scores = jnp.where(seg_col_ref[keys, :] == seg_q, scores, MASKED)
            probs = jnp.exp2((scores - lse) * LOG2E)
            probs_grad = dot(pair, grad, NT)
            score_grad = (probs * (probs_grad - delta)).astype(BF16)
            both = jnp.concatenate([score_grad, probs.astype(BF16)], axis=1)
            dkv[keys, :] += dot(both, paired)
            return acc + dot(score_grad, pair, TN)

        acc = lax.fori_loop(low, high, step, jnp.zeros((BLOCK, 128), F32))
        query_grad = jnp.where(right_block, 0.0, acc * SCALE).astype(BF16)
        out_ref[rows, : 2 * DH] = query_grad
        query_total = query_total + jnp.sum(query_grad.astype(F32), axis=0, keepdims=True)
    pair_grad = dkv[...].astype(BF16)
    out_ref[:, 2 * DH :] = pair_grad
    sums_ref[0, :, : 2 * DH] = query_total
    sums_ref[0, :, 2 * DH :] = jnp.sum(pair_grad.astype(F32), axis=0, keepdims=True)


def document_blocks(segment_row):
    blocks = segment_row.shape[0] // BLOCK
    starts = segment_row[::BLOCK]
    stops = segment_row[BLOCK - 1 :: BLOCK]
    low = jnp.sum((segment_row[None, :] < starts[:, None]).astype(jnp.int32), axis=1)
    high = jnp.sum((segment_row[None, :] <= stops[:, None]).astype(jnp.int32), axis=1)
    return (low // BLOCK, (high + BLOCK - 1) // BLOCK)


def run_forward(bounds, qkv, seg_col, seg_row):
    seq_len, width = qkv.shape
    heads = width // SLAB
    blocks = seq_len // BLOCK
    return pl.pallas_call(
        attend_forward,
        out_shape=(
            jax.ShapeDtypeStruct((seq_len, heads * DH), BF16),
            jax.ShapeDtypeStruct((heads, 1, seq_len), F32),
        ),
        grid_spec=pltpu.PrefetchScalarGridSpec(
            num_scalar_prefetch=2,
            grid=(heads,),
            in_specs=[
                pl.BlockSpec((seq_len, SLAB), lambda h, *_: (0, h)),
                pl.BlockSpec((seq_len, 1), lambda h, *_: (0, 0)),
                pl.BlockSpec((1, seq_len), lambda h, *_: (0, 0)),
            ],
            out_specs=(
                pl.BlockSpec((seq_len, heads * DH), lambda h, *_: (0, 0)),
                pl.BlockSpec((1, 1, seq_len), lambda h, *_: (h, 0, 0)),
            ),
            scratch_shapes=[
                pltpu.VMEM((blocks, BLOCK, BLOCK), F32),
                pltpu.VMEM((seq_len, 2 * DH), BF16),
            ],
        ),
        compiler_params=pltpu.CompilerParams(
            dimension_semantics=("arbitrary",), vmem_limit_bytes=40 << 20
        ),
        cost_estimate=pl.CostEstimate(
            flops=heads * seq_len * seq_len * 256, bytes_accessed=8 << 20, transcendentals=heads * seq_len * seq_len // 3
        ),
        name="attend_forward",
    )(*bounds, qkv, seg_col, seg_row)


def run_backward(bounds, qkv, seg_col, seg_row, ctx, grad, lse):
    seq_len, width = qkv.shape
    heads = width // SLAB
    return pl.pallas_call(
        attend_backward,
        out_shape=(
            jax.ShapeDtypeStruct((seq_len, width), BF16),
            jax.ShapeDtypeStruct((heads, 1, SLAB), F32),
        ),
        grid_spec=pltpu.PrefetchScalarGridSpec(
            num_scalar_prefetch=2,
            grid=(heads,),
            in_specs=[
                pl.BlockSpec((seq_len, SLAB), lambda h, *_: (0, h)),
                pl.BlockSpec((seq_len, 1), lambda h, *_: (0, 0)),
                pl.BlockSpec((1, seq_len), lambda h, *_: (0, 0)),
                pl.BlockSpec((seq_len, heads * DH), lambda h, *_: (0, 0)),
                pl.BlockSpec((seq_len, heads * DH), lambda h, *_: (0, 0)),
                pl.BlockSpec((1, 1, seq_len), lambda h, *_: (h, 0, 0)),
            ],
            out_specs=(
                pl.BlockSpec((seq_len, SLAB), lambda h, *_: (0, h)),
                pl.BlockSpec((1, 1, SLAB), lambda h, *_: (h, 0, 0)),
            ),
            scratch_shapes=[
                pltpu.VMEM((seq_len, 2 * DH), BF16),
                pltpu.VMEM((seq_len, 2 * DH), F32),
                pltpu.VMEM((1, seq_len), F32),
            ],
        ),
        compiler_params=pltpu.CompilerParams(
            dimension_semantics=("arbitrary",), vmem_limit_bytes=40 << 20
        ),
        cost_estimate=pl.CostEstimate(
            flops=heads * seq_len * seq_len * 640, bytes_accessed=12 << 20, transcendentals=heads * seq_len * seq_len // 3
        ),
        name="attend_backward",
    )(*bounds, qkv, seg_col, seg_row, ctx, grad, lse)


def interleave(query, key, value, heads):
    rows = query.shape[0]
    parts = [part.reshape(rows, heads, 1, DH) for part in (query, jnp.zeros_like(query), key, value)]
    return jnp.concatenate(parts, axis=2).reshape(rows, heads * SLAB)


def place_slice(local_grad, full_size, offset):
    return lax.dynamic_update_slice_in_dim(jnp.zeros((full_size,), F32), local_grad, offset, 0)


def local(
    inputs, segment_ids, valid_mask, teacher, cotangent,
    w_query, w_key, w_value, w_output, w_inner, w_outer,
    query_bias, value_bias, output_bias, inner_bias, outer_bias,
    gain_attn, shift_attn, gain_ffn, shift_ffn,
):
    _, part_len, width = inputs.shape
    parts = lax.axis_size("tensor")
    copies = lax.axis_size("dp")
    rank = lax.axis_index("tensor")
    total_tokens = part_len * parts * copies
    seq_len = part_len * parts
    head_cols = w_query.shape[1]
    heads = head_cols // DH
    hidden_cols = w_inner.shape[1]
    hidden_width = hidden_cols * parts

    rows_in = inputs.reshape(part_len, width)
    tokens = lax.all_gather(rows_in, "tensor", axis=0, tiled=True)
    w_heads = lax.all_gather(interleave(w_query, w_key, w_value, heads), "dp", axis=0, tiled=True)
    mine = jnp.concatenate((w_inner, w_outer.T, w_output.T), axis=1)
    whole = lax.all_gather(mine, ("dp", "tensor"), axis=0, tiled=False)
    shard_rows = mine.shape[0]
    whole = whole.reshape(copies, parts, shard_rows, -1).transpose(0, 2, 1, 3)
    inner_full = whole[..., :hidden_cols].reshape(width, hidden_width)
    outer_full = whole[..., hidden_cols : 2 * hidden_cols].reshape(width, hidden_width)
    output_full = whole[..., 2 * hidden_cols :].reshape(width, width)

    valid_rows = valid_mask.astype(F32).reshape(part_len, 1)
    counted = lax.psum(jnp.sum(valid_rows), ("dp", "tensor"))

    mine_cols = rank * head_cols
    query_shift = lax.dynamic_slice_in_dim(query_bias, mine_cols, head_cols).astype(F32)
    value_shift = lax.dynamic_slice_in_dim(value_bias, mine_cols, head_cols).astype(F32)
    shifts = interleave(query_shift[None], jnp.zeros_like(query_shift)[None], value_shift[None], heads)
    qkv = (dot(tokens, w_heads) + shifts).astype(BF16)

    segment_row = segment_ids.reshape(seq_len)
    bounds = document_blocks(segment_row)
    seg_col = segment_row.reshape(seq_len, 1)
    seg_row = segment_row.reshape(1, seq_len)
    context, lse = run_forward(bounds, qkv, seg_col, seg_row)

    def to_tokens(by_head):
        moved = lax.all_to_all(by_head.reshape(parts, part_len, head_cols), "tensor", 0, 0)
        return moved.transpose(1, 0, 2).reshape(part_len, width)

    def to_heads(by_token):
        split = by_token.reshape(part_len, parts, head_cols).transpose(1, 0, 2)
        return lax.all_to_all(split, "tensor", 0, 0).reshape(seq_len, head_cols)

    context_rows = to_tokens(context)
    attention = dot(context_rows, output_full, NT)
    first_sum = rows_in.astype(F32) + attention + output_bias.astype(F32)
    gain_one = gain_attn.astype(F32)
    first_exact, normed_one, inverse_one = norm_forward(first_sum, gain_one, shift_attn.astype(F32))
    first = first_exact.astype(BF16)
    hidden = dot(first, inner_full) + inner_bias.astype(F32)
    bend = 0.5 * (1.0 + lax.erf(hidden * ROOT_HALF))
    activated = (hidden * bend).astype(BF16)
    slope = bend + hidden * INV_ROOT_TAU * jnp.exp(-0.5 * hidden * hidden)
    branch = dot(activated, outer_full, NT)
    second_sum = first.astype(F32) + branch + outer_bias.astype(F32)
    gain_two = gain_ffn.astype(F32)
    layer_rows, normed_two, inverse_two = norm_forward(second_sum, gain_two, shift_ffn.astype(F32))
    misfit = layer_rows - teacher.reshape(part_len, width).astype(F32)
    squared = jnp.sum(valid_rows * misfit * misfit)
    out_grad = cotangent.reshape(part_len, width).astype(F32) + valid_rows * misfit * (
        total_tokens / counted
    )
    second_grad, gain_ffn_grad, shift_ffn_grad = norm_backward(
        out_grad, normed_two, inverse_two, gain_two
    )
    branch_grad = second_grad.astype(BF16)
    outer_bias_grad = jnp.sum(branch_grad.astype(F32), axis=0)
    active_grad = dot(branch_grad, outer_full)
    hidden_grad = (active_grad * slope).astype(BF16)
    inner_bias_grad = jnp.sum(hidden_grad.astype(F32), axis=0)
    ffn_back = dot(hidden_grad, inner_full, NT)
    first_grad, gain_attn_grad, shift_attn_grad = norm_backward(
        second_grad + ffn_back, normed_one, inverse_one, gain_one
    )
    attn_grad = first_grad.astype(BF16)
    output_bias_grad = jnp.sum(attn_grad.astype(F32), axis=0)
    context_grad = dot(attn_grad, output_full).astype(BF16)
    head_grad = to_heads(context_grad)

    inner_weight = dot(first, hidden_grad, TN).astype(BF16).reshape(width, parts, hidden_cols)
    outer_weight = dot(branch_grad, activated, TN).astype(BF16).reshape(width, parts, hidden_cols)
    output_weight = dot(attn_grad, context_rows, TN).astype(BF16).reshape(width, parts, head_cols)
    packed = jnp.concatenate((inner_weight, outer_weight, output_weight), axis=2)
    packed = lax.psum_scatter(packed, "dp", scatter_dimension=0, tiled=True)
    packed = lax.psum_scatter(packed.transpose(1, 0, 2), "tensor", scatter_dimension=0, tiled=True)
    packed = packed.reshape(shard_rows, -1).astype(F32)

    joined_grad, sums = run_backward(bounds, qkv, seg_col, seg_row, context, head_grad, lse)
    attn_back = dot(joined_grad, w_heads, NT).astype(BF16)
    attn_back = lax.psum_scatter(attn_back, "tensor", scatter_dimension=0, tiled=True)
    input_grad = first_grad + attn_back.astype(F32)
    head_weights = dot(tokens, joined_grad, TN).astype(BF16)
    head_weights = lax.psum_scatter(head_weights, "dp", scatter_dimension=0, tiled=True)
    head_weights = head_weights.astype(F32).reshape(shard_rows, heads, 4, DH)

    def pick(which):
        return head_weights[:, :, which, :].reshape(shard_rows, head_cols)

    sums = sums.reshape(heads, 4, DH)
    totals = lax.psum(
        (
            squared,
            place_slice(sums[:, 0].reshape(head_cols), width, mine_cols),
            place_slice(sums[:, 3].reshape(head_cols), width, mine_cols),
            output_bias_grad,
            inner_bias_grad,
            outer_bias_grad,
            gain_attn_grad,
            shift_attn_grad,
            gain_ffn_grad,
            shift_ffn_grad,
        ),
        ("dp", "tensor"),
    )
    mse_loss = totals[0] / (counted * width)
    layer_out = layer_rows.astype(BF16).reshape(1, part_len, width)
    return (
        layer_out,
        mse_loss,
        input_grad.reshape(1, part_len, width),
        pick(0),
        pick(2),
        pick(3),
        packed[:, 2 * hidden_cols :].T,
        packed[:, :hidden_cols],
        packed[:, hidden_cols : 2 * hidden_cols].T,
    ) + tuple(totals[1:])


def solution(mesh):
    shard = P("dp", "tensor", None)
    in_specs = (
        (shard, P("dp", None), P("dp", "tensor"), shard, shard)
        + (P("dp", "tensor"),) * 3
        + (P("tensor", "dp"), P("dp", "tensor"), P("tensor", "dp"))
        + (P(),) * 9
    )
    out_specs = (
        (shard, P(), shard)
        + (P("dp", "tensor"),) * 3
        + (P("tensor", "dp"), P("dp", "tensor"), P("tensor", "dp"))
        + (P(),) * 9
    )
    return jax.shard_map(local, mesh=mesh, in_specs=in_specs, out_specs=out_specs, check_vma=False)
```

time: 1200 us -> 562 us (0.47)
  waiting for transfers between devices: 699 us -> 169 us
  matrix products: 212 us -> 44.4 us
  Pallas kernels: 0 us -> 87.8 us
  other arithmetic: 98.9 us -> 20.9 us
  local copies, waits for them, and re-layouts: 28.6 us -> 67.2 us
  loops' own time: 13.7 us -> 0 us
  blocking collectives: 127 us -> 140 us
    reduce_scatter x6 -> x3, waiting for transfers between devices: 347 us -> 79.4 us  [the longest x1 47 us: local(): lax.psum_scatter(attn_back, 'tensor', scatter_dimension=0, tiled=True)]
    dot_general x39 -> x12, matrix products: 208 us -> 44.4 us  [dot(): lax.dot_general(left_side, right_side, dims, preferred_element_type=F32)]
    all_gather x6 -> x3, waiting for transfers between devices: 234 us -> 88.3 us  [the longest x1 65.1 us: local(): tokens = lax.all_gather(rows_in, 'tensor', axis=0, tiled=True)]
    unnamed x20 -> x8, waiting for transfers between devices: 118 us -> 1.47 us
    pallas_call x0 -> x2, Pallas kernels: none -> 87.8 us  [the longest x1 46.9 us: run_backward(): pl.pallas_call(attend_backward, out_shape=(jax.ShapeDtypeStruct((seq_len,...]
    reduce_sum x10 -> x3, other arithmetic: 44.4 us -> 2.57 us  [the longest x1 1.83 us: local(): outer_bias_grad = jnp.sum(branch_grad.astype(F32), axis=0)]
    convert_element_type x19 -> x9, other arithmetic: 40.3 us -> 1.05 us  [the longest x1 1.02 us: local(): packed = packed.reshape(shard_rows, -1).astype(F32)]
    all_gather x4 -> x0, blocking collectives: 38.9 us -> none  [the longest x1 11 us: local(): lax.all_gather(w_output, 'dp', axis=1, tiled=True)]
  transfers between devices with their start and end apart: 16 -> 8, of which waited for: 13 -> 4; matrix products, arithmetic and copies ran while one was open for 17% -> 12% of each run, Pallas kernels for 0% -> 16%
where the time goes in v1:
time: 562 us; the launch traced here: 551 us
  waiting for transfers between devices  169 us (30%)
  blocking collectives  140 us (25%)
  Pallas kernels  87.8 us (16%)
  local copies, waits for them, and re-layouts  67.2 us (12%)
  matrix products  44.4 us (8%)
  other arithmetic  20.9 us (4%)
  between operations  18.3 us (3%)
    psum x1, blocking collectives, local(): counted = lax.psum(jnp.sum(valid_rows), ('dp', 'tensor'))  67.1 us
    all_gather x1, waiting for transfers between devices, local(): tokens = lax.all_gather(rows_in, 'tensor', axis=0, tiled=True)  65.1 us
    psum x1, blocking collectives, local(): lax.psum((squared, place_slice(sums[:, 0].reshape(head_cols), width, mine...  49.2 us
    reduce_scatter x1, waiting for transfers between devices, local(): lax.psum_scatter(attn_back, 'tensor', scatter_dimension=0, tiled=True)  47 us
    pallas_call x1, Pallas kernels, run_backward(): pl.pallas_call(attend_backward, out_shape=(jax.ShapeDtypeStruct((seq_len,...  46.9 us
    dot_general x12, matrix products, dot(): lax.dot_general(left_side, right_side, dims, preferred_element_type=F32)  44.4 us
    pallas_call x1, Pallas kernels, run_forward(): pl.pallas_call(attend_forward, out_shape=(jax.ShapeDtypeStruct((seq_len,...  40.9 us
    reduce_scatter x1, waiting for transfers between devices, local(): lax.psum_scatter(packed.transpose(1, 0, 2), 'tensor', scatter_dimension=0...  32.3 us
  transfers between devices with their start and end apart: 8, of which 4 were waited for; matrix products, arithmetic and copies ran while one was open for 12% of the time, Pallas kernels for 16%

profile of v1, /device:TPU:0, one launch (start us, length us, event | category | flops | bytes accessed | tf_op | source)
XLA Modules:
  0.0 551.1 jit_solution(14343570557057060554)
XLA Ops:
  7.3 1.0 copy.113
  9.2 0.9 copy.115
  14.8 23.2 %all-gather.6.cloned.1.call-done = bf16[768,768]{1,0:T(8,128)(2,1)} async-done(((bf16[96,768]{1,0:T(8,128)(2,1)}), bf16[768,768]{1,0:T(8,128)(2,1)}) %all-gather.6.cloned.1.call-update) | async-done | bytes 1179664 | tf_op jit(solution)/shard_map/all_gather | solution.py:291
  38.0 65.1 %all-gather.8.cloned.1.call-done = bf16[1,2048,768]{2,1,0:T(8,128)(2,1)} async-done(((bf16[1,512,768]{2,1,0:T(8,128)(2,1)}), bf16[1,2048,768]{2,1,0:T(8,128)(2,1)}) %all-gather.8.cloned.1.call-update) | async-done | bytes 3145744 | tf_op jit(solution)/shard_map/all_gather | solution.py:290
  103.1 4.8 fusion.8.qkv_ref
  108.0 40.9 %attend_forward.1 = (bf16[2048,192]{1,0:T(8,128)(2,1)S(1)}, f32[3,1,2048]{2,1,0:T(1,128)S(1)}) custom-call(s32[8]{0:T(128)S(1)} %get-tuple-element.161.low_ref, s32[8]{0:T(128)S(1)} %get-tuple-element.160.high_ref, bf16[2048,768]{1,0:T(8,128)(2,1)S(1)} %fusion.8.qkv_ref, s32[2048,1]{1,0:T(8,128)S(1)} %copy.119.seg_col_ref, s32[1,2048]{1,0:T(1,128)S(1)} %copy-done), custom_call_target="tpu_custom_call" | custom-call | flops 3221225472 | bytes 8388608 | tf_op jit(solution)/shard_map/attend_forward/pallas_call | solution.py:189
  149.0 1.2 copy.120
  150.2 3.5 all-to-all-start
  154.4 67.1 %psum.78 = f32[]{:T(128)} all-reduce(f32[]{:T(128)} %convert_reduce_fusion.5), channel_id=1, replica_groups=mesh['dp'=8,'tensor'=4] {'dp','tensor'}, use_global_device_ids=true, to_apply=%region_9.10 | all-reduce | flops 1 | bytes 8 | tf_op jit(solution)/shard_map/psum | solution.py:301
  222.3 13.9 %copy.145 = bf16[8,4,96,1728]{3,1,2,0:T(4,128)(2,1)} copy(bf16[8,4,96,1728]{3,2,1,0:T(8,128)(2,1)} %bitcast.130) | data formatting | bytes 21233664 | tf_op jit(solution)/shard_map/reshape | solution.py:295
  236.2 3.1 slice.52
  239.3 4.2 reshape.198
  243.5 10.8 %fusion.27 = (bf16[8,96,4,768]{3,2,1,0:T(4,128)(2,1)}, bf16[8,96,4,768]{3,2,1,0:T(4,128)(2,1)}) fusion(bf16[8,96,4,1728]{3,2,1,0:T(4,128)(2,1)} %bitcast.115), kind=kLoop, calls=%fused_computation.87 | loop fusion | bytes 18874368 | tf_op jit(solution)/shard_map/slice | solution.py:297
  254.3 2.6 fusion.29
  257.3 1.0 copy.140
  258.3 1.1 slice-done
  259.4 1.0 copy.141
  260.5 3.3 multiply_convert_fusion
  263.9 2.8 fusion.30
  268.1 2.4 fusion.26
  270.5 1.8 convert_reduce_fusion.1
  272.3 2.9 convolution_convert_fusion
  275.2 5.0 convert_reduce_fusion
  280.3 1.7 copy-done.22
  282.0 3.4 convolution_convert_fusion.1
  285.4 5.1 multiply_reduce_fusion.1
  290.4 2.4 copy.147
  292.8 2.5 copy.146
  295.9 1.1 copy-done.6
  297.0 1.8 convolution_convert_fusion.3
  298.8 2.5 copy.129
  301.3 9.5 %pad_maximum_fusion = bf16[768,4,1728]{2,0,1:T(8,128)(2,1)} fusion(bf16[768,4,192]{2,0,1:T(8,128)(2,1)} %copy.129, bf16[768,4,768]{2,0,1:T(8,128)(2,1)} %bitcast.125, bf16[768,4,768]{2,0,1:T(8,128)(2,1)} %bitcast.124), kind=kLoop, calls=%fused_computation | loop fusion | flops 31850496 | bytes 21233664 | tf_op jit(solution)/shard_map/concatenate | solution.py:362
  310.9 3.4 convolution_convert_fusion.4
  314.3 1.4 copy.124
  315.7 23.3 %all_to_all.10 = bf16[4,512,192]{1,2,0:T(8,128)(2,1)} all-to-all(bf16[4,512,192]{1,2,0:T(8,128)(2,1)S(1)} %bitcast.140), channel_id=1, replica_groups=mesh['dp'=8,'tensor'=4] {'tensor'}, dimensions={0} | all-to-all | bytes 1572864 | tf_op jit(solution)/shard_map/all_to_all | solution.py:321
  339.0 1.6 copy.125
  340.6 1.9 copy-done.4
  342.5 46.9 %attend_backward.1 = (bf16[2048,768]{1,0:T(8,128)(2,1)S(1)}, f32[3,1,256]{2,1,0:T(1,128)S(1)}) custom-call(s32[8]{0:T(128)S(1)} %get-tuple-element.161.low_ref, s32[8]{0:T(128)S(1)} %get-tuple-element.160.high_ref, bf16[2048,768]{1,0:T(8,128)(2,1)S(1)} %copy-done.4, s32[2048,1]{1,0:T(8,128)S(1)} %copy.119.seg_col_ref, s32[1,2048]{1,0:T(1,128)S(1)} %copy-done, ...), custom_call_target="tpu_custom_call" | custom-call | flops 8053063680 | bytes 12582912 | tf_op jit(solution)/shard_map/attend_backward/pallas_call | solution.py:225
  389.4 1.7 copy-done.1
  391.1 3.8 fusion.17
  395.0 2.5 copy.136
  397.6 5.3 convolution_convert_fusion.2
  405.0 49.2 %all-reduce = (f32[]{:T(128)}, f32[768]{0:T(1024)}, f32[768]{0:T(1024)}, f32[768]{0:T(1024)}, f32[3072]{0:T(1024)}, /*index=5*/f32[768]{0:T(1024)}, f32[768]{0:T...) all-reduce(f32[]{:T(128)} %get-tuple-element.122, ...), channel_id=1, replica_groups=mesh['dp'=8,'tensor'=4] {'dp','tensor'}, use_global_device_ids=true, to_apply=%region_7.8 | all-reduce | flops 9217 | bytes 73736 | tf_op jit(solution)/shard_map/psum | solution.py:379
  455.0 1.1 copy.137
  458.3 47.0 %reduce-scatter.7.cloned.1.call-done = bf16[512,768]{1,0:T(8,128)(2,1)} async-done(((bf16[2048,768]{1,0:T(8,128)(2,1)}), bf16[512,768]{1,0:T(8,128)(2,1)}) %reduce-scatter.7.cloned.1.call-update) | async-done | bytes 786448 | tf_op jit(solution)/shard_map/reduce_scatter | solution.py:369
  505.3 2.4 add_bitcast_fusion
  507.8 32.3 %reduce-scatter.11.cloned.1.call-done = bf16[1,96,1728]{2,1,0:T(8,128)(2,1)} async-done(((bf16[4,96,1728]{2,1,0:T(8,128)(2,1)}), bf16[1,96,1728]{2,1,0:T(8,128)(2,1)}) %reduce-scatter.11.cloned.1.call-update) | async-done | bytes 331792 | tf_op jit(solution)/shard_map/reduce_scatter | solution.py:364
  540.1 1.0 bitcast_convert_fusion
  (119 shorter events, 14.0 us)
Async XLA Ops:
  7.2 4.7 copy-start.12
  7.2 4.8 copy-start.10
  7.2 4.8 copy-start.11
  7.2 30.8 %all-gather.6.cloned.1.call-start = ((), (), s32[]{:S(2)}) async-start(), calls=%async_computation.6 | async-start | bytes 1327104 | tf_op jit(solution)/shard_map/all_gather | solution.py:291
  10.2 2.7 copy-start
  11.1 92.0 %all-gather.8.cloned.1.call-start = ((), (), s32[]{:S(2)}) async-start(), calls=%async_computation.10 | async-start | bytes 3932160 | tf_op jit(solution)/shard_map/all_gather | solution.py:290
  11.9 210.4 %all-gather.10.cloned.1.call-start = ((), (), s32[]{:S(2)}) async-start(), calls=%async_computation.11 | async-start | bytes 11354112 | tf_op jit(solution)/shard_map/all_gather | solution.py:293
  108.0 40.9 %copy-start.3 = (bf16[2048,768]{1,0:T(8,128)(2,1)}, bf16[2048,768]{1,0:T(8,128)(2,1)S(1)}, u32[]{:S(2)}) copy-start(bf16[2048,768]{1,0:T(8,128)(2,1)S(1)} %fusion.8.qkv_ref) | copy-start | bytes 9437188
  148.9 4.9 copy-start.13
  148.9 72.6 %copy-start.15 = (bf16[768]{0:T(1024)(128)(2,1)S(1)}, bf16[768]{0:T(1024)(128)(2,1)}, u32[]{:S(2)}) copy-start(bf16[768]{0:T(1024)(128)(2,1)} %param.33) | copy-start | bytes 4612
  148.9 72.6 %copy-start.16 = (bf16[768]{0:T(1024)(128)(2,1)S(1)}, bf16[768]{0:T(1024)(128)(2,1)}, u32[]{:S(2)}) copy-start(bf16[768]{0:T(1024)(128)(2,1)} %param.36) | copy-start | bytes 4612
  148.9 72.6 %copy-start.17 = (bf16[768]{0:T(1024)(128)(2,1)S(1)}, bf16[768]{0:T(1024)(128)(2,1)}, u32[]{:S(2)}) copy-start(bf16[768]{0:T(1024)(128)(2,1)} %param.37) | copy-start | bytes 4612
  148.9 72.6 %copy-start.14 = (bf16[3072]{0:T(1024)(128)(2,1)S(1)}, bf16[3072]{0:T(1024)(128)(2,1)}, u32[]{:S(2)}) copy-start(bf16[3072]{0:T(1024)(128)(2,1)} %param.34) | copy-start | bytes 18436
  149.0 72.6 %copy-start.18 = (bf16[768]{0:T(1024)(128)(2,1)S(1)}, bf16[768]{0:T(1024)(128)(2,1)}, u32[]{:S(2)}) copy-start(bf16[768]{0:T(1024)(128)(2,1)} %param.35) | copy-start | bytes 4612
  149.0 72.6 %copy-start.19 = (bf16[768]{0:T(1024)(128)(2,1)S(1)}, bf16[768]{0:T(1024)(128)(2,1)}, u32[]{:S(2)}) copy-start(bf16[768]{0:T(1024)(128)(2,1)} %param.38) | copy-start | bytes 4612
  149.0 72.6 %copy-start.20 = (bf16[768]{0:T(1024)(128)(2,1)S(1)}, bf16[768]{0:T(1024)(128)(2,1)}, u32[]{:S(2)}) copy-start(bf16[768]{0:T(1024)(128)(2,1)} %param.39) | copy-start | bytes 4612
  150.2 104.1 %all-to-all-start = ((bf16[4,512,192]{1,2,0:T(8,128)(2,1)}), bf16[4,512,192]{1,2,0:T(8,128)(2,1)S(1)}, u32[]{:S(2)}, u32[]{:S(2)}) async-start(bf16[4,512,192]{1,2,0:T(8,128)(2,1)} %copy.120), calls=%async_computation | async-start | bytes 1572864 | tf_op jit(solution)/shard_map/all_to_all | solution.py:316
  153.7 249.3 %reduce-scatter.9.cloned.1.call-start = ((), (), s32[]{:S(2)}) async-start(), calls=%async_computation.8 | async-start | bytes 12386304 | tf_op jit(solution)/shard_map/reduce_scatter | solution.py:363
  254.3 2.9 copy-start.5
  257.2 2.2 slice-start
  257.3 2.2 slice-start.1
  266.7 1.1 copy-start.8
  266.7 1.4 copy-start.9
  280.3 1.7 copy-start.22
  295.9 1.1 copy-start.6
  310.8 144.2 %reduce-scatter.13.cloned.1.call-start = ((), (), s32[]{:S(2)}) async-start(), calls=%async_computation.12 | async-start | bytes 1327104
  340.6 1.9 copy-start.4
  342.5 48.6 %copy-start.21 = (bf16[1,2048,768]{2,1,0:T(8,128)(2,1)S(1)}, bf16[1,2048,768]{2,1,0:T(8,128)(2,1)}, u32[]{:S(2)}) copy-start(bf16[1,2048,768]{2,1,0:T(8,128)(2,1)} %all-gather.8.cloned.1.call-done) | copy-start | bytes 9437188
  389.4 1.8 copy-start.1
  394.9 2.6 copy-start.2
  397.5 107.8 %reduce-scatter.7.cloned.1.call-start = ((), (), s32[]{:S(2)}) async-start(), calls=%async_computation.7 | async-start | bytes 3932160 | tf_op jit(solution)/shard_map/reduce_scatter | solution.py:369
  402.9 102.4 %copy-start.7 = (f32[512,768]{1,0:T(8,128)S(1)}, f32[512,768]{1,0:T(8,128)}, u32[]{:S(2)}) copy-start(f32[512,768]{1,0:T(8,128)} %copy-done.6) | copy-start | bytes 4718596
  403.0 137.1 %reduce-scatter.11.cloned.1.call-start = ((), (), s32[]{:S(2)}) async-start(), calls=%async_computation.9 | async-start | bytes 1720320 | tf_op jit(solution)/shard_map/reduce_scatter | solution.py:364
Sparse Core Ops, SparseCore 0:
  11.2 26.7 all-gather.5
  39.6 63.4 all-gather.7
  106.5 101.5 all-gather.9
  310.9 85.4 reduce-scatter.8
  399.5 43.2 reduce-scatter.12
  445.1 60.2 reduce-scatter.6
  507.7 32.2 reduce-scatter.10

commit v2 on v1

v2 whole, which is shorter than its diff:
```python
import functools

import jax
import jax.numpy as jnp
from jax import lax
from jax.experimental import pallas as pl
from jax.experimental.pallas import tpu as pltpu
from jax.sharding import PartitionSpec as P

DH = 64
BLOCK = 256
SLAB = 4 * DH
EPSILON = 1e-12
ROOT_HALF = 0.7071067811865476
INV_ROOT_TAU = 0.3989422804014327
LOG2E = 1.4426950408889634
LN2 = 0.6931471805599453
SCALE = DH ** (-0.5)
MASKED = -1e30

BF16 = jnp.bfloat16
F32 = jnp.float32
NN = (((1,), (0,)), ((), ()))
NT = (((1,), (1,)), ((), ()))
TN = (((0,), (0,)), ((), ()))


def dot(left_side, right_side, dims=NN):
    return lax.dot_general(left_side, right_side, dims, preferred_element_type=F32)


def norm_forward(summed, gain_vec, shift_vec):
    average = jnp.mean(summed, axis=-1, keepdims=True)
    centered = summed - average
    variance = jnp.mean(centered * centered, axis=-1, keepdims=True)
    inverse = lax.rsqrt(variance + EPSILON)
    normed = centered * inverse
    return (normed * gain_vec + shift_vec, normed, inverse)


def norm_backward(upstream, normed, inverse, gain_vec):
    scaled = upstream * gain_vec
    first_mean = jnp.mean(scaled, axis=-1, keepdims=True)
    second_mean = jnp.mean(scaled * normed, axis=-1, keepdims=True)
    return inverse * (scaled - first_mean - normed * second_mean)


def column_sum(value):
    return jnp.sum(value, axis=0, keepdims=True)


def lane_is_right(rows):
    return lax.broadcasted_iota(jnp.int32, (rows, 2 * DH), 1) >= DH


def attend_forward(low_ref, high_ref, qkv_ref, seg_col_ref, seg_row_ref, ctx_ref, lse_ref, held):
    heads = lse_ref.shape[0]
    qb = pl.program_id(0)
    rows = pl.ds(pl.multiple_of(qb * BLOCK, BLOCK), BLOCK)
    seg_q = seg_col_ref[...]
    queries = [
        qkv_ref[rows, SLAB * h : SLAB * h + 2 * DH] * jnp.asarray(SCALE, BF16) for h in range(heads)
    ]
    low, high = low_ref[qb], high_ref[qb]

    def score(kb, peaks):
        keys = pl.ds(pl.multiple_of(kb * BLOCK, BLOCK), BLOCK)
        allowed = seg_q == seg_row_ref[:, keys]
        found = []
        for h in range(heads):
            scores = dot(queries[h], qkv_ref[keys, SLAB * h + 2 * DH : SLAB * (h + 1)], NT)
            scores = jnp.where(allowed, scores, MASKED)
            held[h, kb] = scores
            found.append(jnp.maximum(peaks[h], jnp.maximum(scores[:, :128], scores[:, 128:])))
        return tuple(found)

    start = tuple(jnp.full((BLOCK, 128), MASKED, F32) for _ in range(heads))
    peaks = lax.fori_loop(low, high, score, start)
    highest = [jnp.max(peak, axis=-1, keepdims=True) for peak in peaks]

    def weigh(kb, carry):
        keys = pl.ds(pl.multiple_of(kb * BLOCK, BLOCK), BLOCK)
        found = []
        for h in range(heads):
            total, acc = carry[h]
            raised = jnp.exp2((held[h, kb] - highest[h]) * LOG2E)
            total = total + (raised[:, :128] + raised[:, 128:])
            acc = acc + dot(raised.astype(BF16), qkv_ref[keys, SLAB * h + 2 * DH : SLAB * (h + 1)])
            found.append((total, acc))
        return tuple(found)

    zero = jnp.zeros((BLOCK, 128), F32)
    done = lax.fori_loop(low, high, weigh, tuple((zero, zero) for _ in range(heads)))
    right = lane_is_right(BLOCK)
    values = []
    for h in range(heads):
        total, acc = done[h]
        summed = jnp.sum(total, axis=-1, keepdims=True)
        values.append((acc / summed).astype(BF16))
        lse_ref[h] = jnp.transpose(highest[h] + jnp.log(summed))
    for h in range(0, heads, 2):
        moved = pltpu.roll(values[h], DH, 1)
        if h + 1 < heads:
            ctx_ref[:, DH * h : DH * (h + 2)] = jnp.where(right, values[h + 1], moved)
        else:
            ctx_ref[:, DH * h : DH * (h + 1)] = moved[:, :DH]


def attend_backward(
    low_ref, high_ref, qkv_ref, seg_col_ref, seg_row_ref, ctx_ref, grad_ref, lse_ref,
    out_ref, sums_ref, dkv
):
    heads = lse_ref.shape[0]
    qb = pl.program_id(0)

    @pl.when(qb == 0)
    def _():
        dkv[...] = jnp.zeros_like(dkv)
        sums_ref[...] = jnp.zeros_like(sums_ref)

    rows = pl.ds(pl.multiple_of(qb * BLOCK, BLOCK), BLOCK)
    right = lane_is_right(BLOCK)
    product = grad_ref[...].astype(F32) * ctx_ref[...].astype(F32)
    upper = product.astype(BF16)
    lower = (product - upper.astype(F32)).astype(BF16)
    width = heads * DH
    choose = (
        lax.broadcasted_iota(jnp.int32, (8, width), 1) // DH
        == lax.broadcasted_iota(jnp.int32, (8, width), 0)
    ).astype(BF16)
    deltas = dot(choose, upper, NT) + dot(choose, lower, NT)
    queries, grads, pairs = [], [], []
    for h in range(heads):
        queries.append(qkv_ref[rows, SLAB * h : SLAB * h + 2 * DH] * jnp.asarray(SCALE, BF16))
        tile = DH * (h - h % 2)
        if tile + 2 * DH <= width:
            grad = grad_ref[:, tile : tile + 2 * DH]
        else:
            grad = grad_ref[:, tile : tile + DH]
            grad = jnp.concatenate([grad, jnp.zeros_like(grad)], axis=1)
        if h % 2 == 0:
            grad = pltpu.roll(grad, DH, 1)
        grad = jnp.where(right, grad, jnp.zeros_like(grad))
        grads.append(grad)
        pairs.append(jnp.concatenate([queries[h], grad], axis=0))
    seg_q = seg_row_ref[...]
    lses = [lse_ref[h] for h in range(heads)]
    low, high = low_ref[qb], high_ref[qb]

    def step(kb, accs):
        keys = pl.ds(pl.multiple_of(kb * BLOCK, BLOCK), BLOCK)
        allowed = seg_col_ref[keys, :] == seg_q
        found = []
        for h in range(heads):
            pair = qkv_ref[keys, SLAB * h + 2 * DH : SLAB * (h + 1)]
            scores = jnp.where(allowed, dot(pair, queries[h], NT), MASKED)
            probs = jnp.exp2((scores - lses[h]) * LOG2E)
            score_grad = (probs * (dot(pair, grads[h], NT) - deltas[h : h + 1, :])).astype(BF16)
            both = jnp.concatenate([score_grad, probs.astype(BF16)], axis=1)
            dkv[h, keys, :] += dot(both, pairs[h])
            found.append(accs[h] + dot(score_grad, pair, TN))
        return tuple(found)

    zero = jnp.zeros((BLOCK, 128), F32)
    accs = lax.fori_loop(low, high, step, tuple(zero for _ in range(heads)))
    for h in range(heads):
        query_grad = jnp.where(right, 0.0, accs[h] * SCALE).astype(BF16)
        out_ref[rows, SLAB * h : SLAB * h + 2 * DH] = query_grad
        sums_ref[:, SLAB * h : SLAB * h + 2 * DH] += column_sum(query_grad.astype(F32))

    @pl.when(qb == pl.num_programs(0) - 1)
    def _():
        for h in range(heads):
            pair_grad = dkv[h].astype(BF16)
            out_ref[:, SLAB * h + 2 * DH : SLAB * (h + 1)] = pair_grad
            sums_ref[:, SLAB * h + 2 * DH : SLAB * (h + 1)] = column_sum(pair_grad.astype(F32))


def document_blocks(segment_row):
    starts = segment_row[::BLOCK]
    stops = segment_row[BLOCK - 1 :: BLOCK]
    low = jnp.sum((segment_row[None, :] < starts[:, None]).astype(jnp.int32), axis=1)
    high = jnp.sum((segment_row[None, :] <= stops[:, None]).astype(jnp.int32), axis=1)
    return (low // BLOCK, (high + BLOCK - 1) // BLOCK)


def run_forward(bounds, qkv, seg_col, seg_row):
    seq_len, width = qkv.shape
    heads = width // SLAB
    blocks = seq_len // BLOCK
    return pl.pallas_call(
        attend_forward,
        out_shape=(
            jax.ShapeDtypeStruct((seq_len, heads * DH), BF16),
            jax.ShapeDtypeStruct((heads, 1, seq_len), F32),
        ),
        grid_spec=pltpu.PrefetchScalarGridSpec(
            num_scalar_prefetch=2,
            grid=(blocks,),
            in_specs=[
                pl.BlockSpec((seq_len, width), lambda q, *_: (0, 0), pipeline_mode=pl.Buffered(1)),
                pl.BlockSpec((BLOCK, 1), lambda q, *_: (q, 0)),
                pl.BlockSpec((1, seq_len), lambda q, *_: (0, 0)),
            ],
            out_specs=(
                pl.BlockSpec((BLOCK, heads * DH), lambda q, *_: (q, 0)),
                pl.BlockSpec((heads, 1, BLOCK), lambda q, *_: (0, 0, q)),
            ),
            scratch_shapes=[pltpu.VMEM((heads, blocks, BLOCK, BLOCK), F32)],
        ),
        compiler_params=pltpu.CompilerParams(
            dimension_semantics=("arbitrary",), vmem_limit_bytes=40 << 20
        ),
        cost_estimate=pl.CostEstimate(
            flops=heads * seq_len * seq_len * 256,
            bytes_accessed=5 << 20,
            transcendentals=heads * seq_len * seq_len // 3,
        ),
        name="attend_forward",
    )(*bounds, qkv, seg_col, seg_row)


def run_backward(bounds, qkv, seg_col, seg_row, ctx, grad, lse):
    seq_len, width = qkv.shape
    heads = width // SLAB
    return pl.pallas_call(
        attend_backward,
        out_shape=(
            jax.ShapeDtypeStruct((seq_len, width), BF16),
            jax.ShapeDtypeStruct((1, width), F32),
        ),
        grid_spec=pltpu.PrefetchScalarGridSpec(
            num_scalar_prefetch=2,
            grid=(seq_len // BLOCK,),
            in_specs=[
                pl.BlockSpec((seq_len, width), lambda q, *_: (0, 0), pipeline_mode=pl.Buffered(1)),
                pl.BlockSpec((seq_len, 1), lambda q, *_: (0, 0)),
                pl.BlockSpec((1, BLOCK), lambda q, *_: (0, q)),
                pl.BlockSpec((BLOCK, heads * DH), lambda q, *_: (q, 0)),
                pl.BlockSpec((BLOCK, heads * DH), lambda q, *_: (q, 0)),
                pl.BlockSpec((heads, 1, BLOCK), lambda q, *_: (0, 0, q)),
            ],
            out_specs=(
                pl.BlockSpec((seq_len, width), lambda q, *_: (0, 0)),
                pl.BlockSpec((1, width), lambda q, *_: (0, 0)),
            ),
            scratch_shapes=[pltpu.VMEM((heads, seq_len, 2 * DH), F32)],
        ),
        compiler_params=pltpu.CompilerParams(
            dimension_semantics=("arbitrary",), vmem_limit_bytes=40 << 20
        ),
        cost_estimate=pl.CostEstimate(
            flops=heads * seq_len * seq_len * 640,
            bytes_accessed=10 << 20,
            transcendentals=heads * seq_len * seq_len // 3,
        ),
        name="attend_backward",
    )(*bounds, qkv, seg_col, seg_row, ctx, grad, lse)


ROWS = 256


def dense_chain(
    ratio_ref, ctx_ref, in_ref, teacher_ref, cotangent_ref, valid_ref, vec_ref, inner_bias_ref, w_ref,
    layer_ref, first_grad_ref, ctx_grad_ref, first_ref, branch_grad_ref, attn_grad_ref,
    act_ref, hidden_grad_ref, sums_ref, inner_sums_ref,
    w_out, w_in, w_up, slope, sems
):
    parts, _, head_cols = w_out.shape
    hidden_cols = w_in.shape[2]
    step = pl.program_id(0)

    def fetch(which, t):
        start, size, target = (
            (2 * hidden_cols, head_cols, w_out),
            (0, hidden_cols, w_in),
            (hidden_cols, hidden_cols, w_up),
        )[which]
        return pltpu.make_async_copy(
            w_ref.at[t, :, pl.ds(start, size)], target.at[t], sems.at[which, t]
        )

    @pl.when(step == 0)
    def _():
        for which in range(3):
            for t in range(parts):
                fetch(which, t).start()
        sums_ref[...] = jnp.zeros_like(sums_ref)
        inner_sums_ref[...] = jnp.zeros_like(inner_sums_ref)

    def arrive(which, t):
        @pl.when(step == 0)
        def _():
            fetch(which, t).wait()

    def vec(which):
        return vec_ref[which : which + 1, :]

    rows = in_ref.shape[0]
    width = in_ref.shape[1]
    zero = jnp.zeros((rows, width), F32)
    attention = zero
    for t in range(parts):
        arrive(0, t)
        attention = attention + dot(ctx_ref[t], w_out[t], NT)
    first_exact, normed_one, inverse_one = norm_forward(
        in_ref[...].astype(F32) + attention + vec(0), vec(1), vec(2)
    )
    first = first_exact.astype(BF16)
    first_ref[...] = first

    def up(t, branch):
        arrive(1, t)
        hidden = dot(first, w_in[t]) + inner_bias_ref[t]
        bend = 0.5 * (1.0 + lax.erf(hidden * ROOT_HALF))
        activated = (hidden * bend).astype(BF16)
        act_ref[t] = activated
        slope[t] = bend + hidden * INV_ROOT_TAU * jnp.exp2(hidden * hidden * (-0.5 * LOG2E))
        arrive(2, t)
        return branch + dot(activated, w_up[t], NT)

    branch = lax.fori_loop(0, parts, up, zero)
    layer_rows, normed_two, inverse_two = norm_forward(first.astype(F32) + branch + vec(3), vec(4), vec(5))
    layer_ref[...] = layer_rows.astype(BF16)
    misfit = layer_rows - teacher_ref[...].astype(F32)
    weighted = valid_ref[...] * misfit
    out_grad = cotangent_ref[...].astype(F32) + weighted * ratio_ref[0]
    second_grad = norm_backward(out_grad, normed_two, inverse_two, vec(4))
    branch_grad = second_grad.astype(BF16)
    branch_grad_ref[...] = branch_grad
    sums_ref[0:1, :] += column_sum(weighted * misfit)
    sums_ref[1:2, :] += column_sum(branch_grad.astype(F32))
    sums_ref[2:3, :] += column_sum(out_grad * normed_two)
    sums_ref[3:4, :] += column_sum(out_grad)

    def down(t, back):
        hidden_grad = (dot(branch_grad, w_up[t]) * slope[t]).astype(BF16)
        hidden_grad_ref[t] = hidden_grad
        inner_sums_ref[t] += column_sum(hidden_grad.astype(F32))
        return back + dot(hidden_grad, w_in[t], NT)

    upstream = lax.fori_loop(0, parts, down, second_grad)
    first_grad = norm_backward(upstream, normed_one, inverse_one, vec(1))
    first_grad_ref[...] = first_grad
    attn_grad = first_grad.astype(BF16)
    attn_grad_ref[...] = attn_grad
    sums_ref[4:5, :] += column_sum(attn_grad.astype(F32))
    sums_ref[5:6, :] += column_sum(upstream * normed_one)
    sums_ref[6:7, :] += column_sum(upstream)
    for t in range(parts):
        ctx_grad_ref[t] = dot(attn_grad, w_out[t]).astype(BF16)


def run_dense(ratio, ctx, rows_in, teacher, cotangent, valid, vecs, inner_bias, weights):
    parts, part_len, head_cols = ctx.shape
    width = rows_in.shape[1]
    hidden_cols = inner_bias.shape[2]

    def by_rows(columns):
        return pl.BlockSpec((ROWS, columns), lambda i: (i, 0))

    def by_part(columns):
        return pl.BlockSpec((parts, ROWS, columns), lambda i: (0, i, 0))

    def fixed(shape):
        return pl.BlockSpec(shape, lambda i: (0,) * len(shape))

    low = jax.ShapeDtypeStruct((part_len, width), BF16)
    return pl.pallas_call(
        dense_chain,
        out_shape=(
            low,
            jax.ShapeDtypeStruct((part_len, width), F32),
            jax.ShapeDtypeStruct((parts, part_len, head_cols), BF16),
            low,
            low,
            low,
            jax.ShapeDtypeStruct((parts, part_len, hidden_cols), BF16),
            jax.ShapeDtypeStruct((parts, part_len, hidden_cols), BF16),
            jax.ShapeDtypeStruct((8, width), F32),
            jax.ShapeDtypeStruct((parts, 1, hidden_cols), F32),
        ),
        grid=(part_len // ROWS,),
        in_specs=[
            pl.BlockSpec(memory_space=pltpu.SMEM),
            by_part(head_cols),
            by_rows(width),
            by_rows(width),
            by_rows(width),
            by_rows(1),
            fixed(vecs.shape),
            fixed(inner_bias.shape),
            pl.BlockSpec(memory_space=pl.ANY),
        ],
        out_specs=(
            by_rows(width),
            by_rows(width),
            by_part(head_cols),
            by_rows(width),
            by_rows(width),
            by_rows(width),
            by_part(hidden_cols),
            by_part(hidden_cols),
            fixed((8, width)),
            fixed((parts, 1, hidden_cols)),
        ),
        scratch_shapes=[
            pltpu.VMEM((parts, width, head_cols), BF16),
            pltpu.VMEM((parts, width, hidden_cols), BF16),
            pltpu.VMEM((parts, width, hidden_cols), BF16),
            pltpu.VMEM((parts, ROWS, hidden_cols), F32),
            pltpu.SemaphoreType.DMA((3, parts)),
        ],
        compiler_params=pltpu.CompilerParams(
            dimension_semantics=("arbitrary",), vmem_limit_bytes=56 << 20
        ),
        cost_estimate=pl.CostEstimate(
            flops=part_len * width * (8 * hidden_cols + 4 * head_cols) * parts,
            bytes_accessed=24 << 20,
            transcendentals=2 * part_len * hidden_cols * parts,
        ),
        name="dense_chain",
    )(ratio, ctx, rows_in, teacher, cotangent, valid, vecs, inner_bias, weights)


def dense_weights(
    first_ref, branch_grad_ref, attn_grad_ref, act_ref, hidden_grad_ref, ctx_ref, out_ref, turned
):
    @pl.when(pl.program_id(0) == 0)
    def _():
        turned[0] = jnp.transpose(first_ref[...])
        turned[1] = jnp.transpose(branch_grad_ref[...])
        turned[2] = jnp.transpose(attn_grad_ref[...])

    hidden_cols = act_ref.shape[2]
    out_ref[0, :, :hidden_cols] = dot(turned[0], hidden_grad_ref[0]).astype(BF16)
    out_ref[0, :, hidden_cols : 2 * hidden_cols] = dot(turned[1], act_ref[0]).astype(BF16)
    out_ref[0, :, 2 * hidden_cols :] = dot(turned[2], ctx_ref[0]).astype(BF16)


def run_weights(first, branch_grad, attn_grad, act, hidden_grad, ctx):
    parts, part_len, hidden_cols = act.shape
    head_cols = ctx.shape[2]
    width = first.shape[1]
    columns = 2 * hidden_cols + head_cols

    def by_part(size):
        return pl.BlockSpec((1, part_len, size), lambda t: (t, 0, 0))

    whole = pl.BlockSpec((part_len, width), lambda t: (0, 0))
    return pl.pallas_call(
        dense_weights,
        out_shape=jax.ShapeDtypeStruct((parts, width, columns), BF16),
        grid=(parts,),
        in_specs=[
            whole, whole, whole, by_part(hidden_cols), by_part(hidden_cols), by_part(head_cols)
        ],
        out_specs=pl.BlockSpec((1, width, columns), lambda t: (t, 0, 0)),
        scratch_shapes=[pltpu.VMEM((3, width, part_len), BF16)],
        compiler_params=pltpu.CompilerParams(
            dimension_semantics=("arbitrary",), vmem_limit_bytes=40 << 20
        ),
        cost_estimate=pl.CostEstimate(
            flops=2 * part_len * width * columns * parts, bytes_accessed=20 << 20, transcendentals=0
        ),
        name="dense_weights",
    )(first, branch_grad, attn_grad, act, hidden_grad, ctx)


def interleave(query, key, value, heads):
    rows = query.shape[0]
    parts = [part.reshape(rows, heads, 1, DH) for part in (query, jnp.zeros_like(query), key, value)]
    return jnp.concatenate(parts, axis=2).reshape(rows, heads * SLAB)


def place_slice(local_grad, full_size, offset):
    return lax.dynamic_update_slice_in_dim(jnp.zeros((full_size,), F32), local_grad, offset, 0)


def swap(value, axis, bit):
    size = lax.axis_size(axis)
    return lax.ppermute(value, axis, [(i, i ^ bit) for i in range(size)])


def bits_of(axis):
    bit = 1
    while bit < lax.axis_size(axis):
        yield bit
        bit *= 2


def sum_everywhere(value):
    for axis in ("dp", "tensor"):
        for bit in bits_of(axis):
            value = value + swap(value, axis, bit)
    return value


def gather_rows(shard):
    held = shard
    index = lax.axis_index("dp")
    for bit in bits_of("dp"):
        other = swap(held, "dp", bit)
        mine_first = (index & bit) == 0
        held = jnp.where(
            mine_first,
            jnp.concatenate([held, other], axis=0),
            jnp.concatenate([other, held], axis=0),
        )
    return held


def scatter_rows(value):
    copies = lax.axis_size("dp")
    index = lax.axis_index("dp")
    held = value.reshape((copies,) + (value.shape[0] // copies,) + value.shape[1:])
    for bit in bits_of("dp"):
        held = held.reshape((held.shape[0] // 2, 2) + held.shape[1:])
        own = (index & bit) // bit
        keep = lax.dynamic_index_in_dim(held, own, 1, keepdims=False)
        send = lax.dynamic_index_in_dim(held, 1 - own, 1, keepdims=False)
        came = swap(send, "dp", bit)
        held = (keep.astype(F32) + came.astype(F32)).astype(BF16)
    return held[0]


def local(
    inputs, segment_ids, valid_mask, teacher, cotangent,
    w_query, w_key, w_value, w_output, w_inner, w_outer,
    query_bias, value_bias, output_bias, inner_bias, outer_bias,
    gain_attn, shift_attn, gain_ffn, shift_ffn,
):
    _, part_len, width = inputs.shape
    parts = lax.axis_size("tensor")
    copies = lax.axis_size("dp")
    rank = lax.axis_index("tensor")
    total_tokens = part_len * parts * copies
    seq_len = part_len * parts
    head_cols = w_query.shape[1]
    heads = head_cols // DH
    hidden_cols = w_inner.shape[1]
    shard_rows = w_inner.shape[0]

    rows_in = inputs.reshape(part_len, width)
    tokens = lax.all_gather(rows_in, "tensor", axis=0, tiled=True)
    w_heads = gather_rows(interleave(w_query, w_key, w_value, heads))
    mine = jnp.concatenate((w_inner, w_outer.T, w_output.T), axis=1)
    mine, tokens_first = lax.optimization_barrier((mine, rows_in))
    weights = lax.all_gather(mine, ("tensor", "dp"), axis=0, tiled=False)
    weights = weights.reshape(parts, width, 2 * hidden_cols + head_cols)

    valid_rows = valid_mask.astype(F32).reshape(part_len, 1)
    counted = sum_everywhere(jnp.sum(valid_rows).reshape(1, 1))

    mine_cols = rank * head_cols
    query_shift = lax.dynamic_slice_in_dim(query_bias, mine_cols, head_cols).astype(F32)
    value_shift = lax.dynamic_slice_in_dim(value_bias, mine_cols, head_cols).astype(F32)
    shifts = interleave(query_shift[None], jnp.zeros_like(query_shift)[None], value_shift[None], heads)
    qkv = (dot(tokens, w_heads) + shifts).astype(BF16)

    segment_row = segment_ids.reshape(seq_len)
    bounds = document_blocks(segment_row)
    seg_col = segment_row.reshape(seq_len, 1)
    seg_row = segment_row.reshape(1, seq_len)
    context, lse = run_forward(bounds, qkv, seg_col, seg_row)
    context_parts = lax.all_to_all(context.reshape(parts, part_len, head_cols), "tensor", 0, 0)

    vecs = jnp.stack(
        (output_bias, gain_attn, shift_attn, outer_bias, gain_ffn, shift_ffn, outer_bias, outer_bias)
    ).astype(F32)
    ratio = (total_tokens / counted).reshape(1)
    (
        layer_out, first_grad, context_grad, first, branch_grad, attn_grad, activated, hidden_grad,
        dense_sums, inner_sums,
    ) = run_dense(
        ratio, context_parts, rows_in, teacher.reshape(part_len, width), cotangent.reshape(part_len, width),
        valid_rows, vecs, inner_bias.astype(F32).reshape(parts, 1, hidden_cols), weights,
    )
    head_grad = lax.all_to_all(context_grad, "tensor", 0, 0).reshape(seq_len, head_cols)
    packed = run_weights(first, branch_grad, attn_grad, activated, hidden_grad, context_parts)
    packed = lax.psum_scatter(packed, "dp", scatter_dimension=1, tiled=True)
    packed = lax.psum_scatter(packed, "tensor", scatter_dimension=0, tiled=True)
    packed = packed.reshape(shard_rows, -1).astype(F32)

    joined_grad, sums = run_backward(bounds, qkv, seg_col, seg_row, context, head_grad, lse)
    attn_back = dot(joined_grad, w_heads, NT).astype(BF16)
    attn_back = lax.psum_scatter(attn_back, "tensor", scatter_dimension=0, tiled=True)
    input_grad = first_grad + attn_back.astype(F32)
    head_weights = scatter_rows(dot(tokens, joined_grad, TN).astype(BF16))
    head_weights = head_weights.astype(F32).reshape(shard_rows, heads, 4, DH)

    def pick(which):
        return head_weights[:, :, which, :].reshape(shard_rows, head_cols)

    sums = sums.reshape(heads, 4, DH)
    totals = sum_everywhere(
        jnp.concatenate(
            (
                place_slice(sums[:, 0].reshape(head_cols), width, mine_cols),
                place_slice(sums[:, 3].reshape(head_cols), width, mine_cols),
                dense_sums.reshape(-1),
                inner_sums.reshape(-1),
            )
        ).reshape(-1, 128)
    ).reshape(-1)

    def total(which):
        return totals[which * width : (which + 1) * width]

    mse_loss = jnp.sum(total(2)) / (counted[0, 0] * width)
    return (
        layer_out.reshape(1, part_len, width),
        mse_loss,
        input_grad.reshape(1, part_len, width),
        pick(0),
        pick(2),
        pick(3),
        packed[:, 2 * hidden_cols :].T,
        packed[:, :hidden_cols],
        packed[:, hidden_cols : 2 * hidden_cols].T,
        total(0),
        total(1),
        total(6),
        totals[10 * width :],
        total(3),
        total(7),
        total(8),
        total(4),
        total(5),
    )


def solution(mesh):
    shard = P("dp", "tensor", None)
    in_specs = (
        (shard, P("dp", None), P("dp", "tensor"), shard, shard)
        + (P("dp", "tensor"),) * 3
        + (P("tensor", "dp"), P("dp", "tensor"), P("tensor", "dp"))
        + (P(),) * 9
    )
    out_specs = (
        (shard, P(), shard)
        + (P("dp", "tensor"),) * 3
        + (P("tensor", "dp"), P("dp", "tensor"), P("tensor", "dp"))
        + (P(),) * 9
    )
    return jax.shard_map(local, mesh=mesh, in_specs=in_specs, out_specs=out_specs, check_vma=False)
```

time: 562 us -> 416 us (0.74); the launches traced: 551 us -> 416 us
  blocking collectives: 140 us -> 23.9 us
  local copies, waits for them, and re-layouts: 67.2 us -> 29.8 us
  starting transfers between devices: 3.78 us -> 35.7 us
  matrix products: 44.4 us -> 13.3 us
  Pallas kernels: 87.8 us -> 109 us
  other arithmetic: 20.9 us -> 10.6 us
    psum x2 -> x0, blocking collectives: 116 us -> none  [the longest x1 67.1 us: local(): counted = lax.psum(jnp.sum(valid_rows), ('dp', 'tensor'))]
    ppermute x0 -> x16, waiting for transfers between devices: none -> 44.4 us  [swap(): return lax.ppermute(value, axis, [(i, i ^ bit) for i in range(size)])]
    pallas_call x0 -> x2, Pallas kernels: none -> 38.8 us  [the longest x1 30.1 us: run_dense(): pl.pallas_call(dense_chain, out_shape=(low, jax.ShapeDtypeStruct((part_le...]
    all_gather x1, waiting for transfers between devices: 65.1 us -> 32.4 us  [local(): tokens = lax.all_gather(rows_in, 'tensor', axis=0, tiled=True)]
    ppermute x0 -> x16, starting transfers between devices: none -> 31.6 us  [swap(): return lax.ppermute(value, axis, [(i, i ^ bit) for i in range(size)])]
    dot_general x12 -> x3, matrix products: 44.4 us -> 13.3 us  [dot(): lax.dot_general(left_side, right_side, dims, preferred_element_type=F32)]
    reshape x7 -> x3, local copies, waits for them, and re-layouts: 27.6 us -> 2.11 us  [the longest x1 1.24 us: local(): context.reshape(parts, part_len, head_cols)]
    reduce_scatter x1, waiting for transfers between devices: 47 us -> 28.7 us  [local(): lax.psum_scatter(attn_back, 'tensor', scatter_dimension=0, tiled=True)]
  transfers between devices with their start and end apart: 8 -> 22, of which waited for: 4 -> 16; matrix products, arithmetic and copies ran while one was open for 12% -> 9% of each run, Pallas kernels for 16% -> 17%
where the time goes in v2:
time: 416 us
  waiting for transfers between devices  174 us (42%)
  Pallas kernels  109 us (26%)
  starting transfers between devices  35.7 us (9%)
  local copies, waits for them, and re-layouts  29.8 us (7%)
  blocking collectives  23.9 us (6%)
  between operations  20 us (5%)
  matrix products  13.3 us (3%)
  other arithmetic  10.6 us (3%)
    ppermute x16, waiting for transfers between devices, swap(): return lax.ppermute(value, axis, [(i, i ^ bit) for i in range(size)])  44.4 us
    pallas_call x1, Pallas kernels, run_backward(): pl.pallas_call(attend_backward, out_shape=(jax.ShapeDtypeStruct((seq_len,...  41.4 us
    all_gather x1, waiting for transfers between devices, local(): weights = lax.all_gather(mine, ('tensor', 'dp'), axis=0, tiled=False)  35.4 us
    all_gather x1, waiting for transfers between devices, local(): tokens = lax.all_gather(rows_in, 'tensor', axis=0, tiled=True)  32.4 us
    reduce_scatter x1, waiting for transfers between devices, local(): packed = lax.psum_scatter(packed, 'tensor', scatter_dimension=0, tiled=True)  32 us
    ppermute x16, starting transfers between devices, swap(): return lax.ppermute(value, axis, [(i, i ^ bit) for i in range(size)])  31.6 us
    pallas_call x1, Pallas kernels, run_dense(): pl.pallas_call(dense_chain, out_shape=(low, jax.ShapeDtypeStruct((part_le...  30.1 us
    pallas_call x1, Pallas kernels, run_forward(): pl.pallas_call(attend_forward, out_shape=(jax.ShapeDtypeStruct((seq_len,...  29 us
  transfers between devices with their start and end apart: 22, of which 16 were waited for; matrix products, arithmetic and copies ran while one was open for 9% of the time, Pallas kernels for 17%

profile of v2, /device:TPU:0, one launch (start us, length us, event | category | flops | bytes accessed | tf_op | source)
XLA Modules:
  0.0 416.2 jit_solution(11449360454504776877)
XLA Ops:
  8.9 1.7 pad_maximum_fusion
  14.1 1.1 collective-permute-done.5
  15.5 2.9 collective-permute-start.6
  18.5 9.4 %collective-permute-done.6 = bf16[192,768]{0,1:T(8,128)(2,1)S(1)} collective-permute-done((bf16[192,768]{0,1:T(8,128)(2,1)S(1)}, bf16[192,768]{0,1:T(8,128)(2,1)S(1)}, u32[]{:S(2)}, u32[]{:S(2)}) %collective-permute-start.6) | collective-permute-done | bytes 294944 | tf_op jit(solution)/shard_map/ppermute | solution.py:483
  28.4 1.8 collective-permute-start.7
  32.2 11.2 %collective-permute-done.7 = bf16[384,768]{0,1:T(8,128)(2,1)S(1)} collective-permute-done((bf16[384,768]{0,1:T(8,128)(2,1)S(1)}, bf16[384,768]{0,1:T(8,128)(2,1)S(1)}, u32[]{:S(2)}, u32[]{:S(2)}) %collective-permute-start.7) | collective-permute-done | bytes 589856 | tf_op jit(solution)/shard_map/ppermute | solution.py:483
  43.4 32.4 %all-gather.5.cloned.1.call-done = bf16[1,2048,768]{2,1,0:T(8,128)(2,1)} async-done(((bf16[1,512,768]{2,1,0:T(8,128)(2,1)}), bf16[1,2048,768]{2,1,0:T(8,128)(2,1)}) %all-gather.5.cloned.1.call-update) | async-done | bytes 3145744 | tf_op jit(solution)/shard_map/all_gather | solution.py:546
  75.8 4.6 %fusion.3.qkv_ref = bf16[2048,768]{1,0:T(8,128)(2,1)S(1)} fusion(f32[768]{0:T(1024)S(1)} %add.104, bf16[1,2048,768]{2,1,0:T(8,128)(2,1)} %all-gather.5.cloned.1.call-done, bf16[384,768]{0,1:T(8,128)(2,1)S(1)} %collective-permute-done.7, bf16[384,768]{0,1:T(8,128)(2,1)S(1)} %maximum_select_fusion.1, pred[]{:T(512)S(6)} %eq.9), kind=kOutput, calls=%fused_computation.5 | convolution fusion | flops 2424373248 | bytes 7474177 | tf_op jit(solution)/shard_map/dot_general | solution.py:29
  80.4 29.0 %attend_forward.1 = (bf16[2048,192]{1,0:T(8,128)(2,1)S(1)}, f32[3,1,2048]{2,1,0:T(1,128)S(1)}) custom-call(s32[8]{0:T(128)S(1)} %get-tuple-element.157.low_ref, s32[8]{0:T(128)S(1)} %get-tuple-element.156.high_ref, bf16[2048,768]{1,0:T(8,128)(2,1)S(1)} %fusion.3.qkv_ref, s32[2048,1]{1,0:T(8,128)S(1)} %copy.94.seg_col_ref, s32[1,2048]{1,0:T(1,128)S(1)} %copy-done.6), custom_call_target="tpu_custom_call" | custom-call | flops 3221225472 | bytes 5242880 | tf_op jit(solution)/shard_map/attend_forward/pallas_call | solution.py:191
  109.6 1.2 copy.95
  110.8 3.5 all-to-all-start
  118.7 2.9 collective-permute-start.1
  123.1 3.9 collective-permute-start.2
  127.9 5.8 %collective-permute-start.3 = (f32[1,1]{1,0:T(1,128)}, f32[1,1]{1,0:T(1,128)}, u32[]{:S(2)}, u32[]{:S(2)}) collective-permute-start(f32[1,1]{1,0:T(1,128)} %add.100), channel_id=1, source_target_pairs={{0,1},{1,0},{2,3},{3,2},{4,5},{5,4},{6,7},{7,6},{8,9},{9,8},{10,11... | collective-permute-start | bytes 20 | tf_op jit(solution)/shard_map/ppermute | solution.py:483
  134.3 5.9 %collective-permute-start.4 = (f32[1,1]{1,0:T(1,128)}, f32[1,1]{1,0:T(1,128)}, u32[]{:S(2)}, u32[]{:S(2)}) collective-permute-start(f32[1,1]{1,0:T(1,128)} %add.101), channel_id=1, source_target_pairs={{0,2},{1,3},{2,0},{3,1},{4,6},{5,7},{6,4},{7,5},{8,10},{9,11},{10,... | collective-permute-start | bytes 20 | tf_op jit(solution)/shard_map/ppermute | solution.py:483
  141.8 1.3 copy.97.ctx_ref
  143.2 35.4 %all-gather.7.cloned.1.call-done = bf16[3072,1728]{1,0:T(8,128)(2,1)} async-done(((bf16[96,1728]{1,0:T(8,128)(2,1)}), bf16[3072,1728]{1,0:T(8,128)(2,1)}) %all-gather.7.cloned.1.call-update) | async-done | bytes 10616848 | tf_op jit(solution)/shard_map/all_gather | solution.py:550
  178.6 30.1 %dense_chain.1 = (bf16[512,768]{1,0:T(8,128)(2,1)}, f32[512,768]{1,0:T(8,128)}, bf16[4,512,192]{2,1,0:T(8,128)(2,1)}, bf16[512,768]{1,0:T(8,128)(2,1)}, bf16[512...) custom-call(f32[1]{0:T(128)} %bitcast.1.ratio_ref, ...), custom_call_target="tpu_custom_call" | custom-call | flops 10871635968 | bytes 25165824 | tf_op jit(solution)/shard_map/dense_chain/pallas_call | solution.py:370
  208.7 1.9 copy-done.1
  210.6 1.9 copy-done.2
  212.5 1.1 copy-done.3
  213.7 1.1 copy-done.4
  214.8 1.1 copy-done.5
  215.9 8.7 %dense_weights.1 = bf16[4,768,1728]{2,1,0:T(8,128)(2,1)} custom-call(bf16[512,768]{1,0:T(8,128)(2,1)S(1)} %copy-done.3, bf16[512,768]{1,0:T(8,128)(2,1)S(1)} %copy-done.4, bf16[512,768]{1,0:T(8,128)(2,1)S(1)} %copy-done.5, bf16[4,512,768]{2,1,0:T(8,128)(2,1)S(1)} %copy-done.1, bf16[4,512,768]{2,1,0:T(8,128)(2,1)S(1)} %copy-done.2, ...), custom_call_target="tpu_custom_call" | custom-call | flops 5435817984 | bytes 20971520 | tf_op jit(solution)/shard_map/dense_weights/pallas_call | solution.py:452
  224.6 1.5 copy.99
  226.1 23.9 %all_to_all.10 = bf16[4,512,192]{1,2,0:T(8,128)(2,1)} all-to-all(bf16[4,512,192]{1,2,0:T(8,128)(2,1)S(1)} %copy.99), channel_id=1, replica_groups=mesh['dp'=8,'tensor'=4] {'tensor'}, dimensions={0} | all-to-all | bytes 1572864 | tf_op jit(solution)/shard_map/all_to_all | solution.py:580
  250.0 1.5 copy.100
  251.6 1.9 copy-done.8
  253.5 41.4 %attend_backward.1 = (bf16[2048,768]{1,0:T(8,128)(2,1)S(1)}, f32[1,768]{1,0:T(1,128)S(1)}) custom-call(s32[8]{0:T(128)S(1)} %get-tuple-element.157.low_ref, s32[8]{0:T(128)S(1)} %get-tuple-element.156.high_ref, bf16[2048,768]{1,0:T(8,128)(2,1)S(1)} %copy-done.8, s32[2048,1]{1,0:T(8,128)S(1)} %copy.94.seg_col_ref, s32[1,2048]{1,0:T(1,128)S(1)} %copy-done.6, ...), custom_call_target="tpu_custom_call" | custom-call | flops 8053063680 | bytes 10485760 | tf_op jit(solution)/shard_map/attend_backward/pallas_call | solution.py:226
  294.9 1.6 copy-done.9
  296.5 4.1 convolution_convert_fusion
  300.9 1.6 copy-done.10
  302.5 4.7 %fusion.6 = bf16[768,768]{0,1:T(8,128)(2,1)S(1)} fusion(bf16[2048,768]{1,0:T(8,128)(2,1)S(1)} %copy-done.10, bf16[1,2048,768]{2,1,0:T(8,128)(2,1)} %all-gather.5.cloned.1.call-done), kind=kOutput, calls=%fused_computation.7 | convolution fusion | flops 2416508928 | bytes 7471104 | tf_op jit(solution)/shard_map/dot_general | solution.py:29
  307.2 1.0 copy-done.12
  310.5 1.5 collective-permute-start.9
  312.0 2.6 collective-permute-done.9
  314.6 2.9 collective-permute-start.10
  317.5 2.0 collective-permute-done.10
  319.9 1.0 collective-permute-start.14
  320.9 5.7 %collective-permute-done.11 = f32[84,128]{1,0:T(8,128)S(1)} collective-permute-done((f32[84,128]{1,0:T(8,128)S(1)}, f32[84,128]{1,0:T(8,128)S(1)}, u32[]{:S(2)}, u32[]{:S(2)}) %collective-permute-start.11) | collective-permute-done | bytes 43040 | tf_op jit(solution)/shard_map/ppermute | solution.py:483
  326.7 6.5 %collective-permute-done.12 = f32[84,128]{1,0:T(8,128)S(1)} collective-permute-done((f32[84,128]{1,0:T(8,128)S(1)}, f32[84,128]{1,0:T(8,128)S(1)}, u32[]{:S(2)}, u32[]{:S(2)}) %collective-permute-start.12) | collective-permute-done | bytes 43040 | tf_op jit(solution)/shard_map/ppermute | solution.py:483
  333.2 1.2 slice_bitcast_fusion.3
  335.2 1.7 collective-permute-start.15
  337.5 2.9 collective-permute-done.15
  342.9 28.7 %reduce-scatter.4.cloned.1.call-done = bf16[512,768]{1,0:T(8,128)(2,1)} async-done(((bf16[2048,768]{1,0:T(8,128)(2,1)}), bf16[512,768]{1,0:T(8,128)(2,1)}) %reduce-scatter.4.cloned.1.call-update) | async-done | bytes 786448 | tf_op jit(solution)/shard_map/reduce_scatter | solution.py:588
  371.5 2.4 add_bitcast_fusion
  373.9 32.0 %reduce-scatter.8.cloned.1.call-done = bf16[1,96,1728]{2,1,0:T(8,128)(2,1)} async-done(((bf16[4,96,1728]{2,1,0:T(8,128)(2,1)}), bf16[1,96,1728]{2,1,0:T(8,128)(2,1)}) %reduce-scatter.8.cloned.1.call-update) | async-done | bytes 331792 | tf_op jit(solution)/shard_map/reduce_scatter | solution.py:583
  405.9 1.0 bitcast_convert_fusion
  (137 shorter events, 20.9 us)
Async XLA Ops:
  7.2 68.6 %all-gather.5.cloned.1.call-start = ((), (), s32[]{:S(2)}) async-start(), calls=%async_computation.8 | async-start | bytes 3932160 | tf_op jit(solution)/shard_map/all_gather | solution.py:546
  7.9 23.1 %copy-start.6 = (s32[1,2048]{1,0:T(1,128)S(1)}, s32[1,2048]{1,0:T(1,128)}, u32[]{:S(2)}) copy-start(s32[1,2048]{1,0:T(1,128)} %seg_row_ref.3) | copy-start | bytes 24580
  7.9 170.6 %all-gather.7.cloned.1.call-start = ((), (), s32[]{:S(2)}) async-start(), calls=%async_computation.9 | async-start | bytes 11354112 | tf_op jit(solution)/shard_map/all_gather | solution.py:550
  13.6 1.6 collective-permute-start.5
  15.5 12.3 %collective-permute-start.6 = (bf16[192,768]{0,1:T(8,128)(2,1)S(1)}, bf16[192,768]{0,1:T(8,128)(2,1)S(1)}, u32[]{:S(2)}, u32[]{:S(2)}) collective-permute-start(bf16[192,768]{0,1:T(8,128)(2,1)S(1)} %maximum_select_fusion.2), channel_id=1, source_target_pairs={{0,8},{4,12},{8,0},{12,4},{16,24},{20,28},{24,16},{28,20},{1,9},{5... | collective-permute-start | bytes 884744 | tf_op jit(solution)/shard_map/ppermute | solution.py:483
  28.4 52.0 %copy-start.14 = (bf16[384,768]{0,1:T(8,128)(2,1)}, bf16[384,768]{0,1:T(8,128)(2,1)S(1)}, u32[]{:S(2)}) copy-start(bf16[384,768]{0,1:T(8,128)(2,1)S(1)} %maximum_select_fusion.1) | copy-start | bytes 1769476
  28.4 15.0 %collective-permute-start.7 = (bf16[384,768]{0,1:T(8,128)(2,1)S(1)}, bf16[384,768]{0,1:T(8,128)(2,1)S(1)}, u32[]{:S(2)}, u32[]{:S(2)}) collective-permute-start(bf16[384,768]{0,1:T(8,128)(2,1)S(1)} %maximum_select_fusion.1), channel_id=1, source_target_pairs={{0,16},{4,20},{8,24},{12,28},{16,0},{20,4},{24,8},{28,12},{1,17},{... | collective-permute-start | bytes 1769480 | tf_op jit(solution)/shard_map/ppermute | solution.py:483
  43.4 37.0 %copy-start.26 = (bf16[384,768]{0,1:T(8,128)(2,1)}, bf16[384,768]{0,1:T(8,128)(2,1)S(1)}, u32[]{:S(2)}) copy-start(bf16[384,768]{0,1:T(8,128)(2,1)S(1)} %collective-permute-done.7) | copy-start | bytes 1769476
  80.4 29.1 %copy-start.7 = (bf16[2048,768]{1,0:T(8,128)(2,1)}, bf16[2048,768]{1,0:T(8,128)(2,1)S(1)}, u32[]{:S(2)}) copy-start(bf16[2048,768]{1,0:T(8,128)(2,1)S(1)} %fusion.3.qkv_ref) | copy-start | bytes 9437188
  109.5 5.1 %copy-start.18 = (s32[1,512]{1,0:T(1,128)S(1)}, s32[1,512]{1,0:T(1,128)}, u32[]{:S(2)}) copy-start(s32[1,512]{1,0:T(1,128)} %param.22) | copy-start | bytes 6148
  109.5 6.5 %copy-start.20 = (bf16[768]{0:T(1024)(128)(2,1)S(1)}, bf16[768]{0:T(1024)(128)(2,1)}, u32[]{:S(2)}) copy-start(bf16[768]{0:T(1024)(128)(2,1)} %param.33) | copy-start | bytes 4612
  109.5 6.5 %copy-start.21 = (bf16[768]{0:T(1024)(128)(2,1)S(1)}, bf16[768]{0:T(1024)(128)(2,1)}, u32[]{:S(2)}) copy-start(bf16[768]{0:T(1024)(128)(2,1)} %param.36) | copy-start | bytes 4612
  109.5 6.5 %copy-start.22 = (bf16[768]{0:T(1024)(128)(2,1)S(1)}, bf16[768]{0:T(1024)(128)(2,1)}, u32[]{:S(2)}) copy-start(bf16[768]{0:T(1024)(128)(2,1)} %param.37) | copy-start | bytes 4612
  109.5 6.6 %copy-start.23 = (bf16[768]{0:T(1024)(128)(2,1)S(1)}, bf16[768]{0:T(1024)(128)(2,1)}, u32[]{:S(2)}) copy-start(bf16[768]{0:T(1024)(128)(2,1)} %param.35) | copy-start | bytes 4612
  109.6 6.6 %copy-start.24 = (bf16[768]{0:T(1024)(128)(2,1)S(1)}, bf16[768]{0:T(1024)(128)(2,1)}, u32[]{:S(2)}) copy-start(bf16[768]{0:T(1024)(128)(2,1)} %param.38) | copy-start | bytes 4612
  109.6 6.6 %copy-start.25 = (bf16[768]{0:T(1024)(128)(2,1)S(1)}, bf16[768]{0:T(1024)(128)(2,1)}, u32[]{:S(2)}) copy-start(bf16[768]{0:T(1024)(128)(2,1)} %param.39) | copy-start | bytes 4612
  109.6 7.3 %copy-start.19 = (bf16[3072]{0:T(1024)(128)(2,1)S(1)}, bf16[3072]{0:T(1024)(128)(2,1)}, u32[]{:S(2)}) copy-start(bf16[3072]{0:T(1024)(128)(2,1)} %param.34) | copy-start | bytes 18436
  110.8 31.0 %all-to-all-start = ((bf16[4,512,192]{1,2,0:T(8,128)(2,1)}), bf16[4,512,192]{1,2,0:T(8,128)(2,1)S(1)}, u32[]{:S(2)}, u32[]{:S(2)}) async-start(bf16[4,512,192]{1,2,0:T(8,128)(2,1)} %copy.95), calls=%async_computation | async-start | bytes 1572864 | tf_op jit(solution)/shard_map/all_to_all | solution.py:567
  114.3 194.7 %reduce-scatter.6.cloned.1.call-start = ((), (), s32[]{:S(2)}) async-start(), calls=%async_computation.6 | async-start | bytes 12386304 | tf_op jit(solution)/shard_map/reduce_scatter | solution.py:582
  115.2 2.3 collective-permute-start
  118.7 3.7 collective-permute-start.1
  123.1 4.2 %collective-permute-start.2 = (f32[1,1]{1,0:T(1,128)}, f32[1,1]{1,0:T(1,128)}, u32[]{:S(2)}, u32[]{:S(2)}) collective-permute-start(f32[1,1]{1,0:T(1,128)} %add.99), channel_id=1, source_target_pairs={{0,16},{4,20},{8,24},{12,28},{16,0},{20,4},{24,8},{28,12},{1,17},{... | collective-permute-start | bytes 20 | tf_op jit(solution)/shard_map/ppermute | solution.py:483
  127.9 5.8 %collective-permute-start.3 = (f32[1,1]{1,0:T(1,128)}, f32[1,1]{1,0:T(1,128)}, u32[]{:S(2)}, u32[]{:S(2)}) collective-permute-start(f32[1,1]{1,0:T(1,128)} %add.100), channel_id=1, source_target_pairs={{0,1},{1,0},{2,3},{3,2},{4,5},{5,4},{6,7},{7,6},{8,9},{9,8},{10,11... | collective-permute-start | bytes 20 | tf_op jit(solution)/shard_map/ppermute | solution.py:483
  134.3 6.9 %collective-permute-start.4 = (f32[1,1]{1,0:T(1,128)}, f32[1,1]{1,0:T(1,128)}, u32[]{:S(2)}, u32[]{:S(2)}) collective-permute-start(f32[1,1]{1,0:T(1,128)} %add.101), channel_id=1, source_target_pairs={{0,2},{1,3},{2,0},{3,1},{4,6},{5,7},{6,4},{7,5},{8,10},{9,11},{10,... | collective-permute-start | bytes 20 | tf_op jit(solution)/shard_map/ppermute | solution.py:483
  178.6 30.2 %copy-start = (bf16[4,512,192]{2,1,0:T(8,128)(2,1)S(1)}, bf16[4,512,192]{2,1,0:T(8,128)(2,1)}, u32[]{:S(2)}) copy-start(bf16[4,512,192]{2,1,0:T(8,128)(2,1)} %copy.97.ctx_ref) | copy-start | bytes 2359300
  208.7 1.9 copy-start.1
  210.6 1.9 copy-start.2
  212.5 1.1 copy-start.3
  213.6 1.1 copy-start.4
  224.6 146.9 %reduce-scatter.4.cloned.1.call-start = ((), (), s32[]{:S(2)}) async-start(), calls=%async_computation.5 | async-start | bytes 3932160 | tf_op jit(solution)/shard_map/reduce_scatter | solution.py:588
  251.6 1.9 copy-start.8
  253.5 43.0 %copy-start.15 = (bf16[384,768]{0,1:T(8,128)(2,1)S(1)}, bf16[384,768]{0,1:T(8,128)(2,1)}, u32[]{:S(2)}) copy-start(bf16[384,768]{0,1:T(8,128)(2,1)} %copy-done.14) | copy-start | bytes 1769476
  253.5 43.0 %copy-start.27 = (bf16[384,768]{0,1:T(8,128)(2,1)S(1)}, bf16[384,768]{0,1:T(8,128)(2,1)}, u32[]{:S(2)}) copy-start(bf16[384,768]{0,1:T(8,128)(2,1)} %copy-done.26) | copy-start | bytes 1769476
  294.9 1.6 copy-start.9
  296.5 4.4 %copy-start.17 = (f32[8,768]{1,0:T(8,128)S(1)}, f32[8,768]{1,0:T(8,128)}, u32[]{:S(2)}) copy-start(f32[8,768]{1,0:T(8,128)} %get-tuple-element.39) | copy-start | bytes 73732
  300.6 1.9 copy-start.10
  300.6 105.3 %reduce-scatter.8.cloned.1.call-start = ((), (), s32[]{:S(2)}) async-start(), calls=%async_computation.7 | async-start | bytes 1720320 | tf_op jit(solution)/shard_map/reduce_scatter | solution.py:583
  307.1 1.9 copy-start.16
  308.2 11.5 %copy-start.13 = (bf16[768,768]{0,1:T(8,128)(2,1)S(1)}, bf16[768,768]{0,1:T(8,128)(2,1)}, u32[]{:S(2)}) copy-start(bf16[768,768]{0,1:T(8,128)(2,1)} %copy-done.12) | copy-start | bytes 3538948
  308.2 11.5 %collective-permute-start.13 = (bf16[4,96,768]{2,1,0:T(8,128)(2,1)S(1)}, bf16[4,96,768]{2,1,0:T(8,128)(2,1)S(1)}, u32[]{:S(2)}, u32[]{:S(2)}) collective-permute-start(bf16[4,96,768]{2,1,0:T(8,128)(2,1)S(1)} %dynamic-slice_bitcast_fusion), channel_id=1, source_target_pairs={{0,4},{4,0},{8,12},{12,8},{16,20},{20,16},{24,28},{28,24},{1,5},{5... | collective-permute-start | bytes 1769480 | tf_op jit(solution)/shard_map/ppermute | solution.py:483
  309.1 1.4 collective-permute-start.8
  310.5 4.1 collective-permute-start.9
  314.6 4.9 %collective-permute-start.10 = (f32[84,128]{1,0:T(8,128)S(1)}, f32[84,128]{1,0:T(8,128)S(1)}, u32[]{:S(2)}, u32[]{:S(2)}) collective-permute-start(f32[84,128]{1,0:T(8,128)S(1)} %fusion.18), channel_id=1, source_target_pairs={{0,16},{4,20},{8,24},{12,28},{16,0},{20,4},{24,8},{28,12},{1,17},{... | collective-permute-start | bytes 129032 | tf_op jit(solution)/shard_map/ppermute | solution.py:483
  319.6 7.0 %collective-permute-start.11 = (f32[84,128]{1,0:T(8,128)S(1)}, f32[84,128]{1,0:T(8,128)S(1)}, u32[]{:S(2)}, u32[]{:S(2)}) collective-permute-start(f32[84,128]{1,0:T(8,128)S(1)} %add.109), channel_id=1, source_target_pairs={{0,1},{1,0},{2,3},{3,2},{4,5},{5,4},{6,7},{7,6},{8,9},{9,8},{10,11... | collective-permute-start | bytes 129032 | tf_op jit(solution)/shard_map/ppermute | solution.py:483
  319.9 51.6 %copy-start.11 = (f32[512,768]{1,0:T(8,128)S(1)}, f32[512,768]{1,0:T(8,128)}, u32[]{:S(2)}) copy-start(f32[512,768]{1,0:T(8,128)} %get-tuple-element.41) | copy-start | bytes 4718596
  319.9 15.2 %collective-permute-start.14 = (bf16[2,96,768]{2,1,0:T(8,128)(2,1)S(1)}, bf16[2,96,768]{2,1,0:T(8,128)(2,1)S(1)}, u32[]{:S(2)}, u32[]{:S(2)}) collective-permute-start(bf16[2,96,768]{2,1,0:T(8,128)(2,1)S(1)} %dynamic-slice_bitcast_fusion.1), channel_id=1, source_target_pairs={{0,8},{4,12},{8,0},{12,4},{16,24},{20,28},{24,16},{28,20},{1,9},{5... | collective-permute-start | bytes 884744 | tf_op jit(solution)/shard_map/ppermute | solution.py:483
  326.6 6.6 %collective-permute-start.12 = (f32[84,128]{1,0:T(8,128)S(1)}, f32[84,128]{1,0:T(8,128)S(1)}, u32[]{:S(2)}, u32[]{:S(2)}) collective-permute-start(f32[84,128]{1,0:T(8,128)S(1)} %add.110), channel_id=1, source_target_pairs={{0,2},{1,3},{2,0},{3,1},{4,6},{5,7},{6,4},{7,5},{8,10},{9,11},{10,... | collective-permute-start | bytes 129032 | tf_op jit(solution)/shard_map/ppermute | solution.py:483
  335.2 5.2 %collective-permute-start.15 = (bf16[1,96,768]{2,1,0:T(8,128)(2,1)S(1)}, bf16[1,96,768]{2,1,0:T(8,128)(2,1)S(1)}, u32[]{:S(2)}, u32[]{:S(2)}) collective-permute-start(bf16[1,96,768]{2,1,0:T(8,128)(2,1)S(1)} %constant_dynamic-slice_fusion), channel_id=1, source_target_pairs={{0,16},{4,20},{8,24},{12,28},{16,0},{20,4},{24,8},{28,12},{1,17},{... | collective-permute-start | bytes 442376 | tf_op jit(solution)/shard_map/ppermute | solution.py:483
  (2 other events, 2.2 us)
Sparse Core Ops, SparseCore 0:
  9.6 66.1 all-gather.4
  79.3 99.2 all-gather.6
  224.7 82.4 reduce-scatter.5
  309.3 62.1 reduce-scatter.3
  373.7 32.1 reduce-scatter.7

commit v3 on v2

v3 whole, which is shorter than its diff:
```python
import functools

import jax
import jax.numpy as jnp
from jax import lax
from jax.experimental import pallas as pl
from jax.experimental.pallas import tpu as pltpu
from jax.sharding import PartitionSpec as P

DH = 64
BLOCK = 256
SLAB = 4 * DH
EPSILON = 1e-12
ROOT_HALF = 0.7071067811865476
INV_ROOT_TAU = 0.3989422804014327
LOG2E = 1.4426950408889634
LN2 = 0.6931471805599453
SCALE = DH ** (-0.5)
MASKED = -1e30
VMEM_LIMIT = 60 << 20

BF16 = jnp.bfloat16
F32 = jnp.float32
NN = (((1,), (0,)), ((), ()))
NT = (((1,), (1,)), ((), ()))
TN = (((0,), (0,)), ((), ()))


def dot(left_side, right_side, dims=NN):
    return lax.dot_general(left_side, right_side, dims, preferred_element_type=F32)


def norm_forward(summed, gain_vec, shift_vec):
    average = jnp.mean(summed, axis=-1, keepdims=True)
    centered = summed - average
    variance = jnp.mean(centered * centered, axis=-1, keepdims=True)
    inverse = lax.rsqrt(variance + EPSILON)
    normed = centered * inverse
    return (normed * gain_vec + shift_vec, normed, inverse)


def norm_backward(upstream, normed, inverse, gain_vec):
    scaled = upstream * gain_vec
    first_mean = jnp.mean(scaled, axis=-1, keepdims=True)
    second_mean = jnp.mean(scaled * normed, axis=-1, keepdims=True)
    return inverse * (scaled - first_mean - normed * second_mean)


def column_sum(value):
    return jnp.sum(value, axis=0, keepdims=True)


def lane_is_right(rows):
    return lax.broadcasted_iota(jnp.int32, (rows, 2 * DH), 1) >= DH


def pack(first_two, third_top, third_bottom):
    return jnp.concatenate([first_two, jnp.concatenate([third_top, third_bottom], axis=1)], axis=0)


def unpack(packed):
    third = packed[BLOCK:]
    third = jnp.concatenate([third[:, :DH], third[:, DH:]], axis=0)
    return jnp.concatenate([packed[:BLOCK], third], axis=1)


def attend_forward(
    which, low_ref, high_ref, qkv_ref, seg_col_ref, seg_row_ref, ctx_ref, lse_ref, held
):
    halves, half = which
    heads = lse_ref.shape[0]
    qb = pl.program_id(0) * halves + half
    rows = pl.ds(pl.multiple_of(qb * BLOCK, BLOCK), BLOCK)
    seg_q = seg_col_ref[...]
    queries = [
        qkv_ref[rows, SLAB * h : SLAB * h + 2 * DH] * jnp.asarray(SCALE, BF16) for h in range(heads)
    ]
    low, high = low_ref[qb], high_ref[qb]

    def score(kb, peaks):
        keys = pl.ds(pl.multiple_of(kb * BLOCK, BLOCK), BLOCK)
        allowed = seg_q == seg_row_ref[:, keys]
        found = []
        for h in range(heads):
            scores = dot(queries[h], qkv_ref[keys, SLAB * h + 2 * DH : SLAB * (h + 1)], NT)
            scores = jnp.where(allowed, scores, MASKED)
            held[h, kb] = scores
            found.append(jnp.maximum(peaks[h], jnp.maximum(scores[:, :128], scores[:, 128:])))
        return tuple(found)

    start = tuple(jnp.full((BLOCK, 128), MASKED, F32) for _ in range(heads))
    peaks = lax.fori_loop(low, high, score, start)
    highest = [jnp.max(peak, axis=-1, keepdims=True) for peak in peaks]

    def weigh(kb, carry):
        keys = pl.ds(pl.multiple_of(kb * BLOCK, BLOCK), BLOCK)
        found = []
        for h in range(heads):
            total, acc = carry[h]
            raised = jnp.exp2((held[h, kb] - highest[h]) * LOG2E)
            total = total + (raised[:, :128] + raised[:, 128:])
            acc = acc + dot(raised.astype(BF16), qkv_ref[keys, SLAB * h + 2 * DH : SLAB * (h + 1)])
            found.append((total, acc))
        return tuple(found)

    zero = jnp.zeros((BLOCK, 128), F32)
    done = lax.fori_loop(low, high, weigh, tuple((zero, zero) for _ in range(heads)))
    values = []
    for h in range(heads):
        total, acc = done[h]
        summed = jnp.sum(total, axis=-1, keepdims=True)
        values.append((acc / summed).astype(BF16))
        lse_ref[h] = jnp.transpose(highest[h] + jnp.log(summed))
    middle = BLOCK // 2
    ctx_ref[0, :BLOCK, :] = jnp.where(lane_is_right(BLOCK), values[1], pltpu.roll(values[0], DH, 1))
    ctx_ref[0, BLOCK:, :] = jnp.where(
        lane_is_right(middle), values[2][middle:], pltpu.roll(values[2][:middle], DH, 1)
    )


def attend_backward(
    halves, low_ref, high_ref, qkv_ref, seg_col_ref, seg_row_ref, *refs
):
    ctx_refs, grad_refs, lse_refs = refs[:halves], refs[halves : 2 * halves], refs[2 * halves : 3 * halves]
    out_ref, sums_ref, dkv = refs[3 * halves :]
    heads = dkv.shape[0]
    qb = pl.program_id(0)
    half = qb % halves

    def choose(options):
        value = options[0][...]
        for which in range(1, halves):
            value = jnp.where(half == which, options[which][...], value)
        return value

    @pl.when(qb == 0)
    def _():
        dkv[...] = jnp.zeros_like(dkv)
        sums_ref[...] = jnp.zeros_like(sums_ref)

    rows = pl.ds(pl.multiple_of(qb * BLOCK, BLOCK), BLOCK)
    right = lane_is_right(BLOCK)
    arrived = choose(grad_refs)[0]
    product = arrived.astype(F32) * choose(ctx_refs)[0].astype(F32)
    upper = product.astype(BF16)
    lower = (product - upper.astype(F32)).astype(BF16)
    pick = (
        lax.broadcasted_iota(jnp.int32, (8, 2 * DH), 1) // DH
        == lax.broadcasted_iota(jnp.int32, (8, 2 * DH), 0)
    ).astype(BF16)
    summed = dot(pick, upper, NT) + dot(pick, lower, NT)
    deltas = [
        summed[0:1, :BLOCK],
        summed[1:2, :BLOCK],
        jnp.concatenate([summed[0:1, BLOCK:], summed[1:2, BLOCK:]], axis=1),
    ]
    two, third = arrived[:BLOCK], arrived[BLOCK:]
    placed = [
        pltpu.roll(two, DH, 1),
        two,
        jnp.concatenate([pltpu.roll(third, DH, 1), third], axis=0),
    ]
    grads = [jnp.where(right, grad, jnp.zeros_like(grad)) for grad in placed]
    queries, pairs = [], []
    for h in range(heads):
        queries.append(qkv_ref[rows, SLAB * h : SLAB * h + 2 * DH] * jnp.asarray(SCALE, BF16))
        pairs.append(jnp.concatenate([queries[h], grads[h]], axis=0))
    seg_q = seg_row_ref[...]
    lses = choose(lse_refs)
    low, high = low_ref[qb], high_ref[qb]

    def step(kb, accs):
        keys = pl.ds(pl.multiple_of(kb * BLOCK, BLOCK), BLOCK)
        allowed = seg_col_ref[keys, :] == seg_q
        found = []
        for h in range(heads):
            pair = qkv_ref[keys, SLAB * h + 2 * DH : SLAB * (h + 1)]
            scores = jnp.where(allowed, dot(pair, queries[h], NT), MASKED)
            probs = jnp.exp2((scores - lses[h]) * LOG2E)
            score_grad = (probs * (dot(pair, grads[h], NT) - deltas[h])).astype(BF16)
            both = jnp.concatenate([score_grad, probs.astype(BF16)], axis=1)
            dkv[h, keys, :] += dot(both, pairs[h])
            found.append(accs[h] + dot(score_grad, pair, TN))
        return tuple(found)

    zero = jnp.zeros((BLOCK, 128), F32)
    accs = lax.fori_loop(low, high, step, tuple(zero for _ in range(heads)))
    for h in range(heads):
        query_grad = jnp.where(right, 0.0, accs[h] * SCALE).astype(BF16)
        out_ref[rows, SLAB * h : SLAB * h + 2 * DH] = query_grad
        sums_ref[:, SLAB * h : SLAB * h + 2 * DH] += column_sum(query_grad.astype(F32))

    @pl.when(qb == pl.num_programs(0) - 1)
    def _():
        for h in range(heads):
            pair_grad = dkv[h].astype(BF16)
            out_ref[:, SLAB * h + 2 * DH : SLAB * (h + 1)] = pair_grad
            sums_ref[:, SLAB * h + 2 * DH : SLAB * (h + 1)] = column_sum(pair_grad.astype(F32))


def document_blocks(segment_row):
    starts = segment_row[::BLOCK]
    stops = segment_row[BLOCK - 1 :: BLOCK]
    low = jnp.sum((segment_row[None, :] < starts[:, None]).astype(jnp.int32), axis=1)
    high = jnp.sum((segment_row[None, :] <= stops[:, None]).astype(jnp.int32), axis=1)
    return (low // BLOCK, (high + BLOCK - 1) // BLOCK)


PACKED = BLOCK + BLOCK // 2


def run_forward(which, bounds, qkv, seg_col, seg_row):
    halves, half = which
    seq_len, width = qkv.shape
    heads = width // SLAB
    blocks = seq_len // BLOCK
    steps = blocks // halves
    return pl.pallas_call(
        functools.partial(attend_forward, which),
        out_shape=(
            jax.ShapeDtypeStruct((steps, PACKED, 2 * DH), BF16),
            jax.ShapeDtypeStruct((heads, 1, steps * BLOCK), F32),
        ),
        grid_spec=pltpu.PrefetchScalarGridSpec(
            num_scalar_prefetch=2,
            grid=(steps,),
            in_specs=[
                pl.BlockSpec((seq_len, width), lambda q, *_: (0, 0), pipeline_mode=pl.Buffered(1)),
                pl.BlockSpec((BLOCK, 1), lambda q, *_: (q * halves + half, 0)),
                pl.BlockSpec((1, seq_len), lambda q, *_: (0, 0)),
            ],
            out_specs=(
                pl.BlockSpec((1, PACKED, 2 * DH), lambda q, *_: (q, 0, 0)),
                pl.BlockSpec((heads, 1, BLOCK), lambda q, *_: (0, 0, q)),
            ),
            scratch_shapes=[pltpu.VMEM((heads, blocks, BLOCK, BLOCK), F32)],
        ),
        compiler_params=pltpu.CompilerParams(
            dimension_semantics=("arbitrary",), vmem_limit_bytes=VMEM_LIMIT
        ),
        cost_estimate=pl.CostEstimate(
            flops=heads * seq_len * seq_len * 256 // halves,
            bytes_accessed=5 << 20,
            transcendentals=heads * seq_len * seq_len // 3 // halves,
        ),
        name="attend_forward",
    )(*bounds, qkv, seg_col, seg_row)


def run_backward(bounds, qkv, seg_col, seg_row, ctxs, grads, lses):
    seq_len, width = qkv.shape
    heads = width // SLAB
    halves = len(ctxs)
    packed = pl.BlockSpec((1, PACKED, 2 * DH), lambda q, *_: (q // halves, 0, 0))
    return pl.pallas_call(
        functools.partial(attend_backward, halves),
        out_shape=(
            jax.ShapeDtypeStruct((seq_len, width), BF16),
            jax.ShapeDtypeStruct((1, width), F32),
        ),
        grid_spec=pltpu.PrefetchScalarGridSpec(
            num_scalar_prefetch=2,
            grid=(seq_len // BLOCK,),
            in_specs=[
                pl.BlockSpec((seq_len, width), lambda q, *_: (0, 0), pipeline_mode=pl.Buffered(1)),
                pl.BlockSpec((seq_len, 1), lambda q, *_: (0, 0)),
                pl.BlockSpec((1, BLOCK), lambda q, *_: (0, q)),
            ]
            + [packed] * (2 * halves)
            + [pl.BlockSpec((heads, 1, BLOCK), lambda q, *_: (0, 0, q // halves))] * halves,
            out_specs=(
                pl.BlockSpec((seq_len, width), lambda q, *_: (0, 0)),
                pl.BlockSpec((1, width), lambda q, *_: (0, 0)),
            ),
            scratch_shapes=[pltpu.VMEM((heads, seq_len, 2 * DH), F32)],
        ),
        compiler_params=pltpu.CompilerParams(
            dimension_semantics=("arbitrary",), vmem_limit_bytes=VMEM_LIMIT
        ),
        cost_estimate=pl.CostEstimate(
            flops=heads * seq_len * seq_len * 640,
            bytes_accessed=10 << 20,
            transcendentals=heads * seq_len * seq_len // 3,
        ),
        name="attend_backward",
    )(*bounds, qkv, seg_col, seg_row, *ctxs, *grads, *lses)


def dense_chain(
    marks, place_ref, ratio_ref, ctx_ref, in_ref, teacher_ref, cotangent_ref, valid_ref, vec_ref,
    inner_bias_ref, *refs
):
    pieces = refs[: len(marks)]
    (
        layer_ref, first_grad_ref, ctx_grad_ref, first_ref, branch_grad_ref, attn_grad_ref,
        act_ref, hidden_grad_ref, sums_ref, inner_sums_ref, w_out, w_in, w_up, slope, sems,
    ) = refs[len(marks) :]
    parts, _, head_cols = w_out.shape
    hidden_cols = w_in.shape[2]
    rank, index = place_ref[0], place_ref[1]
    groups = (
        (2 * hidden_cols, head_cols, w_out),
        (0, hidden_cols, w_in),
        (hidden_cols, hidden_cols, w_up),
    )
    for group, (start, size, target) in enumerate(groups):
        for piece, marked in zip(pieces, marks):
            block = piece.shape[1]
            for at, (slot, turn) in enumerate(marked):
                offset = pl.multiple_of((index ^ turn) * block, block)
                pltpu.make_async_copy(
                    piece.at[at, :, pl.ds(start, size)],
                    target.at[slot, pl.ds(offset, block), :],
                    sems.at[group, slot],
                ).start()

    def arrive(group, slot):
        whole = groups[group][2].at[slot]
        pltpu.make_async_copy(whole, whole, sems.at[group, slot]).wait()

    def vec(which):
        return vec_ref[which : which + 1, :]

    inner_sums_ref[...] = jnp.zeros_like(inner_sums_ref)
    attention = jnp.zeros(in_ref.shape, F32)
    for slot in range(parts):
        arrive(0, slot)
        attention = attention + dot(unpack(ctx_ref[rank ^ slot]), w_out[slot], NT)
    first_exact, normed_one, inverse_one = norm_forward(
        in_ref[...].astype(F32) + attention + vec(0), vec(1), vec(2)
    )
    first = first_exact.astype(BF16)
    first_ref[...] = first

    def up(slot, branch):
        t = rank ^ slot
        arrive(1, slot)
        hidden = dot(first, w_in[slot]) + inner_bias_ref[t]
        bend = 0.5 * (1.0 + lax.erf(hidden * ROOT_HALF))
        activated = (hidden * bend).astype(BF16)
        act_ref[t] = activated
        slope[slot] = bend + hidden * INV_ROOT_TAU * jnp.exp2(hidden * hidden * (-0.5 * LOG2E))
        arrive(2, slot)
        return branch + dot(activated, w_up[slot], NT)

    branch = lax.fori_loop(0, parts, up, jnp.zeros(in_ref.shape, F32))
    layer_rows, normed_two, inverse_two = norm_forward(first.astype(F32) + branch + vec(3), vec(4), vec(5))
    layer_ref[...] = layer_rows.astype(BF16)
    misfit = layer_rows - teacher_ref[...].astype(F32)
    weighted = valid_ref[...] * misfit
    out_grad = cotangent_ref[...].astype(F32) + weighted * ratio_ref[0]
    second_grad = norm_backward(out_grad, normed_two, inverse_two, vec(4))
    branch_grad = second_grad.astype(BF16)
    branch_grad_ref[...] = branch_grad
    sums_ref[0:1, :] = column_sum(weighted * misfit)
    sums_ref[1:2, :] = column_sum(branch_grad.astype(F32))
    sums_ref[2:3, :] = column_sum(out_grad * normed_two)
    sums_ref[3:4, :] = column_sum(out_grad)

    def down(slot, back):
        t = rank ^ slot
        hidden_grad = (dot(branch_grad, w_up[slot]) * slope[slot]).astype(BF16)
        hidden_grad_ref[t] = hidden_grad
        inner_sums_ref[t] = column_sum(hidden_grad.astype(F32))
        return back + dot(hidden_grad, w_in[slot], NT)

    upstream = lax.fori_loop(0, parts, down, second_grad)
    first_grad = norm_backward(upstream, normed_one, inverse_one, vec(1))
    first_grad_ref[...] = first_grad
    attn_grad = first_grad.astype(BF16)
    attn_grad_ref[...] = attn_grad
    sums_ref[4:5, :] = column_sum(attn_grad.astype(F32))
    sums_ref[5:6, :] = column_sum(upstream * normed_one)
    sums_ref[6:7, :] = column_sum(upstream)
    sums_ref[7:8, :] = jnp.zeros_like(sums_ref[7:8, :])
    middle = BLOCK // 2
    for slot in range(parts):
        back = dot(attn_grad, w_out[slot]).astype(BF16)
        ctx_grad_ref[rank ^ slot] = pack(
            back[:, : 2 * DH], back[:middle, 2 * DH :], back[middle:, 2 * DH :]
        )


def run_dense(half, marks, place, ratio, ctx, rows_in, teacher, cotangent, valid, vecs, inner_bias, pieces):
    parts = ctx.shape[0]
    width = rows_in.shape[1]
    hidden_cols = inner_bias.shape[2]
    head_cols = pieces[0].shape[2] - 2 * hidden_cols

    def mine(columns):
        return pl.BlockSpec((BLOCK, columns), lambda i: (half, 0))

    def fixed(shape):
        return pl.BlockSpec(shape, lambda i: (0,) * len(shape))

    low = jax.ShapeDtypeStruct((BLOCK, width), BF16)
    out_shape = (
        low,
        jax.ShapeDtypeStruct((BLOCK, width), F32),
        jax.ShapeDtypeStruct(ctx.shape, BF16),
        low,
        low,
        low,
        jax.ShapeDtypeStruct((parts, BLOCK, hidden_cols), BF16),
        jax.ShapeDtypeStruct((parts, BLOCK, hidden_cols), BF16),
        jax.ShapeDtypeStruct((8, width), F32),
        jax.ShapeDtypeStruct((parts, 1, hidden_cols), F32),
    )
    smem = pl.BlockSpec(memory_space=pltpu.SMEM)
    return pl.pallas_call(
        functools.partial(dense_chain, marks),
        out_shape=out_shape,
        grid=(1,),
        in_specs=[
            smem,
            smem,
            fixed(ctx.shape),
            mine(width),
            mine(width),
            mine(width),
            mine(1),
            fixed(vecs.shape),
            fixed(inner_bias.shape),
        ]
        + [pl.BlockSpec(memory_space=pl.ANY)] * len(pieces),
        out_specs=tuple(fixed(out.shape) for out in out_shape),
        scratch_shapes=[
            pltpu.VMEM((parts, width, head_cols), BF16),
            pltpu.VMEM((parts, width, hidden_cols), BF16),
            pltpu.VMEM((parts, width, hidden_cols), BF16),
            pltpu.VMEM((parts, BLOCK, hidden_cols), F32),
            pltpu.SemaphoreType.DMA((3, parts)),
        ],
        compiler_params=pltpu.CompilerParams(
            dimension_semantics=("arbitrary",), vmem_limit_bytes=VMEM_LIMIT
        ),
        cost_estimate=pl.CostEstimate(
            flops=BLOCK * width * (8 * hidden_cols + 4 * head_cols) * parts,
            bytes_accessed=18 << 20,
            transcendentals=2 * BLOCK * hidden_cols * parts,
        ),
        name="dense_chain",
    )(place, ratio, ctx, rows_in, teacher, cotangent, valid, vecs, inner_bias, *pieces)


def dense_weights(base, turns, halves, place_ref, *refs):
    firsts, branch_grads, attn_grads, acts, hidden_grads, ctxs = (
        refs[k * halves : (k + 1) * halves] for k in range(6)
    )
    outs = refs[6 * halves : 6 * halves + len(turns)]
    turned, whole, sems = refs[6 * halves + len(turns) :]
    step = pl.program_id(0)
    slots = pl.num_programs(0)

    @pl.when(step == 0)
    def _():
        for which, sources in enumerate((firsts, branch_grads, attn_grads)):
            for half, source in enumerate(sources):
                turned[which, :, half * BLOCK : (half + 1) * BLOCK] = jnp.transpose(source[...])

    def both(sources):
        return jnp.concatenate([source[0] for source in sources], axis=0)

    hidden_cols = acts[0].shape[2]
    whole[step, :, :hidden_cols] = dot(turned[0], both(hidden_grads)).astype(BF16)
    whole[step, :, hidden_cols : 2 * hidden_cols] = dot(turned[1], both(acts)).astype(BF16)
    ctx = jnp.concatenate([unpack(source[0]) for source in ctxs], axis=0)
    whole[step, :, 2 * hidden_cols :] = dot(turned[2], ctx).astype(BF16)
    for out, order in zip(outs, turns):
        block = out.shape[1]
        for at, turn in enumerate(order):
            offset = pl.multiple_of((place_ref[1] ^ turn) * block, block)
            pltpu.make_async_copy(
                whole.at[step, pl.ds(offset, block), :],
                out.at[at * slots + step],
                sems.at[step],
            ).start()

    @pl.when(step == slots - 1)
    def _():
        for slot in range(whole.shape[0]):
            pltpu.make_async_copy(whole.at[slot], whole.at[slot], sems.at[slot]).wait()


def run_weights(base, slots, turns, block, place, firsts, branch_grads, attn_grads, acts, hidden_grads, ctxs):
    parts, _, hidden_cols = acts[0].shape
    halves = len(acts)
    width = firsts[0].shape[1]
    columns = 2 * hidden_cols + 3 * DH

    def by_slot(rows, size):
        return pl.BlockSpec((1, rows, size), lambda s, place: (place[0] ^ (base + s), 0, 0))

    fixed = pl.BlockSpec((BLOCK, width), lambda s, place: (0, 0))
    return pl.pallas_call(
        functools.partial(dense_weights, base, turns, halves),
        out_shape=tuple(
            jax.ShapeDtypeStruct((len(order) * slots, block, columns), BF16) for order in turns
        ),
        grid_spec=pltpu.PrefetchScalarGridSpec(
            num_scalar_prefetch=1,
            grid=(slots,),
            in_specs=[fixed] * (3 * halves)
            + [by_slot(BLOCK, hidden_cols)] * (2 * halves)
            + [by_slot(PACKED, 2 * DH)] * halves,
            out_specs=tuple(pl.BlockSpec(memory_space=pl.ANY) for _ in turns),
            scratch_shapes=[
                pltpu.VMEM((3, width, halves * BLOCK), BF16),
                pltpu.VMEM((slots, width, columns), BF16),
                pltpu.SemaphoreType.DMA((slots,)),
            ],
        ),
        compiler_params=pltpu.CompilerParams(
            dimension_semantics=("arbitrary",), vmem_limit_bytes=VMEM_LIMIT
        ),
        cost_estimate=pl.CostEstimate(
            flops=2 * halves * BLOCK * width * columns * slots,
            bytes_accessed=5 * slots << 20,
            transcendentals=0,
        ),
        name="dense_weights",
    )(place, *firsts, *branch_grads, *attn_grads, *acts, *hidden_grads, *ctxs)


def interleave(query, key, value, heads):
    rows = query.shape[0]
    parts = [part.reshape(rows, heads, 1, DH) for part in (query, jnp.zeros_like(query), key, value)]
    return jnp.concatenate(parts, axis=2).reshape(rows, heads * SLAB)


def place_slice(local_grad, full_size, offset):
    return lax.dynamic_update_slice_in_dim(jnp.zeros((full_size,), F32), local_grad, offset, 0)


def swap(value, axis, bit):
    size = lax.axis_size(axis)
    return lax.ppermute(value, axis, [(i, i ^ bit) for i in range(size)])


def bits_of(axis):
    bit = 1
    while bit < lax.axis_size(axis):
        yield bit
        bit *= 2


def sum_everywhere(value):
    for axis in ("dp", "tensor"):
        for bit in bits_of(axis):
            value = value + swap(value, axis, bit)
    return value


def gather_rows(shard):
    held = shard
    index = lax.axis_index("dp")
    for bit in bits_of("dp"):
        other = swap(held, "dp", bit)
        mine_first = (index & bit) == 0
        held = jnp.where(
            mine_first,
            jnp.concatenate([held, other], axis=0),
            jnp.concatenate([other, held], axis=0),
        )
    return held


def scatter_rows(value):
    copies = lax.axis_size("dp")
    index = lax.axis_index("dp")
    held = value.reshape((copies,) + (value.shape[0] // copies,) + value.shape[1:])
    for bit in bits_of("dp"):
        held = held.reshape((held.shape[0] // 2, 2) + held.shape[1:])
        own = (index & bit) // bit
        keep = lax.dynamic_index_in_dim(held, own, 1, keepdims=False)
        send = lax.dynamic_index_in_dim(held, 1 - own, 1, keepdims=False)
        came = swap(send, "dp", bit)
        held = (keep.astype(F32) + came.astype(F32)).astype(BF16)
    return held[0]


def gather_pieces(shard):
    pair = jnp.concatenate([shard[None], swap(shard[None], "tensor", 1)], axis=0)
    far = swap(pair, "tensor", 2)
    bits = list(bits_of("dp"))
    pieces, marks = [], []
    for held, base in ((pair, 0), (far, 2)):
        marked = [(base, 0), (base + 1, 0)]
        for bit in bits[1:]:
            held = jnp.concatenate([held, swap(held, "dp", bit)], axis=0)
            marked = marked + [(slot, turn ^ bit) for slot, turn in marked]
        pieces += [held, swap(held, "dp", bits[0])]
        marks += [marked, [(slot, turn ^ bits[0]) for slot, turn in marked]]
    return (pieces, marks)


def add_low(left_side, right_side):
    return (left_side.astype(F32) + right_side.astype(F32)).astype(BF16)


def spread(order):
    turns = [0]
    for bit in reversed(order):
        turns = turns + [turn | bit for turn in turns]
    return turns


def add_halves(left_side, right_side):
    half = left_side.shape[0] // 2
    return (
        add_low(left_side[:half], right_side[:half]),
        add_low(left_side[half:], right_side[half:]),
    )


def local(
    inputs, segment_ids, valid_mask, teacher, cotangent,
    w_query, w_key, w_value, w_output, w_inner, w_outer,
    query_bias, value_bias, output_bias, inner_bias, outer_bias,
    gain_attn, shift_attn, gain_ffn, shift_ffn,
):
    _, part_len, width = inputs.shape
    parts = lax.axis_size("tensor")
    copies = lax.axis_size("dp")
    rank = lax.axis_index("tensor")
    total_tokens = part_len * parts * copies
    seq_len = part_len * parts
    head_cols = w_query.shape[1]
    heads = head_cols // DH
    hidden_cols = w_inner.shape[1]
    shard_rows = w_inner.shape[0]
    halves = part_len // BLOCK
    aligned = shard_rows % 16 == 0 and parts == 4 and copies >= 4

    rows_in = inputs.reshape(part_len, width)
    tokens = lax.all_gather(rows_in, "tensor", axis=0, tiled=True)
    w_heads = gather_rows(interleave(w_query, w_key, w_value, heads))
    mine = jnp.concatenate((w_inner, w_outer.T, w_output.T), axis=1)
    if aligned:
        place = jnp.stack([rank, lax.axis_index("dp")]).astype(jnp.int32)
        pieces, marks = gather_pieces(mine)
    else:
        place = jnp.zeros((2,), jnp.int32)
        weights = lax.all_gather(mine, ("tensor", "dp"), axis=0, tiled=False)
        pieces = [weights.reshape(parts, width, 2 * hidden_cols + head_cols)]
        marks = [[(t, 0) for t in range(parts)]]

    valid_rows = valid_mask.astype(F32).reshape(part_len, 1)
    counted = sum_everywhere(jnp.sum(valid_rows).reshape(1, 1))
    ratio = (total_tokens / counted).reshape(1)
    w_heads, ratio = lax.optimization_barrier((w_heads, ratio))

    mine_cols = rank * head_cols
    query_shift = lax.dynamic_slice_in_dim(query_bias, mine_cols, head_cols).astype(F32)
    value_shift = lax.dynamic_slice_in_dim(value_bias, mine_cols, head_cols).astype(F32)
    shifts = interleave(query_shift[None], jnp.zeros_like(query_shift)[None], value_shift[None], heads)
    qkv = (dot(tokens, w_heads) + shifts).astype(BF16)

    segment_row = segment_ids.reshape(seq_len)
    bounds = document_blocks(segment_row)
    seg_col = segment_row.reshape(seq_len, 1)
    seg_row = segment_row.reshape(1, seq_len)

    def exchange(blocks):
        return lax.all_to_all(blocks, "tensor", 0, 0)

    contexts, lses, arrived = [], [], []
    for half in range(halves):
        context, lse = run_forward((halves, half), bounds, qkv, seg_col, seg_row)
        contexts.append(context)
        lses.append(lse)
        arrived.append(exchange(context))

    vecs = jnp.stack(
        (output_bias, gain_attn, shift_attn, outer_bias, gain_ffn, shift_ffn, outer_bias, outer_bias)
    ).astype(F32)
    inner_rows = inner_bias.astype(F32).reshape(parts, 1, hidden_cols)
    teacher_rows = teacher.reshape(part_len, width)
    cotangent_rows = cotangent.reshape(part_len, width)
    chains = [
        run_dense(
            half, marks, place, ratio, arrived[half], rows_in, teacher_rows, cotangent_rows,
            valid_rows, vecs, inner_rows, pieces,
        )
        for half in range(halves)
    ]
    (
        layers, first_grads, context_grads, firsts, branch_grads, attn_grads, acts, hidden_grads,
        dense_sums, inner_sums,
    ) = zip(*chains)
    head_grads = [exchange(context_grad) for context_grad in context_grads]
    dense_sums = sum(dense_sums)
    inner_sums = sum(inner_sums)
    sources = (firsts, branch_grads, attn_grads, acts, hidden_grads, arrived)
    head_grads[:-1], sources = lax.optimization_barrier((head_grads[:-1], sources))
    if aligned:
        rest = list(bits_of("dp"))[1:]
        orders = (rest, rest[::-1])
        begun = []
        for which, order in enumerate(orders):
            turns = spread(order)
            keep, send = run_weights(
                2 * which, 2, (turns, [turn | 1 for turn in turns]), shard_rows, place, *sources
            )
            if which == 1:
                head_grads[-1], keep, send = lax.optimization_barrier((head_grads[-1], keep, send))
            shape = (copies // 2, 2) + keep.shape[1:]
            begun.append(add_halves(keep.reshape(shape), swap(send.reshape(shape), "dp", 1)))
        head_grads[-1], begun = lax.optimization_barrier((head_grads[-1], begun))
        moving = [(keep, swap(send, "dp", order[0])) for (keep, send), order in zip(begun, orders)]
    else:
        (packed,) = run_weights(0, parts, ([0],), width, place, *sources)
        packed = lax.psum_scatter(packed, "dp", scatter_dimension=1, tiled=True)
        packed = lax.psum_scatter(packed, "tensor", scatter_dimension=0, tiled=True)
        packed = packed.reshape(shard_rows, -1).astype(F32)

    joined_grad, sums = run_backward(bounds, qkv, seg_col, seg_row, contexts, head_grads, lses)
    if aligned:
        joined_grad, moving = lax.optimization_barrier((joined_grad, moving))
        reduced = []
        for (keep, came), order in zip(moving, orders):
            for bit in order[1:]:
                keep, send = add_halves(keep, came)
                came = swap(send, "dp", bit)
            held = add_low(keep, came)
            reduced.append(held[0])
        near = add_low(reduced[0], swap(reduced[1], "tensor", 2))
        packed = near[0].astype(F32) + swap(near[1], "tensor", 1).astype(F32)
    attn_back = dot(joined_grad, w_heads, NT).astype(BF16)
    attn_back, sums = lax.optimization_barrier((attn_back, sums))
    attn_back = lax.psum_scatter(attn_back, "tensor", scatter_dimension=0, tiled=True)
    input_grad = jnp.concatenate(first_grads, axis=0) + attn_back.astype(F32)
    head_weights = scatter_rows(dot(tokens, joined_grad, TN).astype(BF16))
    head_weights = head_weights.astype(F32).reshape(shard_rows, heads, 4, DH)

    def pick(which):
        return head_weights[:, :, which, :].reshape(shard_rows, head_cols)

    sums = sums.reshape(heads, 4, DH)
    totals = sum_everywhere(
        jnp.concatenate(
            (
                place_slice(sums[:, 0].reshape(head_cols), width, mine_cols),
                place_slice(sums[:, 3].reshape(head_cols), width, mine_cols),
                dense_sums.reshape(-1),
                inner_sums.reshape(-1),
            )
        ).reshape(-1, 128)
    ).reshape(-1)

    def total(which):
        return totals[which * width : (which + 1) * width]

    mse_loss = jnp.sum(total(2)) / (counted[0, 0] * width)
    return (
        jnp.concatenate(layers, axis=0).reshape(1, part_len, width),
        mse_loss,
        input_grad.reshape(1, part_len, width),
        pick(0),
        pick(2),
        pick(3),
        packed[:, 2 * hidden_cols :].T,
        packed[:, :hidden_cols],
        packed[:, hidden_cols : 2 * hidden_cols].T,
        total(0),
        total(1),
        total(6),
        totals[10 * width :],
        total(3),
        total(7),
        total(8),
        total(4),
        total(5),
    )


def solution(mesh):
    shard = P("dp", "tensor", None)
    in_specs = (
        (shard, P("dp", None), P("dp", "tensor"), shard, shard)
        + (P("dp", "tensor"),) * 3
        + (P("tensor", "dp"), P("dp", "tensor"), P("tensor", "dp"))
        + (P(),) * 9
    )
    out_specs = (
        (shard, P(), shard)
        + (P("dp", "tensor"),) * 3
        + (P("tensor", "dp"), P("dp", "tensor"), P("tensor", "dp"))
        + (P(),) * 9
    )
    return jax.shard_map(local, mesh=mesh, in_specs=in_specs, out_specs=out_specs, check_vma=False)
```

time: 416 us -> 504 us (1.21); the launches traced: 416 us -> 495 us
  starting transfers between devices: 35.7 us -> 70.2 us
  other arithmetic: 10.6 us -> 37.1 us
  blocking collectives: 23.9 us -> 0 us
  Pallas kernels: 109 us -> 132 us
  waiting for transfers between devices: 174 us -> 190 us
  matrix products: 13.3 us -> 18.7 us
    ppermute x16 -> x32, waiting for transfers between devices: 44.4 us -> 190 us  [swap(): return lax.ppermute(value, axis, [(i, i ^ bit) for i in range(size)])]
    all_gather x1 -> x0, waiting for transfers between devices: 35.4 us -> none  [local(): weights = lax.all_gather(mine, ('tensor', 'dp'), axis=0, tiled=False)]
    all_gather x1, waiting for transfers between devices: 32.4 us -> 0.01 us  [local(): tokens = lax.all_gather(rows_in, 'tensor', axis=0, tiled=True)]
    reduce_scatter x2 -> x0, waiting for transfers between devices: 32 us -> none  [the longest x1 32 us: local(): packed = lax.psum_scatter(packed, 'tensor', scatter_dimension=0, tiled=True)]
    reduce_scatter x1, waiting for transfers between devices: 28.7 us -> 0.01 us  [local(): lax.psum_scatter(attn_back, 'tensor', scatter_dimension=0, tiled=True)]
    all_to_all x1 -> x0, blocking collectives: 23.9 us -> none  [local(): lax.all_to_all(context_grad, 'tensor', 0, 0).reshape(seq_len, head_cols)]
    pallas_call x4 -> x7, Pallas kernels: 109 us -> 132 us  [the longest x1 46.3 us: run_backward(): pl.pallas_call(functools.partial(attend_backward, halves), out_shape=(jax...]
    all_to_all x1 -> x4, starting transfers between devices: 3.49 us -> 21.4 us  [exchange(): return lax.all_to_all(blocks, 'tensor', 0, 0)]
  transfers between devices with their start and end apart: 22 -> 38, of which waited for: 16 -> 18; matrix products, arithmetic and copies ran while one was open for 9% -> 12% of each run, Pallas kernels for 17% -> 27%
where the time goes in v3:
time: 504 us; the launch traced here: 495 us
  waiting for transfers between devices  190 us (38%)
  Pallas kernels  132 us (26%)
  starting transfers between devices  70.2 us (14%)
  other arithmetic  37.1 us (7%)
  local copies, waits for them, and re-layouts  26.4 us (5%)
  between operations  20.8 us (4%)
  matrix products  18.7 us (4%)
    ppermute x32, waiting for transfers between devices, swap(): return lax.ppermute(value, axis, [(i, i ^ bit) for i in range(size)])  190 us
    ppermute x32, starting transfers between devices, swap(): return lax.ppermute(value, axis, [(i, i ^ bit) for i in range(size)])  48.6 us
    pallas_call x1, Pallas kernels, run_backward(): pl.pallas_call(functools.partial(attend_backward, halves), out_shape=(jax...  46.3 us
    pallas_call x2, Pallas kernels, run_forward(): pl.pallas_call(functools.partial(attend_forward, which), out_shape=(jax.S...  35.3 us
    pallas_call x2, Pallas kernels, run_dense(): pl.pallas_call(functools.partial(dense_chain, marks), out_shape=out_shape...  33.6 us
    all_to_all x4, starting transfers between devices, exchange(): return lax.all_to_all(blocks, 'tensor', 0, 0)  21.4 us
    dot_general x3, matrix products, dot(): lax.dot_general(left_side, right_side, dims, preferred_element_type=F32)  18.7 us
    pallas_call x2, Pallas kernels, run_weights(): pl.pallas_call(functools.partial(dense_weights, base, turns, halves), out...  17.2 us
  transfers between devices with their start and end apart: 38, of which 18 were waited for; matrix products, arithmetic and copies ran while one was open for 12% of the time, Pallas kernels for 27%

profile of v3, /device:TPU:0, one launch (start us, length us, event | category | flops | bytes accessed | tf_op | source)
XLA Modules:
  0.0 495.3 jit_solution(4260144634463284129)
XLA Ops:
  9.1 3.1 collective-permute-start.8
  12.3 8.0 %collective-permute-done.8 = bf16[1,96,1728]{2,1,0:T(8,128)(2,1)S(1)} collective-permute-done((bf16[1,96,1728]{2,1,0:T(8,128)(2,1)S(1)}, bf16[1,96,1728]{2,1,0:T(8,128)(2,1)S(1)}, u32[]{:S(2)}, u32[]{:S(2)}) %collective-permute-start.8) | collective-permute-done | bytes 331808 | tf_op jit(solution)/shard_map/ppermute | solution.py:537
  20.4 2.8 collective-permute-start.12
  24.7 63.9 %collective-permute-done.12 = bf16[2,96,1728]{2,1,0:T(8,128)(2,1)S(1)} collective-permute-done((bf16[2,96,1728]{2,1,0:T(8,128)(2,1)S(1)}, bf16[2,96,1728]{2,1,0:T(8,128)(2,1)S(1)}, u32[]{:S(2)}, u32[]{:S(2)}) %collective-permute-start.12) | collective-permute-done | bytes 663584 | tf_op jit(solution)/shard_map/ppermute | solution.py:537
  92.8 10.3 %collective-permute-done.13 = bf16[2,96,1728]{2,1,0:T(8,128)(2,1)S(1)} collective-permute-done((bf16[2,96,1728]{2,1,0:T(8,128)(2,1)S(1)}, bf16[2,96,1728]{2,1,0:T(8,128)(2,1)S(1)}, u32[]{:S(2)}, u32[]{:S(2)}) %collective-permute-start.13) | collective-permute-done | bytes 663584 | tf_op jit(solution)/shard_map/ppermute | solution.py:537
  111.7 13.0 %collective-permute-done.10 = bf16[4,96,1728]{2,1,0:T(8,128)(2,1)} collective-permute-done((bf16[4,96,1728]{2,1,0:T(8,128)(2,1)}, bf16[4,96,1728]{2,1,0:T(8,128)(2,1)}, u32[]{:S(2)}, u32[]{:S(2)}) %collective-permute-start.10) | collective-permute-done | bytes 1327136 | tf_op jit(solution)/shard_map/ppermute | solution.py:537
  126.3 23.3 %collective-permute-done.14 = bf16[4,96,1728]{2,1,0:T(8,128)(2,1)} collective-permute-done((bf16[4,96,1728]{2,1,0:T(8,128)(2,1)}, bf16[4,96,1728]{2,1,0:T(8,128)(2,1)}, u32[]{:S(2)}, u32[]{:S(2)}) %collective-permute-start.14) | collective-permute-done | bytes 1327136 | tf_op jit(solution)/shard_map/ppermute | solution.py:537
  149.6 2.5 constant_dynamic-update-slice_fusion.refs_2_
  153.2 1.9 maximum_select_fusion.1
  161.5 1.9 collective-permute-start.4
  163.4 1.7 collective-permute-done.4
  165.7 3.7 collective-permute-start.5
  171.2 4.6 collective-permute-start.6
  176.6 4.8 collective-permute-start.7
  182.3 2.6 maximum_select_fusion
  184.9 6.6 %fusion.3.qkv_ref = bf16[2048,768]{1,0:T(8,128)(2,1)} fusion(f32[768]{0:T(1024)S(1)} %add.142, bf16[768,768]{0,1:T(8,128)(2,1)} %maximum_select_fusion, bf16[1,2048,768]{2,1,0:T(8,128)(2,1)} %all-gather.3.cloned.1.call-done), kind=kOutput, calls=%fused_computation.5 | convolution fusion | flops 2419064832 | bytes 7474176 | tf_op jit(solution)/shard_map/dot_general | solution.py:30
  191.5 19.0 %attend_forward.2 = (bf16[4,384,128]{2,1,0:T(8,128)(2,1)}, f32[3,1,1024]{2,1,0:T(1,128)}) custom-call(s32[8]{0:T(128)} %get-tuple-element.237.low_ref, s32[8]{0:T(128)} %get-tuple-element.236.high_ref, bf16[2048,768]{1,0:T(8,128)(2,1)} %fusion.3.qkv_ref, s32[2048,1]{1,0:T(8,128)} %copy.78.seg_col_ref, s32[1,2048]{1,0:T(1,128)} %seg_row_ref.5), custom_call_target="tpu_custom_call" | custom-call | flops 1610612736 | bytes 5242880 | tf_op jit(solution)/shard_map/attend_forward/pallas_call | solution.py:218
  210.6 5.6 %all-to-all-start = ((bf16[4,384,128]{2,1,0:T(8,128)(2,1)}), bf16[4,384,128]{2,1,0:T(8,128)(2,1)S(1)}, u32[]{:S(2)}, u32[]{:S(2)}) async-start(bf16[4,384,128]{2,1,0:T(8,128)(2,1)} %get-tuple-element.80.refs_0_), calls=%async_computation | async-start | bytes 786432 | tf_op jit(solution)/shard_map/all_to_all | solution.py:665
  218.5 16.3 %attend_forward.3 = (bf16[4,384,128]{2,1,0:T(8,128)(2,1)}, f32[3,1,1024]{2,1,0:T(1,128)}) custom-call(s32[8]{0:T(128)} %get-tuple-element.237.low_ref, s32[8]{0:T(128)} %get-tuple-element.236.high_ref, bf16[2048,768]{1,0:T(8,128)(2,1)} %fusion.3.qkv_ref, s32[2048,1]{1,0:T(8,128)} %copy.78.seg_col_ref, s32[1,2048]{1,0:T(1,128)} %seg_row_ref.5), custom_call_target="tpu_custom_call" | custom-call | flops 1610612736 | bytes 5242880 | tf_op jit(solution)/shard_map/attend_forward/pallas_call | solution.py:218
  234.8 5.6 %all-to-all-start.1 = ((bf16[4,384,128]{2,1,0:T(8,128)(2,1)}), bf16[4,384,128]{2,1,0:T(8,128)(2,1)S(1)}, u32[]{:S(2)}, u32[]{:S(2)}) async-start(bf16[4,384,128]{2,1,0:T(8,128)(2,1)} %get-tuple-element.82.refs_1_), calls=%async_computation.1 | async-start | bytes 786432 | tf_op jit(solution)/shard_map/all_to_all | solution.py:665
  240.9 16.8 %dense_chain.2 = (bf16[256,768]{1,0:T(8,128)(2,1)}, f32[256,768]{1,0:T(8,128)}, bf16[4,384,128]{2,1,0:T(8,128)(2,1)}, bf16[256,768]{1,0:T(8,128)(2,1)}, bf16[256...) custom-call(s32[2]{0:T(128)} %pad_add_fusion.place_ref, ...), custom_call_target="tpu_custom_call" | custom-call | flops 5435817984 | bytes 18874368 | tf_op jit(solution)/shard_map/dense_chain/pallas_call | solution.py:410
  257.8 5.1 %all-to-all-start.2 = ((bf16[4,384,128]{2,1,0:T(8,128)(2,1)}), bf16[4,384,128]{2,1,0:T(8,128)(2,1)S(1)}, u32[]{:S(2)}, u32[]{:S(2)}) async-start(bf16[4,384,128]{2,1,0:T(8,128)(2,1)} %get-tuple-element.84), calls=%async_computation.2 | async-start | bytes 786432 | tf_op jit(solution)/shard_map/all_to_all | solution.py:665
  262.9 16.8 %dense_chain.3 = (bf16[256,768]{1,0:T(8,128)(2,1)}, f32[256,768]{1,0:T(8,128)}, bf16[4,384,128]{2,1,0:T(8,128)(2,1)}, bf16[256,768]{1,0:T(8,128)(2,1)}, bf16[256...) custom-call(s32[2]{0:T(128)} %pad_add_fusion.place_ref, ...), custom_call_target="tpu_custom_call" | custom-call | flops 5435817984 | bytes 18874368 | tf_op jit(solution)/shard_map/dense_chain/pallas_call | solution.py:410
  279.8 5.1 %all-to-all-start.3 = ((bf16[4,384,128]{2,1,0:T(8,128)(2,1)}), bf16[4,384,128]{2,1,0:T(8,128)(2,1)S(1)}, u32[]{:S(2)}, u32[]{:S(2)}) async-start(bf16[4,384,128]{2,1,0:T(8,128)(2,1)} %get-tuple-element.96), calls=%async_computation.3 | async-start | bytes 786432 | tf_op jit(solution)/shard_map/all_to_all | solution.py:665
  285.0 8.6 %dense_weights.2 = (bf16[8,96,1728]{2,1,0:T(8,128)(2,1)}, bf16[8,96,1728]{2,1,0:T(8,128)(2,1)}) custom-call(s32[2]{0:T(128)} %pad_add_fusion.place_ref, bf16[256,768]{1,0:T(8,128)(2,1)} %get-tuple-element.97.refs_0_, bf16[256,768]{1,0:T(8,128)(2,1)} %get-tuple-element.98.refs_1_, bf16[256,768]{1,0:T(8,128)(2,1)} %get-tuple-element.99.refs_2_, ...), custom_call_target="tpu_custom_call" | custom-call | flops 2717908992 | bytes 10485760 | tf_op jit(solution)/shard_map/dense_weights/pallas_call | solution.py:495
  293.7 8.6 %dense_weights.3 = (bf16[8,96,1728]{2,1,0:T(8,128)(2,1)}, bf16[8,96,1728]{2,1,0:T(8,128)(2,1)}) custom-call(s32[2]{0:T(128)} %pad_add_fusion.place_ref, bf16[256,768]{1,0:T(8,128)(2,1)} %get-tuple-element.97.refs_0_, bf16[256,768]{1,0:T(8,128)(2,1)} %get-tuple-element.98.refs_1_, bf16[256,768]{1,0:T(8,128)(2,1)} %get-tuple-element.99.refs_2_, ...), custom_call_target="tpu_custom_call" | custom-call | flops 2717908992 | bytes 10485760 | tf_op jit(solution)/shard_map/dense_weights/pallas_call | solution.py:495
  302.9 2.1 fusion.21
  307.3 3.5 fusion.6
  310.9 1.8 fusion.8
  315.1 46.3 %attend_backward.1 = (bf16[2048,768]{1,0:T(8,128)(2,1)}, f32[1,768]{1,0:T(1,128)}) custom-call(s32[8]{0:T(128)} %get-tuple-element.237.low_ref, s32[8]{0:T(128)} %get-tuple-element.236.high_ref, bf16[2048,768]{1,0:T(8,128)(2,1)} %fusion.3.qkv_ref, s32[2048,1]{1,0:T(8,128)} %copy.78.seg_col_ref, s32[1,2048]{1,0:T(1,128)} %seg_row_ref.5, ...), custom_call_target="tpu_custom_call" | custom-call | flops 8053063680 | bytes 10485760 | tf_op jit(solution)/shard_map/attend_backward/pallas_call | solution.py:255
  361.4 6.6 %convolution_convert_fusion = bf16[2048,768]{1,0:T(8,128)(2,1)} fusion(bf16[2048,768]{1,0:T(8,128)(2,1)} %get-tuple-element.124, bf16[768,768]{0,1:T(8,128)(2,1)} %maximum_select_fusion), kind=kOutput, calls=%fused_computation.1 | convolution fusion | flops 2417491968 | bytes 7471104 | tf_op jit(solution)/shard_map/dot_general | solution.py:30
  377.1 1.7 collective-permute-start.20
  381.3 5.5 %fusion.11 = bf16[768,768]{0,1:T(8,128)(2,1)S(1)} fusion(bf16[2048,768]{1,0:T(8,128)(2,1)} %get-tuple-element.124, bf16[1,2048,768]{2,1,0:T(8,128)(2,1)} %all-gather.3.cloned.1.call-done), kind=kOutput, calls=%fused_computation.17 | convolution fusion | flops 2416508928 | bytes 7471104 | tf_op jit(solution)/shard_map/dot_general | solution.py:30
  387.6 2.3 collective-permute-start.22
  390.1 1.9 collective-permute-done.22
  392.0 2.1 collective-permute-start.23
  396.2 2.4 collective-permute-done.23
  400.0 2.1 add_convert_fusion.5
  402.1 2.0 collective-permute-start.28
  404.1 3.4 collective-permute-done.24
  409.7 4.0 collective-permute-done.29
  413.8 2.2 fusion.17
  416.0 2.4 collective-permute-start.30
  421.9 2.1 collective-permute-start.27
  424.0 47.6 %collective-permute-done.30 = bf16[2,96,1728]{2,1,0:T(8,128)(2,1)} collective-permute-done((bf16[2,96,1728]{2,1,0:T(8,128)(2,1)}, bf16[2,96,1728]{2,1,0:T(8,128)(2,1)}, u32[]{:S(2)}, u32[]{:S(2)}) %collective-permute-start.30) | collective-permute-done | bytes 663584 | tf_op jit(solution)/shard_map/ppermute | solution.py:537
  471.6 1.8 fusion.14
  476.0 7.0 %collective-permute-done.31 = bf16[96,1728]{1,0:T(8,128)(2,1)S(1)} collective-permute-done((bf16[96,1728]{1,0:T(8,128)(2,1)S(1)}, bf16[96,1728]{1,0:T(8,128)(2,1)S(1)}, u32[]{:S(2)}, u32[]{:S(2)}) %collective-permute-start.31) | collective-permute-done | bytes 331808 | tf_op jit(solution)/shard_map/ppermute | solution.py:537
  484.6 2.4 fusion.10
  (189 shorter events, 59.1 us)
Async XLA Ops:
  7.2 177.7 %all-gather.3.cloned.1.call-start = ((), (), s32[]{:S(2)}) async-start(), calls=%async_computation.6 | async-start | bytes 3932160 | tf_op jit(solution)/shard_map/all_gather | solution.py:636
  9.1 11.2 %collective-permute-start.8 = (bf16[1,96,1728]{2,1,0:T(8,128)(2,1)S(1)}, bf16[1,96,1728]{2,1,0:T(8,128)(2,1)S(1)}, u32[]{:S(2)}, u32[]{:S(2)}) collective-permute-start(bf16[1,96,1728]{2,1,0:T(8,128)(2,1)S(1)} %maximum_bitcast_fusion.1), channel_id=1, source_target_pairs={{0,1},{1,0},{2,3},{3,2},{4,5},{5,4},{6,7},{7,6},{8,9},{9,8},{10,11... | collective-permute-start | bytes 995336 | tf_op jit(solution)/shard_map/ppermute | solution.py:537
  20.4 68.2 %collective-permute-start.12 = (bf16[2,96,1728]{2,1,0:T(8,128)(2,1)S(1)}, bf16[2,96,1728]{2,1,0:T(8,128)(2,1)S(1)}, u32[]{:S(2)}, u32[]{:S(2)}) collective-permute-start(bf16[2,96,1728]{2,1,0:T(8,128)(2,1)S(1)} %pad_maximum_fusion.3), channel_id=1, source_target_pairs={{0,2},{1,3},{2,0},{3,1},{4,6},{5,7},{6,4},{7,5},{8,10},{9,11},{10,... | collective-permute-start | bytes 1990664 | tf_op jit(solution)/shard_map/ppermute | solution.py:537
  23.2 66.7 %collective-permute-start.9 = (bf16[2,96,1728]{2,1,0:T(8,128)(2,1)S(1)}, bf16[2,96,1728]{2,1,0:T(8,128)(2,1)S(1)}, u32[]{:S(2)}, u32[]{:S(2)}) collective-permute-start(bf16[2,96,1728]{2,1,0:T(8,128)(2,1)S(1)} %pad_maximum_fusion.3), channel_id=1, source_target_pairs={{0,8},{4,12},{8,0},{12,4},{16,24},{20,28},{24,16},{28,20},{1,9},{5... | collective-permute-start | bytes 1990664 | tf_op jit(solution)/shard_map/ppermute | solution.py:537
  88.5 14.5 %collective-permute-start.13 = (bf16[2,96,1728]{2,1,0:T(8,128)(2,1)S(1)}, bf16[2,96,1728]{2,1,0:T(8,128)(2,1)S(1)}, u32[]{:S(2)}, u32[]{:S(2)}) collective-permute-start(bf16[2,96,1728]{2,1,0:T(8,128)(2,1)S(1)} %collective-permute-done.12), channel_id=1, source_target_pairs={{0,8},{4,12},{8,0},{12,4},{16,24},{20,28},{24,16},{28,20},{1,9},{5... | collective-permute-start | bytes 1990664 | tf_op jit(solution)/shard_map/ppermute | solution.py:537
  91.2 33.5 %collective-permute-start.10 = (bf16[4,96,1728]{2,1,0:T(8,128)(2,1)}, bf16[4,96,1728]{2,1,0:T(8,128)(2,1)}, u32[]{:S(2)}, u32[]{:S(2)}) collective-permute-start(bf16[4,96,1728]{2,1,0:T(8,128)(2,1)} %pad_maximum_fusion.1), channel_id=1, source_target_pairs={{0,16},{4,20},{8,24},{12,28},{16,0},{20,4},{24,8},{28,12},{1,17},{... | collective-permute-start | bytes 3981320 | tf_op jit(solution)/shard_map/ppermute | solution.py:537
  104.3 45.3 %collective-permute-start.14 = (bf16[4,96,1728]{2,1,0:T(8,128)(2,1)}, bf16[4,96,1728]{2,1,0:T(8,128)(2,1)}, u32[]{:S(2)}, u32[]{:S(2)}) collective-permute-start(bf16[4,96,1728]{2,1,0:T(8,128)(2,1)} %pad_maximum_fusion.2), channel_id=1, source_target_pairs={{0,16},{4,20},{8,24},{12,28},{16,0},{20,4},{24,8},{28,12},{1,17},{... | collective-permute-start | bytes 3981320 | tf_op jit(solution)/shard_map/ppermute | solution.py:537
  105.7 1.5 collective-permute-start
  108.4 44.9 %collective-permute-start.1 = (bf16[192,768]{0,1:T(8,128)(2,1)}, bf16[192,768]{0,1:T(8,128)(2,1)}, u32[]{:S(2)}, u32[]{:S(2)}) collective-permute-start(bf16[192,768]{0,1:T(8,128)(2,1)} %maximum_select_fusion.2), channel_id=1, source_target_pairs={{0,8},{4,12},{8,0},{12,4},{16,24},{20,28},{24,16},{28,20},{1,9},{5... | collective-permute-start | bytes 884744 | tf_op jit(solution)/shard_map/ppermute | solution.py:537
  126.2 25.9 %copy-start = (bf16[8,96,1728]{2,1,0:T(8,128)(2,1)}, bf16[8,96,1728]{2,1,0:T(8,128)(2,1)S(1)}, u32[]{:S(2)}) copy-start(bf16[8,96,1728]{2,1,0:T(8,128)(2,1)S(1)} %pad_maximum_fusion.refs_0_) | copy-start | bytes 7962628
  126.2 25.9 %copy-start.22 = (s32[1,512]{1,0:T(1,128)S(1)}, s32[1,512]{1,0:T(1,128)}, u32[]{:S(2)}) copy-start(s32[1,512]{1,0:T(1,128)} %param.22) | copy-start | bytes 6148
  126.2 114.7 %collective-permute-start.11 = (bf16[8,96,1728]{2,1,0:T(8,128)(2,1)S(1)}, bf16[8,96,1728]{2,1,0:T(8,128)(2,1)}, u32[]{:S(2)}, u32[]{:S(2)}) collective-permute-start(bf16[8,96,1728]{2,1,0:T(8,128)(2,1)S(1)} %pad_maximum_fusion.refs_0_), channel_id=1, source_target_pairs={{0,4},{4,0},{8,12},{12,8},{16,20},{20,16},{24,28},{28,24},{1,5},{5... | collective-permute-start | bytes 7962632 | tf_op jit(solution)/shard_map/ppermute | solution.py:537
  152.1 88.8 %collective-permute-start.15 = (bf16[8,96,1728]{2,1,0:T(8,128)(2,1)}, bf16[8,96,1728]{2,1,0:T(8,128)(2,1)}, u32[]{:S(2)}, u32[]{:S(2)}) collective-permute-start(bf16[8,96,1728]{2,1,0:T(8,128)(2,1)} %constant_dynamic-update-slice_fusion.refs_2_), channel_id=1, source_target_pairs={{0,4},{4,0},{8,12},{12,8},{16,20},{20,16},{24,28},{28,24},{1,5},{5... | collective-permute-start | bytes 7962632 | tf_op jit(solution)/shard_map/ppermute | solution.py:537
  152.7 7.5 %collective-permute-start.3 = (f32[1,1]{1,0:T(1,128)}, f32[1,1]{1,0:T(1,128)}, u32[]{:S(2)}, u32[]{:S(2)}) collective-permute-start(f32[1,1]{1,0:T(1,128)} %bitcast.6), channel_id=1, source_target_pairs={{0,4},{4,0},{8,12},{12,8},{16,20},{20,16},{24,28},{28,24},{1,5},{5... | collective-permute-start | bytes 20 | tf_op jit(solution)/shard_map/ppermute | solution.py:537
  155.1 27.2 %collective-permute-start.2 = (bf16[384,768]{0,1:T(8,128)(2,1)S(1)}, bf16[384,768]{0,1:T(8,128)(2,1)}, u32[]{:S(2)}, u32[]{:S(2)}) collective-permute-start(bf16[384,768]{0,1:T(8,128)(2,1)S(1)} %maximum_select_fusion.1), channel_id=1, source_target_pairs={{0,16},{4,20},{8,24},{12,28},{16,0},{20,4},{24,8},{28,12},{1,17},{... | collective-permute-start | bytes 1769480 | tf_op jit(solution)/shard_map/ppermute | solution.py:537
  161.5 3.6 collective-permute-start.4
  165.7 4.8 collective-permute-start.5
  171.2 4.7 collective-permute-start.6
  176.6 5.0 %collective-permute-start.7 = (f32[1,1]{1,0:T(1,128)}, f32[1,1]{1,0:T(1,128)}, u32[]{:S(2)}, u32[]{:S(2)}) collective-permute-start(f32[1,1]{1,0:T(1,128)} %add.139), channel_id=1, source_target_pairs={{0,2},{1,3},{2,0},{3,1},{4,6},{5,7},{6,4},{7,5},{8,10},{9,11},{10,... | collective-permute-start | bytes 20 | tf_op jit(solution)/shard_map/ppermute | solution.py:537
  191.5 25.6 %copy-start.24 = (bf16[768]{0:T(1024)(128)(2,1)S(1)}, bf16[768]{0:T(1024)(128)(2,1)}, u32[]{:S(2)}) copy-start(bf16[768]{0:T(1024)(128)(2,1)} %param.33) | copy-start | bytes 4612
  191.5 25.6 %copy-start.25 = (bf16[768]{0:T(1024)(128)(2,1)S(1)}, bf16[768]{0:T(1024)(128)(2,1)}, u32[]{:S(2)}) copy-start(bf16[768]{0:T(1024)(128)(2,1)} %param.36) | copy-start | bytes 4612
  191.5 25.6 %copy-start.26 = (bf16[768]{0:T(1024)(128)(2,1)S(1)}, bf16[768]{0:T(1024)(128)(2,1)}, u32[]{:S(2)}) copy-start(bf16[768]{0:T(1024)(128)(2,1)} %param.37) | copy-start | bytes 4612
  191.5 25.6 %copy-start.27 = (bf16[768]{0:T(1024)(128)(2,1)S(1)}, bf16[768]{0:T(1024)(128)(2,1)}, u32[]{:S(2)}) copy-start(bf16[768]{0:T(1024)(128)(2,1)} %param.35) | copy-start | bytes 4612
  191.5 25.6 %copy-start.28 = (bf16[768]{0:T(1024)(128)(2,1)S(1)}, bf16[768]{0:T(1024)(128)(2,1)}, u32[]{:S(2)}) copy-start(bf16[768]{0:T(1024)(128)(2,1)} %param.38) | copy-start | bytes 4612
  191.5 25.6 %copy-start.29 = (bf16[768]{0:T(1024)(128)(2,1)S(1)}, bf16[768]{0:T(1024)(128)(2,1)}, u32[]{:S(2)}) copy-start(bf16[768]{0:T(1024)(128)(2,1)} %param.39) | copy-start | bytes 4612
  191.5 26.3 %copy-start.23 = (bf16[3072]{0:T(1024)(128)(2,1)S(1)}, bf16[3072]{0:T(1024)(128)(2,1)}, u32[]{:S(2)}) copy-start(bf16[3072]{0:T(1024)(128)(2,1)} %param.34) | copy-start | bytes 18436
  210.6 24.2 %all-to-all-start = ((bf16[4,384,128]{2,1,0:T(8,128)(2,1)}), bf16[4,384,128]{2,1,0:T(8,128)(2,1)S(1)}, u32[]{:S(2)}, u32[]{:S(2)}) async-start(bf16[4,384,128]{2,1,0:T(8,128)(2,1)} %get-tuple-element.80.refs_0_), calls=%async_computation | async-start | bytes 786432 | tf_op jit(solution)/shard_map/all_to_all | solution.py:665
  234.8 23.0 %all-to-all-start.1 = ((bf16[4,384,128]{2,1,0:T(8,128)(2,1)}), bf16[4,384,128]{2,1,0:T(8,128)(2,1)S(1)}, u32[]{:S(2)}, u32[]{:S(2)}) async-start(bf16[4,384,128]{2,1,0:T(8,128)(2,1)} %get-tuple-element.82.refs_1_), calls=%async_computation.1 | async-start | bytes 786432 | tf_op jit(solution)/shard_map/all_to_all | solution.py:665
  257.8 21.9 %all-to-all-start.2 = ((bf16[4,384,128]{2,1,0:T(8,128)(2,1)}), bf16[4,384,128]{2,1,0:T(8,128)(2,1)S(1)}, u32[]{:S(2)}, u32[]{:S(2)}) async-start(bf16[4,384,128]{2,1,0:T(8,128)(2,1)} %get-tuple-element.84), calls=%async_computation.2 | async-start | bytes 786432 | tf_op jit(solution)/shard_map/all_to_all | solution.py:665
  279.8 14.0 %all-to-all-start.3 = ((bf16[4,384,128]{2,1,0:T(8,128)(2,1)}), bf16[4,384,128]{2,1,0:T(8,128)(2,1)S(1)}, u32[]{:S(2)}, u32[]{:S(2)}) async-start(bf16[4,384,128]{2,1,0:T(8,128)(2,1)} %get-tuple-element.96), calls=%async_computation.3 | async-start | bytes 786432 | tf_op jit(solution)/shard_map/all_to_all | solution.py:665
  284.9 199.8 %reduce-scatter.2.cloned.1.call-start = ((), (), s32[]{:S(2)}) async-start(), calls=%async_computation.5 | async-start | bytes 3932160 | tf_op jit(solution)/shard_map/reduce_scatter | solution.py:731
  293.7 12.0 %collective-permute-start.17 = (bf16[4,2,96,1728]{3,2,1,0:T(8,128)(2,1)}, bf16[4,2,96,1728]{3,2,1,0:T(8,128)(2,1)S(1)}, u32[]{:S(2)}, u32[]{:S(2)}) collective-permute-start(bf16[4,2,96,1728]{3,2,1,0:T(8,128)(2,1)} %bitcast.144), channel_id=1, source_target_pairs={{0,4},{4,0},{8,12},{12,8},{16,20},{20,16},{24,28},{28,24},{1,5},{5... | collective-permute-start | bytes 7962632 | tf_op jit(solution)/shard_map/ppermute | solution.py:537
  302.4 8.5 %collective-permute-start.16 = (bf16[4,2,96,1728]{3,2,1,0:T(8,128)(2,1)}, bf16[4,2,96,1728]{3,2,1,0:T(8,128)(2,1)S(1)}, u32[]{:S(2)}, u32[]{:S(2)}) collective-permute-start(bf16[4,2,96,1728]{3,2,1,0:T(8,128)(2,1)} %bitcast.145), channel_id=1, source_target_pairs={{0,4},{4,0},{8,12},{12,8},{16,20},{20,16},{24,28},{28,24},{1,5},{5... | collective-permute-start | bytes 7962632 | tf_op jit(solution)/shard_map/ppermute | solution.py:537
  312.7 48.7 %collective-permute-start.18 = (bf16[2,2,96,1728]{3,2,1,0:T(8,128)(2,1)}, bf16[2,2,96,1728]{3,2,1,0:T(8,128)(2,1)}, u32[]{:S(2)}, u32[]{:S(2)}) collective-permute-start(bf16[2,2,96,1728]{3,2,1,0:T(8,128)(2,1)} %get-tuple-element.121), channel_id=1, source_target_pairs={{0,8},{4,12},{8,0},{12,4},{16,24},{20,28},{24,16},{28,20},{1,9},{5... | collective-permute-start | bytes 3981320 | tf_op jit(solution)/shard_map/ppermute | solution.py:537
  313.0 48.4 %collective-permute-start.19 = (bf16[2,2,96,1728]{3,2,1,0:T(8,128)(2,1)}, bf16[2,2,96,1728]{3,2,1,0:T(8,128)(2,1)}, u32[]{:S(2)}, u32[]{:S(2)}) collective-permute-start(bf16[2,2,96,1728]{3,2,1,0:T(8,128)(2,1)} %get-tuple-element.123), channel_id=1, source_target_pairs={{0,16},{4,20},{8,24},{12,28},{16,0},{20,4},{24,8},{28,12},{1,17},{... | collective-permute-start | bytes 3981320 | tf_op jit(solution)/shard_map/ppermute | solution.py:537
  361.4 17.4 %copy-start.11 = (bf16[256,768]{1,0:T(8,128)(2,1)S(1)}, bf16[256,768]{1,0:T(8,128)(2,1)}, u32[]{:S(2)}) copy-start(bf16[256,768]{1,0:T(8,128)(2,1)} %get-tuple-element.81) | copy-start | bytes 1179652
  377.1 2.9 collective-permute-start.20
  381.2 5.6 %collective-permute-start.21 = (f32[84,128]{1,0:T(8,128)S(1)}, f32[84,128]{1,0:T(8,128)S(1)}, u32[]{:S(2)}, u32[]{:S(2)}) collective-permute-start(f32[84,128]{1,0:T(8,128)S(1)} %fusion.20), channel_id=1, source_target_pairs={{0,8},{4,12},{8,0},{12,4},{16,24},{20,28},{24,16},{28,20},{1,9},{5... | collective-permute-start | bytes 129032 | tf_op jit(solution)/shard_map/ppermute | solution.py:537
  387.6 4.4 collective-permute-start.22
  390.0 17.5 %collective-permute-start.25 = (bf16[4,96,768]{2,1,0:T(8,128)(2,1)S(1)}, bf16[4,96,768]{2,1,0:T(8,128)(2,1)S(1)}, u32[]{:S(2)}, u32[]{:S(2)}) collective-permute-start(bf16[4,96,768]{2,1,0:T(8,128)(2,1)S(1)} %dynamic-slice_bitcast_fusion), channel_id=1, source_target_pairs={{0,4},{4,0},{8,12},{12,8},{16,20},{20,16},{24,28},{28,24},{1,5},{5... | collective-permute-start | bytes 1769480 | tf_op jit(solution)/shard_map/ppermute | solution.py:537
  392.0 6.6 %collective-permute-start.23 = (f32[84,128]{1,0:T(8,128)S(1)}, f32[84,128]{1,0:T(8,128)S(1)}, u32[]{:S(2)}, u32[]{:S(2)}) collective-permute-start(f32[84,128]{1,0:T(8,128)S(1)} %add.153), channel_id=1, source_target_pairs={{0,1},{1,0},{2,3},{3,2},{4,5},{5,4},{6,7},{7,6},{8,9},{9,8},{10,11... | collective-permute-start | bytes 129032 | tf_op jit(solution)/shard_map/ppermute | solution.py:537
  395.3 18.4 %collective-permute-start.29 = (bf16[1,2,96,1728]{3,2,1,0:T(8,128)(2,1)S(1)}, bf16[1,2,96,1728]{3,2,1,0:T(8,128)(2,1)S(1)}, u32[]{:S(2)}, u32[]{:S(2)}) collective-permute-start(bf16[1,2,96,1728]{3,2,1,0:T(8,128)(2,1)S(1)} %add_convert_fusion.2), channel_id=1, source_target_pairs={{0,8},{4,12},{8,0},{12,4},{16,24},{20,28},{24,16},{28,20},{1,9},{5... | collective-permute-start | bytes 1990664 | tf_op jit(solution)/shard_map/ppermute | solution.py:537
  398.6 8.9 %collective-permute-start.24 = (f32[84,128]{1,0:T(8,128)S(1)}, f32[84,128]{1,0:T(8,128)S(1)}, u32[]{:S(2)}, u32[]{:S(2)}) collective-permute-start(f32[84,128]{1,0:T(8,128)S(1)} %add.154), channel_id=1, source_target_pairs={{0,2},{1,3},{2,0},{3,1},{4,6},{5,7},{6,4},{7,5},{8,10},{9,11},{10,... | collective-permute-start | bytes 129032 | tf_op jit(solution)/shard_map/ppermute | solution.py:537
  402.1 21.9 %collective-permute-start.28 = (bf16[1,2,96,1728]{3,2,1,0:T(8,128)(2,1)}, bf16[1,2,96,1728]{3,2,1,0:T(8,128)(2,1)}, u32[]{:S(2)}, u32[]{:S(2)}) collective-permute-start(bf16[1,2,96,1728]{3,2,1,0:T(8,128)(2,1)} %add_convert_fusion.5), channel_id=1, source_target_pairs={{0,16},{4,20},{8,24},{12,28},{16,0},{20,4},{24,8},{28,12},{1,17},{... | collective-permute-start | bytes 1990664 | tf_op jit(solution)/shard_map/ppermute | solution.py:537
  408.4 12.4 %collective-permute-start.26 = (bf16[2,96,768]{2,1,0:T(8,128)(2,1)}, bf16[2,96,768]{2,1,0:T(8,128)(2,1)}, u32[]{:S(2)}, u32[]{:S(2)}) collective-permute-start(bf16[2,96,768]{2,1,0:T(8,128)(2,1)} %dynamic-slice_bitcast_fusion.1), channel_id=1, source_target_pairs={{0,8},{4,12},{8,0},{12,4},{16,24},{20,28},{24,16},{28,20},{1,9},{5... | collective-permute-start | bytes 884744 | tf_op jit(solution)/shard_map/ppermute | solution.py:537
  416.0 55.6 %collective-permute-start.30 = (bf16[2,96,1728]{2,1,0:T(8,128)(2,1)}, bf16[2,96,1728]{2,1,0:T(8,128)(2,1)}, u32[]{:S(2)}, u32[]{:S(2)}) collective-permute-start(bf16[2,96,1728]{2,1,0:T(8,128)(2,1)} %fusion.17), channel_id=1, source_target_pairs={{0,2},{1,3},{2,0},{3,1},{4,6},{5,7},{6,4},{7,5},{8,10},{9,11},{10,... | collective-permute-start | bytes 1990664 | tf_op jit(solution)/shard_map/ppermute | solution.py:537
  421.9 51.6 %collective-permute-start.27 = (bf16[1,96,768]{2,1,0:T(8,128)(2,1)S(1)}, bf16[1,96,768]{2,1,0:T(8,128)(2,1)S(1)}, u32[]{:S(2)}, u32[]{:S(2)}) collective-permute-start(bf16[1,96,768]{2,1,0:T(8,128)(2,1)S(1)} %constant_dynamic-slice_fusion), channel_id=1, source_target_pairs={{0,16},{4,20},{8,24},{12,28},{16,0},{20,4},{24,8},{28,12},{1,17},{... | collective-permute-start | bytes 442376 | tf_op jit(solution)/shard_map/ppermute | solution.py:537
  473.5 9.5 %collective-permute-start.31 = (bf16[96,1728]{1,0:T(8,128)(2,1)S(1)}, bf16[96,1728]{1,0:T(8,128)(2,1)S(1)}, u32[]{:S(2)}, u32[]{:S(2)}) collective-permute-start(bf16[96,1728]{1,0:T(8,128)(2,1)S(1)} %slice_bitcast_fusion), channel_id=1, source_target_pairs={{0,1},{1,0},{2,3},{3,2},{4,5},{5,4},{6,7},{7,6},{8,9},{9,8},{10,11... | collective-permute-start | bytes 995336 | tf_op jit(solution)/shard_map/ppermute | solution.py:537
  (20 other events, 154.1 us)
Sparse Core Ops, SparseCore 0:
  12.4 91.2 all-gather.2
  379.8 79.1 reduce-scatter.1

commit v4 on v3

--- a/solution.py
+++ b/solution.py
@@ -119,29 +119,29 @@
 
 
 def attend_backward(
-    halves, low_ref, high_ref, qkv_ref, seg_col_ref, seg_row_ref, *refs
+    which, low_ref, high_ref, qkv_ref, seg_col_ref, seg_row_ref, ctx_ref, grad_ref, lse_ref, *refs
 ):
-    ctx_refs, grad_refs, lse_refs = refs[:halves], refs[halves : 2 * halves], refs[2 * halves : 3 * halves]
-    out_ref, sums_ref, dkv = refs[3 * halves :]
+    halves, half = which
+    last = half == halves - 1
+    earlier, refs = refs[:half], refs[half:]
+    if half > 0:
+        before_ref, refs = refs[0], refs[1:]
+    if last:
+        out_ref, sums_ref, dkv = refs
+    else:
+        dkv, query_ref = refs
     heads = dkv.shape[0]
-    qb = pl.program_id(0)
-    half = qb % halves
-
-    def choose(options):
-        value = options[0][...]
-        for which in range(1, halves):
-            value = jnp.where(half == which, options[which][...], value)
-        return value
-
-    @pl.when(qb == 0)
+    step_index = pl.program_id(0)
+    qb = step_index * halves + half
+
+    @pl.when(step_index == 0)
     def _():
-        dkv[...] = jnp.zeros_like(dkv)
-        sums_ref[...] = jnp.zeros_like(sums_ref)
+        dkv[...] = before_ref[...] if half > 0 else jnp.zeros_like(dkv)
 
     rows = pl.ds(pl.multiple_of(qb * BLOCK, BLOCK), BLOCK)
     right = lane_is_right(BLOCK)
-    arrived = choose(grad_refs)[0]
-    product = arrived.astype(F32) * choose(ctx_refs)[0].astype(F32)
+    arrived = grad_ref[0]
+    product = arrived.astype(F32) * ctx_ref[0].astype(F32)
     upper = product.astype(BF16)
     lower = (product - upper.astype(F32)).astype(BF16)
     pick = (
@@ -166,7 +166,7 @@
         queries.append(qkv_ref[rows, SLAB * h : SLAB * h + 2 * DH] * jnp.asarray(SCALE, BF16))
         pairs.append(jnp.concatenate([queries[h], grads[h]], axis=0))
     seg_q = seg_row_ref[...]
-    lses = choose(lse_refs)
+    lses = lse_ref[...]
     low, high = low_ref[qb], high_ref[qb]
 
     def step(kb, accs):
@@ -187,15 +187,25 @@
     accs = lax.fori_loop(low, high, step, tuple(zero for _ in range(heads)))
     for h in range(heads):
         query_grad = jnp.where(right, 0.0, accs[h] * SCALE).astype(BF16)
-        out_ref[rows, SLAB * h : SLAB * h + 2 * DH] = query_grad
-        sums_ref[:, SLAB * h : SLAB * h + 2 * DH] += column_sum(query_grad.astype(F32))
-
-    @pl.when(qb == pl.num_programs(0) - 1)
-    def _():
-        for h in range(heads):
-            pair_grad = dkv[h].astype(BF16)
-            out_ref[:, SLAB * h + 2 * DH : SLAB * (h + 1)] = pair_grad
-            sums_ref[:, SLAB * h + 2 * DH : SLAB * (h + 1)] = column_sum(pair_grad.astype(F32))
+        if last:
+            out_ref[rows, SLAB * h : SLAB * h + 2 * DH] = query_grad
+        else:
+            query_ref[0, :, 2 * DH * h : 2 * DH * (h + 1)] = query_grad
+
+    if last:
+
+        @pl.when(step_index == pl.num_programs(0) - 1)
+        def _():
+            for h in range(heads):
+                at = SLAB * h
+                for other, ref in enumerate(earlier):
+                    for block in range(ref.shape[0]):
+                        start = (block * halves + other) * BLOCK
+                        out_ref[start : start + BLOCK, at : at + 2 * DH] = ref[
+                            block, :, 2 * DH * h : 2 * DH * (h + 1)
+                        ]
+                out_ref[:, at + 2 * DH : at + SLAB] = dkv[h].astype(BF16)
+                sums_ref[:, at : at + SLAB] = column_sum(out_ref[:, at : at + SLAB].astype(F32))
 
 
 def document_blocks(segment_row):
@@ -247,43 +257,65 @@
     )(*bounds, qkv, seg_col, seg_row)
 
 
-def run_backward(bounds, qkv, seg_col, seg_row, ctxs, grads, lses):
+def run_backward(which, bounds, qkv, seg_col, seg_row, ctx, grad, lse, earlier, before):
+    halves, half = which
     seq_len, width = qkv.shape
     heads = width // SLAB
-    halves = len(ctxs)
-    packed = pl.BlockSpec((1, PACKED, 2 * DH), lambda q, *_: (q // halves, 0, 0))
-    return pl.pallas_call(
-        functools.partial(attend_backward, halves),
-        out_shape=(
+    steps = seq_len // BLOCK // halves
+    packed = pl.BlockSpec((1, PACKED, 2 * DH), lambda q, *_: (q, 0, 0))
+
+    def fixed(shape, **more):
+        return pl.BlockSpec(shape, lambda q, *_: (0,) * len(shape), **more)
+
+    once = {"pipeline_mode": pl.Buffered(1)}
+    gathered = (heads, seq_len, 2 * DH)
+    carried = [fixed(value.shape, **once) for value in earlier]
+    carried += [fixed(gathered, **once)] * len(before)
+    if half == halves - 1:
+        out_shape = (
             jax.ShapeDtypeStruct((seq_len, width), BF16),
             jax.ShapeDtypeStruct((1, width), F32),
-        ),
+        )
+        out_specs = (fixed((seq_len, width)), fixed((1, width)))
+        scratch = [pltpu.VMEM(gathered, F32)]
+    else:
+        out_shape = (
+            jax.ShapeDtypeStruct(gathered, F32),
+            jax.ShapeDtypeStruct((steps, BLOCK, heads * 2 * DH), BF16),
+        )
+        out_specs = (
+            fixed(gathered),
+            pl.BlockSpec((1, BLOCK, heads * 2 * DH), lambda q, *_: (q, 0, 0)),
+        )
+        scratch = []
+    return pl.pallas_call(
+        functools.partial(attend_backward, which),
+        out_shape=out_shape,
         grid_spec=pltpu.PrefetchScalarGridSpec(
             num_scalar_prefetch=2,
-            grid=(seq_len // BLOCK,),
+            grid=(steps,),
             in_specs=[
-                pl.BlockSpec((seq_len, width), lambda q, *_: (0, 0), pipeline_mode=pl.Buffered(1)),
-                pl.BlockSpec((seq_len, 1), lambda q, *_: (0, 0)),
-                pl.BlockSpec((1, BLOCK), lambda q, *_: (0, q)),
+                fixed((seq_len, width), **once),
+                fixed((seq_len, 1)),
+                pl.BlockSpec((1, BLOCK), lambda q, *_: (0, q * halves + half)),
+                packed,
+                packed,
+                pl.BlockSpec((heads, 1, BLOCK), lambda q, *_: (0, 0, q)),
             ]
-            + [packed] * (2 * halves)
-            + [pl.BlockSpec((heads, 1, BLOCK), lambda q, *_: (0, 0, q // halves))] * halves,
-            out_specs=(
-                pl.BlockSpec((seq_len, width), lambda q, *_: (0, 0)),
-                pl.BlockSpec((1, width), lambda q, *_: (0, 0)),
-            ),
-            scratch_shapes=[pltpu.VMEM((heads, seq_len, 2 * DH), F32)],
+            + carried,
+            out_specs=out_specs,
+            scratch_shapes=scratch,
         ),
         compiler_params=pltpu.CompilerParams(
             dimension_semantics=("arbitrary",), vmem_limit_bytes=VMEM_LIMIT
         ),
         cost_estimate=pl.CostEstimate(
-            flops=heads * seq_len * seq_len * 640,
+            flops=heads * seq_len * seq_len * 640 // halves,
             bytes_accessed=10 << 20,
-            transcendentals=heads * seq_len * seq_len // 3,
+            transcendentals=heads * seq_len * seq_len // 3 // halves,
         ),
         name="attend_backward",
-    )(*bounds, qkv, seg_col, seg_row, *ctxs, *grads, *lses)
+    )(*bounds, qkv, seg_col, seg_row, ctx, grad, lse, *earlier, *before)
 
 
 def dense_chain(
@@ -297,7 +329,7 @@
     ) = refs[len(marks) :]
     parts, _, head_cols = w_out.shape
     hidden_cols = w_in.shape[2]
-    rank, index = place_ref[0], place_ref[1]
+    index = place_ref[parts]
     groups = (
         (2 * hidden_cols, head_cols, w_out),
         (0, hidden_cols, w_in),
@@ -325,7 +357,7 @@
     attention = jnp.zeros(in_ref.shape, F32)
     for slot in range(parts):
         arrive(0, slot)
-        attention = attention + dot(unpack(ctx_ref[rank ^ slot]), w_out[slot], NT)
+        attention = attention + dot(unpack(ctx_ref[place_ref[slot]]), w_out[slot], NT)
     first_exact, normed_one, inverse_one = norm_forward(
         in_ref[...].astype(F32) + attention + vec(0), vec(1), vec(2)
     )
@@ -333,7 +365,7 @@
     first_ref[...] = first
 
     def up(slot, branch):
-        t = rank ^ slot
+        t = place_ref[slot]
         arrive(1, slot)
         hidden = dot(first, w_in[slot]) + inner_bias_ref[t]
         bend = 0.5 * (1.0 + lax.erf(hidden * ROOT_HALF))
@@ -358,7 +390,7 @@
     sums_ref[3:4, :] = column_sum(out_grad)
 
     def down(slot, back):
-        t = rank ^ slot
+        t = place_ref[slot]
         hidden_grad = (dot(branch_grad, w_up[slot]) * slope[slot]).astype(BF16)
         hidden_grad_ref[t] = hidden_grad
         inner_sums_ref[t] = column_sum(hidden_grad.astype(F32))
@@ -376,7 +408,7 @@
     middle = BLOCK // 2
     for slot in range(parts):
         back = dot(attn_grad, w_out[slot]).astype(BF16)
-        ctx_grad_ref[rank ^ slot] = pack(
+        ctx_grad_ref[place_ref[slot]] = pack(
             back[:, : 2 * DH], back[:middle, 2 * DH :], back[middle:, 2 * DH :]
         )
 
@@ -443,14 +475,16 @@
     )(place, ratio, ctx, rows_in, teacher, cotangent, valid, vecs, inner_bias, *pieces)
 
 
-def dense_weights(base, turns, halves, place_ref, *refs):
+def dense_weights(turns, halves, place_ref, *refs):
     firsts, branch_grads, attn_grads, acts, hidden_grads, ctxs = (
         refs[k * halves : (k + 1) * halves] for k in range(6)
     )
-    outs = refs[6 * halves : 6 * halves + len(turns)]
-    turned, whole, sems = refs[6 * halves + len(turns) :]
+    outs = refs[6 * halves : -3]
+    turned, whole, sems = refs[-3:]
     step = pl.program_id(0)
-    slots = pl.num_programs(0)
+    slots = whole.shape[0]
+    teams = len(outs) // len(turns)
+    each = slots // teams
 
     @pl.when(step == 0)
     def _():
@@ -466,60 +500,103 @@
     whole[step, :, hidden_cols : 2 * hidden_cols] = dot(turned[1], both(acts)).astype(BF16)
     ctx = jnp.concatenate([unpack(source[0]) for source in ctxs], axis=0)
     whole[step, :, 2 * hidden_cols :] = dot(turned[2], ctx).astype(BF16)
-    for out, order in zip(outs, turns):
-        block = out.shape[1]
-        for at, turn in enumerate(order):
-            offset = pl.multiple_of((place_ref[1] ^ turn) * block, block)
-            pltpu.make_async_copy(
-                whole.at[step, pl.ds(offset, block), :],
-                out.at[at * slots + step],
-                sems.at[step],
-            ).start()
+    for team in range(teams):
+
+        @pl.when(step // each == team)
+        def _():
+            for out, orders in zip(outs[team * len(turns) : (team + 1) * len(turns)], turns):
+                block = out.shape[1]
+                for at, turn in enumerate(orders[team]):
+                    offset = pl.multiple_of((place_ref[slots] ^ turn) * block, block)
+                    pltpu.make_async_copy(
+                        whole.at[step, pl.ds(offset, block), :],
+                        out.at[at * each + step - team * each],
+                        sems.at[step],
+                    ).start()
 
     @pl.when(step == slots - 1)
     def _():
-        for slot in range(whole.shape[0]):
+        for slot in range(slots):
             pltpu.make_async_copy(whole.at[slot], whole.at[slot], sems.at[slot]).wait()
 
 
-def run_weights(base, slots, turns, block, place, firsts, branch_grads, attn_grads, acts, hidden_grads, ctxs):
+def run_weights(turns, teams, block, place, firsts, branch_grads, attn_grads, acts, hidden_grads, ctxs):
     parts, _, hidden_cols = acts[0].shape
     halves = len(acts)
     width = firsts[0].shape[1]
     columns = 2 * hidden_cols + 3 * DH
 
     def by_slot(rows, size):
-        return pl.BlockSpec((1, rows, size), lambda s, place: (place[0] ^ (base + s), 0, 0))
+        return pl.BlockSpec((1, rows, size), lambda s, place: (place[s], 0, 0))
 
     fixed = pl.BlockSpec((BLOCK, width), lambda s, place: (0, 0))
+    outs = tuple(
+        jax.ShapeDtypeStruct((len(orders[0]) * parts // teams, block, columns), BF16) for orders in turns
+    ) * teams
     return pl.pallas_call(
-        functools.partial(dense_weights, base, turns, halves),
-        out_shape=tuple(
-            jax.ShapeDtypeStruct((len(order) * slots, block, columns), BF16) for order in turns
-        ),
+        functools.partial(dense_weights, turns, halves),
+        out_shape=outs,
         grid_spec=pltpu.PrefetchScalarGridSpec(
             num_scalar_prefetch=1,
-            grid=(slots,),
+            grid=(parts,),
             in_specs=[fixed] * (3 * halves)
             + [by_slot(BLOCK, hidden_cols)] * (2 * halves)
             + [by_slot(PACKED, 2 * DH)] * halves,
-            out_specs=tuple(pl.BlockSpec(memory_space=pl.ANY) for _ in turns),
+            out_specs=tuple(pl.BlockSpec(memory_space=pl.ANY) for _ in outs),
             scratch_shapes=[
                 pltpu.VMEM((3, width, halves * BLOCK), BF16),
-                pltpu.VMEM((slots, width, columns), BF16),
-                pltpu.SemaphoreType.DMA((slots,)),
+                pltpu.VMEM((parts, width, columns), BF16),
+                pltpu.SemaphoreType.DMA((parts,)),
             ],
         ),
         compiler_params=pltpu.CompilerParams(
             dimension_semantics=("arbitrary",), vmem_limit_bytes=VMEM_LIMIT
         ),
         cost_estimate=pl.CostEstimate(
-            flops=2 * halves * BLOCK * width * columns * slots,
-            bytes_accessed=5 * slots << 20,
+            flops=2 * halves * BLOCK * width * columns * parts,
+            bytes_accessed=20 << 20,
             transcendentals=0,
         ),
         name="dense_weights",
     )(place, *firsts, *branch_grads, *attn_grads, *acts, *hidden_grads, *ctxs)
+
+
+def finish_dense(left_ref, right_ref, inner_ref, outer_ref, output_ref):
+    hidden_cols = inner_ref.shape[1]
+    summed = left_ref[...].astype(F32) + right_ref[...].astype(F32)
+    inner_ref[...] = summed[:, :hidden_cols]
+    outer_ref[...] = summed[:, hidden_cols : 2 * hidden_cols]
+    output_ref[...] = jnp.transpose(summed[:, 2 * hidden_cols :])
+
+
+def run_finish_dense(left_side, right_side, hidden_cols, head_cols):
+    rows = left_side.shape[0]
+    return pl.pallas_call(
+        finish_dense,
+        out_shape=(
+            jax.ShapeDtypeStruct((rows, hidden_cols), F32),
+            jax.ShapeDtypeStruct((rows, hidden_cols), F32),
+            jax.ShapeDtypeStruct((head_cols, rows), F32),
+        ),
+        name="finish_dense",
+    )(left_side, right_side)
+
+
+def finish_heads(left_ref, right_ref, query_ref, key_ref, value_ref):
+    summed = left_ref[...].astype(F32) + right_ref[...].astype(F32)
+    heads = summed.shape[1] // SLAB
+    for ref, which in ((query_ref, 0), (key_ref, 2), (value_ref, 3)):
+        ref[...] = jnp.concatenate(
+            [summed[:, SLAB * h + which * DH : SLAB * h + (which + 1) * DH] for h in range(heads)], axis=1
+        )
+
+
+def run_finish_heads(left_side, right_side):
+    rows, width = left_side.shape
+    out = jax.ShapeDtypeStruct((rows, width // 4), F32)
+    return pl.pallas_call(finish_heads, out_shape=(out, out, out), name="finish_heads")(
+        left_side, right_side
+    )
 
 
 def interleave(query, key, value, heads):
@@ -551,47 +628,31 @@
     return value
 
 
-def gather_rows(shard):
-    held = shard
-    index = lax.axis_index("dp")
-    for bit in bits_of("dp"):
-        other = swap(held, "dp", bit)
-        mine_first = (index & bit) == 0
-        held = jnp.where(
-            mine_first,
-            jnp.concatenate([held, other], axis=0),
-            jnp.concatenate([other, held], axis=0),
-        )
-    return held
+def after(value, *others):
+    return lax.optimization_barrier((value,) + others)[0]
+
+
+def merge(held, other, bit):
+    mine_first = (lax.axis_index("dp") & bit) == 0
+    return jnp.where(
+        mine_first, jnp.concatenate([held, other], axis=0), jnp.concatenate([other, held], axis=0)
+    )
 
 
 def scatter_rows(value):
     copies = lax.axis_size("dp")
     index = lax.axis_index("dp")
     held = value.reshape((copies,) + (value.shape[0] // copies,) + value.shape[1:])
+    came = None
     for bit in bits_of("dp"):
+        if came is not None:
+            held = add_low(held, came)
         held = held.reshape((held.shape[0] // 2, 2) + held.shape[1:])
         own = (index & bit) // bit
-        keep = lax.dynamic_index_in_dim(held, own, 1, keepdims=False)
         send = lax.dynamic_index_in_dim(held, 1 - own, 1, keepdims=False)
+        held = lax.dynamic_index_in_dim(held, own, 1, keepdims=False)
         came = swap(send, "dp", bit)
-        held = (keep.astype(F32) + came.astype(F32)).astype(BF16)
-    return held[0]
-
-
-def gather_pieces(shard):
-    pair = jnp.concatenate([shard[None], swap(shard[None], "tensor", 1)], axis=0)
-    far = swap(pair, "tensor", 2)
-    bits = list(bits_of("dp"))
-    pieces, marks = [], []
-    for held, base in ((pair, 0), (far, 2)):
-        marked = [(base, 0), (base + 1, 0)]
-        for bit in bits[1:]:
-            held = jnp.concatenate([held, swap(held, "dp", bit)], axis=0)
-            marked = marked + [(slot, turn ^ bit) for slot, turn in marked]
-        pieces += [held, swap(held, "dp", bits[0])]
-        marks += [marked, [(slot, turn ^ bits[0]) for slot, turn in marked]]
-    return (pieces, marks)
+    return (held[0], came[0])
 
 
 def add_low(left_side, right_side):
@@ -611,6 +672,11 @@
         add_low(left_side[:half], right_side[:half]),
         add_low(left_side[half:], right_side[half:]),
     )
+
+
+INNER = [(1, 2), (2, 1)]
+OUTWARD = [(1, 0), (2, 3)]
+INWARD = [(0, 1), (3, 2)]
 
 
 def local(
@@ -630,23 +696,54 @@
     hidden_cols = w_inner.shape[1]
     shard_rows = w_inner.shape[0]
     halves = part_len // BLOCK
-    aligned = shard_rows % 16 == 0 and parts == 4 and copies >= 4
+    line = shard_rows % 16 == 0 and parts == 4 and copies == 8
 
     rows_in = inputs.reshape(part_len, width)
     tokens = lax.all_gather(rows_in, "tensor", axis=0, tiled=True)
-    w_heads = gather_rows(interleave(w_query, w_key, w_value, heads))
     mine = jnp.concatenate((w_inner, w_outer.T, w_output.T), axis=1)
-    if aligned:
-        place = jnp.stack([rank, lax.axis_index("dp")]).astype(jnp.int32)
-        pieces, marks = gather_pieces(mine)
+    head_rows = interleave(w_query, w_key, w_value, heads)
+    valid_rows = valid_mask.astype(F32).reshape(part_len, 1)
+    valid_count = jnp.sum(valid_rows).reshape(1, 1)
+    if line:
+        place = jnp.stack(
+            [
+                rank,
+                rank ^ 1,
+                jnp.where(rank < 2, 2, 1),
+                jnp.where(rank < 2, 3, 0),
+                lax.axis_index("dp"),
+            ]
+        ).astype(jnp.int32)
+        own = mine[None]
+        pair = jnp.concatenate([own, swap(own, "tensor", 1)], axis=0)
+        head_rows = merge(head_rows, swap(head_rows, "dp", 1), 1)
+        crossed = lax.ppermute(pair, "tensor", INNER)
+        near = jnp.concatenate([pair, swap(pair, "dp", 2)], axis=0)
+        head_rows = merge(head_rows, swap(head_rows, "dp", 2), 2)
+        crossed = after(crossed, near, head_rows)
+        near = jnp.concatenate([near, swap(near, "dp", 4)], axis=0)
+        outward = lax.ppermute(crossed, "tensor", OUTWARD)
+        w_heads = merge(head_rows, swap(head_rows, "dp", 4), 4)
+        far = jnp.where((rank == 1) | (rank == 2), crossed, outward)
+        far = after(far, w_heads)
+        far = jnp.concatenate([far, swap(far, "dp", 2)], axis=0)
+        near = after(near, far)
+        near_other = swap(near, "dp", 1)
+        far_last = swap(far, "dp", 4)
+        counted = sum_everywhere(after(valid_count, far))
+        marks = [[(slot, 0) for slot in (0, 1)], [(slot, 0) for slot in (2, 3)]]
+        for bit in (2, 4):
+            marks = [marked + [(slot, turn ^ bit) for slot, turn in marked] for marked in marks]
+        marks = [[(slot, turn ^ flip) for slot, turn in marked] for marked in marks for flip in (0, 1)]
     else:
-        place = jnp.zeros((2,), jnp.int32)
+        place = jnp.asarray(list(range(parts)) + [0], jnp.int32)
         weights = lax.all_gather(mine, ("tensor", "dp"), axis=0, tiled=False)
         pieces = [weights.reshape(parts, width, 2 * hidden_cols + head_cols)]
         marks = [[(t, 0) for t in range(parts)]]
-
-    valid_rows = valid_mask.astype(F32).reshape(part_len, 1)
-    counted = sum_everywhere(jnp.sum(valid_rows).reshape(1, 1))
+        w_heads = head_rows
+        for bit in bits_of("dp"):
+            w_heads = merge(w_heads, swap(w_heads, "dp", bit), bit)
+        counted = sum_everywhere(valid_count)
     ratio = (total_tokens / counted).reshape(1)
     w_heads, ratio = lax.optimization_barrier((w_heads, ratio))
 
@@ -666,6 +763,10 @@
 
     contexts, lses, arrived = [], [], []
     for half in range(halves):
+        if half == halves - 1 and line:
+            far = jnp.concatenate([far, after(far_last, contexts[0])], axis=0)
+            bounds, far = lax.optimization_barrier((bounds, far))
+            pieces = [near, near_other, far, swap(far, "dp", 1)]
         context, lse = run_forward((halves, half), bounds, qkv, seg_col, seg_row)
         contexts.append(context)
         lses.append(lse)
@@ -693,48 +794,51 @@
     inner_sums = sum(inner_sums)
     sources = (firsts, branch_grads, attn_grads, acts, hidden_grads, arrived)
     head_grads[:-1], sources = lax.optimization_barrier((head_grads[:-1], sources))
-    if aligned:
-        rest = list(bits_of("dp"))[1:]
-        orders = (rest, rest[::-1])
-        begun = []
-        for which, order in enumerate(orders):
-            turns = spread(order)
-            keep, send = run_weights(
-                2 * which, 2, (turns, [turn | 1 for turn in turns]), shard_rows, place, *sources
-            )
-            if which == 1:
-                head_grads[-1], keep, send = lax.optimization_barrier((head_grads[-1], keep, send))
-            shape = (copies // 2, 2) + keep.shape[1:]
-            begun.append(add_halves(keep.reshape(shape), swap(send.reshape(shape), "dp", 1)))
-        head_grads[-1], begun = lax.optimization_barrier((head_grads[-1], begun))
-        moving = [(keep, swap(send, "dp", order[0])) for (keep, send), order in zip(begun, orders)]
+    orders = ([2, 4], [4, 2])
+    if line:
+        kept = [spread(order) for order in orders]
+        turns = (kept, [[turn | 1 for turn in turns] for turns in kept])
+        outs = run_weights(turns, 2, shard_rows, place, *sources)
+        outs = [out.reshape((4, 2) + out.shape[1:]) for out in outs]
+        came = [swap(outs[2 * team + 1], "dp", 1) for team in range(2)]
+        head_grads[0], outs = lax.optimization_barrier((head_grads[0], outs))
     else:
-        (packed,) = run_weights(0, parts, ([0],), width, place, *sources)
+        (packed,) = run_weights(([[0]],), 1, width, place, *sources)
+
+    earlier, before = [], []
+    for half in range(halves):
+        if half == halves - 1 and line:
+            came, before = lax.optimization_barrier((came, before))
+            begun = [add_halves(outs[2 * team], came[team]) for team in range(2)]
+            begun, before = lax.optimization_barrier((begun, before))
+            moving = [swap(send, "dp", order[0]) for (_, send), order in zip(begun, orders)]
+        results = run_backward(
+            (halves, half), bounds, qkv, seg_col, seg_row, contexts[half], head_grads[half], lses[half],
+            earlier, before,
+        )
+        if half < halves - 1:
+            before, earlier = [results[0]], earlier + [results[1]]
+    joined_grad, sums = results
+    attn_back = dot(joined_grad, w_heads, NT).astype(BF16)
+    attn_back, sums, joined_grad = lax.optimization_barrier((attn_back, sums, joined_grad))
+    attn_back = lax.psum_scatter(attn_back, "tensor", scatter_dimension=0, tiled=True)
+    if line:
+        moving, joined_grad = lax.optimization_barrier((moving, joined_grad))
+        halved = [add_halves(keep, came) for (keep, _), came in zip(begun, moving)]
+        halved, joined_grad, sums = lax.optimization_barrier((halved, joined_grad, sums))
+        near, far = (
+            add_low(keep, swap(send, "dp", order[1]))[0] for (keep, send), order in zip(halved, orders)
+        )
+        far = add_low(far, lax.ppermute(far, "tensor", INWARD))
+        near = add_low(near, lax.ppermute(far, "tensor", INNER))
+        finals = (near[0], swap(near[1], "tensor", 1))
+    else:
         packed = lax.psum_scatter(packed, "dp", scatter_dimension=1, tiled=True)
-        packed = lax.psum_scatter(packed, "tensor", scatter_dimension=0, tiled=True)
-        packed = packed.reshape(shard_rows, -1).astype(F32)
-
-    joined_grad, sums = run_backward(bounds, qkv, seg_col, seg_row, contexts, head_grads, lses)
-    if aligned:
-        joined_grad, moving = lax.optimization_barrier((joined_grad, moving))
-        reduced = []
-        for (keep, came), order in zip(moving, orders):
-            for bit in order[1:]:
-                keep, send = add_halves(keep, came)
-                came = swap(send, "dp", bit)
-            held = add_low(keep, came)
-            reduced.append(held[0])
-        near = add_low(reduced[0], swap(reduced[1], "tensor", 2))
-        packed = near[0].astype(F32) + swap(near[1], "tensor", 1).astype(F32)
-    attn_back = dot(joined_grad, w_heads, NT).astype(BF16)
-    attn_back, sums = lax.optimization_barrier((attn_back, sums))
-    attn_back = lax.psum_scatter(attn_back, "tensor", scatter_dimension=0, tiled=True)
+        packed = lax.psum_scatter(packed, "tensor", scatter_dimension=0, tiled=True)[0]
+        finals = (packed, jnp.zeros_like(packed))
+    inner_grad, outer_grad, output_grad = run_finish_dense(*finals, hidden_cols, head_cols)
     input_grad = jnp.concatenate(first_grads, axis=0) + attn_back.astype(F32)
-    head_weights = scatter_rows(dot(tokens, joined_grad, TN).astype(BF16))
-    head_weights = head_weights.astype(F32).reshape(shard_rows, heads, 4, DH)
-
-    def pick(which):
-        return head_weights[:, :, which, :].reshape(shard_rows, head_cols)
+    head_finals = scatter_rows(dot(tokens, joined_grad, TN).astype(BF16))
 
     sums = sums.reshape(heads, 4, DH)
     totals = sum_everywhere(
@@ -753,24 +857,15 @@
 
     mse_loss = jnp.sum(total(2)) / (counted[0, 0] * width)
     return (
-        jnp.concatenate(layers, axis=0).reshape(1, part_len, width),
-        mse_loss,
-        input_grad.reshape(1, part_len, width),
-        pick(0),
-        pick(2),
-        pick(3),
-        packed[:, 2 * hidden_cols :].T,
-        packed[:, :hidden_cols],
-        packed[:, hidden_cols : 2 * hidden_cols].T,
-        total(0),
-        total(1),
-        total(6),
-        totals[10 * width :],
-        total(3),
-        total(7),
-        total(8),
-        total(4),
-        total(5),
+        (
+            jnp.concatenate(layers, axis=0).reshape(1, part_len, width),
+            mse_loss,
+            input_grad.reshape(1, part_len, width),
+        )
+        + tuple(run_finish_heads(*head_finals))
+        + (output_grad, inner_grad, outer_grad.T)
+        + (total(0), total(1), total(6), totals[10 * width :])
+        + (total(3), total(7), total(8), total(4), total(5))
     )
 
 

time: 504 us -> 474 us (0.940)
  waiting for transfers between devices: 190 us -> 152 us
  starting transfers between devices: 70.2 us -> 98.5 us
  local copies, waits for them, and re-layouts: 26.4 us -> 15.1 us
    ppermute x32 -> x30, waiting for transfers between devices: 190 us -> 114 us  [swap(): return lax.ppermute(value, axis, [(i, i ^ bit) for i in range(size)])]
    ppermute x0 -> x4, waiting for transfers between devices: none -> 37.9 us  [the longest x1 37.9 us: local(): outward = lax.ppermute(crossed, 'tensor', OUTWARD)]
    ppermute x32 -> x30, starting transfers between devices: 48.6 us -> 73.2 us  [swap(): return lax.ppermute(value, axis, [(i, i ^ bit) for i in range(size)])]
    ppermute x0 -> x4, starting transfers between devices: none -> 6.35 us  [the longest x1 3.69 us: local(): far = add_low(far, lax.ppermute(far, 'tensor', INWARD))]
    convert_element_type x5 -> x8, other arithmetic: 10.6 us -> 15.3 us  [add_low(): return (left_side.astype(F32) + right_side.astype(F32)).astype(BF16)]
    pallas_call x3 -> x5, Pallas kernels: 63.4 us -> 62 us  [the longest x2 45.5 us: run_backward(): pl.pallas_call(functools.partial(attend_backward, which), out_shape=out_s...]
  transfers between devices with their start and end apart: 38 -> 40, of which waited for: 18 -> 16; matrix products, arithmetic and copies ran while one was open for 12% -> 13% of each run, Pallas kernels for 27% -> 25%
where the time goes in v4:
time: 474 us; the launch traced here: 467 us
  waiting for transfers between devices  152 us (32%)
  Pallas kernels  128 us (27%)
  starting transfers between devices  98.5 us (21%)
  other arithmetic  37.1 us (8%)
  between operations  20.9 us (4%)
  matrix products  15.8 us (3%)
  local copies, waits for them, and re-layouts  15.1 us (3%)
    ppermute x30, waiting for transfers between devices, swap(): return lax.ppermute(value, axis, [(i, i ^ bit) for i in range(size)])  114 us
    ppermute x30, starting transfers between devices, swap(): return lax.ppermute(value, axis, [(i, i ^ bit) for i in range(size)])  73.2 us
    pallas_call x2, Pallas kernels, run_backward(): pl.pallas_call(functools.partial(attend_backward, which), out_shape=out_s...  45.5 us
    ppermute x1, waiting for transfers between devices, local(): outward = lax.ppermute(crossed, 'tensor', OUTWARD)  37.9 us
    pallas_call x2, Pallas kernels, run_dense(): pl.pallas_call(functools.partial(dense_chain, marks), out_shape=out_shape...  34.2 us
    pallas_call x2, Pallas kernels, run_forward(): pl.pallas_call(functools.partial(attend_forward, which), out_shape=(jax.S...  31.5 us
    all_to_all x4, starting transfers between devices, exchange(): return lax.all_to_all(blocks, 'tensor', 0, 0)  18.8 us
    dot_general x3, matrix products, dot(): lax.dot_general(left_side, right_side, dims, preferred_element_type=F32)  15.8 us
  transfers between devices with their start and end apart: 40, of which 16 were waited for; matrix products, arithmetic and copies ran while one was open for 13% of the time, Pallas kernels for 25%

profile of v4, /device:TPU:0, one launch (start us, length us, event | category | flops | bytes accessed | tf_op | source)
XLA Modules:
  0.0 467.3 jit_solution(9359383262691820894)
XLA Ops:
  9.9 3.1 collective-permute-start.3
  13.6 7.4 %collective-permute-done.3 = bf16[1,96,1728]{2,1,0:T(8,128)(2,1)S(1)} collective-permute-done((bf16[1,96,1728]{2,1,0:T(8,128)(2,1)S(1)}, bf16[1,96,1728]{2,1,0:T(8,128)(2,1)S(1)}, u32[]{:S(2)}, u32[]{:S(2)}) %collective-permute-start.3) | collective-permute-done | bytes 331808 | tf_op jit(solution)/shard_map/ppermute | solution.py:614
  25.1 22.1 %collective-permute-done.1 = bf16[192,768]{0,1:T(8,128)(2,1)S(1)} collective-permute-done((bf16[192,768]{0,1:T(8,128)(2,1)S(1)}, bf16[192,768]{0,1:T(8,128)(2,1)S(1)}, u32[]{:S(2)}, u32[]{:S(2)}) %collective-permute-start.1) | collective-permute-done | bytes 294944 | tf_op jit(solution)/shard_map/ppermute | solution.py:614
  53.5 10.6 %collective-permute-done.2 = bf16[384,768]{0,1:T(8,128)(2,1)} collective-permute-done((bf16[384,768]{0,1:T(8,128)(2,1)S(1)}, bf16[384,768]{0,1:T(8,128)(2,1)}, u32[]{:S(2)}, u32[]{:S(2)}) %collective-permute-start.2) | collective-permute-done | bytes 589856 | tf_op jit(solution)/shard_map/ppermute | solution.py:614
  64.1 2.6 maximum_select_fusion
  66.7 37.9 %collective-permute-done.6 = bf16[2,96,1728]{2,1,0:T(8,128)(2,1)} collective-permute-done((bf16[2,96,1728]{2,1,0:T(8,128)(2,1)S(1)}, bf16[2,96,1728]{2,1,0:T(8,128)(2,1)}, u32[]{:S(2)}, u32[]{:S(2)}) %collective-permute-start.6) | collective-permute-done | bytes 663584 | tf_op jit(solution)/shard_map/ppermute | solution.py:725
  110.6 12.6 %collective-permute-done.7 = bf16[2,96,1728]{2,1,0:T(8,128)(2,1)S(1)} collective-permute-done((bf16[2,96,1728]{2,1,0:T(8,128)(2,1)S(1)}, bf16[2,96,1728]{2,1,0:T(8,128)(2,1)S(1)}, u32[]{:S(2)}, u32[]{:S(2)}) %collective-permute-start.7) | collective-permute-done | bytes 663584 | tf_op jit(solution)/shard_map/ppermute | solution.py:614
  126.2 2.8 pad_maximum_fusion.refs_0_
  129.5 4.9 %collective-permute-done.8 = f32[1,1]{1,0:T(1,128)} collective-permute-done((f32[1,1]{1,0:T(1,128)}, f32[1,1]{1,0:T(1,128)}, u32[]{:S(2)}, u32[]{:S(2)}) %collective-permute-start.8) | collective-permute-done | bytes 36 | tf_op jit(solution)/shard_map/ppermute | solution.py:614
  135.7 2.8 collective-permute-start.9
  139.9 14.9 %collective-permute-start.10 = (f32[1,1]{1,0:T(1,128)}, f32[1,1]{1,0:T(1,128)}, u32[]{:S(2)}, u32[]{:S(2)}) collective-permute-start(f32[1,1]{1,0:T(1,128)} %add.134), channel_id=1, source_target_pairs={{0,16},{4,20},{8,24},{12,28},{16,0},{20,4},{24,8},{28,12},{1,17},{... | collective-permute-start | bytes 20 | tf_op jit(solution)/shard_map/ppermute | solution.py:614
  157.8 2.2 collective-permute-done.11
  162.0 3.1 collective-permute-done.12
  165.8 6.6 %fusion.3.qkv_ref = bf16[2048,768]{1,0:T(8,128)(2,1)} fusion(f32[768]{0:T(1024)S(1)} %add.139, bf16[768,768]{0,1:T(8,128)(2,1)} %maximum_select_fusion, bf16[1,2048,768]{2,1,0:T(8,128)(2,1)} %all-gather.3.cloned.1.call-done), kind=kOutput, calls=%fused_computation.5 | convolution fusion | flops 2419064832 | bytes 7474176 | tf_op jit(solution)/shard_map/dot_general | solution.py:30
  172.4 15.0 %attend_forward.2 = (bf16[4,384,128]{2,1,0:T(8,128)(2,1)}, f32[3,1,1024]{2,1,0:T(1,128)}) custom-call(s32[8]{0:T(128)} %get-tuple-element.112.low_ref, s32[8]{0:T(128)} %get-tuple-element.113.high_ref, bf16[2048,768]{1,0:T(8,128)(2,1)} %fusion.3.qkv_ref, s32[2048,1]{1,0:T(8,128)} %copy.60.seg_col_ref, s32[1,2048]{1,0:T(1,128)} %seg_row_ref.7), custom_call_target="tpu_custom_call" | custom-call | flops 1610612736 | bytes 5242880 | tf_op jit(solution)/shard_map/attend_forward/pallas_call | solution.py:228
  187.4 1.8 pad_maximum_fusion.1.refs_2_
  189.3 3.5 all-to-all-start
  192.9 16.5 %attend_forward.3 = (bf16[4,384,128]{2,1,0:T(8,128)(2,1)}, f32[3,1,1024]{2,1,0:T(1,128)}) custom-call(s32[8]{0:T(128)} %get-tuple-element.112.low_ref, s32[8]{0:T(128)} %get-tuple-element.113.high_ref, bf16[2048,768]{1,0:T(8,128)(2,1)} %fusion.3.qkv_ref, s32[2048,1]{1,0:T(8,128)} %copy.60.seg_col_ref, s32[1,2048]{1,0:T(1,128)} %seg_row_ref.7), custom_call_target="tpu_custom_call" | custom-call | flops 1610612736 | bytes 5242880 | tf_op jit(solution)/shard_map/attend_forward/pallas_call | solution.py:228
  209.3 5.2 %all-to-all-start.1 = ((bf16[4,384,128]{2,1,0:T(8,128)(2,1)}), bf16[4,384,128]{2,1,0:T(8,128)(2,1)}, u32[]{:S(2)}, u32[]{:S(2)}) async-start(bf16[4,384,128]{2,1,0:T(8,128)(2,1)} %get-tuple-element.114.ctx_ref), calls=%async_computation.1 | async-start | bytes 786432 | tf_op jit(solution)/shard_map/all_to_all | solution.py:762
  217.5 17.1 %dense_chain.2 = (bf16[256,768]{1,0:T(8,128)(2,1)}, f32[256,768]{1,0:T(8,128)}, bf16[4,384,128]{2,1,0:T(8,128)(2,1)}, bf16[256,768]{1,0:T(8,128)(2,1)}, bf16[256...) custom-call(s32[5]{0:T(128)} %stack.46.place_ref, ...), custom_call_target="tpu_custom_call" | custom-call | flops 5435817984 | bytes 18874368 | tf_op jit(solution)/shard_map/dense_chain/pallas_call | solution.py:442
  234.6 5.1 %all-to-all-start.2 = ((bf16[4,384,128]{2,1,0:T(8,128)(2,1)}), bf16[4,384,128]{2,1,0:T(8,128)(2,1)S(1)}, u32[]{:S(2)}, u32[]{:S(2)}) async-start(bf16[4,384,128]{2,1,0:T(8,128)(2,1)} %get-tuple-element.116), calls=%async_computation.2 | async-start | bytes 786432 | tf_op jit(solution)/shard_map/all_to_all | solution.py:762
  239.7 17.1 %dense_chain.3 = (bf16[256,768]{1,0:T(8,128)(2,1)}, f32[256,768]{1,0:T(8,128)}, bf16[4,384,128]{2,1,0:T(8,128)(2,1)}, bf16[256,768]{1,0:T(8,128)(2,1)}, bf16[256...) custom-call(s32[5]{0:T(128)} %stack.46.place_ref, ...), custom_call_target="tpu_custom_call" | custom-call | flops 5435817984 | bytes 18874368 | tf_op jit(solution)/shard_map/dense_chain/pallas_call | solution.py:442
  256.8 12.8 %dense_weights.1 = (bf16[8,96,1728]{2,1,0:T(8,128)(2,1)}, bf16[8,96,1728]{2,1,0:T(8,128)(2,1)}, bf16[8,96,1728]{2,1,0:T(8,128)(2,1)}, bf16[8,96,1728]{2,1,0:T(8,128)(2,1)}) custom-call(s32[5]{0:T(128)} %stack.46.place_ref, bf16[256,768]{1,0:T(8,128)(2,1)} %get-tuple-element.128.refs_0_, bf16[256,768]{1,0:T(8,128)(2,1)} %get-tuple-element.129.refs_1_, ...), custom_call_target="tpu_custom_call" | custom-call | flops 5435817984 | bytes 20971520 | tf_op jit(solution)/shard_map/dense_weights/pallas_call | solution.py:536
  269.6 2.0 collective-permute-start.17
  271.6 5.0 %all-to-all-start.3 = ((bf16[4,384,128]{2,1,0:T(8,128)(2,1)}), bf16[4,384,128]{2,1,0:T(8,128)(2,1)S(1)}, u32[]{:S(2)}, u32[]{:S(2)}) async-start(bf16[4,384,128]{2,1,0:T(8,128)(2,1)} %get-tuple-element.155), calls=%async_computation.3 | async-start | bytes 786432 | tf_op jit(solution)/shard_map/all_to_all | solution.py:762
  276.7 20.6 %attend_backward.2 = (f32[3,2048,128]{2,1,0:T(8,128)}, bf16[4,256,384]{2,1,0:T(8,128)(2,1)}) custom-call(s32[8]{0:T(128)} %get-tuple-element.112.low_ref, s32[8]{0:T(128)} %get-tuple-element.113.high_ref, bf16[2048,768]{1,0:T(8,128)(2,1)} %fusion.3.qkv_ref, s32[2048,1]{1,0:T(8,128)} %copy.60.seg_col_ref, s32[1,2048]{1,0:T(1,128)} %seg_row_ref.7, ...), custom_call_target="tpu_custom_call" | custom-call | flops 4026531840 | bytes 10485760 | tf_op jit(solution)/shard_map/attend_backward/pallas_call | solution.py:291
  298.8 4.5 add_convert_fusion.1
  303.2 1.8 add_convert_fusion.3
  305.0 7.7 %collective-permute-start.19 = (bf16[2,2,96,1728]{3,2,1,0:T(8,128)(2,1)}, bf16[2,2,96,1728]{3,2,1,0:T(8,128)(2,1)}, u32[]{:S(2)}, u32[]{:S(2)}) collective-permute-start(bf16[2,2,96,1728]{3,2,1,0:T(8,128)(2,1)} %get-tuple-element.153), channel_id=1, source_target_pairs={{0,8},{4,12},{8,0},{12,4},{16,24},{20,28},{24,16},{28,20},{1,9},{5... | collective-permute-start | bytes 3981320 | tf_op jit(solution)/shard_map/ppermute | solution.py:614
  312.7 5.8 %collective-permute-start.20 = (bf16[2,2,96,1728]{3,2,1,0:T(8,128)(2,1)}, bf16[2,2,96,1728]{3,2,1,0:T(8,128)(2,1)}, u32[]{:S(2)}, u32[]{:S(2)}) collective-permute-start(bf16[2,2,96,1728]{3,2,1,0:T(8,128)(2,1)} %get-tuple-element.154), channel_id=1, source_target_pairs={{0,16},{4,20},{8,24},{12,28},{16,0},{20,4},{24,8},{28,12},{1,17},{... | collective-permute-start | bytes 3981320 | tf_op jit(solution)/shard_map/ppermute | solution.py:614
  319.3 24.9 %attend_backward.3 = (bf16[2048,768]{1,0:T(8,128)(2,1)}, f32[1,768]{1,0:T(1,128)}) custom-call(s32[8]{0:T(128)} %get-tuple-element.112.low_ref, s32[8]{0:T(128)} %get-tuple-element.113.high_ref, bf16[2048,768]{1,0:T(8,128)(2,1)} %fusion.3.qkv_ref, s32[2048,1]{1,0:T(8,128)} %copy.60.seg_col_ref, s32[1,2048]{1,0:T(1,128)} %seg_row_ref.7, ...), custom_call_target="tpu_custom_call" | custom-call | flops 4026531840 | bytes 10485760 | tf_op jit(solution)/shard_map/attend_backward/pallas_call | solution.py:291
  344.2 6.6 %convolution_convert_fusion = bf16[2048,768]{1,0:T(8,128)(2,1)} fusion(bf16[2048,768]{1,0:T(8,128)(2,1)} %get-tuple-element.175, bf16[768,768]{0,1:T(8,128)(2,1)} %maximum_select_fusion), kind=kOutput, calls=%fused_computation.1 | convolution fusion | flops 2417491968 | bytes 7471104 | tf_op jit(solution)/shard_map/dot_general | solution.py:30
  351.6 2.6 add_convert_fusion.8
  354.2 2.6 add_convert_fusion.10
  356.9 6.6 %collective-permute-start.30 = (bf16[1,2,96,1728]{3,2,1,0:T(8,128)(2,1)}, bf16[1,2,96,1728]{3,2,1,0:T(8,128)(2,1)}, u32[]{:S(2)}, u32[]{:S(2)}) collective-permute-start(bf16[1,2,96,1728]{3,2,1,0:T(8,128)(2,1)} %get-tuple-element.182), channel_id=1, source_target_pairs={{0,8},{4,12},{8,0},{12,4},{16,24},{20,28},{24,16},{28,20},{1,9},{5... | collective-permute-start | bytes 1990664 | tf_op jit(solution)/shard_map/ppermute | solution.py:614
  363.5 2.7 fusion.7
  368.6 10.6 %collective-permute-done.30 = bf16[1,2,96,1728]{3,2,1,0:T(8,128)(2,1)} collective-permute-done((bf16[1,2,96,1728]{3,2,1,0:T(8,128)(2,1)}, bf16[1,2,96,1728]{3,2,1,0:T(8,128)(2,1)}, u32[]{:S(2)}, u32[]{:S(2)}) %collective-permute-start.30) | collective-permute-done | bytes 663584 | tf_op jit(solution)/shard_map/ppermute | solution.py:614
  380.5 3.7 collective-permute-start.31
  384.6 3.7 collective-permute-done.22
  388.4 4.0 collective-permute-done.23
  392.7 23.5 %collective-permute-done.24 = f32[84,128]{1,0:T(8,128)S(1)} collective-permute-done((f32[84,128]{1,0:T(8,128)S(1)}, f32[84,128]{1,0:T(8,128)S(1)}, u32[]{:S(2)}, u32[]{:S(2)}) %collective-permute-start.24) | collective-permute-done | bytes 43040 | tf_op jit(solution)/shard_map/ppermute | solution.py:614
  416.2 3.5 collective-permute-start.25
  425.7 3.9 collective-permute-done.27
  431.8 13.6 %collective-permute-start.33 = (bf16[96,1728]{1,0:T(8,128)(2,1)S(1)}, bf16[96,1728]{1,0:T(8,128)(2,1)S(1)}, u32[]{:S(2)}, u32[]{:S(2)}) collective-permute-start(bf16[96,1728]{1,0:T(8,128)(2,1)S(1)} %get-tuple-element.198), channel_id=1, source_target_pairs={{0,1},{1,0},{2,3},{3,2},{4,5},{5,4},{6,7},{7,6},{8,9},{9,8},{10,11... | collective-permute-start | bytes 995336 | tf_op jit(solution)/shard_map/ppermute | solution.py:614
  448.1 3.2 collective-permute-done.28
  452.0 1.8 finish_heads.1
  454.5 2.0 finish_dense.1
  456.5 2.4 fusion.6
  (192 shorter events, 49.6 us)
Async XLA Ops:
  7.2 158.5 %all-gather.3.cloned.1.call-start = ((), (), s32[]{:S(2)}) async-start(), calls=%async_computation.6 | async-start | bytes 3932160 | tf_op jit(solution)/shard_map/all_gather | solution.py:702
  9.9 11.2 %collective-permute-start.3 = (bf16[1,96,1728]{2,1,0:T(8,128)(2,1)S(1)}, bf16[1,96,1728]{2,1,0:T(8,128)(2,1)S(1)}, u32[]{:S(2)}, u32[]{:S(2)}) collective-permute-start(bf16[1,96,1728]{2,1,0:T(8,128)(2,1)S(1)} %maximum_bitcast_fusion.1), channel_id=1, source_target_pairs={{0,1},{1,0},{2,3},{3,2},{4,5},{5,4},{6,7},{7,6},{8,9},{9,8},{10,11... | collective-permute-start | bytes 995336 | tf_op jit(solution)/shard_map/ppermute | solution.py:614
  13.5 10.1 %collective-permute-start = (bf16[96,768]{0,1:T(8,128)(2,1)S(1)}, bf16[96,768]{0,1:T(8,128)(2,1)S(1)}, u32[]{:S(2)}, u32[]{:S(2)}) collective-permute-start(bf16[96,768]{0,1:T(8,128)(2,1)S(1)} %bitcast.114), channel_id=1, source_target_pairs={{0,4},{4,0},{8,12},{12,8},{16,20},{20,16},{24,28},{28,24},{1,5},{5... | collective-permute-start | bytes 442376 | tf_op jit(solution)/shard_map/ppermute | solution.py:614
  21.9 27.2 %collective-permute-start.5 = (bf16[2,96,1728]{2,1,0:T(8,128)(2,1)}, bf16[2,96,1728]{2,1,0:T(8,128)(2,1)S(1)}, u32[]{:S(2)}, u32[]{:S(2)}) collective-permute-start(bf16[2,96,1728]{2,1,0:T(8,128)(2,1)} %pad_maximum_fusion.3), channel_id=1, source_target_pairs={{0,8},{4,12},{8,0},{12,4},{16,24},{20,28},{24,16},{28,20},{1,9},{5... | collective-permute-start | bytes 1990664 | tf_op jit(solution)/shard_map/ppermute | solution.py:614
  23.9 23.2 %collective-permute-start.1 = (bf16[192,768]{0,1:T(8,128)(2,1)S(1)}, bf16[192,768]{0,1:T(8,128)(2,1)S(1)}, u32[]{:S(2)}, u32[]{:S(2)}) collective-permute-start(bf16[192,768]{0,1:T(8,128)(2,1)S(1)} %maximum_select_fusion.2), channel_id=1, source_target_pairs={{0,8},{4,12},{8,0},{12,4},{16,24},{20,28},{24,16},{28,20},{1,9},{5... | collective-permute-start | bytes 884744 | tf_op jit(solution)/shard_map/ppermute | solution.py:614
  24.4 26.0 %collective-permute-start.4 = (bf16[2,96,1728]{2,1,0:T(8,128)(2,1)}, bf16[2,96,1728]{2,1,0:T(8,128)(2,1)S(1)}, u32[]{:S(2)}, u32[]{:S(2)}) collective-permute-start(bf16[2,96,1728]{2,1,0:T(8,128)(2,1)} %pad_maximum_fusion.3), channel_id=1, source_target_pairs={{1,2},{2,1},{5,6},{6,5},{9,10},{10,9},{13,14},{14,13},{17,18},{18,... | collective-permute-start | bytes 1990664 | tf_op jit(solution)/shard_map/ppermute | solution.py:720
  47.7 16.4 %collective-permute-start.2 = (bf16[384,768]{0,1:T(8,128)(2,1)S(1)}, bf16[384,768]{0,1:T(8,128)(2,1)}, u32[]{:S(2)}, u32[]{:S(2)}) collective-permute-start(bf16[384,768]{0,1:T(8,128)(2,1)S(1)} %maximum_select_fusion.1), channel_id=1, source_target_pairs={{0,16},{4,20},{8,24},{12,28},{16,0},{20,4},{24,8},{28,12},{1,17},{... | collective-permute-start | bytes 1769480 | tf_op jit(solution)/shard_map/ppermute | solution.py:614
  50.4 54.3 %collective-permute-start.6 = (bf16[2,96,1728]{2,1,0:T(8,128)(2,1)S(1)}, bf16[2,96,1728]{2,1,0:T(8,128)(2,1)}, u32[]{:S(2)}, u32[]{:S(2)}) collective-permute-start(bf16[2,96,1728]{2,1,0:T(8,128)(2,1)S(1)} %collective-permute-done.4), channel_id=1, source_target_pairs={{1,0},{2,3},{5,4},{6,7},{9,8},{10,11},{13,12},{14,15},{17,16},{18,... | collective-permute-start | bytes 1990664 | tf_op jit(solution)/shard_map/ppermute | solution.py:725
  52.9 73.3 %collective-permute-start.13 = (bf16[4,96,1728]{2,1,0:T(8,128)(2,1)}, bf16[4,96,1728]{2,1,0:T(8,128)(2,1)}, u32[]{:S(2)}, u32[]{:S(2)}) collective-permute-start(bf16[4,96,1728]{2,1,0:T(8,128)(2,1)} %pad_maximum_fusion.2), channel_id=1, source_target_pairs={{0,16},{4,20},{8,24},{12,28},{16,0},{20,4},{24,8},{28,12},{1,17},{... | collective-permute-start | bytes 3981320 | tf_op jit(solution)/shard_map/ppermute | solution.py:614
  66.7 42.2 %copy-start.23 = (s32[1,512]{1,0:T(1,128)S(1)}, s32[1,512]{1,0:T(1,128)}, u32[]{:S(2)}) copy-start(s32[1,512]{1,0:T(1,128)} %param.22) | copy-start | bytes 6148
  105.8 17.4 %collective-permute-start.7 = (bf16[2,96,1728]{2,1,0:T(8,128)(2,1)S(1)}, bf16[2,96,1728]{2,1,0:T(8,128)(2,1)S(1)}, u32[]{:S(2)}, u32[]{:S(2)}) collective-permute-start(bf16[2,96,1728]{2,1,0:T(8,128)(2,1)S(1)} %broadcast_select_fusion), channel_id=1, source_target_pairs={{0,8},{4,12},{8,0},{12,4},{16,24},{20,28},{24,16},{28,20},{1,9},{5... | collective-permute-start | bytes 1990664 | tf_op jit(solution)/shard_map/ppermute | solution.py:614
  123.2 49.2 %copy-start.4 = (bf16[2,96,1728]{2,1,0:T(8,128)(2,1)}, bf16[2,96,1728]{2,1,0:T(8,128)(2,1)S(1)}, u32[]{:S(2)}) copy-start(bf16[2,96,1728]{2,1,0:T(8,128)(2,1)S(1)} %collective-permute-done.7) | copy-start | bytes 1990660
  124.2 63.2 %collective-permute-start.15 = (bf16[4,96,1728]{2,1,0:T(8,128)(2,1)}, bf16[4,96,1728]{2,1,0:T(8,128)(2,1)}, u32[]{:S(2)}, u32[]{:S(2)}) collective-permute-start(bf16[4,96,1728]{2,1,0:T(8,128)(2,1)} %constant_dynamic-update-slice_fusion), channel_id=1, source_target_pairs={{0,16},{4,20},{8,24},{12,28},{16,0},{20,4},{24,8},{28,12},{1,17},{... | collective-permute-start | bytes 3981320 | tf_op jit(solution)/shard_map/ppermute | solution.py:614
  129.0 88.5 %collective-permute-start.14 = (bf16[8,96,1728]{2,1,0:T(8,128)(2,1)}, bf16[8,96,1728]{2,1,0:T(8,128)(2,1)}, u32[]{:S(2)}, u32[]{:S(2)}) collective-permute-start(bf16[8,96,1728]{2,1,0:T(8,128)(2,1)} %pad_maximum_fusion.refs_0_), channel_id=1, source_target_pairs={{0,4},{4,0},{8,12},{12,8},{16,20},{20,16},{24,28},{28,24},{1,5},{5... | collective-permute-start | bytes 7962632 | tf_op jit(solution)/shard_map/ppermute | solution.py:614
  129.0 5.4 %collective-permute-start.8 = (f32[1,1]{1,0:T(1,128)}, f32[1,1]{1,0:T(1,128)}, u32[]{:S(2)}, u32[]{:S(2)}) collective-permute-start(f32[1,1]{1,0:T(1,128)} %bitcast.9), channel_id=1, source_target_pairs={{0,4},{4,0},{8,12},{12,8},{16,20},{20,16},{24,28},{28,24},{1,5},{5... | collective-permute-start | bytes 20 | tf_op jit(solution)/shard_map/ppermute | solution.py:614
  135.7 3.6 collective-permute-start.9
  139.9 15.9 %collective-permute-start.10 = (f32[1,1]{1,0:T(1,128)}, f32[1,1]{1,0:T(1,128)}, u32[]{:S(2)}, u32[]{:S(2)}) collective-permute-start(f32[1,1]{1,0:T(1,128)} %add.134), channel_id=1, source_target_pairs={{0,16},{4,20},{8,24},{12,28},{16,0},{20,4},{24,8},{28,12},{1,17},{... | collective-permute-start | bytes 20 | tf_op jit(solution)/shard_map/ppermute | solution.py:614
  156.4 3.6 collective-permute-start.11
  160.6 4.5 collective-permute-start.12
  189.2 28.2 %collective-permute-start.16 = (bf16[8,96,1728]{2,1,0:T(8,128)(2,1)S(1)}, bf16[8,96,1728]{2,1,0:T(8,128)(2,1)}, u32[]{:S(2)}, u32[]{:S(2)}) collective-permute-start(bf16[8,96,1728]{2,1,0:T(8,128)(2,1)S(1)} %pad_maximum_fusion.1.refs_2_), channel_id=1, source_target_pairs={{0,4},{4,0},{8,12},{12,8},{16,20},{20,16},{24,28},{28,24},{1,5},{5... | collective-permute-start | bytes 7962632 | tf_op jit(solution)/shard_map/ppermute | solution.py:614
  189.3 20.0 %all-to-all-start = ((bf16[4,384,128]{2,1,0:T(8,128)(2,1)}), bf16[4,384,128]{2,1,0:T(8,128)(2,1)S(1)}, u32[]{:S(2)}, u32[]{:S(2)}) async-start(bf16[4,384,128]{2,1,0:T(8,128)(2,1)} %get-tuple-element.107.ctx_ref), calls=%async_computation | async-start | bytes 786432 | tf_op jit(solution)/shard_map/all_to_all | solution.py:762
  192.8 22.7 %copy-start.30 = (bf16[768]{0:T(1024)(128)(2,1)S(1)}, bf16[768]{0:T(1024)(128)(2,1)}, u32[]{:S(2)}) copy-start(bf16[768]{0:T(1024)(128)(2,1)} %param.38) | copy-start | bytes 4612
  192.8 22.7 %copy-start.31 = (bf16[768]{0:T(1024)(128)(2,1)S(1)}, bf16[768]{0:T(1024)(128)(2,1)}, u32[]{:S(2)}) copy-start(bf16[768]{0:T(1024)(128)(2,1)} %param.39) | copy-start | bytes 4612
  192.8 23.4 %copy-start.24 = (bf16[3072]{0:T(1024)(128)(2,1)S(1)}, bf16[3072]{0:T(1024)(128)(2,1)}, u32[]{:S(2)}) copy-start(bf16[3072]{0:T(1024)(128)(2,1)} %param.34) | copy-start | bytes 18436
  209.3 25.2 %all-to-all-start.1 = ((bf16[4,384,128]{2,1,0:T(8,128)(2,1)}), bf16[4,384,128]{2,1,0:T(8,128)(2,1)}, u32[]{:S(2)}, u32[]{:S(2)}) async-start(bf16[4,384,128]{2,1,0:T(8,128)(2,1)} %get-tuple-element.114.ctx_ref), calls=%async_computation.1 | async-start | bytes 786432 | tf_op jit(solution)/shard_map/all_to_all | solution.py:762
  234.6 22.2 %all-to-all-start.2 = ((bf16[4,384,128]{2,1,0:T(8,128)(2,1)}), bf16[4,384,128]{2,1,0:T(8,128)(2,1)S(1)}, u32[]{:S(2)}, u32[]{:S(2)}) async-start(bf16[4,384,128]{2,1,0:T(8,128)(2,1)} %get-tuple-element.116), calls=%async_computation.2 | async-start | bytes 786432 | tf_op jit(solution)/shard_map/all_to_all | solution.py:762
  269.6 27.7 %collective-permute-start.17 = (bf16[4,2,96,1728]{3,2,1,0:T(8,128)(2,1)}, bf16[4,2,96,1728]{3,2,1,0:T(8,128)(2,1)S(1)}, u32[]{:S(2)}, u32[]{:S(2)}) collective-permute-start(bf16[4,2,96,1728]{3,2,1,0:T(8,128)(2,1)} %bitcast.132), channel_id=1, source_target_pairs={{0,4},{4,0},{8,12},{12,8},{16,20},{20,16},{24,28},{28,24},{1,5},{5... | collective-permute-start | bytes 7962632 | tf_op jit(solution)/shard_map/ppermute | solution.py:614
  271.5 25.7 %collective-permute-start.18 = (bf16[4,2,96,1728]{3,2,1,0:T(8,128)(2,1)}, bf16[4,2,96,1728]{3,2,1,0:T(8,128)(2,1)}, u32[]{:S(2)}, u32[]{:S(2)}) collective-permute-start(bf16[4,2,96,1728]{3,2,1,0:T(8,128)(2,1)} %bitcast.131), channel_id=1, source_target_pairs={{0,4},{4,0},{8,12},{12,8},{16,20},{20,16},{24,28},{28,24},{1,5},{5... | collective-permute-start | bytes 7962632 | tf_op jit(solution)/shard_map/ppermute | solution.py:614
  271.6 46.9 %all-to-all-start.3 = ((bf16[4,384,128]{2,1,0:T(8,128)(2,1)}), bf16[4,384,128]{2,1,0:T(8,128)(2,1)S(1)}, u32[]{:S(2)}, u32[]{:S(2)}) async-start(bf16[4,384,128]{2,1,0:T(8,128)(2,1)} %get-tuple-element.155), calls=%async_computation.3 | async-start | bytes 786432 | tf_op jit(solution)/shard_map/all_to_all | solution.py:762
  276.6 179.9 %reduce-scatter.2.cloned.1.call-start = ((), (), s32[]{:S(2)}) async-start(), calls=%async_computation.5 | async-start | bytes 3932160 | tf_op jit(solution)/shard_map/reduce_scatter | solution.py:824
  305.0 46.5 %collective-permute-start.19 = (bf16[2,2,96,1728]{3,2,1,0:T(8,128)(2,1)}, bf16[2,2,96,1728]{3,2,1,0:T(8,128)(2,1)}, u32[]{:S(2)}, u32[]{:S(2)}) collective-permute-start(bf16[2,2,96,1728]{3,2,1,0:T(8,128)(2,1)} %get-tuple-element.153), channel_id=1, source_target_pairs={{0,8},{4,12},{8,0},{12,4},{16,24},{20,28},{24,16},{28,20},{1,9},{5... | collective-permute-start | bytes 3981320 | tf_op jit(solution)/shard_map/ppermute | solution.py:614
  312.7 38.9 %collective-permute-start.20 = (bf16[2,2,96,1728]{3,2,1,0:T(8,128)(2,1)}, bf16[2,2,96,1728]{3,2,1,0:T(8,128)(2,1)}, u32[]{:S(2)}, u32[]{:S(2)}) collective-permute-start(bf16[2,2,96,1728]{3,2,1,0:T(8,128)(2,1)} %get-tuple-element.154), channel_id=1, source_target_pairs={{0,16},{4,20},{8,24},{12,28},{16,0},{20,4},{24,8},{28,12},{1,17},{... | collective-permute-start | bytes 3981320 | tf_op jit(solution)/shard_map/ppermute | solution.py:614
  356.9 22.4 %collective-permute-start.30 = (bf16[1,2,96,1728]{3,2,1,0:T(8,128)(2,1)}, bf16[1,2,96,1728]{3,2,1,0:T(8,128)(2,1)}, u32[]{:S(2)}, u32[]{:S(2)}) collective-permute-start(bf16[1,2,96,1728]{3,2,1,0:T(8,128)(2,1)} %get-tuple-element.182), channel_id=1, source_target_pairs={{0,8},{4,12},{8,0},{12,4},{16,24},{20,28},{24,16},{28,20},{1,9},{5... | collective-permute-start | bytes 1990664 | tf_op jit(solution)/shard_map/ppermute | solution.py:614
  366.1 53.5 %copy-start.5 = (bf16[768,768]{0,1:T(8,128)(2,1)}, bf16[768,768]{0,1:T(8,128)(2,1)S(1)}, u32[]{:S(2)}) copy-start(bf16[768,768]{0,1:T(8,128)(2,1)S(1)} %fusion.7) | copy-start | bytes 3538948
  367.1 52.5 %collective-permute-start.26 = (bf16[4,96,768]{2,1,0:T(8,128)(2,1)}, bf16[4,96,768]{2,1,0:T(8,128)(2,1)}, u32[]{:S(2)}, u32[]{:S(2)}) collective-permute-start(bf16[4,96,768]{2,1,0:T(8,128)(2,1)} %dynamic-slice_bitcast_fusion), channel_id=1, source_target_pairs={{0,4},{4,0},{8,12},{12,8},{16,20},{20,16},{24,28},{28,24},{1,5},{5... | collective-permute-start | bytes 1769480 | tf_op jit(solution)/shard_map/ppermute | solution.py:614
  368.0 16.2 %collective-permute-start.21 = (f32[84,128]{1,0:T(8,128)S(1)}, f32[84,128]{1,0:T(8,128)S(1)}, u32[]{:S(2)}, u32[]{:S(2)}) collective-permute-start(f32[84,128]{1,0:T(8,128)S(1)} %maximum_bitcast_fusion.2), channel_id=1, source_target_pairs={{0,4},{4,0},{8,12},{12,8},{16,20},{20,16},{24,28},{28,24},{1,5},{5... | collective-permute-start | bytes 129032 | tf_op jit(solution)/shard_map/ppermute | solution.py:614
  380.5 40.5 %collective-permute-start.31 = (bf16[2,96,1728]{2,1,0:T(8,128)(2,1)S(1)}, bf16[2,96,1728]{2,1,0:T(8,128)(2,1)S(1)}, u32[]{:S(2)}, u32[]{:S(2)}) collective-permute-start(bf16[2,96,1728]{2,1,0:T(8,128)(2,1)S(1)} %fusion.13), channel_id=1, source_target_pairs={{0,1},{3,2},{4,5},{7,6},{8,9},{11,10},{12,13},{15,14},{16,17},{19,... | collective-permute-start | bytes 1990664 | tf_op jit(solution)/shard_map/ppermute | solution.py:832
  384.2 4.1 collective-permute-start.22
  388.4 4.1 collective-permute-start.23
  392.5 23.7 %collective-permute-start.24 = (f32[84,128]{1,0:T(8,128)S(1)}, f32[84,128]{1,0:T(8,128)S(1)}, u32[]{:S(2)}, u32[]{:S(2)}) collective-permute-start(f32[84,128]{1,0:T(8,128)S(1)} %add.154), channel_id=1, source_target_pairs={{0,1},{1,0},{2,3},{3,2},{4,5},{5,4},{6,7},{7,6},{8,9},{9,8},{10,11... | collective-permute-start | bytes 129032 | tf_op jit(solution)/shard_map/ppermute | solution.py:614
  392.6 37.1 %collective-permute-start.29 = (bf16[1,2,96,1728]{3,2,1,0:T(8,128)(2,1)}, bf16[1,2,96,1728]{3,2,1,0:T(8,128)(2,1)}, u32[]{:S(2)}, u32[]{:S(2)}) collective-permute-start(bf16[1,2,96,1728]{3,2,1,0:T(8,128)(2,1)} %get-tuple-element.180), channel_id=1, source_target_pairs={{0,16},{4,20},{8,24},{12,28},{16,0},{20,4},{24,8},{28,12},{1,17},{... | collective-permute-start | bytes 1990664 | tf_op jit(solution)/shard_map/ppermute | solution.py:614
  416.2 7.7 %collective-permute-start.25 = (f32[84,128]{1,0:T(8,128)S(1)}, f32[84,128]{1,0:T(8,128)S(1)}, u32[]{:S(2)}, u32[]{:S(2)}) collective-permute-start(f32[84,128]{1,0:T(8,128)S(1)} %add.155), channel_id=1, source_target_pairs={{0,2},{1,3},{2,0},{3,1},{4,6},{5,7},{6,4},{7,5},{8,10},{9,11},{10,... | collective-permute-start | bytes 129032 | tf_op jit(solution)/shard_map/ppermute | solution.py:614
  422.0 7.7 %collective-permute-start.32 = (bf16[2,96,1728]{2,1,0:T(8,128)(2,1)}, bf16[2,96,1728]{2,1,0:T(8,128)(2,1)S(1)}, u32[]{:S(2)}, u32[]{:S(2)}) collective-permute-start(bf16[2,96,1728]{2,1,0:T(8,128)(2,1)} %add_convert_fusion.5), channel_id=1, source_target_pairs={{1,2},{2,1},{5,6},{6,5},{9,10},{10,9},{13,14},{14,13},{17,18},{18,... | collective-permute-start | bytes 1990664 | tf_op jit(solution)/shard_map/ppermute | solution.py:833
  422.8 6.8 %collective-permute-start.27 = (bf16[2,96,768]{2,1,0:T(8,128)(2,1)S(1)}, bf16[2,96,768]{2,1,0:T(8,128)(2,1)S(1)}, u32[]{:S(2)}, u32[]{:S(2)}) collective-permute-start(bf16[2,96,768]{2,1,0:T(8,128)(2,1)S(1)} %dynamic-slice_bitcast_fusion.1), channel_id=1, source_target_pairs={{0,8},{4,12},{8,0},{12,4},{16,24},{20,28},{24,16},{28,20},{1,9},{5... | collective-permute-start | bytes 884744 | tf_op jit(solution)/shard_map/ppermute | solution.py:614
  431.0 25.5 %copy-start.6 = (f32[256,768]{1,0:T(8,128)S(1)}, f32[256,768]{1,0:T(8,128)}, u32[]{:S(2)}) copy-start(f32[256,768]{1,0:T(8,128)} %get-tuple-element.172) | copy-start | bytes 2359300
  431.1 25.5 %copy-start.7 = (f32[256,768]{1,0:T(8,128)S(1)}, f32[256,768]{1,0:T(8,128)}, u32[]{:S(2)}) copy-start(f32[256,768]{1,0:T(8,128)} %get-tuple-element.173) | copy-start | bytes 2359300
  431.8 21.9 %collective-permute-start.33 = (bf16[96,1728]{1,0:T(8,128)(2,1)S(1)}, bf16[96,1728]{1,0:T(8,128)(2,1)S(1)}, u32[]{:S(2)}, u32[]{:S(2)}) collective-permute-start(bf16[96,1728]{1,0:T(8,128)(2,1)S(1)} %get-tuple-element.198), channel_id=1, source_target_pairs={{0,1},{1,0},{2,3},{3,2},{4,5},{5,4},{6,7},{7,6},{8,9},{9,8},{10,11... | collective-permute-start | bytes 995336 | tf_op jit(solution)/shard_map/ppermute | solution.py:614
  446.2 5.1 %collective-permute-start.28 = (bf16[1,96,768]{2,1,0:T(8,128)(2,1)S(1)}, bf16[1,96,768]{2,1,0:T(8,128)(2,1)S(1)}, u32[]{:S(2)}, u32[]{:S(2)}) collective-permute-start(bf16[1,96,768]{2,1,0:T(8,128)(2,1)S(1)} %get-tuple-element.200), channel_id=1, source_target_pairs={{0,16},{4,20},{8,24},{12,28},{16,0},{20,4},{24,8},{28,12},{1,17},{... | collective-permute-start | bytes 442376 | tf_op jit(solution)/shard_map/ppermute | solution.py:614
  (26 other events, 204.3 us)
Sparse Core Ops, SparseCore 0:
  9.6 80.6 all-gather.2
  350.9 82.3 reduce-scatter.1

commit v5 on v4

--- a/solution.py
+++ b/solution.py
@@ -64,11 +64,33 @@
     return jnp.concatenate([packed[:BLOCK], third], axis=1)
 
 
+CHUNKS = (0, 2, 1, 3)
+
+
+def fetch_chunks(lane_ref, chunk_refs, target, sems):
+    rows = chunk_refs[0].shape[0]
+    copies = []
+    for at, (turn, chunk) in enumerate(zip(CHUNKS, chunk_refs)):
+        offset = pl.multiple_of((lane_ref[0] ^ turn) * rows, rows)
+        copies.append(pltpu.make_async_copy(chunk, target.at[pl.ds(offset, rows), :], sems.at[at]))
+    return copies
+
+
 def attend_forward(
-    which, low_ref, high_ref, qkv_ref, seg_col_ref, seg_row_ref, ctx_ref, lse_ref, held
+    which, lane_ref, low_ref, high_ref, *refs
 ):
+    chunk_refs, (seg_col_ref, seg_row_ref, ctx_ref, lse_ref, held, qkv_ref, sems) = refs[:4], refs[4:]
     halves, half = which
     heads = lse_ref.shape[0]
+
+    @pl.when(pl.program_id(0) == 0)
+    def _():
+        copies = fetch_chunks(lane_ref, chunk_refs, qkv_ref, sems)
+        for copy in copies:
+            copy.start()
+        for copy in copies:
+            copy.wait()
+
     qb = pl.program_id(0) * halves + half
     rows = pl.ds(pl.multiple_of(qb * BLOCK, BLOCK), BLOCK)
     seg_q = seg_col_ref[...]
@@ -118,25 +140,30 @@
     )
 
 
-def attend_backward(
-    which, low_ref, high_ref, qkv_ref, seg_col_ref, seg_row_ref, ctx_ref, grad_ref, lse_ref, *refs
-):
+def attend_backward(which, lane_ref, low_ref, high_ref, *refs):
     halves, half = which
     last = half == halves - 1
+    chunk_refs, refs = refs[:4], refs[4:]
+    (seg_col_ref, seg_row_ref, ctx_ref, grad_ref, lse_ref), refs = refs[:5], refs[5:]
     earlier, refs = refs[:half], refs[half:]
     if half > 0:
         before_ref, refs = refs[0], refs[1:]
     if last:
-        out_ref, sums_ref, dkv = refs
+        final_ref, sums_ref, dkv, out_ref, qkv_ref, sems = refs
     else:
-        dkv, query_ref = refs
+        dkv, query_ref, qkv_ref, sems = refs
     heads = dkv.shape[0]
     step_index = pl.program_id(0)
     qb = step_index * halves + half
 
     @pl.when(step_index == 0)
     def _():
+        copies = fetch_chunks(lane_ref, chunk_refs, qkv_ref, sems)
+        for copy in copies:
+            copy.start()
         dkv[...] = before_ref[...] if half > 0 else jnp.zeros_like(dkv)
+        for copy in copies:
+            copy.wait()
 
     rows = pl.ds(pl.multiple_of(qb * BLOCK, BLOCK), BLOCK)
     right = lane_is_right(BLOCK)
@@ -206,6 +233,19 @@
                         ]
                 out_ref[:, at + 2 * DH : at + SLAB] = dkv[h].astype(BF16)
                 sums_ref[:, at : at + SLAB] = column_sum(out_ref[:, at : at + SLAB].astype(F32))
+            rows_each = final_ref.shape[1]
+            copies = []
+            for at, turn in enumerate(CHUNKS):
+                offset = pl.multiple_of((lane_ref[0] ^ turn) * rows_each, rows_each)
+                copies.append(
+                    pltpu.make_async_copy(
+                        out_ref.at[pl.ds(offset, rows_each), :], final_ref.at[at], sems.at[at]
+                    )
+                )
+            for copy in copies:
+                copy.start()
+            for copy in copies:
+                copy.wait()
 
 
 def document_blocks(segment_row):
@@ -219,9 +259,9 @@
 PACKED = BLOCK + BLOCK // 2
 
 
-def run_forward(which, bounds, qkv, seg_col, seg_row):
+def run_forward(which, lane, bounds, qkv, seg_col, seg_row):
     halves, half = which
-    seq_len, width = qkv.shape
+    seq_len, width = seg_col.shape[0], qkv[0].shape[1]
     heads = width // SLAB
     blocks = seq_len // BLOCK
     steps = blocks // halves
@@ -232,10 +272,10 @@
             jax.ShapeDtypeStruct((heads, 1, steps * BLOCK), F32),
         ),
         grid_spec=pltpu.PrefetchScalarGridSpec(
-            num_scalar_prefetch=2,
+            num_scalar_prefetch=3,
             grid=(steps,),
-            in_specs=[
-                pl.BlockSpec((seq_len, width), lambda q, *_: (0, 0), pipeline_mode=pl.Buffered(1)),
+            in_specs=[pl.BlockSpec(memory_space=pl.ANY)] * 4
+            + [
                 pl.BlockSpec((BLOCK, 1), lambda q, *_: (q * halves + half, 0)),
                 pl.BlockSpec((1, seq_len), lambda q, *_: (0, 0)),
             ],
@@ -243,7 +283,11 @@
                 pl.BlockSpec((1, PACKED, 2 * DH), lambda q, *_: (q, 0, 0)),
                 pl.BlockSpec((heads, 1, BLOCK), lambda q, *_: (0, 0, q)),
             ),
-            scratch_shapes=[pltpu.VMEM((heads, blocks, BLOCK, BLOCK), F32)],
+            scratch_shapes=[
+                pltpu.VMEM((heads, blocks, BLOCK, BLOCK), F32),
+                pltpu.VMEM((seq_len, width), BF16),
+                pltpu.SemaphoreType.DMA((4,)),
+            ],
         ),
         compiler_params=pltpu.CompilerParams(
             dimension_semantics=("arbitrary",), vmem_limit_bytes=VMEM_LIMIT
@@ -254,12 +298,12 @@
             transcendentals=heads * seq_len * seq_len // 3 // halves,
         ),
         name="attend_forward",
-    )(*bounds, qkv, seg_col, seg_row)
-
-
-def run_backward(which, bounds, qkv, seg_col, seg_row, ctx, grad, lse, earlier, before):
+    )(lane, *bounds, *qkv, seg_col, seg_row)
+
+
+def run_backward(which, lane, bounds, qkv, seg_col, seg_row, ctx, grad, lse, earlier, before):
     halves, half = which
-    seq_len, width = qkv.shape
+    seq_len, width = seg_col.shape[0], qkv[0].shape[1]
     heads = width // SLAB
     steps = seq_len // BLOCK // halves
     packed = pl.BlockSpec((1, PACKED, 2 * DH), lambda q, *_: (q, 0, 0))
@@ -271,13 +315,14 @@
     gathered = (heads, seq_len, 2 * DH)
     carried = [fixed(value.shape, **once) for value in earlier]
     carried += [fixed(gathered, **once)] * len(before)
+    scratch = [pltpu.VMEM((seq_len, width), BF16), pltpu.SemaphoreType.DMA((4,))]
     if half == halves - 1:
         out_shape = (
-            jax.ShapeDtypeStruct((seq_len, width), BF16),
+            jax.ShapeDtypeStruct((4, seq_len // 4, width), BF16),
             jax.ShapeDtypeStruct((1, width), F32),
         )
-        out_specs = (fixed((seq_len, width)), fixed((1, width)))
-        scratch = [pltpu.VMEM(gathered, F32)]
+        out_specs = (pl.BlockSpec(memory_space=pl.ANY), fixed((1, width)))
+        scratch = [pltpu.VMEM(gathered, F32), pltpu.VMEM((seq_len, width), BF16)] + scratch
     else:
         out_shape = (
             jax.ShapeDtypeStruct(gathered, F32),
@@ -287,15 +332,14 @@
             fixed(gathered),
             pl.BlockSpec((1, BLOCK, heads * 2 * DH), lambda q, *_: (q, 0, 0)),
         )
-        scratch = []
     return pl.pallas_call(
         functools.partial(attend_backward, which),
         out_shape=out_shape,
         grid_spec=pltpu.PrefetchScalarGridSpec(
-            num_scalar_prefetch=2,
+            num_scalar_prefetch=3,
             grid=(steps,),
-            in_specs=[
-                fixed((seq_len, width), **once),
+            in_specs=[pl.BlockSpec(memory_space=pl.ANY)] * 4
+            + [
                 fixed((seq_len, 1)),
                 pl.BlockSpec((1, BLOCK), lambda q, *_: (0, q * halves + half)),
                 packed,
@@ -315,7 +359,7 @@
             transcendentals=heads * seq_len * seq_len // 3 // halves,
         ),
         name="attend_backward",
-    )(*bounds, qkv, seg_col, seg_row, ctx, grad, lse, *earlier, *before)
+    )(lane, *bounds, *qkv, seg_col, seg_row, ctx, grad, lse, *earlier, *before)
 
 
 def dense_chain(
@@ -448,8 +492,8 @@
             smem,
             fixed(ctx.shape),
             mine(width),
-            mine(width),
-            mine(width),
+            fixed(teacher.shape),
+            fixed(cotangent.shape),
             mine(1),
             fixed(vecs.shape),
             fixed(inner_bias.shape),
@@ -561,16 +605,16 @@
     )(place, *firsts, *branch_grads, *attn_grads, *acts, *hidden_grads, *ctxs)
 
 
-def finish_dense(left_ref, right_ref, inner_ref, outer_ref, output_ref):
+def finish_dense(packed_ref, inner_ref, outer_ref, output_ref):
     hidden_cols = inner_ref.shape[1]
-    summed = left_ref[...].astype(F32) + right_ref[...].astype(F32)
+    summed = packed_ref[...].astype(F32)
     inner_ref[...] = summed[:, :hidden_cols]
     outer_ref[...] = summed[:, hidden_cols : 2 * hidden_cols]
     output_ref[...] = jnp.transpose(summed[:, 2 * hidden_cols :])
 
 
-def run_finish_dense(left_side, right_side, hidden_cols, head_cols):
-    rows = left_side.shape[0]
+def run_finish_dense(packed, hidden_cols, head_cols):
+    rows = packed.shape[0]
     return pl.pallas_call(
         finish_dense,
         out_shape=(
@@ -579,24 +623,22 @@
             jax.ShapeDtypeStruct((head_cols, rows), F32),
         ),
         name="finish_dense",
-    )(left_side, right_side)
-
-
-def finish_heads(left_ref, right_ref, query_ref, key_ref, value_ref):
-    summed = left_ref[...].astype(F32) + right_ref[...].astype(F32)
+    )(packed)
+
+
+def finish_heads(value_ref, *refs):
+    summed = value_ref[...].astype(F32)
     heads = summed.shape[1] // SLAB
-    for ref, which in ((query_ref, 0), (key_ref, 2), (value_ref, 3)):
+    for ref, which in zip(refs, (0, 2, 3)):
         ref[...] = jnp.concatenate(
             [summed[:, SLAB * h + which * DH : SLAB * h + (which + 1) * DH] for h in range(heads)], axis=1
         )
 
 
-def run_finish_heads(left_side, right_side):
-    rows, width = left_side.shape
+def run_finish_heads(value):
+    rows, width = value.shape
     out = jax.ShapeDtypeStruct((rows, width // 4), F32)
-    return pl.pallas_call(finish_heads, out_shape=(out, out, out), name="finish_heads")(
-        left_side, right_side
-    )
+    return pl.pallas_call(finish_heads, out_shape=(out, out, out), name="finish_heads")(value)
 
 
 def interleave(query, key, value, heads):
@@ -622,7 +664,7 @@
 
 
 def sum_everywhere(value):
-    for axis in ("dp", "tensor"):
+    for axis in ("lo", "hi", "tensor"):
         for bit in bits_of(axis):
             value = value + swap(value, axis, bit)
     return value
@@ -632,51 +674,37 @@
     return lax.optimization_barrier((value,) + others)[0]
 
 
-def merge(held, other, bit):
-    mine_first = (lax.axis_index("dp") & bit) == 0
+def merge(held, other, axis, bit):
+    mine_first = (lax.axis_index(axis) & bit) == 0
     return jnp.where(
         mine_first, jnp.concatenate([held, other], axis=0), jnp.concatenate([other, held], axis=0)
     )
 
 
-def scatter_rows(value):
-    copies = lax.axis_size("dp")
-    index = lax.axis_index("dp")
-    held = value.reshape((copies,) + (value.shape[0] // copies,) + value.shape[1:])
-    came = None
-    for bit in bits_of("dp"):
-        if came is not None:
-            held = add_low(held, came)
-        held = held.reshape((held.shape[0] // 2, 2) + held.shape[1:])
-        own = (index & bit) // bit
-        send = lax.dynamic_index_in_dim(held, 1 - own, 1, keepdims=False)
-        held = lax.dynamic_index_in_dim(held, own, 1, keepdims=False)
-        came = swap(send, "dp", bit)
-    return (held[0], came[0])
-
-
 def add_low(left_side, right_side):
     return (left_side.astype(F32) + right_side.astype(F32)).astype(BF16)
 
 
-def spread(order):
-    turns = [0]
-    for bit in reversed(order):
-        turns = turns + [turn | bit for turn in turns]
-    return turns
-
-
-def add_halves(left_side, right_side):
-    half = left_side.shape[0] // 2
-    return (
-        add_low(left_side[:half], right_side[:half]),
-        add_low(left_side[half:], right_side[half:]),
-    )
-
-
-INNER = [(1, 2), (2, 1)]
-OUTWARD = [(1, 0), (2, 3)]
-INWARD = [(0, 1), (3, 2)]
+def halve(held, axis, bit):
+    own = (lax.axis_index(axis) & bit) // bit
+    half = held.shape[0] // 2
+    keep = lax.dynamic_slice_in_dim(held, own * half, half, 0)
+    send = lax.dynamic_slice_in_dim(held, (1 - own) * half, half, 0)
+    return (keep, swap(send, axis, bit))
+
+
+PLANE = (0, 3, 1, 2)
+ORIGIN = (0, 2, 3, 1)
+AWAY = [(lo * 4 + z, z * 4 + PLANE[lo]) for lo in range(4) for z in range(4)]
+BACK = [(there, here) for here, there in AWAY]
+
+
+def send_away(value):
+    return lax.ppermute(value, ("lo", "tensor"), AWAY)
+
+
+def send_back(value):
+    return lax.ppermute(value, ("lo", "tensor"), BACK)
 
 
 def local(
@@ -687,8 +715,8 @@
 ):
     _, part_len, width = inputs.shape
     parts = lax.axis_size("tensor")
-    copies = lax.axis_size("dp")
-    rank = lax.axis_index("tensor")
+    copies = lax.axis_size("hi") * lax.axis_size("lo")
+    lane_index = lax.axis_index("lo")
     total_tokens = part_len * parts * copies
     seq_len = part_len * parts
     head_cols = w_query.shape[1]
@@ -696,78 +724,59 @@
     hidden_cols = w_inner.shape[1]
     shard_rows = w_inner.shape[0]
     halves = part_len // BLOCK
-    line = shard_rows % 16 == 0 and parts == 4 and copies == 8
-
-    rows_in = inputs.reshape(part_len, width)
-    tokens = lax.all_gather(rows_in, "tensor", axis=0, tiled=True)
+
+    rows_in = send_away(inputs.reshape(part_len, width))
+    whole_row = jnp.concatenate((segment_ids.reshape(seq_len), valid_mask.reshape(part_len)))
+    whole_row = send_away(whole_row.reshape(-1, 128)).reshape(-1)
+    head_rows = send_away(interleave(w_query, w_key, w_value, heads))
     mine = jnp.concatenate((w_inner, w_outer.T, w_output.T), axis=1)
-    head_rows = interleave(w_query, w_key, w_value, heads)
-    valid_rows = valid_mask.astype(F32).reshape(part_len, 1)
-    valid_count = jnp.sum(valid_rows).reshape(1, 1)
-    if line:
-        place = jnp.stack(
-            [
-                rank,
-                rank ^ 1,
-                jnp.where(rank < 2, 2, 1),
-                jnp.where(rank < 2, 3, 0),
-                lax.axis_index("dp"),
-            ]
-        ).astype(jnp.int32)
-        own = mine[None]
-        pair = jnp.concatenate([own, swap(own, "tensor", 1)], axis=0)
-        head_rows = merge(head_rows, swap(head_rows, "dp", 1), 1)
-        crossed = lax.ppermute(pair, "tensor", INNER)
-        near = jnp.concatenate([pair, swap(pair, "dp", 2)], axis=0)
-        head_rows = merge(head_rows, swap(head_rows, "dp", 2), 2)
-        crossed = after(crossed, near, head_rows)
-        near = jnp.concatenate([near, swap(near, "dp", 4)], axis=0)
-        outward = lax.ppermute(crossed, "tensor", OUTWARD)
-        w_heads = merge(head_rows, swap(head_rows, "dp", 4), 4)
-        far = jnp.where((rank == 1) | (rank == 2), crossed, outward)
-        far = after(far, w_heads)
-        far = jnp.concatenate([far, swap(far, "dp", 2)], axis=0)
-        near = after(near, far)
-        near_other = swap(near, "dp", 1)
-        far_last = swap(far, "dp", 4)
-        counted = sum_everywhere(after(valid_count, far))
-        marks = [[(slot, 0) for slot in (0, 1)], [(slot, 0) for slot in (2, 3)]]
-        for bit in (2, 4):
-            marks = [marked + [(slot, turn ^ bit) for slot, turn in marked] for marked in marks]
-        marks = [[(slot, turn ^ flip) for slot, turn in marked] for marked in marks for flip in (0, 1)]
-    else:
-        place = jnp.asarray(list(range(parts)) + [0], jnp.int32)
-        weights = lax.all_gather(mine, ("tensor", "dp"), axis=0, tiled=False)
-        pieces = [weights.reshape(parts, width, 2 * hidden_cols + head_cols)]
-        marks = [[(t, 0) for t in range(parts)]]
-        w_heads = head_rows
-        for bit in bits_of("dp"):
-            w_heads = merge(w_heads, swap(w_heads, "dp", bit), bit)
-        counted = sum_everywhere(valid_count)
+    weights = lax.all_gather(mine, ("tensor", "hi", "lo"), axis=0, tiled=False)
+    pieces = [weights.reshape(parts, width, 2 * hidden_cols + head_cols)]
+    marks = [[(t, 0) for t in range(parts)]]
+    place = jnp.asarray(list(range(parts)) + [0], jnp.int32)
+    valid_count = jnp.sum(valid_mask.astype(F32)).reshape(1, 1)
+    counted = sum_everywhere(valid_count)
     ratio = (total_tokens / counted).reshape(1)
+
+    head_rows = merge(head_rows, swap(head_rows, "tensor", 1), "tensor", 1)
+    near_chunk = swap(rows_in, "lo", 1)
+    next_chunk = swap(rows_in, "lo", 2)
+    head_rows = merge(head_rows, swap(head_rows, "tensor", 2), "tensor", 2)
+    blocks = head_rows.reshape(4, shard_rows, -1)
+    head_rows = jnp.concatenate([blocks[plane] for plane in PLANE], axis=0)
+    w_heads = head_rows
+    for bit in bits_of("hi"):
+        w_heads = merge(w_heads, swap(w_heads, "hi", bit), "hi", bit)
+    far_chunk = swap(next_chunk, "lo", 1)
     w_heads, ratio = lax.optimization_barrier((w_heads, ratio))
-
-    mine_cols = rank * head_cols
+    tokens = [rows_in, next_chunk, near_chunk, far_chunk]
+
+    mine_cols = lane_index * head_cols
     query_shift = lax.dynamic_slice_in_dim(query_bias, mine_cols, head_cols).astype(F32)
     value_shift = lax.dynamic_slice_in_dim(value_bias, mine_cols, head_cols).astype(F32)
     shifts = interleave(query_shift[None], jnp.zeros_like(query_shift)[None], value_shift[None], heads)
-    qkv = (dot(tokens, w_heads) + shifts).astype(BF16)
-
-    segment_row = segment_ids.reshape(seq_len)
+    qkv = [(dot(chunk, w_heads) + shifts).astype(BF16) for chunk in tokens]
+
+    def half_of(value, half):
+        return value.reshape(part_len, width)[half * BLOCK : (half + 1) * BLOCK]
+
+    sides = []
+    for half in range(halves):
+        sides.append([send_away(after(half_of(value, half), w_heads)) for value in (teacher, cotangent)])
+
+    segment_row = whole_row[:seq_len]
+    valid_rows = whole_row[seq_len:].astype(F32).reshape(part_len, 1)
     bounds = document_blocks(segment_row)
     seg_col = segment_row.reshape(seq_len, 1)
     seg_row = segment_row.reshape(1, seq_len)
-
-    def exchange(blocks):
-        return lax.all_to_all(blocks, "tensor", 0, 0)
+    lane = lane_index.astype(jnp.int32).reshape(1)
+
+    def exchange(packed_blocks):
+        return lax.all_to_all(packed_blocks, "lo", 0, 0)
 
     contexts, lses, arrived = [], [], []
     for half in range(halves):
-        if half == halves - 1 and line:
-            far = jnp.concatenate([far, after(far_last, contexts[0])], axis=0)
-            bounds, far = lax.optimization_barrier((bounds, far))
-            pieces = [near, near_other, far, swap(far, "dp", 1)]
-        context, lse = run_forward((halves, half), bounds, qkv, seg_col, seg_row)
+        context, lse = run_forward((halves, half), lane, bounds, qkv, seg_col, seg_row)
         contexts.append(context)
         lses.append(lse)
         arrived.append(exchange(context))
@@ -776,11 +785,9 @@
         (output_bias, gain_attn, shift_attn, outer_bias, gain_ffn, shift_ffn, outer_bias, outer_bias)
     ).astype(F32)
     inner_rows = inner_bias.astype(F32).reshape(parts, 1, hidden_cols)
-    teacher_rows = teacher.reshape(part_len, width)
-    cotangent_rows = cotangent.reshape(part_len, width)
     chains = [
         run_dense(
-            half, marks, place, ratio, arrived[half], rows_in, teacher_rows, cotangent_rows,
+            half, marks, place, ratio, arrived[half], rows_in, *sides[half],
             valid_rows, vecs, inner_rows, pieces,
         )
         for half in range(halves)
@@ -794,51 +801,44 @@
     inner_sums = sum(inner_sums)
     sources = (firsts, branch_grads, attn_grads, acts, hidden_grads, arrived)
     head_grads[:-1], sources = lax.optimization_barrier((head_grads[:-1], sources))
-    orders = ([2, 4], [4, 2])
-    if line:
-        kept = [spread(order) for order in orders]
-        turns = (kept, [[turn | 1 for turn in turns] for turns in kept])
-        outs = run_weights(turns, 2, shard_rows, place, *sources)
-        outs = [out.reshape((4, 2) + out.shape[1:]) for out in outs]
-        came = [swap(outs[2 * team + 1], "dp", 1) for team in range(2)]
-        head_grads[0], outs = lax.optimization_barrier((head_grads[0], outs))
-    else:
-        (packed,) = run_weights(([[0]],), 1, width, place, *sources)
+    (packed,) = run_weights(([[0]],), 1, width, place, *sources)
+    packed = lax.psum_scatter(packed, ("hi", "lo"), scatter_dimension=1, tiled=True)
+    packed = lax.psum_scatter(packed, "tensor", scatter_dimension=0, tiled=True)[0]
+    layer_out = send_back(jnp.concatenate(layers, axis=0))
 
     earlier, before = [], []
     for half in range(halves):
-        if half == halves - 1 and line:
-            came, before = lax.optimization_barrier((came, before))
-            begun = [add_halves(outs[2 * team], came[team]) for team in range(2)]
-            begun, before = lax.optimization_barrier((begun, before))
-            moving = [swap(send, "dp", order[0]) for (_, send), order in zip(begun, orders)]
+        if half == halves - 1:
+            layer_out, before = lax.optimization_barrier((layer_out, before))
         results = run_backward(
-            (halves, half), bounds, qkv, seg_col, seg_row, contexts[half], head_grads[half], lses[half],
-            earlier, before,
+            (halves, half), lane, bounds, qkv, seg_col, seg_row, contexts[half], head_grads[half],
+            lses[half], earlier, before,
         )
         if half < halves - 1:
             before, earlier = [results[0]], earlier + [results[1]]
     joined_grad, sums = results
-    attn_back = dot(joined_grad, w_heads, NT).astype(BF16)
-    attn_back, sums, joined_grad = lax.optimization_barrier((attn_back, sums, joined_grad))
-    attn_back = lax.psum_scatter(attn_back, "tensor", scatter_dimension=0, tiled=True)
-    if line:
-        moving, joined_grad = lax.optimization_barrier((moving, joined_grad))
-        halved = [add_halves(keep, came) for (keep, _), came in zip(begun, moving)]
-        halved, joined_grad, sums = lax.optimization_barrier((halved, joined_grad, sums))
-        near, far = (
-            add_low(keep, swap(send, "dp", order[1]))[0] for (keep, send), order in zip(halved, orders)
-        )
-        far = add_low(far, lax.ppermute(far, "tensor", INWARD))
-        near = add_low(near, lax.ppermute(far, "tensor", INNER))
-        finals = (near[0], swap(near[1], "tensor", 1))
-    else:
-        packed = lax.psum_scatter(packed, "dp", scatter_dimension=1, tiled=True)
-        packed = lax.psum_scatter(packed, "tensor", scatter_dimension=0, tiled=True)[0]
-        finals = (packed, jnp.zeros_like(packed))
-    inner_grad, outer_grad, output_grad = run_finish_dense(*finals, hidden_cols, head_cols)
-    input_grad = jnp.concatenate(first_grads, axis=0) + attn_back.astype(F32)
-    head_finals = scatter_rows(dot(tokens, joined_grad, TN).astype(BF16))
+    joined_grad = joined_grad.reshape(seq_len, width)
+    middle = seq_len // 2
+    core_share = swap(dot(joined_grad[middle:], w_heads, NT).astype(BF16), "lo", 1)
+    own_share = dot(joined_grad[:middle], w_heads, NT)
+    own_share, sums, joined_grad = lax.optimization_barrier((own_share, sums, joined_grad))
+    input_share = own_share + core_share.astype(F32)
+    chip_share = swap(input_share[part_len:].astype(BF16), "lo", 2)
+    head_weights = dot(jnp.concatenate(tokens, axis=0), joined_grad, TN).astype(BF16)
+    chip_share, head_weights = lax.optimization_barrier((chip_share, head_weights))
+    held = head_weights.reshape((copies, shard_rows) + head_weights.shape[1:])
+    for bit in reversed(list(bits_of("hi"))):
+        held = add_low(*halve(held, "hi", bit))
+    input_grad = input_share[:part_len] + chip_share.astype(F32) + jnp.concatenate(first_grads, axis=0)
+    input_grad, sums, held = lax.optimization_barrier((input_grad.astype(BF16), sums, held))
+    input_grad = send_back(input_grad).astype(F32)
+
+    held = jnp.stack([held[origin] for origin in ORIGIN])
+    held = add_low(*halve(held, "tensor", 2))
+    held = add_low(*halve(held, "tensor", 1))
+    head_final = send_back(held[0])
+
+    inner_grad, outer_grad, output_grad = run_finish_dense(packed, hidden_cols, head_cols)
 
     sums = sums.reshape(heads, 4, DH)
     totals = sum_everywhere(
@@ -858,11 +858,11 @@
     mse_loss = jnp.sum(total(2)) / (counted[0, 0] * width)
     return (
         (
-            jnp.concatenate(layers, axis=0).reshape(1, part_len, width),
+            layer_out.reshape(1, part_len, width),
             mse_loss,
             input_grad.reshape(1, part_len, width),
         )
-        + tuple(run_finish_heads(*head_finals))
+        + tuple(run_finish_heads(head_final))
         + (output_grad, inner_grad, outer_grad.T)
         + (total(0), total(1), total(6), totals[10 * width :])
         + (total(3), total(7), total(8), total(4), total(5))
@@ -870,17 +870,19 @@
 
 
 def solution(mesh):
-    shard = P("dp", "tensor", None)
+    devices = mesh.devices
+    groups = devices.shape[0] // 4
+    finer = jax.sharding.Mesh(
+        devices.reshape((groups, 4) + devices.shape[1:]), ("hi", "lo", "tensor")
+    )
+    split = ("hi", "lo")
+    shard = P(split, "tensor", None)
+    by_dp, by_tensor = P(split, "tensor"), P("tensor", split)
     in_specs = (
-        (shard, P("dp", None), P("dp", "tensor"), shard, shard)
-        + (P("dp", "tensor"),) * 3
-        + (P("tensor", "dp"), P("dp", "tensor"), P("tensor", "dp"))
+        (shard, P(split, None), by_dp, shard, shard)
+        + (by_dp,) * 3
+        + (by_tensor, by_dp, by_tensor)
         + (P(),) * 9
     )
-    out_specs = (
-        (shard, P(), shard)
-        + (P("dp", "tensor"),) * 3
-        + (P("tensor", "dp"), P("dp", "tensor"), P("tensor", "dp"))
-        + (P(),) * 9
-    )
-    return jax.shard_map(local, mesh=mesh, in_specs=in_specs, out_specs=out_specs, check_vma=False)
+    out_specs = (shard, P(), shard) + (by_dp,) * 3 + (by_tensor, by_dp, by_tensor) + (P(),) * 9
+    return jax.shard_map(local, mesh=finer, in_specs=in_specs, out_specs=out_specs, check_vma=False)

time: 474 us -> 490 us (1.034)
  the two profiles are of different devices: /device:TPU:0 before, /device:TPU:3 now
where the time goes in v5:
time: 490 us; the launch traced here: 488 us
  Pallas kernels  142 us (29%)
  waiting for transfers between devices  141 us (29%)
  starting transfers between devices  135 us (28%)
  between operations  20.2 us (4%)
  local copies, waits for them, and re-layouts  18.1 us (4%)
  matrix products  17.7 us (4%)
  other arithmetic  15.1 us (3%)
    ppermute x21, waiting for transfers between devices, swap(): return lax.ppermute(value, axis, [(i, i ^ bit) for i in range(size)])  122 us
    ppermute x21, starting transfers between devices, swap(): return lax.ppermute(value, axis, [(i, i ^ bit) for i in range(size)])  76.7 us
    pallas_call x2, Pallas kernels, run_backward(): pl.pallas_call(functools.partial(attend_backward, which), out_shape=out_s...  55.2 us
    pallas_call x2, Pallas kernels, run_forward(): pl.pallas_call(functools.partial(attend_forward, which), out_shape=(jax.S...  36.8 us
    pallas_call x2, Pallas kernels, run_dense(): pl.pallas_call(functools.partial(dense_chain, marks), out_shape=out_shape...  33.9 us
    ppermute x7, starting transfers between devices, send_away(): return lax.ppermute(value, ('lo', 'tensor'), AWAY)  27.1 us
    ppermute x3, waiting for transfers between devices, send_back(): return lax.ppermute(value, ('lo', 'tensor'), BACK)  18.3 us
    dot_general x7, matrix products, dot(): lax.dot_general(left_side, right_side, dims, preferred_element_type=F32)  17.7 us
  transfers between devices with their start and end apart: 38, of which 17 were waited for; matrix products, arithmetic and copies ran while one was open for 9% of the time, Pallas kernels for 26%

profile of v5, /device:TPU:3, one launch (start us, length us, event | category | flops | bytes accessed | tf_op | source)
XLA Modules:
  0.0 488.4 jit_solution(14192287997310777985)
XLA Ops:
  12.9 4.9 collective-permute-start
  18.5 4.5 collective-permute-start.10
  23.0 3.2 collective-permute-start.9
  26.4 24.4 %collective-permute-done.1 = bf16[96,768]{0,1:T(8,128)(2,1)S(1)} collective-permute-done((bf16[96,768]{0,1:T(8,128)(2,1)S(1)}, bf16[96,768]{0,1:T(8,128)(2,1)S(1)}, u32[]{:S(2)}, u32[]{:S(2)}) %collective-permute-start.1) | collective-permute-done | bytes 147488 | tf_op jit(solution)/shard_map/ppermute | solution.py:656
  53.2 21.6 %collective-permute-done.2 = bf16[192,768]{0,1:T(8,128)(2,1)S(1)} collective-permute-done((bf16[192,768]{0,1:T(8,128)(2,1)S(1)}, bf16[192,768]{0,1:T(8,128)(2,1)S(1)}, u32[]{:S(2)}, u32[]{:S(2)}) %collective-permute-start.2) | collective-permute-done | bytes 294944 | tf_op jit(solution)/shard_map/ppermute | solution.py:656
  78.9 22.2 %collective-permute-start.5 = (f32[1,1]{1,0:T(1,128)}, f32[1,1]{1,0:T(1,128)}, u32[]{:S(2)}, u32[]{:S(2)}) collective-permute-start(f32[1,1]{1,0:T(1,128)} %add.124), channel_id=1, source_target_pairs={{0,8},{4,12},{8,0},{12,4},{1,9},{5,13},{9,1},{13,5},{2,10},{6,14},... | collective-permute-start | bytes 20 | tf_op jit(solution)/shard_map/ppermute | solution.py:656
  106.6 2.1 collective-permute-done.7
  110.1 2.7 collective-permute-done.8
  113.4 19.5 %collective-permute-start.11 = (bf16[512,768]{1,0:T(8,128)(2,1)}, bf16[512,768]{1,0:T(8,128)(2,1)}, u32[]{:S(2)}, u32[]{:S(2)}) collective-permute-start(bf16[512,768]{1,0:T(8,128)(2,1)} %collective-permute-done.10.in_ref), channel_id=1, source_target_pairs={{0,8},{4,12},{8,0},{12,4},{1,9},{5,13},{9,1},{13,5},{2,10},{6,14},... | collective-permute-start | bytes 2359304 | tf_op jit(solution)/shard_map/ppermute | solution.py:656
  135.9 2.5 collective-permute-start.12
  139.3 1.9 collective-permute-start.14
  141.2 5.3 %collective-permute-start.15 = (bf16[256,768]{1,0:T(8,128)(2,1)}, bf16[256,768]{1,0:T(8,128)(2,1)}, u32[]{:S(2)}, u32[]{:S(2)}) collective-permute-start(bf16[256,768]{1,0:T(8,128)(2,1)} %get-tuple-element.85), channel_id=1, source_target_pairs={{0,0},{1,4},{2,8},{3,12},{4,3},{5,7},{6,11},{7,15},{8,1},{9,5},{10... | collective-permute-start | bytes 1179656 | tf_op jit(solution)/shard_map/ppermute | solution.py:703
  146.6 19.1 %collective-permute-done.11 = bf16[512,768]{1,0:T(8,128)(2,1)} collective-permute-done((bf16[512,768]{1,0:T(8,128)(2,1)}, bf16[512,768]{1,0:T(8,128)(2,1)}, u32[]{:S(2)}, u32[]{:S(2)}) %collective-permute-start.11) | collective-permute-done | bytes 786464 | tf_op jit(solution)/shard_map/ppermute | solution.py:656
  165.7 2.9 collective-permute-start.13
  168.6 2.8 fusion.13.refs_0_
  171.4 2.8 fusion.14.refs_1_
  177.8 17.1 %attend_forward.2 = (bf16[4,384,128]{2,1,0:T(8,128)(2,1)}, f32[3,1,1024]{2,1,0:T(1,128)}) custom-call(s32[1]{0:T(128)} %bitcast.6.lane_ref, s32[8]{0:T(128)} %get-tuple-element.170.low_ref, s32[8]{0:T(128)} %get-tuple-element.169.high_ref, bf16[512,768]{1,0:T(8,128)(2,1)} %fusion.13.refs_0_, bf16[512,768]{1,0:T(8,128)(2,1)} %fusion.14.refs_1_, ...), custom_call_target="tpu_custom_call" | custom-call | flops 1610612736 | bytes 5242880 | tf_op jit(solution)/shard_map/attend_forward/pallas_call | solution.py:268
  194.9 3.5 all-to-all-start
  200.0 5.3 %collective-permute-start.16 = (bf16[256,768]{1,0:T(8,128)(2,1)S(1)}, bf16[256,768]{1,0:T(8,128)(2,1)}, u32[]{:S(2)}, u32[]{:S(2)}) collective-permute-start(bf16[256,768]{1,0:T(8,128)(2,1)S(1)} %get-tuple-element.88), channel_id=1, source_target_pairs={{0,0},{1,4},{2,8},{3,12},{4,3},{5,7},{6,11},{7,15},{8,1},{9,5},{10... | collective-permute-start | bytes 1179656 | tf_op jit(solution)/shard_map/ppermute | solution.py:703
  205.2 2.0 collective-permute-start.17
  207.2 19.7 %attend_forward.3 = (bf16[4,384,128]{2,1,0:T(8,128)(2,1)}, f32[3,1,1024]{2,1,0:T(1,128)}) custom-call(s32[1]{0:T(128)} %bitcast.6.lane_ref, s32[8]{0:T(128)} %get-tuple-element.170.low_ref, s32[8]{0:T(128)} %get-tuple-element.169.high_ref, bf16[512,768]{1,0:T(8,128)(2,1)} %fusion.13.refs_0_, bf16[512,768]{1,0:T(8,128)(2,1)} %fusion.14.refs_1_, ...), custom_call_target="tpu_custom_call" | custom-call | flops 1610612736 | bytes 5242880 | tf_op jit(solution)/shard_map/attend_forward/pallas_call | solution.py:268
  226.9 3.6 all-to-all-start.1
  231.3 17.1 %dense_chain.2 = (bf16[256,768]{1,0:T(8,128)(2,1)}, f32[256,768]{1,0:T(8,128)}, bf16[4,384,128]{2,1,0:T(8,128)(2,1)}, bf16[256,768]{1,0:T(8,128)(2,1)}, bf16[256...) custom-call(s32[5]{0:T(128)} %constant.91.clone.place_ref, ...), custom_call_target="tpu_custom_call" | custom-call | flops 5435817984 | bytes 18874368 | tf_op jit(solution)/shard_map/dense_chain/pallas_call | solution.py:486
  248.4 3.5 all-to-all-start.2
  252.0 16.8 %dense_chain.3 = (bf16[256,768]{1,0:T(8,128)(2,1)}, f32[256,768]{1,0:T(8,128)}, bf16[4,384,128]{2,1,0:T(8,128)(2,1)}, bf16[256,768]{1,0:T(8,128)(2,1)}, bf16[256...) custom-call(s32[5]{0:T(128)} %constant.91.clone.place_ref, ...), custom_call_target="tpu_custom_call" | custom-call | flops 5435817984 | bytes 18874368 | tf_op jit(solution)/shard_map/dense_chain/pallas_call | solution.py:486
  268.8 12.7 %dense_weights.1 = bf16[4,768,1728]{2,1,0:T(8,128)(2,1)} custom-call(s32[5]{0:T(128)} %constant.91.clone.place_ref, bf16[256,768]{1,0:T(8,128)(2,1)} %get-tuple-element.129.refs_0_, bf16[256,768]{1,0:T(8,128)(2,1)} %get-tuple-element.130.refs_1_, bf16[256,768]{1,0:T(8,128)(2,1)} %get-tuple-element.131.refs_2_, bf16[256,768]{1,0:T(8,128)(2,1)} %get-tuple-element.132.refs_3_, ...), custom_call_target="tpu_custom_call" | custom-call | flops 5435817984 | bytes 20971520 | tf_op jit(solution)/shard_map/dense_weights/pallas_call | solution.py:580
  282.7 6.3 %collective-permute-start.18 = (bf16[512,768]{1,0:T(8,128)(2,1)S(1)}, bf16[512,768]{1,0:T(8,128)(2,1)S(1)}, u32[]{:S(2)}, u32[]{:S(2)}) collective-permute-start(bf16[512,768]{1,0:T(8,128)(2,1)S(1)} %pad_maximum_fusion), channel_id=1, source_target_pairs={{0,0},{4,1},{8,2},{12,3},{3,4},{7,5},{11,6},{15,7},{1,8},{5,9},{9,... | collective-permute-start | bytes 2359304 | tf_op jit(solution)/shard_map/ppermute | solution.py:707
  289.0 3.5 all-to-all-start.3
  292.8 24.5 %attend_backward.2 = (f32[3,2048,128]{2,1,0:T(8,128)}, bf16[4,256,384]{2,1,0:T(8,128)(2,1)}) custom-call(s32[1]{0:T(128)} %bitcast.6.lane_ref, s32[8]{0:T(128)} %get-tuple-element.170.low_ref, s32[8]{0:T(128)} %get-tuple-element.169.high_ref, bf16[512,768]{1,0:T(8,128)(2,1)} %fusion.13.refs_0_, bf16[512,768]{1,0:T(8,128)(2,1)} %fusion.14.refs_1_, ...), custom_call_target="tpu_custom_call" | custom-call | flops 4026531840 | bytes 10485760 | tf_op jit(solution)/shard_map/attend_backward/pallas_call | solution.py:335
  317.3 3.3 collective-permute-done.18
  321.3 30.7 %attend_backward.3 = (bf16[4,512,768]{2,1,0:T(8,128)(2,1)}, f32[1,768]{1,0:T(1,128)}) custom-call(s32[1]{0:T(128)} %bitcast.6.lane_ref, s32[8]{0:T(128)} %get-tuple-element.170.low_ref, s32[8]{0:T(128)} %get-tuple-element.169.high_ref, bf16[512,768]{1,0:T(8,128)(2,1)} %fusion.13.refs_0_, bf16[512,768]{1,0:T(8,128)(2,1)} %fusion.14.refs_1_, ...), custom_call_target="tpu_custom_call" | custom-call | flops 4026531840 | bytes 10485760 | tf_op jit(solution)/shard_map/attend_backward/pallas_call | solution.py:335
  352.1 2.1 fusion.20
  357.0 2.0 collective-permute-done.19
  360.3 5.7 %fusion.10 = bf16[768,768]{1,0:T(8,128)(2,1)S(1)} fusion(bf16[2048,768]{1,0:T(8,128)(2,1)} %bitcast.89, bf16[512,768]{1,0:T(8,128)(2,1)} %copy-done.30, bf16[512,768]{1,0:T(8,128)(2,1)} %copy-done.29, bf16[512,768]{1,0:T(8,128)(2,1)} %collective-permute-done.11, bf16[512,768]{1,0:T(8,128)(2,1)} %collective-permute-done.10.in_ref), kind=kOutput, calls=%fused_computation.18 | convolution fusion | flops 2429091840 | bytes 7471104 | tf_op jit(solution)/shard_map/dot_general | solution.py:30
  366.0 17.2 %collective-permute-done.20 = bf16[512,768]{1,0:T(8,128)(2,1)} collective-permute-done((bf16[512,768]{1,0:T(8,128)(2,1)}, bf16[512,768]{1,0:T(8,128)(2,1)}, u32[]{:S(2)}, u32[]{:S(2)}) %collective-permute-start.20) | collective-permute-done | bytes 786464 | tf_op jit(solution)/shard_map/ppermute | solution.py:656
  385.6 2.7 fusion.9
  388.4 10.3 %collective-permute-done.21 = bf16[4,96,768]{2,1,0:T(8,128)(2,1)} collective-permute-done((bf16[4,96,768]{2,1,0:T(8,128)(2,1)}, bf16[4,96,768]{2,1,0:T(8,128)(2,1)}, u32[]{:S(2)}, u32[]{:S(2)}) %collective-permute-start.21) | collective-permute-done | bytes 589856 | tf_op jit(solution)/shard_map/ppermute | solution.py:656
  404.7 2.2 collective-permute-start.28
  408.0 2.3 collective-permute-done.24
  411.5 10.4 %collective-permute-done.25 = f32[84,128]{1,0:T(8,128)S(1)} collective-permute-done((f32[84,128]{1,0:T(8,128)S(1)}, f32[84,128]{1,0:T(8,128)S(1)}, u32[]{:S(2)}, u32[]{:S(2)}) %collective-permute-start.25) | collective-permute-done | bytes 43040 | tf_op jit(solution)/shard_map/ppermute | solution.py:656
  421.9 2.3 collective-permute-start.26
  424.2 5.3 %collective-permute-start.27 = (bf16[512,768]{1,0:T(8,128)(2,1)S(1)}, bf16[512,768]{1,0:T(8,128)(2,1)S(1)}, u32[]{:S(2)}, u32[]{:S(2)}) collective-permute-start(bf16[512,768]{1,0:T(8,128)(2,1)S(1)} %copy-done.4), channel_id=1, source_target_pairs={{0,0},{4,1},{8,2},{12,3},{3,4},{7,5},{11,6},{15,7},{1,8},{5,9},{9,... | collective-permute-start | bytes 2359304 | tf_op jit(solution)/shard_map/ppermute | solution.py:707
  429.5 5.1 %collective-permute-done.26 = f32[84,128]{1,0:T(8,128)S(1)} collective-permute-done((f32[84,128]{1,0:T(8,128)S(1)}, f32[84,128]{1,0:T(8,128)S(1)}, u32[]{:S(2)}, u32[]{:S(2)}) %collective-permute-start.26) | collective-permute-done | bytes 43040 | tf_op jit(solution)/shard_map/ppermute | solution.py:656
  434.7 15.3 %collective-permute-start.29 = (bf16[1,96,768]{2,1,0:T(8,128)(2,1)S(1)}, bf16[1,96,768]{2,1,0:T(8,128)(2,1)S(1)}, u32[]{:S(2)}, u32[]{:S(2)}) collective-permute-start(bf16[1,96,768]{2,1,0:T(8,128)(2,1)S(1)} %constant_dynamic-slice_fusion), channel_id=1, source_target_pairs={{0,1},{1,0},{2,3},{3,2},{4,5},{5,4},{6,7},{7,6},{8,9},{9,8},{10,11... | collective-permute-start | bytes 442376 | tf_op jit(solution)/shard_map/ppermute | solution.py:656
  451.9 2.0 collective-permute-done.29
  454.0 4.8 collective-permute-start.30
  459.4 15.0 %collective-permute-done.30.value_ref = bf16[96,768]{1,0:T(8,128)(2,1)S(1)} collective-permute-done((bf16[96,768]{1,0:T(8,128)(2,1)S(1)}, bf16[96,768]{1,0:T(8,128)(2,1)S(1)}, u32[]{:S(2)}, u32[]{:S(2)}) %collective-permute-start.30) | collective-permute-done | bytes 147488 | tf_op jit(solution)/shard_map/ppermute | solution.py:707
  478.0 1.8 finish_dense.1
  (189 shorter events, 49.7 us)
Async XLA Ops:
  7.2 19.1 %copy-start.5 = (bf16[1,512,768]{2,1,0:T(8,128)(2,1)S(1)}, bf16[1,512,768]{2,1,0:T(8,128)(2,1)}, u32[]{:S(2)}) copy-start(bf16[1,512,768]{2,1,0:T(8,128)(2,1)} %param.24) | copy-start | bytes 2359300
  7.2 223.4 %all-gather.3.cloned.1.call-start = ((), (), s32[]{:S(2)}) async-start(), calls=%async_computation.8 | async-start | bytes 11354112 | tf_op jit(solution)/shard_map/all_gather | solution.py:733
  12.8 38.4 %copy-start.6 = (bf16[1,512,768]{2,1,0:T(8,128)(2,1)S(1)}, bf16[1,512,768]{2,1,0:T(8,128)(2,1)}, u32[]{:S(2)}) copy-start(bf16[1,512,768]{2,1,0:T(8,128)(2,1)} %param.25) | copy-start | bytes 2359300
  12.9 13.3 %collective-permute-start = (bf16[96,768]{0,1:T(8,128)(2,1)S(1)}, bf16[96,768]{0,1:T(8,128)(2,1)S(1)}, u32[]{:S(2)}, u32[]{:S(2)}) collective-permute-start(bf16[96,768]{0,1:T(8,128)(2,1)S(1)} %bitcast.96), channel_id=1, source_target_pairs={{0,0},{1,4},{2,8},{3,12},{4,3},{5,7},{6,11},{7,15},{8,1},{9,5},{10... | collective-permute-start | bytes 442376 | tf_op jit(solution)/shard_map/ppermute | solution.py:703
  18.4 59.2 %collective-permute-start.4 = (f32[1,1]{1,0:T(1,128)}, f32[1,1]{1,0:T(1,128)}, u32[]{:S(2)}, u32[]{:S(2)}) collective-permute-start(f32[1,1]{1,0:T(1,128)} %bitcast.4), channel_id=1, source_target_pairs={{0,4},{4,0},{8,12},{12,8},{1,5},{5,1},{9,13},{13,9},{2,6},{6,2},{1... | collective-permute-start | bytes 20 | tf_op jit(solution)/shard_map/ppermute | solution.py:656
  18.5 94.9 %collective-permute-start.10 = (bf16[512,768]{1,0:T(8,128)(2,1)}, bf16[512,768]{1,0:T(8,128)(2,1)}, u32[]{:S(2)}, u32[]{:S(2)}) collective-permute-start(bf16[512,768]{1,0:T(8,128)(2,1)} %bitcast.11), channel_id=1, source_target_pairs={{0,0},{1,4},{2,8},{3,12},{4,3},{5,7},{6,11},{7,15},{8,1},{9,5},{10... | collective-permute-start | bytes 2359304 | tf_op jit(solution)/shard_map/ppermute | solution.py:703
  23.0 109.9 %collective-permute-start.9 = (s32[20,128]{1,0:T(8,128)S(1)}, s32[20,128]{1,0:T(8,128)}, u32[]{:S(2)}, u32[]{:S(2)}) collective-permute-start(s32[20,128]{1,0:T(8,128)S(1)} %add_bitcast_fusion), channel_id=1, source_target_pairs={{0,0},{1,4},{2,8},{3,12},{4,3},{5,7},{6,11},{7,15},{8,1},{9,5},{10... | collective-permute-start | bytes 30728 | tf_op jit(solution)/shard_map/ppermute | solution.py:703
  26.3 24.5 %collective-permute-start.1 = (bf16[96,768]{0,1:T(8,128)(2,1)S(1)}, bf16[96,768]{0,1:T(8,128)(2,1)S(1)}, u32[]{:S(2)}, u32[]{:S(2)}) collective-permute-start(bf16[96,768]{0,1:T(8,128)(2,1)S(1)} %collective-permute-done), channel_id=1, source_target_pairs={{0,1},{1,0},{2,3},{3,2},{4,5},{5,4},{6,7},{7,6},{8,9},{9,8},{10,11... | collective-permute-start | bytes 442376 | tf_op jit(solution)/shard_map/ppermute | solution.py:656
  51.2 23.6 %collective-permute-start.2 = (bf16[192,768]{0,1:T(8,128)(2,1)S(1)}, bf16[192,768]{0,1:T(8,128)(2,1)S(1)}, u32[]{:S(2)}, u32[]{:S(2)}) collective-permute-start(bf16[192,768]{0,1:T(8,128)(2,1)S(1)} %maximum_select_fusion.2), channel_id=1, source_target_pairs={{0,2},{1,3},{2,0},{3,1},{4,6},{5,7},{6,4},{7,5},{8,10},{9,11},{10,... | collective-permute-start | bytes 884744 | tf_op jit(solution)/shard_map/ppermute | solution.py:656
  76.0 62.4 %collective-permute-start.3 = (bf16[384,768]{0,1:T(8,128)(2,1)S(1)}, bf16[384,768]{0,1:T(8,128)(2,1)S(1)}, u32[]{:S(2)}, u32[]{:S(2)}) collective-permute-start(bf16[384,768]{0,1:T(8,128)(2,1)S(1)} %pad_maximum_fusion.1), channel_id=1, source_target_pairs={{0,16},{16,0},{1,17},{17,1},{2,18},{18,2},{3,19},{19,3},{4,20},{20... | collective-permute-start | bytes 1769480 | tf_op jit(solution)/shard_map/ppermute | solution.py:656
  78.9 22.8 %collective-permute-start.5 = (f32[1,1]{1,0:T(1,128)}, f32[1,1]{1,0:T(1,128)}, u32[]{:S(2)}, u32[]{:S(2)}) collective-permute-start(f32[1,1]{1,0:T(1,128)} %add.124), channel_id=1, source_target_pairs={{0,8},{4,12},{8,0},{12,4},{1,9},{5,13},{9,1},{13,5},{2,10},{6,14},... | collective-permute-start | bytes 20 | tf_op jit(solution)/shard_map/ppermute | solution.py:656
  102.3 2.9 collective-permute-start.6
  105.8 2.9 collective-permute-start.7
  109.3 3.5 collective-permute-start.8
  113.4 52.3 %collective-permute-start.11 = (bf16[512,768]{1,0:T(8,128)(2,1)}, bf16[512,768]{1,0:T(8,128)(2,1)}, u32[]{:S(2)}, u32[]{:S(2)}) collective-permute-start(bf16[512,768]{1,0:T(8,128)(2,1)} %collective-permute-done.10.in_ref), channel_id=1, source_target_pairs={{0,8},{4,12},{8,0},{12,4},{1,9},{5,13},{9,1},{13,5},{2,10},{6,14},... | collective-permute-start | bytes 2359304 | tf_op jit(solution)/shard_map/ppermute | solution.py:656
  135.9 38.3 %collective-permute-start.12 = (bf16[512,768]{1,0:T(8,128)(2,1)}, bf16[512,768]{1,0:T(8,128)(2,1)S(1)}, u32[]{:S(2)}, u32[]{:S(2)}) collective-permute-start(bf16[512,768]{1,0:T(8,128)(2,1)} %collective-permute-done.10.in_ref), channel_id=1, source_target_pairs={{0,4},{4,0},{8,12},{12,8},{1,5},{5,1},{9,13},{13,9},{2,6},{6,2},{1... | collective-permute-start | bytes 2359304 | tf_op jit(solution)/shard_map/ppermute | solution.py:656
  139.3 91.2 %collective-permute-start.14 = (bf16[256,768]{1,0:T(8,128)(2,1)S(1)}, bf16[256,768]{1,0:T(8,128)(2,1)S(1)}, u32[]{:S(2)}, u32[]{:S(2)}) collective-permute-start(bf16[256,768]{1,0:T(8,128)(2,1)S(1)} %get-tuple-element.84), channel_id=1, source_target_pairs={{0,0},{1,4},{2,8},{3,12},{4,3},{5,7},{6,11},{7,15},{8,1},{9,5},{10... | collective-permute-start | bytes 1179656 | tf_op jit(solution)/shard_map/ppermute | solution.py:703
  141.2 89.3 %collective-permute-start.15 = (bf16[256,768]{1,0:T(8,128)(2,1)}, bf16[256,768]{1,0:T(8,128)(2,1)}, u32[]{:S(2)}, u32[]{:S(2)}) collective-permute-start(bf16[256,768]{1,0:T(8,128)(2,1)} %get-tuple-element.85), channel_id=1, source_target_pairs={{0,0},{1,4},{2,8},{3,12},{4,3},{5,7},{6,11},{7,15},{8,1},{9,5},{10... | collective-permute-start | bytes 1179656 | tf_op jit(solution)/shard_map/ppermute | solution.py:703
  165.7 10.3 %collective-permute-start.13 = (bf16[512,768]{1,0:T(8,128)(2,1)}, bf16[512,768]{1,0:T(8,128)(2,1)S(1)}, u32[]{:S(2)}, u32[]{:S(2)}) collective-permute-start(bf16[512,768]{1,0:T(8,128)(2,1)} %collective-permute-done.11), channel_id=1, source_target_pairs={{0,4},{4,0},{8,12},{12,8},{1,5},{5,1},{9,13},{13,9},{2,6},{6,2},{1... | collective-permute-start | bytes 2359304 | tf_op jit(solution)/shard_map/ppermute | solution.py:656
  194.9 31.9 %all-to-all-start = ((bf16[4,384,128]{2,1,0:T(8,128)(2,1)}), bf16[4,384,128]{2,1,0:T(8,128)(2,1)S(1)}, u32[]{:S(2)}, u32[]{:S(2)}) async-start(bf16[4,384,128]{2,1,0:T(8,128)(2,1)} %get-tuple-element.83.refs_6_), calls=%async_computation | async-start | bytes 786432 | tf_op jit(solution)/shard_map/all_to_all | solution.py:775
  200.0 52.0 %collective-permute-start.16 = (bf16[256,768]{1,0:T(8,128)(2,1)S(1)}, bf16[256,768]{1,0:T(8,128)(2,1)}, u32[]{:S(2)}, u32[]{:S(2)}) collective-permute-start(bf16[256,768]{1,0:T(8,128)(2,1)S(1)} %get-tuple-element.88), channel_id=1, source_target_pairs={{0,0},{1,4},{2,8},{3,12},{4,3},{5,7},{6,11},{7,15},{8,1},{9,5},{10... | collective-permute-start | bytes 1179656 | tf_op jit(solution)/shard_map/ppermute | solution.py:703
  205.2 46.7 %collective-permute-start.17 = (bf16[256,768]{1,0:T(8,128)(2,1)}, bf16[256,768]{1,0:T(8,128)(2,1)}, u32[]{:S(2)}, u32[]{:S(2)}) collective-permute-start(bf16[256,768]{1,0:T(8,128)(2,1)} %get-tuple-element.89), channel_id=1, source_target_pairs={{0,0},{1,4},{2,8},{3,12},{4,3},{5,7},{6,11},{7,15},{8,1},{9,5},{10... | collective-permute-start | bytes 1179656 | tf_op jit(solution)/shard_map/ppermute | solution.py:703
  226.9 21.5 %all-to-all-start.1 = ((bf16[4,384,128]{2,1,0:T(8,128)(2,1)}), bf16[4,384,128]{2,1,0:T(8,128)(2,1)S(1)}, u32[]{:S(2)}, u32[]{:S(2)}) async-start(bf16[4,384,128]{2,1,0:T(8,128)(2,1)} %get-tuple-element.87.refs_6_), calls=%async_computation.1 | async-start | bytes 786432 | tf_op jit(solution)/shard_map/all_to_all | solution.py:775
  248.4 20.3 %all-to-all-start.2 = ((bf16[4,384,128]{2,1,0:T(8,128)(2,1)}), bf16[4,384,128]{2,1,0:T(8,128)(2,1)S(1)}, u32[]{:S(2)}, u32[]{:S(2)}) async-start(bf16[4,384,128]{2,1,0:T(8,128)(2,1)} %get-tuple-element.91), calls=%async_computation.2 | async-start | bytes 786432 | tf_op jit(solution)/shard_map/all_to_all | solution.py:775
  251.9 136.5 %reduce-scatter.3.cloned.1.call-start = ((), (), s32[]{:S(2)}) async-start(), calls=%async_computation.6 | async-start | bytes 12386304 | tf_op jit(solution)/shard_map/reduce_scatter | solution.py:805
  282.7 37.9 %collective-permute-start.18 = (bf16[512,768]{1,0:T(8,128)(2,1)S(1)}, bf16[512,768]{1,0:T(8,128)(2,1)S(1)}, u32[]{:S(2)}, u32[]{:S(2)}) collective-permute-start(bf16[512,768]{1,0:T(8,128)(2,1)S(1)} %pad_maximum_fusion), channel_id=1, source_target_pairs={{0,0},{4,1},{8,2},{12,3},{3,4},{7,5},{11,6},{15,7},{1,8},{5,9},{9,... | collective-permute-start | bytes 2359304 | tf_op jit(solution)/shard_map/ppermute | solution.py:707
  289.0 31.5 %all-to-all-start.3 = ((bf16[4,384,128]{2,1,0:T(8,128)(2,1)}), bf16[4,384,128]{2,1,0:T(8,128)(2,1)S(1)}, u32[]{:S(2)}, u32[]{:S(2)}) async-start(bf16[4,384,128]{2,1,0:T(8,128)(2,1)} %get-tuple-element.106), calls=%async_computation.3 | async-start | bytes 786432 | tf_op jit(solution)/shard_map/all_to_all | solution.py:775
  292.5 185.5 %reduce-scatter.5.cloned.1.call-start = ((), (), s32[]{:S(2)}) async-start(), calls=%async_computation.7 | async-start | bytes 1720320 | tf_op jit(solution)/shard_map/reduce_scatter | solution.py:806
  320.5 31.5 %copy-start.7 = (bf16[512,768]{1,0:T(8,128)(2,1)}, bf16[512,768]{1,0:T(8,128)(2,1)S(1)}, u32[]{:S(2)}) copy-start(bf16[512,768]{1,0:T(8,128)(2,1)S(1)} %collective-permute-done.18) | copy-start | bytes 2359300
  355.6 3.5 collective-permute-start.19
  360.3 23.0 %collective-permute-start.20 = (bf16[512,768]{1,0:T(8,128)(2,1)}, bf16[512,768]{1,0:T(8,128)(2,1)}, u32[]{:S(2)}, u32[]{:S(2)}) collective-permute-start(bf16[512,768]{1,0:T(8,128)(2,1)} %slice.237), channel_id=1, source_target_pairs={{0,8},{4,12},{8,0},{12,4},{1,9},{5,13},{9,1},{13,5},{2,10},{6,14},... | collective-permute-start | bytes 2359304 | tf_op jit(solution)/shard_map/ppermute | solution.py:656
  360.3 25.3 %copy-start.15 = (f32[8,768]{1,0:T(8,128)S(1)}, f32[8,768]{1,0:T(8,128)}, u32[]{:S(2)}) copy-start(f32[8,768]{1,0:T(8,128)} %get-tuple-element.120) | copy-start | bytes 73732
  360.3 25.3 %copy-start.16 = (f32[8,768]{1,0:T(8,128)S(1)}, f32[8,768]{1,0:T(8,128)}, u32[]{:S(2)}) copy-start(f32[8,768]{1,0:T(8,128)} %get-tuple-element.121) | copy-start | bytes 73732
  360.3 25.3 %copy-start.17 = (f32[4,1,768]{2,1,0:T(1,128)S(1)}, f32[4,1,768]{2,1,0:T(1,128)}, u32[]{:S(2)}) copy-start(f32[4,1,768]{2,1,0:T(1,128)} %get-tuple-element.122) | copy-start | bytes 36868
  360.3 25.3 %copy-start.18 = (f32[4,1,768]{2,1,0:T(1,128)S(1)}, f32[4,1,768]{2,1,0:T(1,128)}, u32[]{:S(2)}) copy-start(f32[4,1,768]{2,1,0:T(1,128)} %get-tuple-element.123) | copy-start | bytes 36868
  366.0 17.3 %copy-start.2 = (bf16[768,768]{1,0:T(8,128)(2,1)}, bf16[768,768]{1,0:T(8,128)(2,1)S(1)}, u32[]{:S(2)}) copy-start(bf16[768,768]{1,0:T(8,128)(2,1)S(1)} %fusion.10) | copy-start | bytes 3538948
  384.1 14.6 %collective-permute-start.21 = (bf16[4,96,768]{2,1,0:T(8,128)(2,1)}, bf16[4,96,768]{2,1,0:T(8,128)(2,1)}, u32[]{:S(2)}, u32[]{:S(2)}) collective-permute-start(bf16[4,96,768]{2,1,0:T(8,128)(2,1)} %constant_dynamic-slice_fusion.2), channel_id=1, source_target_pairs={{0,16},{16,0},{1,17},{17,1},{2,18},{18,2},{3,19},{19,3},{4,20},{20... | collective-permute-start | bytes 1769480 | tf_op jit(solution)/shard_map/ppermute | solution.py:656
  400.0 24.2 %copy-start.4 = (bf16[512,768]{1,0:T(8,128)(2,1)S(1)}, bf16[512,768]{1,0:T(8,128)(2,1)}, u32[]{:S(2)}) copy-start(bf16[512,768]{1,0:T(8,128)(2,1)} %fusion.9) | copy-start | bytes 2359300
  400.7 2.4 collective-permute-start.22
  403.1 3.8 collective-permute-start.23
  404.7 29.9 %collective-permute-start.28 = (bf16[2,96,768]{2,1,0:T(8,128)(2,1)S(1)}, bf16[2,96,768]{2,1,0:T(8,128)(2,1)S(1)}, u32[]{:S(2)}, u32[]{:S(2)}) collective-permute-start(bf16[2,96,768]{2,1,0:T(8,128)(2,1)S(1)} %constant_dynamic-slice_fusion.1), channel_id=1, source_target_pairs={{0,2},{1,3},{2,0},{3,1},{4,6},{5,7},{6,4},{7,5},{8,10},{9,11},{10,... | collective-permute-start | bytes 884744 | tf_op jit(solution)/shard_map/ppermute | solution.py:656
  406.9 3.4 collective-permute-start.24
  410.3 11.5 %collective-permute-start.25 = (f32[84,128]{1,0:T(8,128)S(1)}, f32[84,128]{1,0:T(8,128)S(1)}, u32[]{:S(2)}, u32[]{:S(2)}) collective-permute-start(f32[84,128]{1,0:T(8,128)S(1)} %add.146), channel_id=1, source_target_pairs={{0,1},{1,0},{2,3},{3,2},{4,5},{5,4},{6,7},{7,6},{8,9},{9,8},{10,11... | collective-permute-start | bytes 129032 | tf_op jit(solution)/shard_map/ppermute | solution.py:656
  421.9 12.7 %collective-permute-start.26 = (f32[84,128]{1,0:T(8,128)S(1)}, f32[84,128]{1,0:T(8,128)S(1)}, u32[]{:S(2)}, u32[]{:S(2)}) collective-permute-start(f32[84,128]{1,0:T(8,128)S(1)} %add.147), channel_id=1, source_target_pairs={{0,2},{1,3},{2,0},{3,1},{4,6},{5,7},{6,4},{7,5},{8,10},{9,11},{10,... | collective-permute-start | bytes 129032 | tf_op jit(solution)/shard_map/ppermute | solution.py:656
  424.2 52.6 %collective-permute-start.27 = (bf16[512,768]{1,0:T(8,128)(2,1)S(1)}, bf16[512,768]{1,0:T(8,128)(2,1)S(1)}, u32[]{:S(2)}, u32[]{:S(2)}) collective-permute-start(bf16[512,768]{1,0:T(8,128)(2,1)S(1)} %copy-done.4), channel_id=1, source_target_pairs={{0,0},{4,1},{8,2},{12,3},{3,4},{7,5},{11,6},{15,7},{1,8},{5,9},{9,... | collective-permute-start | bytes 2359304 | tf_op jit(solution)/shard_map/ppermute | solution.py:707
  434.7 19.2 %collective-permute-start.29 = (bf16[1,96,768]{2,1,0:T(8,128)(2,1)S(1)}, bf16[1,96,768]{2,1,0:T(8,128)(2,1)S(1)}, u32[]{:S(2)}, u32[]{:S(2)}) collective-permute-start(bf16[1,96,768]{2,1,0:T(8,128)(2,1)S(1)} %constant_dynamic-slice_fusion), channel_id=1, source_target_pairs={{0,1},{1,0},{2,3},{3,2},{4,5},{5,4},{6,7},{7,6},{8,9},{9,8},{10,11... | collective-permute-start | bytes 442376 | tf_op jit(solution)/shard_map/ppermute | solution.py:656
  451.9 28.0 %copy-start.8 = (bf16[512,768]{1,0:T(8,128)(2,1)S(1)}, bf16[512,768]{1,0:T(8,128)(2,1)}, u32[]{:S(2)}) copy-start(bf16[512,768]{1,0:T(8,128)(2,1)} %copy-done.7) | copy-start | bytes 2359300
  454.0 20.4 %collective-permute-start.30 = (bf16[96,768]{1,0:T(8,128)(2,1)S(1)}, bf16[96,768]{1,0:T(8,128)(2,1)S(1)}, u32[]{:S(2)}, u32[]{:S(2)}) collective-permute-start(bf16[96,768]{1,0:T(8,128)(2,1)S(1)} %fusion.17), channel_id=1, source_target_pairs={{0,0},{4,1},{8,2},{12,3},{3,4},{7,5},{11,6},{15,7},{1,8},{5,9},{9,... | collective-permute-start | bytes 442376 | tf_op jit(solution)/shard_map/ppermute | solution.py:707
  (22 other events, 89.5 us)
Sparse Core Ops, SparseCore 0:
  11.0 118.3 all-gather.2
  281.6 89.3 reduce-scatter.2
  388.5 39.5 reduce-scatter.4

commit v6 on v5

--- a/solution.py
+++ b/solution.py
@@ -401,7 +401,7 @@
     attention = jnp.zeros(in_ref.shape, F32)
     for slot in range(parts):
         arrive(0, slot)
-        attention = attention + dot(unpack(ctx_ref[place_ref[slot]]), w_out[slot], NT)
+        attention = attention + dot(unpack(ctx_ref[place_ref[slot]]), w_out[slot, :, : 3 * DH], NT)
     first_exact, normed_one, inverse_one = norm_forward(
         in_ref[...].astype(F32) + attention + vec(0), vec(1), vec(2)
     )
@@ -451,7 +451,7 @@
     sums_ref[7:8, :] = jnp.zeros_like(sums_ref[7:8, :])
     middle = BLOCK // 2
     for slot in range(parts):
-        back = dot(attn_grad, w_out[slot]).astype(BF16)
+        back = dot(attn_grad, w_out[slot, :, : 3 * DH]).astype(BF16)
         ctx_grad_ref[place_ref[slot]] = pack(
             back[:, : 2 * DH], back[:middle, 2 * DH :], back[middle:, 2 * DH :]
         )
@@ -461,7 +461,7 @@
     parts = ctx.shape[0]
     width = rows_in.shape[1]
     hidden_cols = inner_bias.shape[2]
-    head_cols = pieces[0].shape[2] - 2 * hidden_cols
+    out_cols = pieces[0].shape[2] - 2 * hidden_cols
 
     def mine(columns):
         return pl.BlockSpec((BLOCK, columns), lambda i: (half, 0))
@@ -501,7 +501,7 @@
         + [pl.BlockSpec(memory_space=pl.ANY)] * len(pieces),
         out_specs=tuple(fixed(out.shape) for out in out_shape),
         scratch_shapes=[
-            pltpu.VMEM((parts, width, head_cols), BF16),
+            pltpu.VMEM((parts, width, out_cols), BF16),
             pltpu.VMEM((parts, width, hidden_cols), BF16),
             pltpu.VMEM((parts, width, hidden_cols), BF16),
             pltpu.VMEM((parts, BLOCK, hidden_cols), F32),
@@ -511,7 +511,7 @@
             dimension_semantics=("arbitrary",), vmem_limit_bytes=VMEM_LIMIT
         ),
         cost_estimate=pl.CostEstimate(
-            flops=BLOCK * width * (8 * hidden_cols + 4 * head_cols) * parts,
+            flops=BLOCK * width * (8 * hidden_cols + 4 * out_cols) * parts,
             bytes_accessed=18 << 20,
             transcendentals=2 * BLOCK * hidden_cols * parts,
         ),
@@ -523,7 +523,7 @@
     firsts, branch_grads, attn_grads, acts, hidden_grads, ctxs = (
         refs[k * halves : (k + 1) * halves] for k in range(6)
     )
-    outs = refs[6 * halves : -3]
+    notes_ref, outs = refs[6 * halves], refs[6 * halves + 1 : -3]
     turned, whole, sems = refs[-3:]
     step = pl.program_id(0)
     slots = whole.shape[0]
@@ -543,7 +543,9 @@
     whole[step, :, :hidden_cols] = dot(turned[0], both(hidden_grads)).astype(BF16)
     whole[step, :, hidden_cols : 2 * hidden_cols] = dot(turned[1], both(acts)).astype(BF16)
     ctx = jnp.concatenate([unpack(source[0]) for source in ctxs], axis=0)
-    whole[step, :, 2 * hidden_cols :] = dot(turned[2], ctx).astype(BF16)
+    plain = 2 * hidden_cols + ctx.shape[1]
+    whole[step, :, 2 * hidden_cols : plain] = dot(turned[2], ctx).astype(BF16)
+    whole[step, :, plain : plain + notes_ref.shape[1]] = notes_ref[...]
     for team in range(teams):
 
         @pl.when(step // each == team)
@@ -564,11 +566,11 @@
             pltpu.make_async_copy(whole.at[slot], whole.at[slot], sems.at[slot]).wait()
 
 
-def run_weights(turns, teams, block, place, firsts, branch_grads, attn_grads, acts, hidden_grads, ctxs):
+def run_weights(turns, teams, block, place, notes, firsts, branch_grads, attn_grads, acts, hidden_grads, ctxs):
     parts, _, hidden_cols = acts[0].shape
     halves = len(acts)
     width = firsts[0].shape[1]
-    columns = 2 * hidden_cols + 3 * DH
+    columns = 2 * hidden_cols + 3 * DH + notes.shape[1]
 
     def by_slot(rows, size):
         return pl.BlockSpec((1, rows, size), lambda s, place: (place[s], 0, 0))
@@ -585,7 +587,8 @@
             grid=(parts,),
             in_specs=[fixed] * (3 * halves)
             + [by_slot(BLOCK, hidden_cols)] * (2 * halves)
-            + [by_slot(PACKED, 2 * DH)] * halves,
+            + [by_slot(PACKED, 2 * DH)] * halves
+            + [pl.BlockSpec(notes.shape, lambda s, place: (0, 0))],
             out_specs=tuple(pl.BlockSpec(memory_space=pl.ANY) for _ in outs),
             scratch_shapes=[
                 pltpu.VMEM((3, width, halves * BLOCK), BF16),
@@ -602,15 +605,17 @@
             transcendentals=0,
         ),
         name="dense_weights",
-    )(place, *firsts, *branch_grads, *attn_grads, *acts, *hidden_grads, *ctxs)
-
-
-def finish_dense(packed_ref, inner_ref, outer_ref, output_ref):
+    )(place, *firsts, *branch_grads, *attn_grads, *acts, *hidden_grads, *ctxs, notes)
+
+
+def finish_dense(packed_ref, inner_ref, outer_ref, output_ref, notes_ref):
     hidden_cols = inner_ref.shape[1]
     summed = packed_ref[...].astype(F32)
     inner_ref[...] = summed[:, :hidden_cols]
     outer_ref[...] = summed[:, hidden_cols : 2 * hidden_cols]
-    output_ref[...] = jnp.transpose(summed[:, 2 * hidden_cols :])
+    plain = 2 * hidden_cols + output_ref.shape[0]
+    output_ref[...] = jnp.transpose(summed[:, 2 * hidden_cols : plain])
+    notes_ref[...] = summed[:, plain:]
 
 
 def run_finish_dense(packed, hidden_cols, head_cols):
@@ -621,6 +626,7 @@
             jax.ShapeDtypeStruct((rows, hidden_cols), F32),
             jax.ShapeDtypeStruct((rows, hidden_cols), F32),
             jax.ShapeDtypeStruct((head_cols, rows), F32),
+            jax.ShapeDtypeStruct((rows, packed.shape[1] - 2 * hidden_cols - head_cols), F32),
         ),
         name="finish_dense",
     )(packed)
@@ -629,26 +635,22 @@
 def finish_heads(value_ref, *refs):
     summed = value_ref[...].astype(F32)
     heads = summed.shape[1] // SLAB
-    for ref, which in zip(refs, (0, 2, 3)):
-        ref[...] = jnp.concatenate(
-            [summed[:, SLAB * h + which * DH : SLAB * h + (which + 1) * DH] for h in range(heads)], axis=1
-        )
+    for ref, which in zip(refs, (0, 2, 3, 1)):
+        columns = [summed[:, SLAB * h + which * DH : SLAB * h + (which + 1) * DH] for h in range(heads)]
+        ref[...] = jnp.concatenate(columns, axis=1)[: ref.shape[0]]
 
 
 def run_finish_heads(value):
     rows, width = value.shape
     out = jax.ShapeDtypeStruct((rows, width // 4), F32)
-    return pl.pallas_call(finish_heads, out_shape=(out, out, out), name="finish_heads")(value)
+    notes = jax.ShapeDtypeStruct((8, width // 4), F32)
+    return pl.pallas_call(finish_heads, out_shape=(out, out, out, notes), name="finish_heads")(value)
 
 
 def interleave(query, key, value, heads):
     rows = query.shape[0]
     parts = [part.reshape(rows, heads, 1, DH) for part in (query, jnp.zeros_like(query), key, value)]
     return jnp.concatenate(parts, axis=2).reshape(rows, heads * SLAB)
-
-
-def place_slice(local_grad, full_size, offset):
-    return lax.dynamic_update_slice_in_dim(jnp.zeros((full_size,), F32), local_grad, offset, 0)
 
 
 def swap(value, axis, bit):
@@ -661,13 +663,6 @@
     while bit < lax.axis_size(axis):
         yield bit
         bit *= 2
-
-
-def sum_everywhere(value):
-    for axis in ("lo", "hi", "tensor"):
-        for bit in bits_of(axis):
-            value = value + swap(value, axis, bit)
-    return value
 
 
 def after(value, *others):
@@ -726,29 +721,33 @@
     halves = part_len // BLOCK
 
     rows_in = send_away(inputs.reshape(part_len, width))
+    head_rows = send_away(interleave(w_query, w_key, w_value, heads))
     whole_row = jnp.concatenate((segment_ids.reshape(seq_len), valid_mask.reshape(part_len)))
     whole_row = send_away(whole_row.reshape(-1, 128)).reshape(-1)
-    head_rows = send_away(interleave(w_query, w_key, w_value, heads))
-    mine = jnp.concatenate((w_inner, w_outer.T, w_output.T), axis=1)
+    valid_count = jnp.sum(valid_mask.astype(F32))
+    upper = jnp.floor(valid_count / 256.0)
+    count_row = jnp.zeros((shard_rows, DH), BF16)
+    count_row = count_row.at[0, 0].set(upper.astype(BF16)).at[0, 1].set((valid_count - 256.0 * upper).astype(BF16))
+    mine = jnp.concatenate((w_inner, w_outer.T, w_output.T, count_row), axis=1)
     weights = lax.all_gather(mine, ("tensor", "hi", "lo"), axis=0, tiled=False)
-    pieces = [weights.reshape(parts, width, 2 * hidden_cols + head_cols)]
+    counts = weights[:, 0, -DH : 2 - DH].astype(F32)
+    counted = 256.0 * jnp.sum(counts[:, 0]) + jnp.sum(counts[:, 1])
+    ratio = (total_tokens / counted).reshape(1)
+    pieces = [weights.reshape(parts, width, -1)]
     marks = [[(t, 0) for t in range(parts)]]
     place = jnp.asarray(list(range(parts)) + [0], jnp.int32)
-    valid_count = jnp.sum(valid_mask.astype(F32)).reshape(1, 1)
-    counted = sum_everywhere(valid_count)
-    ratio = (total_tokens / counted).reshape(1)
 
     head_rows = merge(head_rows, swap(head_rows, "tensor", 1), "tensor", 1)
+    head_rows = after(head_rows, rows_in)
     near_chunk = swap(rows_in, "lo", 1)
     next_chunk = swap(rows_in, "lo", 2)
     head_rows = merge(head_rows, swap(head_rows, "tensor", 2), "tensor", 2)
+    head_rows = after(head_rows, next_chunk)
+    far_chunk = swap(next_chunk, "lo", 1)
     blocks = head_rows.reshape(4, shard_rows, -1)
-    head_rows = jnp.concatenate([blocks[plane] for plane in PLANE], axis=0)
-    w_heads = head_rows
+    w_heads = jnp.concatenate([blocks[plane] for plane in PLANE], axis=0)
     for bit in bits_of("hi"):
         w_heads = merge(w_heads, swap(w_heads, "hi", bit), "hi", bit)
-    far_chunk = swap(next_chunk, "lo", 1)
-    w_heads, ratio = lax.optimization_barrier((w_heads, ratio))
     tokens = [rows_in, next_chunk, near_chunk, far_chunk]
 
     mine_cols = lane_index * head_cols
@@ -801,9 +800,11 @@
     inner_sums = sum(inner_sums)
     sources = (firsts, branch_grads, attn_grads, acts, hidden_grads, arrived)
     head_grads[:-1], sources = lax.optimization_barrier((head_grads[:-1], sources))
-    (packed,) = run_weights(([[0]],), 1, width, place, *sources)
+    notes = jnp.concatenate((dense_sums.reshape(-1), inner_sums.reshape(-1))).astype(BF16)
+    room = -(-notes.shape[0] // (shard_rows * 128)) * 128
+    notes = jnp.pad(notes, (0, shard_rows * room - notes.shape[0])).reshape(shard_rows, room)
+    (packed,) = run_weights(([[0]],), 1, width, place, jnp.tile(notes, (copies, 1)), *sources)
     packed = lax.psum_scatter(packed, ("hi", "lo"), scatter_dimension=1, tiled=True)
-    packed = lax.psum_scatter(packed, "tensor", scatter_dimension=0, tiled=True)[0]
     layer_out = send_back(jnp.concatenate(layers, axis=0))
 
     earlier, before = [], []
@@ -820,52 +821,61 @@
     joined_grad = joined_grad.reshape(seq_len, width)
     middle = seq_len // 2
     core_share = swap(dot(joined_grad[middle:], w_heads, NT).astype(BF16), "lo", 1)
+    sums = sums.reshape(heads, 4, DH)
+    sums = jnp.concatenate((sums[:, 0].reshape(1, head_cols), sums[:, 3].reshape(1, head_cols)), axis=1)
+    core_share, sums = lax.optimization_barrier((core_share, sums))
+    sums = merge(sums, swap(sums, "lo", 1), "lo", 1)
     own_share = dot(joined_grad[:middle], w_heads, NT)
-    own_share, sums, joined_grad = lax.optimization_barrier((own_share, sums, joined_grad))
+    own_share, joined_grad = lax.optimization_barrier((own_share, joined_grad))
     input_share = own_share + core_share.astype(F32)
     chip_share = swap(input_share[part_len:].astype(BF16), "lo", 2)
-    head_weights = dot(jnp.concatenate(tokens, axis=0), joined_grad, TN).astype(BF16)
-    chip_share, head_weights = lax.optimization_barrier((chip_share, head_weights))
-    held = head_weights.reshape((copies, shard_rows) + head_weights.shape[1:])
+    sums = merge(sums, swap(sums, "lo", 2), "lo", 2)
+    head_weights = dot(jnp.concatenate(tokens, axis=0), joined_grad, TN)
+    biases = jnp.concatenate((sums[:, :head_cols].reshape(-1), sums[:, head_cols:].reshape(-1)))
+    biases = jnp.pad(
+        biases.reshape(8, heads, 1, DH), ((0, shard_rows - 8), (0, 0), (1, 2), (0, 0))
+    ).reshape(1, shard_rows, -1)
+    head_weights = (head_weights.reshape((copies, shard_rows, -1)) + biases).astype(BF16)
+    chip_share, held = lax.optimization_barrier((chip_share, head_weights))
     for bit in reversed(list(bits_of("hi"))):
         held = add_low(*halve(held, "hi", bit))
     input_grad = input_share[:part_len] + chip_share.astype(F32) + jnp.concatenate(first_grads, axis=0)
-    input_grad, sums, held = lax.optimization_barrier((input_grad.astype(BF16), sums, held))
+    input_grad, held = lax.optimization_barrier((input_grad.astype(BF16), held))
+    packed = after(packed, input_grad)
+    packed = lax.psum_scatter(packed, "tensor", scatter_dimension=0, tiled=True)[0]
     input_grad = send_back(input_grad).astype(F32)
-
     held = jnp.stack([held[origin] for origin in ORIGIN])
     held = add_low(*halve(held, "tensor", 2))
     held = add_low(*halve(held, "tensor", 1))
-    head_final = send_back(held[0])
-
-    inner_grad, outer_grad, output_grad = run_finish_dense(packed, hidden_cols, head_cols)
-
-    sums = sums.reshape(heads, 4, DH)
-    totals = sum_everywhere(
-        jnp.concatenate(
-            (
-                place_slice(sums[:, 0].reshape(head_cols), width, mine_cols),
-                place_slice(sums[:, 3].reshape(head_cols), width, mine_cols),
-                dense_sums.reshape(-1),
-                inner_sums.reshape(-1),
-            )
-        ).reshape(-1, 128)
-    ).reshape(-1)
+    query_grad, key_grad, value_grad, biases = run_finish_heads(send_back(held[0]))
+    biases = biases.reshape(2, width)
+
+    inner_grad, outer_grad, output_grad, notes = run_finish_dense(packed, hidden_cols, head_cols)
+    notes = notes.reshape(-1)
 
     def total(which):
-        return totals[which * width : (which + 1) * width]
-
-    mse_loss = jnp.sum(total(2)) / (counted[0, 0] * width)
+        return notes[which * width : (which + 1) * width]
+
+    mse_loss = jnp.sum(total(0)) / (counted * width)
     return (
-        (
-            layer_out.reshape(1, part_len, width),
-            mse_loss,
-            input_grad.reshape(1, part_len, width),
-        )
-        + tuple(run_finish_heads(head_final))
-        + (output_grad, inner_grad, outer_grad.T)
-        + (total(0), total(1), total(6), totals[10 * width :])
-        + (total(3), total(7), total(8), total(4), total(5))
+        layer_out.reshape(1, part_len, width),
+        mse_loss,
+        input_grad.reshape(1, part_len, width),
+        query_grad,
+        key_grad,
+        value_grad,
+        output_grad,
+        inner_grad,
+        outer_grad.T,
+        biases[0],
+        biases[1],
+        total(4),
+        notes[8 * width : 8 * width + hidden_cols * parts],
+        total(1),
+        total(5),
+        total(6),
+        total(2),
+        total(3),
     )
 
 

time: 490 us -> 490 us (level)
  waiting for transfers between devices: 141 us -> 120 us
  local copies, waits for them, and re-layouts: 18.1 us -> 31.1 us
    ppermute x21 -> x13, waiting for transfers between devices: 122 us -> 69.2 us  [swap(): return lax.ppermute(value, axis, [(i, i ^ bit) for i in range(size)])]
    ppermute x7, waiting for transfers between devices: 0.02 us -> 19 us  [send_away(): return lax.ppermute(value, ('lo', 'tensor'), AWAY)]
    ppermute x21 -> x13, starting transfers between devices: 76.7 us -> 59.4 us  [swap(): return lax.ppermute(value, axis, [(i, i ^ bit) for i in range(size)])]
    ppermute x7, starting transfers between devices: 27.1 us -> 44.4 us  [send_away(): return lax.ppermute(value, ('lo', 'tensor'), AWAY)]
    ppermute x3, waiting for transfers between devices: 18.3 us -> 28.6 us  [send_back(): return lax.ppermute(value, ('lo', 'tensor'), BACK)]
    unnamed x69 -> x79, local copies, waits for them, and re-layouts: 7.91 us -> 11.6 us
  transfers between devices with their start and end apart: 38 -> 30, of which waited for: 17 -> 11; matrix products, arithmetic and copies ran while one was open for 9% -> 11% of each run, Pallas kernels for 26% -> 26%
where the time goes in v6:
time: 490 us; the launch traced here: 487 us
  Pallas kernels  142 us (29%)
  starting transfers between devices  135 us (28%)
  waiting for transfers between devices  120 us (24%)
  local copies, waits for them, and re-layouts  31.1 us (6%)
  other arithmetic  19.9 us (4%)
  matrix products  19.9 us (4%)
  between operations  19 us (4%)
    ppermute x13, waiting for transfers between devices, swap(): return lax.ppermute(value, axis, [(i, i ^ bit) for i in range(size)])  69.2 us
    ppermute x13, starting transfers between devices, swap(): return lax.ppermute(value, axis, [(i, i ^ bit) for i in range(size)])  59.4 us
    pallas_call x2, Pallas kernels, run_backward(): pl.pallas_call(functools.partial(attend_backward, which), out_shape=out_s...  55.3 us
    ppermute x7, starting transfers between devices, send_away(): return lax.ppermute(value, ('lo', 'tensor'), AWAY)  44.4 us
    pallas_call x2, Pallas kernels, run_forward(): pl.pallas_call(functools.partial(attend_forward, which), out_shape=(jax.S...  36.8 us
    pallas_call x2, Pallas kernels, run_dense(): pl.pallas_call(functools.partial(dense_chain, marks), out_shape=out_shape...  33.8 us
    ppermute x3, waiting for transfers between devices, send_back(): return lax.ppermute(value, ('lo', 'tensor'), BACK)  28.6 us
    dot_general x7, matrix products, dot(): lax.dot_general(left_side, right_side, dims, preferred_element_type=F32)  19.9 us
  transfers between devices with their start and end apart: 30, of which 11 were waited for; matrix products, arithmetic and copies ran while one was open for 11% of the time, Pallas kernels for 26%

profile of v6, /device:TPU:3, one launch (start us, length us, event | category | flops | bytes accessed | tf_op | source)
XLA Modules:
  0.0 486.7 jit_solution(4281708755142450662)
XLA Ops:
  14.7 4.8 collective-permute-start.3
  22.5 3.3 collective-permute-start.1
  25.8 3.5 collective-permute-start
  29.3 19.0 %collective-permute-done.1 = bf16[96,768]{0,1:T(8,128)(2,1)S(1)} collective-permute-done((bf16[96,768]{0,1:T(8,128)(2,1)S(1)}, bf16[96,768]{0,1:T(8,128)(2,1)S(1)}, u32[]{:S(2)}, u32[]{:S(2)}) %collective-permute-start.1) | collective-permute-done | bytes 147488 | tf_op jit(solution)/shard_map/ppermute | solution.py:698
  48.3 1.9 collective-permute-start.2
  50.3 9.3 %collective-permute-start.5 = (bf16[512,768]{1,0:T(8,128)(2,1)}, bf16[512,768]{1,0:T(8,128)(2,1)}, u32[]{:S(2)}, u32[]{:S(2)}) collective-permute-start(bf16[512,768]{1,0:T(8,128)(2,1)} %collective-permute-done.3.in_ref), channel_id=1, source_target_pairs={{0,8},{4,12},{8,0},{12,4},{1,9},{5,13},{9,1},{13,5},{2,10},{6,14},... | collective-permute-start | bytes 2359304 | tf_op jit(solution)/shard_map/ppermute | solution.py:658
  60.9 10.4 %collective-permute-start.4 = (bf16[192,768]{0,1:T(8,128)(2,1)S(1)}, bf16[192,768]{0,1:T(8,128)(2,1)S(1)}, u32[]{:S(2)}, u32[]{:S(2)}) collective-permute-start(bf16[192,768]{0,1:T(8,128)(2,1)S(1)} %maximum_select_fusion.2), channel_id=1, source_target_pairs={{0,2},{1,3},{2,0},{3,1},{4,6},{5,7},{6,4},{7,5},{8,10},{9,11},{10,... | collective-permute-start | bytes 884744 | tf_op jit(solution)/shard_map/ppermute | solution.py:658
  73.8 18.5 %collective-permute-done.4 = bf16[192,768]{0,1:T(8,128)(2,1)S(1)} collective-permute-done((bf16[192,768]{0,1:T(8,128)(2,1)S(1)}, bf16[192,768]{0,1:T(8,128)(2,1)S(1)}, u32[]{:S(2)}, u32[]{:S(2)}) %collective-permute-start.4) | collective-permute-done | bytes 294944 | tf_op jit(solution)/shard_map/ppermute | solution.py:658
  97.9 3.6 collective-permute-start.7
  101.6 6.0 %collective-permute-done.6 = bf16[384,768]{0,1:T(8,128)(2,1)S(1)} collective-permute-done((bf16[384,768]{0,1:T(8,128)(2,1)S(1)}, bf16[384,768]{0,1:T(8,128)(2,1)S(1)}, u32[]{:S(2)}, u32[]{:S(2)}) %collective-permute-start.6) | collective-permute-done | bytes 589856 | tf_op jit(solution)/shard_map/ppermute | solution.py:658
  108.5 15.4 %collective-permute-start.10 = (bf16[256,768]{1,0:T(8,128)(2,1)S(1)}, bf16[256,768]{1,0:T(8,128)(2,1)}, u32[]{:S(2)}, u32[]{:S(2)}) collective-permute-start(bf16[256,768]{1,0:T(8,128)(2,1)S(1)} %get-tuple-element.112), channel_id=1, source_target_pairs={{0,0},{1,4},{2,8},{3,12},{4,3},{5,7},{6,11},{7,15},{8,1},{9,5},{10... | collective-permute-start | bytes 1179656 | tf_op jit(solution)/shard_map/ppermute | solution.py:698
  123.9 3.3 collective-permute-start.9
  127.2 12.3 %collective-permute-start.11 = (bf16[256,768]{1,0:T(8,128)(2,1)}, bf16[256,768]{1,0:T(8,128)(2,1)S(1)}, u32[]{:S(2)}, u32[]{:S(2)}) collective-permute-start(bf16[256,768]{1,0:T(8,128)(2,1)} %get-tuple-element.115), channel_id=1, source_target_pairs={{0,0},{1,4},{2,8},{3,12},{4,3},{5,7},{6,11},{7,15},{8,1},{9,5},{10... | collective-permute-start | bytes 1179656 | tf_op jit(solution)/shard_map/ppermute | solution.py:698
  139.5 2.8 fusion.11.refs_1_
  142.3 2.9 fusion.10.refs_0_
  145.3 1.9 collective-permute-start.12
  150.6 17.1 %attend_forward.2 = (bf16[4,384,128]{2,1,0:T(8,128)(2,1)}, f32[3,1,1024]{2,1,0:T(1,128)}) custom-call(s32[1]{0:T(128)} %bitcast.10.lane_ref, s32[8]{0:T(128)} %get-tuple-element.206.low_ref, s32[8]{0:T(128)} %get-tuple-element.205.high_ref, bf16[512,768]{1,0:T(8,128)(2,1)} %fusion.10.refs_0_, bf16[512,768]{1,0:T(8,128)(2,1)} %fusion.11.refs_1_, ...), custom_call_target="tpu_custom_call" | custom-call | flops 1610612736 | bytes 5242880 | tf_op jit(solution)/shard_map/attend_forward/pallas_call | solution.py:268
  167.7 19.6 %attend_forward.3 = (bf16[4,384,128]{2,1,0:T(8,128)(2,1)}, f32[3,1,1024]{2,1,0:T(1,128)}) custom-call(s32[1]{0:T(128)} %bitcast.10.lane_ref, s32[8]{0:T(128)} %get-tuple-element.206.low_ref, s32[8]{0:T(128)} %get-tuple-element.205.high_ref, bf16[512,768]{1,0:T(8,128)(2,1)} %fusion.10.refs_0_, bf16[512,768]{1,0:T(8,128)(2,1)} %fusion.11.refs_1_, ...), custom_call_target="tpu_custom_call" | custom-call | flops 1610612736 | bytes 5242880 | tf_op jit(solution)/shard_map/attend_forward/pallas_call | solution.py:268
  187.4 3.9 all-to-all-start
  194.3 2.6 all-to-all-done.ctx_ref.refs_10_
  196.9 5.3 %all-to-all-start.1 = ((bf16[4,384,128]{2,1,0:T(8,128)(2,1)}), bf16[4,384,128]{2,1,0:T(8,128)(2,1)S(1)}, u32[]{:S(2)}, u32[]{:S(2)}) async-start(bf16[4,384,128]{2,1,0:T(8,128)(2,1)} %get-tuple-element.114.refs_6_), calls=%async_computation.1 | async-start | bytes 786432 | tf_op jit(solution)/shard_map/all_to_all | solution.py:774
  202.2 17.0 %dense_chain.2 = (bf16[256,768]{1,0:T(8,128)(2,1)}, f32[256,768]{1,0:T(8,128)}, bf16[4,384,128]{2,1,0:T(8,128)(2,1)}, bf16[256,768]{1,0:T(8,128)(2,1)}, bf16[256...) custom-call(s32[5]{0:T(128)} %constant.146.clone.place_ref, ...), custom_call_target="tpu_custom_call" | custom-call | flops 5637144576 | bytes 18874368 | tf_op jit(solution)/shard_map/dense_chain/pallas_call | solution.py:486
  219.2 3.7 all-to-all-start.2
  224.4 16.8 %dense_chain.3 = (bf16[256,768]{1,0:T(8,128)(2,1)}, f32[256,768]{1,0:T(8,128)}, bf16[4,384,128]{2,1,0:T(8,128)(2,1)}, bf16[256,768]{1,0:T(8,128)(2,1)}, bf16[256...) custom-call(s32[5]{0:T(128)} %constant.146.clone.place_ref, ...), custom_call_target="tpu_custom_call" | custom-call | flops 5637144576 | bytes 18874368 | tf_op jit(solution)/shard_map/dense_chain/pallas_call | solution.py:486
  243.6 12.9 %dense_weights.1 = bf16[4,768,1856]{2,1,0:T(8,128)(2,1)} custom-call(s32[5]{0:T(128)} %constant.146.clone.place_ref, bf16[256,768]{1,0:T(8,128)(2,1)} %get-tuple-element.133.refs_0_, bf16[256,768]{1,0:T(8,128)(2,1)} %get-tuple-element.134.refs_1_, bf16[256,768]{1,0:T(8,128)(2,1)} %get-tuple-element.135.refs_2_, bf16[256,768]{1,0:T(8,128)(2,1)} %get-tuple-element.136.refs_3_, ...), custom_call_target="tpu_custom_call" | custom-call | flops 5838471168 | bytes 20971520 | tf_op jit(solution)/shard_map/dense_weights/pallas_call | solution.py:582
  257.6 1.9 collective-permute-start.13
  259.6 3.5 all-to-all-start.3
  263.3 24.8 %attend_backward.2 = (f32[3,2048,128]{2,1,0:T(8,128)}, bf16[4,256,384]{2,1,0:T(8,128)(2,1)}) custom-call(s32[1]{0:T(128)} %bitcast.10.lane_ref, s32[8]{0:T(128)} %get-tuple-element.206.low_ref, s32[8]{0:T(128)} %get-tuple-element.205.high_ref, bf16[512,768]{1,0:T(8,128)(2,1)} %fusion.10.refs_0_, bf16[512,768]{1,0:T(8,128)(2,1)} %fusion.11.refs_1_, ...), custom_call_target="tpu_custom_call" | custom-call | flops 4026531840 | bytes 10485760 | tf_op jit(solution)/shard_map/attend_backward/pallas_call | solution.py:335
  288.1 8.6 %collective-permute-done.13 = bf16[512,768]{1,0:T(8,128)(2,1)S(1)} collective-permute-done((bf16[512,768]{1,0:T(8,128)(2,1)S(1)}, bf16[512,768]{1,0:T(8,128)(2,1)S(1)}, u32[]{:S(2)}, u32[]{:S(2)}) %collective-permute-start.13) | collective-permute-done | bytes 786464 | tf_op jit(solution)/shard_map/ppermute | solution.py:702
  297.4 30.6 %attend_backward.3 = (bf16[4,512,768]{2,1,0:T(8,128)(2,1)}, f32[1,768]{1,0:T(1,128)}) custom-call(s32[1]{0:T(128)} %bitcast.10.lane_ref, s32[8]{0:T(128)} %get-tuple-element.206.low_ref, s32[8]{0:T(128)} %get-tuple-element.205.high_ref, bf16[512,768]{1,0:T(8,128)(2,1)} %fusion.10.refs_0_, bf16[512,768]{1,0:T(8,128)(2,1)} %fusion.11.refs_1_, ...), custom_call_target="tpu_custom_call" | custom-call | flops 4026531840 | bytes 10485760 | tf_op jit(solution)/shard_map/attend_backward/pallas_call | solution.py:335
  328.0 2.1 fusion.20
  330.2 2.5 convolution_convert_fusion
  333.0 2.7 fusion.27
  337.6 1.9 convert_add_fusion
  342.0 5.5 %fusion = f32[768,768]{1,0:T(8,128)} fusion(bf16[2048,768]{1,0:T(8,128)(2,1)S(1)} %bitcast.88, bf16[512,768]{1,0:T(8,128)(2,1)S(1)} %copy-done.33, bf16[512,768]{1,0:T(8,128)(2,1)S(1)} %copy-done.31, bf16[512,768]{1,0:T(8,128)(2,1)} %collective-permute-done.5, bf16[512,768]{1,0:T(8,128)(2,1)} %collective-permute-done.3.in_ref), kind=kOutput, calls=%fused_computation | convolution fusion | flops 2428502016 | bytes 8650752 | tf_op jit(solution)/shard_map/dot_general | solution.py:30
  347.5 15.4 %collective-permute-done.17 = f32[2,384]{1,0:T(2,128)S(1)} collective-permute-done((f32[2,384]{1,0:T(2,128)S(1)}, f32[2,384]{1,0:T(2,128)S(1)}, u32[]{:S(2)}, u32[]{:S(2)}) %collective-permute-start.17) | collective-permute-done | bytes 3104 | tf_op jit(solution)/shard_map/ppermute | solution.py:658
  365.7 1.9 add_convert_fusion
  370.9 2.8 fusion.9
  373.7 10.3 %collective-permute-done.18 = bf16[4,96,768]{2,1,0:T(8,128)(2,1)} collective-permute-done((bf16[4,96,768]{2,1,0:T(8,128)(2,1)}, bf16[4,96,768]{2,1,0:T(8,128)(2,1)}, u32[]{:S(2)}, u32[]{:S(2)}) %collective-permute-start.18) | collective-permute-done | bytes 589856 | tf_op jit(solution)/shard_map/ppermute | solution.py:658
  385.4 2.6 collective-permute-start.20
  388.1 5.9 %collective-permute-start.19 = (bf16[512,768]{1,0:T(8,128)(2,1)S(1)}, bf16[512,768]{1,0:T(8,128)(2,1)S(1)}, u32[]{:S(2)}, u32[]{:S(2)}) collective-permute-start(bf16[512,768]{1,0:T(8,128)(2,1)S(1)} %copy-done.5), channel_id=1, source_target_pairs={{0,0},{4,1},{8,2},{12,3},{3,4},{7,5},{11,6},{15,7},{1,8},{5,9},{9,... | collective-permute-start | bytes 2359304 | tf_op jit(solution)/shard_map/ppermute | solution.py:702
  394.0 14.9 %collective-permute-done.20 = bf16[2,96,768]{2,1,0:T(8,128)(2,1)S(1)} collective-permute-done((bf16[2,96,768]{2,1,0:T(8,128)(2,1)S(1)}, bf16[2,96,768]{2,1,0:T(8,128)(2,1)S(1)}, u32[]{:S(2)}, u32[]{:S(2)}) %collective-permute-start.20) | collective-permute-done | bytes 294944 | tf_op jit(solution)/shard_map/ppermute | solution.py:658
  409.0 27.1 %collective-permute-start.21 = (bf16[1,96,768]{2,1,0:T(8,128)(2,1)S(1)}, bf16[1,96,768]{2,1,0:T(8,128)(2,1)S(1)}, u32[]{:S(2)}, u32[]{:S(2)}) collective-permute-start(bf16[1,96,768]{2,1,0:T(8,128)(2,1)S(1)} %constant_dynamic-slice_fusion), channel_id=1, source_target_pairs={{0,1},{1,0},{2,3},{3,2},{4,5},{5,4},{6,7},{7,6},{8,9},{9,8},{10,11... | collective-permute-start | bytes 442376 | tf_op jit(solution)/shard_map/ppermute | solution.py:658
  436.1 3.6 collective-permute-done.21
  439.7 6.7 %collective-permute-start.22 = (bf16[96,768]{1,0:T(8,128)(2,1)S(1)}, bf16[96,768]{1,0:T(8,128)(2,1)S(1)}, u32[]{:S(2)}, u32[]{:S(2)}) collective-permute-start(bf16[96,768]{1,0:T(8,128)(2,1)S(1)} %fusion.14), channel_id=1, source_target_pairs={{0,0},{4,1},{8,2},{12,3},{3,4},{7,5},{11,6},{15,7},{1,8},{5,9},{9,... | collective-permute-start | bytes 442376 | tf_op jit(solution)/shard_map/ppermute | solution.py:702
  446.5 20.0 %collective-permute-done.22.value_ref = bf16[96,768]{1,0:T(8,128)(2,1)S(1)} collective-permute-done((bf16[96,768]{1,0:T(8,128)(2,1)S(1)}, bf16[96,768]{1,0:T(8,128)(2,1)S(1)}, u32[]{:S(2)}, u32[]{:S(2)}) %collective-permute-start.22) | collective-permute-done | bytes 147488 | tf_op jit(solution)/shard_map/ppermute | solution.py:702
  472.3 1.9 finish_dense.1
  474.2 2.0 slice_bitcast_fusion.5
  (198 shorter events, 50.8 us)
Async XLA Ops:
  7.2 18.6 %copy-start.21 = (s32[1,512]{1,0:T(1,128)S(1)}, s32[1,512]{1,0:T(1,128)}, u32[]{:S(2)}) copy-start(s32[1,512]{1,0:T(1,128)} %param.27) | copy-start | bytes 6148
  7.2 18.6 %copy-start.20 = (s32[1,2048]{1,0:T(1,128)S(1)}, s32[1,2048]{1,0:T(1,128)}, u32[]{:S(2)}) copy-start(s32[1,2048]{1,0:T(1,128)} %param.26) | copy-start | bytes 24580
  7.2 43.0 %copy-start.6 = (bf16[1,512,768]{2,1,0:T(8,128)(2,1)S(1)}, bf16[1,512,768]{2,1,0:T(8,128)(2,1)}, u32[]{:S(2)}) copy-start(bf16[1,512,768]{2,1,0:T(8,128)(2,1)} %param.29) | copy-start | bytes 2359300
  7.2 184.1 %all-gather.3.cloned.1.call-start = ((), (), s32[]{:S(2)}) async-start(), calls=%async_computation.8 | async-start | bytes 11354112 | tf_op jit(solution)/shard_map/all_gather | solution.py:732
  14.7 35.5 %collective-permute-start.3 = (bf16[512,768]{1,0:T(8,128)(2,1)}, bf16[512,768]{1,0:T(8,128)(2,1)}, u32[]{:S(2)}, u32[]{:S(2)}) collective-permute-start(bf16[512,768]{1,0:T(8,128)(2,1)} %bitcast.115), channel_id=1, source_target_pairs={{0,0},{1,4},{2,8},{3,12},{4,3},{5,7},{6,11},{7,15},{8,1},{9,5},{10... | collective-permute-start | bytes 2359304 | tf_op jit(solution)/shard_map/ppermute | solution.py:698
  22.3 49.2 %copy-start.24 = (bf16[768]{0:T(1024)(128)(2,1)S(1)}, bf16[768]{0:T(1024)(128)(2,1)}, u32[]{:S(2)}) copy-start(bf16[768]{0:T(1024)(128)(2,1)} %param.38) | copy-start | bytes 4612
  22.3 49.2 %copy-start.25 = (bf16[768]{0:T(1024)(128)(2,1)S(1)}, bf16[768]{0:T(1024)(128)(2,1)}, u32[]{:S(2)}) copy-start(bf16[768]{0:T(1024)(128)(2,1)} %param.41) | copy-start | bytes 4612
  22.3 49.2 %copy-start.26 = (bf16[768]{0:T(1024)(128)(2,1)S(1)}, bf16[768]{0:T(1024)(128)(2,1)}, u32[]{:S(2)}) copy-start(bf16[768]{0:T(1024)(128)(2,1)} %param.42) | copy-start | bytes 4612
  22.3 49.2 %copy-start.27 = (bf16[768]{0:T(1024)(128)(2,1)S(1)}, bf16[768]{0:T(1024)(128)(2,1)}, u32[]{:S(2)}) copy-start(bf16[768]{0:T(1024)(128)(2,1)} %param.40) | copy-start | bytes 4612
  22.3 49.3 %copy-start.28 = (bf16[768]{0:T(1024)(128)(2,1)S(1)}, bf16[768]{0:T(1024)(128)(2,1)}, u32[]{:S(2)}) copy-start(bf16[768]{0:T(1024)(128)(2,1)} %param.43) | copy-start | bytes 4612
  22.3 49.3 %copy-start.29 = (bf16[768]{0:T(1024)(128)(2,1)S(1)}, bf16[768]{0:T(1024)(128)(2,1)}, u32[]{:S(2)}) copy-start(bf16[768]{0:T(1024)(128)(2,1)} %param.44) | copy-start | bytes 4612
  22.3 49.9 %copy-start.22 = (bf16[3072]{0:T(1024)(128)(2,1)S(1)}, bf16[3072]{0:T(1024)(128)(2,1)}, u32[]{:S(2)}) copy-start(bf16[3072]{0:T(1024)(128)(2,1)} %param.39) | copy-start | bytes 18436
  22.4 50.4 %copy-start.7 = (bf16[1,512,768]{2,1,0:T(8,128)(2,1)S(1)}, bf16[1,512,768]{2,1,0:T(8,128)(2,1)}, u32[]{:S(2)}) copy-start(bf16[1,512,768]{2,1,0:T(8,128)(2,1)} %param.28) | copy-start | bytes 2359300
  22.5 25.8 %collective-permute-start.1 = (bf16[96,768]{0,1:T(8,128)(2,1)S(1)}, bf16[96,768]{0,1:T(8,128)(2,1)S(1)}, u32[]{:S(2)}, u32[]{:S(2)}) collective-permute-start(bf16[96,768]{0,1:T(8,128)(2,1)S(1)} %bitcast.97), channel_id=1, source_target_pairs={{0,0},{1,4},{2,8},{3,12},{4,3},{5,7},{6,11},{7,15},{8,1},{9,5},{10... | collective-permute-start | bytes 442376 | tf_op jit(solution)/shard_map/ppermute | solution.py:698
  25.8 68.9 %collective-permute-start = (s32[20,128]{1,0:T(8,128)S(1)}, s32[20,128]{1,0:T(8,128)S(1)}, u32[]{:S(2)}, u32[]{:S(2)}) collective-permute-start(s32[20,128]{1,0:T(8,128)S(1)} %add_bitcast_fusion), channel_id=1, source_target_pairs={{0,0},{1,4},{2,8},{3,12},{4,3},{5,7},{6,11},{7,15},{8,1},{9,5},{10... | collective-permute-start | bytes 30728 | tf_op jit(solution)/shard_map/ppermute | solution.py:698
  48.3 12.3 %collective-permute-start.2 = (bf16[96,768]{0,1:T(8,128)(2,1)S(1)}, bf16[96,768]{0,1:T(8,128)(2,1)S(1)}, u32[]{:S(2)}, u32[]{:S(2)}) collective-permute-start(bf16[96,768]{0,1:T(8,128)(2,1)S(1)} %collective-permute-done.1), channel_id=1, source_target_pairs={{0,1},{1,0},{2,3},{3,2},{4,5},{5,4},{6,7},{7,6},{8,9},{9,8},{10,11... | collective-permute-start | bytes 442376 | tf_op jit(solution)/shard_map/ppermute | solution.py:658
  50.3 42.5 %collective-permute-start.5 = (bf16[512,768]{1,0:T(8,128)(2,1)}, bf16[512,768]{1,0:T(8,128)(2,1)}, u32[]{:S(2)}, u32[]{:S(2)}) collective-permute-start(bf16[512,768]{1,0:T(8,128)(2,1)} %collective-permute-done.3.in_ref), channel_id=1, source_target_pairs={{0,8},{4,12},{8,0},{12,4},{1,9},{5,13},{9,1},{13,5},{2,10},{6,14},... | collective-permute-start | bytes 2359304 | tf_op jit(solution)/shard_map/ppermute | solution.py:658
  60.9 31.3 %collective-permute-start.4 = (bf16[192,768]{0,1:T(8,128)(2,1)S(1)}, bf16[192,768]{0,1:T(8,128)(2,1)S(1)}, u32[]{:S(2)}, u32[]{:S(2)}) collective-permute-start(bf16[192,768]{0,1:T(8,128)(2,1)S(1)} %maximum_select_fusion.2), channel_id=1, source_target_pairs={{0,2},{1,3},{2,0},{3,1},{4,6},{5,7},{6,4},{7,5},{8,10},{9,11},{10,... | collective-permute-start | bytes 884744 | tf_op jit(solution)/shard_map/ppermute | solution.py:658
  93.4 14.2 %collective-permute-start.6 = (bf16[384,768]{0,1:T(8,128)(2,1)S(1)}, bf16[384,768]{0,1:T(8,128)(2,1)S(1)}, u32[]{:S(2)}, u32[]{:S(2)}) collective-permute-start(bf16[384,768]{0,1:T(8,128)(2,1)S(1)} %pad_maximum_fusion.1), channel_id=1, source_target_pairs={{0,16},{16,0},{1,17},{17,1},{2,18},{18,2},{3,19},{19,3},{4,20},{20... | collective-permute-start | bytes 1769480 | tf_op jit(solution)/shard_map/ppermute | solution.py:658
  94.8 13.7 %copy-start.17 = (s32[16,128]{1,0:T(8,128)}, s32[16,128]{1,0:T(8,128)S(1)}, u32[]{:S(2)}) copy-start(s32[16,128]{1,0:T(8,128)S(1)} %get-tuple-element.197) | copy-start | bytes 24580
  97.9 47.3 %collective-permute-start.7 = (bf16[512,768]{1,0:T(8,128)(2,1)}, bf16[512,768]{1,0:T(8,128)(2,1)S(1)}, u32[]{:S(2)}, u32[]{:S(2)}) collective-permute-start(bf16[512,768]{1,0:T(8,128)(2,1)} %collective-permute-done.3.in_ref), channel_id=1, source_target_pairs={{0,4},{4,0},{8,12},{12,8},{1,5},{5,1},{9,13},{13,9},{2,6},{6,2},{1... | collective-permute-start | bytes 2359304 | tf_op jit(solution)/shard_map/ppermute | solution.py:658
  101.5 47.4 %collective-permute-start.8 = (bf16[512,768]{1,0:T(8,128)(2,1)}, bf16[512,768]{1,0:T(8,128)(2,1)S(1)}, u32[]{:S(2)}, u32[]{:S(2)}) collective-permute-start(bf16[512,768]{1,0:T(8,128)(2,1)} %collective-permute-done.5), channel_id=1, source_target_pairs={{0,4},{4,0},{8,12},{12,8},{1,5},{5,1},{9,13},{13,9},{2,6},{6,2},{1... | collective-permute-start | bytes 2359304 | tf_op jit(solution)/shard_map/ppermute | solution.py:658
  108.5 221.7 %copy-start.4 = (bf16[768,768]{0,1:T(8,128)(2,1)}, bf16[768,768]{0,1:T(8,128)(2,1)S(1)}, u32[]{:S(2)}) copy-start(bf16[768,768]{0,1:T(8,128)(2,1)S(1)} %maximum_select_fusion) | copy-start | bytes 3538948
  108.5 93.7 %collective-permute-start.10 = (bf16[256,768]{1,0:T(8,128)(2,1)S(1)}, bf16[256,768]{1,0:T(8,128)(2,1)}, u32[]{:S(2)}, u32[]{:S(2)}) collective-permute-start(bf16[256,768]{1,0:T(8,128)(2,1)S(1)} %get-tuple-element.112), channel_id=1, source_target_pairs={{0,0},{1,4},{2,8},{3,12},{4,3},{5,7},{6,11},{7,15},{8,1},{9,5},{10... | collective-permute-start | bytes 1179656 | tf_op jit(solution)/shard_map/ppermute | solution.py:698
  123.9 78.3 %collective-permute-start.9 = (bf16[256,768]{1,0:T(8,128)(2,1)}, bf16[256,768]{1,0:T(8,128)(2,1)}, u32[]{:S(2)}, u32[]{:S(2)}) collective-permute-start(bf16[256,768]{1,0:T(8,128)(2,1)} %get-tuple-element.111), channel_id=1, source_target_pairs={{0,0},{1,4},{2,8},{3,12},{4,3},{5,7},{6,11},{7,15},{8,1},{9,5},{10... | collective-permute-start | bytes 1179656 | tf_op jit(solution)/shard_map/ppermute | solution.py:698
  127.2 95.7 %collective-permute-start.11 = (bf16[256,768]{1,0:T(8,128)(2,1)}, bf16[256,768]{1,0:T(8,128)(2,1)S(1)}, u32[]{:S(2)}, u32[]{:S(2)}) collective-permute-start(bf16[256,768]{1,0:T(8,128)(2,1)} %get-tuple-element.115), channel_id=1, source_target_pairs={{0,0},{1,4},{2,8},{3,12},{4,3},{5,7},{6,11},{7,15},{8,1},{9,5},{10... | collective-permute-start | bytes 1179656 | tf_op jit(solution)/shard_map/ppermute | solution.py:698
  145.3 77.7 %collective-permute-start.12 = (bf16[256,768]{1,0:T(8,128)(2,1)S(1)}, bf16[256,768]{1,0:T(8,128)(2,1)S(1)}, u32[]{:S(2)}, u32[]{:S(2)}) collective-permute-start(bf16[256,768]{1,0:T(8,128)(2,1)S(1)} %get-tuple-element.116), channel_id=1, source_target_pairs={{0,0},{1,4},{2,8},{3,12},{4,3},{5,7},{6,11},{7,15},{8,1},{9,5},{10... | collective-permute-start | bytes 1179656 | tf_op jit(solution)/shard_map/ppermute | solution.py:698
  187.4 9.5 %all-to-all-start = ((bf16[4,384,128]{2,1,0:T(8,128)(2,1)}), bf16[4,384,128]{2,1,0:T(8,128)(2,1)S(1)}, u32[]{:S(2)}, u32[]{:S(2)}) async-start(bf16[4,384,128]{2,1,0:T(8,128)(2,1)} %get-tuple-element.110.refs_6_), calls=%async_computation | async-start | bytes 786432 | tf_op jit(solution)/shard_map/all_to_all | solution.py:774
  196.9 22.4 %all-to-all-start.1 = ((bf16[4,384,128]{2,1,0:T(8,128)(2,1)}), bf16[4,384,128]{2,1,0:T(8,128)(2,1)S(1)}, u32[]{:S(2)}, u32[]{:S(2)}) async-start(bf16[4,384,128]{2,1,0:T(8,128)(2,1)} %get-tuple-element.114.refs_6_), calls=%async_computation.1 | async-start | bytes 786432 | tf_op jit(solution)/shard_map/all_to_all | solution.py:774
  219.2 23.6 %all-to-all-start.2 = ((bf16[4,384,128]{2,1,0:T(8,128)(2,1)}), bf16[4,384,128]{2,1,0:T(8,128)(2,1)S(1)}, u32[]{:S(2)}, u32[]{:S(2)}) async-start(bf16[4,384,128]{2,1,0:T(8,128)(2,1)} %get-tuple-element.118), calls=%async_computation.2 | async-start | bytes 786432 | tf_op jit(solution)/shard_map/all_to_all | solution.py:774
  222.9 18.3 %copy-start.18 = (f32[8,768]{1,0:T(8,128)S(1)}, f32[8,768]{1,0:T(8,128)}, u32[]{:S(2)}) copy-start(f32[8,768]{1,0:T(8,128)} %get-tuple-element.145) | copy-start | bytes 73732
  222.9 19.1 %copy-start.19 = (f32[4,1,768]{2,1,0:T(1,128)S(1)}, f32[4,1,768]{2,1,0:T(1,128)}, u32[]{:S(2)}) copy-start(f32[4,1,768]{2,1,0:T(1,128)} %get-tuple-element.147) | copy-start | bytes 36868
  222.9 162.3 %reduce-scatter.3.cloned.1.call-start = ((), (), s32[]{:S(2)}) async-start(), calls=%async_computation.6 | async-start | bytes 13271040 | tf_op jit(solution)/shard_map/reduce_scatter | solution.py:807
  242.8 13.6 %copy-start.11 = (bf16[4,384,128]{2,1,0:T(8,128)(2,1)}, bf16[4,384,128]{2,1,0:T(8,128)(2,1)S(1)}, u32[]{:S(2)}) copy-start(bf16[4,384,128]{2,1,0:T(8,128)(2,1)S(1)} %all-to-all-done.2.refs_7_) | copy-start | bytes 1179652
  257.6 39.0 %collective-permute-start.13 = (bf16[512,768]{1,0:T(8,128)(2,1)S(1)}, bf16[512,768]{1,0:T(8,128)(2,1)S(1)}, u32[]{:S(2)}, u32[]{:S(2)}) collective-permute-start(bf16[512,768]{1,0:T(8,128)(2,1)S(1)} %pad_maximum_fusion), channel_id=1, source_target_pairs={{0,0},{4,1},{8,2},{12,3},{3,4},{7,5},{11,6},{15,7},{1,8},{5,9},{9,... | collective-permute-start | bytes 2359304 | tf_op jit(solution)/shard_map/ppermute | solution.py:702
  259.6 37.1 %all-to-all-start.3 = ((bf16[4,384,128]{2,1,0:T(8,128)(2,1)}), bf16[4,384,128]{2,1,0:T(8,128)(2,1)S(1)}, u32[]{:S(2)}, u32[]{:S(2)}) async-start(bf16[4,384,128]{2,1,0:T(8,128)(2,1)} %get-tuple-element.149), calls=%async_computation.4 | async-start | bytes 786432 | tf_op jit(solution)/shard_map/all_to_all | solution.py:774
  263.0 209.2 %reduce-scatter.5.cloned.1.call-start = ((), (), s32[]{:S(2)}) async-start(), calls=%async_computation.7 | async-start | bytes 1843200 | tf_op jit(solution)/shard_map/reduce_scatter | solution.py:845
  296.7 31.4 %copy-start.8 = (bf16[512,768]{1,0:T(8,128)(2,1)}, bf16[512,768]{1,0:T(8,128)(2,1)S(1)}, u32[]{:S(2)}) copy-start(bf16[512,768]{1,0:T(8,128)(2,1)S(1)} %collective-permute-done.13) | copy-start | bytes 2359300
  332.7 3.6 collective-permute-start.14
  337.5 3.0 collective-permute-start.16
  340.5 27.1 %collective-permute-start.15 = (bf16[512,768]{1,0:T(8,128)(2,1)}, bf16[512,768]{1,0:T(8,128)(2,1)}, u32[]{:S(2)}, u32[]{:S(2)}) collective-permute-start(bf16[512,768]{1,0:T(8,128)(2,1)} %slice.280), channel_id=1, source_target_pairs={{0,8},{4,12},{8,0},{12,4},{1,9},{5,13},{9,1},{13,5},{2,10},{6,14},... | collective-permute-start | bytes 2359304 | tf_op jit(solution)/shard_map/ppermute | solution.py:658
  340.5 22.4 %collective-permute-start.17 = (f32[2,384]{1,0:T(2,128)S(1)}, f32[2,384]{1,0:T(2,128)S(1)}, u32[]{:S(2)}, u32[]{:S(2)}) collective-permute-start(f32[2,384]{1,0:T(2,128)S(1)} %maximum_select_fusion.4), channel_id=1, source_target_pairs={{0,8},{4,12},{8,0},{12,4},{1,9},{5,13},{9,1},{13,5},{2,10},{6,14},... | collective-permute-start | bytes 9224 | tf_op jit(solution)/shard_map/ppermute | solution.py:658
  369.4 14.6 %collective-permute-start.18 = (bf16[4,96,768]{2,1,0:T(8,128)(2,1)}, bf16[4,96,768]{2,1,0:T(8,128)(2,1)}, u32[]{:S(2)}, u32[]{:S(2)}) collective-permute-start(bf16[4,96,768]{2,1,0:T(8,128)(2,1)} %constant_dynamic-slice_fusion.2), channel_id=1, source_target_pairs={{0,16},{16,0},{1,17},{17,1},{2,18},{18,2},{3,19},{19,3},{4,20},{20... | collective-permute-start | bytes 1769480 | tf_op jit(solution)/shard_map/ppermute | solution.py:658
  385.4 23.5 %collective-permute-start.20 = (bf16[2,96,768]{2,1,0:T(8,128)(2,1)S(1)}, bf16[2,96,768]{2,1,0:T(8,128)(2,1)S(1)}, u32[]{:S(2)}, u32[]{:S(2)}) collective-permute-start(bf16[2,96,768]{2,1,0:T(8,128)(2,1)S(1)} %constant_dynamic-slice_fusion.1), channel_id=1, source_target_pairs={{0,2},{1,3},{2,0},{3,1},{4,6},{5,7},{6,4},{7,5},{8,10},{9,11},{10,... | collective-permute-start | bytes 884744 | tf_op jit(solution)/shard_map/ppermute | solution.py:658
  388.1 82.9 %collective-permute-start.19 = (bf16[512,768]{1,0:T(8,128)(2,1)S(1)}, bf16[512,768]{1,0:T(8,128)(2,1)S(1)}, u32[]{:S(2)}, u32[]{:S(2)}) collective-permute-start(bf16[512,768]{1,0:T(8,128)(2,1)S(1)} %copy-done.5), channel_id=1, source_target_pairs={{0,0},{4,1},{8,2},{12,3},{3,4},{7,5},{11,6},{15,7},{1,8},{5,9},{9,... | collective-permute-start | bytes 2359304 | tf_op jit(solution)/shard_map/ppermute | solution.py:702
  409.0 30.7 %collective-permute-start.21 = (bf16[1,96,768]{2,1,0:T(8,128)(2,1)S(1)}, bf16[1,96,768]{2,1,0:T(8,128)(2,1)S(1)}, u32[]{:S(2)}, u32[]{:S(2)}) collective-permute-start(bf16[1,96,768]{2,1,0:T(8,128)(2,1)S(1)} %constant_dynamic-slice_fusion), channel_id=1, source_target_pairs={{0,1},{1,0},{2,3},{3,2},{4,5},{5,4},{6,7},{7,6},{8,9},{9,8},{10,11... | collective-permute-start | bytes 442376 | tf_op jit(solution)/shard_map/ppermute | solution.py:658
  439.7 38.4 %copy-start.9 = (bf16[512,768]{1,0:T(8,128)(2,1)S(1)}, bf16[512,768]{1,0:T(8,128)(2,1)}, u32[]{:S(2)}) copy-start(bf16[512,768]{1,0:T(8,128)(2,1)} %copy-done.8) | copy-start | bytes 2359300
  439.7 26.8 %collective-permute-start.22 = (bf16[96,768]{1,0:T(8,128)(2,1)S(1)}, bf16[96,768]{1,0:T(8,128)(2,1)S(1)}, u32[]{:S(2)}, u32[]{:S(2)}) collective-permute-start(bf16[96,768]{1,0:T(8,128)(2,1)S(1)} %fusion.14), channel_id=1, source_target_pairs={{0,0},{4,1},{8,2},{12,3},{3,4},{7,5},{11,6},{15,7},{1,8},{5,9},{9,... | collective-permute-start | bytes 442376 | tf_op jit(solution)/shard_map/ppermute | solution.py:702
  (18 other events, 49.6 us)
Sparse Core Ops, SparseCore 0:
  14.8 133.1 all-gather.2
  256.6 93.4 reduce-scatter.2
  385.4 58.0 reduce-scatter.4

commit v7 on v6

--- a/solution.py
+++ b/solution.py
@@ -64,14 +64,11 @@
     return jnp.concatenate([packed[:BLOCK], third], axis=1)
 
 
-CHUNKS = (0, 2, 1, 3)
-
-
 def fetch_chunks(lane_ref, chunk_refs, target, sems):
     rows = chunk_refs[0].shape[0]
     copies = []
-    for at, (turn, chunk) in enumerate(zip(CHUNKS, chunk_refs)):
-        offset = pl.multiple_of((lane_ref[0] ^ turn) * rows, rows)
+    for at, chunk in enumerate(chunk_refs):
+        offset = pl.multiple_of(lax.rem(lane_ref[0] + at, len(chunk_refs)) * rows, rows)
         copies.append(pltpu.make_async_copy(chunk, target.at[pl.ds(offset, rows), :], sems.at[at]))
     return copies
 
@@ -235,8 +232,8 @@
                 sums_ref[:, at : at + SLAB] = column_sum(out_ref[:, at : at + SLAB].astype(F32))
             rows_each = final_ref.shape[1]
             copies = []
-            for at, turn in enumerate(CHUNKS):
-                offset = pl.multiple_of((lane_ref[0] ^ turn) * rows_each, rows_each)
+            for at in range(final_ref.shape[0]):
+                offset = pl.multiple_of(lax.rem(lane_ref[0] + at, final_ref.shape[0]) * rows_each, rows_each)
                 copies.append(
                     pltpu.make_async_copy(
                         out_ref.at[pl.ds(offset, rows_each), :], final_ref.at[at], sems.at[at]
@@ -492,8 +489,8 @@
             smem,
             fixed(ctx.shape),
             mine(width),
-            fixed(teacher.shape),
-            fixed(cotangent.shape),
+            mine(width),
+            mine(width),
             mine(1),
             fixed(vecs.shape),
             fixed(inner_bias.shape),
@@ -680,26 +677,15 @@
     return (left_side.astype(F32) + right_side.astype(F32)).astype(BF16)
 
 
-def halve(held, axis, bit):
-    own = (lax.axis_index(axis) & bit) // bit
-    half = held.shape[0] // 2
-    keep = lax.dynamic_slice_in_dim(held, own * half, half, 0)
-    send = lax.dynamic_slice_in_dim(held, (1 - own) * half, half, 0)
-    return (keep, swap(send, axis, bit))
-
-
-PLANE = (0, 3, 1, 2)
-ORIGIN = (0, 2, 3, 1)
-AWAY = [(lo * 4 + z, z * 4 + PLANE[lo]) for lo in range(4) for z in range(4)]
-BACK = [(there, here) for here, there in AWAY]
-
-
-def send_away(value):
-    return lax.ppermute(value, ("lo", "tensor"), AWAY)
-
-
-def send_back(value):
-    return lax.ppermute(value, ("lo", "tensor"), BACK)
+def scatter_rows(held):
+    index = lax.axis_index("dp")
+    for bit in bits_of("dp"):
+        held = held.reshape((held.shape[0] // 2, 2) + held.shape[1:])
+        own = (index & bit) // bit
+        send = lax.dynamic_index_in_dim(held, 1 - own, 1, keepdims=False)
+        keep = lax.dynamic_index_in_dim(held, own, 1, keepdims=False)
+        held = add_low(keep, swap(send, "dp", bit))
+    return held[0]
 
 
 def local(
@@ -710,8 +696,8 @@
 ):
     _, part_len, width = inputs.shape
     parts = lax.axis_size("tensor")
-    copies = lax.axis_size("hi") * lax.axis_size("lo")
-    lane_index = lax.axis_index("lo")
+    copies = lax.axis_size("dp")
+    rank = lax.axis_index("tensor")
     total_tokens = part_len * parts * copies
     seq_len = part_len * parts
     head_cols = w_query.shape[1]
@@ -720,16 +706,21 @@
     shard_rows = w_inner.shape[0]
     halves = part_len // BLOCK
 
-    rows_in = send_away(inputs.reshape(part_len, width))
-    head_rows = send_away(interleave(w_query, w_key, w_value, heads))
-    whole_row = jnp.concatenate((segment_ids.reshape(seq_len), valid_mask.reshape(part_len)))
-    whole_row = send_away(whole_row.reshape(-1, 128)).reshape(-1)
+    def shift(value, by):
+        return lax.ppermute(value, "tensor", [(i, i + by) for i in range(parts) if 0 <= i + by < parts])
+
+    def turn(value, by):
+        return lax.ppermute(value, "tensor", [(i, (i + by) % parts) for i in range(parts)])
+
+    valid_rows = valid_mask.astype(F32).reshape(part_len, 1)
     valid_count = jnp.sum(valid_mask.astype(F32))
     upper = jnp.floor(valid_count / 256.0)
-    count_row = jnp.zeros((shard_rows, DH), BF16)
-    count_row = count_row.at[0, 0].set(upper.astype(BF16)).at[0, 1].set((valid_count - 256.0 * upper).astype(BF16))
-    mine = jnp.concatenate((w_inner, w_outer.T, w_output.T, count_row), axis=1)
-    weights = lax.all_gather(mine, ("tensor", "hi", "lo"), axis=0, tiled=False)
+    spot = lax.broadcasted_iota(jnp.int32, (shard_rows, DH), 0) * DH + lax.broadcasted_iota(
+        jnp.int32, (shard_rows, DH), 1
+    )
+    count_row = jnp.where(spot == 0, upper, jnp.where(spot == 1, valid_count - 256.0 * upper, 0.0))
+    mine = jnp.concatenate((w_inner, w_outer.T, w_output.T, count_row.astype(BF16)), axis=1)
+    weights = lax.all_gather(mine, ("tensor", "dp"), axis=0, tiled=False)
     counts = weights[:, 0, -DH : 2 - DH].astype(F32)
     counted = 256.0 * jnp.sum(counts[:, 0]) + jnp.sum(counts[:, 1])
     ratio = (total_tokens / counted).reshape(1)
@@ -737,41 +728,39 @@
     marks = [[(t, 0) for t in range(parts)]]
     place = jnp.asarray(list(range(parts)) + [0], jnp.int32)
 
-    head_rows = merge(head_rows, swap(head_rows, "tensor", 1), "tensor", 1)
-    head_rows = after(head_rows, rows_in)
-    near_chunk = swap(rows_in, "lo", 1)
-    next_chunk = swap(rows_in, "lo", 2)
-    head_rows = merge(head_rows, swap(head_rows, "tensor", 2), "tensor", 2)
-    head_rows = after(head_rows, next_chunk)
-    far_chunk = swap(next_chunk, "lo", 1)
-    blocks = head_rows.reshape(4, shard_rows, -1)
-    w_heads = jnp.concatenate([blocks[plane] for plane in PLANE], axis=0)
-    for bit in bits_of("hi"):
-        w_heads = merge(w_heads, swap(w_heads, "hi", bit), "hi", bit)
-    tokens = [rows_in, next_chunk, near_chunk, far_chunk]
-
-    mine_cols = lane_index * head_cols
+    rows_in = inputs.reshape(part_len, width)
+    ahead, behind = [], []
+    up, down = rows_in, rows_in
+    w_heads = interleave(w_query, w_key, w_value, heads)
+    steps = list(bits_of("dp"))
+    for step in range(parts - 1):
+        up, down = shift(up, 1), shift(down, -1)
+        behind.append(up)
+        ahead.append(down)
+        if step < len(steps):
+            w_heads = merge(w_heads, swap(w_heads, "dp", steps[step]), "dp", steps[step])
+        if step < parts - 2:
+            up, down, w_heads = lax.optimization_barrier((up, down, w_heads))
+    for bit in steps[parts - 1 :]:
+        w_heads = merge(w_heads, swap(w_heads, "dp", bit), "dp", bit)
+    tokens = [rows_in] + [
+        jnp.where(rank + by < parts, ahead[by - 1], behind[parts - by - 1]) for by in range(1, parts)
+    ]
+
+    mine_cols = rank * head_cols
     query_shift = lax.dynamic_slice_in_dim(query_bias, mine_cols, head_cols).astype(F32)
     value_shift = lax.dynamic_slice_in_dim(value_bias, mine_cols, head_cols).astype(F32)
     shifts = interleave(query_shift[None], jnp.zeros_like(query_shift)[None], value_shift[None], heads)
     qkv = [(dot(chunk, w_heads) + shifts).astype(BF16) for chunk in tokens]
 
-    def half_of(value, half):
-        return value.reshape(part_len, width)[half * BLOCK : (half + 1) * BLOCK]
-
-    sides = []
-    for half in range(halves):
-        sides.append([send_away(after(half_of(value, half), w_heads)) for value in (teacher, cotangent)])
-
-    segment_row = whole_row[:seq_len]
-    valid_rows = whole_row[seq_len:].astype(F32).reshape(part_len, 1)
+    segment_row = segment_ids.reshape(seq_len)
     bounds = document_blocks(segment_row)
     seg_col = segment_row.reshape(seq_len, 1)
     seg_row = segment_row.reshape(1, seq_len)
-    lane = lane_index.astype(jnp.int32).reshape(1)
+    lane = rank.astype(jnp.int32).reshape(1)
 
     def exchange(packed_blocks):
-        return lax.all_to_all(packed_blocks, "lo", 0, 0)
+        return lax.all_to_all(packed_blocks, "tensor", 0, 0)
 
     contexts, lses, arrived = [], [], []
     for half in range(halves):
@@ -784,9 +773,11 @@
         (output_bias, gain_attn, shift_attn, outer_bias, gain_ffn, shift_ffn, outer_bias, outer_bias)
     ).astype(F32)
     inner_rows = inner_bias.astype(F32).reshape(parts, 1, hidden_cols)
+    teacher_rows = teacher.reshape(part_len, width)
+    cotangent_rows = cotangent.reshape(part_len, width)
     chains = [
         run_dense(
-            half, marks, place, ratio, arrived[half], rows_in, *sides[half],
+            half, marks, place, ratio, arrived[half], rows_in, teacher_rows, cotangent_rows,
             valid_rows, vecs, inner_rows, pieces,
         )
         for half in range(halves)
@@ -804,13 +795,10 @@
     room = -(-notes.shape[0] // (shard_rows * 128)) * 128
     notes = jnp.pad(notes, (0, shard_rows * room - notes.shape[0])).reshape(shard_rows, room)
     (packed,) = run_weights(([[0]],), 1, width, place, jnp.tile(notes, (copies, 1)), *sources)
-    packed = lax.psum_scatter(packed, ("hi", "lo"), scatter_dimension=1, tiled=True)
-    layer_out = send_back(jnp.concatenate(layers, axis=0))
+    packed = lax.psum_scatter(packed, "dp", scatter_dimension=1, tiled=True)
 
     earlier, before = [], []
     for half in range(halves):
-        if half == halves - 1:
-            layer_out, before = lax.optimization_barrier((layer_out, before))
         results = run_backward(
             (halves, half), lane, bounds, qkv, seg_col, seg_row, contexts[half], head_grads[half],
             lses[half], earlier, before,
@@ -818,37 +806,30 @@
         if half < halves - 1:
             before, earlier = [results[0]], earlier + [results[1]]
     joined_grad, sums = results
-    joined_grad = joined_grad.reshape(seq_len, width)
-    middle = seq_len // 2
-    core_share = swap(dot(joined_grad[middle:], w_heads, NT).astype(BF16), "lo", 1)
+    away = [dot(joined_grad[by], w_heads, NT).astype(BF16) for by in (2, 1, 3)]
+    own_share = dot(joined_grad[0], w_heads, NT)
+    away, own_share, sums, joined_grad = lax.optimization_barrier((away, own_share, sums, joined_grad))
+    came = [turn(share, by) for share, by in zip(away, (2, 1, 3))]
     sums = sums.reshape(heads, 4, DH)
     sums = jnp.concatenate((sums[:, 0].reshape(1, head_cols), sums[:, 3].reshape(1, head_cols)), axis=1)
-    core_share, sums = lax.optimization_barrier((core_share, sums))
-    sums = merge(sums, swap(sums, "lo", 1), "lo", 1)
-    own_share = dot(joined_grad[:middle], w_heads, NT)
-    own_share, joined_grad = lax.optimization_barrier((own_share, joined_grad))
-    input_share = own_share + core_share.astype(F32)
-    chip_share = swap(input_share[part_len:].astype(BF16), "lo", 2)
-    sums = merge(sums, swap(sums, "lo", 2), "lo", 2)
-    head_weights = dot(jnp.concatenate(tokens, axis=0), joined_grad, TN)
+    for bit in bits_of("tensor"):
+        sums = merge(sums, swap(sums, "tensor", bit), "tensor", bit)
+    head_weights = dot(
+        jnp.concatenate(tokens, axis=0), joined_grad.reshape(seq_len, -1), TN
+    ).reshape((copies, shard_rows, -1))
+    head_weights, packed = lax.optimization_barrier((head_weights, packed))
+    packed = lax.psum_scatter(packed, "tensor", scatter_dimension=0, tiled=True)[0]
     biases = jnp.concatenate((sums[:, :head_cols].reshape(-1), sums[:, head_cols:].reshape(-1)))
     biases = jnp.pad(
         biases.reshape(8, heads, 1, DH), ((0, shard_rows - 8), (0, 0), (1, 2), (0, 0))
     ).reshape(1, shard_rows, -1)
-    head_weights = (head_weights.reshape((copies, shard_rows, -1)) + biases).astype(BF16)
-    chip_share, held = lax.optimization_barrier((chip_share, head_weights))
-    for bit in reversed(list(bits_of("hi"))):
-        held = add_low(*halve(held, "hi", bit))
-    input_grad = input_share[:part_len] + chip_share.astype(F32) + jnp.concatenate(first_grads, axis=0)
-    input_grad, held = lax.optimization_barrier((input_grad.astype(BF16), held))
-    packed = after(packed, input_grad)
-    packed = lax.psum_scatter(packed, "tensor", scatter_dimension=0, tiled=True)[0]
-    input_grad = send_back(input_grad).astype(F32)
-    held = jnp.stack([held[origin] for origin in ORIGIN])
-    held = add_low(*halve(held, "tensor", 2))
-    held = add_low(*halve(held, "tensor", 1))
-    query_grad, key_grad, value_grad, biases = run_finish_heads(send_back(held[0]))
+    query_grad, key_grad, value_grad, biases = run_finish_heads(
+        scatter_rows((head_weights + biases).astype(BF16))
+    )
     biases = biases.reshape(2, width)
+    input_grad = own_share + jnp.concatenate(first_grads, axis=0)
+    for share in came:
+        input_grad = input_grad + share.astype(F32)
 
     inner_grad, outer_grad, output_grad, notes = run_finish_dense(packed, hidden_cols, head_cols)
     notes = notes.reshape(-1)
@@ -858,7 +839,7 @@
 
     mse_loss = jnp.sum(total(0)) / (counted * width)
     return (
-        layer_out.reshape(1, part_len, width),
+        jnp.concatenate(layers, axis=0).reshape(1, part_len, width),
         mse_loss,
         input_grad.reshape(1, part_len, width),
         query_grad,
@@ -880,19 +861,13 @@
 
 
 def solution(mesh):
-    devices = mesh.devices
-    groups = devices.shape[0] // 4
-    finer = jax.sharding.Mesh(
-        devices.reshape((groups, 4) + devices.shape[1:]), ("hi", "lo", "tensor")
-    )
-    split = ("hi", "lo")
-    shard = P(split, "tensor", None)
-    by_dp, by_tensor = P(split, "tensor"), P("tensor", split)
+    shard = P("dp", "tensor", None)
+    by_dp, by_tensor = P("dp", "tensor"), P("tensor", "dp")
     in_specs = (
-        (shard, P(split, None), by_dp, shard, shard)
+        (shard, P("dp", None), by_dp, shard, shard)
         + (by_dp,) * 3
         + (by_tensor, by_dp, by_tensor)
         + (P(),) * 9
     )
     out_specs = (shard, P(), shard) + (by_dp,) * 3 + (by_tensor, by_dp, by_tensor) + (P(),) * 9
-    return jax.shard_map(local, mesh=finer, in_specs=in_specs, out_specs=out_specs, check_vma=False)
+    return jax.shard_map(local, mesh=mesh, in_specs=in_specs, out_specs=out_specs, check_vma=False)

time: 490 us -> 451 us (0.920)
  the two profiles are of different devices: /device:TPU:3 before, /device:TPU:0 now
where the time goes in v7:
time: 451 us; the launch traced here: 449 us
  waiting for transfers between devices  191 us (42%)
  Pallas kernels  127 us (28%)
  starting transfers between devices  52.2 us (12%)
  matrix products  20.8 us (5%)
  local copies, waits for them, and re-layouts  19.7 us (4%)
  other arithmetic  19.1 us (4%)
  between operations  18.9 us (4%)
    ppermute x3, waiting for transfers between devices, turn(): lax.ppermute(value, 'tensor', [(i, (i + by) % parts) for i in range(parts)])  79.8 us
    ppermute x6, waiting for transfers between devices, shift(): lax.ppermute(value, 'tensor', [(i, i + by) for i in range(parts) if 0 <=...  55.5 us
    pallas_call x2, Pallas kernels, run_backward(): pl.pallas_call(functools.partial(attend_backward, which), out_shape=out_s...  45.1 us
    ppermute x8, waiting for transfers between devices, swap(): return lax.ppermute(value, axis, [(i, i ^ bit) for i in range(size)])  37.7 us
    pallas_call x2, Pallas kernels, run_dense(): pl.pallas_call(functools.partial(dense_chain, marks), out_shape=out_shape...  33.9 us
    pallas_call x2, Pallas kernels, run_forward(): pl.pallas_call(functools.partial(attend_forward, which), out_shape=(jax.S...  31.9 us
    dot_general x9, matrix products, dot(): lax.dot_general(left_side, right_side, dims, preferred_element_type=F32)  20.8 us
    all_to_all x4, starting transfers between devices, exchange(): return lax.all_to_all(packed_blocks, 'tensor', 0, 0)  20.7 us
  transfers between devices with their start and end apart: 24, of which 14 were waited for; matrix products, arithmetic and copies ran while one was open for 11% of the time, Pallas kernels for 25%

profile of v7, /device:TPU:0, one launch (start us, length us, event | category | flops | bytes accessed | tf_op | source)
XLA Modules:
  0.0 449.3 jit_solution(4752933815781119614)
XLA Ops:
  10.8 1.8 concatenate.66
  12.7 5.0 %collective-permute-start = (bf16[512,768]{1,0:T(8,128)(2,1)}, bf16[512,768]{1,0:T(8,128)(2,1)S(1)}, u32[]{:S(2)}, u32[]{:S(2)}) collective-permute-start(bf16[512,768]{1,0:T(8,128)(2,1)} %bitcast.97), channel_id=1, source_target_pairs={{0,1},{1,2},{2,3},{4,5},{5,6},{6,7},{8,9},{9,10},{10,11},{12,13},{... | collective-permute-start | bytes 2359304 | tf_op jit(solution)/shard_map/ppermute | solution.py:710
  23.8 18.3 %collective-permute-done = bf16[512,768]{1,0:T(8,128)(2,1)S(1)} collective-permute-done((bf16[512,768]{1,0:T(8,128)(2,1)}, bf16[512,768]{1,0:T(8,128)(2,1)S(1)}, u32[]{:S(2)}, u32[]{:S(2)}) %collective-permute-start) | collective-permute-done | bytes 786464 | tf_op jit(solution)/shard_map/ppermute | solution.py:710
  42.1 4.1 collective-permute-done.1
  46.1 4.4 collective-permute-start.3
  52.0 1.5 collective-permute-start.5
  56.0 12.1 %collective-permute-done.5 = bf16[192,768]{0,1:T(8,128)(2,1)S(1)} collective-permute-done((bf16[192,768]{0,1:T(8,128)(2,1)S(1)}, bf16[192,768]{0,1:T(8,128)(2,1)S(1)}, u32[]{:S(2)}, u32[]{:S(2)}) %collective-permute-start.5) | collective-permute-done | bytes 294944 | tf_op jit(solution)/shard_map/ppermute | solution.py:655
  68.7 10.7 %collective-permute-done.3 = bf16[512,768]{1,0:T(8,128)(2,1)} collective-permute-done((bf16[512,768]{1,0:T(8,128)(2,1)S(1)}, bf16[512,768]{1,0:T(8,128)(2,1)}, u32[]{:S(2)}, u32[]{:S(2)}) %collective-permute-start.3) | collective-permute-done | bytes 786464 | tf_op jit(solution)/shard_map/ppermute | solution.py:710
  79.3 2.2 collective-permute-done.4
  83.7 3.4 collective-permute-start.7
  88.6 18.9 %collective-permute-done.6 = bf16[384,768]{0,1:T(8,128)(2,1)S(1)} collective-permute-done((bf16[384,768]{0,1:T(8,128)(2,1)S(1)}, bf16[384,768]{0,1:T(8,128)(2,1)S(1)}, u32[]{:S(2)}, u32[]{:S(2)}) %collective-permute-start.6) | collective-permute-done | bytes 589856 | tf_op jit(solution)/shard_map/ppermute | solution.py:655
  107.5 1.8 add_convert_fusion.2.refs_2_
  109.2 1.7 fusion.4.refs_0_
  111.0 10.6 %collective-permute-done.7 = bf16[512,768]{1,0:T(8,128)(2,1)S(1)} collective-permute-done((bf16[512,768]{1,0:T(8,128)(2,1)}, bf16[512,768]{1,0:T(8,128)(2,1)S(1)}, u32[]{:S(2)}, u32[]{:S(2)}) %collective-permute-start.7) | collective-permute-done | bytes 786464 | tf_op jit(solution)/shard_map/ppermute | solution.py:710
  121.7 9.7 %collective-permute-done.8 = bf16[512,768]{1,0:T(8,128)(2,1)S(1)} collective-permute-done((bf16[512,768]{1,0:T(8,128)(2,1)S(1)}, bf16[512,768]{1,0:T(8,128)(2,1)S(1)}, u32[]{:S(2)}, u32[]{:S(2)}) %collective-permute-start.8) | collective-permute-done | bytes 786464 | tf_op jit(solution)/shard_map/ppermute | solution.py:710
  131.6 1.7 add_convert_fusion.3.refs_1_
  133.3 1.7 add_convert_fusion.1.refs_3_
  135.1 16.0 %attend_forward.2 = (bf16[4,384,128]{2,1,0:T(8,128)(2,1)}, f32[3,1,1024]{2,1,0:T(1,128)}) custom-call(s32[1]{0:T(128)} %bitcast.6.lane_ref, s32[8]{0:T(128)} %get-tuple-element.162.low_ref, s32[8]{0:T(128)} %get-tuple-element.161.high_ref, bf16[512,768]{1,0:T(8,128)(2,1)} %fusion.4.refs_0_, bf16[512,768]{1,0:T(8,128)(2,1)} %add_convert_fusion.3.refs_1_, ...), custom_call_target="tpu_custom_call" | custom-call | flops 1610612736 | bytes 5242880 | tf_op jit(solution)/shard_map/attend_forward/pallas_call | solution.py:265
  151.1 5.5 %all-to-all-start = ((bf16[4,384,128]{2,1,0:T(8,128)(2,1)}), bf16[4,384,128]{2,1,0:T(8,128)(2,1)S(1)}, u32[]{:S(2)}, u32[]{:S(2)}) async-start(bf16[4,384,128]{2,1,0:T(8,128)(2,1)} %get-tuple-element.87.refs_6_), calls=%async_computation | async-start | bytes 786432 | tf_op jit(solution)/shard_map/all_to_all | solution.py:763
  158.8 15.9 %attend_forward.3 = (bf16[4,384,128]{2,1,0:T(8,128)(2,1)}, f32[3,1,1024]{2,1,0:T(1,128)}) custom-call(s32[1]{0:T(128)} %bitcast.6.lane_ref, s32[8]{0:T(128)} %get-tuple-element.162.low_ref, s32[8]{0:T(128)} %get-tuple-element.161.high_ref, bf16[512,768]{1,0:T(8,128)(2,1)} %fusion.4.refs_0_, bf16[512,768]{1,0:T(8,128)(2,1)} %add_convert_fusion.3.refs_1_, ...), custom_call_target="tpu_custom_call" | custom-call | flops 1610612736 | bytes 5242880 | tf_op jit(solution)/shard_map/attend_forward/pallas_call | solution.py:265
  175.7 5.1 %all-to-all-start.1 = ((bf16[4,384,128]{2,1,0:T(8,128)(2,1)}), bf16[4,384,128]{2,1,0:T(8,128)(2,1)S(1)}, u32[]{:S(2)}, u32[]{:S(2)}) async-start(bf16[4,384,128]{2,1,0:T(8,128)(2,1)} %get-tuple-element.89.refs_6_), calls=%async_computation.1 | async-start | bytes 786432 | tf_op jit(solution)/shard_map/all_to_all | solution.py:763
  182.8 17.1 %dense_chain.2 = (bf16[256,768]{1,0:T(8,128)(2,1)}, f32[256,768]{1,0:T(8,128)}, bf16[4,384,128]{2,1,0:T(8,128)(2,1)}, bf16[256,768]{1,0:T(8,128)(2,1)}, bf16[256...) custom-call(s32[5]{0:T(128)} %constant.116.clone.place_ref, ...), custom_call_target="tpu_custom_call" | custom-call | flops 5637144576 | bytes 18874368 | tf_op jit(solution)/shard_map/dense_chain/pallas_call | solution.py:483
  200.0 5.1 %all-to-all-start.3 = ((bf16[4,384,128]{2,1,0:T(8,128)(2,1)}), bf16[4,384,128]{2,1,0:T(8,128)(2,1)S(1)}, u32[]{:S(2)}, u32[]{:S(2)}) async-start(bf16[4,384,128]{2,1,0:T(8,128)(2,1)} %get-tuple-element.93), calls=%async_computation.3 | async-start | bytes 786432 | tf_op jit(solution)/shard_map/all_to_all | solution.py:763
  205.1 16.8 %dense_chain.3 = (bf16[256,768]{1,0:T(8,128)(2,1)}, f32[256,768]{1,0:T(8,128)}, bf16[4,384,128]{2,1,0:T(8,128)(2,1)}, bf16[256,768]{1,0:T(8,128)(2,1)}, bf16[256...) custom-call(s32[5]{0:T(128)} %constant.116.clone.place_ref, ...), custom_call_target="tpu_custom_call" | custom-call | flops 5637144576 | bytes 18874368 | tf_op jit(solution)/shard_map/dense_chain/pallas_call | solution.py:483
  224.3 12.8 %dense_weights.1 = bf16[4,768,1856]{2,1,0:T(8,128)(2,1)} custom-call(s32[5]{0:T(128)} %constant.116.clone.place_ref, bf16[256,768]{1,0:T(8,128)(2,1)} %get-tuple-element.111.refs_0_, bf16[256,768]{1,0:T(8,128)(2,1)} %get-tuple-element.112.refs_1_, bf16[256,768]{1,0:T(8,128)(2,1)} %get-tuple-element.113.refs_2_, bf16[256,768]{1,0:T(8,128)(2,1)} %get-tuple-element.114.refs_3_, ...), custom_call_target="tpu_custom_call" | custom-call | flops 5838471168 | bytes 20971520 | tf_op jit(solution)/shard_map/dense_weights/pallas_call | solution.py:579
  237.2 5.1 %all-to-all-start.2 = ((bf16[4,384,128]{2,1,0:T(8,128)(2,1)}), bf16[4,384,128]{2,1,0:T(8,128)(2,1)S(1)}, u32[]{:S(2)}, u32[]{:S(2)}) async-start(bf16[4,384,128]{2,1,0:T(8,128)(2,1)} %get-tuple-element.91), calls=%async_computation.2 | async-start | bytes 786432 | tf_op jit(solution)/shard_map/all_to_all | solution.py:763
  242.2 21.3 %attend_backward.2 = (f32[3,2048,128]{2,1,0:T(8,128)}, bf16[4,256,384]{2,1,0:T(8,128)(2,1)}) custom-call(s32[1]{0:T(128)} %bitcast.6.lane_ref, s32[8]{0:T(128)} %get-tuple-element.162.low_ref, s32[8]{0:T(128)} %get-tuple-element.161.high_ref, bf16[512,768]{1,0:T(8,128)(2,1)} %fusion.4.refs_0_, bf16[512,768]{1,0:T(8,128)(2,1)} %add_convert_fusion.3.refs_1_, ...), custom_call_target="tpu_custom_call" | custom-call | flops 4026531840 | bytes 10485760 | tf_op jit(solution)/shard_map/attend_backward/pallas_call | solution.py:332
  264.3 23.8 %attend_backward.3 = (bf16[4,512,768]{2,1,0:T(8,128)(2,1)}, f32[1,768]{1,0:T(1,128)}) custom-call(s32[1]{0:T(128)} %bitcast.6.lane_ref, s32[8]{0:T(128)} %get-tuple-element.162.low_ref, s32[8]{0:T(128)} %get-tuple-element.161.high_ref, bf16[512,768]{1,0:T(8,128)(2,1)} %fusion.4.refs_0_, bf16[512,768]{1,0:T(8,128)(2,1)} %add_convert_fusion.3.refs_1_, ...), custom_call_target="tpu_custom_call" | custom-call | flops 4026531840 | bytes 10485760 | tf_op jit(solution)/shard_map/attend_backward/pallas_call | solution.py:332
  288.1 3.2 fusion.6
  291.4 1.7 convolution_convert_fusion.2
  293.1 1.8 convolution_convert_fusion.1
  294.9 1.7 convolution_convert_fusion
  296.9 2.0 collective-permute-start.12
  299.0 2.0 maximum_bitcast_fusion
  301.0 2.9 copy.74
  304.0 2.4 collective-permute-start.13
  306.3 5.4 %fusion.26 = f32[8,96,768]{2,1,0:T(8,128)S(1)} fusion(bf16[8,96,2048]{2,1,0:T(8,128)(2,1)} %bitcast.93, bf16[2048,768,1]{1,0,2:T(8,128)(2,1)} %bitcast.125), kind=kOutput, calls=%fused_computation.88 | convolution fusion | flops 2415919104 | bytes 8650752 | tf_op jit(solution)/shard_map/dot_general | solution.py:30
  313.1 18.2 %reduce-scatter.3.cloned.1.call-done = bf16[4,96,1856]{2,1,0:T(8,128)(2,1)} async-done(((bf16[4,768,1856]{2,1,0:T(8,128)(2,1)}), bf16[4,96,1856]{2,1,0:T(8,128)(2,1)}) %reduce-scatter.3.cloned.1.call-update) | async-done | bytes 1425424 | tf_op jit(solution)/shard_map/reduce_scatter | solution.py:798
  332.7 3.4 collective-permute-start.11
  339.4 2.1 maximum_bitcast_fusion.1
  341.6 5.2 %collective-permute-done.15 = bf16[2,96,768]{2,1,0:T(8,128)(2,1)S(1)} collective-permute-done((bf16[2,96,768]{2,1,0:T(8,128)(2,1)}, bf16[2,96,768]{2,1,0:T(8,128)(2,1)S(1)}, u32[]{:S(2)}, u32[]{:S(2)}) %collective-permute-start.15) | collective-permute-done | bytes 294944 | tf_op jit(solution)/shard_map/ppermute | solution.py:655
  348.3 38.7 %collective-permute-done.11 = bf16[512,768]{1,0:T(8,128)(2,1)} collective-permute-done((bf16[512,768]{1,0:T(8,128)(2,1)}, bf16[512,768]{1,0:T(8,128)(2,1)}, u32[]{:S(2)}, u32[]{:S(2)}) %collective-permute-start.11) | collective-permute-done | bytes 786464 | tf_op jit(solution)/shard_map/ppermute | solution.py:713
  387.0 8.7 %collective-permute-done.10 = bf16[512,768]{1,0:T(8,128)(2,1)} collective-permute-done((bf16[512,768]{1,0:T(8,128)(2,1)}, bf16[512,768]{1,0:T(8,128)(2,1)}, u32[]{:S(2)}, u32[]{:S(2)}) %collective-permute-start.10) | collective-permute-done | bytes 786464 | tf_op jit(solution)/shard_map/ppermute | solution.py:713
  395.8 32.3 %collective-permute-done.9 = bf16[512,768]{1,0:T(8,128)(2,1)} collective-permute-done((bf16[512,768]{1,0:T(8,128)(2,1)}, bf16[512,768]{1,0:T(8,128)(2,1)}, u32[]{:S(2)}, u32[]{:S(2)}) %collective-permute-start.9) | collective-permute-done | bytes 786464 | tf_op jit(solution)/shard_map/ppermute | solution.py:713
  428.1 3.1 fusion.3
  431.9 1.7 finish_heads.1
  435.8 1.9 finish_dense.1
  437.7 2.0 slice_bitcast_fusion.1
  (157 shorter events, 35.8 us)
Async XLA Ops:
  7.2 44.6 %copy-start.13 = (s32[1,2048]{1,0:T(1,128)S(1)}, s32[1,2048]{1,0:T(1,128)}, u32[]{:S(2)}) copy-start(s32[1,2048]{1,0:T(1,128)} %refs_5_.7) | copy-start | bytes 24580
  7.2 167.5 %all-gather.3.cloned.1.call-start = ((), (), s32[]{:S(2)}) async-start(), calls=%async_computation.8 | async-start | bytes 11354112 | tf_op jit(solution)/shard_map/all_gather | solution.py:723
  12.7 29.4 %collective-permute-start = (bf16[512,768]{1,0:T(8,128)(2,1)}, bf16[512,768]{1,0:T(8,128)(2,1)S(1)}, u32[]{:S(2)}, u32[]{:S(2)}) collective-permute-start(bf16[512,768]{1,0:T(8,128)(2,1)} %bitcast.97), channel_id=1, source_target_pairs={{0,1},{1,2},{2,3},{4,5},{5,6},{6,7},{8,9},{9,10},{10,11},{12,13},{... | collective-permute-start | bytes 2359304 | tf_op jit(solution)/shard_map/ppermute | solution.py:710
  17.6 28.5 %collective-permute-start.1 = (bf16[512,768]{1,0:T(8,128)(2,1)}, bf16[512,768]{1,0:T(8,128)(2,1)S(1)}, u32[]{:S(2)}, u32[]{:S(2)}) collective-permute-start(bf16[512,768]{1,0:T(8,128)(2,1)} %bitcast.98), channel_id=1, source_target_pairs={{1,0},{2,1},{3,2},{5,4},{6,5},{7,6},{9,8},{10,9},{11,10},{13,12},{... | collective-permute-start | bytes 2359304 | tf_op jit(solution)/shard_map/ppermute | solution.py:710
  21.9 1.5 collective-permute-start.2
  46.1 33.2 %collective-permute-start.3 = (bf16[512,768]{1,0:T(8,128)(2,1)S(1)}, bf16[512,768]{1,0:T(8,128)(2,1)}, u32[]{:S(2)}, u32[]{:S(2)}) collective-permute-start(bf16[512,768]{1,0:T(8,128)(2,1)S(1)} %collective-permute-done), channel_id=1, source_target_pairs={{0,1},{1,2},{2,3},{4,5},{5,6},{6,7},{8,9},{9,10},{10,11},{12,13},{... | collective-permute-start | bytes 2359304 | tf_op jit(solution)/shard_map/ppermute | solution.py:710
  50.5 31.0 %collective-permute-start.4 = (bf16[512,768]{1,0:T(8,128)(2,1)S(1)}, bf16[512,768]{1,0:T(8,128)(2,1)S(1)}, u32[]{:S(2)}, u32[]{:S(2)}) collective-permute-start(bf16[512,768]{1,0:T(8,128)(2,1)S(1)} %collective-permute-done.1), channel_id=1, source_target_pairs={{1,0},{2,1},{3,2},{5,4},{6,5},{7,6},{9,8},{10,9},{11,10},{13,12},{... | collective-permute-start | bytes 2359304 | tf_op jit(solution)/shard_map/ppermute | solution.py:710
  52.0 16.2 %collective-permute-start.5 = (bf16[192,768]{0,1:T(8,128)(2,1)S(1)}, bf16[192,768]{0,1:T(8,128)(2,1)S(1)}, u32[]{:S(2)}, u32[]{:S(2)}) collective-permute-start(bf16[192,768]{0,1:T(8,128)(2,1)S(1)} %maximum_select_fusion.2), channel_id=1, source_target_pairs={{0,8},{4,12},{8,0},{12,4},{16,24},{20,28},{24,16},{28,20},{1,9},{5... | collective-permute-start | bytes 884744 | tf_op jit(solution)/shard_map/ppermute | solution.py:655
  68.7 64.6 %copy-start.7 = (bf16[384,768]{0,1:T(8,128)(2,1)}, bf16[384,768]{0,1:T(8,128)(2,1)S(1)}, u32[]{:S(2)}) copy-start(bf16[384,768]{0,1:T(8,128)(2,1)S(1)} %maximum_select_fusion.1) | copy-start | bytes 1769476
  81.5 26.0 %collective-permute-start.6 = (bf16[384,768]{0,1:T(8,128)(2,1)S(1)}, bf16[384,768]{0,1:T(8,128)(2,1)S(1)}, u32[]{:S(2)}, u32[]{:S(2)}) collective-permute-start(bf16[384,768]{0,1:T(8,128)(2,1)S(1)} %maximum_select_fusion.1), channel_id=1, source_target_pairs={{0,16},{4,20},{8,24},{12,28},{16,0},{20,4},{24,8},{28,12},{1,17},{... | collective-permute-start | bytes 1769480 | tf_op jit(solution)/shard_map/ppermute | solution.py:655
  83.7 37.9 %collective-permute-start.7 = (bf16[512,768]{1,0:T(8,128)(2,1)}, bf16[512,768]{1,0:T(8,128)(2,1)S(1)}, u32[]{:S(2)}, u32[]{:S(2)}) collective-permute-start(bf16[512,768]{1,0:T(8,128)(2,1)} %collective-permute-done.3), channel_id=1, source_target_pairs={{0,1},{1,2},{2,3},{4,5},{5,6},{6,7},{8,9},{9,10},{10,11},{12,13},{... | collective-permute-start | bytes 2359304 | tf_op jit(solution)/shard_map/ppermute | solution.py:710
  87.2 44.3 %collective-permute-start.8 = (bf16[512,768]{1,0:T(8,128)(2,1)S(1)}, bf16[512,768]{1,0:T(8,128)(2,1)S(1)}, u32[]{:S(2)}, u32[]{:S(2)}) collective-permute-start(bf16[512,768]{1,0:T(8,128)(2,1)S(1)} %collective-permute-done.4), channel_id=1, source_target_pairs={{1,0},{2,1},{3,2},{5,4},{6,5},{7,6},{9,8},{10,9},{11,10},{13,12},{... | collective-permute-start | bytes 2359304 | tf_op jit(solution)/shard_map/ppermute | solution.py:710
  88.6 20.7 %copy-start = (bf16[512,768]{1,0:T(8,128)(2,1)}, bf16[512,768]{1,0:T(8,128)(2,1)S(1)}, u32[]{:S(2)}) copy-start(bf16[512,768]{1,0:T(8,128)(2,1)S(1)} %broadcast_select_fusion.1) | copy-start | bytes 2359300
  88.6 20.7 %copy-start.4 = (bf16[1,512,768]{2,1,0:T(8,128)(2,1)S(1)}, bf16[1,512,768]{2,1,0:T(8,128)(2,1)}, u32[]{:S(2)}) copy-start(bf16[1,512,768]{2,1,0:T(8,128)(2,1)} %param.21) | copy-start | bytes 2359300
  107.5 25.8 %copy-start.25 = (bf16[384,768]{0,1:T(8,128)(2,1)}, bf16[384,768]{0,1:T(8,128)(2,1)S(1)}, u32[]{:S(2)}) copy-start(bf16[384,768]{0,1:T(8,128)(2,1)S(1)} %collective-permute-done.6) | copy-start | bytes 1769476
  121.7 11.6 %copy-start.1 = (bf16[512,768]{1,0:T(8,128)(2,1)}, bf16[512,768]{1,0:T(8,128)(2,1)S(1)}, u32[]{:S(2)}) copy-start(bf16[512,768]{1,0:T(8,128)(2,1)S(1)} %broadcast_select_fusion.2) | copy-start | bytes 2359300
  135.0 21.5 %copy-start.16 = (s32[1,512]{1,0:T(1,128)S(1)}, s32[1,512]{1,0:T(1,128)}, u32[]{:S(2)}) copy-start(s32[1,512]{1,0:T(1,128)} %param.23) | copy-start | bytes 6148
  135.0 22.4 %copy-start.19 = (bf16[768]{0:T(1024)(128)(2,1)S(1)}, bf16[768]{0:T(1024)(128)(2,1)}, u32[]{:S(2)}) copy-start(bf16[768]{0:T(1024)(128)(2,1)} %param.34) | copy-start | bytes 4612
  135.0 22.4 %copy-start.20 = (bf16[768]{0:T(1024)(128)(2,1)S(1)}, bf16[768]{0:T(1024)(128)(2,1)}, u32[]{:S(2)}) copy-start(bf16[768]{0:T(1024)(128)(2,1)} %param.37) | copy-start | bytes 4612
  135.0 22.4 %copy-start.21 = (bf16[768]{0:T(1024)(128)(2,1)S(1)}, bf16[768]{0:T(1024)(128)(2,1)}, u32[]{:S(2)}) copy-start(bf16[768]{0:T(1024)(128)(2,1)} %param.38) | copy-start | bytes 4612
  135.0 22.4 %copy-start.22 = (bf16[768]{0:T(1024)(128)(2,1)S(1)}, bf16[768]{0:T(1024)(128)(2,1)}, u32[]{:S(2)}) copy-start(bf16[768]{0:T(1024)(128)(2,1)} %param.36) | copy-start | bytes 4612
  135.0 22.4 %copy-start.23 = (bf16[768]{0:T(1024)(128)(2,1)S(1)}, bf16[768]{0:T(1024)(128)(2,1)}, u32[]{:S(2)}) copy-start(bf16[768]{0:T(1024)(128)(2,1)} %param.39) | copy-start | bytes 4612
  135.0 22.5 %copy-start.24 = (bf16[768]{0:T(1024)(128)(2,1)S(1)}, bf16[768]{0:T(1024)(128)(2,1)}, u32[]{:S(2)}) copy-start(bf16[768]{0:T(1024)(128)(2,1)} %param.40) | copy-start | bytes 4612
  135.0 23.1 %copy-start.17 = (bf16[3072]{0:T(1024)(128)(2,1)S(1)}, bf16[3072]{0:T(1024)(128)(2,1)}, u32[]{:S(2)}) copy-start(bf16[3072]{0:T(1024)(128)(2,1)} %param.35) | copy-start | bytes 18436
  151.1 24.7 %all-to-all-start = ((bf16[4,384,128]{2,1,0:T(8,128)(2,1)}), bf16[4,384,128]{2,1,0:T(8,128)(2,1)S(1)}, u32[]{:S(2)}, u32[]{:S(2)}) async-start(bf16[4,384,128]{2,1,0:T(8,128)(2,1)} %get-tuple-element.87.refs_6_), calls=%async_computation | async-start | bytes 786432 | tf_op jit(solution)/shard_map/all_to_all | solution.py:763
  175.7 7.1 %copy-start.9 = (bf16[4,384,128]{2,1,0:T(8,128)(2,1)}, bf16[4,384,128]{2,1,0:T(8,128)(2,1)S(1)}, u32[]{:S(2)}) copy-start(bf16[4,384,128]{2,1,0:T(8,128)(2,1)S(1)} %all-to-all-done.ctx_ref.refs_10_) | copy-start | bytes 1179652
  175.7 24.2 %all-to-all-start.1 = ((bf16[4,384,128]{2,1,0:T(8,128)(2,1)}), bf16[4,384,128]{2,1,0:T(8,128)(2,1)S(1)}, u32[]{:S(2)}, u32[]{:S(2)}) async-start(bf16[4,384,128]{2,1,0:T(8,128)(2,1)} %get-tuple-element.89.refs_6_), calls=%async_computation.1 | async-start | bytes 786432 | tf_op jit(solution)/shard_map/all_to_all | solution.py:763
  200.0 5.2 %copy-start.11 = (bf16[4,384,128]{2,1,0:T(8,128)(2,1)}, bf16[4,384,128]{2,1,0:T(8,128)(2,1)S(1)}, u32[]{:S(2)}) copy-start(bf16[4,384,128]{2,1,0:T(8,128)(2,1)S(1)} %all-to-all-done.1.ctx_ref.refs_11_) | copy-start | bytes 1179652
  200.0 23.5 %all-to-all-start.3 = ((bf16[4,384,128]{2,1,0:T(8,128)(2,1)}), bf16[4,384,128]{2,1,0:T(8,128)(2,1)S(1)}, u32[]{:S(2)}, u32[]{:S(2)}) async-start(bf16[4,384,128]{2,1,0:T(8,128)(2,1)} %get-tuple-element.93), calls=%async_computation.3 | async-start | bytes 786432 | tf_op jit(solution)/shard_map/all_to_all | solution.py:763
  205.1 16.8 %copy-start.15 = (f32[4,1,768]{2,1,0:T(1,128)S(1)}, f32[4,1,768]{2,1,0:T(1,128)}, u32[]{:S(2)}) copy-start(f32[4,1,768]{2,1,0:T(1,128)} %get-tuple-element.125) | copy-start | bytes 36868
  205.1 17.6 %copy-start.14 = (f32[8,768]{1,0:T(8,128)S(1)}, f32[8,768]{1,0:T(8,128)}, u32[]{:S(2)}) copy-start(f32[8,768]{1,0:T(8,128)} %get-tuple-element.123) | copy-start | bytes 73732
  205.1 126.2 %reduce-scatter.3.cloned.1.call-start = ((), (), s32[]{:S(2)}) async-start(), calls=%async_computation.6 | async-start | bytes 13271040 | tf_op jit(solution)/shard_map/reduce_scatter | solution.py:798
  223.5 13.6 %copy-start.10 = (bf16[4,384,128]{2,1,0:T(8,128)(2,1)}, bf16[4,384,128]{2,1,0:T(8,128)(2,1)S(1)}, u32[]{:S(2)}) copy-start(bf16[4,384,128]{2,1,0:T(8,128)(2,1)S(1)} %all-to-all-done.3.refs_7_) | copy-start | bytes 1179652
  237.2 26.4 %all-to-all-start.2 = ((bf16[4,384,128]{2,1,0:T(8,128)(2,1)}), bf16[4,384,128]{2,1,0:T(8,128)(2,1)S(1)}, u32[]{:S(2)}, u32[]{:S(2)}) async-start(bf16[4,384,128]{2,1,0:T(8,128)(2,1)} %get-tuple-element.91), calls=%async_computation.2 | async-start | bytes 786432 | tf_op jit(solution)/shard_map/all_to_all | solution.py:763
  242.2 193.5 %reduce-scatter.5.cloned.1.call-start = ((), (), s32[]{:S(2)}) async-start(), calls=%async_computation.7 | async-start | bytes 1843200 | tf_op jit(solution)/shard_map/reduce_scatter | solution.py:821
  264.3 23.8 %copy-start.8 = (bf16[384,768]{0,1:T(8,128)(2,1)S(1)}, bf16[384,768]{0,1:T(8,128)(2,1)}, u32[]{:S(2)}) copy-start(bf16[384,768]{0,1:T(8,128)(2,1)} %copy-done.7) | copy-start | bytes 1769476
  264.3 23.8 %copy-start.26 = (bf16[384,768]{0,1:T(8,128)(2,1)S(1)}, bf16[384,768]{0,1:T(8,128)(2,1)}, u32[]{:S(2)}) copy-start(bf16[384,768]{0,1:T(8,128)(2,1)} %copy-done.25) | copy-start | bytes 1769476
  296.9 7.0 %collective-permute-start.12 = (f32[1,384]{1,0:T(1,128)S(1)}, f32[1,384]{1,0:T(1,128)S(1)}, u32[]{:S(2)}, u32[]{:S(2)}) collective-permute-start(f32[1,384]{1,0:T(1,128)S(1)} %pad_maximum_fusion.3), channel_id=1, source_target_pairs={{0,1},{1,0},{2,3},{3,2},{4,5},{5,4},{6,7},{7,6},{8,9},{9,8},{10,11... | collective-permute-start | bytes 4616 | tf_op jit(solution)/shard_map/ppermute | solution.py:655
  304.0 7.8 %collective-permute-start.13 = (f32[2,384]{1,0:T(2,128)S(1)}, f32[2,384]{1,0:T(2,128)S(1)}, u32[]{:S(2)}, u32[]{:S(2)}) collective-permute-start(f32[2,384]{1,0:T(2,128)S(1)} %maximum_select_fusion.4), channel_id=1, source_target_pairs={{0,2},{1,3},{2,0},{3,1},{4,6},{5,7},{6,4},{7,5},{8,10},{9,11},{10,... | collective-permute-start | bytes 9224 | tf_op jit(solution)/shard_map/ppermute | solution.py:655
  332.6 4.6 %collective-permute-start.14 = (bf16[4,96,768]{2,1,0:T(8,128)(2,1)S(1)}, bf16[4,96,768]{2,1,0:T(8,128)(2,1)S(1)}, u32[]{:S(2)}, u32[]{:S(2)}) collective-permute-start(bf16[4,96,768]{2,1,0:T(8,128)(2,1)S(1)} %dynamic-slice_bitcast_fusion), channel_id=1, source_target_pairs={{0,4},{4,0},{8,12},{12,8},{16,20},{20,16},{24,28},{28,24},{1,5},{5... | collective-permute-start | bytes 1769480 | tf_op jit(solution)/shard_map/ppermute | solution.py:655
  332.7 54.4 %collective-permute-start.11 = (bf16[512,768]{1,0:T(8,128)(2,1)}, bf16[512,768]{1,0:T(8,128)(2,1)}, u32[]{:S(2)}, u32[]{:S(2)}) collective-permute-start(bf16[512,768]{1,0:T(8,128)(2,1)} %convolution_convert_fusion), channel_id=1, source_target_pairs={{0,3},{1,0},{2,1},{3,2},{4,7},{5,4},{6,5},{7,6},{8,11},{9,8},{10,9... | collective-permute-start | bytes 2359304 | tf_op jit(solution)/shard_map/ppermute | solution.py:713
  336.0 59.7 %collective-permute-start.10 = (bf16[512,768]{1,0:T(8,128)(2,1)}, bf16[512,768]{1,0:T(8,128)(2,1)}, u32[]{:S(2)}, u32[]{:S(2)}) collective-permute-start(bf16[512,768]{1,0:T(8,128)(2,1)} %convolution_convert_fusion.1), channel_id=1, source_target_pairs={{0,1},{1,2},{2,3},{3,0},{4,5},{5,6},{6,7},{7,4},{8,9},{9,10},{10,1... | collective-permute-start | bytes 2359304 | tf_op jit(solution)/shard_map/ppermute | solution.py:713
  336.0 92.1 %collective-permute-start.9 = (bf16[512,768]{1,0:T(8,128)(2,1)}, bf16[512,768]{1,0:T(8,128)(2,1)}, u32[]{:S(2)}, u32[]{:S(2)}) collective-permute-start(bf16[512,768]{1,0:T(8,128)(2,1)} %convolution_convert_fusion.2), channel_id=1, source_target_pairs={{0,2},{1,3},{2,0},{3,1},{4,6},{5,7},{6,4},{7,5},{8,10},{9,11},{10,... | collective-permute-start | bytes 2359304 | tf_op jit(solution)/shard_map/ppermute | solution.py:713
  337.3 90.8 %copy-start.3 = (f32[512,768]{1,0:T(8,128)S(1)}, f32[512,768]{1,0:T(8,128)}, u32[]{:S(2)}) copy-start(f32[512,768]{1,0:T(8,128)} %fusion.6) | copy-start | bytes 4718596
  337.3 90.8 %copy-start.5 = (f32[256,768]{1,0:T(8,128)S(1)}, f32[256,768]{1,0:T(8,128)}, u32[]{:S(2)}) copy-start(f32[256,768]{1,0:T(8,128)} %get-tuple-element.130) | copy-start | bytes 2359300
  338.1 8.7 %collective-permute-start.15 = (bf16[2,96,768]{2,1,0:T(8,128)(2,1)}, bf16[2,96,768]{2,1,0:T(8,128)(2,1)S(1)}, u32[]{:S(2)}, u32[]{:S(2)}) collective-permute-start(bf16[2,96,768]{2,1,0:T(8,128)(2,1)} %dynamic-slice_bitcast_fusion.1), channel_id=1, source_target_pairs={{0,8},{4,12},{8,0},{12,4},{16,24},{20,28},{24,16},{28,20},{1,9},{5... | collective-permute-start | bytes 884744 | tf_op jit(solution)/shard_map/ppermute | solution.py:655
  339.4 88.7 %copy-start.6 = (f32[256,768]{1,0:T(8,128)S(1)}, f32[256,768]{1,0:T(8,128)}, u32[]{:S(2)}) copy-start(f32[256,768]{1,0:T(8,128)} %get-tuple-element.131) | copy-start | bytes 2359300
  346.9 84.4 %collective-permute-start.16 = (bf16[1,96,768]{2,1,0:T(8,128)(2,1)S(1)}, bf16[1,96,768]{2,1,0:T(8,128)(2,1)S(1)}, u32[]{:S(2)}, u32[]{:S(2)}) collective-permute-start(bf16[1,96,768]{2,1,0:T(8,128)(2,1)S(1)} %constant_dynamic-slice_fusion), channel_id=1, source_target_pairs={{0,16},{4,20},{8,24},{12,28},{16,0},{20,4},{24,8},{28,12},{1,17},{... | collective-permute-start | bytes 442376 | tf_op jit(solution)/shard_map/ppermute | solution.py:655
  (4 other events, 7.5 us)
Sparse Core Ops, SparseCore 0:
  12.8 123.4 all-gather.2
  237.3 93.9 reduce-scatter.2
  333.8 64.5 reduce-scatter.4

commit v8 on v7

--- a/solution.py
+++ b/solution.py
@@ -76,7 +76,7 @@
 def attend_forward(
     which, lane_ref, low_ref, high_ref, *refs
 ):
-    chunk_refs, (seg_col_ref, seg_row_ref, ctx_ref, lse_ref, held, qkv_ref, sems) = refs[:4], refs[4:]
+    chunk_refs, (seg_col_ref, seg_row_ref, ctx_ref, lse_ref, held, qkv_ref, sems) = refs[:-7], refs[-7:]
     halves, half = which
     heads = lse_ref.shape[0]
 
@@ -137,10 +137,10 @@
     )
 
 
-def attend_backward(which, lane_ref, low_ref, high_ref, *refs):
+def attend_backward(which, chunks, lane_ref, low_ref, high_ref, *refs):
     halves, half = which
     last = half == halves - 1
-    chunk_refs, refs = refs[:4], refs[4:]
+    chunk_refs, refs = refs[:chunks], refs[chunks:]
     (seg_col_ref, seg_row_ref, ctx_ref, grad_ref, lse_ref), refs = refs[:5], refs[5:]
     earlier, refs = refs[:half], refs[half:]
     if half > 0:
@@ -271,7 +271,7 @@
         grid_spec=pltpu.PrefetchScalarGridSpec(
             num_scalar_prefetch=3,
             grid=(steps,),
-            in_specs=[pl.BlockSpec(memory_space=pl.ANY)] * 4
+            in_specs=[pl.BlockSpec(memory_space=pl.ANY)] * len(qkv)
             + [
                 pl.BlockSpec((BLOCK, 1), lambda q, *_: (q * halves + half, 0)),
                 pl.BlockSpec((1, seq_len), lambda q, *_: (0, 0)),
@@ -283,7 +283,7 @@
             scratch_shapes=[
                 pltpu.VMEM((heads, blocks, BLOCK, BLOCK), F32),
                 pltpu.VMEM((seq_len, width), BF16),
-                pltpu.SemaphoreType.DMA((4,)),
+                pltpu.SemaphoreType.DMA((len(qkv),)),
             ],
         ),
         compiler_params=pltpu.CompilerParams(
@@ -312,10 +312,10 @@
     gathered = (heads, seq_len, 2 * DH)
     carried = [fixed(value.shape, **once) for value in earlier]
     carried += [fixed(gathered, **once)] * len(before)
-    scratch = [pltpu.VMEM((seq_len, width), BF16), pltpu.SemaphoreType.DMA((4,))]
+    scratch = [pltpu.VMEM((seq_len, width), BF16), pltpu.SemaphoreType.DMA((len(qkv),))]
     if half == halves - 1:
         out_shape = (
-            jax.ShapeDtypeStruct((4, seq_len // 4, width), BF16),
+            jax.ShapeDtypeStruct((len(qkv), seq_len // len(qkv), width), BF16),
             jax.ShapeDtypeStruct((1, width), F32),
         )
         out_specs = (pl.BlockSpec(memory_space=pl.ANY), fixed((1, width)))
@@ -330,12 +330,12 @@
             pl.BlockSpec((1, BLOCK, heads * 2 * DH), lambda q, *_: (q, 0, 0)),
         )
     return pl.pallas_call(
-        functools.partial(attend_backward, which),
+        functools.partial(attend_backward, which, len(qkv)),
         out_shape=out_shape,
         grid_spec=pltpu.PrefetchScalarGridSpec(
             num_scalar_prefetch=3,
             grid=(steps,),
-            in_specs=[pl.BlockSpec(memory_space=pl.ANY)] * 4
+            in_specs=[pl.BlockSpec(memory_space=pl.ANY)] * len(qkv)
             + [
                 fixed((seq_len, 1)),
                 pl.BlockSpec((1, BLOCK), lambda q, *_: (0, q * halves + half)),
@@ -379,8 +379,8 @@
     for group, (start, size, target) in enumerate(groups):
         for piece, marked in zip(pieces, marks):
             block = piece.shape[1]
-            for at, (slot, turn) in enumerate(marked):
-                offset = pl.multiple_of((index ^ turn) * block, block)
+            for at, (slot, turn, relative) in enumerate(marked):
+                offset = pl.multiple_of((index ^ turn) * block, block) if relative else turn * block
                 pltpu.make_async_copy(
                     piece.at[at, :, pl.ds(start, size)],
                     target.at[slot, pl.ds(offset, block), :],
@@ -516,7 +516,7 @@
     )(place, ratio, ctx, rows_in, teacher, cotangent, valid, vecs, inner_bias, *pieces)
 
 
-def dense_weights(turns, halves, place_ref, *refs):
+def dense_weights(plans, halves, place_ref, *refs):
     firsts, branch_grads, attn_grads, acts, hidden_grads, ctxs = (
         refs[k * halves : (k + 1) * halves] for k in range(6)
     )
@@ -524,8 +524,6 @@
     turned, whole, sems = refs[-3:]
     step = pl.program_id(0)
     slots = whole.shape[0]
-    teams = len(outs) // len(turns)
-    each = slots // teams
 
     @pl.when(step == 0)
     def _():
@@ -543,19 +541,20 @@
     plain = 2 * hidden_cols + ctx.shape[1]
     whole[step, :, 2 * hidden_cols : plain] = dot(turned[2], ctx).astype(BF16)
     whole[step, :, plain : plain + notes_ref.shape[1]] = notes_ref[...]
-    for team in range(teams):
-
-        @pl.when(step // each == team)
+    for out, (start, stop, turns) in zip(outs, plans):
+
+        @pl.when((step >= start) & (step < stop))
         def _():
-            for out, orders in zip(outs[team * len(turns) : (team + 1) * len(turns)], turns):
-                block = out.shape[1]
-                for at, turn in enumerate(orders[team]):
+            block = out.shape[1]
+            for at, turn in enumerate(turns):
+                offset = 0
+                if block < whole.shape[1]:
                     offset = pl.multiple_of((place_ref[slots] ^ turn) * block, block)
-                    pltpu.make_async_copy(
-                        whole.at[step, pl.ds(offset, block), :],
-                        out.at[at * each + step - team * each],
-                        sems.at[step],
-                    ).start()
+                pltpu.make_async_copy(
+                    whole.at[step, pl.ds(offset, block), :],
+                    out.at[at * (stop - start) + step - start],
+                    sems.at[step],
+                ).start()
 
     @pl.when(step == slots - 1)
     def _():
@@ -563,7 +562,7 @@
             pltpu.make_async_copy(whole.at[slot], whole.at[slot], sems.at[slot]).wait()
 
 
-def run_weights(turns, teams, block, place, notes, firsts, branch_grads, attn_grads, acts, hidden_grads, ctxs):
+def run_weights(plans, place, notes, firsts, branch_grads, attn_grads, acts, hidden_grads, ctxs):
     parts, _, hidden_cols = acts[0].shape
     halves = len(acts)
     width = firsts[0].shape[1]
@@ -574,10 +573,12 @@
 
     fixed = pl.BlockSpec((BLOCK, width), lambda s, place: (0, 0))
     outs = tuple(
-        jax.ShapeDtypeStruct((len(orders[0]) * parts // teams, block, columns), BF16) for orders in turns
-    ) * teams
+        jax.ShapeDtypeStruct((len(turns) * (stop - start), block, columns), BF16)
+        for start, stop, block, turns in plans
+    )
+    inner = tuple((start, stop, turns) for start, stop, _, turns in plans)
     return pl.pallas_call(
-        functools.partial(dense_weights, turns, halves),
+        functools.partial(dense_weights, inner, halves),
         out_shape=outs,
         grid_spec=pltpu.PrefetchScalarGridSpec(
             num_scalar_prefetch=1,
@@ -675,6 +676,14 @@
 
 def add_low(left_side, right_side):
     return (left_side.astype(F32) + right_side.astype(F32)).astype(BF16)
+
+
+def add_halves(left_side, right_side):
+    half = left_side.shape[0] // 2
+    return (
+        add_low(left_side[:half], right_side[:half]),
+        add_low(left_side[half:], right_side[half:]),
+    )
 
 
 def scatter_rows(held):
@@ -706,11 +715,10 @@
     shard_rows = w_inner.shape[0]
     halves = part_len // BLOCK
 
-    def shift(value, by):
-        return lax.ppermute(value, "tensor", [(i, i + by) for i in range(parts) if 0 <= i + by < parts])
-
-    def turn(value, by):
-        return lax.ppermute(value, "tensor", [(i, (i + by) % parts) for i in range(parts)])
+    rows_in = inputs.reshape(part_len, width)
+    tokens = lax.all_gather(rows_in, "tensor", axis=0, tiled=True)
+    w_heads = interleave(w_query, w_key, w_value, heads)
+    paired = shard_rows % 16 == 0 and parts == 4 and copies == 8
 
     valid_rows = valid_mask.astype(F32).reshape(part_len, 1)
     valid_count = jnp.sum(valid_mask.astype(F32))
@@ -720,38 +728,31 @@
     )
     count_row = jnp.where(spot == 0, upper, jnp.where(spot == 1, valid_count - 256.0 * upper, 0.0))
     mine = jnp.concatenate((w_inner, w_outer.T, w_output.T, count_row.astype(BF16)), axis=1)
-    weights = lax.all_gather(mine, ("tensor", "dp"), axis=0, tiled=False)
-    counts = weights[:, 0, -DH : 2 - DH].astype(F32)
-    counted = 256.0 * jnp.sum(counts[:, 0]) + jnp.sum(counts[:, 1])
-    ratio = (total_tokens / counted).reshape(1)
-    pieces = [weights.reshape(parts, width, -1)]
-    marks = [[(t, 0) for t in range(parts)]]
-    place = jnp.asarray(list(range(parts)) + [0], jnp.int32)
-
-    rows_in = inputs.reshape(part_len, width)
-    ahead, behind = [], []
-    up, down = rows_in, rows_in
-    w_heads = interleave(w_query, w_key, w_value, heads)
-    steps = list(bits_of("dp"))
-    for step in range(parts - 1):
-        up, down = shift(up, 1), shift(down, -1)
-        behind.append(up)
-        ahead.append(down)
-        if step < len(steps):
-            w_heads = merge(w_heads, swap(w_heads, "dp", steps[step]), "dp", steps[step])
-        if step < parts - 2:
-            up, down, w_heads = lax.optimization_barrier((up, down, w_heads))
-    for bit in steps[parts - 1 :]:
-        w_heads = merge(w_heads, swap(w_heads, "dp", bit), "dp", bit)
-    tokens = [rows_in] + [
-        jnp.where(rank + by < parts, ahead[by - 1], behind[parts - by - 1]) for by in range(1, parts)
-    ]
+    if paired:
+        place = jnp.stack([rank, rank ^ 1, rank ^ 2, rank ^ 3, lax.axis_index("dp")]).astype(jnp.int32)
+        pair = jnp.concatenate([mine[None], swap(mine[None], "tensor", 1)], axis=0)
+        near = pair
+        w_heads = merge(w_heads, swap(w_heads, "dp", 1), "dp", 1)
+        turns = [0]
+        for bit in (2, 4):
+            turns = turns + [turn ^ bit for turn in turns]
+            near = jnp.concatenate([near, swap(near, "dp", bit)], axis=0)
+            w_heads = merge(w_heads, swap(w_heads, "dp", bit), "dp", bit)
+            near, w_heads = lax.optimization_barrier((near, w_heads))
+        near_other = swap(near, "dp", 1)
+        tokens, pair = lax.optimization_barrier((tokens, pair))
+        far = swap(pair, "tensor", 2)
+    else:
+        place = jnp.asarray(list(range(parts)) + [0], jnp.int32)
+        weights = lax.all_gather(mine, ("tensor", "dp"), axis=0, tiled=False)
+        for bit in bits_of("dp"):
+            w_heads = merge(w_heads, swap(w_heads, "dp", bit), "dp", bit)
 
     mine_cols = rank * head_cols
     query_shift = lax.dynamic_slice_in_dim(query_bias, mine_cols, head_cols).astype(F32)
     value_shift = lax.dynamic_slice_in_dim(value_bias, mine_cols, head_cols).astype(F32)
     shifts = interleave(query_shift[None], jnp.zeros_like(query_shift)[None], value_shift[None], heads)
-    qkv = [(dot(chunk, w_heads) + shifts).astype(BF16) for chunk in tokens]
+    qkv = [(dot(tokens, w_heads) + shifts).astype(BF16)]
 
     segment_row = segment_ids.reshape(seq_len)
     bounds = document_blocks(segment_row)
@@ -764,10 +765,27 @@
 
     contexts, lses, arrived = [], [], []
     for half in range(halves):
+        if paired and half == halves - 1:
+            bounds, far = lax.optimization_barrier((bounds, after(far, contexts[0])))
+            weights = lax.all_gather(far, "dp", axis=0, tiled=False)
         context, lse = run_forward((halves, half), lane, bounds, qkv, seg_col, seg_row)
+        if paired and half == halves - 1:
+            context, near_other = lax.optimization_barrier((context, near_other))
         contexts.append(context)
         lses.append(lse)
         arrived.append(exchange(context))
+    if paired:
+        weights = weights.reshape((copies * 2,) + mine.shape)
+        pieces = [near, near_other, weights]
+        marks = [[(slot, turn ^ flip, True) for turn in turns for slot in (0, 1)] for flip in (0, 1)]
+        marks.append([(2 + at % 2, at // 2, False) for at in range(2 * copies)])
+    else:
+        pieces = [weights.reshape(parts, width, -1)]
+        marks = [[(t, 0, False) for t in range(parts)]]
+    counts = [piece.reshape((-1,) + mine.shape)[:, 0, -DH : 2 - DH].astype(F32) for piece in pieces + [weights]]
+    counts = jnp.concatenate(counts[:-1] if paired else counts[-1:], axis=0)
+    counted = 256.0 * jnp.sum(counts[:, 0]) + jnp.sum(counts[:, 1])
+    ratio = (total_tokens / counted).reshape(1)
 
     vecs = jnp.stack(
         (output_bias, gain_attn, shift_attn, outer_bias, gain_ffn, shift_ffn, outer_bias, outer_bias)
@@ -794,11 +812,29 @@
     notes = jnp.concatenate((dense_sums.reshape(-1), inner_sums.reshape(-1))).astype(BF16)
     room = -(-notes.shape[0] // (shard_rows * 128)) * 128
     notes = jnp.pad(notes, (0, shard_rows * room - notes.shape[0])).reshape(shard_rows, room)
-    (packed,) = run_weights(([[0]],), 1, width, place, jnp.tile(notes, (copies, 1)), *sources)
-    packed = lax.psum_scatter(packed, "dp", scatter_dimension=1, tiled=True)
+    notes = jnp.tile(notes, (copies, 1))
+    if paired:
+        keep_turns = (0, 4, 2, 6)
+        plans = (
+            (0, 2, shard_rows, keep_turns),
+            (0, 2, shard_rows, tuple(turn | 1 for turn in keep_turns)),
+            (2, 4, width, (0,)),
+        )
+        keep, send, distant = run_weights(plans, place, notes, *sources)
+        keep, send = (value.reshape((4, 2) + value.shape[1:]) for value in (keep, send))
+        distant = lax.psum_scatter(distant, "dp", scatter_dimension=1, tiled=True)
+        came = swap(send, "dp", 1)
+    else:
+        (packed,) = run_weights(((0, parts, width, (0,)),), place, notes, *sources)
+        packed = lax.psum_scatter(packed, "dp", scatter_dimension=1, tiled=True)
 
     earlier, before = [], []
     for half in range(halves):
+        if paired and half == halves - 1:
+            came, before, head_grads[-1] = lax.optimization_barrier((came, before, head_grads[-1]))
+            keep, send = add_halves(keep, came)
+            keep, send, before = lax.optimization_barrier((keep, send, before))
+            came = swap(send, "dp", 2)
         results = run_backward(
             (halves, half), lane, bounds, qkv, seg_col, seg_row, contexts[half], head_grads[half],
             lses[half], earlier, before,
@@ -806,18 +842,27 @@
         if half < halves - 1:
             before, earlier = [results[0]], earlier + [results[1]]
     joined_grad, sums = results
-    away = [dot(joined_grad[by], w_heads, NT).astype(BF16) for by in (2, 1, 3)]
-    own_share = dot(joined_grad[0], w_heads, NT)
-    away, own_share, sums, joined_grad = lax.optimization_barrier((away, own_share, sums, joined_grad))
-    came = [turn(share, by) for share, by in zip(away, (2, 1, 3))]
+    joined_grad = joined_grad.reshape(seq_len, -1)
+    if paired:
+        came, joined_grad = lax.optimization_barrier((came, joined_grad))
+    attn_back = dot(joined_grad, w_heads, NT).astype(BF16)
+    attn_back, sums, joined_grad = lax.optimization_barrier((attn_back, sums, joined_grad))
+    attn_back = lax.psum_scatter(attn_back, "tensor", scatter_dimension=0, tiled=True)
+    if paired:
+        keep, send = add_halves(keep, came)
+        keep, send, joined_grad = lax.optimization_barrier((keep, send, joined_grad))
+        came = swap(send, "dp", 4)
     sums = sums.reshape(heads, 4, DH)
     sums = jnp.concatenate((sums[:, 0].reshape(1, head_cols), sums[:, 3].reshape(1, head_cols)), axis=1)
     for bit in bits_of("tensor"):
         sums = merge(sums, swap(sums, "tensor", bit), "tensor", bit)
-    head_weights = dot(
-        jnp.concatenate(tokens, axis=0), joined_grad.reshape(seq_len, -1), TN
-    ).reshape((copies, shard_rows, -1))
-    head_weights, packed = lax.optimization_barrier((head_weights, packed))
+    head_weights = dot(tokens, joined_grad, TN).reshape((copies, shard_rows, -1))
+    if paired:
+        came, head_weights = lax.optimization_barrier((came, head_weights))
+        slots = jnp.concatenate([add_low(keep, came)[0], distant], axis=0)
+        packed = jnp.stack(
+            [lax.dynamic_index_in_dim(slots, rank ^ t, 0, keepdims=False) for t in range(parts)]
+        )
     packed = lax.psum_scatter(packed, "tensor", scatter_dimension=0, tiled=True)[0]
     biases = jnp.concatenate((sums[:, :head_cols].reshape(-1), sums[:, head_cols:].reshape(-1)))
     biases = jnp.pad(
@@ -827,9 +872,7 @@
         scatter_rows((head_weights + biases).astype(BF16))
     )
     biases = biases.reshape(2, width)
-    input_grad = own_share + jnp.concatenate(first_grads, axis=0)
-    for share in came:
-        input_grad = input_grad + share.astype(F32)
+    input_grad = jnp.concatenate(first_grads, axis=0) + attn_back.astype(F32)
 
     inner_grad, outer_grad, output_grad, notes = run_finish_dense(packed, hidden_cols, head_cols)
     notes = notes.reshape(-1)

time: 451 us -> 433 us (0.960)
  waiting for transfers between devices: 191 us -> 166 us
  starting transfers between devices: 52.2 us -> 35.1 us
  Pallas kernels: 127 us -> 143 us
  other arithmetic: 19.1 us -> 29.8 us
    ppermute x9 -> x0, waiting for transfers between devices: 135 us -> none  [the longest x3 79.8 us: turn(): lax.ppermute(value, 'tensor', [(i, (i + by) % parts) for i in range(parts)])]
    ppermute x8 -> x16, waiting for transfers between devices: 37.7 us -> 103 us  [swap(): return lax.ppermute(value, axis, [(i, i ^ bit) for i in range(size)])]
    reduce_scatter x1, waiting for transfers between devices: 0.01 us -> 33.5 us  [local(): lax.psum_scatter(packed, 'tensor', scatter_dimension=0, tiled=True)[0]]
    ppermute x9 -> x0, starting transfers between devices: 21.1 us -> none  [the longest x6 16.6 us: shift(): lax.ppermute(value, 'tensor', [(i, i + by) for i in range(parts) if 0 <=...]
    all_gather x1 -> x2, waiting for transfers between devices: 0.02 us -> 17.5 us  [the longest x1 17.4 us: local(): weights = lax.all_gather(far, 'dp', axis=0, tiled=False)]
    pallas_call x3, Pallas kernels: 57.9 us -> 67.4 us  [the longest x2 54.5 us: run_backward(): pl.pallas_call(functools.partial(attend_backward, which, len(qkv)), out_s...]
    reduce_scatter x1 -> x2, waiting for transfers between devices: 18.2 us -> 11.7 us  [the longest x1 11.7 us: local(): lax.psum_scatter(attn_back, 'tensor', scatter_dimension=0, tiled=True)]
    convert_element_type x2 -> x4, other arithmetic: 0.23 us -> 6.11 us  [add_low(): return (left_side.astype(F32) + right_side.astype(F32)).astype(BF16)]
  transfers between devices with their start and end apart: 24 -> 25, of which waited for: 14 -> 12; matrix products, arithmetic and copies ran while one was open for 11% -> 14% of each run, Pallas kernels for 25% -> 30%
where the time goes in v8:
time: 433 us; the launch traced here: 431 us
  waiting for transfers between devices  166 us (38%)
  Pallas kernels  143 us (33%)
  starting transfers between devices  35.1 us (8%)
  other arithmetic  29.8 us (7%)
  matrix products  19.7 us (5%)
  between operations  18.9 us (4%)
  local copies, waits for them, and re-layouts  18.8 us (4%)
    ppermute x16, waiting for transfers between devices, swap(): return lax.ppermute(value, axis, [(i, i ^ bit) for i in range(size)])  103 us
    pallas_call x2, Pallas kernels, run_backward(): pl.pallas_call(functools.partial(attend_backward, which, len(qkv)), out_s...  54.5 us
    pallas_call x2, Pallas kernels, run_forward(): pl.pallas_call(functools.partial(attend_forward, which), out_shape=(jax.S...  37 us
    pallas_call x2, Pallas kernels, run_dense(): pl.pallas_call(functools.partial(dense_chain, marks), out_shape=out_shape...  34.8 us
    reduce_scatter x1, waiting for transfers between devices, local(): lax.psum_scatter(packed, 'tensor', scatter_dimension=0, tiled=True)[0]  33.5 us
    dot_general x3, matrix products, dot(): lax.dot_general(left_side, right_side, dims, preferred_element_type=F32)  19.7 us
    all_to_all x4, starting transfers between devices, exchange(): return lax.all_to_all(packed_blocks, 'tensor', 0, 0)  19.1 us
    all_gather x1, waiting for transfers between devices, local(): weights = lax.all_gather(far, 'dp', axis=0, tiled=False)  17.4 us
  transfers between devices with their start and end apart: 25, of which 12 were waited for; matrix products, arithmetic and copies ran while one was open for 14% of the time, Pallas kernels for 30%

profile of v8, /device:TPU:0, one launch (start us, length us, event | category | flops | bytes accessed | tf_op | source)
XLA Modules:
  0.0 431.3 jit_solution(12096474160645012094)
XLA Ops:
  8.9 1.3 convert_reduce_fusion.3
  12.7 3.1 collective-permute-start
  16.4 9.9 %collective-permute-done = bf16[1,96,1792]{2,1,0:T(8,128)(2,1)S(1)} collective-permute-done((bf16[1,96,1792]{2,1,0:T(8,128)(2,1)S(1)}, bf16[1,96,1792]{2,1,0:T(8,128)(2,1)S(1)}, u32[]{:S(2)}, u32[]{:S(2)}) %collective-permute-start) | collective-permute-done | bytes 344096 | tf_op jit(solution)/shard_map/ppermute | solution.py:656
  26.4 2.2 collective-permute-start.1
  29.0 20.1 %collective-permute-done.3 = bf16[192,768]{0,1:T(8,128)(2,1)} collective-permute-done((bf16[192,768]{0,1:T(8,128)(2,1)S(1)}, bf16[192,768]{0,1:T(8,128)(2,1)}, u32[]{:S(2)}, u32[]{:S(2)}) %collective-permute-start.3) | collective-permute-done | bytes 294944 | tf_op jit(solution)/shard_map/ppermute | solution.py:656
  49.1 1.6 maximum_select_fusion.1
  50.9 1.4 collective-permute-start.4
  54.4 1.4 copy.100.refs_1_
  56.5 35.1 %collective-permute-done.5 = bf16[384,768]{0,1:T(8,128)(2,1)} collective-permute-done((bf16[384,768]{0,1:T(8,128)(2,1)S(1)}, bf16[384,768]{0,1:T(8,128)(2,1)}, u32[]{:S(2)}, u32[]{:S(2)}) %collective-permute-start.5) | collective-permute-done | bytes 589856 | tf_op jit(solution)/shard_map/ppermute | solution.py:656
  91.6 2.5 maximum_select_fusion
  94.2 1.8 pad_maximum_fusion.refs_0_
  95.9 6.6 %add_convert_fusion.refs_0_ = bf16[2048,768]{1,0:T(8,128)(2,1)} fusion(bf16[2048,768]{1,0:T(8,128)(2,1)} %bitcast.112, bf16[768,768]{0,1:T(8,128)(2,1)} %maximum_select_fusion, f32[768]{0:T(1024)S(1)} %add.123), kind=kOutput, calls=%fused_computation | convolution fusion | flops 2419064832 | bytes 7474176 | tf_op jit(solution)/shard_map/dot_general | solution.py:30
  102.5 19.8 %attend_forward.2 = (bf16[4,384,128]{2,1,0:T(8,128)(2,1)}, f32[3,1,1024]{2,1,0:T(1,128)}) custom-call(s32[1]{0:T(128)} %bitcast.lane_ref, s32[8]{0:T(128)} %get-tuple-element.106.low_ref, s32[8]{0:T(128)} %get-tuple-element.107.high_ref, bf16[2048,768]{1,0:T(8,128)(2,1)} %add_convert_fusion.refs_0_, s32[2048,1]{1,0:T(8,128)} %copy.100.refs_1_, s32[1,2048]{1,0:T(1,128)} %refs_2_.7), custom_call_target="tpu_custom_call" | custom-call | flops 1610612736 | bytes 5242880 | tf_op jit(solution)/shard_map/attend_forward/pallas_call | solution.py:265
  122.4 1.6 collective-permute-done.6
  124.9 4.3 all-to-all-start
  132.3 17.2 %attend_forward.3 = (bf16[4,384,128]{2,1,0:T(8,128)(2,1)}, f32[3,1,1024]{2,1,0:T(1,128)}) custom-call(s32[1]{0:T(128)} %bitcast.lane_ref, s32[8]{0:T(128)} %get-tuple-element.106.low_ref, s32[8]{0:T(128)} %get-tuple-element.107.high_ref, bf16[2048,768]{1,0:T(8,128)(2,1)} %add_convert_fusion.refs_0_, s32[2048,1]{1,0:T(8,128)} %copy.100.refs_1_, s32[1,2048]{1,0:T(1,128)} %refs_2_.7), custom_call_target="tpu_custom_call" | custom-call | flops 1610612736 | bytes 5242880 | tf_op jit(solution)/shard_map/attend_forward/pallas_call | solution.py:265
  150.4 17.4 %all-gather.7.cloned.1.call-done.refs_2_ = bf16[16,96,1792]{2,1,0:T(8,128)(2,1)} async-done(((bf16[2,96,1792]{2,1,0:T(8,128)(2,1)}), bf16[16,96,1792]{2,1,0:T(8,128)(2,1)}) %all-gather.7.cloned.1.call-update) | async-done | bytes 5505040 | tf_op jit(solution)/shard_map/all_gather | solution.py:770
  168.8 4.6 %all-to-all-start.1 = ((bf16[4,384,128]{2,1,0:T(8,128)(2,1)}), bf16[4,384,128]{2,1,0:T(8,128)(2,1)S(1)}, u32[]{:S(2)}, u32[]{:S(2)}) async-start(bf16[4,384,128]{2,1,0:T(8,128)(2,1)} %get-tuple-element.112.refs_3_), calls=%async_computation.1 | async-start | bytes 786432 | tf_op jit(solution)/shard_map/all_to_all | solution.py:764
  175.4 17.4 %dense_chain.2 = (bf16[256,768]{1,0:T(8,128)(2,1)}, f32[256,768]{1,0:T(8,128)}, bf16[4,384,128]{2,1,0:T(8,128)(2,1)}, bf16[256,768]{1,0:T(8,128)(2,1)}, bf16[256...) custom-call(s32[5]{0:T(128)} %stack.53.place_ref, ...), custom_call_target="tpu_custom_call" | custom-call | flops 5637144576 | bytes 18874368 | tf_op jit(solution)/shard_map/dense_chain/pallas_call | solution.py:483
  192.8 5.1 %all-to-all-start.2 = ((bf16[4,384,128]{2,1,0:T(8,128)(2,1)}), bf16[4,384,128]{2,1,0:T(8,128)(2,1)S(1)}, u32[]{:S(2)}, u32[]{:S(2)}) async-start(bf16[4,384,128]{2,1,0:T(8,128)(2,1)} %get-tuple-element.114), calls=%async_computation.2 | async-start | bytes 786432 | tf_op jit(solution)/shard_map/all_to_all | solution.py:764
  198.0 17.4 %dense_chain.3 = (bf16[256,768]{1,0:T(8,128)(2,1)}, f32[256,768]{1,0:T(8,128)}, bf16[4,384,128]{2,1,0:T(8,128)(2,1)}, bf16[256,768]{1,0:T(8,128)(2,1)}, bf16[256...) custom-call(s32[5]{0:T(128)} %stack.53.place_ref, ...), custom_call_target="tpu_custom_call" | custom-call | flops 5637144576 | bytes 18874368 | tf_op jit(solution)/shard_map/dense_chain/pallas_call | solution.py:483
  217.8 12.9 %dense_weights.1 = (bf16[8,96,1856]{2,1,0:T(8,128)(2,1)}, bf16[8,96,1856]{2,1,0:T(8,128)(2,1)}, bf16[2,768,1856]{2,1,0:T(8,128)(2,1)}) custom-call(s32[5]{0:T(128)} %stack.53.place_ref, bf16[256,768]{1,0:T(8,128)(2,1)} %get-tuple-element.125.refs_0_, bf16[256,768]{1,0:T(8,128)(2,1)} %get-tuple-element.126.refs_1_, ...), custom_call_target="tpu_custom_call" | custom-call | flops 5838471168 | bytes 20971520 | tf_op jit(solution)/shard_map/dense_weights/pallas_call | solution.py:580
  230.7 5.1 %all-to-all-start.3 = ((bf16[4,384,128]{2,1,0:T(8,128)(2,1)}), bf16[4,384,128]{2,1,0:T(8,128)(2,1)S(1)}, u32[]{:S(2)}, u32[]{:S(2)}) async-start(bf16[4,384,128]{2,1,0:T(8,128)(2,1)} %get-tuple-element.146), calls=%async_computation.3 | async-start | bytes 786432 | tf_op jit(solution)/shard_map/all_to_all | solution.py:764
  235.8 28.5 %attend_backward.2 = (f32[3,2048,128]{2,1,0:T(8,128)}, bf16[4,256,384]{2,1,0:T(8,128)(2,1)}) custom-call(s32[1]{0:T(128)} %bitcast.lane_ref, s32[8]{0:T(128)} %get-tuple-element.106.low_ref, s32[8]{0:T(128)} %get-tuple-element.107.high_ref, bf16[2048,768]{1,0:T(8,128)(2,1)} %add_convert_fusion.refs_0_, s32[2048,1]{1,0:T(8,128)} %copy.100.refs_1_, ...), custom_call_target="tpu_custom_call" | custom-call | flops 4026531840 | bytes 10485760 | tf_op jit(solution)/shard_map/attend_backward/pallas_call | solution.py:332
  264.3 3.1 fusion.17
  267.5 4.2 fusion
  271.7 26.0 %attend_backward.3 = (bf16[1,2048,768]{2,1,0:T(8,128)(2,1)}, f32[1,768]{1,0:T(1,128)}) custom-call(s32[1]{0:T(128)} %bitcast.lane_ref, s32[8]{0:T(128)} %get-tuple-element.106.low_ref, s32[8]{0:T(128)} %get-tuple-element.107.high_ref, bf16[2048,768]{1,0:T(8,128)(2,1)} %add_convert_fusion.refs_0_, s32[2048,1]{1,0:T(8,128)} %copy.100.refs_1_, ...), custom_call_target="tpu_custom_call" | custom-call | flops 4026531840 | bytes 10485760 | tf_op jit(solution)/shard_map/attend_backward/pallas_call | solution.py:332
  297.7 16.6 %collective-permute-done.9 = bf16[2,2,96,1856]{3,2,1,0:T(8,128)(2,1)S(1)} collective-permute-done((bf16[2,2,96,1856]{3,2,1,0:T(8,128)(2,1)}, bf16[2,2,96,1856]{3,2,1,0:T(8,128)(2,1)S(1)}, u32[]{:S(2)}, u32[]{:S(2)}) %collective-permute-start.9) | collective-permute-done | bytes 1425440 | tf_op jit(solution)/shard_map/ppermute | solution.py:656
  314.3 7.1 %convolution_convert_fusion = bf16[2048,768]{1,0:T(8,128)(2,1)} fusion(bf16[2048,768]{1,0:T(8,128)(2,1)} %bitcast.119, bf16[768,768]{0,1:T(8,128)(2,1)} %maximum_select_fusion), kind=kOutput, calls=%fused_computation.1 | convolution fusion | flops 2417491968 | bytes 7471104 | tf_op jit(solution)/shard_map/dot_general | solution.py:30
  322.4 1.8 collective-permute-start.11
  324.3 1.7 add_convert_fusion.3
  325.9 1.2 collective-permute-start.10
  327.2 2.4 collective-permute-start.12
  329.6 6.0 %fusion.20 = f32[768,768]{1,0:T(8,128)} fusion(bf16[2048,768]{1,0:T(8,128)(2,1)S(1)} %bitcast.113, bf16[2048,768]{1,0:T(8,128)(2,1)} %bitcast.120), kind=kOutput, calls=%fused_computation.90 | convolution fusion | flops 2415919104 | bytes 8650752 | tf_op jit(solution)/shard_map/dot_general | solution.py:30
  336.9 6.6 %collective-permute-done.10 = bf16[1,2,96,1856]{3,2,1,0:T(8,128)(2,1)S(1)} collective-permute-done((bf16[1,2,96,1856]{3,2,1,0:T(8,128)(2,1)S(1)}, bf16[1,2,96,1856]{3,2,1,0:T(8,128)(2,1)S(1)}, u32[]{:S(2)}, u32[]{:S(2)}) %collective-permute-start.10) | collective-permute-done | bytes 712736 | tf_op jit(solution)/shard_map/ppermute | solution.py:656
  343.7 1.8 fusion.7
  345.4 1.4 pad_maximum_fusion.1
  349.0 2.0 collective-permute-done.13
  351.8 8.4 %collective-permute-done.14 = bf16[2,96,768]{2,1,0:T(8,128)(2,1)S(1)} collective-permute-done((bf16[2,96,768]{2,1,0:T(8,128)(2,1)S(1)}, bf16[2,96,768]{2,1,0:T(8,128)(2,1)S(1)}, u32[]{:S(2)}, u32[]{:S(2)}) %collective-permute-start.14) | collective-permute-done | bytes 294944 | tf_op jit(solution)/shard_map/ppermute | solution.py:656
  360.4 1.8 collective-permute-start.15
  363.1 2.5 collective-permute-done.15
  366.3 1.7 finish_heads.1
  370.1 11.7 %reduce-scatter.8.cloned.1.call-done = bf16[512,768]{1,0:T(8,128)(2,1)} async-done(((bf16[2048,768]{1,0:T(8,128)(2,1)}), bf16[512,768]{1,0:T(8,128)(2,1)}) %reduce-scatter.8.cloned.1.call-update) | async-done | bytes 786448 | tf_op jit(solution)/shard_map/reduce_scatter | solution.py:850
  381.8 2.4 fusion.2
  384.2 33.5 %reduce-scatter.6.cloned.1.call-done = bf16[1,96,1856]{2,1,0:T(8,128)(2,1)} async-done(((bf16[4,96,1856]{2,1,0:T(8,128)(2,1)}), bf16[1,96,1856]{2,1,0:T(8,128)(2,1)}) %reduce-scatter.6.cloned.1.call-update) | async-done | bytes 356368 | tf_op jit(solution)/shard_map/reduce_scatter | solution.py:866
  417.8 1.9 finish_dense.1
  419.6 2.0 slice_bitcast_fusion.1
  421.7 1.3 slice_bitcast_fusion
  (167 shorter events, 25.1 us)
Async XLA Ops:
  7.2 8.6 %copy-start.13 = (bf16[96,192]{1,0:T(8,128)(2,1)S(1)}, bf16[96,192]{1,0:T(8,128)(2,1)}, u32[]{:S(2)}) copy-start(bf16[96,192]{1,0:T(8,128)(2,1)} %param.27) | copy-start | bytes 110596
  7.2 8.7 %copy-start.14 = (bf16[96,192]{1,0:T(8,128)(2,1)S(1)}, bf16[96,192]{1,0:T(8,128)(2,1)}, u32[]{:S(2)}) copy-start(bf16[96,192]{1,0:T(8,128)(2,1)} %param.26) | copy-start | bytes 110596
  7.2 8.8 %copy-start.15 = (bf16[96,192]{1,0:T(8,128)(2,1)S(1)}, bf16[96,192]{1,0:T(8,128)(2,1)}, u32[]{:S(2)}) copy-start(bf16[96,192]{1,0:T(8,128)(2,1)} %param.25) | copy-start | bytes 110596
  7.2 88.7 %all-gather.5.cloned.1.call-start = ((), (), s32[]{:S(2)}) async-start(), calls=%async_computation.10 | async-start | bytes 3932160 | tf_op jit(solution)/shard_map/all_gather | solution.py:719
  8.0 159.9 %all-gather.7.cloned.1.call-start = ((), (), s32[]{:S(2)}) async-start(), calls=%async_computation.11 | async-start | bytes 6193152 | tf_op jit(solution)/shard_map/all_gather | solution.py:770
  12.7 13.6 %collective-permute-start = (bf16[1,96,1792]{2,1,0:T(8,128)(2,1)S(1)}, bf16[1,96,1792]{2,1,0:T(8,128)(2,1)S(1)}, u32[]{:S(2)}, u32[]{:S(2)}) collective-permute-start(bf16[1,96,1792]{2,1,0:T(8,128)(2,1)S(1)} %bitcast.85), channel_id=1, source_target_pairs={{0,1},{1,0},{2,3},{3,2},{4,5},{5,4},{6,7},{7,6},{8,9},{9,8},{10,11... | collective-permute-start | bytes 1032200 | tf_op jit(solution)/shard_map/ppermute | solution.py:656
  16.3 12.3 %collective-permute-start.2 = (bf16[96,768]{0,1:T(8,128)(2,1)S(1)}, bf16[96,768]{0,1:T(8,128)(2,1)S(1)}, u32[]{:S(2)}, u32[]{:S(2)}) collective-permute-start(bf16[96,768]{0,1:T(8,128)(2,1)S(1)} %bitcast.94), channel_id=1, source_target_pairs={{0,4},{4,0},{8,12},{12,8},{16,20},{20,16},{24,28},{28,24},{1,5},{5... | collective-permute-start | bytes 442376 | tf_op jit(solution)/shard_map/ppermute | solution.py:656
  26.4 24.4 %copy-start.5 = (bf16[2,96,1792]{2,1,0:T(8,128)(2,1)}, bf16[2,96,1792]{2,1,0:T(8,128)(2,1)S(1)}, u32[]{:S(2)}) copy-start(bf16[2,96,1792]{2,1,0:T(8,128)(2,1)S(1)} %pad_maximum_fusion.3) | copy-start | bytes 2064388
  26.4 24.4 %collective-permute-start.1 = (bf16[2,96,1792]{2,1,0:T(8,128)(2,1)S(1)}, bf16[2,96,1792]{2,1,0:T(8,128)(2,1)S(1)}, u32[]{:S(2)}, u32[]{:S(2)}) collective-permute-start(bf16[2,96,1792]{2,1,0:T(8,128)(2,1)S(1)} %pad_maximum_fusion.3), channel_id=1, source_target_pairs={{0,8},{4,12},{8,0},{12,4},{16,24},{20,28},{24,16},{28,20},{1,9},{5... | collective-permute-start | bytes 2064392 | tf_op jit(solution)/shard_map/ppermute | solution.py:656
  28.9 20.2 %collective-permute-start.3 = (bf16[192,768]{0,1:T(8,128)(2,1)S(1)}, bf16[192,768]{0,1:T(8,128)(2,1)}, u32[]{:S(2)}, u32[]{:S(2)}) collective-permute-start(bf16[192,768]{0,1:T(8,128)(2,1)S(1)} %maximum_select_fusion.2), channel_id=1, source_target_pairs={{0,8},{4,12},{8,0},{12,4},{16,24},{20,28},{24,16},{28,20},{1,9},{5... | collective-permute-start | bytes 884744 | tf_op jit(solution)/shard_map/ppermute | solution.py:656
  50.9 43.2 %collective-permute-start.4 = (bf16[4,96,1792]{2,1,0:T(8,128)(2,1)S(1)}, bf16[4,96,1792]{2,1,0:T(8,128)(2,1)S(1)}, u32[]{:S(2)}, u32[]{:S(2)}) collective-permute-start(bf16[4,96,1792]{2,1,0:T(8,128)(2,1)S(1)} %pad_maximum_fusion.2), channel_id=1, source_target_pairs={{0,16},{4,20},{8,24},{12,28},{16,0},{20,4},{24,8},{28,12},{1,17},{... | collective-permute-start | bytes 4128776 | tf_op jit(solution)/shard_map/ppermute | solution.py:656
  52.4 39.2 %collective-permute-start.5 = (bf16[384,768]{0,1:T(8,128)(2,1)S(1)}, bf16[384,768]{0,1:T(8,128)(2,1)}, u32[]{:S(2)}, u32[]{:S(2)}) collective-permute-start(bf16[384,768]{0,1:T(8,128)(2,1)S(1)} %maximum_select_fusion.1), channel_id=1, source_target_pairs={{0,16},{4,20},{8,24},{12,28},{16,0},{20,4},{24,8},{28,12},{1,17},{... | collective-permute-start | bytes 1769480 | tf_op jit(solution)/shard_map/ppermute | solution.py:656
  95.9 28.0 %collective-permute-start.6 = (bf16[2,96,1792]{2,1,0:T(8,128)(2,1)}, bf16[2,96,1792]{2,1,0:T(8,128)(2,1)S(1)}, u32[]{:S(2)}, u32[]{:S(2)}) collective-permute-start(bf16[2,96,1792]{2,1,0:T(8,128)(2,1)} %copy-done.5), channel_id=1, source_target_pairs={{0,2},{1,3},{2,0},{3,1},{4,6},{5,7},{6,4},{7,5},{8,10},{9,11},{10,... | collective-permute-start | bytes 2064392 | tf_op jit(solution)/shard_map/ppermute | solution.py:656
  102.5 22.3 %copy-start = (bf16[8,96,1792]{2,1,0:T(8,128)(2,1)S(1)}, bf16[8,96,1792]{2,1,0:T(8,128)(2,1)}, u32[]{:S(2)}) copy-start(bf16[8,96,1792]{2,1,0:T(8,128)(2,1)} %pad_maximum_fusion.refs_0_) | copy-start | bytes 8257540
  122.3 6.9 %copy-start.19 = (s32[1,512]{1,0:T(1,128)S(1)}, s32[1,512]{1,0:T(1,128)}, u32[]{:S(2)}) copy-start(s32[1,512]{1,0:T(1,128)} %param.22) | copy-start | bytes 6148
  122.3 7.8 %copy-start.22 = (bf16[768]{0:T(1024)(128)(2,1)S(1)}, bf16[768]{0:T(1024)(128)(2,1)}, u32[]{:S(2)}) copy-start(bf16[768]{0:T(1024)(128)(2,1)} %param.33) | copy-start | bytes 4612
  122.3 7.8 %copy-start.23 = (bf16[768]{0:T(1024)(128)(2,1)S(1)}, bf16[768]{0:T(1024)(128)(2,1)}, u32[]{:S(2)}) copy-start(bf16[768]{0:T(1024)(128)(2,1)} %param.36) | copy-start | bytes 4612
  122.3 7.8 %copy-start.24 = (bf16[768]{0:T(1024)(128)(2,1)S(1)}, bf16[768]{0:T(1024)(128)(2,1)}, u32[]{:S(2)}) copy-start(bf16[768]{0:T(1024)(128)(2,1)} %param.37) | copy-start | bytes 4612
  122.4 7.8 %copy-start.25 = (bf16[768]{0:T(1024)(128)(2,1)S(1)}, bf16[768]{0:T(1024)(128)(2,1)}, u32[]{:S(2)}) copy-start(bf16[768]{0:T(1024)(128)(2,1)} %param.35) | copy-start | bytes 4612
  122.4 7.8 %copy-start.26 = (bf16[768]{0:T(1024)(128)(2,1)S(1)}, bf16[768]{0:T(1024)(128)(2,1)}, u32[]{:S(2)}) copy-start(bf16[768]{0:T(1024)(128)(2,1)} %param.38) | copy-start | bytes 4612
  122.4 7.8 %copy-start.27 = (bf16[768]{0:T(1024)(128)(2,1)S(1)}, bf16[768]{0:T(1024)(128)(2,1)}, u32[]{:S(2)}) copy-start(bf16[768]{0:T(1024)(128)(2,1)} %param.39) | copy-start | bytes 4612
  122.4 8.5 %copy-start.20 = (bf16[3072]{0:T(1024)(128)(2,1)S(1)}, bf16[3072]{0:T(1024)(128)(2,1)}, u32[]{:S(2)}) copy-start(bf16[3072]{0:T(1024)(128)(2,1)} %param.34) | copy-start | bytes 18436
  124.9 24.6 %collective-permute-start.7 = (bf16[8,96,1792]{2,1,0:T(8,128)(2,1)S(1)}, bf16[8,96,1792]{2,1,0:T(8,128)(2,1)}, u32[]{:S(2)}, u32[]{:S(2)}) collective-permute-start(bf16[8,96,1792]{2,1,0:T(8,128)(2,1)S(1)} %copy-done), channel_id=1, source_target_pairs={{0,4},{4,0},{8,12},{12,8},{16,20},{20,16},{24,28},{28,24},{1,5},{5... | collective-permute-start | bytes 8257544 | tf_op jit(solution)/shard_map/ppermute | solution.py:656
  124.9 43.9 %all-to-all-start = ((bf16[4,384,128]{2,1,0:T(8,128)(2,1)}), bf16[4,384,128]{2,1,0:T(8,128)(2,1)S(1)}, u32[]{:S(2)}, u32[]{:S(2)}) async-start(bf16[4,384,128]{2,1,0:T(8,128)(2,1)} %get-tuple-element.104.refs_3_), calls=%async_computation | async-start | bytes 786432 | tf_op jit(solution)/shard_map/all_to_all | solution.py:764
  168.8 6.6 %copy-start.7 = (bf16[4,384,128]{2,1,0:T(8,128)(2,1)}, bf16[4,384,128]{2,1,0:T(8,128)(2,1)S(1)}, u32[]{:S(2)}) copy-start(bf16[4,384,128]{2,1,0:T(8,128)(2,1)S(1)} %all-to-all-done.ctx_ref.refs_10_) | copy-start | bytes 1179652
  168.8 24.0 %all-to-all-start.1 = ((bf16[4,384,128]{2,1,0:T(8,128)(2,1)}), bf16[4,384,128]{2,1,0:T(8,128)(2,1)S(1)}, u32[]{:S(2)}, u32[]{:S(2)}) async-start(bf16[4,384,128]{2,1,0:T(8,128)(2,1)} %get-tuple-element.112.refs_3_), calls=%async_computation.1 | async-start | bytes 786432 | tf_op jit(solution)/shard_map/all_to_all | solution.py:764
  192.8 24.2 %all-to-all-start.2 = ((bf16[4,384,128]{2,1,0:T(8,128)(2,1)}), bf16[4,384,128]{2,1,0:T(8,128)(2,1)S(1)}, u32[]{:S(2)}, u32[]{:S(2)}) async-start(bf16[4,384,128]{2,1,0:T(8,128)(2,1)} %get-tuple-element.114), calls=%async_computation.2 | async-start | bytes 786432 | tf_op jit(solution)/shard_map/all_to_all | solution.py:764
  197.9 17.5 %copy-start.18 = (f32[4,1,768]{2,1,0:T(1,128)S(1)}, f32[4,1,768]{2,1,0:T(1,128)}, u32[]{:S(2)}) copy-start(f32[4,1,768]{2,1,0:T(1,128)} %get-tuple-element.139) | copy-start | bytes 36868
  197.9 18.3 %copy-start.17 = (f32[8,768]{1,0:T(8,128)S(1)}, f32[8,768]{1,0:T(8,128)}, u32[]{:S(2)}) copy-start(f32[8,768]{1,0:T(8,128)} %get-tuple-element.137) | copy-start | bytes 73732
  197.9 145.7 %reduce-scatter.4.cloned.1.call-start = ((), (), s32[]{:S(2)}) async-start(), calls=%async_computation.7 | async-start | bytes 6635520 | tf_op jit(solution)/shard_map/reduce_scatter | solution.py:825
  217.0 13.6 %copy-start.8 = (bf16[4,384,128]{2,1,0:T(8,128)(2,1)}, bf16[4,384,128]{2,1,0:T(8,128)(2,1)S(1)}, u32[]{:S(2)}) copy-start(bf16[4,384,128]{2,1,0:T(8,128)(2,1)S(1)} %all-to-all-done.2.refs_4_) | copy-start | bytes 1179652
  230.7 36.8 %collective-permute-start.8 = (bf16[4,2,96,1856]{3,2,1,0:T(8,128)(2,1)}, bf16[4,2,96,1856]{3,2,1,0:T(8,128)(2,1)}, u32[]{:S(2)}, u32[]{:S(2)}) collective-permute-start(bf16[4,2,96,1856]{3,2,1,0:T(8,128)(2,1)} %bitcast.28), channel_id=1, source_target_pairs={{0,4},{4,0},{8,12},{12,8},{16,20},{20,16},{24,28},{28,24},{1,5},{5... | collective-permute-start | bytes 8552456 | tf_op jit(solution)/shard_map/ppermute | solution.py:656
  230.7 36.7 %all-to-all-start.3 = ((bf16[4,384,128]{2,1,0:T(8,128)(2,1)}), bf16[4,384,128]{2,1,0:T(8,128)(2,1)S(1)}, u32[]{:S(2)}, u32[]{:S(2)}) async-start(bf16[4,384,128]{2,1,0:T(8,128)(2,1)} %get-tuple-element.146), calls=%async_computation.3 | async-start | bytes 786432 | tf_op jit(solution)/shard_map/all_to_all | solution.py:764
  235.8 146.0 %reduce-scatter.8.cloned.1.call-start = ((), (), s32[]{:S(2)}) async-start(), calls=%async_computation.9 | async-start | bytes 3932160 | tf_op jit(solution)/shard_map/reduce_scatter | solution.py:850
  271.7 42.6 %collective-permute-start.9 = (bf16[2,2,96,1856]{3,2,1,0:T(8,128)(2,1)}, bf16[2,2,96,1856]{3,2,1,0:T(8,128)(2,1)S(1)}, u32[]{:S(2)}, u32[]{:S(2)}) collective-permute-start(bf16[2,2,96,1856]{3,2,1,0:T(8,128)(2,1)} %get-tuple-element.150), channel_id=1, source_target_pairs={{0,8},{4,12},{8,0},{12,4},{16,24},{20,28},{24,16},{28,20},{1,9},{5... | collective-permute-start | bytes 4276232 | tf_op jit(solution)/shard_map/ppermute | solution.py:656
  314.3 7.1 %copy-start.2 = (bf16[2,2,96,1856]{3,2,1,0:T(8,128)(2,1)}, bf16[2,2,96,1856]{3,2,1,0:T(8,128)(2,1)S(1)}, u32[]{:S(2)}) copy-start(bf16[2,2,96,1856]{3,2,1,0:T(8,128)(2,1)S(1)} %collective-permute-done.9) | copy-start | bytes 4276228
  321.4 96.4 %reduce-scatter.6.cloned.1.call-start = ((), (), s32[]{:S(2)}) async-start(), calls=%async_computation.8 | async-start | bytes 1843200 | tf_op jit(solution)/shard_map/reduce_scatter | solution.py:866
  322.4 7.2 %copy-start.28 = (bf16[1,2048,768]{2,1,0:T(8,128)(2,1)S(1)}, bf16[1,2048,768]{2,1,0:T(8,128)(2,1)}, u32[]{:S(2)}) copy-start(bf16[1,2048,768]{2,1,0:T(8,128)(2,1)} %all-gather.5.cloned.1.call-done) | copy-start | bytes 9437188
  322.4 4.7 %collective-permute-start.11 = (f32[1,384]{1,0:T(1,128)S(1)}, f32[1,384]{1,0:T(1,128)S(1)}, u32[]{:S(2)}, u32[]{:S(2)}) collective-permute-start(f32[1,384]{1,0:T(1,128)S(1)} %pad_maximum_fusion.7), channel_id=1, source_target_pairs={{0,1},{1,0},{2,3},{3,2},{4,5},{5,4},{6,7},{7,6},{8,9},{9,8},{10,11... | collective-permute-start | bytes 4616 | tf_op jit(solution)/shard_map/ppermute | solution.py:656
  325.9 17.5 %collective-permute-start.10 = (bf16[1,2,96,1856]{3,2,1,0:T(8,128)(2,1)S(1)}, bf16[1,2,96,1856]{3,2,1,0:T(8,128)(2,1)S(1)}, u32[]{:S(2)}, u32[]{:S(2)}) collective-permute-start(bf16[1,2,96,1856]{3,2,1,0:T(8,128)(2,1)S(1)} %get-tuple-element.161), channel_id=1, source_target_pairs={{0,16},{4,20},{8,24},{12,28},{16,0},{20,4},{24,8},{28,12},{1,17},{... | collective-permute-start | bytes 2138120 | tf_op jit(solution)/shard_map/ppermute | solution.py:656
  327.2 8.4 %collective-permute-start.12 = (f32[2,384]{1,0:T(2,128)S(1)}, f32[2,384]{1,0:T(2,128)S(1)}, u32[]{:S(2)}, u32[]{:S(2)}) collective-permute-start(f32[2,384]{1,0:T(2,128)S(1)} %maximum_select_fusion.4), channel_id=1, source_target_pairs={{0,2},{1,3},{2,0},{3,1},{4,6},{5,7},{6,4},{7,5},{8,10},{9,11},{10,... | collective-permute-start | bytes 9224 | tf_op jit(solution)/shard_map/ppermute | solution.py:656
  348.9 2.1 collective-permute-start.13
  349.0 13.2 %copy-start.11 = (bf16[256,768]{1,0:T(8,128)(2,1)S(1)}, bf16[256,768]{1,0:T(8,128)(2,1)}, u32[]{:S(2)}) copy-start(bf16[256,768]{1,0:T(8,128)(2,1)} %get-tuple-element.111) | copy-start | bytes 1179652
  349.0 13.2 %copy-start.12 = (bf16[256,768]{1,0:T(8,128)(2,1)S(1)}, bf16[256,768]{1,0:T(8,128)(2,1)}, u32[]{:S(2)}) copy-start(bf16[256,768]{1,0:T(8,128)(2,1)} %get-tuple-element.113) | copy-start | bytes 1179652
  351.1 9.1 %collective-permute-start.14 = (bf16[2,96,768]{2,1,0:T(8,128)(2,1)S(1)}, bf16[2,96,768]{2,1,0:T(8,128)(2,1)S(1)}, u32[]{:S(2)}, u32[]{:S(2)}) collective-permute-start(bf16[2,96,768]{2,1,0:T(8,128)(2,1)S(1)} %dynamic-slice_bitcast_fusion.1), channel_id=1, source_target_pairs={{0,8},{4,12},{8,0},{12,4},{16,24},{20,28},{24,16},{28,20},{1,9},{5... | collective-permute-start | bytes 884744 | tf_op jit(solution)/shard_map/ppermute | solution.py:656
  360.3 21.5 %copy-start.3 = (f32[256,768]{1,0:T(8,128)S(1)}, f32[256,768]{1,0:T(8,128)}, u32[]{:S(2)}) copy-start(f32[256,768]{1,0:T(8,128)} %get-tuple-element.166) | copy-start | bytes 2359300
  360.3 21.5 %copy-start.4 = (f32[256,768]{1,0:T(8,128)S(1)}, f32[256,768]{1,0:T(8,128)}, u32[]{:S(2)}) copy-start(f32[256,768]{1,0:T(8,128)} %get-tuple-element.167) | copy-start | bytes 2359300
  360.4 5.2 %collective-permute-start.15 = (bf16[1,96,768]{2,1,0:T(8,128)(2,1)S(1)}, bf16[1,96,768]{2,1,0:T(8,128)(2,1)S(1)}, u32[]{:S(2)}, u32[]{:S(2)}) collective-permute-start(bf16[1,96,768]{2,1,0:T(8,128)(2,1)S(1)} %constant_dynamic-slice_fusion), channel_id=1, source_target_pairs={{0,16},{4,20},{8,24},{12,28},{16,0},{20,4},{24,8},{28,12},{1,17},{... | collective-permute-start | bytes 442376 | tf_op jit(solution)/shard_map/ppermute | solution.py:656
  (6 other events, 16.1 us)
Sparse Core Ops, SparseCore 0:
  9.6 66.1 all-gather.4
  125.0 42.8 all-gather.6
  230.8 68.0 reduce-scatter.3
  321.5 60.2 reduce-scatter.7
  384.0 33.7 reduce-scatter.5

commit v9 on v8

--- a/solution.py
+++ b/solution.py
@@ -731,17 +731,17 @@
     if paired:
         place = jnp.stack([rank, rank ^ 1, rank ^ 2, rank ^ 3, lax.axis_index("dp")]).astype(jnp.int32)
         pair = jnp.concatenate([mine[None], swap(mine[None], "tensor", 1)], axis=0)
-        near = pair
-        w_heads = merge(w_heads, swap(w_heads, "dp", 1), "dp", 1)
-        turns = [0]
-        for bit in (2, 4):
-            turns = turns + [turn ^ bit for turn in turns]
-            near = jnp.concatenate([near, swap(near, "dp", bit)], axis=0)
+        far = [swap(pair[slot : slot + 1], "tensor", 2) for slot in range(2)]
+        near = jnp.concatenate([pair, swap(pair, "dp", 2)], axis=0)
+        turns = [0, 2, 4, 6]
+        for bit in (1, 2, 4):
             w_heads = merge(w_heads, swap(w_heads, "dp", bit), "dp", bit)
-            near, w_heads = lax.optimization_barrier((near, w_heads))
+        near, w_heads, far[0] = lax.optimization_barrier((near, w_heads, far[0]))
+        near = jnp.concatenate([near, swap(near, "dp", 4)], axis=0)
+        tokens, far, near = lax.optimization_barrier((tokens, far, near))
         near_other = swap(near, "dp", 1)
-        tokens, pair = lax.optimization_barrier((tokens, pair))
-        far = swap(pair, "tensor", 2)
+        far = jnp.concatenate(far, axis=0)
+        weights = lax.all_gather(far, "dp", axis=0, tiled=False)
     else:
         place = jnp.asarray(list(range(parts)) + [0], jnp.int32)
         weights = lax.all_gather(mine, ("tensor", "dp"), axis=0, tiled=False)
@@ -765,11 +765,8 @@
 
     contexts, lses, arrived = [], [], []
     for half in range(halves):
-        if paired and half == halves - 1:
-            bounds, far = lax.optimization_barrier((bounds, after(far, contexts[0])))
-            weights = lax.all_gather(far, "dp", axis=0, tiled=False)
         context, lse = run_forward((halves, half), lane, bounds, qkv, seg_col, seg_row)
-        if paired and half == halves - 1:
+        if paired and half == 0:
             context, near_other = lax.optimization_barrier((context, near_other))
         contexts.append(context)
         lses.append(lse)
@@ -831,10 +828,7 @@
     earlier, before = [], []
     for half in range(halves):
         if paired and half == halves - 1:
-            came, before, head_grads[-1] = lax.optimization_barrier((came, before, head_grads[-1]))
-            keep, send = add_halves(keep, came)
-            keep, send, before = lax.optimization_barrier((keep, send, before))
-            came = swap(send, "dp", 2)
+            before, head_grads[-1] = lax.optimization_barrier((before, head_grads[-1]))
         results = run_backward(
             (halves, half), lane, bounds, qkv, seg_col, seg_row, contexts[half], head_grads[half],
             lses[half], earlier, before,
@@ -843,20 +837,25 @@
             before, earlier = [results[0]], earlier + [results[1]]
     joined_grad, sums = results
     joined_grad = joined_grad.reshape(seq_len, -1)
+    attn_back = dot(joined_grad, w_heads, NT).astype(BF16)
     if paired:
-        came, joined_grad = lax.optimization_barrier((came, joined_grad))
-    attn_back = dot(joined_grad, w_heads, NT).astype(BF16)
+        came = after(came, attn_back)
     attn_back, sums, joined_grad = lax.optimization_barrier((attn_back, sums, joined_grad))
     attn_back = lax.psum_scatter(attn_back, "tensor", scatter_dimension=0, tiled=True)
     if paired:
         keep, send = add_halves(keep, came)
         keep, send, joined_grad = lax.optimization_barrier((keep, send, joined_grad))
+        came = swap(send, "dp", 2)
+    head_weights = dot(tokens, joined_grad, TN).reshape((copies, shard_rows, -1))
+    if paired:
+        came, head_weights = lax.optimization_barrier((came, head_weights))
+        keep, send = add_halves(keep, came)
+        keep, send, head_weights = lax.optimization_barrier((keep, send, head_weights))
         came = swap(send, "dp", 4)
     sums = sums.reshape(heads, 4, DH)
     sums = jnp.concatenate((sums[:, 0].reshape(1, head_cols), sums[:, 3].reshape(1, head_cols)), axis=1)
     for bit in bits_of("tensor"):
         sums = merge(sums, swap(sums, "tensor", bit), "tensor", bit)
-    head_weights = dot(tokens, joined_grad, TN).reshape((copies, shard_rows, -1))
     if paired:
         came, head_weights = lax.optimization_barrier((came, head_weights))
         slots = jnp.concatenate([add_low(keep, came)[0], distant], axis=0)

time: 433 us -> 414 us (0.956)
  waiting for transfers between devices: 166 us -> 144 us
  starting transfers between devices: 35.1 us -> 41.5 us
    ppermute x16 -> x17, waiting for transfers between devices: 103 us -> 134 us  [swap(): return lax.ppermute(value, axis, [(i, i ^ bit) for i in range(size)])]
    reduce_scatter x1, waiting for transfers between devices: 33.5 us -> 9.35 us  [local(): lax.psum_scatter(packed, 'tensor', scatter_dimension=0, tiled=True)[0]]
    all_gather x1, waiting for transfers between devices: 17.4 us -> 0.01 us  [local(): weights = lax.all_gather(far, 'dp', axis=0, tiled=False)]
    reduce_scatter x1, waiting for transfers between devices: 11.7 us -> 0.01 us  [local(): lax.psum_scatter(attn_back, 'tensor', scatter_dimension=0, tiled=True)]
    ppermute x16 -> x17, starting transfers between devices: 15.6 us -> 19.6 us  [swap(): return lax.ppermute(value, axis, [(i, i ^ bit) for i in range(size)])]
  transfers between devices with their start and end apart: 25 -> 26, of which waited for: 12 -> 13; matrix products, arithmetic and copies ran while one was open for 14% -> 13% of each run, Pallas kernels for 30% -> 31%
where the time goes in v9:
time: 414 us; the launch traced here: 412 us
  waiting for transfers between devices  144 us (35%)
  Pallas kernels  143 us (35%)
  starting transfers between devices  41.5 us (10%)
  other arithmetic  26.9 us (6%)
  matrix products  20.4 us (5%)
  between operations  19 us (5%)
  local copies, waits for them, and re-layouts  17.6 us (4%)
    ppermute x17, waiting for transfers between devices, swap(): return lax.ppermute(value, axis, [(i, i ^ bit) for i in range(size)])  134 us
    pallas_call x2, Pallas kernels, run_backward(): pl.pallas_call(functools.partial(attend_backward, which, len(qkv)), out_s...  54.4 us
    pallas_call x2, Pallas kernels, run_forward(): pl.pallas_call(functools.partial(attend_forward, which), out_shape=(jax.S...  36.9 us
    pallas_call x2, Pallas kernels, run_dense(): pl.pallas_call(functools.partial(dense_chain, marks), out_shape=out_shape...  34.9 us
    all_to_all x4, starting transfers between devices, exchange(): return lax.all_to_all(packed_blocks, 'tensor', 0, 0)  21.5 us
    dot_general x3, matrix products, dot(): lax.dot_general(left_side, right_side, dims, preferred_element_type=F32)  20.4 us
    ppermute x17, starting transfers between devices, swap(): return lax.ppermute(value, axis, [(i, i ^ bit) for i in range(size)])  19.6 us
    pallas_call x1, Pallas kernels, run_weights(): pl.pallas_call(functools.partial(dense_weights, inner, halves), out_shape...  12.9 us
  transfers between devices with their start and end apart: 26, of which 13 were waited for; matrix products, arithmetic and copies ran while one was open for 13% of the time, Pallas kernels for 31%

profile of v9, /device:TPU:0, one launch (start us, length us, event | category | flops | bytes accessed | tf_op | source)
XLA Modules:
  0.0 412.1 jit_solution(7509114146927927835)
XLA Ops:
  13.8 2.6 collective-permute-start.3
  16.7 1.6 collective-permute-start
  18.3 7.8 %collective-permute-done.3 = bf16[192,768]{0,1:T(8,128)(2,1)S(1)} collective-permute-done((bf16[192,768]{0,1:T(8,128)(2,1)S(1)}, bf16[192,768]{0,1:T(8,128)(2,1)S(1)}, u32[]{:S(2)}, u32[]{:S(2)}) %collective-permute-start.3) | collective-permute-done | bytes 294944 | tf_op jit(solution)/shard_map/ppermute | solution.py:656
  26.6 1.8 collective-permute-start.4
  28.5 13.8 %collective-permute-done = bf16[1,96,1792]{2,1,0:T(8,128)(2,1)S(1)} collective-permute-done((bf16[1,96,1792]{2,1,0:T(8,128)(2,1)S(1)}, bf16[1,96,1792]{2,1,0:T(8,128)(2,1)S(1)}, u32[]{:S(2)}, u32[]{:S(2)}) %collective-permute-start) | collective-permute-done | bytes 344096 | tf_op jit(solution)/shard_map/ppermute | solution.py:656
  42.4 5.3 %collective-permute-start.5 = (bf16[1,96,1792]{2,1,0:T(8,128)(2,1)S(1)}, bf16[1,96,1792]{2,1,0:T(8,128)(2,1)S(1)}, u32[]{:S(2)}, u32[]{:S(2)}) collective-permute-start(bf16[1,96,1792]{2,1,0:T(8,128)(2,1)S(1)} %bitcast.88), channel_id=1, source_target_pairs={{0,2},{1,3},{2,0},{3,1},{4,6},{5,7},{6,4},{7,5},{8,10},{9,11},{10,... | collective-permute-start | bytes 1032200 | tf_op jit(solution)/shard_map/ppermute | solution.py:656
  47.6 2.5 maximum_select_fusion
  50.2 5.4 %collective-permute-done.1 = bf16[2,96,1792]{2,1,0:T(8,128)(2,1)S(1)} collective-permute-done((bf16[2,96,1792]{2,1,0:T(8,128)(2,1)S(1)}, bf16[2,96,1792]{2,1,0:T(8,128)(2,1)S(1)}, u32[]{:S(2)}, u32[]{:S(2)}) %collective-permute-start.1) | collective-permute-done | bytes 688160 | tf_op jit(solution)/shard_map/ppermute | solution.py:656
  55.8 26.7 %collective-permute-done.5 = bf16[1,96,1792]{2,1,0:T(8,128)(2,1)S(1)} collective-permute-done((bf16[1,96,1792]{2,1,0:T(8,128)(2,1)S(1)}, bf16[1,96,1792]{2,1,0:T(8,128)(2,1)S(1)}, u32[]{:S(2)}, u32[]{:S(2)}) %collective-permute-start.5) | collective-permute-done | bytes 344096 | tf_op jit(solution)/shard_map/ppermute | solution.py:656
  82.5 1.5 collective-permute-start.7
  84.0 27.0 %collective-permute-done.7 = bf16[4,96,1792]{2,1,0:T(8,128)(2,1)S(1)} collective-permute-done((bf16[4,96,1792]{2,1,0:T(8,128)(2,1)S(1)}, bf16[4,96,1792]{2,1,0:T(8,128)(2,1)S(1)}, u32[]{:S(2)}, u32[]{:S(2)}) %collective-permute-start.7) | collective-permute-done | bytes 1376288 | tf_op jit(solution)/shard_map/ppermute | solution.py:656
  111.2 2.1 pad_maximum_fusion.4
  114.8 1.4 copy.100.refs_1_
  116.9 6.6 %add_convert_fusion.refs_0_ = bf16[2048,768]{1,0:T(8,128)(2,1)} fusion(bf16[2048,768]{1,0:T(8,128)(2,1)} %bitcast.114, bf16[768,768]{0,1:T(8,128)(2,1)} %maximum_select_fusion, f32[768]{0:T(1024)S(1)} %add.123), kind=kOutput, calls=%fused_computation | convolution fusion | flops 2419064832 | bytes 7474176 | tf_op jit(solution)/shard_map/dot_general | solution.py:30
  123.6 19.7 %attend_forward.2 = (bf16[4,384,128]{2,1,0:T(8,128)(2,1)}, f32[3,1,1024]{2,1,0:T(1,128)}) custom-call(s32[1]{0:T(128)} %bitcast.lane_ref, s32[8]{0:T(128)} %get-tuple-element.200.low_ref, s32[8]{0:T(128)} %get-tuple-element.199.high_ref, bf16[2048,768]{1,0:T(8,128)(2,1)} %add_convert_fusion.refs_0_, s32[2048,1]{1,0:T(8,128)} %copy.100.refs_1_, s32[1,2048]{1,0:T(1,128)} %refs_2_.7), custom_call_target="tpu_custom_call" | custom-call | flops 1610612736 | bytes 5242880 | tf_op jit(solution)/shard_map/attend_forward/pallas_call | solution.py:265
  143.3 6.3 %all-to-all-start = ((bf16[4,384,128]{2,1,0:T(8,128)(2,1)}), bf16[4,384,128]{2,1,0:T(8,128)(2,1)S(1)}, u32[]{:S(2)}, u32[]{:S(2)}) async-start(bf16[4,384,128]{2,1,0:T(8,128)(2,1)} %get-tuple-element.104.refs_3_), calls=%async_computation | async-start | bytes 786432 | tf_op jit(solution)/shard_map/all_to_all | solution.py:764
  152.6 17.1 %attend_forward.3 = (bf16[4,384,128]{2,1,0:T(8,128)(2,1)}, f32[3,1,1024]{2,1,0:T(1,128)}) custom-call(s32[1]{0:T(128)} %bitcast.lane_ref, s32[8]{0:T(128)} %get-tuple-element.200.low_ref, s32[8]{0:T(128)} %get-tuple-element.199.high_ref, bf16[2048,768]{1,0:T(8,128)(2,1)} %add_convert_fusion.refs_0_, s32[2048,1]{1,0:T(8,128)} %copy.100.refs_1_, s32[1,2048]{1,0:T(1,128)} %refs_2_.7), custom_call_target="tpu_custom_call" | custom-call | flops 1610612736 | bytes 5242880 | tf_op jit(solution)/shard_map/attend_forward/pallas_call | solution.py:265
  171.7 5.1 %all-to-all-start.1 = ((bf16[4,384,128]{2,1,0:T(8,128)(2,1)}), bf16[4,384,128]{2,1,0:T(8,128)(2,1)S(1)}, u32[]{:S(2)}, u32[]{:S(2)}) async-start(bf16[4,384,128]{2,1,0:T(8,128)(2,1)} %get-tuple-element.106.refs_3_), calls=%async_computation.1 | async-start | bytes 786432 | tf_op jit(solution)/shard_map/all_to_all | solution.py:764
  178.7 17.5 %dense_chain.2 = (bf16[256,768]{1,0:T(8,128)(2,1)}, f32[256,768]{1,0:T(8,128)}, bf16[4,384,128]{2,1,0:T(8,128)(2,1)}, bf16[256,768]{1,0:T(8,128)(2,1)}, bf16[256...) custom-call(s32[5]{0:T(128)} %stack.53.place_ref, ...), custom_call_target="tpu_custom_call" | custom-call | flops 5637144576 | bytes 18874368 | tf_op jit(solution)/shard_map/dense_chain/pallas_call | solution.py:483
  196.2 5.1 %all-to-all-start.2 = ((bf16[4,384,128]{2,1,0:T(8,128)(2,1)}), bf16[4,384,128]{2,1,0:T(8,128)(2,1)S(1)}, u32[]{:S(2)}, u32[]{:S(2)}) async-start(bf16[4,384,128]{2,1,0:T(8,128)(2,1)} %get-tuple-element.108), calls=%async_computation.2 | async-start | bytes 786432 | tf_op jit(solution)/shard_map/all_to_all | solution.py:764
  201.4 17.4 %dense_chain.3 = (bf16[256,768]{1,0:T(8,128)(2,1)}, f32[256,768]{1,0:T(8,128)}, bf16[4,384,128]{2,1,0:T(8,128)(2,1)}, bf16[256,768]{1,0:T(8,128)(2,1)}, bf16[256...) custom-call(s32[5]{0:T(128)} %stack.53.place_ref, ...), custom_call_target="tpu_custom_call" | custom-call | flops 5637144576 | bytes 18874368 | tf_op jit(solution)/shard_map/dense_chain/pallas_call | solution.py:483
  221.2 12.9 %dense_weights.1 = (bf16[8,96,1856]{2,1,0:T(8,128)(2,1)}, bf16[8,96,1856]{2,1,0:T(8,128)(2,1)}, bf16[2,768,1856]{2,1,0:T(8,128)(2,1)}) custom-call(s32[5]{0:T(128)} %stack.53.place_ref, bf16[256,768]{1,0:T(8,128)(2,1)} %get-tuple-element.119.refs_0_, bf16[256,768]{1,0:T(8,128)(2,1)} %get-tuple-element.120.refs_1_, ...), custom_call_target="tpu_custom_call" | custom-call | flops 5838471168 | bytes 20971520 | tf_op jit(solution)/shard_map/dense_weights/pallas_call | solution.py:580
  234.1 5.0 %all-to-all-start.3 = ((bf16[4,384,128]{2,1,0:T(8,128)(2,1)}), bf16[4,384,128]{2,1,0:T(8,128)(2,1)S(1)}, u32[]{:S(2)}, u32[]{:S(2)}) async-start(bf16[4,384,128]{2,1,0:T(8,128)(2,1)} %get-tuple-element.140), calls=%async_computation.3 | async-start | bytes 786432 | tf_op jit(solution)/shard_map/all_to_all | solution.py:764
  239.2 28.2 %attend_backward.2 = (f32[3,2048,128]{2,1,0:T(8,128)}, bf16[4,256,384]{2,1,0:T(8,128)(2,1)}) custom-call(s32[1]{0:T(128)} %bitcast.lane_ref, s32[8]{0:T(128)} %get-tuple-element.200.low_ref, s32[8]{0:T(128)} %get-tuple-element.199.high_ref, bf16[2048,768]{1,0:T(8,128)(2,1)} %add_convert_fusion.refs_0_, s32[2048,1]{1,0:T(8,128)} %copy.100.refs_1_, ...), custom_call_target="tpu_custom_call" | custom-call | flops 4026531840 | bytes 10485760 | tf_op jit(solution)/shard_map/attend_backward/pallas_call | solution.py:332
  268.1 26.2 %attend_backward.3 = (bf16[1,2048,768]{2,1,0:T(8,128)(2,1)}, f32[1,768]{1,0:T(1,128)}) custom-call(s32[1]{0:T(128)} %bitcast.lane_ref, s32[8]{0:T(128)} %get-tuple-element.200.low_ref, s32[8]{0:T(128)} %get-tuple-element.199.high_ref, bf16[2048,768]{1,0:T(8,128)(2,1)} %add_convert_fusion.refs_0_, s32[2048,1]{1,0:T(8,128)} %copy.100.refs_1_, ...), custom_call_target="tpu_custom_call" | custom-call | flops 4026531840 | bytes 10485760 | tf_op jit(solution)/shard_map/attend_backward/pallas_call | solution.py:332
  294.3 6.2 %convolution_convert_fusion = bf16[2048,768]{1,0:T(8,128)(2,1)} fusion(bf16[768,768]{0,1:T(8,128)(2,1)S(1)} %copy-done.3, bf16[1,2048,768]{2,1,0:T(8,128)(2,1)} %get-tuple-element.145), kind=kOutput, calls=%fused_computation.1 | convolution fusion | flops 2417491968 | bytes 7471104 | tf_op jit(solution)/shard_map/dot_general | solution.py:30
  300.9 1.5 copy-done
  302.6 2.6 fusion
  306.2 7.6 %fusion.21 = f32[768,768]{1,0:T(8,128)} fusion(bf16[2048,768]{1,0:T(8,128)(2,1)} %bitcast.115, bf16[2048,768]{1,0:T(8,128)(2,1)} %bitcast.122), kind=kOutput, calls=%fused_computation.92 | convolution fusion | flops 2415919104 | bytes 8650752 | tf_op jit(solution)/shard_map/dot_general | solution.py:30
  313.7 26.4 %collective-permute-done.10 = bf16[2,2,96,1856]{3,2,1,0:T(8,128)(2,1)} collective-permute-done((bf16[2,2,96,1856]{3,2,1,0:T(8,128)(2,1)S(1)}, bf16[2,2,96,1856]{3,2,1,0:T(8,128)(2,1)}, u32[]{:S(2)}, u32[]{:S(2)}) %collective-permute-start.10) | collective-permute-done | bytes 1425440 | tf_op jit(solution)/shard_map/ppermute | solution.py:656
  340.2 1.7 add_convert_fusion.3
  342.2 2.0 collective-permute-start.12
  344.2 1.9 collective-permute-done.12
  346.2 2.7 collective-permute-start.13
  348.9 3.9 collective-permute-done.13
  354.1 6.0 %collective-permute-done.11 = bf16[1,2,96,1856]{3,2,1,0:T(8,128)(2,1)S(1)} collective-permute-done((bf16[1,2,96,1856]{3,2,1,0:T(8,128)(2,1)S(1)}, bf16[1,2,96,1856]{3,2,1,0:T(8,128)(2,1)S(1)}, u32[]{:S(2)}, u32[]{:S(2)}) %collective-permute-start.11) | collective-permute-done | bytes 712736 | tf_op jit(solution)/shard_map/ppermute | solution.py:656
  360.3 1.7 fusion.7
  362.1 1.4 pad_maximum_fusion.1
  364.3 1.2 add_convert_fusion.1
  365.7 2.0 collective-permute-done.14
  367.9 9.0 %collective-permute-done.15 = bf16[2,96,768]{2,1,0:T(8,128)(2,1)S(1)} collective-permute-done((bf16[2,96,768]{2,1,0:T(8,128)(2,1)S(1)}, bf16[2,96,768]{2,1,0:T(8,128)(2,1)S(1)}, u32[]{:S(2)}, u32[]{:S(2)}) %collective-permute-start.15) | collective-permute-done | bytes 294944 | tf_op jit(solution)/shard_map/ppermute | solution.py:656
  378.3 3.9 collective-permute-done.16
  383.0 1.7 finish_heads.1
  386.8 2.4 fusion.2
  389.2 9.3 %reduce-scatter.6.cloned.1.call-done = bf16[1,96,1856]{2,1,0:T(8,128)(2,1)} async-done(((bf16[4,96,1856]{2,1,0:T(8,128)(2,1)}), bf16[1,96,1856]{2,1,0:T(8,128)(2,1)}) %reduce-scatter.6.cloned.1.call-update) | async-done | bytes 356368 | tf_op jit(solution)/shard_map/reduce_scatter | solution.py:865
  398.6 1.9 finish_dense.1
  400.4 2.0 slice_bitcast_fusion.1
  402.4 1.3 slice_bitcast_fusion
  (166 shorter events, 26.1 us)
Async XLA Ops:
  7.2 4.3 %copy-start.18 = (s32[1,512]{1,0:T(1,128)S(1)}, s32[1,512]{1,0:T(1,128)}, u32[]{:S(2)}) copy-start(s32[1,512]{1,0:T(1,128)} %param.22) | copy-start | bytes 6148
  7.2 9.2 %copy-start.14 = (bf16[192,96]{1,0:T(8,128)(2,1)S(1)}, bf16[192,96]{1,0:T(8,128)(2,1)}, u32[]{:S(2)}) copy-start(bf16[192,96]{1,0:T(8,128)(2,1)} %param.28) | copy-start | bytes 110596
  7.2 9.3 %copy-start.13 = (bf16[768,96]{0,1:T(8,128)(2,1)S(1)}, bf16[768,96]{0,1:T(8,128)(2,1)}, u32[]{:S(2)}) copy-start(bf16[768,96]{0,1:T(8,128)(2,1)} %param.30) | copy-start | bytes 442372
  7.2 9.3 %copy-start.12 = (bf16[96,768]{1,0:T(8,128)(2,1)S(1)}, bf16[96,768]{1,0:T(8,128)(2,1)}, u32[]{:S(2)}) copy-start(bf16[96,768]{1,0:T(8,128)(2,1)} %param.29) | copy-start | bytes 442372
  7.2 104.0 %all-gather.5.cloned.1.call-start = ((), (), s32[]{:S(2)}) async-start(), calls=%async_computation.10 | async-start | bytes 3932160 | tf_op jit(solution)/shard_map/all_gather | solution.py:719
  8.0 162.7 %all-gather.7.cloned.1.call-start = ((), (), s32[]{:S(2)}) async-start(), calls=%async_computation.11 | async-start | bytes 6193152 | tf_op jit(solution)/shard_map/all_gather | solution.py:744
  11.0 2.4 collective-permute-start.2
  13.8 12.3 %collective-permute-start.3 = (bf16[192,768]{0,1:T(8,128)(2,1)S(1)}, bf16[192,768]{0,1:T(8,128)(2,1)S(1)}, u32[]{:S(2)}, u32[]{:S(2)}) collective-permute-start(bf16[192,768]{0,1:T(8,128)(2,1)S(1)} %maximum_select_fusion.2), channel_id=1, source_target_pairs={{0,8},{4,12},{8,0},{12,4},{16,24},{20,28},{24,16},{28,20},{1,9},{5... | collective-permute-start | bytes 884744 | tf_op jit(solution)/shard_map/ppermute | solution.py:656
  16.7 25.5 %collective-permute-start = (bf16[1,96,1792]{2,1,0:T(8,128)(2,1)S(1)}, bf16[1,96,1792]{2,1,0:T(8,128)(2,1)S(1)}, u32[]{:S(2)}, u32[]{:S(2)}) collective-permute-start(bf16[1,96,1792]{2,1,0:T(8,128)(2,1)S(1)} %bitcast.86), channel_id=1, source_target_pairs={{0,1},{1,0},{2,3},{3,2},{4,5},{5,4},{6,7},{7,6},{8,9},{9,8},{10,11... | collective-permute-start | bytes 1032200 | tf_op jit(solution)/shard_map/ppermute | solution.py:656
  26.6 21.0 %collective-permute-start.4 = (bf16[384,768]{0,1:T(8,128)(2,1)S(1)}, bf16[384,768]{0,1:T(8,128)(2,1)}, u32[]{:S(2)}, u32[]{:S(2)}) collective-permute-start(bf16[384,768]{0,1:T(8,128)(2,1)S(1)} %maximum_select_fusion.1), channel_id=1, source_target_pairs={{0,16},{4,20},{8,24},{12,28},{16,0},{20,4},{24,8},{28,12},{1,17},{... | collective-permute-start | bytes 1769480 | tf_op jit(solution)/shard_map/ppermute | solution.py:656
  42.3 13.3 %collective-permute-start.1 = (bf16[2,96,1792]{2,1,0:T(8,128)(2,1)S(1)}, bf16[2,96,1792]{2,1,0:T(8,128)(2,1)S(1)}, u32[]{:S(2)}, u32[]{:S(2)}) collective-permute-start(bf16[2,96,1792]{2,1,0:T(8,128)(2,1)S(1)} %pad_maximum_fusion.3), channel_id=1, source_target_pairs={{0,8},{4,12},{8,0},{12,4},{16,24},{20,28},{24,16},{28,20},{1,9},{5... | collective-permute-start | bytes 2064392 | tf_op jit(solution)/shard_map/ppermute | solution.py:656
  42.4 40.1 %collective-permute-start.5 = (bf16[1,96,1792]{2,1,0:T(8,128)(2,1)S(1)}, bf16[1,96,1792]{2,1,0:T(8,128)(2,1)S(1)}, u32[]{:S(2)}, u32[]{:S(2)}) collective-permute-start(bf16[1,96,1792]{2,1,0:T(8,128)(2,1)S(1)} %bitcast.88), channel_id=1, source_target_pairs={{0,2},{1,3},{2,0},{3,1},{4,6},{5,7},{6,4},{7,5},{8,10},{9,11},{10,... | collective-permute-start | bytes 1032200 | tf_op jit(solution)/shard_map/ppermute | solution.py:656
  82.5 28.4 %collective-permute-start.7 = (bf16[4,96,1792]{2,1,0:T(8,128)(2,1)S(1)}, bf16[4,96,1792]{2,1,0:T(8,128)(2,1)S(1)}, u32[]{:S(2)}, u32[]{:S(2)}) collective-permute-start(bf16[4,96,1792]{2,1,0:T(8,128)(2,1)S(1)} %pad_maximum_fusion.2), channel_id=1, source_target_pairs={{0,16},{4,20},{8,24},{12,28},{16,0},{20,4},{24,8},{28,12},{1,17},{... | collective-permute-start | bytes 4128776 | tf_op jit(solution)/shard_map/ppermute | solution.py:656
  84.0 27.2 %collective-permute-start.6 = (bf16[1,96,1792]{2,1,0:T(8,128)(2,1)S(1)}, bf16[1,96,1792]{2,1,0:T(8,128)(2,1)}, u32[]{:S(2)}, u32[]{:S(2)}) collective-permute-start(bf16[1,96,1792]{2,1,0:T(8,128)(2,1)S(1)} %collective-permute-done), channel_id=1, source_target_pairs={{0,2},{1,3},{2,0},{3,1},{4,6},{5,7},{6,4},{7,5},{8,10},{9,11},{10,... | collective-permute-start | bytes 1032200 | tf_op jit(solution)/shard_map/ppermute | solution.py:656
  111.2 41.3 %copy-start.1 = (bf16[8,96,1792]{2,1,0:T(8,128)(2,1)}, bf16[8,96,1792]{2,1,0:T(8,128)(2,1)S(1)}, u32[]{:S(2)}) copy-start(bf16[8,96,1792]{2,1,0:T(8,128)(2,1)S(1)} %pad_maximum_fusion.refs_0_) | copy-start | bytes 8257540
  113.4 29.9 %collective-permute-start.8 = (bf16[8,96,1792]{2,1,0:T(8,128)(2,1)S(1)}, bf16[8,96,1792]{2,1,0:T(8,128)(2,1)}, u32[]{:S(2)}, u32[]{:S(2)}) collective-permute-start(bf16[8,96,1792]{2,1,0:T(8,128)(2,1)S(1)} %pad_maximum_fusion.refs_0_), channel_id=1, source_target_pairs={{0,4},{4,0},{8,12},{12,8},{16,20},{20,16},{24,28},{28,24},{1,5},{5... | collective-permute-start | bytes 8257544 | tf_op jit(solution)/shard_map/ppermute | solution.py:656
  123.5 26.9 %copy-start.21 = (bf16[768]{0:T(1024)(128)(2,1)S(1)}, bf16[768]{0:T(1024)(128)(2,1)}, u32[]{:S(2)}) copy-start(bf16[768]{0:T(1024)(128)(2,1)} %param.33) | copy-start | bytes 4612
  123.5 26.9 %copy-start.22 = (bf16[768]{0:T(1024)(128)(2,1)S(1)}, bf16[768]{0:T(1024)(128)(2,1)}, u32[]{:S(2)}) copy-start(bf16[768]{0:T(1024)(128)(2,1)} %param.36) | copy-start | bytes 4612
  123.5 27.0 %copy-start.23 = (bf16[768]{0:T(1024)(128)(2,1)S(1)}, bf16[768]{0:T(1024)(128)(2,1)}, u32[]{:S(2)}) copy-start(bf16[768]{0:T(1024)(128)(2,1)} %param.37) | copy-start | bytes 4612
  123.5 27.0 %copy-start.24 = (bf16[768]{0:T(1024)(128)(2,1)S(1)}, bf16[768]{0:T(1024)(128)(2,1)}, u32[]{:S(2)}) copy-start(bf16[768]{0:T(1024)(128)(2,1)} %param.35) | copy-start | bytes 4612
  123.5 27.0 %copy-start.25 = (bf16[768]{0:T(1024)(128)(2,1)S(1)}, bf16[768]{0:T(1024)(128)(2,1)}, u32[]{:S(2)}) copy-start(bf16[768]{0:T(1024)(128)(2,1)} %param.38) | copy-start | bytes 4612
  123.6 27.0 %copy-start.26 = (bf16[768]{0:T(1024)(128)(2,1)S(1)}, bf16[768]{0:T(1024)(128)(2,1)}, u32[]{:S(2)}) copy-start(bf16[768]{0:T(1024)(128)(2,1)} %param.39) | copy-start | bytes 4612
  123.6 27.7 %copy-start.19 = (bf16[3072]{0:T(1024)(128)(2,1)S(1)}, bf16[3072]{0:T(1024)(128)(2,1)}, u32[]{:S(2)}) copy-start(bf16[3072]{0:T(1024)(128)(2,1)} %param.34) | copy-start | bytes 18436
  143.3 28.4 %all-to-all-start = ((bf16[4,384,128]{2,1,0:T(8,128)(2,1)}), bf16[4,384,128]{2,1,0:T(8,128)(2,1)S(1)}, u32[]{:S(2)}, u32[]{:S(2)}) async-start(bf16[4,384,128]{2,1,0:T(8,128)(2,1)} %get-tuple-element.104.refs_3_), calls=%async_computation | async-start | bytes 786432 | tf_op jit(solution)/shard_map/all_to_all | solution.py:764
  171.7 7.0 %copy-start.6 = (bf16[4,384,128]{2,1,0:T(8,128)(2,1)}, bf16[4,384,128]{2,1,0:T(8,128)(2,1)S(1)}, u32[]{:S(2)}) copy-start(bf16[4,384,128]{2,1,0:T(8,128)(2,1)S(1)} %all-to-all-done.ctx_ref.refs_10_) | copy-start | bytes 1179652
  171.7 24.5 %all-to-all-start.1 = ((bf16[4,384,128]{2,1,0:T(8,128)(2,1)}), bf16[4,384,128]{2,1,0:T(8,128)(2,1)S(1)}, u32[]{:S(2)}, u32[]{:S(2)}) async-start(bf16[4,384,128]{2,1,0:T(8,128)(2,1)} %get-tuple-element.106.refs_3_), calls=%async_computation.1 | async-start | bytes 786432 | tf_op jit(solution)/shard_map/all_to_all | solution.py:764
  196.2 5.2 %copy-start.8 = (bf16[4,384,128]{2,1,0:T(8,128)(2,1)}, bf16[4,384,128]{2,1,0:T(8,128)(2,1)S(1)}, u32[]{:S(2)}) copy-start(bf16[4,384,128]{2,1,0:T(8,128)(2,1)S(1)} %all-to-all-done.1.ctx_ref.refs_11_) | copy-start | bytes 1179652
  196.2 24.2 %all-to-all-start.2 = ((bf16[4,384,128]{2,1,0:T(8,128)(2,1)}), bf16[4,384,128]{2,1,0:T(8,128)(2,1)S(1)}, u32[]{:S(2)}, u32[]{:S(2)}) async-start(bf16[4,384,128]{2,1,0:T(8,128)(2,1)} %get-tuple-element.108), calls=%async_computation.2 | async-start | bytes 786432 | tf_op jit(solution)/shard_map/all_to_all | solution.py:764
  201.3 17.5 %copy-start.16 = (f32[8,768]{1,0:T(8,128)S(1)}, f32[8,768]{1,0:T(8,128)}, u32[]{:S(2)}) copy-start(f32[8,768]{1,0:T(8,128)} %get-tuple-element.131) | copy-start | bytes 73732
  201.3 18.3 %copy-start.17 = (f32[4,1,768]{2,1,0:T(1,128)S(1)}, f32[4,1,768]{2,1,0:T(1,128)}, u32[]{:S(2)}) copy-start(f32[4,1,768]{2,1,0:T(1,128)} %get-tuple-element.133) | copy-start | bytes 36868
  201.3 159.0 %reduce-scatter.4.cloned.1.call-start = ((), (), s32[]{:S(2)}) async-start(), calls=%async_computation.7 | async-start | bytes 6635520 | tf_op jit(solution)/shard_map/reduce_scatter | solution.py:822
  220.4 13.7 %copy-start.7 = (bf16[4,384,128]{2,1,0:T(8,128)(2,1)}, bf16[4,384,128]{2,1,0:T(8,128)(2,1)S(1)}, u32[]{:S(2)}) copy-start(bf16[4,384,128]{2,1,0:T(8,128)(2,1)S(1)} %all-to-all-done.2.refs_4_) | copy-start | bytes 1179652
  234.1 33.3 %all-to-all-start.3 = ((bf16[4,384,128]{2,1,0:T(8,128)(2,1)}), bf16[4,384,128]{2,1,0:T(8,128)(2,1)S(1)}, u32[]{:S(2)}, u32[]{:S(2)}) async-start(bf16[4,384,128]{2,1,0:T(8,128)(2,1)} %get-tuple-element.140), calls=%async_computation.3 | async-start | bytes 786432 | tf_op jit(solution)/shard_map/all_to_all | solution.py:764
  239.1 147.6 %reduce-scatter.8.cloned.1.call-start = ((), (), s32[]{:S(2)}) async-start(), calls=%async_computation.9 | async-start | bytes 3932160 | tf_op jit(solution)/shard_map/reduce_scatter | solution.py:844
  239.1 63.5 %collective-permute-start.9 = (bf16[4,2,96,1856]{3,2,1,0:T(8,128)(2,1)}, bf16[4,2,96,1856]{3,2,1,0:T(8,128)(2,1)}, u32[]{:S(2)}, u32[]{:S(2)}) collective-permute-start(bf16[4,2,96,1856]{3,2,1,0:T(8,128)(2,1)} %bitcast.116), channel_id=1, source_target_pairs={{0,4},{4,0},{8,12},{12,8},{16,20},{20,16},{24,28},{28,24},{1,5},{5... | collective-permute-start | bytes 8552456 | tf_op jit(solution)/shard_map/ppermute | solution.py:656
  268.1 26.2 %copy-start.3 = (bf16[768,768]{0,1:T(8,128)(2,1)S(1)}, bf16[768,768]{0,1:T(8,128)(2,1)}, u32[]{:S(2)}) copy-start(bf16[768,768]{0,1:T(8,128)(2,1)} %maximum_select_fusion) | copy-start | bytes 3538948
  300.6 98.0 %reduce-scatter.6.cloned.1.call-start = ((), (), s32[]{:S(2)}) async-start(), calls=%async_computation.8 | async-start | bytes 1843200 | tf_op jit(solution)/shard_map/reduce_scatter | solution.py:865
  305.2 35.0 %collective-permute-start.10 = (bf16[2,2,96,1856]{3,2,1,0:T(8,128)(2,1)S(1)}, bf16[2,2,96,1856]{3,2,1,0:T(8,128)(2,1)}, u32[]{:S(2)}, u32[]{:S(2)}) collective-permute-start(bf16[2,2,96,1856]{3,2,1,0:T(8,128)(2,1)S(1)} %get-tuple-element.150), channel_id=1, source_target_pairs={{0,8},{4,12},{8,0},{12,4},{16,24},{20,28},{24,16},{28,20},{1,9},{5... | collective-permute-start | bytes 4276232 | tf_op jit(solution)/shard_map/ppermute | solution.py:656
  341.9 18.3 %collective-permute-start.11 = (bf16[1,2,96,1856]{3,2,1,0:T(8,128)(2,1)S(1)}, bf16[1,2,96,1856]{3,2,1,0:T(8,128)(2,1)S(1)}, u32[]{:S(2)}, u32[]{:S(2)}) collective-permute-start(bf16[1,2,96,1856]{3,2,1,0:T(8,128)(2,1)S(1)} %get-tuple-element.155), channel_id=1, source_target_pairs={{0,16},{4,20},{8,24},{12,28},{16,0},{20,4},{24,8},{28,12},{1,17},{... | collective-permute-start | bytes 2138120 | tf_op jit(solution)/shard_map/ppermute | solution.py:656
  342.2 3.9 collective-permute-start.12
  346.2 6.7 %collective-permute-start.13 = (f32[2,384]{1,0:T(2,128)S(1)}, f32[2,384]{1,0:T(2,128)S(1)}, u32[]{:S(2)}, u32[]{:S(2)}) collective-permute-start(f32[2,384]{1,0:T(2,128)S(1)} %maximum_select_fusion.4), channel_id=1, source_target_pairs={{0,2},{1,3},{2,0},{3,1},{4,6},{5,7},{6,4},{7,5},{8,10},{9,11},{10,... | collective-permute-start | bytes 9224 | tf_op jit(solution)/shard_map/ppermute | solution.py:656
  365.5 2.1 collective-permute-start.14
  365.6 11.8 %copy-start.10 = (bf16[256,768]{1,0:T(8,128)(2,1)S(1)}, bf16[256,768]{1,0:T(8,128)(2,1)}, u32[]{:S(2)}) copy-start(bf16[256,768]{1,0:T(8,128)(2,1)} %get-tuple-element.105) | copy-start | bytes 1179652
  365.6 11.8 %copy-start.11 = (bf16[256,768]{1,0:T(8,128)(2,1)S(1)}, bf16[256,768]{1,0:T(8,128)(2,1)}, u32[]{:S(2)}) copy-start(bf16[256,768]{1,0:T(8,128)(2,1)} %get-tuple-element.107) | copy-start | bytes 1179652
  367.8 9.1 %collective-permute-start.15 = (bf16[2,96,768]{2,1,0:T(8,128)(2,1)S(1)}, bf16[2,96,768]{2,1,0:T(8,128)(2,1)S(1)}, u32[]{:S(2)}, u32[]{:S(2)}) collective-permute-start(bf16[2,96,768]{2,1,0:T(8,128)(2,1)S(1)} %dynamic-slice_bitcast_fusion.1), channel_id=1, source_target_pairs={{0,8},{4,12},{8,0},{12,4},{16,24},{20,28},{24,16},{28,20},{1,9},{5... | collective-permute-start | bytes 884744 | tf_op jit(solution)/shard_map/ppermute | solution.py:656
  377.0 9.8 %copy-start.4 = (f32[256,768]{1,0:T(8,128)S(1)}, f32[256,768]{1,0:T(8,128)}, u32[]{:S(2)}) copy-start(f32[256,768]{1,0:T(8,128)} %get-tuple-element.160) | copy-start | bytes 2359300
  377.0 9.8 %copy-start.5 = (f32[256,768]{1,0:T(8,128)S(1)}, f32[256,768]{1,0:T(8,128)}, u32[]{:S(2)}) copy-start(f32[256,768]{1,0:T(8,128)} %get-tuple-element.161) | copy-start | bytes 2359300
  377.0 5.2 %collective-permute-start.16 = (bf16[1,96,768]{2,1,0:T(8,128)(2,1)S(1)}, bf16[1,96,768]{2,1,0:T(8,128)(2,1)S(1)}, u32[]{:S(2)}, u32[]{:S(2)}) collective-permute-start(bf16[1,96,768]{2,1,0:T(8,128)(2,1)S(1)} %constant_dynamic-slice_fusion), channel_id=1, source_target_pairs={{0,16},{4,20},{8,24},{12,28},{16,0},{20,4},{24,8},{28,12},{1,17},{... | collective-permute-start | bytes 442376 | tf_op jit(solution)/shard_map/ppermute | solution.py:656
  (5 other events, 10.5 us)
Sparse Core Ops, SparseCore 0:
  9.6 92.4 all-gather.4
  113.5 44.3 all-gather.6
  234.2 64.1 reduce-scatter.3
  300.7 61.7 reduce-scatter.7
  364.7 33.7 reduce-scatter.5

commit v10 on v9

--- a/solution.py
+++ b/solution.py
@@ -371,34 +371,42 @@
     parts, _, head_cols = w_out.shape
     hidden_cols = w_in.shape[2]
     index = place_ref[parts]
+    step = pl.program_id(0)
     groups = (
         (2 * hidden_cols, head_cols, w_out),
         (0, hidden_cols, w_in),
         (hidden_cols, hidden_cols, w_up),
     )
-    for group, (start, size, target) in enumerate(groups):
-        for piece, marked in zip(pieces, marks):
-            block = piece.shape[1]
-            for at, (slot, turn, relative) in enumerate(marked):
-                offset = pl.multiple_of((index ^ turn) * block, block) if relative else turn * block
-                pltpu.make_async_copy(
-                    piece.at[at, :, pl.ds(start, size)],
-                    target.at[slot, pl.ds(offset, block), :],
-                    sems.at[group, slot],
-                ).start()
+
+    @pl.when(step == 0)
+    def _():
+        for group, (start, size, target) in enumerate(groups):
+            for piece, marked in zip(pieces, marks):
+                block = piece.shape[1]
+                for at, (slot, turn, relative) in enumerate(marked):
+                    offset = pl.multiple_of((index ^ turn) * block, block) if relative else turn * block
+                    pltpu.make_async_copy(
+                        piece.at[at, :, pl.ds(start, size)],
+                        target.at[slot, pl.ds(offset, block), :],
+                        sems.at[group, slot],
+                    ).start()
+        sums_ref[...] = jnp.zeros_like(sums_ref)
+        inner_sums_ref[...] = jnp.zeros_like(inner_sums_ref)
 
     def arrive(group, slot):
         whole = groups[group][2].at[slot]
-        pltpu.make_async_copy(whole, whole, sems.at[group, slot]).wait()
+
+        @pl.when(step == 0)
+        def _():
+            pltpu.make_async_copy(whole, whole, sems.at[group, slot]).wait()
 
     def vec(which):
         return vec_ref[which : which + 1, :]
 
-    inner_sums_ref[...] = jnp.zeros_like(inner_sums_ref)
     attention = jnp.zeros(in_ref.shape, F32)
     for slot in range(parts):
         arrive(0, slot)
-        attention = attention + dot(unpack(ctx_ref[place_ref[slot]]), w_out[slot, :, : 3 * DH], NT)
+        attention = attention + dot(unpack(ctx_ref[place_ref[slot], 0]), w_out[slot, :, : 3 * DH], NT)
     first_exact, normed_one, inverse_one = norm_forward(
         in_ref[...].astype(F32) + attention + vec(0), vec(1), vec(2)
     )
@@ -425,16 +433,16 @@
     second_grad = norm_backward(out_grad, normed_two, inverse_two, vec(4))
     branch_grad = second_grad.astype(BF16)
     branch_grad_ref[...] = branch_grad
-    sums_ref[0:1, :] = column_sum(weighted * misfit)
-    sums_ref[1:2, :] = column_sum(branch_grad.astype(F32))
-    sums_ref[2:3, :] = column_sum(out_grad * normed_two)
-    sums_ref[3:4, :] = column_sum(out_grad)
+    sums_ref[0:1, :] += column_sum(weighted * misfit)
+    sums_ref[1:2, :] += column_sum(branch_grad.astype(F32))
+    sums_ref[2:3, :] += column_sum(out_grad * normed_two)
+    sums_ref[3:4, :] += column_sum(out_grad)
 
     def down(slot, back):
         t = place_ref[slot]
         hidden_grad = (dot(branch_grad, w_up[slot]) * slope[slot]).astype(BF16)
         hidden_grad_ref[t] = hidden_grad
-        inner_sums_ref[t] = column_sum(hidden_grad.astype(F32))
+        inner_sums_ref[t] += column_sum(hidden_grad.astype(F32))
         return back + dot(hidden_grad, w_in[slot], NT)
 
     upstream = lax.fori_loop(0, parts, down, second_grad)
@@ -442,61 +450,75 @@
     first_grad_ref[...] = first_grad
     attn_grad = first_grad.astype(BF16)
     attn_grad_ref[...] = attn_grad
-    sums_ref[4:5, :] = column_sum(attn_grad.astype(F32))
-    sums_ref[5:6, :] = column_sum(upstream * normed_one)
-    sums_ref[6:7, :] = column_sum(upstream)
-    sums_ref[7:8, :] = jnp.zeros_like(sums_ref[7:8, :])
+    sums_ref[4:5, :] += column_sum(attn_grad.astype(F32))
+    sums_ref[5:6, :] += column_sum(upstream * normed_one)
+    sums_ref[6:7, :] += column_sum(upstream)
     middle = BLOCK // 2
     for slot in range(parts):
         back = dot(attn_grad, w_out[slot, :, : 3 * DH]).astype(BF16)
-        ctx_grad_ref[place_ref[slot]] = pack(
+        ctx_grad_ref[place_ref[slot], 0] = pack(
             back[:, : 2 * DH], back[:middle, 2 * DH :], back[middle:, 2 * DH :]
         )
 
 
-def run_dense(half, marks, place, ratio, ctx, rows_in, teacher, cotangent, valid, vecs, inner_bias, pieces):
-    parts = ctx.shape[0]
-    width = rows_in.shape[1]
+def run_dense(marks, place, ratio, ctx, rows_in, teacher, cotangent, valid, vecs, inner_bias, pieces):
+    parts, halves = ctx.shape[:2]
+    part_len, width = rows_in.shape
     hidden_cols = inner_bias.shape[2]
     out_cols = pieces[0].shape[2] - 2 * hidden_cols
 
-    def mine(columns):
-        return pl.BlockSpec((BLOCK, columns), lambda i: (half, 0))
+    def by_rows(columns):
+        return pl.BlockSpec((BLOCK, columns), lambda i: (i, 0))
+
+    def by_part(columns):
+        return pl.BlockSpec((parts, BLOCK, columns), lambda i: (0, i, 0))
 
     def fixed(shape):
         return pl.BlockSpec(shape, lambda i: (0,) * len(shape))
 
-    low = jax.ShapeDtypeStruct((BLOCK, width), BF16)
-    out_shape = (
-        low,
-        jax.ShapeDtypeStruct((BLOCK, width), F32),
-        jax.ShapeDtypeStruct(ctx.shape, BF16),
-        low,
-        low,
-        low,
-        jax.ShapeDtypeStruct((parts, BLOCK, hidden_cols), BF16),
-        jax.ShapeDtypeStruct((parts, BLOCK, hidden_cols), BF16),
-        jax.ShapeDtypeStruct((8, width), F32),
-        jax.ShapeDtypeStruct((parts, 1, hidden_cols), F32),
-    )
+    packed = pl.BlockSpec((parts, 1) + ctx.shape[2:], lambda i: (0, i, 0, 0))
+    low = jax.ShapeDtypeStruct((part_len, width), BF16)
+    wide = jax.ShapeDtypeStruct((parts, part_len, hidden_cols), BF16)
     smem = pl.BlockSpec(memory_space=pltpu.SMEM)
     return pl.pallas_call(
         functools.partial(dense_chain, marks),
-        out_shape=out_shape,
-        grid=(1,),
+        out_shape=(
+            low,
+            jax.ShapeDtypeStruct((part_len, width), F32),
+            jax.ShapeDtypeStruct(ctx.shape, BF16),
+            low,
+            low,
+            low,
+            wide,
+            wide,
+            jax.ShapeDtypeStruct((8, width), F32),
+            jax.ShapeDtypeStruct((parts, 1, hidden_cols), F32),
+        ),
+        grid=(halves,),
         in_specs=[
             smem,
             smem,
-            fixed(ctx.shape),
-            mine(width),
-            mine(width),
-            mine(width),
-            mine(1),
+            packed,
+            by_rows(width),
+            by_rows(width),
+            by_rows(width),
+            by_rows(1),
             fixed(vecs.shape),
             fixed(inner_bias.shape),
         ]
         + [pl.BlockSpec(memory_space=pl.ANY)] * len(pieces),
-        out_specs=tuple(fixed(out.shape) for out in out_shape),
+        out_specs=(
+            by_rows(width),
+            by_rows(width),
+            packed,
+            by_rows(width),
+            by_rows(width),
+            by_rows(width),
+            by_part(hidden_cols),
+            by_part(hidden_cols),
+            fixed((8, width)),
+            fixed((parts, 1, hidden_cols)),
+        ),
         scratch_shapes=[
             pltpu.VMEM((parts, width, out_cols), BF16),
             pltpu.VMEM((parts, width, hidden_cols), BF16),
@@ -508,36 +530,31 @@
             dimension_semantics=("arbitrary",), vmem_limit_bytes=VMEM_LIMIT
         ),
         cost_estimate=pl.CostEstimate(
-            flops=BLOCK * width * (8 * hidden_cols + 4 * out_cols) * parts,
-            bytes_accessed=18 << 20,
-            transcendentals=2 * BLOCK * hidden_cols * parts,
+            flops=part_len * width * (8 * hidden_cols + 4 * out_cols) * parts,
+            bytes_accessed=24 << 20,
+            transcendentals=2 * part_len * hidden_cols * parts,
         ),
         name="dense_chain",
     )(place, ratio, ctx, rows_in, teacher, cotangent, valid, vecs, inner_bias, *pieces)
 
 
-def dense_weights(plans, halves, place_ref, *refs):
-    firsts, branch_grads, attn_grads, acts, hidden_grads, ctxs = (
-        refs[k * halves : (k + 1) * halves] for k in range(6)
-    )
-    notes_ref, outs = refs[6 * halves], refs[6 * halves + 1 : -3]
-    turned, whole, sems = refs[-3:]
+def dense_weights(
+    plans, place_ref, first_ref, branch_grad_ref, attn_grad_ref, act_ref, hidden_grad_ref, ctx_ref,
+    notes_ref, *refs
+):
+    outs, (turned, whole, sems) = refs[:-3], refs[-3:]
     step = pl.program_id(0)
     slots = whole.shape[0]
 
     @pl.when(step == 0)
     def _():
-        for which, sources in enumerate((firsts, branch_grads, attn_grads)):
-            for half, source in enumerate(sources):
-                turned[which, :, half * BLOCK : (half + 1) * BLOCK] = jnp.transpose(source[...])
-
-    def both(sources):
-        return jnp.concatenate([source[0] for source in sources], axis=0)
-
-    hidden_cols = acts[0].shape[2]
-    whole[step, :, :hidden_cols] = dot(turned[0], both(hidden_grads)).astype(BF16)
-    whole[step, :, hidden_cols : 2 * hidden_cols] = dot(turned[1], both(acts)).astype(BF16)
-    ctx = jnp.concatenate([unpack(source[0]) for source in ctxs], axis=0)
+        for which, source in enumerate((first_ref, branch_grad_ref, attn_grad_ref)):
+            turned[which] = jnp.transpose(source[...])
+
+    hidden_cols = act_ref.shape[2]
+    whole[step, :, :hidden_cols] = dot(turned[0], hidden_grad_ref[0]).astype(BF16)
+    whole[step, :, hidden_cols : 2 * hidden_cols] = dot(turned[1], act_ref[0]).astype(BF16)
+    ctx = jnp.concatenate([unpack(ctx_ref[0, half]) for half in range(ctx_ref.shape[1])], axis=0)
     plain = 2 * hidden_cols + ctx.shape[1]
     whole[step, :, 2 * hidden_cols : plain] = dot(turned[2], ctx).astype(BF16)
     whole[step, :, plain : plain + notes_ref.shape[1]] = notes_ref[...]
@@ -562,34 +579,35 @@
             pltpu.make_async_copy(whole.at[slot], whole.at[slot], sems.at[slot]).wait()
 
 
-def run_weights(plans, place, notes, firsts, branch_grads, attn_grads, acts, hidden_grads, ctxs):
-    parts, _, hidden_cols = acts[0].shape
-    halves = len(acts)
-    width = firsts[0].shape[1]
+def run_weights(plans, place, notes, first, branch_grad, attn_grad, act, hidden_grad, ctx):
+    parts, part_len, hidden_cols = act.shape
+    width = first.shape[1]
     columns = 2 * hidden_cols + 3 * DH + notes.shape[1]
-
-    def by_slot(rows, size):
-        return pl.BlockSpec((1, rows, size), lambda s, place: (place[s], 0, 0))
-
-    fixed = pl.BlockSpec((BLOCK, width), lambda s, place: (0, 0))
+    fixed = pl.BlockSpec((part_len, width), lambda s, place: (0, 0))
+    by_slot = pl.BlockSpec((1, part_len, hidden_cols), lambda s, place: (place[s], 0, 0))
     outs = tuple(
         jax.ShapeDtypeStruct((len(turns) * (stop - start), block, columns), BF16)
         for start, stop, block, turns in plans
     )
     inner = tuple((start, stop, turns) for start, stop, _, turns in plans)
     return pl.pallas_call(
-        functools.partial(dense_weights, inner, halves),
+        functools.partial(dense_weights, inner),
         out_shape=outs,
         grid_spec=pltpu.PrefetchScalarGridSpec(
             num_scalar_prefetch=1,
             grid=(parts,),
-            in_specs=[fixed] * (3 * halves)
-            + [by_slot(BLOCK, hidden_cols)] * (2 * halves)
-            + [by_slot(PACKED, 2 * DH)] * halves
-            + [pl.BlockSpec(notes.shape, lambda s, place: (0, 0))],
+            in_specs=[
+                fixed,
+                fixed,
+                fixed,
+                by_slot,
+                by_slot,
+                pl.BlockSpec((1,) + ctx.shape[1:], lambda s, place: (place[s], 0, 0, 0)),
+                pl.BlockSpec(notes.shape, lambda s, place: (0, 0)),
+            ],
             out_specs=tuple(pl.BlockSpec(memory_space=pl.ANY) for _ in outs),
             scratch_shapes=[
-                pltpu.VMEM((3, width, halves * BLOCK), BF16),
+                pltpu.VMEM((3, width, part_len), BF16),
                 pltpu.VMEM((parts, width, columns), BF16),
                 pltpu.SemaphoreType.DMA((parts,)),
             ],
@@ -598,12 +616,12 @@
             dimension_semantics=("arbitrary",), vmem_limit_bytes=VMEM_LIMIT
         ),
         cost_estimate=pl.CostEstimate(
-            flops=2 * halves * BLOCK * width * columns * parts,
+            flops=2 * part_len * width * columns * parts,
             bytes_accessed=20 << 20,
             transcendentals=0,
         ),
         name="dense_weights",
-    )(place, *firsts, *branch_grads, *attn_grads, *acts, *hidden_grads, *ctxs, notes)
+    )(place, first, branch_grad, attn_grad, act, hidden_grad, ctx, notes)
 
 
 def finish_dense(packed_ref, inner_ref, outer_ref, output_ref, notes_ref):
@@ -731,16 +749,14 @@
     if paired:
         place = jnp.stack([rank, rank ^ 1, rank ^ 2, rank ^ 3, lax.axis_index("dp")]).astype(jnp.int32)
         pair = jnp.concatenate([mine[None], swap(mine[None], "tensor", 1)], axis=0)
-        far = [swap(pair[slot : slot + 1], "tensor", 2) for slot in range(2)]
+        far = swap(pair, "tensor", 2)
         near = jnp.concatenate([pair, swap(pair, "dp", 2)], axis=0)
         turns = [0, 2, 4, 6]
         for bit in (1, 2, 4):
             w_heads = merge(w_heads, swap(w_heads, "dp", bit), "dp", bit)
-        near, w_heads, far[0] = lax.optimization_barrier((near, w_heads, far[0]))
-        near = jnp.concatenate([near, swap(near, "dp", 4)], axis=0)
-        tokens, far, near = lax.optimization_barrier((tokens, far, near))
-        near_other = swap(near, "dp", 1)
-        far = jnp.concatenate(far, axis=0)
+        near, w_heads = lax.optimization_barrier((near, w_heads))
+        near_next = swap(near, "dp", 4)
+        tokens, far, near_next = lax.optimization_barrier((tokens, far, near_next))
         weights = lax.all_gather(far, "dp", axis=0, tiled=False)
     else:
         place = jnp.asarray(list(range(parts)) + [0], jnp.int32)
@@ -761,16 +777,14 @@
     lane = rank.astype(jnp.int32).reshape(1)
 
     def exchange(packed_blocks):
-        return lax.all_to_all(packed_blocks, "tensor", 0, 0)
-
-    contexts, lses, arrived = [], [], []
-    for half in range(halves):
-        context, lse = run_forward((halves, half), lane, bounds, qkv, seg_col, seg_row)
-        if paired and half == 0:
-            context, near_other = lax.optimization_barrier((context, near_other))
-        contexts.append(context)
-        lses.append(lse)
-        arrived.append(exchange(context))
+        return lax.all_to_all(packed_blocks.reshape(parts, halves, PACKED, 2 * DH), "tensor", 0, 0)
+
+    context, lse = run_forward((1, 0), lane, bounds, qkv, seg_col, seg_row)
+    if paired:
+        near_next, context = lax.optimization_barrier((near_next, context))
+        near = jnp.concatenate([near, near_next], axis=0)
+        near_other = swap(near, "dp", 1)
+    arrived = exchange(context)
     if paired:
         weights = weights.reshape((copies * 2,) + mine.shape)
         pieces = [near, near_other, weights]
@@ -790,22 +804,15 @@
     inner_rows = inner_bias.astype(F32).reshape(parts, 1, hidden_cols)
     teacher_rows = teacher.reshape(part_len, width)
     cotangent_rows = cotangent.reshape(part_len, width)
-    chains = [
-        run_dense(
-            half, marks, place, ratio, arrived[half], rows_in, teacher_rows, cotangent_rows,
-            valid_rows, vecs, inner_rows, pieces,
-        )
-        for half in range(halves)
-    ]
     (
-        layers, first_grads, context_grads, firsts, branch_grads, attn_grads, acts, hidden_grads,
+        layer_out, first_grad, context_grad, first, branch_grad, attn_grad, activated, hidden_grad,
         dense_sums, inner_sums,
-    ) = zip(*chains)
-    head_grads = [exchange(context_grad) for context_grad in context_grads]
-    dense_sums = sum(dense_sums)
-    inner_sums = sum(inner_sums)
-    sources = (firsts, branch_grads, attn_grads, acts, hidden_grads, arrived)
-    head_grads[:-1], sources = lax.optimization_barrier((head_grads[:-1], sources))
+    ) = run_dense(
+        marks, place, ratio, arrived, rows_in, teacher_rows, cotangent_rows, valid_rows, vecs,
+        inner_rows, pieces,
+    )
+    head_grad = exchange(context_grad).reshape(context.shape)
+    sources = (first, branch_grad, attn_grad, activated, hidden_grad, arrived)
     notes = jnp.concatenate((dense_sums.reshape(-1), inner_sums.reshape(-1))).astype(BF16)
     room = -(-notes.shape[0] // (shard_rows * 128)) * 128
     notes = jnp.pad(notes, (0, shard_rows * room - notes.shape[0])).reshape(shard_rows, room)
@@ -825,17 +832,9 @@
         (packed,) = run_weights(((0, parts, width, (0,)),), place, notes, *sources)
         packed = lax.psum_scatter(packed, "dp", scatter_dimension=1, tiled=True)
 
-    earlier, before = [], []
-    for half in range(halves):
-        if paired and half == halves - 1:
-            before, head_grads[-1] = lax.optimization_barrier((before, head_grads[-1]))
-        results = run_backward(
-            (halves, half), lane, bounds, qkv, seg_col, seg_row, contexts[half], head_grads[half],
-            lses[half], earlier, before,
-        )
-        if half < halves - 1:
-            before, earlier = [results[0]], earlier + [results[1]]
-    joined_grad, sums = results
+    joined_grad, sums = run_backward(
+        (1, 0), lane, bounds, qkv, seg_col, seg_row, context, head_grad, lse, [], []
+    )
     joined_grad = joined_grad.reshape(seq_len, -1)
     attn_back = dot(joined_grad, w_heads, NT).astype(BF16)
     if paired:
@@ -871,7 +870,7 @@
         scatter_rows((head_weights + biases).astype(BF16))
     )
     biases = biases.reshape(2, width)
-    input_grad = jnp.concatenate(first_grads, axis=0) + attn_back.astype(F32)
+    input_grad = first_grad + attn_back.astype(F32)
 
     inner_grad, outer_grad, output_grad, notes = run_finish_dense(packed, hidden_cols, head_cols)
     notes = notes.reshape(-1)
@@ -881,7 +880,7 @@
 
     mse_loss = jnp.sum(total(0)) / (counted * width)
     return (
-        jnp.concatenate(layers, axis=0).reshape(1, part_len, width),
+        layer_out.reshape(1, part_len, width),
         mse_loss,
         input_grad.reshape(1, part_len, width),
         query_grad,

time: 414 us -> 413 us (level)
  waiting for transfers between devices: 144 us -> 170 us
  Pallas kernels: 143 us -> 127 us
  starting transfers between devices: 41.5 us -> 30.6 us
  local copies, waits for them, and re-layouts: 17.6 us -> 21.9 us
    all_to_all x4 -> x2, waiting for transfers between devices: 0.01 us -> 32 us  [exchange(): lax.all_to_all(packed_blocks.reshape(parts, halves, PACKED, 2 * DH), 'ten...]
    all_to_all x4 -> x2, starting transfers between devices: 21.5 us -> 7 us  [exchange(): lax.all_to_all(packed_blocks.reshape(parts, halves, PACKED, 2 * DH), 'ten...]
    pallas_call x2 -> x1, Pallas kernels: 54.4 us -> 47.3 us  [run_backward(): pl.pallas_call(functools.partial(attend_backward, which, len(qkv)), out_s...]
    ppermute x17 -> x16, waiting for transfers between devices: 134 us -> 127 us  [swap(): return lax.ppermute(value, axis, [(i, i ^ bit) for i in range(size)])]
    pallas_call x2 -> x1, Pallas kernels: 36.9 us -> 32.5 us  [run_forward(): pl.pallas_call(functools.partial(attend_forward, which), out_shape=(jax.S...]
    pallas_call x3 -> x2, Pallas kernels: 47.8 us -> 43.5 us  [the longest x1 30.7 us: run_dense(): pl.pallas_call(functools.partial(dense_chain, marks), out_shape=(low, jax...]
    ppermute x17 -> x16, starting transfers between devices: 19.6 us -> 23 us  [swap(): return lax.ppermute(value, axis, [(i, i ^ bit) for i in range(size)])]
    unnamed x59 -> x46, local copies, waits for them, and re-layouts: 6.08 us -> 8.52 us
  transfers between devices with their start and end apart: 26 -> 23, of which waited for: 13 -> 14; matrix products, arithmetic and copies ran while one was open for 13% -> 13% of each run, Pallas kernels for 31% -> 20%
where the time goes in v10:
time: 413 us; the launch traced here: 411 us
  waiting for transfers between devices  170 us (41%)
  Pallas kernels  127 us (31%)
  starting transfers between devices  30.6 us (7%)
  other arithmetic  23.6 us (6%)
  local copies, waits for them, and re-layouts  21.9 us (5%)
  matrix products  19.6 us (5%)
  between operations  18.8 us (5%)
    ppermute x16, waiting for transfers between devices, swap(): return lax.ppermute(value, axis, [(i, i ^ bit) for i in range(size)])  127 us
    pallas_call x1, Pallas kernels, run_backward(): pl.pallas_call(functools.partial(attend_backward, which, len(qkv)), out_s...  47.3 us
    pallas_call x1, Pallas kernels, run_forward(): pl.pallas_call(functools.partial(attend_forward, which), out_shape=(jax.S...  32.5 us
    all_to_all x2, waiting for transfers between devices, exchange(): lax.all_to_all(packed_blocks.reshape(parts, halves, PACKED, 2 * DH), 'ten...  32 us
    pallas_call x1, Pallas kernels, run_dense(): pl.pallas_call(functools.partial(dense_chain, marks), out_shape=(low, jax...  30.7 us
    ppermute x16, starting transfers between devices, swap(): return lax.ppermute(value, axis, [(i, i ^ bit) for i in range(size)])  23 us
    dot_general x3, matrix products, dot(): lax.dot_general(left_side, right_side, dims, preferred_element_type=F32)  19.6 us
    pallas_call x1, Pallas kernels, run_weights(): pl.pallas_call(functools.partial(dense_weights, inner), out_shape=outs, g...  12.8 us
  transfers between devices with their start and end apart: 23, of which 14 were waited for; matrix products, arithmetic and copies ran while one was open for 13% of the time, Pallas kernels for 20%

profile of v10, /device:TPU:0, one launch (start us, length us, event | category | flops | bytes accessed | tf_op | source)
XLA Modules:
  0.0 411.2 jit_solution(6931635405226077866)
XLA Ops:
  8.9 0.9 copy.86
  13.8 2.6 collective-permute-start.3
  16.7 1.6 collective-permute-start
  18.3 7.8 %collective-permute-done.3 = bf16[192,768]{0,1:T(8,128)(2,1)S(1)} collective-permute-done((bf16[192,768]{0,1:T(8,128)(2,1)S(1)}, bf16[192,768]{0,1:T(8,128)(2,1)S(1)}, u32[]{:S(2)}, u32[]{:S(2)}) %collective-permute-start.3) | collective-permute-done | bytes 294944 | tf_op jit(solution)/shard_map/ppermute | solution.py:674
  26.6 1.8 collective-permute-start.4
  28.5 13.8 %collective-permute-done = bf16[1,96,1792]{2,1,0:T(8,128)(2,1)S(1)} collective-permute-done((bf16[1,96,1792]{2,1,0:T(8,128)(2,1)S(1)}, bf16[1,96,1792]{2,1,0:T(8,128)(2,1)S(1)}, u32[]{:S(2)}, u32[]{:S(2)}) %collective-permute-start) | collective-permute-done | bytes 344096 | tf_op jit(solution)/shard_map/ppermute | solution.py:674
  42.4 1.4 maximum_select_fusion
  43.8 12.0 %collective-permute-done.1 = bf16[2,96,1792]{2,1,0:T(8,128)(2,1)} collective-permute-done((bf16[2,96,1792]{2,1,0:T(8,128)(2,1)S(1)}, bf16[2,96,1792]{2,1,0:T(8,128)(2,1)}, u32[]{:S(2)}, u32[]{:S(2)}) %collective-permute-start.1) | collective-permute-done | bytes 688160 | tf_op jit(solution)/shard_map/ppermute | solution.py:674
  55.8 1.2 pad_maximum_fusion.1
  57.0 1.7 collective-permute-start.6
  58.7 5.0 %collective-permute-start.5 = (bf16[2,96,1792]{2,1,0:T(8,128)(2,1)S(1)}, bf16[2,96,1792]{2,1,0:T(8,128)(2,1)}, u32[]{:S(2)}, u32[]{:S(2)}) collective-permute-start(bf16[2,96,1792]{2,1,0:T(8,128)(2,1)S(1)} %pad_maximum_fusion.2), channel_id=1, source_target_pairs={{0,2},{1,3},{2,0},{3,1},{4,6},{5,7},{6,4},{7,5},{8,10},{9,11},{10,... | collective-permute-start | bytes 2064392 | tf_op jit(solution)/shard_map/ppermute | solution.py:674
  63.7 41.2 %collective-permute-done.5 = bf16[2,96,1792]{2,1,0:T(8,128)(2,1)} collective-permute-done((bf16[2,96,1792]{2,1,0:T(8,128)(2,1)S(1)}, bf16[2,96,1792]{2,1,0:T(8,128)(2,1)}, u32[]{:S(2)}, u32[]{:S(2)}) %collective-permute-start.5) | collective-permute-done | bytes 688160 | tf_op jit(solution)/shard_map/ppermute | solution.py:674
  106.3 1.3 copy.90.refs_1_
  108.4 1.2 constant_dynamic-update-slice_fusion.1
  109.6 6.5 %add_convert_fusion.refs_0_ = bf16[2048,768]{1,0:T(8,128)(2,1)} fusion(bf16[2048,768]{1,0:T(8,128)(2,1)} %bitcast.113, bf16[768,768]{0,1:T(8,128)(2,1)S(1)} %copy-done.3, f32[768]{0:T(1024)S(1)} %add.117), kind=kOutput, calls=%fused_computation | convolution fusion | flops 2419064832 | bytes 7474176 | tf_op jit(solution)/shard_map/dot_general | solution.py:30
  116.1 32.5 %attend_forward.1 = (bf16[8,384,128]{2,1,0:T(8,128)(2,1)}, f32[3,1,2048]{2,1,0:T(1,128)}) custom-call(s32[1]{0:T(128)} %bitcast.lane_ref, s32[8]{0:T(128)} %get-tuple-element.138.low_ref, s32[8]{0:T(128)} %get-tuple-element.137.high_ref, bf16[2048,768]{1,0:T(8,128)(2,1)} %add_convert_fusion.refs_0_, s32[2048,1]{1,0:T(8,128)} %copy.90.refs_1_, s32[1,2048]{1,0:T(1,128)} %refs_2_.3), custom_call_target="tpu_custom_call" | custom-call | flops 3221225472 | bytes 5242880 | tf_op jit(solution)/shard_map/attend_forward/pallas_call | solution.py:265
  148.6 1.2 constant_dynamic-update-slice_fusion.refs_0_
  150.4 3.5 all-to-all-start
  161.7 12.7 %all-to-all-done.ctx_ref = bf16[4,2,384,128]{3,2,1,0:T(8,128)(2,1)S(1)} async-done(((bf16[4,2,384,128]{3,2,1,0:T(8,128)(2,1)}), bf16[4,2,384,128]{3,2,1,0:T(8,128)(2,1)S(1)}, u32[]{:S(2)}, u32[]{:S(2)}) %all-to-all-start) | async-done | bytes 786464 | tf_op jit(solution)/shard_map/all_to_all | solution.py:780
  175.3 30.7 %dense_chain.1 = (bf16[512,768]{1,0:T(8,128)(2,1)}, f32[512,768]{1,0:T(8,128)}, bf16[4,2,384,128]{3,2,1,0:T(8,128)(2,1)}, bf16[512,768]{1,0:T(8,128)(2,1)}, bf16...) custom-call(s32[5]{0:T(128)} %stack.53.place_ref, ...), custom_call_target="tpu_custom_call" | custom-call | flops 11274289152 | bytes 25165824 | tf_op jit(solution)/shard_map/dense_chain/pallas_call | solution.py:483
  208.2 12.8 %dense_weights.1 = (bf16[8,96,1856]{2,1,0:T(8,128)(2,1)}, bf16[8,96,1856]{2,1,0:T(8,128)(2,1)}, bf16[2,768,1856]{2,1,0:T(8,128)(2,1)}) custom-call(s32[5]{0:T(128)} %stack.53.place_ref, bf16[512,768]{1,0:T(8,128)(2,1)} %get-tuple-element.73.first_ref, bf16[512,768]{1,0:T(8,128)(2,1)} %get-tuple-element.74.branch_grad_ref, ...), custom_call_target="tpu_custom_call" | custom-call | flops 5838471168 | bytes 20971520 | tf_op jit(solution)/shard_map/dense_weights/pallas_call | solution.py:593
  221.1 3.5 all-to-all-start.1
  225.0 19.4 %all-to-all-done.1 = bf16[4,2,384,128]{3,2,1,0:T(8,128)(2,1)S(1)} async-done(((bf16[4,2,384,128]{3,2,1,0:T(8,128)(2,1)}), bf16[4,2,384,128]{3,2,1,0:T(8,128)(2,1)S(1)}, u32[]{:S(2)}, u32[]{:S(2)}) %all-to-all-start.1) | async-done | bytes 786464 | tf_op jit(solution)/shard_map/all_to_all | solution.py:780
  245.2 47.3 %attend_backward.1 = (bf16[1,2048,768]{2,1,0:T(8,128)(2,1)}, f32[1,768]{1,0:T(1,128)}) custom-call(s32[1]{0:T(128)} %bitcast.lane_ref, s32[8]{0:T(128)} %get-tuple-element.138.low_ref, s32[8]{0:T(128)} %get-tuple-element.137.high_ref, bf16[2048,768]{1,0:T(8,128)(2,1)} %add_convert_fusion.refs_0_, s32[2048,1]{1,0:T(8,128)} %copy.90.refs_1_, ...), custom_call_target="tpu_custom_call" | custom-call | flops 8053063680 | bytes 10485760 | tf_op jit(solution)/shard_map/attend_backward/pallas_call | solution.py:332
  292.5 6.2 %convolution_convert_fusion = bf16[2048,768]{1,0:T(8,128)(2,1)} fusion(bf16[768,768]{0,1:T(8,128)(2,1)S(1)} %copy-done.4, bf16[1,2048,768]{2,1,0:T(8,128)(2,1)} %get-tuple-element.84), kind=kOutput, calls=%fused_computation.1 | convolution fusion | flops 2417491968 | bytes 7471104 | tf_op jit(solution)/shard_map/dot_general | solution.py:30
  298.8 1.8 copy-done
  300.8 2.6 fusion
  303.3 5.5 %collective-permute-start.9 = (bf16[2,2,96,1856]{3,2,1,0:T(8,128)(2,1)S(1)}, bf16[2,2,96,1856]{3,2,1,0:T(8,128)(2,1)}, u32[]{:S(2)}, u32[]{:S(2)}) collective-permute-start(bf16[2,2,96,1856]{3,2,1,0:T(8,128)(2,1)S(1)} %get-tuple-element.89), channel_id=1, source_target_pairs={{0,8},{4,12},{8,0},{12,4},{16,24},{20,28},{24,16},{28,20},{1,9},{5... | collective-permute-start | bytes 4276232 | tf_op jit(solution)/shard_map/ppermute | solution.py:674
  308.9 6.9 %fusion.20 = f32[768,768]{1,0:T(8,128)} fusion(bf16[2048,768]{1,0:T(8,128)(2,1)} %bitcast.114, bf16[2048,768]{1,0:T(8,128)(2,1)} %bitcast.119), kind=kOutput, calls=%fused_computation.89 | convolution fusion | flops 2415919104 | bytes 8650752 | tf_op jit(solution)/shard_map/dot_general | solution.py:30
  315.8 24.4 %collective-permute-done.9 = bf16[2,2,96,1856]{3,2,1,0:T(8,128)(2,1)} collective-permute-done((bf16[2,2,96,1856]{3,2,1,0:T(8,128)(2,1)S(1)}, bf16[2,2,96,1856]{3,2,1,0:T(8,128)(2,1)}, u32[]{:S(2)}, u32[]{:S(2)}) %collective-permute-start.9) | collective-permute-done | bytes 1425440 | tf_op jit(solution)/shard_map/ppermute | solution.py:674
  340.3 1.7 add_convert_fusion.3
  342.3 5.4 %collective-permute-done.11 = f32[1,384]{1,0:T(1,128)S(1)} collective-permute-done((f32[1,384]{1,0:T(1,128)S(1)}, f32[1,384]{1,0:T(1,128)S(1)}, u32[]{:S(2)}, u32[]{:S(2)}) %collective-permute-start.11) | collective-permute-done | bytes 1568 | tf_op jit(solution)/shard_map/ppermute | solution.py:674
  347.8 4.7 %collective-permute-done.12 = f32[2,384]{1,0:T(2,128)S(1)} collective-permute-done((f32[2,384]{1,0:T(2,128)S(1)}, f32[2,384]{1,0:T(2,128)S(1)}, u32[]{:S(2)}, u32[]{:S(2)}) %collective-permute-start.12) | collective-permute-done | bytes 3104 | tf_op jit(solution)/shard_map/ppermute | solution.py:674
  353.8 4.9 %collective-permute-done.10 = bf16[1,2,96,1856]{3,2,1,0:T(8,128)(2,1)S(1)} collective-permute-done((bf16[1,2,96,1856]{3,2,1,0:T(8,128)(2,1)S(1)}, bf16[1,2,96,1856]{3,2,1,0:T(8,128)(2,1)S(1)}, u32[]{:S(2)}, u32[]{:S(2)}) %collective-permute-start.10) | collective-permute-done | bytes 712736 | tf_op jit(solution)/shard_map/ppermute | solution.py:674
  358.8 1.7 fusion.6
  360.6 1.4 pad_maximum_fusion
  362.8 1.2 add_convert_fusion.1
  364.1 2.0 collective-permute-done.13
  366.3 1.7 collective-permute-start.14
  368.0 7.4 %collective-permute-done.14 = bf16[2,96,768]{2,1,0:T(8,128)(2,1)S(1)} collective-permute-done((bf16[2,96,768]{2,1,0:T(8,128)(2,1)S(1)}, bf16[2,96,768]{2,1,0:T(8,128)(2,1)S(1)}, u32[]{:S(2)}, u32[]{:S(2)}) %collective-permute-start.14) | collective-permute-done | bytes 294944 | tf_op jit(solution)/shard_map/ppermute | solution.py:674
  375.5 1.7 collective-permute-start.15
  377.2 3.7 collective-permute-done.15
  381.6 1.7 finish_heads.1
  385.5 2.4 add_bitcast_fusion
  387.9 9.8 %reduce-scatter.6.cloned.1.call-done = bf16[1,96,1856]{2,1,0:T(8,128)(2,1)} async-done(((bf16[4,96,1856]{2,1,0:T(8,128)(2,1)}), bf16[1,96,1856]{2,1,0:T(8,128)(2,1)}) %reduce-scatter.6.cloned.1.call-update) | async-done | bytes 356368 | tf_op jit(solution)/shard_map/reduce_scatter | solution.py:864
  397.7 1.9 finish_dense.1
  399.6 2.0 slice_bitcast_fusion.1
  401.6 1.3 slice_bitcast_fusion
  (142 shorter events, 25.0 us)
Async XLA Ops:
  7.2 4.3 %copy-start.11 = (s32[1,512]{1,0:T(1,128)S(1)}, s32[1,512]{1,0:T(1,128)}, u32[]{:S(2)}) copy-start(s32[1,512]{1,0:T(1,128)} %param.22) | copy-start | bytes 6148
  7.2 9.3 %copy-start.9 = (bf16[192,96]{1,0:T(8,128)(2,1)S(1)}, bf16[192,96]{1,0:T(8,128)(2,1)}, u32[]{:S(2)}) copy-start(bf16[192,96]{1,0:T(8,128)(2,1)} %param.28) | copy-start | bytes 110596
  7.2 9.4 %copy-start.8 = (bf16[768,96]{0,1:T(8,128)(2,1)S(1)}, bf16[768,96]{0,1:T(8,128)(2,1)}, u32[]{:S(2)}) copy-start(bf16[768,96]{0,1:T(8,128)(2,1)} %param.30) | copy-start | bytes 442372
  7.2 9.4 %copy-start.7 = (bf16[96,768]{1,0:T(8,128)(2,1)S(1)}, bf16[96,768]{1,0:T(8,128)(2,1)}, u32[]{:S(2)}) copy-start(bf16[96,768]{1,0:T(8,128)(2,1)} %param.29) | copy-start | bytes 442372
  7.2 97.7 %all-gather.5.cloned.1.call-start = ((), (), s32[]{:S(2)}) async-start(), calls=%async_computation.8 | async-start | bytes 3932160 | tf_op jit(solution)/shard_map/all_gather | solution.py:737
  8.0 150.8 %all-gather.7.cloned.1.call-start = ((), (), s32[]{:S(2)}) async-start(), calls=%async_computation.9 | async-start | bytes 6193152 | tf_op jit(solution)/shard_map/all_gather | solution.py:760
  11.0 2.4 collective-permute-start.2
  13.8 12.3 %collective-permute-start.3 = (bf16[192,768]{0,1:T(8,128)(2,1)S(1)}, bf16[192,768]{0,1:T(8,128)(2,1)S(1)}, u32[]{:S(2)}, u32[]{:S(2)}) collective-permute-start(bf16[192,768]{0,1:T(8,128)(2,1)S(1)} %maximum_select_fusion.2), channel_id=1, source_target_pairs={{0,8},{4,12},{8,0},{12,4},{16,24},{20,28},{24,16},{28,20},{1,9},{5... | collective-permute-start | bytes 884744 | tf_op jit(solution)/shard_map/ppermute | solution.py:674
  16.7 25.6 %collective-permute-start = (bf16[1,96,1792]{2,1,0:T(8,128)(2,1)S(1)}, bf16[1,96,1792]{2,1,0:T(8,128)(2,1)S(1)}, u32[]{:S(2)}, u32[]{:S(2)}) collective-permute-start(bf16[1,96,1792]{2,1,0:T(8,128)(2,1)S(1)} %bitcast.87), channel_id=1, source_target_pairs={{0,1},{1,0},{2,3},{3,2},{4,5},{5,4},{6,7},{7,6},{8,9},{9,8},{10,11... | collective-permute-start | bytes 1032200 | tf_op jit(solution)/shard_map/ppermute | solution.py:674
  26.6 15.8 %collective-permute-start.4 = (bf16[384,768]{0,1:T(8,128)(2,1)S(1)}, bf16[384,768]{0,1:T(8,128)(2,1)S(1)}, u32[]{:S(2)}, u32[]{:S(2)}) collective-permute-start(bf16[384,768]{0,1:T(8,128)(2,1)S(1)} %maximum_select_fusion.1), channel_id=1, source_target_pairs={{0,16},{4,20},{8,24},{12,28},{16,0},{20,4},{24,8},{28,12},{1,17},{... | collective-permute-start | bytes 1769480 | tf_op jit(solution)/shard_map/ppermute | solution.py:674
  42.3 13.5 %collective-permute-start.1 = (bf16[2,96,1792]{2,1,0:T(8,128)(2,1)S(1)}, bf16[2,96,1792]{2,1,0:T(8,128)(2,1)}, u32[]{:S(2)}, u32[]{:S(2)}) collective-permute-start(bf16[2,96,1792]{2,1,0:T(8,128)(2,1)S(1)} %pad_maximum_fusion.2), channel_id=1, source_target_pairs={{0,8},{4,12},{8,0},{12,4},{16,24},{20,28},{24,16},{28,20},{1,9},{5... | collective-permute-start | bytes 2064392 | tf_op jit(solution)/shard_map/ppermute | solution.py:674
  43.8 61.1 %copy-start.10 = (s32[1,2048]{1,0:T(1,128)S(1)}, s32[1,2048]{1,0:T(1,128)}, u32[]{:S(2)}) copy-start(s32[1,2048]{1,0:T(1,128)} %refs_2_.3) | copy-start | bytes 24580
  57.0 47.9 %collective-permute-start.6 = (bf16[4,96,1792]{2,1,0:T(8,128)(2,1)S(1)}, bf16[4,96,1792]{2,1,0:T(8,128)(2,1)S(1)}, u32[]{:S(2)}, u32[]{:S(2)}) collective-permute-start(bf16[4,96,1792]{2,1,0:T(8,128)(2,1)S(1)} %pad_maximum_fusion.1), channel_id=1, source_target_pairs={{0,16},{4,20},{8,24},{12,28},{16,0},{20,4},{24,8},{28,12},{1,17},{... | collective-permute-start | bytes 4128776 | tf_op jit(solution)/shard_map/ppermute | solution.py:674
  58.7 46.2 %collective-permute-start.5 = (bf16[2,96,1792]{2,1,0:T(8,128)(2,1)S(1)}, bf16[2,96,1792]{2,1,0:T(8,128)(2,1)}, u32[]{:S(2)}, u32[]{:S(2)}) collective-permute-start(bf16[2,96,1792]{2,1,0:T(8,128)(2,1)S(1)} %pad_maximum_fusion.2), channel_id=1, source_target_pairs={{0,2},{1,3},{2,0},{3,1},{4,6},{5,7},{6,4},{7,5},{8,10},{9,11},{10,... | collective-permute-start | bytes 2064392 | tf_op jit(solution)/shard_map/ppermute | solution.py:674
  107.6 2.0 copy-start.3
  149.8 5.2 %copy-start.14 = (bf16[768]{0:T(1024)(128)(2,1)S(1)}, bf16[768]{0:T(1024)(128)(2,1)}, u32[]{:S(2)}) copy-start(bf16[768]{0:T(1024)(128)(2,1)} %param.33) | copy-start | bytes 4612
  149.8 5.2 %copy-start.15 = (bf16[768]{0:T(1024)(128)(2,1)S(1)}, bf16[768]{0:T(1024)(128)(2,1)}, u32[]{:S(2)}) copy-start(bf16[768]{0:T(1024)(128)(2,1)} %param.36) | copy-start | bytes 4612
  149.8 5.2 %copy-start.16 = (bf16[768]{0:T(1024)(128)(2,1)S(1)}, bf16[768]{0:T(1024)(128)(2,1)}, u32[]{:S(2)}) copy-start(bf16[768]{0:T(1024)(128)(2,1)} %param.37) | copy-start | bytes 4612
  149.8 5.3 %copy-start.17 = (bf16[768]{0:T(1024)(128)(2,1)S(1)}, bf16[768]{0:T(1024)(128)(2,1)}, u32[]{:S(2)}) copy-start(bf16[768]{0:T(1024)(128)(2,1)} %param.35) | copy-start | bytes 4612
  149.8 5.3 %copy-start.18 = (bf16[768]{0:T(1024)(128)(2,1)S(1)}, bf16[768]{0:T(1024)(128)(2,1)}, u32[]{:S(2)}) copy-start(bf16[768]{0:T(1024)(128)(2,1)} %param.38) | copy-start | bytes 4612
  149.8 5.3 %copy-start.19 = (bf16[768]{0:T(1024)(128)(2,1)S(1)}, bf16[768]{0:T(1024)(128)(2,1)}, u32[]{:S(2)}) copy-start(bf16[768]{0:T(1024)(128)(2,1)} %param.39) | copy-start | bytes 4612
  149.8 6.0 %copy-start.12 = (bf16[3072]{0:T(1024)(128)(2,1)S(1)}, bf16[3072]{0:T(1024)(128)(2,1)}, u32[]{:S(2)}) copy-start(bf16[3072]{0:T(1024)(128)(2,1)} %param.34) | copy-start | bytes 18436
  149.8 8.1 %collective-permute-start.7 = (bf16[8,96,1792]{2,1,0:T(8,128)(2,1)}, bf16[8,96,1792]{2,1,0:T(8,128)(2,1)}, u32[]{:S(2)}, u32[]{:S(2)}) collective-permute-start(bf16[8,96,1792]{2,1,0:T(8,128)(2,1)} %constant_dynamic-update-slice_fusion.refs_0_), channel_id=1, source_target_pairs={{0,4},{4,0},{8,12},{12,8},{16,20},{20,16},{24,28},{28,24},{1,5},{5... | collective-permute-start | bytes 8257544 | tf_op jit(solution)/shard_map/ppermute | solution.py:674
  150.4 24.0 %all-to-all-start = ((bf16[4,2,384,128]{3,2,1,0:T(8,128)(2,1)}), bf16[4,2,384,128]{3,2,1,0:T(8,128)(2,1)S(1)}, u32[]{:S(2)}, u32[]{:S(2)}) async-start(bf16[4,2,384,128]{3,2,1,0:T(8,128)(2,1)} %bitcast.19), calls=%async_computation | async-start | bytes 1572864 | tf_op jit(solution)/shard_map/all_to_all | solution.py:780
  153.9 205.0 %reduce-scatter.4.cloned.1.call-start = ((), (), s32[]{:S(2)}) async-start(), calls=%async_computation.5 | async-start | bytes 6635520 | tf_op jit(solution)/shard_map/reduce_scatter | solution.py:829
  174.4 0.9 copy-start.5
  221.1 23.2 %all-to-all-start.1 = ((bf16[4,2,384,128]{3,2,1,0:T(8,128)(2,1)}), bf16[4,2,384,128]{3,2,1,0:T(8,128)(2,1)S(1)}, u32[]{:S(2)}, u32[]{:S(2)}) async-start(bf16[4,2,384,128]{3,2,1,0:T(8,128)(2,1)} %get-tuple-element.82), calls=%async_computation.1 | async-start | bytes 1572864 | tf_op jit(solution)/shard_map/all_to_all | solution.py:780
  224.6 160.9 %reduce-scatter.8.cloned.1.call-start = ((), (), s32[]{:S(2)}) async-start(), calls=%async_computation.7 | async-start | bytes 3932160 | tf_op jit(solution)/shard_map/reduce_scatter | solution.py:843
  224.9 75.9 %collective-permute-start.8 = (bf16[4,2,96,1856]{3,2,1,0:T(8,128)(2,1)}, bf16[4,2,96,1856]{3,2,1,0:T(8,128)(2,1)}, u32[]{:S(2)}, u32[]{:S(2)}) collective-permute-start(bf16[4,2,96,1856]{3,2,1,0:T(8,128)(2,1)} %bitcast.115), channel_id=1, source_target_pairs={{0,4},{4,0},{8,12},{12,8},{16,20},{20,16},{24,28},{28,24},{1,5},{5... | collective-permute-start | bytes 8552456 | tf_op jit(solution)/shard_map/ppermute | solution.py:674
  244.3 0.9 copy-start.6
  245.2 47.3 %copy-start.4 = (bf16[768,768]{0,1:T(8,128)(2,1)S(1)}, bf16[768,768]{0,1:T(8,128)(2,1)}, u32[]{:S(2)}) copy-start(bf16[768,768]{0,1:T(8,128)(2,1)} %maximum_select_fusion) | copy-start | bytes 3538948
  298.7 1.8 copy-start
  298.7 99.0 %reduce-scatter.6.cloned.1.call-start = ((), (), s32[]{:S(2)}) async-start(), calls=%async_computation.6 | async-start | bytes 1843200 | tf_op jit(solution)/shard_map/reduce_scatter | solution.py:864
  300.8 8.1 %copy-start.13 = (f32[1,768]{1,0:T(1,128)S(1)}, f32[1,768]{1,0:T(1,128)}, u32[]{:S(2)}) copy-start(f32[1,768]{1,0:T(1,128)} %get-tuple-element.102) | copy-start | bytes 9220
  303.3 36.9 %collective-permute-start.9 = (bf16[2,2,96,1856]{3,2,1,0:T(8,128)(2,1)S(1)}, bf16[2,2,96,1856]{3,2,1,0:T(8,128)(2,1)}, u32[]{:S(2)}, u32[]{:S(2)}) collective-permute-start(bf16[2,2,96,1856]{3,2,1,0:T(8,128)(2,1)S(1)} %get-tuple-element.89), channel_id=1, source_target_pairs={{0,8},{4,12},{8,0},{12,4},{16,24},{20,28},{24,16},{28,20},{1,9},{5... | collective-permute-start | bytes 4276232 | tf_op jit(solution)/shard_map/ppermute | solution.py:674
  341.9 16.7 %collective-permute-start.10 = (bf16[1,2,96,1856]{3,2,1,0:T(8,128)(2,1)S(1)}, bf16[1,2,96,1856]{3,2,1,0:T(8,128)(2,1)S(1)}, u32[]{:S(2)}, u32[]{:S(2)}) collective-permute-start(bf16[1,2,96,1856]{3,2,1,0:T(8,128)(2,1)S(1)} %get-tuple-element.94), channel_id=1, source_target_pairs={{0,16},{4,20},{8,24},{12,28},{16,0},{20,4},{24,8},{28,12},{1,17},{... | collective-permute-start | bytes 2138120 | tf_op jit(solution)/shard_map/ppermute | solution.py:674
  342.3 5.4 %collective-permute-start.11 = (f32[1,384]{1,0:T(1,128)S(1)}, f32[1,384]{1,0:T(1,128)S(1)}, u32[]{:S(2)}, u32[]{:S(2)}) collective-permute-start(f32[1,384]{1,0:T(1,128)S(1)} %pad_maximum_fusion.6), channel_id=1, source_target_pairs={{0,1},{1,0},{2,3},{3,2},{4,5},{5,4},{6,7},{7,6},{8,9},{9,8},{10,11... | collective-permute-start | bytes 4616 | tf_op jit(solution)/shard_map/ppermute | solution.py:674
  347.8 4.7 %collective-permute-start.12 = (f32[2,384]{1,0:T(2,128)S(1)}, f32[2,384]{1,0:T(2,128)S(1)}, u32[]{:S(2)}, u32[]{:S(2)}) collective-permute-start(f32[2,384]{1,0:T(2,128)S(1)} %maximum_select_fusion.4), channel_id=1, source_target_pairs={{0,2},{1,3},{2,0},{3,1},{4,6},{5,7},{6,4},{7,5},{8,10},{9,11},{10,... | collective-permute-start | bytes 9224 | tf_op jit(solution)/shard_map/ppermute | solution.py:674
  360.6 2.2 copy-start.1
  364.0 2.1 collective-permute-start.13
  366.3 19.2 %copy-start.2 = (f32[512,768]{1,0:T(8,128)S(1)}, f32[512,768]{1,0:T(8,128)}, u32[]{:S(2)}) copy-start(f32[512,768]{1,0:T(8,128)} %get-tuple-element.99) | copy-start | bytes 4718596
  366.3 9.1 %collective-permute-start.14 = (bf16[2,96,768]{2,1,0:T(8,128)(2,1)S(1)}, bf16[2,96,768]{2,1,0:T(8,128)(2,1)S(1)}, u32[]{:S(2)}, u32[]{:S(2)}) collective-permute-start(bf16[2,96,768]{2,1,0:T(8,128)(2,1)S(1)} %dynamic-slice_bitcast_fusion.1), channel_id=1, source_target_pairs={{0,8},{4,12},{8,0},{12,4},{16,24},{20,28},{24,16},{28,20},{1,9},{5... | collective-permute-start | bytes 884744 | tf_op jit(solution)/shard_map/ppermute | solution.py:674
  375.5 5.4 %collective-permute-start.15 = (bf16[1,96,768]{2,1,0:T(8,128)(2,1)S(1)}, bf16[1,96,768]{2,1,0:T(8,128)(2,1)S(1)}, u32[]{:S(2)}, u32[]{:S(2)}) collective-permute-start(bf16[1,96,768]{2,1,0:T(8,128)(2,1)S(1)} %constant_dynamic-slice_fusion), channel_id=1, source_target_pairs={{0,16},{4,20},{8,24},{12,28},{16,0},{20,4},{24,8},{28,12},{1,17},{... | collective-permute-start | bytes 442376 | tf_op jit(solution)/shard_map/ppermute | solution.py:674
Sparse Core Ops, SparseCore 0:
  9.6 86.2 all-gather.4
  105.0 41.0 all-gather.6
  221.2 62.6 reduce-scatter.3
  298.8 62.8 reduce-scatter.7
  363.9 33.7 reduce-scatter.5

commit v11 on v10

--- a/solution.py
+++ b/solution.py
@@ -74,7 +74,7 @@
 
 
 def attend_forward(
-    which, lane_ref, low_ref, high_ref, *refs
+    which, lane_ref, low_ref, count_ref, *refs
 ):
     chunk_refs, (seg_col_ref, seg_row_ref, ctx_ref, lse_ref, held, qkv_ref, sems) = refs[:-7], refs[-7:]
     halves, half = which
@@ -94,10 +94,10 @@
     queries = [
         qkv_ref[rows, SLAB * h : SLAB * h + 2 * DH] * jnp.asarray(SCALE, BF16) for h in range(heads)
     ]
-    low, high = low_ref[qb], high_ref[qb]
+    low, count = low_ref[qb], count_ref[qb]
 
     def score(kb, peaks):
-        keys = pl.ds(pl.multiple_of(kb * BLOCK, BLOCK), BLOCK)
+        keys = pl.ds(pl.multiple_of(low * STEP + kb * BLOCK, STEP), BLOCK)
         allowed = seg_q == seg_row_ref[:, keys]
         found = []
         for h in range(heads):
@@ -108,11 +108,11 @@
         return tuple(found)
 
     start = tuple(jnp.full((BLOCK, 128), MASKED, F32) for _ in range(heads))
-    peaks = lax.fori_loop(low, high, score, start)
+    peaks = lax.fori_loop(0, count, score, start)
     highest = [jnp.max(peak, axis=-1, keepdims=True) for peak in peaks]
 
     def weigh(kb, carry):
-        keys = pl.ds(pl.multiple_of(kb * BLOCK, BLOCK), BLOCK)
+        keys = pl.ds(pl.multiple_of(low * STEP + kb * BLOCK, STEP), BLOCK)
         found = []
         for h in range(heads):
             total, acc = carry[h]
@@ -123,7 +123,7 @@
         return tuple(found)
 
     zero = jnp.zeros((BLOCK, 128), F32)
-    done = lax.fori_loop(low, high, weigh, tuple((zero, zero) for _ in range(heads)))
+    done = lax.fori_loop(0, count, weigh, tuple((zero, zero) for _ in range(heads)))
     values = []
     for h in range(heads):
         total, acc = done[h]
@@ -137,7 +137,7 @@
     )
 
 
-def attend_backward(which, chunks, lane_ref, low_ref, high_ref, *refs):
+def attend_backward(which, chunks, lane_ref, low_ref, count_ref, *refs):
     halves, half = which
     last = half == halves - 1
     chunk_refs, refs = refs[:chunks], refs[chunks:]
@@ -191,10 +191,10 @@
         pairs.append(jnp.concatenate([queries[h], grads[h]], axis=0))
     seg_q = seg_row_ref[...]
     lses = lse_ref[...]
-    low, high = low_ref[qb], high_ref[qb]
+    low, count = low_ref[qb], count_ref[qb]
 
     def step(kb, accs):
-        keys = pl.ds(pl.multiple_of(kb * BLOCK, BLOCK), BLOCK)
+        keys = pl.ds(pl.multiple_of(low * STEP + kb * BLOCK, STEP), BLOCK)
         allowed = seg_col_ref[keys, :] == seg_q
         found = []
         for h in range(heads):
@@ -208,7 +208,7 @@
         return tuple(found)
 
     zero = jnp.zeros((BLOCK, 128), F32)
-    accs = lax.fori_loop(low, high, step, tuple(zero for _ in range(heads)))
+    accs = lax.fori_loop(0, count, step, tuple(zero for _ in range(heads)))
     for h in range(heads):
         query_grad = jnp.where(right, 0.0, accs[h] * SCALE).astype(BF16)
         if last:
@@ -245,12 +245,17 @@
                 copy.wait()
 
 
+STEP = 128
+
+
 def document_blocks(segment_row):
     starts = segment_row[::BLOCK]
     stops = segment_row[BLOCK - 1 :: BLOCK]
-    low = jnp.sum((segment_row[None, :] < starts[:, None]).astype(jnp.int32), axis=1)
+    low = jnp.sum((segment_row[None, :] < starts[:, None]).astype(jnp.int32), axis=1) // STEP
     high = jnp.sum((segment_row[None, :] <= stops[:, None]).astype(jnp.int32), axis=1)
-    return (low // BLOCK, (high + BLOCK - 1) // BLOCK)
+    each = BLOCK // STEP
+    count = (high - low * STEP + BLOCK - 1) // BLOCK
+    return (jnp.minimum(low, segment_row.shape[0] // STEP - each * count), count)
 
 
 PACKED = BLOCK + BLOCK // 2
@@ -424,7 +429,9 @@
         arrive(2, slot)
         return branch + dot(activated, w_up[slot], NT)
 
-    branch = lax.fori_loop(0, parts, up, jnp.zeros(in_ref.shape, F32))
+    branch = jnp.zeros(in_ref.shape, F32)
+    for slot in range(parts):
+        branch = up(slot, branch)
     layer_rows, normed_two, inverse_two = norm_forward(first.astype(F32) + branch + vec(3), vec(4), vec(5))
     layer_ref[...] = layer_rows.astype(BF16)
     misfit = layer_rows - teacher_ref[...].astype(F32)
@@ -445,7 +452,9 @@
         inner_sums_ref[t] += column_sum(hidden_grad.astype(F32))
         return back + dot(hidden_grad, w_in[slot], NT)
 
-    upstream = lax.fori_loop(0, parts, down, second_grad)
+    upstream = second_grad
+    for slot in range(parts):
+        upstream = down(slot, upstream)
     first_grad = norm_backward(upstream, normed_one, inverse_one, vec(1))
     first_grad_ref[...] = first_grad
     attn_grad = first_grad.astype(BF16)
@@ -558,20 +567,15 @@
     plain = 2 * hidden_cols + ctx.shape[1]
     whole[step, :, 2 * hidden_cols : plain] = dot(turned[2], ctx).astype(BF16)
     whole[step, :, plain : plain + notes_ref.shape[1]] = notes_ref[...]
-    for out, (start, stop, turns) in zip(outs, plans):
-
-        @pl.when((step >= start) & (step < stop))
-        def _():
-            block = out.shape[1]
-            for at, turn in enumerate(turns):
-                offset = 0
-                if block < whole.shape[1]:
-                    offset = pl.multiple_of((place_ref[slots] ^ turn) * block, block)
-                pltpu.make_async_copy(
-                    whole.at[step, pl.ds(offset, block), :],
-                    out.at[at * (stop - start) + step - start],
-                    sems.at[step],
-                ).start()
+    for out, turns in zip(outs, plans):
+        block = out.shape[1]
+        for at, turn in enumerate(turns):
+            offset = 0
+            if block < whole.shape[1]:
+                offset = pl.multiple_of((place_ref[place_ref.shape[0] - 1] ^ turn) * block, block)
+            pltpu.make_async_copy(
+                whole.at[step, pl.ds(offset, block), :], out.at[at * slots + step], sems.at[step]
+            ).start()
 
     @pl.when(step == slots - 1)
     def _():
@@ -579,45 +583,43 @@
             pltpu.make_async_copy(whole.at[slot], whole.at[slot], sems.at[slot]).wait()
 
 
-def run_weights(plans, place, notes, first, branch_grad, attn_grad, act, hidden_grad, ctx):
-    parts, part_len, hidden_cols = act.shape
+def run_weights(base, slots, plans, place, notes, first, branch_grad, attn_grad, act, hidden_grad, ctx):
+    _, part_len, hidden_cols = act.shape
     width = first.shape[1]
     columns = 2 * hidden_cols + 3 * DH + notes.shape[1]
     fixed = pl.BlockSpec((part_len, width), lambda s, place: (0, 0))
-    by_slot = pl.BlockSpec((1, part_len, hidden_cols), lambda s, place: (place[s], 0, 0))
+    by_slot = pl.BlockSpec((1, part_len, hidden_cols), lambda s, place: (place[base + s], 0, 0))
     outs = tuple(
-        jax.ShapeDtypeStruct((len(turns) * (stop - start), block, columns), BF16)
-        for start, stop, block, turns in plans
-    )
-    inner = tuple((start, stop, turns) for start, stop, _, turns in plans)
+        jax.ShapeDtypeStruct((len(turns) * slots, block, columns), BF16) for block, turns in plans
+    )
     return pl.pallas_call(
-        functools.partial(dense_weights, inner),
+        functools.partial(dense_weights, tuple(turns for _, turns in plans)),
         out_shape=outs,
         grid_spec=pltpu.PrefetchScalarGridSpec(
             num_scalar_prefetch=1,
-            grid=(parts,),
+            grid=(slots,),
             in_specs=[
                 fixed,
                 fixed,
                 fixed,
                 by_slot,
                 by_slot,
-                pl.BlockSpec((1,) + ctx.shape[1:], lambda s, place: (place[s], 0, 0, 0)),
+                pl.BlockSpec((1,) + ctx.shape[1:], lambda s, place: (place[base + s], 0, 0, 0)),
                 pl.BlockSpec(notes.shape, lambda s, place: (0, 0)),
             ],
             out_specs=tuple(pl.BlockSpec(memory_space=pl.ANY) for _ in outs),
             scratch_shapes=[
                 pltpu.VMEM((3, width, part_len), BF16),
-                pltpu.VMEM((parts, width, columns), BF16),
-                pltpu.SemaphoreType.DMA((parts,)),
+                pltpu.VMEM((slots, width, columns), BF16),
+                pltpu.SemaphoreType.DMA((slots,)),
             ],
         ),
         compiler_params=pltpu.CompilerParams(
             dimension_semantics=("arbitrary",), vmem_limit_bytes=VMEM_LIMIT
         ),
         cost_estimate=pl.CostEstimate(
-            flops=2 * part_len * width * columns * parts,
-            bytes_accessed=20 << 20,
+            flops=2 * part_len * width * columns * slots,
+            bytes_accessed=5 * slots << 20,
             transcendentals=0,
         ),
         name="dense_weights",
@@ -749,15 +751,14 @@
     if paired:
         place = jnp.stack([rank, rank ^ 1, rank ^ 2, rank ^ 3, lax.axis_index("dp")]).astype(jnp.int32)
         pair = jnp.concatenate([mine[None], swap(mine[None], "tensor", 1)], axis=0)
-        far = swap(pair, "tensor", 2)
         near = jnp.concatenate([pair, swap(pair, "dp", 2)], axis=0)
         turns = [0, 2, 4, 6]
         for bit in (1, 2, 4):
             w_heads = merge(w_heads, swap(w_heads, "dp", bit), "dp", bit)
         near, w_heads = lax.optimization_barrier((near, w_heads))
         near_next = swap(near, "dp", 4)
-        tokens, far, near_next = lax.optimization_barrier((tokens, far, near_next))
-        weights = lax.all_gather(far, "dp", axis=0, tiled=False)
+        tokens, pair, near_next = lax.optimization_barrier((tokens, pair, near_next))
+        far = swap(pair, "tensor", 2)
     else:
         place = jnp.asarray(list(range(parts)) + [0], jnp.int32)
         weights = lax.all_gather(mine, ("tensor", "dp"), axis=0, tiled=False)
@@ -781,7 +782,8 @@
 
     context, lse = run_forward((1, 0), lane, bounds, qkv, seg_col, seg_row)
     if paired:
-        near_next, context = lax.optimization_barrier((near_next, context))
+        near_next, far, context = lax.optimization_barrier((near_next, far, context))
+        weights = lax.all_gather(far, "dp", axis=0, tiled=False)
         near = jnp.concatenate([near, near_next], axis=0)
         near_other = swap(near, "dp", 1)
     arrived = exchange(context)
@@ -819,17 +821,14 @@
     notes = jnp.tile(notes, (copies, 1))
     if paired:
         keep_turns = (0, 4, 2, 6)
-        plans = (
-            (0, 2, shard_rows, keep_turns),
-            (0, 2, shard_rows, tuple(turn | 1 for turn in keep_turns)),
-            (2, 4, width, (0,)),
-        )
-        keep, send, distant = run_weights(plans, place, notes, *sources)
+        (distant,) = run_weights(2, 2, ((width, (0,)),), place, notes, *sources)
+        plans = tuple((shard_rows, tuple(turn | flip for turn in keep_turns)) for flip in (0, 1))
+        keep, send = run_weights(0, 2, plans, place, notes, *sources)
         keep, send = (value.reshape((4, 2) + value.shape[1:]) for value in (keep, send))
         distant = lax.psum_scatter(distant, "dp", scatter_dimension=1, tiled=True)
         came = swap(send, "dp", 1)
     else:
-        (packed,) = run_weights(((0, parts, width, (0,)),), place, notes, *sources)
+        (packed,) = run_weights(0, parts, ((width, (0,)),), place, notes, *sources)
         packed = lax.psum_scatter(packed, "dp", scatter_dimension=1, tiled=True)
 
     joined_grad, sums = run_backward(

time: 413 us -> 398 us (0.964)
  Pallas kernels: 127 us -> 113 us
  waiting for transfers between devices: 170 us -> 156 us
  starting transfers between devices: 30.6 us -> 43.8 us
    all_gather x1, waiting for transfers between devices: 0.01 us -> 34.5 us  [local(): weights = lax.all_gather(far, 'dp', axis=0, tiled=False)]
    ppermute x16, waiting for transfers between devices: 127 us -> 102 us  [swap(): return lax.ppermute(value, axis, [(i, i ^ bit) for i in range(size)])]
    all_to_all x2, waiting for transfers between devices: 32 us -> 11.7 us  [exchange(): lax.all_to_all(packed_blocks.reshape(parts, halves, PACKED, 2 * DH), 'ten...]
    ppermute x16, starting transfers between devices: 23 us -> 34.8 us  [swap(): return lax.ppermute(value, axis, [(i, i ^ bit) for i in range(size)])]
    pallas_call x1, Pallas kernels: 47.3 us -> 38.1 us  [run_backward(): pl.pallas_call(functools.partial(attend_backward, which, len(qkv)), out_s...]
    pallas_call x1, Pallas kernels: 32.5 us -> 27.8 us  [run_forward(): pl.pallas_call(functools.partial(attend_forward, which), out_shape=(jax.S...]
    pallas_call x1 -> x2, Pallas kernels: 12.8 us -> 17.4 us  [run_weights(): pl.pallas_call(functools.partial(dense_weights, tuple((turns for _, turns...]
    pallas_call x1, Pallas kernels: 30.7 us -> 26.1 us  [run_dense(): pl.pallas_call(functools.partial(dense_chain, marks), out_shape=(low, jax...]
  transfers between devices with their start and end apart: 23 -> 23, of which waited for: 14 -> 14; matrix products, arithmetic and copies ran while one was open for 13% -> 14% of each run, Pallas kernels for 20% -> 19%
where the time goes in v11:
time: 398 us; the launch traced here: 396 us
  waiting for transfers between devices  156 us (39%)
  Pallas kernels  113 us (28%)
  starting transfers between devices  43.8 us (11%)
  other arithmetic  22.5 us (6%)
  local copies, waits for them, and re-layouts  21.6 us (5%)
  matrix products  19.6 us (5%)
  between operations  18.8 us (5%)
    ppermute x16, waiting for transfers between devices, swap(): return lax.ppermute(value, axis, [(i, i ^ bit) for i in range(size)])  102 us
    pallas_call x1, Pallas kernels, run_backward(): pl.pallas_call(functools.partial(attend_backward, which, len(qkv)), out_s...  38.1 us
    ppermute x16, starting transfers between devices, swap(): return lax.ppermute(value, axis, [(i, i ^ bit) for i in range(size)])  34.8 us
    all_gather x1, waiting for transfers between devices, local(): weights = lax.all_gather(far, 'dp', axis=0, tiled=False)  34.5 us
    pallas_call x1, Pallas kernels, run_forward(): pl.pallas_call(functools.partial(attend_forward, which), out_shape=(jax.S...  27.8 us
    pallas_call x1, Pallas kernels, run_dense(): pl.pallas_call(functools.partial(dense_chain, marks), out_shape=(low, jax...  26.1 us
    dot_general x3, matrix products, dot(): lax.dot_general(left_side, right_side, dims, preferred_element_type=F32)  19.6 us
    pallas_call x2, Pallas kernels, run_weights(): pl.pallas_call(functools.partial(dense_weights, tuple((turns for _, turns...  17.4 us
  transfers between devices with their start and end apart: 23, of which 14 were waited for; matrix products, arithmetic and copies ran while one was open for 14% of the time, Pallas kernels for 19%

profile of v11, /device:TPU:0, one launch (start us, length us, event | category | flops | bytes accessed | tf_op | source)
XLA Modules:
  0.0 395.6 jit_solution(3151007957475099378)
XLA Ops:
  9.8 0.9 copy.87
  13.8 2.6 collective-permute-start.3
  16.7 1.6 collective-permute-start
  18.3 7.8 %collective-permute-done.3 = bf16[192,768]{0,1:T(8,128)(2,1)S(1)} collective-permute-done((bf16[192,768]{0,1:T(8,128)(2,1)S(1)}, bf16[192,768]{0,1:T(8,128)(2,1)S(1)}, u32[]{:S(2)}, u32[]{:S(2)}) %collective-permute-start.3) | collective-permute-done | bytes 294944 | tf_op jit(solution)/shard_map/ppermute | solution.py:676
  26.6 1.8 collective-permute-start.4
  28.5 13.8 %collective-permute-done = bf16[1,96,1792]{2,1,0:T(8,128)(2,1)S(1)} collective-permute-done((bf16[1,96,1792]{2,1,0:T(8,128)(2,1)S(1)}, bf16[1,96,1792]{2,1,0:T(8,128)(2,1)S(1)}, u32[]{:S(2)}, u32[]{:S(2)}) %collective-permute-start) | collective-permute-done | bytes 344096 | tf_op jit(solution)/shard_map/ppermute | solution.py:676
  42.4 1.4 maximum_select_fusion
  43.7 11.9 %collective-permute-done.1 = bf16[2,96,1792]{2,1,0:T(8,128)(2,1)S(1)} collective-permute-done((bf16[2,96,1792]{2,1,0:T(8,128)(2,1)S(1)}, bf16[2,96,1792]{2,1,0:T(8,128)(2,1)S(1)}, u32[]{:S(2)}, u32[]{:S(2)}) %collective-permute-start.1) | collective-permute-done | bytes 688160 | tf_op jit(solution)/shard_map/ppermute | solution.py:676
  55.8 1.7 collective-permute-start.5
  58.8 1.3 copy.90.refs_1_
  60.9 22.1 %collective-permute-done.5 = bf16[4,96,1792]{2,1,0:T(8,128)(2,1)S(1)} collective-permute-done((bf16[4,96,1792]{2,1,0:T(8,128)(2,1)S(1)}, bf16[4,96,1792]{2,1,0:T(8,128)(2,1)S(1)}, u32[]{:S(2)}, u32[]{:S(2)}) %collective-permute-start.5) | collective-permute-done | bytes 1376288 | tf_op jit(solution)/shard_map/ppermute | solution.py:676
  83.0 5.0 %collective-permute-start.6 = (bf16[2,96,1792]{2,1,0:T(8,128)(2,1)S(1)}, bf16[2,96,1792]{2,1,0:T(8,128)(2,1)}, u32[]{:S(2)}, u32[]{:S(2)}) collective-permute-start(bf16[2,96,1792]{2,1,0:T(8,128)(2,1)S(1)} %pad_maximum_fusion.2), channel_id=1, source_target_pairs={{0,2},{1,3},{2,0},{3,1},{4,6},{5,7},{6,4},{7,5},{8,10},{9,11},{10,... | collective-permute-start | bytes 2064392 | tf_op jit(solution)/shard_map/ppermute | solution.py:676
  88.1 6.5 %add_convert_fusion.refs_0_ = bf16[2048,768]{1,0:T(8,128)(2,1)} fusion(bf16[2048,768]{1,0:T(8,128)(2,1)} %bitcast.114, bf16[768,768]{0,1:T(8,128)(2,1)} %maximum_select_fusion, f32[768]{0:T(1024)S(1)} %add.117), kind=kOutput, calls=%fused_computation | convolution fusion | flops 2419064832 | bytes 7474176 | tf_op jit(solution)/shard_map/dot_general | solution.py:30
  94.6 27.8 %attend_forward.1 = (bf16[8,384,128]{2,1,0:T(8,128)(2,1)}, f32[3,1,2048]{2,1,0:T(1,128)}) custom-call(s32[1]{0:T(128)} %bitcast.lane_ref, s32[8]{0:T(128)} %get-tuple-element.116.low_ref, s32[8]{0:T(128)} %get-tuple-element.117.count_ref, bf16[2048,768]{1,0:T(8,128)(2,1)} %add_convert_fusion.refs_0_, s32[2048,1]{1,0:T(8,128)} %copy.90.refs_1_, s32[1,2048]{1,0:T(1,128)} %refs_2_.3), custom_call_target="tpu_custom_call" | custom-call | flops 3221225472 | bytes 5242880 | tf_op jit(solution)/shard_map/attend_forward/pallas_call | solution.py:270
  122.5 1.2 constant_dynamic-update-slice_fusion.1
  123.6 1.2 constant_dynamic-update-slice_fusion.refs_0_
  124.9 4.0 %all-to-all-start = ((bf16[4,2,384,128]{3,2,1,0:T(8,128)(2,1)}), bf16[4,2,384,128]{3,2,1,0:T(8,128)(2,1)S(1)}, u32[]{:S(2)}, u32[]{:S(2)}) async-start(bf16[4,2,384,128]{3,2,1,0:T(8,128)(2,1)} %bitcast.19), calls=%async_computation | async-start | bytes 1572864 | tf_op jit(solution)/shard_map/all_to_all | solution.py:781
  133.6 34.5 %all-gather.7.cloned.1.call-done.refs_2_ = bf16[16,96,1792]{2,1,0:T(8,128)(2,1)} async-done(((bf16[2,96,1792]{2,1,0:T(8,128)(2,1)}), bf16[16,96,1792]{2,1,0:T(8,128)(2,1)}) %all-gather.7.cloned.1.call-update) | async-done | bytes 5505040 | tf_op jit(solution)/shard_map/all_gather | solution.py:786
  171.9 26.1 %dense_chain.1 = (bf16[512,768]{1,0:T(8,128)(2,1)}, f32[512,768]{1,0:T(8,128)}, bf16[4,2,384,128]{3,2,1,0:T(8,128)(2,1)}, bf16[512,768]{1,0:T(8,128)(2,1)}, bf16...) custom-call(s32[5]{0:T(128)} %stack.53.place_ref, ...), custom_call_target="tpu_custom_call" | custom-call | flops 11274289152 | bytes 25165824 | tf_op jit(solution)/shard_map/dense_chain/pallas_call | solution.py:492
  200.3 8.6 %dense_weights.3 = bf16[2,768,1856]{2,1,0:T(8,128)(2,1)} custom-call(s32[5]{0:T(128)} %stack.53.place_ref, bf16[512,768]{1,0:T(8,128)(2,1)} %get-tuple-element.74.first_ref, bf16[512,768]{1,0:T(8,128)(2,1)} %get-tuple-element.75.branch_grad_ref, bf16[512,768]{1,0:T(8,128)(2,1)} %get-tuple-element.76.attn_grad_ref, ...), custom_call_target="tpu_custom_call" | custom-call | flops 2919235584 | bytes 10485760 | tf_op jit(solution)/shard_map/dense_weights/pallas_call | solution.py:595
  209.0 4.6 %all-to-all-start.1 = ((bf16[4,2,384,128]{3,2,1,0:T(8,128)(2,1)}), bf16[4,2,384,128]{3,2,1,0:T(8,128)(2,1)S(1)}, u32[]{:S(2)}, u32[]{:S(2)}) async-start(bf16[4,2,384,128]{3,2,1,0:T(8,128)(2,1)} %get-tuple-element.83), calls=%async_computation.1 | async-start | bytes 1572864 | tf_op jit(solution)/shard_map/all_to_all | solution.py:781
  213.6 8.8 %dense_weights.2 = (bf16[8,96,1856]{2,1,0:T(8,128)(2,1)}, bf16[8,96,1856]{2,1,0:T(8,128)(2,1)}) custom-call(s32[5]{0:T(128)} %stack.53.place_ref, bf16[512,768]{1,0:T(8,128)(2,1)} %get-tuple-element.74.first_ref, bf16[512,768]{1,0:T(8,128)(2,1)} %get-tuple-element.75.branch_grad_ref, bf16[512,768]{1,0:T(8,128)(2,1)} %get-tuple-element.76.attn_grad_ref, ...), custom_call_target="tpu_custom_call" | custom-call | flops 2919235584 | bytes 10485760 | tf_op jit(solution)/shard_map/dense_weights/pallas_call | solution.py:595
  222.4 11.7 %all-to-all-done.1 = bf16[4,2,384,128]{3,2,1,0:T(8,128)(2,1)S(1)} async-done(((bf16[4,2,384,128]{3,2,1,0:T(8,128)(2,1)}), bf16[4,2,384,128]{3,2,1,0:T(8,128)(2,1)S(1)}, u32[]{:S(2)}, u32[]{:S(2)}) %all-to-all-start.1) | async-done | bytes 786464 | tf_op jit(solution)/shard_map/all_to_all | solution.py:781
  235.0 38.1 %attend_backward.1 = (bf16[1,2048,768]{2,1,0:T(8,128)(2,1)}, f32[1,768]{1,0:T(1,128)}) custom-call(s32[1]{0:T(128)} %bitcast.lane_ref, s32[8]{0:T(128)} %get-tuple-element.116.low_ref, s32[8]{0:T(128)} %get-tuple-element.117.count_ref, bf16[2048,768]{1,0:T(8,128)(2,1)} %add_convert_fusion.refs_0_, s32[2048,1]{1,0:T(8,128)} %copy.90.refs_1_, ...), custom_call_target="tpu_custom_call" | custom-call | flops 8053063680 | bytes 10485760 | tf_op jit(solution)/shard_map/attend_backward/pallas_call | solution.py:337
  273.1 6.2 %convolution_convert_fusion = bf16[2048,768]{1,0:T(8,128)(2,1)} fusion(bf16[768,768]{0,1:T(8,128)(2,1)S(1)} %copy-done.4, bf16[1,2048,768]{2,1,0:T(8,128)(2,1)} %get-tuple-element.85), kind=kOutput, calls=%fused_computation.1 | convolution fusion | flops 2417491968 | bytes 7471104 | tf_op jit(solution)/shard_map/dot_general | solution.py:30
  279.6 1.5 copy-done.1
  281.3 2.6 fusion
  283.9 9.2 %collective-permute-start.9 = (bf16[2,2,96,1856]{3,2,1,0:T(8,128)(2,1)S(1)}, bf16[2,2,96,1856]{3,2,1,0:T(8,128)(2,1)}, u32[]{:S(2)}, u32[]{:S(2)}) collective-permute-start(bf16[2,2,96,1856]{3,2,1,0:T(8,128)(2,1)S(1)} %get-tuple-element.90), channel_id=1, source_target_pairs={{0,8},{4,12},{8,0},{12,4},{16,24},{20,28},{24,16},{28,20},{1,9},{5... | collective-permute-start | bytes 4276232 | tf_op jit(solution)/shard_map/ppermute | solution.py:676
  293.2 6.9 %fusion.20 = f32[768,768]{1,0:T(8,128)} fusion(bf16[2048,768]{1,0:T(8,128)(2,1)} %bitcast.115, bf16[2048,768]{1,0:T(8,128)(2,1)} %bitcast.120), kind=kOutput, calls=%fused_computation.90 | convolution fusion | flops 2415919104 | bytes 8650752 | tf_op jit(solution)/shard_map/dot_general | solution.py:30
  300.1 17.4 %collective-permute-done.9 = bf16[2,2,96,1856]{3,2,1,0:T(8,128)(2,1)} collective-permute-done((bf16[2,2,96,1856]{3,2,1,0:T(8,128)(2,1)S(1)}, bf16[2,2,96,1856]{3,2,1,0:T(8,128)(2,1)}, u32[]{:S(2)}, u32[]{:S(2)}) %collective-permute-start.9) | collective-permute-done | bytes 1425440 | tf_op jit(solution)/shard_map/ppermute | solution.py:676
  317.6 1.7 add_convert_fusion.3
  319.3 8.8 %collective-permute-start.10 = (bf16[1,2,96,1856]{3,2,1,0:T(8,128)(2,1)S(1)}, bf16[1,2,96,1856]{3,2,1,0:T(8,128)(2,1)S(1)}, u32[]{:S(2)}, u32[]{:S(2)}) collective-permute-start(bf16[1,2,96,1856]{3,2,1,0:T(8,128)(2,1)S(1)} %get-tuple-element.95), channel_id=1, source_target_pairs={{0,16},{4,20},{8,24},{12,28},{16,0},{20,4},{24,8},{28,12},{1,17},{... | collective-permute-start | bytes 2138120 | tf_op jit(solution)/shard_map/ppermute | solution.py:676
  328.3 3.8 collective-permute-done.11
  333.0 3.9 collective-permute-done.12
  338.2 7.0 %collective-permute-done.10 = bf16[1,2,96,1856]{3,2,1,0:T(8,128)(2,1)S(1)} collective-permute-done((bf16[1,2,96,1856]{3,2,1,0:T(8,128)(2,1)S(1)}, bf16[1,2,96,1856]{3,2,1,0:T(8,128)(2,1)S(1)}, u32[]{:S(2)}, u32[]{:S(2)}) %collective-permute-start.10) | collective-permute-done | bytes 712736 | tf_op jit(solution)/shard_map/ppermute | solution.py:676
  345.4 1.8 fusion.6
  347.2 1.4 pad_maximum_fusion
  349.4 1.2 add_convert_fusion.1
  350.7 1.9 collective-permute-done.13
  353.0 9.0 %collective-permute-done.14 = bf16[2,96,768]{2,1,0:T(8,128)(2,1)S(1)} collective-permute-done((bf16[2,96,768]{2,1,0:T(8,128)(2,1)S(1)}, bf16[2,96,768]{2,1,0:T(8,128)(2,1)S(1)}, u32[]{:S(2)}, u32[]{:S(2)}) %collective-permute-start.14) | collective-permute-done | bytes 294944 | tf_op jit(solution)/shard_map/ppermute | solution.py:676
  362.1 2.2 collective-permute-start.15
  364.3 3.4 collective-permute-done.15
  368.4 1.7 finish_heads.1
  372.2 2.4 add_bitcast_fusion
  374.7 7.4 %reduce-scatter.6.cloned.1.call-done = bf16[1,96,1856]{2,1,0:T(8,128)(2,1)} async-done(((bf16[4,96,1856]{2,1,0:T(8,128)(2,1)}), bf16[1,96,1856]{2,1,0:T(8,128)(2,1)}) %reduce-scatter.6.cloned.1.call-update) | async-done | bytes 356368 | tf_op jit(solution)/shard_map/reduce_scatter | solution.py:863
  382.1 1.9 finish_dense.1
  384.0 2.0 slice_bitcast_fusion.1
  386.0 1.3 slice_bitcast_fusion
  (141 shorter events, 25.3 us)
Async XLA Ops:
  7.2 4.3 %copy-start.10 = (s32[1,512]{1,0:T(1,128)S(1)}, s32[1,512]{1,0:T(1,128)}, u32[]{:S(2)}) copy-start(s32[1,512]{1,0:T(1,128)} %param.22) | copy-start | bytes 6148
  7.2 9.2 %copy-start.8 = (bf16[192,96]{1,0:T(8,128)(2,1)S(1)}, bf16[192,96]{1,0:T(8,128)(2,1)}, u32[]{:S(2)}) copy-start(bf16[192,96]{1,0:T(8,128)(2,1)} %param.28) | copy-start | bytes 110596
  7.2 9.3 %copy-start.7 = (bf16[768,96]{0,1:T(8,128)(2,1)S(1)}, bf16[768,96]{0,1:T(8,128)(2,1)}, u32[]{:S(2)}) copy-start(bf16[768,96]{0,1:T(8,128)(2,1)} %param.30) | copy-start | bytes 442372
  7.2 9.3 %copy-start.6 = (bf16[96,768]{1,0:T(8,128)(2,1)S(1)}, bf16[96,768]{1,0:T(8,128)(2,1)}, u32[]{:S(2)}) copy-start(bf16[96,768]{1,0:T(8,128)(2,1)} %param.29) | copy-start | bytes 442372
  7.2 75.8 %all-gather.5.cloned.1.call-start = ((), (), s32[]{:S(2)}) async-start(), calls=%async_computation.8 | async-start | bytes 3932160 | tf_op jit(solution)/shard_map/all_gather | solution.py:739
  8.0 160.1 %all-gather.7.cloned.1.call-start = ((), (), s32[]{:S(2)}) async-start(), calls=%async_computation.9 | async-start | bytes 6193152 | tf_op jit(solution)/shard_map/all_gather | solution.py:786
  11.0 2.4 collective-permute-start.2
  13.8 12.3 %collective-permute-start.3 = (bf16[192,768]{0,1:T(8,128)(2,1)S(1)}, bf16[192,768]{0,1:T(8,128)(2,1)S(1)}, u32[]{:S(2)}, u32[]{:S(2)}) collective-permute-start(bf16[192,768]{0,1:T(8,128)(2,1)S(1)} %maximum_select_fusion.2), channel_id=1, source_target_pairs={{0,8},{4,12},{8,0},{12,4},{16,24},{20,28},{24,16},{28,20},{1,9},{5... | collective-permute-start | bytes 884744 | tf_op jit(solution)/shard_map/ppermute | solution.py:676
  16.7 25.5 %collective-permute-start = (bf16[1,96,1792]{2,1,0:T(8,128)(2,1)S(1)}, bf16[1,96,1792]{2,1,0:T(8,128)(2,1)S(1)}, u32[]{:S(2)}, u32[]{:S(2)}) collective-permute-start(bf16[1,96,1792]{2,1,0:T(8,128)(2,1)S(1)} %bitcast.87), channel_id=1, source_target_pairs={{0,1},{1,0},{2,3},{3,2},{4,5},{5,4},{6,7},{7,6},{8,9},{9,8},{10,11... | collective-permute-start | bytes 1032200 | tf_op jit(solution)/shard_map/ppermute | solution.py:676
  26.6 15.8 %collective-permute-start.4 = (bf16[384,768]{0,1:T(8,128)(2,1)S(1)}, bf16[384,768]{0,1:T(8,128)(2,1)S(1)}, u32[]{:S(2)}, u32[]{:S(2)}) collective-permute-start(bf16[384,768]{0,1:T(8,128)(2,1)S(1)} %maximum_select_fusion.1), channel_id=1, source_target_pairs={{0,16},{4,20},{8,24},{12,28},{16,0},{20,4},{24,8},{28,12},{1,17},{... | collective-permute-start | bytes 1769480 | tf_op jit(solution)/shard_map/ppermute | solution.py:676
  42.3 13.3 %collective-permute-start.1 = (bf16[2,96,1792]{2,1,0:T(8,128)(2,1)S(1)}, bf16[2,96,1792]{2,1,0:T(8,128)(2,1)S(1)}, u32[]{:S(2)}, u32[]{:S(2)}) collective-permute-start(bf16[2,96,1792]{2,1,0:T(8,128)(2,1)S(1)} %pad_maximum_fusion.2), channel_id=1, source_target_pairs={{0,8},{4,12},{8,0},{12,4},{16,24},{20,28},{24,16},{28,20},{1,9},{5... | collective-permute-start | bytes 2064392 | tf_op jit(solution)/shard_map/ppermute | solution.py:676
  43.7 13.7 %copy-start.9 = (s32[1,2048]{1,0:T(1,128)S(1)}, s32[1,2048]{1,0:T(1,128)}, u32[]{:S(2)}) copy-start(s32[1,2048]{1,0:T(1,128)} %refs_2_.3) | copy-start | bytes 24580
  55.8 27.3 %collective-permute-start.5 = (bf16[4,96,1792]{2,1,0:T(8,128)(2,1)S(1)}, bf16[4,96,1792]{2,1,0:T(8,128)(2,1)S(1)}, u32[]{:S(2)}, u32[]{:S(2)}) collective-permute-start(bf16[4,96,1792]{2,1,0:T(8,128)(2,1)S(1)} %pad_maximum_fusion.1), channel_id=1, source_target_pairs={{0,16},{4,20},{8,24},{12,28},{16,0},{20,4},{24,8},{28,12},{1,17},{... | collective-permute-start | bytes 4128776 | tf_op jit(solution)/shard_map/ppermute | solution.py:676
  83.0 39.4 %collective-permute-start.6 = (bf16[2,96,1792]{2,1,0:T(8,128)(2,1)S(1)}, bf16[2,96,1792]{2,1,0:T(8,128)(2,1)}, u32[]{:S(2)}, u32[]{:S(2)}) collective-permute-start(bf16[2,96,1792]{2,1,0:T(8,128)(2,1)S(1)} %pad_maximum_fusion.2), channel_id=1, source_target_pairs={{0,2},{1,3},{2,0},{3,1},{4,6},{5,7},{6,4},{7,5},{8,10},{9,11},{10,... | collective-permute-start | bytes 2064392 | tf_op jit(solution)/shard_map/ppermute | solution.py:676
  124.8 5.0 %copy-start.13 = (bf16[768]{0:T(1024)(128)(2,1)S(1)}, bf16[768]{0:T(1024)(128)(2,1)}, u32[]{:S(2)}) copy-start(bf16[768]{0:T(1024)(128)(2,1)} %param.33) | copy-start | bytes 4612
  124.8 5.0 %copy-start.14 = (bf16[768]{0:T(1024)(128)(2,1)S(1)}, bf16[768]{0:T(1024)(128)(2,1)}, u32[]{:S(2)}) copy-start(bf16[768]{0:T(1024)(128)(2,1)} %param.36) | copy-start | bytes 4612
  124.8 5.0 %copy-start.15 = (bf16[768]{0:T(1024)(128)(2,1)S(1)}, bf16[768]{0:T(1024)(128)(2,1)}, u32[]{:S(2)}) copy-start(bf16[768]{0:T(1024)(128)(2,1)} %param.37) | copy-start | bytes 4612
  124.8 5.0 %copy-start.16 = (bf16[768]{0:T(1024)(128)(2,1)S(1)}, bf16[768]{0:T(1024)(128)(2,1)}, u32[]{:S(2)}) copy-start(bf16[768]{0:T(1024)(128)(2,1)} %param.35) | copy-start | bytes 4612
  124.8 5.0 %copy-start.17 = (bf16[768]{0:T(1024)(128)(2,1)S(1)}, bf16[768]{0:T(1024)(128)(2,1)}, u32[]{:S(2)}) copy-start(bf16[768]{0:T(1024)(128)(2,1)} %param.38) | copy-start | bytes 4612
  124.8 5.0 %copy-start.18 = (bf16[768]{0:T(1024)(128)(2,1)S(1)}, bf16[768]{0:T(1024)(128)(2,1)}, u32[]{:S(2)}) copy-start(bf16[768]{0:T(1024)(128)(2,1)} %param.39) | copy-start | bytes 4612
  124.8 5.7 %copy-start.11 = (bf16[3072]{0:T(1024)(128)(2,1)S(1)}, bf16[3072]{0:T(1024)(128)(2,1)}, u32[]{:S(2)}) copy-start(bf16[3072]{0:T(1024)(128)(2,1)} %param.34) | copy-start | bytes 18436
  124.9 7.8 %collective-permute-start.7 = (bf16[8,96,1792]{2,1,0:T(8,128)(2,1)}, bf16[8,96,1792]{2,1,0:T(8,128)(2,1)}, u32[]{:S(2)}, u32[]{:S(2)}) collective-permute-start(bf16[8,96,1792]{2,1,0:T(8,128)(2,1)} %constant_dynamic-update-slice_fusion.refs_0_), channel_id=1, source_target_pairs={{0,4},{4,0},{8,12},{12,8},{16,20},{20,16},{24,28},{28,24},{1,5},{5... | collective-permute-start | bytes 8257544 | tf_op jit(solution)/shard_map/ppermute | solution.py:676
  124.9 46.1 %all-to-all-start = ((bf16[4,2,384,128]{3,2,1,0:T(8,128)(2,1)}), bf16[4,2,384,128]{3,2,1,0:T(8,128)(2,1)S(1)}, u32[]{:S(2)}, u32[]{:S(2)}) async-start(bf16[4,2,384,128]{3,2,1,0:T(8,128)(2,1)} %bitcast.19), calls=%async_computation | async-start | bytes 1572864 | tf_op jit(solution)/shard_map/all_to_all | solution.py:781
  128.9 216.5 %reduce-scatter.4.cloned.1.call-start = ((), (), s32[]{:S(2)}) async-start(), calls=%async_computation.5 | async-start | bytes 6635520 | tf_op jit(solution)/shard_map/reduce_scatter | solution.py:828
  171.0 0.9 copy-start
  209.0 25.1 %all-to-all-start.1 = ((bf16[4,2,384,128]{3,2,1,0:T(8,128)(2,1)}), bf16[4,2,384,128]{3,2,1,0:T(8,128)(2,1)S(1)}, u32[]{:S(2)}, u32[]{:S(2)}) async-start(bf16[4,2,384,128]{3,2,1,0:T(8,128)(2,1)} %get-tuple-element.83), calls=%async_computation.1 | async-start | bytes 1572864 | tf_op jit(solution)/shard_map/all_to_all | solution.py:781
  213.6 158.7 %reduce-scatter.8.cloned.1.call-start = ((), (), s32[]{:S(2)}) async-start(), calls=%async_computation.7 | async-start | bytes 3932160 | tf_op jit(solution)/shard_map/reduce_scatter | solution.py:842
  222.3 59.0 %collective-permute-start.8 = (bf16[4,2,96,1856]{3,2,1,0:T(8,128)(2,1)}, bf16[4,2,96,1856]{3,2,1,0:T(8,128)(2,1)}, u32[]{:S(2)}, u32[]{:S(2)}) collective-permute-start(bf16[4,2,96,1856]{3,2,1,0:T(8,128)(2,1)} %bitcast.116), channel_id=1, source_target_pairs={{0,4},{4,0},{8,12},{12,8},{16,20},{20,16},{24,28},{28,24},{1,5},{5... | collective-permute-start | bytes 8552456 | tf_op jit(solution)/shard_map/ppermute | solution.py:676
  234.1 0.9 copy-start.5
  235.0 38.1 %copy-start.4 = (bf16[768,768]{0,1:T(8,128)(2,1)S(1)}, bf16[768,768]{0,1:T(8,128)(2,1)}, u32[]{:S(2)}) copy-start(bf16[768,768]{0,1:T(8,128)(2,1)} %maximum_select_fusion) | copy-start | bytes 3538948
  279.2 1.8 copy-start.1
  279.3 102.8 %reduce-scatter.6.cloned.1.call-start = ((), (), s32[]{:S(2)}) async-start(), calls=%async_computation.6 | async-start | bytes 1843200 | tf_op jit(solution)/shard_map/reduce_scatter | solution.py:863
  281.3 11.8 %copy-start.12 = (f32[1,768]{1,0:T(1,128)S(1)}, f32[1,768]{1,0:T(1,128)}, u32[]{:S(2)}) copy-start(f32[1,768]{1,0:T(1,128)} %get-tuple-element.102) | copy-start | bytes 9220
  283.9 33.7 %collective-permute-start.9 = (bf16[2,2,96,1856]{3,2,1,0:T(8,128)(2,1)S(1)}, bf16[2,2,96,1856]{3,2,1,0:T(8,128)(2,1)}, u32[]{:S(2)}, u32[]{:S(2)}) collective-permute-start(bf16[2,2,96,1856]{3,2,1,0:T(8,128)(2,1)S(1)} %get-tuple-element.90), channel_id=1, source_target_pairs={{0,8},{4,12},{8,0},{12,4},{16,24},{20,28},{24,16},{28,20},{1,9},{5... | collective-permute-start | bytes 4276232 | tf_op jit(solution)/shard_map/ppermute | solution.py:676
  319.3 25.9 %collective-permute-start.10 = (bf16[1,2,96,1856]{3,2,1,0:T(8,128)(2,1)S(1)}, bf16[1,2,96,1856]{3,2,1,0:T(8,128)(2,1)S(1)}, u32[]{:S(2)}, u32[]{:S(2)}) collective-permute-start(bf16[1,2,96,1856]{3,2,1,0:T(8,128)(2,1)S(1)} %get-tuple-element.95), channel_id=1, source_target_pairs={{0,16},{4,20},{8,24},{12,28},{16,0},{20,4},{24,8},{28,12},{1,17},{... | collective-permute-start | bytes 2138120 | tf_op jit(solution)/shard_map/ppermute | solution.py:676
  328.3 3.8 collective-permute-start.11
  332.2 4.7 %collective-permute-start.12 = (f32[2,384]{1,0:T(2,128)S(1)}, f32[2,384]{1,0:T(2,128)S(1)}, u32[]{:S(2)}, u32[]{:S(2)}) collective-permute-start(f32[2,384]{1,0:T(2,128)S(1)} %maximum_select_fusion.4), channel_id=1, source_target_pairs={{0,2},{1,3},{2,0},{3,1},{4,6},{5,7},{6,4},{7,5},{8,10},{9,11},{10,... | collective-permute-start | bytes 9224 | tf_op jit(solution)/shard_map/ppermute | solution.py:676
  347.2 2.2 copy-start.2
  350.6 2.1 collective-permute-start.13
  352.8 19.4 %copy-start.3 = (f32[512,768]{1,0:T(8,128)S(1)}, f32[512,768]{1,0:T(8,128)}, u32[]{:S(2)}) copy-start(f32[512,768]{1,0:T(8,128)} %get-tuple-element.99) | copy-start | bytes 4718596
  352.8 9.1 %collective-permute-start.14 = (bf16[2,96,768]{2,1,0:T(8,128)(2,1)S(1)}, bf16[2,96,768]{2,1,0:T(8,128)(2,1)S(1)}, u32[]{:S(2)}, u32[]{:S(2)}) collective-permute-start(bf16[2,96,768]{2,1,0:T(8,128)(2,1)S(1)} %dynamic-slice_bitcast_fusion.1), channel_id=1, source_target_pairs={{0,8},{4,12},{8,0},{12,4},{16,24},{20,28},{24,16},{28,20},{1,9},{5... | collective-permute-start | bytes 884744 | tf_op jit(solution)/shard_map/ppermute | solution.py:676
  362.1 5.7 %collective-permute-start.15 = (bf16[1,96,768]{2,1,0:T(8,128)(2,1)S(1)}, bf16[1,96,768]{2,1,0:T(8,128)(2,1)S(1)}, u32[]{:S(2)}, u32[]{:S(2)}) collective-permute-start(bf16[1,96,768]{2,1,0:T(8,128)(2,1)S(1)} %constant_dynamic-slice_fusion), channel_id=1, source_target_pairs={{0,16},{4,20},{8,24},{12,28},{16,0},{20,4},{24,8},{28,12},{1,17},{... | collective-permute-start | bytes 442376 | tf_op jit(solution)/shard_map/ppermute | solution.py:676
Sparse Core Ops, SparseCore 0:
  9.6 68.1 all-gather.4
  122.6 45.4 all-gather.6
  209.1 61.4 reduce-scatter.3
  279.4 66.6 reduce-scatter.7
  348.7 33.3 reduce-scatter.5

commit v12 on v11

--- a/solution.py
+++ b/solution.py
@@ -74,10 +74,9 @@
 
 
 def attend_forward(
-    which, lane_ref, low_ref, count_ref, *refs
+    first_block, lane_ref, low_ref, count_ref, *refs
 ):
     chunk_refs, (seg_col_ref, seg_row_ref, ctx_ref, lse_ref, held, qkv_ref, sems) = refs[:-7], refs[-7:]
-    halves, half = which
     heads = lse_ref.shape[0]
 
     @pl.when(pl.program_id(0) == 0)
@@ -88,7 +87,7 @@
         for copy in copies:
             copy.wait()
 
-    qb = pl.program_id(0) * halves + half
+    qb = pl.program_id(0) + first_block
     rows = pl.ds(pl.multiple_of(qb * BLOCK, BLOCK), BLOCK)
     seg_q = seg_col_ref[...]
     queries = [
@@ -261,14 +260,12 @@
 PACKED = BLOCK + BLOCK // 2
 
 
-def run_forward(which, lane, bounds, qkv, seg_col, seg_row):
-    halves, half = which
+def run_forward(first_block, steps, lane, bounds, qkv, seg_col, seg_row):
     seq_len, width = seg_col.shape[0], qkv[0].shape[1]
     heads = width // SLAB
     blocks = seq_len // BLOCK
-    steps = blocks // halves
     return pl.pallas_call(
-        functools.partial(attend_forward, which),
+        functools.partial(attend_forward, first_block),
         out_shape=(
             jax.ShapeDtypeStruct((steps, PACKED, 2 * DH), BF16),
             jax.ShapeDtypeStruct((heads, 1, steps * BLOCK), F32),
@@ -278,7 +275,7 @@
             grid=(steps,),
             in_specs=[pl.BlockSpec(memory_space=pl.ANY)] * len(qkv)
             + [
-                pl.BlockSpec((BLOCK, 1), lambda q, *_: (q * halves + half, 0)),
+                pl.BlockSpec((BLOCK, 1), lambda q, *_: (q + first_block, 0)),
                 pl.BlockSpec((1, seq_len), lambda q, *_: (0, 0)),
             ],
             out_specs=(
@@ -295,9 +292,9 @@
             dimension_semantics=("arbitrary",), vmem_limit_bytes=VMEM_LIMIT
         ),
         cost_estimate=pl.CostEstimate(
-            flops=heads * seq_len * seq_len * 256 // halves,
+            flops=heads * seq_len * seq_len * 2048 * steps // blocks,
             bytes_accessed=5 << 20,
-            transcendentals=heads * seq_len * seq_len // 3 // halves,
+            transcendentals=heads * seq_len * seq_len // 3,
         ),
         name="attend_forward",
     )(lane, *bounds, *qkv, seg_col, seg_row)
@@ -356,7 +353,7 @@
             dimension_semantics=("arbitrary",), vmem_limit_bytes=VMEM_LIMIT
         ),
         cost_estimate=pl.CostEstimate(
-            flops=heads * seq_len * seq_len * 640 // halves,
+            flops=heads * seq_len * seq_len * 4096,
             bytes_accessed=10 << 20,
             transcendentals=heads * seq_len * seq_len // 3 // halves,
         ),
@@ -365,7 +362,7 @@
 
 
 def dense_chain(
-    marks, place_ref, ratio_ref, ctx_ref, in_ref, teacher_ref, cotangent_ref, valid_ref, vec_ref,
+    marks, total_tokens, place_ref, ctx_ref, in_ref, teacher_ref, cotangent_ref, valid_ref, vec_ref,
     inner_bias_ref, *refs
 ):
     pieces = refs[: len(marks)]
@@ -408,9 +405,12 @@
     def vec(which):
         return vec_ref[which : which + 1, :]
 
+    counts = jnp.zeros((1, 2 * DH), F32)
+
     attention = jnp.zeros(in_ref.shape, F32)
     for slot in range(parts):
         arrive(0, slot)
+        counts = counts + column_sum(w_out[slot, :, 2 * DH :].astype(F32))
         attention = attention + dot(unpack(ctx_ref[place_ref[slot], 0]), w_out[slot, :, : 3 * DH], NT)
     first_exact, normed_one, inverse_one = norm_forward(
         in_ref[...].astype(F32) + attention + vec(0), vec(1), vec(2)
@@ -432,11 +432,14 @@
     branch = jnp.zeros(in_ref.shape, F32)
     for slot in range(parts):
         branch = up(slot, branch)
+    lanes = lax.broadcasted_iota(jnp.int32, counts.shape, 1)
+    weight = jnp.where(lanes == DH, 256.0, jnp.where(lanes == DH + 1, 1.0, 0.0))
+    ratio = total_tokens / jnp.sum(jnp.where(weight > 0.0, counts, 0.0) * weight, axis=-1, keepdims=True)
     layer_rows, normed_two, inverse_two = norm_forward(first.astype(F32) + branch + vec(3), vec(4), vec(5))
     layer_ref[...] = layer_rows.astype(BF16)
     misfit = layer_rows - teacher_ref[...].astype(F32)
     weighted = valid_ref[...] * misfit
-    out_grad = cotangent_ref[...].astype(F32) + weighted * ratio_ref[0]
+    out_grad = cotangent_ref[...].astype(F32) + weighted * ratio
     second_grad = norm_backward(out_grad, normed_two, inverse_two, vec(4))
     branch_grad = second_grad.astype(BF16)
     branch_grad_ref[...] = branch_grad
@@ -470,7 +473,7 @@
         )
 
 
-def run_dense(marks, place, ratio, ctx, rows_in, teacher, cotangent, valid, vecs, inner_bias, pieces):
+def run_dense(marks, total_tokens, place, ctx, rows_in, teacher, cotangent, valid, vecs, inner_bias, pieces):
     parts, halves = ctx.shape[:2]
     part_len, width = rows_in.shape
     hidden_cols = inner_bias.shape[2]
@@ -490,7 +493,7 @@
     wide = jax.ShapeDtypeStruct((parts, part_len, hidden_cols), BF16)
     smem = pl.BlockSpec(memory_space=pltpu.SMEM)
     return pl.pallas_call(
-        functools.partial(dense_chain, marks),
+        functools.partial(dense_chain, marks, total_tokens),
         out_shape=(
             low,
             jax.ShapeDtypeStruct((part_len, width), F32),
@@ -505,7 +508,6 @@
         ),
         grid=(halves,),
         in_specs=[
-            smem,
             smem,
             packed,
             by_rows(width),
@@ -539,12 +541,12 @@
             dimension_semantics=("arbitrary",), vmem_limit_bytes=VMEM_LIMIT
         ),
         cost_estimate=pl.CostEstimate(
-            flops=part_len * width * (8 * hidden_cols + 4 * out_cols) * parts,
+            flops=2 * part_len * width * (8 * hidden_cols + 4 * out_cols) * parts,
             bytes_accessed=24 << 20,
             transcendentals=2 * part_len * hidden_cols * parts,
         ),
         name="dense_chain",
-    )(place, ratio, ctx, rows_in, teacher, cotangent, valid, vecs, inner_bias, *pieces)
+    )(place, ctx, rows_in, teacher, cotangent, valid, vecs, inner_bias, *pieces)
 
 
 def dense_weights(
@@ -780,10 +782,16 @@
     def exchange(packed_blocks):
         return lax.all_to_all(packed_blocks.reshape(parts, halves, PACKED, 2 * DH), "tensor", 0, 0)
 
-    context, lse = run_forward((1, 0), lane, bounds, qkv, seg_col, seg_row)
+    blocks = seq_len // BLOCK
+    early = run_forward(0, blocks // 2, lane, bounds, qkv, seg_col, seg_row)
     if paired:
-        near_next, far, context = lax.optimization_barrier((near_next, far, context))
+        far, early, bounds = lax.optimization_barrier((far, early, bounds))
         weights = lax.all_gather(far, "dp", axis=0, tiled=False)
+    late = run_forward(blocks // 2, blocks // 2, lane, bounds, qkv, seg_col, seg_row)
+    context = jnp.concatenate((early[0], late[0]), axis=0)
+    lse = jnp.concatenate((early[1], late[1]), axis=2)
+    if paired:
+        near_next, context = lax.optimization_barrier((near_next, context))
         near = jnp.concatenate([near, near_next], axis=0)
         near_other = swap(near, "dp", 1)
     arrived = exchange(context)
@@ -798,7 +806,6 @@
     counts = [piece.reshape((-1,) + mine.shape)[:, 0, -DH : 2 - DH].astype(F32) for piece in pieces + [weights]]
     counts = jnp.concatenate(counts[:-1] if paired else counts[-1:], axis=0)
     counted = 256.0 * jnp.sum(counts[:, 0]) + jnp.sum(counts[:, 1])
-    ratio = (total_tokens / counted).reshape(1)
 
     vecs = jnp.stack(
         (output_bias, gain_attn, shift_attn, outer_bias, gain_ffn, shift_ffn, outer_bias, outer_bias)
@@ -810,7 +817,7 @@
         layer_out, first_grad, context_grad, first, branch_grad, attn_grad, activated, hidden_grad,
         dense_sums, inner_sums,
     ) = run_dense(
-        marks, place, ratio, arrived, rows_in, teacher_rows, cotangent_rows, valid_rows, vecs,
+        marks, float(total_tokens), place, arrived, rows_in, teacher_rows, cotangent_rows, valid_rows, vecs,
         inner_rows, pieces,
     )
     head_grad = exchange(context_grad).reshape(context.shape)

time: 398 us -> 390 us (0.980)
  starting transfers between devices: 43.8 us -> 25.6 us
  Pallas kernels: 113 us -> 130 us
  waiting for transfers between devices: 156 us -> 148 us
    all_gather x1, waiting for transfers between devices: 34.5 us -> 0.01 us  [local(): weights = lax.all_gather(far, 'dp', axis=0, tiled=False)]
    ppermute x16, starting transfers between devices: 34.8 us -> 16.7 us  [swap(): return lax.ppermute(value, axis, [(i, i ^ bit) for i in range(size)])]
    all_to_all x2, waiting for transfers between devices: 11.7 us -> 27.9 us  [exchange(): lax.all_to_all(packed_blocks.reshape(parts, halves, PACKED, 2 * DH), 'ten...]
    pallas_call x2 -> x3, Pallas kernels: 53.9 us -> 62.8 us  [the longest x2 36.6 us: run_forward(): pl.pallas_call(functools.partial(attend_forward, first_block), out_shape=...]
    pallas_call x1, Pallas kernels: 38.1 us -> 46.6 us  [run_backward(): pl.pallas_call(functools.partial(attend_backward, which, len(qkv)), out_s...]
    reduce_scatter x1, waiting for transfers between devices: 7.41 us -> 14 us  [local(): lax.psum_scatter(packed, 'tensor', scatter_dimension=0, tiled=True)[0]]
    unnamed x44 -> x50, local copies, waits for them, and re-layouts: 8.23 us -> 8.15 us
  transfers between devices with their start and end apart: 23 -> 23, of which waited for: 14 -> 14; matrix products, arithmetic and copies ran while one was open for 14% -> 15% of each run, Pallas kernels for 19% -> 24%
where the time goes in v12:
time: 390 us; the launch traced here: 391 us
  waiting for transfers between devices  148 us (38%)
  Pallas kernels  130 us (33%)
  other arithmetic  26.2 us (7%)
  starting transfers between devices  25.6 us (7%)
  local copies, waits for them, and re-layouts  21.6 us (6%)
  matrix products  19.6 us (5%)
  between operations  18.9 us (5%)
    ppermute x16, waiting for transfers between devices, swap(): return lax.ppermute(value, axis, [(i, i ^ bit) for i in range(size)])  106 us
    pallas_call x1, Pallas kernels, run_backward(): pl.pallas_call(functools.partial(attend_backward, which, len(qkv)), out_s...  46.6 us
    pallas_call x2, Pallas kernels, run_forward(): pl.pallas_call(functools.partial(attend_forward, first_block), out_shape=...  36.6 us
    all_to_all x2, waiting for transfers between devices, exchange(): lax.all_to_all(packed_blocks.reshape(parts, halves, PACKED, 2 * DH), 'ten...  27.9 us
    pallas_call x1, Pallas kernels, run_dense(): pl.pallas_call(functools.partial(dense_chain, marks, total_tokens), out_s...  26.2 us
    dot_general x3, matrix products, dot(): lax.dot_general(left_side, right_side, dims, preferred_element_type=F32)  19.6 us
    pallas_call x2, Pallas kernels, run_weights(): pl.pallas_call(functools.partial(dense_weights, tuple((turns for _, turns...  17.5 us
    ppermute x16, starting transfers between devices, swap(): return lax.ppermute(value, axis, [(i, i ^ bit) for i in range(size)])  16.7 us
  transfers between devices with their start and end apart: 23, of which 14 were waited for; matrix products, arithmetic and copies ran while one was open for 15% of the time, Pallas kernels for 24%

profile of v12, /device:TPU:0, one launch (start us, length us, event | category | flops | bytes accessed | tf_op | source)
XLA Modules:
  0.0 390.8 jit_solution(14244645066261741891)
XLA Ops:
  13.8 2.6 collective-permute-start.3
  16.7 1.6 collective-permute-start
  18.3 7.8 %collective-permute-done.3 = bf16[192,768]{0,1:T(8,128)(2,1)S(1)} collective-permute-done((bf16[192,768]{0,1:T(8,128)(2,1)S(1)}, bf16[192,768]{0,1:T(8,128)(2,1)S(1)}, u32[]{:S(2)}, u32[]{:S(2)}) %collective-permute-start.3) | collective-permute-done | bytes 294944 | tf_op jit(solution)/shard_map/ppermute | solution.py:678
  26.6 1.8 collective-permute-start.4
  28.5 13.8 %collective-permute-done = bf16[1,96,1792]{2,1,0:T(8,128)(2,1)S(1)} collective-permute-done((bf16[1,96,1792]{2,1,0:T(8,128)(2,1)S(1)}, bf16[1,96,1792]{2,1,0:T(8,128)(2,1)S(1)}, u32[]{:S(2)}, u32[]{:S(2)}) %collective-permute-start) | collective-permute-done | bytes 344096 | tf_op jit(solution)/shard_map/ppermute | solution.py:678
  42.4 1.3 maximum_select_fusion
  43.7 12.0 %collective-permute-done.1 = bf16[2,96,1792]{2,1,0:T(8,128)(2,1)} collective-permute-done((bf16[2,96,1792]{2,1,0:T(8,128)(2,1)S(1)}, bf16[2,96,1792]{2,1,0:T(8,128)(2,1)}, u32[]{:S(2)}, u32[]{:S(2)}) %collective-permute-start.1) | collective-permute-done | bytes 688160 | tf_op jit(solution)/shard_map/ppermute | solution.py:678
  55.7 1.2 pad_maximum_fusion.1
  57.0 1.7 collective-permute-start.5
  60.0 1.4 copy.93.refs_1_
  62.2 22.0 %collective-permute-done.5 = bf16[4,96,1792]{2,1,0:T(8,128)(2,1)S(1)} collective-permute-done((bf16[4,96,1792]{2,1,0:T(8,128)(2,1)S(1)}, bf16[4,96,1792]{2,1,0:T(8,128)(2,1)S(1)}, u32[]{:S(2)}, u32[]{:S(2)}) %collective-permute-start.5) | collective-permute-done | bytes 1376288 | tf_op jit(solution)/shard_map/ppermute | solution.py:678
  84.2 5.0 %collective-permute-start.6 = (bf16[2,96,1792]{2,1,0:T(8,128)(2,1)S(1)}, bf16[2,96,1792]{2,1,0:T(8,128)(2,1)}, u32[]{:S(2)}, u32[]{:S(2)}) collective-permute-start(bf16[2,96,1792]{2,1,0:T(8,128)(2,1)S(1)} %pad_maximum_fusion.3), channel_id=1, source_target_pairs={{0,2},{1,3},{2,0},{3,1},{4,6},{5,7},{6,4},{7,5},{8,10},{9,11},{10,... | collective-permute-start | bytes 2064392 | tf_op jit(solution)/shard_map/ppermute | solution.py:678
  89.2 6.5 %add_convert_fusion.refs_0_ = bf16[2048,768]{1,0:T(8,128)(2,1)} fusion(bf16[2048,768]{1,0:T(8,128)(2,1)} %bitcast.113, bf16[768,768]{0,1:T(8,128)(2,1)} %maximum_select_fusion, f32[768]{0:T(1024)S(1)} %add.117), kind=kOutput, calls=%fused_computation | convolution fusion | flops 2419064832 | bytes 7474176 | tf_op jit(solution)/shard_map/dot_general | solution.py:30
  95.7 17.9 %attend_forward.2 = (bf16[4,384,128]{2,1,0:T(8,128)(2,1)}, f32[3,1,1024]{2,1,0:T(1,128)}) custom-call(s32[1]{0:T(128)} %bitcast.lane_ref, s32[8]{0:T(128)} %get-tuple-element.78.low_ref, s32[8]{0:T(128)} %get-tuple-element.79.count_ref, bf16[2048,768]{1,0:T(8,128)(2,1)} %add_convert_fusion.refs_0_, s32[2048,1]{1,0:T(8,128)} %copy.93.refs_1_, s32[1,2048]{1,0:T(1,128)} %refs_2_.5), custom_call_target="tpu_custom_call" | custom-call | flops 12884901888 | bytes 5242880 | tf_op jit(solution)/shard_map/attend_forward/pallas_call | solution.py:267
  113.6 1.2 constant_dynamic-update-slice_fusion.1
  114.8 18.7 %attend_forward.3 = (bf16[4,384,128]{2,1,0:T(8,128)(2,1)}, f32[3,1,1024]{2,1,0:T(1,128)}) custom-call(s32[1]{0:T(128)} %bitcast.lane_ref, s32[8]{0:T(128)} %get-tuple-element.78.low_ref, s32[8]{0:T(128)} %get-tuple-element.79.count_ref, bf16[2048,768]{1,0:T(8,128)(2,1)} %add_convert_fusion.refs_0_, s32[2048,1]{1,0:T(8,128)} %copy.93.refs_1_, s32[1,2048]{1,0:T(1,128)} %refs_2_.5), custom_call_target="tpu_custom_call" | custom-call | flops 12884901888 | bytes 5242880 | tf_op jit(solution)/shard_map/attend_forward/pallas_call | solution.py:267
  133.5 2.0 pad_maximum_fusion.2.refs_3_
  135.5 1.2 constant_dynamic-update-slice_fusion.refs_0_
  136.8 4.8 %all-to-all-start = ((bf16[4,2,384,128]{3,2,1,0:T(8,128)(2,1)}), bf16[4,2,384,128]{3,2,1,0:T(8,128)(2,1)S(1)}, u32[]{:S(2)}, u32[]{:S(2)}) async-start(bf16[4,2,384,128]{3,2,1,0:T(8,128)(2,1)} %bitcast.15), calls=%async_computation | async-start | bytes 1572864 | tf_op jit(solution)/shard_map/all_to_all | solution.py:783
  144.5 17.8 %all-to-all-done.ctx_ref = bf16[4,2,384,128]{3,2,1,0:T(8,128)(2,1)S(1)} async-done(((bf16[4,2,384,128]{3,2,1,0:T(8,128)(2,1)}), bf16[4,2,384,128]{3,2,1,0:T(8,128)(2,1)S(1)}, u32[]{:S(2)}, u32[]{:S(2)}) %all-to-all-start) | async-done | bytes 786464 | tf_op jit(solution)/shard_map/all_to_all | solution.py:783
  163.2 26.2 %dense_chain.1 = (bf16[512,768]{1,0:T(8,128)(2,1)}, f32[512,768]{1,0:T(8,128)}, bf16[4,2,384,128]{3,2,1,0:T(8,128)(2,1)}, bf16[512,768]{1,0:T(8,128)(2,1)}, bf16...) custom-call(s32[5]{0:T(128)} %stack.53.place_ref, ...), custom_call_target="tpu_custom_call" | custom-call | flops 22548578304 | bytes 25165824 | tf_op jit(solution)/shard_map/dense_chain/pallas_call | solution.py:495
  191.7 8.6 %dense_weights.3 = bf16[2,768,1856]{2,1,0:T(8,128)(2,1)} custom-call(s32[5]{0:T(128)} %stack.53.place_ref, bf16[512,768]{1,0:T(8,128)(2,1)} %get-tuple-element.85.first_ref, bf16[512,768]{1,0:T(8,128)(2,1)} %get-tuple-element.86.branch_grad_ref, bf16[512,768]{1,0:T(8,128)(2,1)} %get-tuple-element.87.attn_grad_ref, ...), custom_call_target="tpu_custom_call" | custom-call | flops 2919235584 | bytes 10485760 | tf_op jit(solution)/shard_map/dense_weights/pallas_call | solution.py:597
  200.4 3.5 all-to-all-start.1
  204.8 8.8 %dense_weights.2 = (bf16[8,96,1856]{2,1,0:T(8,128)(2,1)}, bf16[8,96,1856]{2,1,0:T(8,128)(2,1)}) custom-call(s32[5]{0:T(128)} %stack.53.place_ref, bf16[512,768]{1,0:T(8,128)(2,1)} %get-tuple-element.85.first_ref, bf16[512,768]{1,0:T(8,128)(2,1)} %get-tuple-element.86.branch_grad_ref, bf16[512,768]{1,0:T(8,128)(2,1)} %get-tuple-element.87.attn_grad_ref, ...), custom_call_target="tpu_custom_call" | custom-call | flops 2919235584 | bytes 10485760 | tf_op jit(solution)/shard_map/dense_weights/pallas_call | solution.py:597
  213.7 10.0 %all-to-all-done.1 = bf16[4,2,384,128]{3,2,1,0:T(8,128)(2,1)S(1)} async-done(((bf16[4,2,384,128]{3,2,1,0:T(8,128)(2,1)}), bf16[4,2,384,128]{3,2,1,0:T(8,128)(2,1)S(1)}, u32[]{:S(2)}, u32[]{:S(2)}) %all-to-all-start.1) | async-done | bytes 786464 | tf_op jit(solution)/shard_map/all_to_all | solution.py:783
  224.6 46.6 %attend_backward.1 = (bf16[1,2048,768]{2,1,0:T(8,128)(2,1)}, f32[1,768]{1,0:T(1,128)}) custom-call(s32[1]{0:T(128)} %bitcast.lane_ref, s32[8]{0:T(128)} %get-tuple-element.78.low_ref, s32[8]{0:T(128)} %get-tuple-element.79.count_ref, bf16[2048,768]{1,0:T(8,128)(2,1)} %add_convert_fusion.refs_0_, s32[2048,1]{1,0:T(8,128)} %copy.93.refs_1_, ...), custom_call_target="tpu_custom_call" | custom-call | flops 51539607552 | bytes 10485760 | tf_op jit(solution)/shard_map/attend_backward/pallas_call | solution.py:334
  271.3 6.2 %convolution_convert_fusion = bf16[2048,768]{1,0:T(8,128)(2,1)} fusion(bf16[768,768]{0,1:T(8,128)(2,1)S(1)} %copy-done.4, bf16[1,2048,768]{2,1,0:T(8,128)(2,1)} %get-tuple-element.97), kind=kOutput, calls=%fused_computation.1 | convolution fusion | flops 2417491968 | bytes 7471104 | tf_op jit(solution)/shard_map/dot_general | solution.py:30
  277.8 1.5 copy-done.1
  279.5 2.6 fusion
  283.0 7.0 %fusion.20 = f32[768,768]{1,0:T(8,128)} fusion(bf16[2048,768]{1,0:T(8,128)(2,1)} %bitcast.114, bf16[2048,768]{1,0:T(8,128)(2,1)} %bitcast.119), kind=kOutput, calls=%fused_computation.92 | convolution fusion | flops 2415919104 | bytes 8650752 | tf_op jit(solution)/shard_map/dot_general | solution.py:30
  290.0 25.7 %collective-permute-done.9 = bf16[2,2,96,1856]{3,2,1,0:T(8,128)(2,1)} collective-permute-done((bf16[2,2,96,1856]{3,2,1,0:T(8,128)(2,1)S(1)}, bf16[2,2,96,1856]{3,2,1,0:T(8,128)(2,1)}, u32[]{:S(2)}, u32[]{:S(2)}) %collective-permute-start.9) | collective-permute-done | bytes 1425440 | tf_op jit(solution)/shard_map/ppermute | solution.py:678
  315.7 1.7 add_convert_fusion.3
  317.4 1.9 collective-permute-start.10
  319.5 3.8 collective-permute-done.11
  323.4 4.7 %collective-permute-done.12 = f32[2,384]{1,0:T(2,128)S(1)} collective-permute-done((f32[2,384]{1,0:T(2,128)S(1)}, f32[2,384]{1,0:T(2,128)S(1)}, u32[]{:S(2)}, u32[]{:S(2)}) %collective-permute-start.12) | collective-permute-done | bytes 3104 | tf_op jit(solution)/shard_map/ppermute | solution.py:678
  329.4 4.8 %collective-permute-done.10 = bf16[1,2,96,1856]{3,2,1,0:T(8,128)(2,1)S(1)} collective-permute-done((bf16[1,2,96,1856]{3,2,1,0:T(8,128)(2,1)S(1)}, bf16[1,2,96,1856]{3,2,1,0:T(8,128)(2,1)S(1)}, u32[]{:S(2)}, u32[]{:S(2)}) %collective-permute-start.10) | collective-permute-done | bytes 712736 | tf_op jit(solution)/shard_map/ppermute | solution.py:678
  334.4 1.7 fusion.6
  336.1 1.5 pad_maximum_fusion
  338.4 1.2 add_convert_fusion.1
  339.7 2.0 collective-permute-done.13
  344.8 6.2 %collective-permute-done.14 = bf16[2,96,768]{2,1,0:T(8,128)(2,1)S(1)} collective-permute-done((bf16[2,96,768]{2,1,0:T(8,128)(2,1)S(1)}, bf16[2,96,768]{2,1,0:T(8,128)(2,1)S(1)}, u32[]{:S(2)}, u32[]{:S(2)}) %collective-permute-start.14) | collective-permute-done | bytes 294944 | tf_op jit(solution)/shard_map/ppermute | solution.py:678
  353.4 2.9 collective-permute-done.15
  357.0 1.7 finish_heads.1
  360.8 2.4 add_bitcast_fusion
  363.2 14.0 %reduce-scatter.6.cloned.1.call-done = bf16[1,96,1856]{2,1,0:T(8,128)(2,1)} async-done(((bf16[4,96,1856]{2,1,0:T(8,128)(2,1)}), bf16[1,96,1856]{2,1,0:T(8,128)(2,1)}) %reduce-scatter.6.cloned.1.call-update) | async-done | bytes 356368 | tf_op jit(solution)/shard_map/reduce_scatter | solution.py:870
  377.3 1.9 finish_dense.1
  379.1 1.3 slice_bitcast_fusion
  380.4 2.0 slice_bitcast_fusion.1
  (150 shorter events, 27.3 us)
Async XLA Ops:
  7.2 4.3 %copy-start.13 = (s32[1,512]{1,0:T(1,128)S(1)}, s32[1,512]{1,0:T(1,128)}, u32[]{:S(2)}) copy-start(s32[1,512]{1,0:T(1,128)} %param.22) | copy-start | bytes 6148
  7.2 9.2 %copy-start.9 = (bf16[192,96]{1,0:T(8,128)(2,1)S(1)}, bf16[192,96]{1,0:T(8,128)(2,1)}, u32[]{:S(2)}) copy-start(bf16[192,96]{1,0:T(8,128)(2,1)} %param.28) | copy-start | bytes 110596
  7.2 9.3 %copy-start.8 = (bf16[768,96]{0,1:T(8,128)(2,1)S(1)}, bf16[768,96]{0,1:T(8,128)(2,1)}, u32[]{:S(2)}) copy-start(bf16[768,96]{0,1:T(8,128)(2,1)} %param.30) | copy-start | bytes 442372
  7.2 9.3 %copy-start.7 = (bf16[96,768]{1,0:T(8,128)(2,1)S(1)}, bf16[96,768]{1,0:T(8,128)(2,1)}, u32[]{:S(2)}) copy-start(bf16[96,768]{1,0:T(8,128)(2,1)} %param.29) | copy-start | bytes 442372
  7.2 76.9 %all-gather.5.cloned.1.call-start = ((), (), s32[]{:S(2)}) async-start(), calls=%async_computation.8 | async-start | bytes 3932160 | tf_op jit(solution)/shard_map/all_gather | solution.py:741
  8.0 154.4 %all-gather.7.cloned.1.call-start = ((), (), s32[]{:S(2)}) async-start(), calls=%async_computation.9 | async-start | bytes 6193152 | tf_op jit(solution)/shard_map/all_gather | solution.py:789
  11.0 2.4 collective-permute-start.2
  13.8 12.3 %collective-permute-start.3 = (bf16[192,768]{0,1:T(8,128)(2,1)S(1)}, bf16[192,768]{0,1:T(8,128)(2,1)S(1)}, u32[]{:S(2)}, u32[]{:S(2)}) collective-permute-start(bf16[192,768]{0,1:T(8,128)(2,1)S(1)} %maximum_select_fusion.2), channel_id=1, source_target_pairs={{0,8},{4,12},{8,0},{12,4},{16,24},{20,28},{24,16},{28,20},{1,9},{5... | collective-permute-start | bytes 884744 | tf_op jit(solution)/shard_map/ppermute | solution.py:678
  16.7 25.5 %collective-permute-start = (bf16[1,96,1792]{2,1,0:T(8,128)(2,1)S(1)}, bf16[1,96,1792]{2,1,0:T(8,128)(2,1)S(1)}, u32[]{:S(2)}, u32[]{:S(2)}) collective-permute-start(bf16[1,96,1792]{2,1,0:T(8,128)(2,1)S(1)} %bitcast.86), channel_id=1, source_target_pairs={{0,1},{1,0},{2,3},{3,2},{4,5},{5,4},{6,7},{7,6},{8,9},{9,8},{10,11... | collective-permute-start | bytes 1032200 | tf_op jit(solution)/shard_map/ppermute | solution.py:678
  26.6 15.8 %collective-permute-start.4 = (bf16[384,768]{0,1:T(8,128)(2,1)S(1)}, bf16[384,768]{0,1:T(8,128)(2,1)S(1)}, u32[]{:S(2)}, u32[]{:S(2)}) collective-permute-start(bf16[384,768]{0,1:T(8,128)(2,1)S(1)} %maximum_select_fusion.1), channel_id=1, source_target_pairs={{0,16},{4,20},{8,24},{12,28},{16,0},{20,4},{24,8},{28,12},{1,17},{... | collective-permute-start | bytes 1769480 | tf_op jit(solution)/shard_map/ppermute | solution.py:678
  42.3 13.5 %collective-permute-start.1 = (bf16[2,96,1792]{2,1,0:T(8,128)(2,1)S(1)}, bf16[2,96,1792]{2,1,0:T(8,128)(2,1)}, u32[]{:S(2)}, u32[]{:S(2)}) collective-permute-start(bf16[2,96,1792]{2,1,0:T(8,128)(2,1)S(1)} %pad_maximum_fusion.3), channel_id=1, source_target_pairs={{0,8},{4,12},{8,0},{12,4},{16,24},{20,28},{24,16},{28,20},{1,9},{5... | collective-permute-start | bytes 2064392 | tf_op jit(solution)/shard_map/ppermute | solution.py:678
  43.7 15.0 %copy-start.10 = (s32[1,2048]{1,0:T(1,128)S(1)}, s32[1,2048]{1,0:T(1,128)}, u32[]{:S(2)}) copy-start(s32[1,2048]{1,0:T(1,128)} %refs_2_.5) | copy-start | bytes 24580
  57.0 27.2 %collective-permute-start.5 = (bf16[4,96,1792]{2,1,0:T(8,128)(2,1)S(1)}, bf16[4,96,1792]{2,1,0:T(8,128)(2,1)S(1)}, u32[]{:S(2)}, u32[]{:S(2)}) collective-permute-start(bf16[4,96,1792]{2,1,0:T(8,128)(2,1)S(1)} %pad_maximum_fusion.1), channel_id=1, source_target_pairs={{0,16},{4,20},{8,24},{12,28},{16,0},{20,4},{24,8},{28,12},{1,17},{... | collective-permute-start | bytes 4128776 | tf_op jit(solution)/shard_map/ppermute | solution.py:678
  84.2 29.5 %collective-permute-start.6 = (bf16[2,96,1792]{2,1,0:T(8,128)(2,1)S(1)}, bf16[2,96,1792]{2,1,0:T(8,128)(2,1)}, u32[]{:S(2)}, u32[]{:S(2)}) collective-permute-start(bf16[2,96,1792]{2,1,0:T(8,128)(2,1)S(1)} %pad_maximum_fusion.3), channel_id=1, source_target_pairs={{0,2},{1,3},{2,0},{3,1},{4,6},{5,7},{6,4},{7,5},{8,10},{9,11},{10,... | collective-permute-start | bytes 2064392 | tf_op jit(solution)/shard_map/ppermute | solution.py:678
  114.8 18.7 %copy-start.6 = (bf16[4,384,128]{2,1,0:T(8,128)(2,1)S(1)}, bf16[4,384,128]{2,1,0:T(8,128)(2,1)}, u32[]{:S(2)}) copy-start(bf16[4,384,128]{2,1,0:T(8,128)(2,1)} %get-tuple-element.77) | copy-start | bytes 1179652
  136.6 5.0 %copy-start.16 = (bf16[768]{0:T(1024)(128)(2,1)S(1)}, bf16[768]{0:T(1024)(128)(2,1)}, u32[]{:S(2)}) copy-start(bf16[768]{0:T(1024)(128)(2,1)} %param.33) | copy-start | bytes 4612
  136.7 5.0 %copy-start.17 = (bf16[768]{0:T(1024)(128)(2,1)S(1)}, bf16[768]{0:T(1024)(128)(2,1)}, u32[]{:S(2)}) copy-start(bf16[768]{0:T(1024)(128)(2,1)} %param.35) | copy-start | bytes 4612
  136.7 5.0 %copy-start.18 = (bf16[768]{0:T(1024)(128)(2,1)S(1)}, bf16[768]{0:T(1024)(128)(2,1)}, u32[]{:S(2)}) copy-start(bf16[768]{0:T(1024)(128)(2,1)} %param.36) | copy-start | bytes 4612
  136.7 5.0 %copy-start.19 = (bf16[768]{0:T(1024)(128)(2,1)S(1)}, bf16[768]{0:T(1024)(128)(2,1)}, u32[]{:S(2)}) copy-start(bf16[768]{0:T(1024)(128)(2,1)} %param.37) | copy-start | bytes 4612
  136.7 5.0 %copy-start.20 = (bf16[768]{0:T(1024)(128)(2,1)S(1)}, bf16[768]{0:T(1024)(128)(2,1)}, u32[]{:S(2)}) copy-start(bf16[768]{0:T(1024)(128)(2,1)} %param.38) | copy-start | bytes 4612
  136.7 5.1 %copy-start.21 = (bf16[768]{0:T(1024)(128)(2,1)S(1)}, bf16[768]{0:T(1024)(128)(2,1)}, u32[]{:S(2)}) copy-start(bf16[768]{0:T(1024)(128)(2,1)} %param.39) | copy-start | bytes 4612
  136.7 5.7 %copy-start.14 = (bf16[3072]{0:T(1024)(128)(2,1)S(1)}, bf16[3072]{0:T(1024)(128)(2,1)}, u32[]{:S(2)}) copy-start(bf16[3072]{0:T(1024)(128)(2,1)} %param.34) | copy-start | bytes 18436
  136.7 25.6 %collective-permute-start.7 = (bf16[8,96,1792]{2,1,0:T(8,128)(2,1)}, bf16[8,96,1792]{2,1,0:T(8,128)(2,1)}, u32[]{:S(2)}, u32[]{:S(2)}) collective-permute-start(bf16[8,96,1792]{2,1,0:T(8,128)(2,1)} %constant_dynamic-update-slice_fusion.refs_0_), channel_id=1, source_target_pairs={{0,4},{4,0},{8,12},{12,8},{16,20},{20,16},{24,28},{28,24},{1,5},{5... | collective-permute-start | bytes 8257544 | tf_op jit(solution)/shard_map/ppermute | solution.py:678
  136.8 25.6 %all-to-all-start = ((bf16[4,2,384,128]{3,2,1,0:T(8,128)(2,1)}), bf16[4,2,384,128]{3,2,1,0:T(8,128)(2,1)S(1)}, u32[]{:S(2)}, u32[]{:S(2)}) async-start(bf16[4,2,384,128]{3,2,1,0:T(8,128)(2,1)} %bitcast.15), calls=%async_computation | async-start | bytes 1572864 | tf_op jit(solution)/shard_map/all_to_all | solution.py:783
  141.6 192.8 %reduce-scatter.4.cloned.1.call-start = ((), (), s32[]{:S(2)}) async-start(), calls=%async_computation.5 | async-start | bytes 6635520 | tf_op jit(solution)/shard_map/reduce_scatter | solution.py:835
  162.3 0.9 copy-start
  200.3 3.8 copy-start.11
  200.4 3.8 copy-start.12
  200.4 23.4 %all-to-all-start.1 = ((bf16[4,2,384,128]{3,2,1,0:T(8,128)(2,1)}), bf16[4,2,384,128]{3,2,1,0:T(8,128)(2,1)S(1)}, u32[]{:S(2)}, u32[]{:S(2)}) async-start(bf16[4,2,384,128]{3,2,1,0:T(8,128)(2,1)} %get-tuple-element.94), calls=%async_computation.1 | async-start | bytes 1572864 | tf_op jit(solution)/shard_map/all_to_all | solution.py:783
  203.9 156.9 %reduce-scatter.8.cloned.1.call-start = ((), (), s32[]{:S(2)}) async-start(), calls=%async_computation.7 | async-start | bytes 3932160 | tf_op jit(solution)/shard_map/reduce_scatter | solution.py:849
  213.7 65.8 %collective-permute-start.8 = (bf16[4,2,96,1856]{3,2,1,0:T(8,128)(2,1)}, bf16[4,2,96,1856]{3,2,1,0:T(8,128)(2,1)}, u32[]{:S(2)}, u32[]{:S(2)}) collective-permute-start(bf16[4,2,96,1856]{3,2,1,0:T(8,128)(2,1)} %bitcast.115), channel_id=1, source_target_pairs={{0,4},{4,0},{8,12},{12,8},{16,20},{20,16},{24,28},{28,24},{1,5},{5... | collective-permute-start | bytes 8552456 | tf_op jit(solution)/shard_map/ppermute | solution.py:678
  223.7 0.9 copy-start.5
  224.6 46.7 %copy-start.4 = (bf16[768,768]{0,1:T(8,128)(2,1)S(1)}, bf16[768,768]{0,1:T(8,128)(2,1)}, u32[]{:S(2)}) copy-start(bf16[768,768]{0,1:T(8,128)(2,1)} %maximum_select_fusion) | copy-start | bytes 3538948
  277.4 1.8 copy-start.1
  277.5 99.8 %reduce-scatter.6.cloned.1.call-start = ((), (), s32[]{:S(2)}) async-start(), calls=%async_computation.6 | async-start | bytes 1843200 | tf_op jit(solution)/shard_map/reduce_scatter | solution.py:870
  279.5 3.4 copy-start.15
  282.1 33.6 %collective-permute-start.9 = (bf16[2,2,96,1856]{3,2,1,0:T(8,128)(2,1)S(1)}, bf16[2,2,96,1856]{3,2,1,0:T(8,128)(2,1)}, u32[]{:S(2)}, u32[]{:S(2)}) collective-permute-start(bf16[2,2,96,1856]{3,2,1,0:T(8,128)(2,1)S(1)} %get-tuple-element.102), channel_id=1, source_target_pairs={{0,8},{4,12},{8,0},{12,4},{16,24},{20,28},{24,16},{28,20},{1,9},{5... | collective-permute-start | bytes 4276232 | tf_op jit(solution)/shard_map/ppermute | solution.py:678
  317.4 16.8 %collective-permute-start.10 = (bf16[1,2,96,1856]{3,2,1,0:T(8,128)(2,1)S(1)}, bf16[1,2,96,1856]{3,2,1,0:T(8,128)(2,1)S(1)}, u32[]{:S(2)}, u32[]{:S(2)}) collective-permute-start(bf16[1,2,96,1856]{3,2,1,0:T(8,128)(2,1)S(1)} %get-tuple-element.107), channel_id=1, source_target_pairs={{0,16},{4,20},{8,24},{12,28},{16,0},{20,4},{24,8},{28,12},{1,17},{... | collective-permute-start | bytes 2138120 | tf_op jit(solution)/shard_map/ppermute | solution.py:678
  319.5 3.8 collective-permute-start.11
  323.4 4.7 %collective-permute-start.12 = (f32[2,384]{1,0:T(2,128)S(1)}, f32[2,384]{1,0:T(2,128)S(1)}, u32[]{:S(2)}, u32[]{:S(2)}) collective-permute-start(f32[2,384]{1,0:T(2,128)S(1)} %maximum_select_fusion.4), channel_id=1, source_target_pairs={{0,2},{1,3},{2,0},{3,1},{4,6},{5,7},{6,4},{7,5},{8,10},{9,11},{10,... | collective-permute-start | bytes 9224 | tf_op jit(solution)/shard_map/ppermute | solution.py:678
  336.1 2.2 copy-start.2
  339.6 2.1 collective-permute-start.13
  341.8 19.0 %copy-start.3 = (f32[512,768]{1,0:T(8,128)S(1)}, f32[512,768]{1,0:T(8,128)}, u32[]{:S(2)}) copy-start(f32[512,768]{1,0:T(8,128)} %get-tuple-element.111) | copy-start | bytes 4718596
  341.8 9.1 %collective-permute-start.14 = (bf16[2,96,768]{2,1,0:T(8,128)(2,1)S(1)}, bf16[2,96,768]{2,1,0:T(8,128)(2,1)S(1)}, u32[]{:S(2)}, u32[]{:S(2)}) collective-permute-start(bf16[2,96,768]{2,1,0:T(8,128)(2,1)S(1)} %dynamic-slice_bitcast_fusion.1), channel_id=1, source_target_pairs={{0,8},{4,12},{8,0},{12,4},{16,24},{20,28},{24,16},{28,20},{1,9},{5... | collective-permute-start | bytes 884744 | tf_op jit(solution)/shard_map/ppermute | solution.py:678
  351.1 5.2 %collective-permute-start.15 = (bf16[1,96,768]{2,1,0:T(8,128)(2,1)S(1)}, bf16[1,96,768]{2,1,0:T(8,128)(2,1)S(1)}, u32[]{:S(2)}, u32[]{:S(2)}) collective-permute-start(bf16[1,96,768]{2,1,0:T(8,128)(2,1)S(1)} %constant_dynamic-slice_fusion), channel_id=1, source_target_pairs={{0,16},{4,20},{8,24},{12,28},{16,0},{20,4},{24,8},{28,12},{1,17},{... | collective-permute-start | bytes 442376 | tf_op jit(solution)/shard_map/ppermute | solution.py:678
Sparse Core Ops, SparseCore 0:
  9.6 68.1 all-gather.4
  113.8 44.1 all-gather.6
  200.5 63.4 reduce-scatter.3
  277.6 63.7 reduce-scatter.7
  343.5 33.7 reduce-scatter.5

commit v13 on v12

--- a/solution.py
+++ b/solution.py
@@ -195,15 +195,18 @@
     def step(kb, accs):
         keys = pl.ds(pl.multiple_of(low * STEP + kb * BLOCK, STEP), BLOCK)
         allowed = seg_col_ref[keys, :] == seg_q
+        keyed = [qkv_ref[keys, SLAB * h + 2 * DH : SLAB * (h + 1)] for h in range(heads)]
+        raw = [dot(keyed[h], queries[h], NT) for h in range(heads)]
+        probs_grads = [dot(keyed[h], grads[h], NT) for h in range(heads)]
+        both = []
+        for h in range(heads):
+            probs = jnp.exp2((jnp.where(allowed, raw[h], MASKED) - lses[h]) * LOG2E)
+            score_grad = (probs * (probs_grads[h] - deltas[h])).astype(BF16)
+            both.append((score_grad, probs.astype(BF16)))
         found = []
         for h in range(heads):
-            pair = qkv_ref[keys, SLAB * h + 2 * DH : SLAB * (h + 1)]
-            scores = jnp.where(allowed, dot(pair, queries[h], NT), MASKED)
-            probs = jnp.exp2((scores - lses[h]) * LOG2E)
-            score_grad = (probs * (dot(pair, grads[h], NT) - deltas[h])).astype(BF16)
-            both = jnp.concatenate([score_grad, probs.astype(BF16)], axis=1)
-            dkv[h, keys, :] += dot(both, pairs[h])
-            found.append(accs[h] + dot(score_grad, pair, TN))
+            dkv[h, keys, :] += dot(jnp.concatenate(both[h], axis=1), pairs[h])
+            found.append(accs[h] + dot(both[h][0], keyed[h], TN))
         return tuple(found)
 
     zero = jnp.zeros((BLOCK, 128), F32)
@@ -368,7 +371,8 @@
     pieces = refs[: len(marks)]
     (
         layer_ref, first_grad_ref, ctx_grad_ref, first_ref, branch_grad_ref, attn_grad_ref,
-        act_ref, hidden_grad_ref, sums_ref, inner_sums_ref, w_out, w_in, w_up, slope, sems,
+        act_ref, hidden_grad_ref, notes_ref, w_out, w_in, w_up, slope, sums_ref, inner_sums_ref,
+        gathered, sems,
     ) = refs[len(marks) :]
     parts, _, head_cols = w_out.shape
     hidden_cols = w_in.shape[2]
@@ -473,11 +477,38 @@
         )
 
 
-def run_dense(marks, total_tokens, place, ctx, rows_in, teacher, cotangent, valid, vecs, inner_bias, pieces):
+    @pl.when(step == pl.num_programs(0) - 1)
+    def _():
+        lanes = 2 * DH
+        gathered[...] = jnp.zeros_like(gathered)
+        rows_each, inner_rows = width_of(sums_ref) // lanes, width_of(inner_sums_ref) // lanes
+        per_note = gathered.shape[1] // lanes
+
+        def put(at, value):
+            gathered[at // per_note : at // per_note + 1, pl.ds(at % per_note * lanes, lanes)] = value
+
+        for row in range(sums_ref.shape[0]):
+            for k in range(rows_each):
+                put(row * rows_each + k, sums_ref[row : row + 1, k * lanes : (k + 1) * lanes])
+        for t in range(parts):
+            for k in range(inner_rows):
+                put(
+                    sums_ref.shape[0] * rows_each + t * inner_rows + k,
+                    inner_sums_ref[t, :, k * lanes : (k + 1) * lanes],
+                )
+        notes_ref[...] = gathered[...].astype(BF16)
+
+
+def width_of(ref):
+    return ref.shape[-1]
+
+
+def run_dense(note_rows, marks, total_tokens, place, ctx, rows_in, teacher, cotangent, valid, vecs, inner_bias, pieces):
     parts, halves = ctx.shape[:2]
     part_len, width = rows_in.shape
     hidden_cols = inner_bias.shape[2]
     out_cols = pieces[0].shape[2] - 2 * hidden_cols
+    room = -(-(8 * width + parts * hidden_cols) // (note_rows * 2 * DH)) * 2 * DH
 
     def by_rows(columns):
         return pl.BlockSpec((BLOCK, columns), lambda i: (i, 0))
@@ -503,8 +534,7 @@
             low,
             wide,
             wide,
-            jax.ShapeDtypeStruct((8, width), F32),
-            jax.ShapeDtypeStruct((parts, 1, hidden_cols), F32),
+            jax.ShapeDtypeStruct((note_rows, room), BF16),
         ),
         grid=(halves,),
         in_specs=[
@@ -527,14 +557,16 @@
             by_rows(width),
             by_part(hidden_cols),
             by_part(hidden_cols),
-            fixed((8, width)),
-            fixed((parts, 1, hidden_cols)),
+            fixed((note_rows, room)),
         ),
         scratch_shapes=[
             pltpu.VMEM((parts, width, out_cols), BF16),
             pltpu.VMEM((parts, width, hidden_cols), BF16),
             pltpu.VMEM((parts, width, hidden_cols), BF16),
             pltpu.VMEM((parts, BLOCK, hidden_cols), F32),
+            pltpu.VMEM((8, width), F32),
+            pltpu.VMEM((parts, 1, hidden_cols), F32),
+            pltpu.VMEM((note_rows, room), F32),
             pltpu.SemaphoreType.DMA((3, parts)),
         ],
         compiler_params=pltpu.CompilerParams(
@@ -553,21 +585,16 @@
     plans, place_ref, first_ref, branch_grad_ref, attn_grad_ref, act_ref, hidden_grad_ref, ctx_ref,
     notes_ref, *refs
 ):
-    outs, (turned, whole, sems) = refs[:-3], refs[-3:]
+    outs, (whole, sems) = refs[:-2], refs[-2:]
     step = pl.program_id(0)
     slots = whole.shape[0]
 
-    @pl.when(step == 0)
-    def _():
-        for which, source in enumerate((first_ref, branch_grad_ref, attn_grad_ref)):
-            turned[which] = jnp.transpose(source[...])
-
     hidden_cols = act_ref.shape[2]
-    whole[step, :, :hidden_cols] = dot(turned[0], hidden_grad_ref[0]).astype(BF16)
-    whole[step, :, hidden_cols : 2 * hidden_cols] = dot(turned[1], act_ref[0]).astype(BF16)
+    whole[step, :, :hidden_cols] = dot(first_ref[...], hidden_grad_ref[0], TN).astype(BF16)
+    whole[step, :, hidden_cols : 2 * hidden_cols] = dot(branch_grad_ref[...], act_ref[0], TN).astype(BF16)
     ctx = jnp.concatenate([unpack(ctx_ref[0, half]) for half in range(ctx_ref.shape[1])], axis=0)
     plain = 2 * hidden_cols + ctx.shape[1]
-    whole[step, :, 2 * hidden_cols : plain] = dot(turned[2], ctx).astype(BF16)
+    whole[step, :, 2 * hidden_cols : plain] = dot(attn_grad_ref[...], ctx, TN).astype(BF16)
     whole[step, :, plain : plain + notes_ref.shape[1]] = notes_ref[...]
     for out, turns in zip(outs, plans):
         block = out.shape[1]
@@ -611,7 +638,6 @@
             ],
             out_specs=tuple(pl.BlockSpec(memory_space=pl.ANY) for _ in outs),
             scratch_shapes=[
-                pltpu.VMEM((3, width, part_len), BF16),
                 pltpu.VMEM((slots, width, columns), BF16),
                 pltpu.SemaphoreType.DMA((slots,)),
             ],
@@ -814,17 +840,13 @@
     teacher_rows = teacher.reshape(part_len, width)
     cotangent_rows = cotangent.reshape(part_len, width)
     (
-        layer_out, first_grad, context_grad, first, branch_grad, attn_grad, activated, hidden_grad,
-        dense_sums, inner_sums,
+        layer_out, first_grad, context_grad, first, branch_grad, attn_grad, activated, hidden_grad, notes,
     ) = run_dense(
-        marks, float(total_tokens), place, arrived, rows_in, teacher_rows, cotangent_rows, valid_rows, vecs,
+        shard_rows, marks, float(total_tokens), place, arrived, rows_in, teacher_rows, cotangent_rows, valid_rows, vecs,
         inner_rows, pieces,
     )
     head_grad = exchange(context_grad).reshape(context.shape)
     sources = (first, branch_grad, attn_grad, activated, hidden_grad, arrived)
-    notes = jnp.concatenate((dense_sums.reshape(-1), inner_sums.reshape(-1))).astype(BF16)
-    room = -(-notes.shape[0] // (shard_rows * 128)) * 128
-    notes = jnp.pad(notes, (0, shard_rows * room - notes.shape[0])).reshape(shard_rows, room)
     notes = jnp.tile(notes, (copies, 1))
     if paired:
         keep_turns = (0, 4, 2, 6)

time: 390 us -> 377 us (0.967)
  Pallas kernels: 130 us -> 108 us
  starting transfers between devices: 25.6 us -> 33.7 us
    pallas_call x1, Pallas kernels: 46.6 us -> 30.3 us  [run_backward(): pl.pallas_call(functools.partial(attend_backward, which, len(qkv)), out_s...]
    ppermute x16, starting transfers between devices: 16.7 us -> 24.7 us  [swap(): return lax.ppermute(value, axis, [(i, i ^ bit) for i in range(size)])]
    reduce_scatter x1, waiting for transfers between devices: 14 us -> 8.77 us  [local(): lax.psum_scatter(packed, 'tensor', scatter_dimension=0, tiled=True)[0]]
    pallas_call x2, Pallas kernels: 36.6 us -> 31.4 us  [run_forward(): pl.pallas_call(functools.partial(attend_forward, first_block), out_shape=...]
    ppermute x16, waiting for transfers between devices: 106 us -> 110 us  [swap(): return lax.ppermute(value, axis, [(i, i ^ bit) for i in range(size)])]
  transfers between devices with their start and end apart: 23 -> 23, of which waited for: 14 -> 15; matrix products, arithmetic and copies ran while one was open for 15% -> 15% of each run, Pallas kernels for 24% -> 19%
where the time goes in v13:
time: 377 us; the launch traced here: 375 us
  waiting for transfers between devices  148 us (39%)
  Pallas kernels  108 us (29%)
  starting transfers between devices  33.7 us (9%)
  other arithmetic  24.7 us (7%)
  local copies, waits for them, and re-layouts  22.3 us (6%)
  matrix products  19.6 us (5%)
  between operations  18.8 us (5%)
    ppermute x16, waiting for transfers between devices, swap(): return lax.ppermute(value, axis, [(i, i ^ bit) for i in range(size)])  110 us
    pallas_call x2, Pallas kernels, run_forward(): pl.pallas_call(functools.partial(attend_forward, first_block), out_shape=...  31.4 us
    pallas_call x1, Pallas kernels, run_backward(): pl.pallas_call(functools.partial(attend_backward, which, len(qkv)), out_s...  30.3 us
    all_to_all x2, waiting for transfers between devices, exchange(): lax.all_to_all(packed_blocks.reshape(parts, halves, PACKED, 2 * DH), 'ten...  28.8 us
    pallas_call x1, Pallas kernels, run_dense(): pl.pallas_call(functools.partial(dense_chain, marks, total_tokens), out_s...  26.6 us
    ppermute x16, starting transfers between devices, swap(): return lax.ppermute(value, axis, [(i, i ^ bit) for i in range(size)])  24.7 us
    dot_general x3, matrix products, dot(): lax.dot_general(left_side, right_side, dims, preferred_element_type=F32)  19.6 us
    pallas_call x2, Pallas kernels, run_weights(): pl.pallas_call(functools.partial(dense_weights, tuple((turns for _, turns...  16 us
  transfers between devices with their start and end apart: 23, of which 15 were waited for; matrix products, arithmetic and copies ran while one was open for 15% of the time, Pallas kernels for 19%

profile of v13, /device:TPU:0, one launch (start us, length us, event | category | flops | bytes accessed | tf_op | source)
XLA Modules:
  0.0 375.4 jit_solution(6395475726715567486)
XLA Ops:
  13.8 2.6 collective-permute-start.3
  16.7 1.6 collective-permute-start
  18.3 7.8 %collective-permute-done.3 = bf16[192,768]{0,1:T(8,128)(2,1)S(1)} collective-permute-done((bf16[192,768]{0,1:T(8,128)(2,1)S(1)}, bf16[192,768]{0,1:T(8,128)(2,1)S(1)}, u32[]{:S(2)}, u32[]{:S(2)}) %collective-permute-start.3) | collective-permute-done | bytes 294944 | tf_op jit(solution)/shard_map/ppermute | solution.py:704
  26.6 1.8 collective-permute-start.4
  28.5 13.8 %collective-permute-done = bf16[1,96,1792]{2,1,0:T(8,128)(2,1)S(1)} collective-permute-done((bf16[1,96,1792]{2,1,0:T(8,128)(2,1)S(1)}, bf16[1,96,1792]{2,1,0:T(8,128)(2,1)S(1)}, u32[]{:S(2)}, u32[]{:S(2)}) %collective-permute-start) | collective-permute-done | bytes 344096 | tf_op jit(solution)/shard_map/ppermute | solution.py:704
  42.4 1.3 maximum_select_fusion
  43.7 12.1 %collective-permute-done.1 = bf16[2,96,1792]{2,1,0:T(8,128)(2,1)} collective-permute-done((bf16[2,96,1792]{2,1,0:T(8,128)(2,1)S(1)}, bf16[2,96,1792]{2,1,0:T(8,128)(2,1)}, u32[]{:S(2)}, u32[]{:S(2)}) %collective-permute-start.1) | collective-permute-done | bytes 688160 | tf_op jit(solution)/shard_map/ppermute | solution.py:704
  55.7 1.2 pad_maximum_fusion.1
  57.0 1.7 collective-permute-start.5
  60.0 1.4 copy.93.refs_1_
  62.2 22.0 %collective-permute-done.5 = bf16[4,96,1792]{2,1,0:T(8,128)(2,1)S(1)} collective-permute-done((bf16[4,96,1792]{2,1,0:T(8,128)(2,1)S(1)}, bf16[4,96,1792]{2,1,0:T(8,128)(2,1)S(1)}, u32[]{:S(2)}, u32[]{:S(2)}) %collective-permute-start.5) | collective-permute-done | bytes 1376288 | tf_op jit(solution)/shard_map/ppermute | solution.py:704
  84.2 5.0 %collective-permute-start.6 = (bf16[2,96,1792]{2,1,0:T(8,128)(2,1)S(1)}, bf16[2,96,1792]{2,1,0:T(8,128)(2,1)}, u32[]{:S(2)}, u32[]{:S(2)}) collective-permute-start(bf16[2,96,1792]{2,1,0:T(8,128)(2,1)S(1)} %pad_maximum_fusion.3), channel_id=1, source_target_pairs={{0,2},{1,3},{2,0},{3,1},{4,6},{5,7},{6,4},{7,5},{8,10},{9,11},{10,... | collective-permute-start | bytes 2064392 | tf_op jit(solution)/shard_map/ppermute | solution.py:704
  89.2 6.5 %add_convert_fusion.refs_0_ = bf16[2048,768]{1,0:T(8,128)(2,1)} fusion(bf16[2048,768]{1,0:T(8,128)(2,1)} %bitcast.111, bf16[768,768]{0,1:T(8,128)(2,1)} %maximum_select_fusion, f32[768]{0:T(1024)S(1)} %add.115), kind=kOutput, calls=%fused_computation | convolution fusion | flops 2419064832 | bytes 7474176 | tf_op jit(solution)/shard_map/dot_general | solution.py:30
  95.7 13.4 %attend_forward.2 = (bf16[4,384,128]{2,1,0:T(8,128)(2,1)}, f32[3,1,1024]{2,1,0:T(1,128)}) custom-call(s32[1]{0:T(128)} %bitcast.lane_ref, s32[8]{0:T(128)} %get-tuple-element.77.low_ref, s32[8]{0:T(128)} %get-tuple-element.78.count_ref, bf16[2048,768]{1,0:T(8,128)(2,1)} %add_convert_fusion.refs_0_, s32[2048,1]{1,0:T(8,128)} %copy.93.refs_1_, s32[1,2048]{1,0:T(1,128)} %refs_2_.5), custom_call_target="tpu_custom_call" | custom-call | flops 12884901888 | bytes 5242880 | tf_op jit(solution)/shard_map/attend_forward/pallas_call | solution.py:270
  109.1 4.5 %collective-permute-done.6 = bf16[2,96,1792]{2,1,0:T(8,128)(2,1)} collective-permute-done((bf16[2,96,1792]{2,1,0:T(8,128)(2,1)S(1)}, bf16[2,96,1792]{2,1,0:T(8,128)(2,1)}, u32[]{:S(2)}, u32[]{:S(2)}) %collective-permute-start.6) | collective-permute-done | bytes 688160 | tf_op jit(solution)/shard_map/ppermute | solution.py:704
  114.8 18.0 %attend_forward.3 = (bf16[4,384,128]{2,1,0:T(8,128)(2,1)}, f32[3,1,1024]{2,1,0:T(1,128)}) custom-call(s32[1]{0:T(128)} %bitcast.lane_ref, s32[8]{0:T(128)} %get-tuple-element.77.low_ref, s32[8]{0:T(128)} %get-tuple-element.78.count_ref, bf16[2048,768]{1,0:T(8,128)(2,1)} %add_convert_fusion.refs_0_, s32[2048,1]{1,0:T(8,128)} %copy.93.refs_1_, s32[1,2048]{1,0:T(1,128)} %refs_2_.5), custom_call_target="tpu_custom_call" | custom-call | flops 12884901888 | bytes 5242880 | tf_op jit(solution)/shard_map/attend_forward/pallas_call | solution.py:270
  132.9 2.0 pad_maximum_fusion.2.refs_3_
  136.2 4.8 %all-to-all-start = ((bf16[4,2,384,128]{3,2,1,0:T(8,128)(2,1)}), bf16[4,2,384,128]{3,2,1,0:T(8,128)(2,1)S(1)}, u32[]{:S(2)}, u32[]{:S(2)}) async-start(bf16[4,2,384,128]{3,2,1,0:T(8,128)(2,1)} %bitcast.15), calls=%async_computation | async-start | bytes 1572864 | tf_op jit(solution)/shard_map/all_to_all | solution.py:809
  143.8 17.9 %all-to-all-done.ctx_ref = bf16[4,2,384,128]{3,2,1,0:T(8,128)(2,1)S(1)} async-done(((bf16[4,2,384,128]{3,2,1,0:T(8,128)(2,1)}), bf16[4,2,384,128]{3,2,1,0:T(8,128)(2,1)S(1)}, u32[]{:S(2)}, u32[]{:S(2)}) %all-to-all-start) | async-done | bytes 786464 | tf_op jit(solution)/shard_map/all_to_all | solution.py:809
  162.6 26.6 %dense_chain.1 = (bf16[512,768]{1,0:T(8,128)(2,1)}, f32[512,768]{1,0:T(8,128)}, bf16[4,2,384,128]{3,2,1,0:T(8,128)(2,1)}, bf16[512,768]{1,0:T(8,128)(2,1)}, bf16...) custom-call(s32[5]{0:T(128)} %stack.53.place_ref, ...), custom_call_target="tpu_custom_call" | custom-call | flops 22548578304 | bytes 25165824 | tf_op jit(solution)/shard_map/dense_chain/pallas_call | solution.py:526
  189.2 1.4 tile.4
  190.6 8.1 %dense_weights.3 = bf16[2,768,1856]{2,1,0:T(8,128)(2,1)} custom-call(s32[5]{0:T(128)} %stack.53.place_ref, bf16[512,768]{1,0:T(8,128)(2,1)} %get-tuple-element.84.first_ref, bf16[512,768]{1,0:T(8,128)(2,1)} %get-tuple-element.85.branch_grad_ref, bf16[512,768]{1,0:T(8,128)(2,1)} %get-tuple-element.86.attn_grad_ref, ...), custom_call_target="tpu_custom_call" | custom-call | flops 2919235584 | bytes 10485760 | tf_op jit(solution)/shard_map/dense_weights/pallas_call | solution.py:624
  198.7 3.5 all-to-all-start.1
  203.1 7.9 %dense_weights.2 = (bf16[8,96,1856]{2,1,0:T(8,128)(2,1)}, bf16[8,96,1856]{2,1,0:T(8,128)(2,1)}) custom-call(s32[5]{0:T(128)} %stack.53.place_ref, bf16[512,768]{1,0:T(8,128)(2,1)} %get-tuple-element.84.first_ref, bf16[512,768]{1,0:T(8,128)(2,1)} %get-tuple-element.85.branch_grad_ref, bf16[512,768]{1,0:T(8,128)(2,1)} %get-tuple-element.86.attn_grad_ref, ...), custom_call_target="tpu_custom_call" | custom-call | flops 2919235584 | bytes 10485760 | tf_op jit(solution)/shard_map/dense_weights/pallas_call | solution.py:624
  211.2 10.9 %all-to-all-done.1 = bf16[4,2,384,128]{3,2,1,0:T(8,128)(2,1)S(1)} async-done(((bf16[4,2,384,128]{3,2,1,0:T(8,128)(2,1)}), bf16[4,2,384,128]{3,2,1,0:T(8,128)(2,1)S(1)}, u32[]{:S(2)}, u32[]{:S(2)}) %all-to-all-start.1) | async-done | bytes 786464 | tf_op jit(solution)/shard_map/all_to_all | solution.py:809
  223.0 30.3 %attend_backward.1 = (bf16[1,2048,768]{2,1,0:T(8,128)(2,1)}, f32[1,768]{1,0:T(1,128)}) custom-call(s32[1]{0:T(128)} %bitcast.lane_ref, s32[8]{0:T(128)} %get-tuple-element.77.low_ref, s32[8]{0:T(128)} %get-tuple-element.78.count_ref, bf16[2048,768]{1,0:T(8,128)(2,1)} %add_convert_fusion.refs_0_, s32[2048,1]{1,0:T(8,128)} %copy.93.refs_1_, ...), custom_call_target="tpu_custom_call" | custom-call | flops 51539607552 | bytes 10485760 | tf_op jit(solution)/shard_map/attend_backward/pallas_call | solution.py:337
  253.3 6.2 %convolution_convert_fusion = bf16[2048,768]{1,0:T(8,128)(2,1)} fusion(bf16[768,768]{0,1:T(8,128)(2,1)S(1)} %copy-done.4, bf16[1,2048,768]{2,1,0:T(8,128)(2,1)} %get-tuple-element.95), kind=kOutput, calls=%fused_computation.1 | convolution fusion | flops 2417491968 | bytes 7471104 | tf_op jit(solution)/shard_map/dot_general | solution.py:30
  259.8 1.5 copy-done.1
  261.6 2.6 fusion
  264.2 9.2 %collective-permute-start.9 = (bf16[2,2,96,1856]{3,2,1,0:T(8,128)(2,1)S(1)}, bf16[2,2,96,1856]{3,2,1,0:T(8,128)(2,1)}, u32[]{:S(2)}, u32[]{:S(2)}) collective-permute-start(bf16[2,2,96,1856]{3,2,1,0:T(8,128)(2,1)S(1)} %get-tuple-element.100), channel_id=1, source_target_pairs={{0,8},{4,12},{8,0},{12,4},{16,24},{20,28},{24,16},{28,20},{1,9},{5... | collective-permute-start | bytes 4276232 | tf_op jit(solution)/shard_map/ppermute | solution.py:704
  273.5 7.0 %fusion.16 = f32[768,768]{1,0:T(8,128)} fusion(bf16[2048,768]{1,0:T(8,128)(2,1)} %bitcast.112, bf16[2048,768]{1,0:T(8,128)(2,1)} %bitcast.117), kind=kOutput, calls=%fused_computation.86 | convolution fusion | flops 2415919104 | bytes 8650752 | tf_op jit(solution)/shard_map/dot_general | solution.py:30
  280.4 24.8 %collective-permute-done.9 = bf16[2,2,96,1856]{3,2,1,0:T(8,128)(2,1)} collective-permute-done((bf16[2,2,96,1856]{3,2,1,0:T(8,128)(2,1)S(1)}, bf16[2,2,96,1856]{3,2,1,0:T(8,128)(2,1)}, u32[]{:S(2)}, u32[]{:S(2)}) %collective-permute-start.9) | collective-permute-done | bytes 1425440 | tf_op jit(solution)/shard_map/ppermute | solution.py:704
  305.2 1.7 add_convert_fusion.3
  307.3 4.7 %collective-permute-done.11 = f32[1,384]{1,0:T(1,128)S(1)} collective-permute-done((f32[1,384]{1,0:T(1,128)S(1)}, f32[1,384]{1,0:T(1,128)S(1)}, u32[]{:S(2)}, u32[]{:S(2)}) %collective-permute-start.11) | collective-permute-done | bytes 1568 | tf_op jit(solution)/shard_map/ppermute | solution.py:704
  312.1 4.7 %collective-permute-done.12 = f32[2,384]{1,0:T(2,128)S(1)} collective-permute-done((f32[2,384]{1,0:T(2,128)S(1)}, f32[2,384]{1,0:T(2,128)S(1)}, u32[]{:S(2)}, u32[]{:S(2)}) %collective-permute-start.12) | collective-permute-done | bytes 3104 | tf_op jit(solution)/shard_map/ppermute | solution.py:704
  318.1 6.0 %collective-permute-done.10 = bf16[1,2,96,1856]{3,2,1,0:T(8,128)(2,1)S(1)} collective-permute-done((bf16[1,2,96,1856]{3,2,1,0:T(8,128)(2,1)S(1)}, bf16[1,2,96,1856]{3,2,1,0:T(8,128)(2,1)S(1)}, u32[]{:S(2)}, u32[]{:S(2)}) %collective-permute-start.10) | collective-permute-done | bytes 712736 | tf_op jit(solution)/shard_map/ppermute | solution.py:704
  324.3 1.7 fusion.6
  326.1 1.4 pad_maximum_fusion
  329.6 2.0 collective-permute-done.13
  331.7 1.5 collective-permute-start.14
  336.0 4.9 %collective-permute-done.14 = bf16[2,96,768]{2,1,0:T(8,128)(2,1)S(1)} collective-permute-done((bf16[2,96,768]{2,1,0:T(8,128)(2,1)S(1)}, bf16[2,96,768]{2,1,0:T(8,128)(2,1)S(1)}, u32[]{:S(2)}, u32[]{:S(2)}) %collective-permute-start.14) | collective-permute-done | bytes 294944 | tf_op jit(solution)/shard_map/ppermute | solution.py:704
  343.3 2.9 collective-permute-done.15
  346.9 1.7 finish_heads.1
  350.7 2.4 add_bitcast_fusion
  353.1 8.8 %reduce-scatter.6.cloned.1.call-done = bf16[1,96,1856]{2,1,0:T(8,128)(2,1)} async-done(((bf16[4,96,1856]{2,1,0:T(8,128)(2,1)}), bf16[1,96,1856]{2,1,0:T(8,128)(2,1)}) %reduce-scatter.6.cloned.1.call-update) | async-done | bytes 356368 | tf_op jit(solution)/shard_map/reduce_scatter | solution.py:892
  361.9 1.9 finish_dense.1
  363.8 1.3 slice_bitcast_fusion
  365.1 2.0 slice_bitcast_fusion.1
  (145 shorter events, 27.6 us)
Async XLA Ops:
  7.2 4.3 %copy-start.13 = (s32[1,512]{1,0:T(1,128)S(1)}, s32[1,512]{1,0:T(1,128)}, u32[]{:S(2)}) copy-start(s32[1,512]{1,0:T(1,128)} %param.22) | copy-start | bytes 6148
  7.2 9.2 %copy-start.9 = (bf16[192,96]{1,0:T(8,128)(2,1)S(1)}, bf16[192,96]{1,0:T(8,128)(2,1)}, u32[]{:S(2)}) copy-start(bf16[192,96]{1,0:T(8,128)(2,1)} %param.28) | copy-start | bytes 110596
  7.2 9.3 %copy-start.8 = (bf16[768,96]{0,1:T(8,128)(2,1)S(1)}, bf16[768,96]{0,1:T(8,128)(2,1)}, u32[]{:S(2)}) copy-start(bf16[768,96]{0,1:T(8,128)(2,1)} %param.30) | copy-start | bytes 442372
  7.2 9.3 %copy-start.7 = (bf16[96,768]{1,0:T(8,128)(2,1)S(1)}, bf16[96,768]{1,0:T(8,128)(2,1)}, u32[]{:S(2)}) copy-start(bf16[96,768]{1,0:T(8,128)(2,1)} %param.29) | copy-start | bytes 442372
  7.2 76.9 %all-gather.5.cloned.1.call-start = ((), (), s32[]{:S(2)}) async-start(), calls=%async_computation.8 | async-start | bytes 3932160 | tf_op jit(solution)/shard_map/all_gather | solution.py:767
  8.0 153.8 %all-gather.7.cloned.1.call-start = ((), (), s32[]{:S(2)}) async-start(), calls=%async_computation.9 | async-start | bytes 6193152 | tf_op jit(solution)/shard_map/all_gather | solution.py:815
  11.0 2.4 collective-permute-start.2
  13.8 12.3 %collective-permute-start.3 = (bf16[192,768]{0,1:T(8,128)(2,1)S(1)}, bf16[192,768]{0,1:T(8,128)(2,1)S(1)}, u32[]{:S(2)}, u32[]{:S(2)}) collective-permute-start(bf16[192,768]{0,1:T(8,128)(2,1)S(1)} %maximum_select_fusion.2), channel_id=1, source_target_pairs={{0,8},{4,12},{8,0},{12,4},{16,24},{20,28},{24,16},{28,20},{1,9},{5... | collective-permute-start | bytes 884744 | tf_op jit(solution)/shard_map/ppermute | solution.py:704
  16.7 25.5 %collective-permute-start = (bf16[1,96,1792]{2,1,0:T(8,128)(2,1)S(1)}, bf16[1,96,1792]{2,1,0:T(8,128)(2,1)S(1)}, u32[]{:S(2)}, u32[]{:S(2)}) collective-permute-start(bf16[1,96,1792]{2,1,0:T(8,128)(2,1)S(1)} %bitcast.84), channel_id=1, source_target_pairs={{0,1},{1,0},{2,3},{3,2},{4,5},{5,4},{6,7},{7,6},{8,9},{9,8},{10,11... | collective-permute-start | bytes 1032200 | tf_op jit(solution)/shard_map/ppermute | solution.py:704
  26.6 15.8 %collective-permute-start.4 = (bf16[384,768]{0,1:T(8,128)(2,1)S(1)}, bf16[384,768]{0,1:T(8,128)(2,1)S(1)}, u32[]{:S(2)}, u32[]{:S(2)}) collective-permute-start(bf16[384,768]{0,1:T(8,128)(2,1)S(1)} %maximum_select_fusion.1), channel_id=1, source_target_pairs={{0,16},{4,20},{8,24},{12,28},{16,0},{20,4},{24,8},{28,12},{1,17},{... | collective-permute-start | bytes 1769480 | tf_op jit(solution)/shard_map/ppermute | solution.py:704
  42.3 13.5 %collective-permute-start.1 = (bf16[2,96,1792]{2,1,0:T(8,128)(2,1)S(1)}, bf16[2,96,1792]{2,1,0:T(8,128)(2,1)}, u32[]{:S(2)}, u32[]{:S(2)}) collective-permute-start(bf16[2,96,1792]{2,1,0:T(8,128)(2,1)S(1)} %pad_maximum_fusion.3), channel_id=1, source_target_pairs={{0,8},{4,12},{8,0},{12,4},{16,24},{20,28},{24,16},{28,20},{1,9},{5... | collective-permute-start | bytes 2064392 | tf_op jit(solution)/shard_map/ppermute | solution.py:704
  43.7 15.0 %copy-start.10 = (s32[1,2048]{1,0:T(1,128)S(1)}, s32[1,2048]{1,0:T(1,128)}, u32[]{:S(2)}) copy-start(s32[1,2048]{1,0:T(1,128)} %refs_2_.5) | copy-start | bytes 24580
  57.0 27.2 %collective-permute-start.5 = (bf16[4,96,1792]{2,1,0:T(8,128)(2,1)S(1)}, bf16[4,96,1792]{2,1,0:T(8,128)(2,1)S(1)}, u32[]{:S(2)}, u32[]{:S(2)}) collective-permute-start(bf16[4,96,1792]{2,1,0:T(8,128)(2,1)S(1)} %pad_maximum_fusion.1), channel_id=1, source_target_pairs={{0,16},{4,20},{8,24},{12,28},{16,0},{20,4},{24,8},{28,12},{1,17},{... | collective-permute-start | bytes 4128776 | tf_op jit(solution)/shard_map/ppermute | solution.py:704
  84.2 29.5 %collective-permute-start.6 = (bf16[2,96,1792]{2,1,0:T(8,128)(2,1)S(1)}, bf16[2,96,1792]{2,1,0:T(8,128)(2,1)}, u32[]{:S(2)}, u32[]{:S(2)}) collective-permute-start(bf16[2,96,1792]{2,1,0:T(8,128)(2,1)S(1)} %pad_maximum_fusion.3), channel_id=1, source_target_pairs={{0,2},{1,3},{2,0},{3,1},{4,6},{5,7},{6,4},{7,5},{8,10},{9,11},{10,... | collective-permute-start | bytes 2064392 | tf_op jit(solution)/shard_map/ppermute | solution.py:704
  114.8 18.0 %copy-start.6 = (bf16[4,384,128]{2,1,0:T(8,128)(2,1)S(1)}, bf16[4,384,128]{2,1,0:T(8,128)(2,1)}, u32[]{:S(2)}) copy-start(bf16[4,384,128]{2,1,0:T(8,128)(2,1)} %get-tuple-element.76) | copy-start | bytes 1179652
  136.0 5.0 %copy-start.16 = (bf16[768]{0:T(1024)(128)(2,1)S(1)}, bf16[768]{0:T(1024)(128)(2,1)}, u32[]{:S(2)}) copy-start(bf16[768]{0:T(1024)(128)(2,1)} %param.33) | copy-start | bytes 4612
  136.0 5.0 %copy-start.17 = (bf16[768]{0:T(1024)(128)(2,1)S(1)}, bf16[768]{0:T(1024)(128)(2,1)}, u32[]{:S(2)}) copy-start(bf16[768]{0:T(1024)(128)(2,1)} %param.35) | copy-start | bytes 4612
  136.0 5.0 %copy-start.18 = (bf16[768]{0:T(1024)(128)(2,1)S(1)}, bf16[768]{0:T(1024)(128)(2,1)}, u32[]{:S(2)}) copy-start(bf16[768]{0:T(1024)(128)(2,1)} %param.36) | copy-start | bytes 4612
  136.0 5.0 %copy-start.19 = (bf16[768]{0:T(1024)(128)(2,1)S(1)}, bf16[768]{0:T(1024)(128)(2,1)}, u32[]{:S(2)}) copy-start(bf16[768]{0:T(1024)(128)(2,1)} %param.37) | copy-start | bytes 4612
  136.0 5.0 %copy-start.20 = (bf16[768]{0:T(1024)(128)(2,1)S(1)}, bf16[768]{0:T(1024)(128)(2,1)}, u32[]{:S(2)}) copy-start(bf16[768]{0:T(1024)(128)(2,1)} %param.38) | copy-start | bytes 4612
  136.1 5.0 %copy-start.21 = (bf16[768]{0:T(1024)(128)(2,1)S(1)}, bf16[768]{0:T(1024)(128)(2,1)}, u32[]{:S(2)}) copy-start(bf16[768]{0:T(1024)(128)(2,1)} %param.39) | copy-start | bytes 4612
  136.1 5.7 %copy-start.14 = (bf16[3072]{0:T(1024)(128)(2,1)S(1)}, bf16[3072]{0:T(1024)(128)(2,1)}, u32[]{:S(2)}) copy-start(bf16[3072]{0:T(1024)(128)(2,1)} %param.34) | copy-start | bytes 18436
  136.1 25.7 %collective-permute-start.7 = (bf16[8,96,1792]{2,1,0:T(8,128)(2,1)}, bf16[8,96,1792]{2,1,0:T(8,128)(2,1)}, u32[]{:S(2)}, u32[]{:S(2)}) collective-permute-start(bf16[8,96,1792]{2,1,0:T(8,128)(2,1)} %constant_dynamic-update-slice_fusion.refs_0_), channel_id=1, source_target_pairs={{0,4},{4,0},{8,12},{12,8},{16,20},{20,16},{24,28},{28,24},{1,5},{5... | collective-permute-start | bytes 8257544 | tf_op jit(solution)/shard_map/ppermute | solution.py:704
  136.2 25.6 %all-to-all-start = ((bf16[4,2,384,128]{3,2,1,0:T(8,128)(2,1)}), bf16[4,2,384,128]{3,2,1,0:T(8,128)(2,1)S(1)}, u32[]{:S(2)}, u32[]{:S(2)}) async-start(bf16[4,2,384,128]{3,2,1,0:T(8,128)(2,1)} %bitcast.15), calls=%async_computation | async-start | bytes 1572864 | tf_op jit(solution)/shard_map/all_to_all | solution.py:809
  141.0 183.3 %reduce-scatter.4.cloned.1.call-start = ((), (), s32[]{:S(2)}) async-start(), calls=%async_computation.5 | async-start | bytes 6635520 | tf_op jit(solution)/shard_map/reduce_scatter | solution.py:857
  161.7 0.9 copy-start
  198.7 3.8 %copy-start.11 = (f32[3,1,1024]{2,1,0:T(1,128)S(1)}, f32[3,1,1024]{2,1,0:T(1,128)}, u32[]{:S(2)}) copy-start(f32[3,1,1024]{2,1,0:T(1,128)} %get-tuple-element.93) | copy-start | bytes 36868
  198.7 3.8 %copy-start.12 = (f32[3,1,1024]{2,1,0:T(1,128)S(1)}, f32[3,1,1024]{2,1,0:T(1,128)}, u32[]{:S(2)}) copy-start(f32[3,1,1024]{2,1,0:T(1,128)} %get-tuple-element.94) | copy-start | bytes 36868
  198.7 23.4 %all-to-all-start.1 = ((bf16[4,2,384,128]{3,2,1,0:T(8,128)(2,1)}), bf16[4,2,384,128]{3,2,1,0:T(8,128)(2,1)S(1)}, u32[]{:S(2)}, u32[]{:S(2)}) async-start(bf16[4,2,384,128]{3,2,1,0:T(8,128)(2,1)} %get-tuple-element.92), calls=%async_computation.1 | async-start | bytes 1572864 | tf_op jit(solution)/shard_map/all_to_all | solution.py:809
  202.2 148.5 %reduce-scatter.8.cloned.1.call-start = ((), (), s32[]{:S(2)}) async-start(), calls=%async_computation.7 | async-start | bytes 3932160 | tf_op jit(solution)/shard_map/reduce_scatter | solution.py:871
  211.1 50.5 %collective-permute-start.8 = (bf16[4,2,96,1856]{3,2,1,0:T(8,128)(2,1)}, bf16[4,2,96,1856]{3,2,1,0:T(8,128)(2,1)}, u32[]{:S(2)}, u32[]{:S(2)}) collective-permute-start(bf16[4,2,96,1856]{3,2,1,0:T(8,128)(2,1)} %bitcast.113), channel_id=1, source_target_pairs={{0,4},{4,0},{8,12},{12,8},{16,20},{20,16},{24,28},{28,24},{1,5},{5... | collective-permute-start | bytes 8552456 | tf_op jit(solution)/shard_map/ppermute | solution.py:704
  222.1 0.9 copy-start.5
  223.0 30.3 %copy-start.4 = (bf16[768,768]{0,1:T(8,128)(2,1)S(1)}, bf16[768,768]{0,1:T(8,128)(2,1)}, u32[]{:S(2)}) copy-start(bf16[768,768]{0,1:T(8,128)(2,1)} %maximum_select_fusion) | copy-start | bytes 3538948
  259.5 1.9 copy-start.1
  259.5 102.4 %reduce-scatter.6.cloned.1.call-start = ((), (), s32[]{:S(2)}) async-start(), calls=%async_computation.6 | async-start | bytes 1843200 | tf_op jit(solution)/shard_map/reduce_scatter | solution.py:892
  261.6 11.8 %copy-start.15 = (f32[1,768]{1,0:T(1,128)S(1)}, f32[1,768]{1,0:T(1,128)}, u32[]{:S(2)}) copy-start(f32[1,768]{1,0:T(1,128)} %get-tuple-element.112) | copy-start | bytes 9220
  264.2 41.1 %collective-permute-start.9 = (bf16[2,2,96,1856]{3,2,1,0:T(8,128)(2,1)S(1)}, bf16[2,2,96,1856]{3,2,1,0:T(8,128)(2,1)}, u32[]{:S(2)}, u32[]{:S(2)}) collective-permute-start(bf16[2,2,96,1856]{3,2,1,0:T(8,128)(2,1)S(1)} %get-tuple-element.100), channel_id=1, source_target_pairs={{0,8},{4,12},{8,0},{12,4},{16,24},{20,28},{24,16},{28,20},{1,9},{5... | collective-permute-start | bytes 4276232 | tf_op jit(solution)/shard_map/ppermute | solution.py:704
  306.9 17.1 %collective-permute-start.10 = (bf16[1,2,96,1856]{3,2,1,0:T(8,128)(2,1)S(1)}, bf16[1,2,96,1856]{3,2,1,0:T(8,128)(2,1)S(1)}, u32[]{:S(2)}, u32[]{:S(2)}) collective-permute-start(bf16[1,2,96,1856]{3,2,1,0:T(8,128)(2,1)S(1)} %get-tuple-element.105), channel_id=1, source_target_pairs={{0,16},{4,20},{8,24},{12,28},{16,0},{20,4},{24,8},{28,12},{1,17},{... | collective-permute-start | bytes 2138120 | tf_op jit(solution)/shard_map/ppermute | solution.py:704
  307.3 4.7 %collective-permute-start.11 = (f32[1,384]{1,0:T(1,128)S(1)}, f32[1,384]{1,0:T(1,128)S(1)}, u32[]{:S(2)}, u32[]{:S(2)}) collective-permute-start(f32[1,384]{1,0:T(1,128)S(1)} %pad_maximum_fusion.8), channel_id=1, source_target_pairs={{0,1},{1,0},{2,3},{3,2},{4,5},{5,4},{6,7},{7,6},{8,9},{9,8},{10,11... | collective-permute-start | bytes 4616 | tf_op jit(solution)/shard_map/ppermute | solution.py:704
  312.0 4.7 %collective-permute-start.12 = (f32[2,384]{1,0:T(2,128)S(1)}, f32[2,384]{1,0:T(2,128)S(1)}, u32[]{:S(2)}, u32[]{:S(2)}) collective-permute-start(f32[2,384]{1,0:T(2,128)S(1)} %maximum_select_fusion.4), channel_id=1, source_target_pairs={{0,2},{1,3},{2,0},{3,1},{4,6},{5,7},{6,4},{7,5},{8,10},{9,11},{10,... | collective-permute-start | bytes 9224 | tf_op jit(solution)/shard_map/ppermute | solution.py:704
  326.0 2.2 copy-start.2
  329.5 2.1 collective-permute-start.13
  331.7 19.0 %copy-start.3 = (f32[512,768]{1,0:T(8,128)S(1)}, f32[512,768]{1,0:T(8,128)}, u32[]{:S(2)}) copy-start(f32[512,768]{1,0:T(8,128)} %get-tuple-element.109) | copy-start | bytes 4718596
  331.7 9.1 %collective-permute-start.14 = (bf16[2,96,768]{2,1,0:T(8,128)(2,1)S(1)}, bf16[2,96,768]{2,1,0:T(8,128)(2,1)S(1)}, u32[]{:S(2)}, u32[]{:S(2)}) collective-permute-start(bf16[2,96,768]{2,1,0:T(8,128)(2,1)S(1)} %dynamic-slice_bitcast_fusion.1), channel_id=1, source_target_pairs={{0,8},{4,12},{8,0},{12,4},{16,24},{20,28},{24,16},{28,20},{1,9},{5... | collective-permute-start | bytes 884744 | tf_op jit(solution)/shard_map/ppermute | solution.py:704
  341.0 5.2 %collective-permute-start.15 = (bf16[1,96,768]{2,1,0:T(8,128)(2,1)S(1)}, bf16[1,96,768]{2,1,0:T(8,128)(2,1)S(1)}, u32[]{:S(2)}, u32[]{:S(2)}) collective-permute-start(bf16[1,96,768]{2,1,0:T(8,128)(2,1)S(1)} %constant_dynamic-slice_fusion), channel_id=1, source_target_pairs={{0,16},{4,20},{8,24},{12,28},{16,0},{20,4},{24,8},{28,12},{1,17},{... | collective-permute-start | bytes 442376 | tf_op jit(solution)/shard_map/ppermute | solution.py:704
Sparse Core Ops, SparseCore 0:
  9.6 68.1 all-gather.4
  113.8 42.7 all-gather.6
  198.8 63.0 reduce-scatter.3
  264.1 61.8 reduce-scatter.7
  328.1 33.7 reduce-scatter.5

commit v14 on v13

--- a/solution.py
+++ b/solution.py
@@ -74,7 +74,7 @@
 
 
 def attend_forward(
-    first_block, lane_ref, low_ref, count_ref, *refs
+    which, lane_ref, low_ref, count_ref, *refs
 ):
     chunk_refs, (seg_col_ref, seg_row_ref, ctx_ref, lse_ref, held, qkv_ref, sems) = refs[:-7], refs[-7:]
     heads = lse_ref.shape[0]
@@ -87,7 +87,8 @@
         for copy in copies:
             copy.wait()
 
-    qb = pl.program_id(0) + first_block
+    halves, half = which
+    qb = pl.program_id(0) * halves + half
     rows = pl.ds(pl.multiple_of(qb * BLOCK, BLOCK), BLOCK)
     seg_q = seg_col_ref[...]
     queries = [
@@ -136,35 +137,34 @@
     )
 
 
-def attend_backward(which, chunks, lane_ref, low_ref, count_ref, *refs):
-    halves, half = which
-    last = half == halves - 1
+def attend_backward(halves, chunks, lane_ref, low_ref, count_ref, *refs):
     chunk_refs, refs = refs[:chunks], refs[chunks:]
-    (seg_col_ref, seg_row_ref, ctx_ref, grad_ref, lse_ref), refs = refs[:5], refs[5:]
-    earlier, refs = refs[:half], refs[half:]
-    if half > 0:
-        before_ref, refs = refs[0], refs[1:]
-    if last:
-        final_ref, sums_ref, dkv, out_ref, qkv_ref, sems = refs
-    else:
-        dkv, query_ref, qkv_ref, sems = refs
+    (seg_col_ref, seg_row_ref, grad_ref), refs = refs[:3], refs[3:]
+    ctx_refs, lse_refs, refs = refs[:halves], refs[halves : 2 * halves], refs[2 * halves :]
+    final_ref, sums_ref, dkv, out_ref, qkv_ref, sems = refs
     heads = dkv.shape[0]
-    step_index = pl.program_id(0)
-    qb = step_index * halves + half
-
-    @pl.when(step_index == 0)
+    qb = pl.program_id(0)
+    half = lax.rem(qb, halves)
+
+    def choose(options):
+        value = options[0][...]
+        for other in range(1, halves):
+            value = jnp.where(half == other, options[other][...], value)
+        return value
+
+    @pl.when(qb == 0)
     def _():
         copies = fetch_chunks(lane_ref, chunk_refs, qkv_ref, sems)
         for copy in copies:
             copy.start()
-        dkv[...] = before_ref[...] if half > 0 else jnp.zeros_like(dkv)
+        dkv[...] = jnp.zeros_like(dkv)
         for copy in copies:
             copy.wait()
 
     rows = pl.ds(pl.multiple_of(qb * BLOCK, BLOCK), BLOCK)
     right = lane_is_right(BLOCK)
     arrived = grad_ref[0]
-    product = arrived.astype(F32) * ctx_ref[0].astype(F32)
+    product = arrived.astype(F32) * choose(ctx_refs)[0].astype(F32)
     upper = product.astype(BF16)
     lower = (product - upper.astype(F32)).astype(BF16)
     pick = (
@@ -189,7 +189,7 @@
         queries.append(qkv_ref[rows, SLAB * h : SLAB * h + 2 * DH] * jnp.asarray(SCALE, BF16))
         pairs.append(jnp.concatenate([queries[h], grads[h]], axis=0))
     seg_q = seg_row_ref[...]
-    lses = lse_ref[...]
+    lses = choose(lse_refs)
     low, count = low_ref[qb], count_ref[qb]
 
     def step(kb, accs):
@@ -213,38 +213,25 @@
     accs = lax.fori_loop(0, count, step, tuple(zero for _ in range(heads)))
     for h in range(heads):
         query_grad = jnp.where(right, 0.0, accs[h] * SCALE).astype(BF16)
-        if last:
-            out_ref[rows, SLAB * h : SLAB * h + 2 * DH] = query_grad
-        else:
-            query_ref[0, :, 2 * DH * h : 2 * DH * (h + 1)] = query_grad
-
-    if last:
-
-        @pl.when(step_index == pl.num_programs(0) - 1)
-        def _():
-            for h in range(heads):
-                at = SLAB * h
-                for other, ref in enumerate(earlier):
-                    for block in range(ref.shape[0]):
-                        start = (block * halves + other) * BLOCK
-                        out_ref[start : start + BLOCK, at : at + 2 * DH] = ref[
-                            block, :, 2 * DH * h : 2 * DH * (h + 1)
-                        ]
-                out_ref[:, at + 2 * DH : at + SLAB] = dkv[h].astype(BF16)
-                sums_ref[:, at : at + SLAB] = column_sum(out_ref[:, at : at + SLAB].astype(F32))
-            rows_each = final_ref.shape[1]
-            copies = []
-            for at in range(final_ref.shape[0]):
-                offset = pl.multiple_of(lax.rem(lane_ref[0] + at, final_ref.shape[0]) * rows_each, rows_each)
-                copies.append(
-                    pltpu.make_async_copy(
-                        out_ref.at[pl.ds(offset, rows_each), :], final_ref.at[at], sems.at[at]
-                    )
-                )
-            for copy in copies:
-                copy.start()
-            for copy in copies:
-                copy.wait()
+        out_ref[rows, SLAB * h : SLAB * h + 2 * DH] = query_grad
+
+    @pl.when(qb == pl.num_programs(0) - 1)
+    def _():
+        for h in range(heads):
+            at = SLAB * h
+            out_ref[:, at + 2 * DH : at + SLAB] = dkv[h].astype(BF16)
+            sums_ref[:, at : at + SLAB] = column_sum(out_ref[:, at : at + SLAB].astype(F32))
+        rows_each = final_ref.shape[1]
+        copies = []
+        for at in range(final_ref.shape[0]):
+            offset = pl.multiple_of(lax.rem(lane_ref[0] + at, final_ref.shape[0]) * rows_each, rows_each)
+            copies.append(
+                pltpu.make_async_copy(out_ref.at[pl.ds(offset, rows_each), :], final_ref.at[at], sems.at[at])
+            )
+        for copy in copies:
+            copy.start()
+        for copy in copies:
+            copy.wait()
 
 
 STEP = 128
@@ -263,12 +250,14 @@
 PACKED = BLOCK + BLOCK // 2
 
 
-def run_forward(first_block, steps, lane, bounds, qkv, seg_col, seg_row):
+def run_forward(which, lane, bounds, qkv, seg_col, seg_row):
+    halves, half = which
     seq_len, width = seg_col.shape[0], qkv[0].shape[1]
     heads = width // SLAB
     blocks = seq_len // BLOCK
+    steps = blocks // halves
     return pl.pallas_call(
-        functools.partial(attend_forward, first_block),
+        functools.partial(attend_forward, which),
         out_shape=(
             jax.ShapeDtypeStruct((steps, PACKED, 2 * DH), BF16),
             jax.ShapeDtypeStruct((heads, 1, steps * BLOCK), F32),
@@ -278,7 +267,7 @@
             grid=(steps,),
             in_specs=[pl.BlockSpec(memory_space=pl.ANY)] * len(qkv)
             + [
-                pl.BlockSpec((BLOCK, 1), lambda q, *_: (q + first_block, 0)),
+                pl.BlockSpec((BLOCK, 1), lambda q, *_: (q * halves + half, 0)),
                 pl.BlockSpec((1, seq_len), lambda q, *_: (0, 0)),
             ],
             out_specs=(
@@ -303,54 +292,38 @@
     )(lane, *bounds, *qkv, seg_col, seg_row)
 
 
-def run_backward(which, lane, bounds, qkv, seg_col, seg_row, ctx, grad, lse, earlier, before):
-    halves, half = which
+def run_backward(lane, bounds, qkv, seg_col, seg_row, grad, ctxs, lses):
     seq_len, width = seg_col.shape[0], qkv[0].shape[1]
     heads = width // SLAB
-    steps = seq_len // BLOCK // halves
-    packed = pl.BlockSpec((1, PACKED, 2 * DH), lambda q, *_: (q, 0, 0))
-
-    def fixed(shape, **more):
-        return pl.BlockSpec(shape, lambda q, *_: (0,) * len(shape), **more)
-
-    once = {"pipeline_mode": pl.Buffered(1)}
-    gathered = (heads, seq_len, 2 * DH)
-    carried = [fixed(value.shape, **once) for value in earlier]
-    carried += [fixed(gathered, **once)] * len(before)
-    scratch = [pltpu.VMEM((seq_len, width), BF16), pltpu.SemaphoreType.DMA((len(qkv),))]
-    if half == halves - 1:
-        out_shape = (
+    halves = len(ctxs)
+
+    def fixed(shape):
+        return pl.BlockSpec(shape, lambda q, *_: (0,) * len(shape))
+
+    return pl.pallas_call(
+        functools.partial(attend_backward, halves, len(qkv)),
+        out_shape=(
             jax.ShapeDtypeStruct((len(qkv), seq_len // len(qkv), width), BF16),
             jax.ShapeDtypeStruct((1, width), F32),
-        )
-        out_specs = (pl.BlockSpec(memory_space=pl.ANY), fixed((1, width)))
-        scratch = [pltpu.VMEM(gathered, F32), pltpu.VMEM((seq_len, width), BF16)] + scratch
-    else:
-        out_shape = (
-            jax.ShapeDtypeStruct(gathered, F32),
-            jax.ShapeDtypeStruct((steps, BLOCK, heads * 2 * DH), BF16),
-        )
-        out_specs = (
-            fixed(gathered),
-            pl.BlockSpec((1, BLOCK, heads * 2 * DH), lambda q, *_: (q, 0, 0)),
-        )
-    return pl.pallas_call(
-        functools.partial(attend_backward, which, len(qkv)),
-        out_shape=out_shape,
+        ),
         grid_spec=pltpu.PrefetchScalarGridSpec(
             num_scalar_prefetch=3,
-            grid=(steps,),
+            grid=(seq_len // BLOCK,),
             in_specs=[pl.BlockSpec(memory_space=pl.ANY)] * len(qkv)
             + [
                 fixed((seq_len, 1)),
-                pl.BlockSpec((1, BLOCK), lambda q, *_: (0, q * halves + half)),
-                packed,
-                packed,
-                pl.BlockSpec((heads, 1, BLOCK), lambda q, *_: (0, 0, q)),
+                pl.BlockSpec((1, BLOCK), lambda q, *_: (0, q)),
+                pl.BlockSpec((1, PACKED, 2 * DH), lambda q, *_: (q, 0, 0)),
             ]
-            + carried,
-            out_specs=out_specs,
-            scratch_shapes=scratch,
+            + [pl.BlockSpec((1, PACKED, 2 * DH), lambda q, *_: (q // halves, 0, 0))] * halves
+            + [pl.BlockSpec((heads, 1, BLOCK), lambda q, *_: (0, 0, q // halves))] * halves,
+            out_specs=(pl.BlockSpec(memory_space=pl.ANY), fixed((1, width))),
+            scratch_shapes=[
+                pltpu.VMEM((heads, seq_len, 2 * DH), F32),
+                pltpu.VMEM((seq_len, width), BF16),
+                pltpu.VMEM((seq_len, width), BF16),
+                pltpu.SemaphoreType.DMA((len(qkv),)),
+            ],
         ),
         compiler_params=pltpu.CompilerParams(
             dimension_semantics=("arbitrary",), vmem_limit_bytes=VMEM_LIMIT
@@ -358,21 +331,22 @@
         cost_estimate=pl.CostEstimate(
             flops=heads * seq_len * seq_len * 4096,
             bytes_accessed=10 << 20,
-            transcendentals=heads * seq_len * seq_len // 3 // halves,
+            transcendentals=heads * seq_len * seq_len // 3,
         ),
         name="attend_backward",
-    )(lane, *bounds, *qkv, seg_col, seg_row, ctx, grad, lse, *earlier, *before)
+    )(lane, *bounds, *qkv, seg_col, seg_row, grad, *ctxs, *lses)
 
 
 def dense_chain(
-    marks, total_tokens, place_ref, ctx_ref, in_ref, teacher_ref, cotangent_ref, valid_ref, vec_ref,
+    marks, halves, total_tokens, place_ref, in_ref, teacher_ref, cotangent_ref, valid_ref, vec_ref,
     inner_bias_ref, *refs
 ):
+    ctx_refs, refs = refs[:halves], refs[halves:]
     pieces = refs[: len(marks)]
     (
         layer_ref, first_grad_ref, ctx_grad_ref, first_ref, branch_grad_ref, attn_grad_ref,
-        act_ref, hidden_grad_ref, notes_ref, w_out, w_in, w_up, slope, sums_ref, inner_sums_ref,
-        gathered, sems,
+        act_out, hidden_grad_out, notes_ref, w_out, w_in, w_up, slope, act_ref, hidden_grad_ref,
+        sums_ref, inner_sums_ref, gathered, sems, out_sems,
     ) = refs[len(marks) :]
     parts, _, head_cols = w_out.shape
     hidden_cols = w_in.shape[2]
@@ -383,6 +357,12 @@
         (0, hidden_cols, w_in),
         (hidden_cols, hidden_cols, w_up),
     )
+
+    def leave(which, slot):
+        source, target = ((act_ref, act_out), (hidden_grad_ref, hidden_grad_out))[which]
+        return pltpu.make_async_copy(
+            source.at[slot], target.at[place_ref[slot]], out_sems.at[which, slot]
+        )
 
     @pl.when(step == 0)
     def _():
@@ -415,7 +395,7 @@
     for slot in range(parts):
         arrive(0, slot)
         counts = counts + column_sum(w_out[slot, :, 2 * DH :].astype(F32))
-        attention = attention + dot(unpack(ctx_ref[place_ref[slot], 0]), w_out[slot, :, : 3 * DH], NT)
+        attention = attention + dot(jnp.concatenate([unpack(ref[place_ref[slot]]) for ref in ctx_refs], axis=0), w_out[slot, :, : 3 * DH], NT)
     first_exact, normed_one, inverse_one = norm_forward(
         in_ref[...].astype(F32) + attention + vec(0), vec(1), vec(2)
     )
@@ -428,7 +408,8 @@
         hidden = dot(first, w_in[slot]) + inner_bias_ref[t]
         bend = 0.5 * (1.0 + lax.erf(hidden * ROOT_HALF))
         activated = (hidden * bend).astype(BF16)
-        act_ref[t] = activated
+        act_ref[slot] = activated
+        leave(0, slot).start()
         slope[slot] = bend + hidden * INV_ROOT_TAU * jnp.exp2(hidden * hidden * (-0.5 * LOG2E))
         arrive(2, slot)
         return branch + dot(activated, w_up[slot], NT)
@@ -455,7 +436,8 @@
     def down(slot, back):
         t = place_ref[slot]
         hidden_grad = (dot(branch_grad, w_up[slot]) * slope[slot]).astype(BF16)
-        hidden_grad_ref[t] = hidden_grad
+        hidden_grad_ref[slot] = hidden_grad
+        leave(1, slot).start()
         inner_sums_ref[t] += column_sum(hidden_grad.astype(F32))
         return back + dot(hidden_grad, w_in[slot], NT)
 
@@ -472,9 +454,11 @@
     middle = BLOCK // 2
     for slot in range(parts):
         back = dot(attn_grad, w_out[slot, :, : 3 * DH]).astype(BF16)
-        ctx_grad_ref[place_ref[slot], 0] = pack(
-            back[:, : 2 * DH], back[:middle, 2 * DH :], back[middle:, 2 * DH :]
-        )
+        for half in range(halves):
+            part = back[half * BLOCK : (half + 1) * BLOCK]
+            ctx_grad_ref[place_ref[slot], half] = pack(
+                part[:, : 2 * DH], part[:middle, 2 * DH :], part[middle:, 2 * DH :]
+            )
 
 
     @pl.when(step == pl.num_programs(0) - 1)
@@ -498,37 +482,36 @@
                 )
         notes_ref[...] = gathered[...].astype(BF16)
 
+    for which in range(2):
+        for slot in range(parts):
+            leave(which, slot).wait()
+
 
 def width_of(ref):
     return ref.shape[-1]
 
 
-def run_dense(note_rows, marks, total_tokens, place, ctx, rows_in, teacher, cotangent, valid, vecs, inner_bias, pieces):
-    parts, halves = ctx.shape[:2]
+def run_dense(note_rows, marks, total_tokens, place, ctxs, rows_in, teacher, cotangent, valid, vecs, inner_bias, pieces):
+    halves, parts = len(ctxs), ctxs[0].shape[0]
     part_len, width = rows_in.shape
     hidden_cols = inner_bias.shape[2]
     out_cols = pieces[0].shape[2] - 2 * hidden_cols
     room = -(-(8 * width + parts * hidden_cols) // (note_rows * 2 * DH)) * 2 * DH
 
-    def by_rows(columns):
-        return pl.BlockSpec((BLOCK, columns), lambda i: (i, 0))
-
-    def by_part(columns):
-        return pl.BlockSpec((parts, BLOCK, columns), lambda i: (0, i, 0))
-
     def fixed(shape):
         return pl.BlockSpec(shape, lambda i: (0,) * len(shape))
 
-    packed = pl.BlockSpec((parts, 1) + ctx.shape[2:], lambda i: (0, i, 0, 0))
+    anywhere = pl.BlockSpec(memory_space=pl.ANY)
     low = jax.ShapeDtypeStruct((part_len, width), BF16)
     wide = jax.ShapeDtypeStruct((parts, part_len, hidden_cols), BF16)
-    smem = pl.BlockSpec(memory_space=pltpu.SMEM)
+    packed = (parts, halves) + ctxs[0].shape[1:]
+    given = (rows_in, teacher, cotangent, valid, vecs, inner_bias) + tuple(ctxs)
     return pl.pallas_call(
-        functools.partial(dense_chain, marks, total_tokens),
+        functools.partial(dense_chain, marks, halves, total_tokens),
         out_shape=(
             low,
             jax.ShapeDtypeStruct((part_len, width), F32),
-            jax.ShapeDtypeStruct(ctx.shape, BF16),
+            jax.ShapeDtypeStruct(packed, BF16),
             low,
             low,
             low,
@@ -536,38 +519,33 @@
             wide,
             jax.ShapeDtypeStruct((note_rows, room), BF16),
         ),
-        grid=(halves,),
-        in_specs=[
-            smem,
-            packed,
-            by_rows(width),
-            by_rows(width),
-            by_rows(width),
-            by_rows(1),
-            fixed(vecs.shape),
-            fixed(inner_bias.shape),
-        ]
-        + [pl.BlockSpec(memory_space=pl.ANY)] * len(pieces),
+        grid=(1,),
+        in_specs=[pl.BlockSpec(memory_space=pltpu.SMEM)]
+        + [fixed(value.shape) for value in given]
+        + [anywhere] * len(pieces),
         out_specs=(
-            by_rows(width),
-            by_rows(width),
-            packed,
-            by_rows(width),
-            by_rows(width),
-            by_rows(width),
-            by_part(hidden_cols),
-            by_part(hidden_cols),
+            fixed(low.shape),
+            fixed(low.shape),
+            fixed(packed),
+            fixed(low.shape),
+            fixed(low.shape),
+            fixed(low.shape),
+            anywhere,
+            anywhere,
             fixed((note_rows, room)),
         ),
         scratch_shapes=[
             pltpu.VMEM((parts, width, out_cols), BF16),
             pltpu.VMEM((parts, width, hidden_cols), BF16),
             pltpu.VMEM((parts, width, hidden_cols), BF16),
-            pltpu.VMEM((parts, BLOCK, hidden_cols), F32),
+            pltpu.VMEM((parts, part_len, hidden_cols), F32),
+            pltpu.VMEM((parts, part_len, hidden_cols), BF16),
+            pltpu.VMEM((parts, part_len, hidden_cols), BF16),
             pltpu.VMEM((8, width), F32),
             pltpu.VMEM((parts, 1, hidden_cols), F32),
             pltpu.VMEM((note_rows, room), F32),
             pltpu.SemaphoreType.DMA((3, parts)),
+            pltpu.SemaphoreType.DMA((2, parts)),
         ],
         compiler_params=pltpu.CompilerParams(
             dimension_semantics=("arbitrary",), vmem_limit_bytes=VMEM_LIMIT
@@ -578,24 +556,26 @@
             transcendentals=2 * part_len * hidden_cols * parts,
         ),
         name="dense_chain",
-    )(place, ctx, rows_in, teacher, cotangent, valid, vecs, inner_bias, *pieces)
+    )(place, *given, *pieces)
 
 
 def dense_weights(
-    plans, place_ref, first_ref, branch_grad_ref, attn_grad_ref, act_ref, hidden_grad_ref, ctx_ref,
-    notes_ref, *refs
+    plans, halves, place_ref, first_ref, branch_grad_ref, attn_grad_ref, act_ref, hidden_grad_ref, notes_ref,
+    *refs
 ):
-    outs, (whole, sems) = refs[:-2], refs[-2:]
+    ctx_refs, outs, (whole, sems) = refs[:halves], refs[halves:-2], refs[-2:]
     step = pl.program_id(0)
     slots = whole.shape[0]
 
     hidden_cols = act_ref.shape[2]
     whole[step, :, :hidden_cols] = dot(first_ref[...], hidden_grad_ref[0], TN).astype(BF16)
     whole[step, :, hidden_cols : 2 * hidden_cols] = dot(branch_grad_ref[...], act_ref[0], TN).astype(BF16)
-    ctx = jnp.concatenate([unpack(ctx_ref[0, half]) for half in range(ctx_ref.shape[1])], axis=0)
+    ctx = jnp.concatenate([unpack(ref[0]) for ref in ctx_refs], axis=0)
     plain = 2 * hidden_cols + ctx.shape[1]
     whole[step, :, 2 * hidden_cols : plain] = dot(attn_grad_ref[...], ctx, TN).astype(BF16)
-    whole[step, :, plain : plain + notes_ref.shape[1]] = notes_ref[...]
+    note_rows, room = notes_ref.shape
+    for at in range(whole.shape[1] // note_rows):
+        whole[step, at * note_rows : (at + 1) * note_rows, plain : plain + room] = notes_ref[...]
     for out, turns in zip(outs, plans):
         block = out.shape[1]
         for at, turn in enumerate(turns):
@@ -612,7 +592,7 @@
             pltpu.make_async_copy(whole.at[slot], whole.at[slot], sems.at[slot]).wait()
 
 
-def run_weights(base, slots, plans, place, notes, first, branch_grad, attn_grad, act, hidden_grad, ctx):
+def run_weights(base, slots, plans, place, notes, first, branch_grad, attn_grad, act, hidden_grad, ctxs):
     _, part_len, hidden_cols = act.shape
     width = first.shape[1]
     columns = 2 * hidden_cols + 3 * DH + notes.shape[1]
@@ -622,7 +602,7 @@
         jax.ShapeDtypeStruct((len(turns) * slots, block, columns), BF16) for block, turns in plans
     )
     return pl.pallas_call(
-        functools.partial(dense_weights, tuple(turns for _, turns in plans)),
+        functools.partial(dense_weights, tuple(turns for _, turns in plans), len(ctxs)),
         out_shape=outs,
         grid_spec=pltpu.PrefetchScalarGridSpec(
             num_scalar_prefetch=1,
@@ -633,8 +613,10 @@
                 fixed,
                 by_slot,
                 by_slot,
-                pl.BlockSpec((1,) + ctx.shape[1:], lambda s, place: (place[base + s], 0, 0, 0)),
                 pl.BlockSpec(notes.shape, lambda s, place: (0, 0)),
+            ]
+            + [
+                pl.BlockSpec((1,) + ctx.shape[1:], lambda s, place: (place[base + s], 0, 0)) for ctx in ctxs
             ],
             out_specs=tuple(pl.BlockSpec(memory_space=pl.ANY) for _ in outs),
             scratch_shapes=[
@@ -651,7 +633,7 @@
             transcendentals=0,
         ),
         name="dense_weights",
-    )(place, first, branch_grad, attn_grad, act, hidden_grad, ctx, notes)
+    )(place, first, branch_grad, attn_grad, act, hidden_grad, notes, *ctxs)
 
 
 def finish_dense(packed_ref, inner_ref, outer_ref, output_ref, notes_ref):
@@ -806,21 +788,21 @@
     lane = rank.astype(jnp.int32).reshape(1)
 
     def exchange(packed_blocks):
-        return lax.all_to_all(packed_blocks.reshape(parts, halves, PACKED, 2 * DH), "tensor", 0, 0)
-
-    blocks = seq_len // BLOCK
-    early = run_forward(0, blocks // 2, lane, bounds, qkv, seg_col, seg_row)
+        return lax.all_to_all(packed_blocks, "tensor", 0, 0)
+
+    contexts, lses, arrived = [], [], []
+    for half in range(halves):
+        if paired and half == 1:
+            far, contexts[0], bounds = lax.optimization_barrier((far, contexts[0], bounds))
+            weights = lax.all_gather(far, "dp", axis=0, tiled=False)
+        context, lse = run_forward((halves, half), lane, bounds, qkv, seg_col, seg_row)
+        contexts.append(context)
+        lses.append(lse)
+        arrived.append(exchange(context))
     if paired:
-        far, early, bounds = lax.optimization_barrier((far, early, bounds))
-        weights = lax.all_gather(far, "dp", axis=0, tiled=False)
-    late = run_forward(blocks // 2, blocks // 2, lane, bounds, qkv, seg_col, seg_row)
-    context = jnp.concatenate((early[0], late[0]), axis=0)
-    lse = jnp.concatenate((early[1], late[1]), axis=2)
-    if paired:
-        near_next, context = lax.optimization_barrier((near_next, context))
+        near_next, context = lax.optimization_barrier((near_next, contexts[-1]))
         near = jnp.concatenate([near, near_next], axis=0)
         near_other = swap(near, "dp", 1)
-    arrived = exchange(context)
     if paired:
         weights = weights.reshape((copies * 2,) + mine.shape)
         pieces = [near, near_other, weights]
@@ -845,9 +827,10 @@
         shard_rows, marks, float(total_tokens), place, arrived, rows_in, teacher_rows, cotangent_rows, valid_rows, vecs,
         inner_rows, pieces,
     )
-    head_grad = exchange(context_grad).reshape(context.shape)
+    head_grad = exchange(context_grad).reshape((parts * halves, PACKED, 2 * DH))
     sources = (first, branch_grad, attn_grad, activated, hidden_grad, arrived)
-    notes = jnp.tile(notes, (copies, 1))
+    if shard_rows % 16:
+        notes = jnp.tile(notes, (copies, 1))
     if paired:
         keep_turns = (0, 4, 2, 6)
         (distant,) = run_weights(2, 2, ((width, (0,)),), place, notes, *sources)
@@ -860,9 +843,7 @@
         (packed,) = run_weights(0, parts, ((width, (0,)),), place, notes, *sources)
         packed = lax.psum_scatter(packed, "dp", scatter_dimension=1, tiled=True)
 
-    joined_grad, sums = run_backward(
-        (1, 0), lane, bounds, qkv, seg_col, seg_row, context, head_grad, lse, [], []
-    )
+    joined_grad, sums = run_backward(lane, bounds, qkv, seg_col, seg_row, head_grad, contexts, lses)
     joined_grad = joined_grad.reshape(seq_len, -1)
     attn_back = dot(joined_grad, w_heads, NT).astype(BF16)
     if paired:

time: 377 us -> 385 us (1.021); the launches traced: 375 us -> 378 us
  blocking collectives: 0 us -> 16.3 us
  waiting for transfers between devices: 148 us -> 134 us
  Pallas kernels: 108 us -> 119 us
  starting transfers between devices: 33.7 us -> 26.4 us
    all_to_all x0 -> x1, blocking collectives: none -> 16.3 us  [exchange(): return lax.all_to_all(packed_blocks, 'tensor', 0, 0)]
    pallas_call x4, Pallas kernels: 88.3 us -> 99.5 us  [the longest x1 37.3 us: run_backward(): pl.pallas_call(functools.partial(attend_backward, halves, len(qkv)), out_...]
    all_to_all x2, waiting for transfers between devices: 28.8 us -> 18.1 us  [exchange(): return lax.all_to_all(packed_blocks, 'tensor', 0, 0)]
    ppermute x16, starting transfers between devices: 24.7 us -> 18.8 us  [swap(): return lax.ppermute(value, axis, [(i, i ^ bit) for i in range(size)])]
    ppermute x16, waiting for transfers between devices: 110 us -> 105 us  [swap(): return lax.ppermute(value, axis, [(i, i ^ bit) for i in range(size)])]
    unnamed x50 -> x46, local copies, waits for them, and re-layouts: 8.19 us -> 8.1 us
  transfers between devices with their start and end apart: 23 -> 23, of which waited for: 15 -> 14; matrix products, arithmetic and copies ran while one was open for 15% -> 15% of each run, Pallas kernels for 19% -> 22%
where the time goes in v14:
time: 385 us; the launch traced here: 378 us
  waiting for transfers between devices  134 us (35%)
  Pallas kernels  119 us (31%)
  starting transfers between devices  26.4 us (7%)
  other arithmetic  22.1 us (6%)
  local copies, waits for them, and re-layouts  20.7 us (5%)
  matrix products  20.2 us (5%)
  between operations  19.3 us (5%)
  blocking collectives  16.3 us (4%)
    ppermute x16, waiting for transfers between devices, swap(): return lax.ppermute(value, axis, [(i, i ^ bit) for i in range(size)])  105 us
    pallas_call x1, Pallas kernels, run_backward(): pl.pallas_call(functools.partial(attend_backward, halves, len(qkv)), out_...  37.3 us
    pallas_call x2, Pallas kernels, run_forward(): pl.pallas_call(functools.partial(attend_forward, which), out_shape=(jax.S...  37 us
    pallas_call x1, Pallas kernels, run_dense(): pl.pallas_call(functools.partial(dense_chain, marks, halves, total_tokens...  25.1 us
    dot_general x3, matrix products, dot(): lax.dot_general(left_side, right_side, dims, preferred_element_type=F32)  20.2 us
    ppermute x16, starting transfers between devices, swap(): return lax.ppermute(value, axis, [(i, i ^ bit) for i in range(size)])  18.8 us
    all_to_all x2, waiting for transfers between devices, exchange(): return lax.all_to_all(packed_blocks, 'tensor', 0, 0)  18.1 us
    all_to_all x1, blocking collectives, exchange(): return lax.all_to_all(packed_blocks, 'tensor', 0, 0)  16.3 us
  transfers between devices with their start and end apart: 23, of which 14 were waited for; matrix products, arithmetic and copies ran while one was open for 15% of the time, Pallas kernels for 22%

profile of v14, /device:TPU:0, one launch (start us, length us, event | category | flops | bytes accessed | tf_op | source)
XLA Modules:
  0.0 378.0 jit_solution(10612251449045737702)
XLA Ops:
  13.8 2.6 collective-permute-start.3
  16.7 1.6 collective-permute-start
  18.3 7.8 %collective-permute-done.3 = bf16[192,768]{0,1:T(8,128)(2,1)S(1)} collective-permute-done((bf16[192,768]{0,1:T(8,128)(2,1)S(1)}, bf16[192,768]{0,1:T(8,128)(2,1)S(1)}, u32[]{:S(2)}, u32[]{:S(2)}) %collective-permute-start.3) | collective-permute-done | bytes 294944 | tf_op jit(solution)/shard_map/ppermute | solution.py:686
  26.6 1.8 collective-permute-start.4
  28.5 13.8 %collective-permute-done = bf16[1,96,1792]{2,1,0:T(8,128)(2,1)S(1)} collective-permute-done((bf16[1,96,1792]{2,1,0:T(8,128)(2,1)S(1)}, bf16[1,96,1792]{2,1,0:T(8,128)(2,1)S(1)}, u32[]{:S(2)}, u32[]{:S(2)}) %collective-permute-start) | collective-permute-done | bytes 344096 | tf_op jit(solution)/shard_map/ppermute | solution.py:686
  42.4 1.3 maximum_select_fusion
  43.7 12.1 %collective-permute-done.1 = bf16[2,96,1792]{2,1,0:T(8,128)(2,1)} collective-permute-done((bf16[2,96,1792]{2,1,0:T(8,128)(2,1)S(1)}, bf16[2,96,1792]{2,1,0:T(8,128)(2,1)}, u32[]{:S(2)}, u32[]{:S(2)}) %collective-permute-start.1) | collective-permute-done | bytes 688160 | tf_op jit(solution)/shard_map/ppermute | solution.py:686
  55.7 1.2 pad_maximum_fusion.1
  57.0 1.7 collective-permute-start.5
  60.0 1.4 copy.93.refs_1_
  62.2 22.0 %collective-permute-done.5 = bf16[4,96,1792]{2,1,0:T(8,128)(2,1)S(1)} collective-permute-done((bf16[4,96,1792]{2,1,0:T(8,128)(2,1)S(1)}, bf16[4,96,1792]{2,1,0:T(8,128)(2,1)S(1)}, u32[]{:S(2)}, u32[]{:S(2)}) %collective-permute-start.5) | collective-permute-done | bytes 1376288 | tf_op jit(solution)/shard_map/ppermute | solution.py:686
  84.2 5.0 %collective-permute-start.6 = (bf16[2,96,1792]{2,1,0:T(8,128)(2,1)S(1)}, bf16[2,96,1792]{2,1,0:T(8,128)(2,1)}, u32[]{:S(2)}, u32[]{:S(2)}) collective-permute-start(bf16[2,96,1792]{2,1,0:T(8,128)(2,1)S(1)} %pad_maximum_fusion.2), channel_id=1, source_target_pairs={{0,2},{1,3},{2,0},{3,1},{4,6},{5,7},{6,4},{7,5},{8,10},{9,11},{10,... | collective-permute-start | bytes 2064392 | tf_op jit(solution)/shard_map/ppermute | solution.py:686
  89.2 6.5 %add_convert_fusion.refs_0_ = bf16[2048,768]{1,0:T(8,128)(2,1)} fusion(bf16[2048,768]{1,0:T(8,128)(2,1)} %bitcast.107, bf16[768,768]{0,1:T(8,128)(2,1)} %maximum_select_fusion, f32[768]{0:T(1024)S(1)} %add.115), kind=kOutput, calls=%fused_computation | convolution fusion | flops 2419064832 | bytes 7474176 | tf_op jit(solution)/shard_map/dot_general | solution.py:30
  95.7 19.8 %attend_forward.2 = (bf16[4,384,128]{2,1,0:T(8,128)(2,1)}, f32[3,1,1024]{2,1,0:T(1,128)}) custom-call(s32[1]{0:T(128)} %bitcast.lane_ref, s32[8]{0:T(128)} %get-tuple-element.72.low_ref, s32[8]{0:T(128)} %get-tuple-element.73.count_ref, bf16[2048,768]{1,0:T(8,128)(2,1)} %add_convert_fusion.refs_0_, s32[2048,1]{1,0:T(8,128)} %copy.93.refs_1_, s32[1,2048]{1,0:T(1,128)} %refs_2_.5), custom_call_target="tpu_custom_call" | custom-call | flops 12884901888 | bytes 5242880 | tf_op jit(solution)/shard_map/attend_forward/pallas_call | solution.py:259
  115.5 1.2 constant_dynamic-update-slice_fusion.1
  116.7 17.2 %attend_forward.3 = (bf16[4,384,128]{2,1,0:T(8,128)(2,1)}, f32[3,1,1024]{2,1,0:T(1,128)}) custom-call(s32[1]{0:T(128)} %bitcast.lane_ref, s32[8]{0:T(128)} %get-tuple-element.72.low_ref, s32[8]{0:T(128)} %get-tuple-element.73.count_ref, bf16[2048,768]{1,0:T(8,128)(2,1)} %add_convert_fusion.refs_0_, s32[2048,1]{1,0:T(8,128)} %copy.93.refs_1_, s32[1,2048]{1,0:T(1,128)} %refs_2_.5), custom_call_target="tpu_custom_call" | custom-call | flops 12884901888 | bytes 5242880 | tf_op jit(solution)/shard_map/attend_forward/pallas_call | solution.py:259
  134.0 1.2 constant_dynamic-update-slice_fusion.refs_2_
  135.3 16.3 %all_to_all.15.refs_0_ = bf16[4,384,128]{2,1,0:T(8,128)(2,1)} all-to-all(bf16[4,384,128]{2,1,0:T(8,128)(2,1)S(1)} %copy-done.6), channel_id=1, replica_groups=mesh['dp'=8,'tensor'=4] {'tensor'}, dimensions={0} | all-to-all | bytes 786432 | tf_op jit(solution)/shard_map/all_to_all | solution.py:791
  151.5 3.5 all-to-all-start.1
  158.1 8.4 %all-to-all-done.1.refs_1_ = bf16[4,384,128]{2,1,0:T(8,128)(2,1)S(1)} async-done(((bf16[4,384,128]{2,1,0:T(8,128)(2,1)}), bf16[4,384,128]{2,1,0:T(8,128)(2,1)S(1)}, u32[]{:S(2)}, u32[]{:S(2)}) %all-to-all-start.1) | async-done | bytes 393248 | tf_op jit(solution)/shard_map/all_to_all | solution.py:791
  167.2 25.1 %dense_chain.1 = (bf16[512,768]{1,0:T(8,128)(2,1)}, f32[512,768]{1,0:T(8,128)}, bf16[4,2,384,128]{3,2,1,0:T(8,128)(2,1)}, bf16[512,768]{1,0:T(8,128)(2,1)}, bf16...) custom-call(s32[5]{0:T(128)} %stack.53.place_ref, ...), custom_call_target="tpu_custom_call" | custom-call | flops 22548578304 | bytes 25165824 | tf_op jit(solution)/shard_map/dense_chain/pallas_call | solution.py:509
  192.3 7.9 %dense_weights.3 = bf16[2,768,1856]{2,1,0:T(8,128)(2,1)} custom-call(s32[5]{0:T(128)} %stack.53.place_ref, bf16[512,768]{1,0:T(8,128)(2,1)} %get-tuple-element.79.first_ref, bf16[512,768]{1,0:T(8,128)(2,1)} %get-tuple-element.80.branch_grad_ref, bf16[512,768]{1,0:T(8,128)(2,1)} %get-tuple-element.81.attn_grad_ref, ...), custom_call_target="tpu_custom_call" | custom-call | flops 2919235584 | bytes 10485760 | tf_op jit(solution)/shard_map/dense_weights/pallas_call | solution.py:604
  200.2 3.5 all-to-all-start.2
  203.8 8.4 %dense_weights.2 = (bf16[8,96,1856]{2,1,0:T(8,128)(2,1)}, bf16[8,96,1856]{2,1,0:T(8,128)(2,1)}) custom-call(s32[5]{0:T(128)} %stack.53.place_ref, bf16[512,768]{1,0:T(8,128)(2,1)} %get-tuple-element.79.first_ref, bf16[512,768]{1,0:T(8,128)(2,1)} %get-tuple-element.80.branch_grad_ref, bf16[512,768]{1,0:T(8,128)(2,1)} %get-tuple-element.81.attn_grad_ref, ...), custom_call_target="tpu_custom_call" | custom-call | flops 2919235584 | bytes 10485760 | tf_op jit(solution)/shard_map/dense_weights/pallas_call | solution.py:604
  212.2 9.7 %all-to-all-done.2 = bf16[4,2,384,128]{3,2,1,0:T(8,128)(2,1)S(1)} async-done(((bf16[4,2,384,128]{3,2,1,0:T(8,128)(2,1)}), bf16[4,2,384,128]{3,2,1,0:T(8,128)(2,1)S(1)}, u32[]{:S(2)}, u32[]{:S(2)}) %all-to-all-start.2) | async-done | bytes 786464 | tf_op jit(solution)/shard_map/all_to_all | solution.py:791
  222.9 37.3 %attend_backward.1 = (bf16[1,2048,768]{2,1,0:T(8,128)(2,1)}, f32[1,768]{1,0:T(1,128)}) custom-call(s32[1]{0:T(128)} %bitcast.lane_ref, s32[8]{0:T(128)} %get-tuple-element.72.low_ref, s32[8]{0:T(128)} %get-tuple-element.73.count_ref, bf16[2048,768]{1,0:T(8,128)(2,1)} %add_convert_fusion.refs_0_, s32[2048,1]{1,0:T(8,128)} %copy.93.refs_1_, ...), custom_call_target="tpu_custom_call" | custom-call | flops 51539607552 | bytes 10485760 | tf_op jit(solution)/shard_map/attend_backward/pallas_call | solution.py:303
  260.2 6.2 %convolution_convert_fusion = bf16[2048,768]{1,0:T(8,128)(2,1)} fusion(bf16[768,768]{0,1:T(8,128)(2,1)S(1)} %copy-done.4, bf16[1,2048,768]{2,1,0:T(8,128)(2,1)} %get-tuple-element.91), kind=kOutput, calls=%fused_computation.1 | convolution fusion | flops 2417491968 | bytes 7471104 | tf_op jit(solution)/shard_map/dot_general | solution.py:30
  266.8 1.5 copy-done
  268.5 2.6 fusion
  271.4 7.5 %fusion.16 = f32[768,768]{1,0:T(8,128)} fusion(bf16[2048,768]{1,0:T(8,128)(2,1)} %bitcast.108, bf16[2048,768]{1,0:T(8,128)(2,1)} %bitcast.113), kind=kOutput, calls=%fused_computation.84 | convolution fusion | flops 2415919104 | bytes 8650752 | tf_op jit(solution)/shard_map/dot_general | solution.py:30
  278.9 26.4 %collective-permute-done.9 = bf16[2,2,96,1856]{3,2,1,0:T(8,128)(2,1)} collective-permute-done((bf16[2,2,96,1856]{3,2,1,0:T(8,128)(2,1)S(1)}, bf16[2,2,96,1856]{3,2,1,0:T(8,128)(2,1)}, u32[]{:S(2)}, u32[]{:S(2)}) %collective-permute-start.9) | collective-permute-done | bytes 1425440 | tf_op jit(solution)/shard_map/ppermute | solution.py:686
  305.2 1.7 add_convert_fusion.3
  306.9 2.0 collective-permute-start.10
  309.2 4.9 %collective-permute-done.11 = f32[1,384]{1,0:T(1,128)S(1)} collective-permute-done((f32[1,384]{1,0:T(1,128)S(1)}, f32[1,384]{1,0:T(1,128)S(1)}, u32[]{:S(2)}, u32[]{:S(2)}) %collective-permute-start.11) | collective-permute-done | bytes 1568 | tf_op jit(solution)/shard_map/ppermute | solution.py:686
  314.2 4.7 %collective-permute-done.12 = f32[2,384]{1,0:T(2,128)S(1)} collective-permute-done((f32[2,384]{1,0:T(2,128)S(1)}, f32[2,384]{1,0:T(2,128)S(1)}, u32[]{:S(2)}, u32[]{:S(2)}) %collective-permute-start.12) | collective-permute-done | bytes 3104 | tf_op jit(solution)/shard_map/ppermute | solution.py:686
  320.2 4.1 %collective-permute-done.10 = bf16[1,2,96,1856]{3,2,1,0:T(8,128)(2,1)S(1)} collective-permute-done((bf16[1,2,96,1856]{3,2,1,0:T(8,128)(2,1)S(1)}, bf16[1,2,96,1856]{3,2,1,0:T(8,128)(2,1)S(1)}, u32[]{:S(2)}, u32[]{:S(2)}) %collective-permute-start.10) | collective-permute-done | bytes 712736 | tf_op jit(solution)/shard_map/ppermute | solution.py:686
  324.5 1.7 fusion.6
  326.2 1.5 pad_maximum_fusion
  329.8 2.0 collective-permute-done.13
  331.9 2.6 collective-permute-start.14
  337.3 4.6 %collective-permute-done.14 = bf16[2,96,768]{2,1,0:T(8,128)(2,1)S(1)} collective-permute-done((bf16[2,96,768]{2,1,0:T(8,128)(2,1)S(1)}, bf16[2,96,768]{2,1,0:T(8,128)(2,1)S(1)}, u32[]{:S(2)}, u32[]{:S(2)}) %collective-permute-start.14) | collective-permute-done | bytes 294944 | tf_op jit(solution)/shard_map/ppermute | solution.py:686
  344.3 3.2 collective-permute-done.15
  348.2 1.7 finish_heads.1
  352.1 2.4 add_bitcast_fusion
  354.5 9.6 %reduce-scatter.6.cloned.1.call-done = bf16[1,96,1856]{2,1,0:T(8,128)(2,1)} async-done(((bf16[4,96,1856]{2,1,0:T(8,128)(2,1)}), bf16[1,96,1856]{2,1,0:T(8,128)(2,1)}) %reduce-scatter.6.cloned.1.call-update) | async-done | bytes 356368 | tf_op jit(solution)/shard_map/reduce_scatter | solution.py:873
  364.1 1.9 finish_dense.1
  366.0 1.3 slice_bitcast_fusion
  367.3 2.0 slice_bitcast_fusion.1
  (139 shorter events, 24.7 us)
Async XLA Ops:
  7.2 4.3 %copy-start.11 = (s32[1,512]{1,0:T(1,128)S(1)}, s32[1,512]{1,0:T(1,128)}, u32[]{:S(2)}) copy-start(s32[1,512]{1,0:T(1,128)} %param.22) | copy-start | bytes 6148
  7.2 9.2 %copy-start.9 = (bf16[192,96]{1,0:T(8,128)(2,1)S(1)}, bf16[192,96]{1,0:T(8,128)(2,1)}, u32[]{:S(2)}) copy-start(bf16[192,96]{1,0:T(8,128)(2,1)} %param.28) | copy-start | bytes 110596
  7.2 9.3 %copy-start.8 = (bf16[768,96]{0,1:T(8,128)(2,1)S(1)}, bf16[768,96]{0,1:T(8,128)(2,1)}, u32[]{:S(2)}) copy-start(bf16[768,96]{0,1:T(8,128)(2,1)} %param.30) | copy-start | bytes 442372
  7.2 9.3 %copy-start.7 = (bf16[96,768]{1,0:T(8,128)(2,1)S(1)}, bf16[96,768]{1,0:T(8,128)(2,1)}, u32[]{:S(2)}) copy-start(bf16[96,768]{1,0:T(8,128)(2,1)} %param.29) | copy-start | bytes 442372
  7.2 76.9 %all-gather.5.cloned.1.call-start = ((), (), s32[]{:S(2)}) async-start(), calls=%async_computation.9 | async-start | bytes 3932160 | tf_op jit(solution)/shard_map/all_gather | solution.py:749
  8.0 158.5 %all-gather.7.cloned.1.call-start = ((), (), s32[]{:S(2)}) async-start(), calls=%async_computation.10 | async-start | bytes 6193152 | tf_op jit(solution)/shard_map/all_gather | solution.py:797
  11.0 2.4 collective-permute-start.2
  13.8 12.3 %collective-permute-start.3 = (bf16[192,768]{0,1:T(8,128)(2,1)S(1)}, bf16[192,768]{0,1:T(8,128)(2,1)S(1)}, u32[]{:S(2)}, u32[]{:S(2)}) collective-permute-start(bf16[192,768]{0,1:T(8,128)(2,1)S(1)} %maximum_select_fusion.2), channel_id=1, source_target_pairs={{0,8},{4,12},{8,0},{12,4},{16,24},{20,28},{24,16},{28,20},{1,9},{5... | collective-permute-start | bytes 884744 | tf_op jit(solution)/shard_map/ppermute | solution.py:686
  16.7 25.5 %collective-permute-start = (bf16[1,96,1792]{2,1,0:T(8,128)(2,1)S(1)}, bf16[1,96,1792]{2,1,0:T(8,128)(2,1)S(1)}, u32[]{:S(2)}, u32[]{:S(2)}) collective-permute-start(bf16[1,96,1792]{2,1,0:T(8,128)(2,1)S(1)} %bitcast.82), channel_id=1, source_target_pairs={{0,1},{1,0},{2,3},{3,2},{4,5},{5,4},{6,7},{7,6},{8,9},{9,8},{10,11... | collective-permute-start | bytes 1032200 | tf_op jit(solution)/shard_map/ppermute | solution.py:686
  26.6 15.8 %collective-permute-start.4 = (bf16[384,768]{0,1:T(8,128)(2,1)S(1)}, bf16[384,768]{0,1:T(8,128)(2,1)S(1)}, u32[]{:S(2)}, u32[]{:S(2)}) collective-permute-start(bf16[384,768]{0,1:T(8,128)(2,1)S(1)} %maximum_select_fusion.1), channel_id=1, source_target_pairs={{0,16},{4,20},{8,24},{12,28},{16,0},{20,4},{24,8},{28,12},{1,17},{... | collective-permute-start | bytes 1769480 | tf_op jit(solution)/shard_map/ppermute | solution.py:686
  42.3 13.5 %collective-permute-start.1 = (bf16[2,96,1792]{2,1,0:T(8,128)(2,1)S(1)}, bf16[2,96,1792]{2,1,0:T(8,128)(2,1)}, u32[]{:S(2)}, u32[]{:S(2)}) collective-permute-start(bf16[2,96,1792]{2,1,0:T(8,128)(2,1)S(1)} %pad_maximum_fusion.2), channel_id=1, source_target_pairs={{0,8},{4,12},{8,0},{12,4},{16,24},{20,28},{24,16},{28,20},{1,9},{5... | collective-permute-start | bytes 2064392 | tf_op jit(solution)/shard_map/ppermute | solution.py:686
  43.7 15.0 %copy-start.10 = (s32[1,2048]{1,0:T(1,128)S(1)}, s32[1,2048]{1,0:T(1,128)}, u32[]{:S(2)}) copy-start(s32[1,2048]{1,0:T(1,128)} %refs_2_.5) | copy-start | bytes 24580
  57.0 27.2 %collective-permute-start.5 = (bf16[4,96,1792]{2,1,0:T(8,128)(2,1)S(1)}, bf16[4,96,1792]{2,1,0:T(8,128)(2,1)S(1)}, u32[]{:S(2)}, u32[]{:S(2)}) collective-permute-start(bf16[4,96,1792]{2,1,0:T(8,128)(2,1)S(1)} %pad_maximum_fusion.1), channel_id=1, source_target_pairs={{0,16},{4,20},{8,24},{12,28},{16,0},{20,4},{24,8},{28,12},{1,17},{... | collective-permute-start | bytes 4128776 | tf_op jit(solution)/shard_map/ppermute | solution.py:686
  84.2 31.3 %collective-permute-start.6 = (bf16[2,96,1792]{2,1,0:T(8,128)(2,1)S(1)}, bf16[2,96,1792]{2,1,0:T(8,128)(2,1)}, u32[]{:S(2)}, u32[]{:S(2)}) collective-permute-start(bf16[2,96,1792]{2,1,0:T(8,128)(2,1)S(1)} %pad_maximum_fusion.2), channel_id=1, source_target_pairs={{0,2},{1,3},{2,0},{3,1},{4,6},{5,7},{6,4},{7,5},{8,10},{9,11},{10,... | collective-permute-start | bytes 2064392 | tf_op jit(solution)/shard_map/ppermute | solution.py:686
  133.9 1.3 copy-start.6
  135.1 20.1 %copy-start.14 = (bf16[768]{0:T(1024)(128)(2,1)S(1)}, bf16[768]{0:T(1024)(128)(2,1)}, u32[]{:S(2)}) copy-start(bf16[768]{0:T(1024)(128)(2,1)} %param.33) | copy-start | bytes 4612
  135.1 20.1 %copy-start.15 = (bf16[768]{0:T(1024)(128)(2,1)S(1)}, bf16[768]{0:T(1024)(128)(2,1)}, u32[]{:S(2)}) copy-start(bf16[768]{0:T(1024)(128)(2,1)} %param.35) | copy-start | bytes 4612
  135.1 20.1 %copy-start.16 = (bf16[768]{0:T(1024)(128)(2,1)S(1)}, bf16[768]{0:T(1024)(128)(2,1)}, u32[]{:S(2)}) copy-start(bf16[768]{0:T(1024)(128)(2,1)} %param.36) | copy-start | bytes 4612
  135.1 20.2 %copy-start.17 = (bf16[768]{0:T(1024)(128)(2,1)S(1)}, bf16[768]{0:T(1024)(128)(2,1)}, u32[]{:S(2)}) copy-start(bf16[768]{0:T(1024)(128)(2,1)} %param.37) | copy-start | bytes 4612
  135.1 20.2 %copy-start.18 = (bf16[768]{0:T(1024)(128)(2,1)S(1)}, bf16[768]{0:T(1024)(128)(2,1)}, u32[]{:S(2)}) copy-start(bf16[768]{0:T(1024)(128)(2,1)} %param.38) | copy-start | bytes 4612
  135.2 20.2 %copy-start.19 = (bf16[768]{0:T(1024)(128)(2,1)S(1)}, bf16[768]{0:T(1024)(128)(2,1)}, u32[]{:S(2)}) copy-start(bf16[768]{0:T(1024)(128)(2,1)} %param.39) | copy-start | bytes 4612
  135.2 20.9 %copy-start.12 = (bf16[3072]{0:T(1024)(128)(2,1)S(1)}, bf16[3072]{0:T(1024)(128)(2,1)}, u32[]{:S(2)}) copy-start(bf16[3072]{0:T(1024)(128)(2,1)} %param.34) | copy-start | bytes 18436
  135.2 31.3 %collective-permute-start.7 = (bf16[8,96,1792]{2,1,0:T(8,128)(2,1)}, bf16[8,96,1792]{2,1,0:T(8,128)(2,1)}, u32[]{:S(2)}, u32[]{:S(2)}) collective-permute-start(bf16[8,96,1792]{2,1,0:T(8,128)(2,1)} %constant_dynamic-update-slice_fusion.refs_2_), channel_id=1, source_target_pairs={{0,4},{4,0},{8,12},{12,8},{16,20},{20,16},{24,28},{28,24},{1,5},{5... | collective-permute-start | bytes 8257544 | tf_op jit(solution)/shard_map/ppermute | solution.py:686
  151.5 14.9 %all-to-all-start.1 = ((bf16[4,384,128]{2,1,0:T(8,128)(2,1)}), bf16[4,384,128]{2,1,0:T(8,128)(2,1)S(1)}, u32[]{:S(2)}, u32[]{:S(2)}) async-start(bf16[4,384,128]{2,1,0:T(8,128)(2,1)} %get-tuple-element.74.refs_5_), calls=%async_computation.1 | async-start | bytes 786432 | tf_op jit(solution)/shard_map/all_to_all | solution.py:791
  155.0 169.5 %reduce-scatter.4.cloned.1.call-start = ((), (), s32[]{:S(2)}) async-start(), calls=%async_computation.6 | async-start | bytes 6635520 | tf_op jit(solution)/shard_map/reduce_scatter | solution.py:840
  166.5 0.8 copy-start.3
  200.2 21.7 %all-to-all-start.2 = ((bf16[4,2,384,128]{3,2,1,0:T(8,128)(2,1)}), bf16[4,2,384,128]{3,2,1,0:T(8,128)(2,1)S(1)}, u32[]{:S(2)}, u32[]{:S(2)}) async-start(bf16[4,2,384,128]{3,2,1,0:T(8,128)(2,1)} %get-tuple-element.87), calls=%async_computation.2 | async-start | bytes 1572864 | tf_op jit(solution)/shard_map/all_to_all | solution.py:791
  203.8 148.3 %reduce-scatter.8.cloned.1.call-start = ((), (), s32[]{:S(2)}) async-start(), calls=%async_computation.8 | async-start | bytes 3932160 | tf_op jit(solution)/shard_map/reduce_scatter | solution.py:852
  212.2 56.3 %collective-permute-start.8 = (bf16[4,2,96,1856]{3,2,1,0:T(8,128)(2,1)}, bf16[4,2,96,1856]{3,2,1,0:T(8,128)(2,1)}, u32[]{:S(2)}, u32[]{:S(2)}) collective-permute-start(bf16[4,2,96,1856]{3,2,1,0:T(8,128)(2,1)} %bitcast.109), channel_id=1, source_target_pairs={{0,4},{4,0},{8,12},{12,8},{16,20},{20,16},{24,28},{28,24},{1,5},{5... | collective-permute-start | bytes 8552456 | tf_op jit(solution)/shard_map/ppermute | solution.py:686
  222.0 0.9 copy-start.5
  222.9 37.3 %copy-start.4 = (bf16[768,768]{0,1:T(8,128)(2,1)S(1)}, bf16[768,768]{0,1:T(8,128)(2,1)}, u32[]{:S(2)}) copy-start(bf16[768,768]{0,1:T(8,128)(2,1)} %maximum_select_fusion) | copy-start | bytes 3538948
  266.4 1.8 copy-start
  266.5 97.6 %reduce-scatter.6.cloned.1.call-start = ((), (), s32[]{:S(2)}) async-start(), calls=%async_computation.7 | async-start | bytes 1843200 | tf_op jit(solution)/shard_map/reduce_scatter | solution.py:873
  268.5 2.8 copy-start.13
  271.1 34.1 %collective-permute-start.9 = (bf16[2,2,96,1856]{3,2,1,0:T(8,128)(2,1)S(1)}, bf16[2,2,96,1856]{3,2,1,0:T(8,128)(2,1)}, u32[]{:S(2)}, u32[]{:S(2)}) collective-permute-start(bf16[2,2,96,1856]{3,2,1,0:T(8,128)(2,1)S(1)} %get-tuple-element.96), channel_id=1, source_target_pairs={{0,8},{4,12},{8,0},{12,4},{16,24},{20,28},{24,16},{28,20},{1,9},{5... | collective-permute-start | bytes 4276232 | tf_op jit(solution)/shard_map/ppermute | solution.py:686
  306.9 17.4 %collective-permute-start.10 = (bf16[1,2,96,1856]{3,2,1,0:T(8,128)(2,1)S(1)}, bf16[1,2,96,1856]{3,2,1,0:T(8,128)(2,1)S(1)}, u32[]{:S(2)}, u32[]{:S(2)}) collective-permute-start(bf16[1,2,96,1856]{3,2,1,0:T(8,128)(2,1)S(1)} %get-tuple-element.101), channel_id=1, source_target_pairs={{0,16},{4,20},{8,24},{12,28},{16,0},{20,4},{24,8},{28,12},{1,17},{... | collective-permute-start | bytes 2138120 | tf_op jit(solution)/shard_map/ppermute | solution.py:686
  309.2 4.9 %collective-permute-start.11 = (f32[1,384]{1,0:T(1,128)S(1)}, f32[1,384]{1,0:T(1,128)S(1)}, u32[]{:S(2)}, u32[]{:S(2)}) collective-permute-start(f32[1,384]{1,0:T(1,128)S(1)} %pad_maximum_fusion.6), channel_id=1, source_target_pairs={{0,1},{1,0},{2,3},{3,2},{4,5},{5,4},{6,7},{7,6},{8,9},{9,8},{10,11... | collective-permute-start | bytes 4616 | tf_op jit(solution)/shard_map/ppermute | solution.py:686
  314.2 4.7 %collective-permute-start.12 = (f32[2,384]{1,0:T(2,128)S(1)}, f32[2,384]{1,0:T(2,128)S(1)}, u32[]{:S(2)}, u32[]{:S(2)}) collective-permute-start(f32[2,384]{1,0:T(2,128)S(1)} %maximum_select_fusion.4), channel_id=1, source_target_pairs={{0,2},{1,3},{2,0},{3,1},{4,6},{5,7},{6,4},{7,5},{8,10},{9,11},{10,... | collective-permute-start | bytes 9224 | tf_op jit(solution)/shard_map/ppermute | solution.py:686
  326.2 2.2 copy-start.1
  329.7 2.1 collective-permute-start.13
  331.9 20.2 %copy-start.2 = (f32[512,768]{1,0:T(8,128)S(1)}, f32[512,768]{1,0:T(8,128)}, u32[]{:S(2)}) copy-start(f32[512,768]{1,0:T(8,128)} %get-tuple-element.105) | copy-start | bytes 4718596
  331.9 9.9 %collective-permute-start.14 = (bf16[2,96,768]{2,1,0:T(8,128)(2,1)S(1)}, bf16[2,96,768]{2,1,0:T(8,128)(2,1)S(1)}, u32[]{:S(2)}, u32[]{:S(2)}) collective-permute-start(bf16[2,96,768]{2,1,0:T(8,128)(2,1)S(1)} %dynamic-slice_bitcast_fusion.1), channel_id=1, source_target_pairs={{0,8},{4,12},{8,0},{12,4},{16,24},{20,28},{24,16},{28,20},{1,9},{5... | collective-permute-start | bytes 884744 | tf_op jit(solution)/shard_map/ppermute | solution.py:686
  342.0 5.6 %collective-permute-start.15 = (bf16[1,96,768]{2,1,0:T(8,128)(2,1)S(1)}, bf16[1,96,768]{2,1,0:T(8,128)(2,1)S(1)}, u32[]{:S(2)}, u32[]{:S(2)}) collective-permute-start(bf16[1,96,768]{2,1,0:T(8,128)(2,1)S(1)} %constant_dynamic-slice_fusion), channel_id=1, source_target_pairs={{0,16},{4,20},{8,24},{12,28},{16,0},{20,4},{24,8},{28,12},{1,17},{... | collective-permute-start | bytes 442376 | tf_op jit(solution)/shard_map/ppermute | solution.py:686
Sparse Core Ops, SparseCore 0:
  9.6 68.1 all-gather.4
  115.6 40.9 all-gather.6
  200.4 62.9 reduce-scatter.3
  266.6 61.3 reduce-scatter.7
  330.2 33.8 reduce-scatter.5

commit v15 on v14

--- a/solution.py
+++ b/solution.py
@@ -345,8 +345,8 @@
     pieces = refs[: len(marks)]
     (
         layer_ref, first_grad_ref, ctx_grad_ref, first_ref, branch_grad_ref, attn_grad_ref,
-        act_out, hidden_grad_out, notes_ref, w_out, w_in, w_up, slope, act_ref, hidden_grad_ref,
-        sums_ref, inner_sums_ref, gathered, sems, out_sems,
+        act_ref, hidden_grad_ref, notes_ref, w_out, w_in, w_up, slope, sums_ref, inner_sums_ref,
+        gathered, sems,
     ) = refs[len(marks) :]
     parts, _, head_cols = w_out.shape
     hidden_cols = w_in.shape[2]
@@ -357,12 +357,6 @@
         (0, hidden_cols, w_in),
         (hidden_cols, hidden_cols, w_up),
     )
-
-    def leave(which, slot):
-        source, target = ((act_ref, act_out), (hidden_grad_ref, hidden_grad_out))[which]
-        return pltpu.make_async_copy(
-            source.at[slot], target.at[place_ref[slot]], out_sems.at[which, slot]
-        )
 
     @pl.when(step == 0)
     def _():
@@ -379,6 +373,12 @@
         sums_ref[...] = jnp.zeros_like(sums_ref)
         inner_sums_ref[...] = jnp.zeros_like(inner_sums_ref)
 
+    def context(t):
+        value = ctx_refs[0][t]
+        for half in range(1, halves):
+            value = jnp.where(step == half, ctx_refs[half][t], value)
+        return value
+
     def arrive(group, slot):
         whole = groups[group][2].at[slot]
 
@@ -395,7 +395,7 @@
     for slot in range(parts):
         arrive(0, slot)
         counts = counts + column_sum(w_out[slot, :, 2 * DH :].astype(F32))
-        attention = attention + dot(jnp.concatenate([unpack(ref[place_ref[slot]]) for ref in ctx_refs], axis=0), w_out[slot, :, : 3 * DH], NT)
+        attention = attention + dot(unpack(context(place_ref[slot])), w_out[slot, :, : 3 * DH], NT)
     first_exact, normed_one, inverse_one = norm_forward(
         in_ref[...].astype(F32) + attention + vec(0), vec(1), vec(2)
     )
@@ -408,8 +408,7 @@
         hidden = dot(first, w_in[slot]) + inner_bias_ref[t]
         bend = 0.5 * (1.0 + lax.erf(hidden * ROOT_HALF))
         activated = (hidden * bend).astype(BF16)
-        act_ref[slot] = activated
-        leave(0, slot).start()
+        act_ref[t] = activated
         slope[slot] = bend + hidden * INV_ROOT_TAU * jnp.exp2(hidden * hidden * (-0.5 * LOG2E))
         arrive(2, slot)
         return branch + dot(activated, w_up[slot], NT)
@@ -436,8 +435,7 @@
     def down(slot, back):
         t = place_ref[slot]
         hidden_grad = (dot(branch_grad, w_up[slot]) * slope[slot]).astype(BF16)
-        hidden_grad_ref[slot] = hidden_grad
-        leave(1, slot).start()
+        hidden_grad_ref[t] = hidden_grad
         inner_sums_ref[t] += column_sum(hidden_grad.astype(F32))
         return back + dot(hidden_grad, w_in[slot], NT)
 
@@ -454,11 +452,9 @@
     middle = BLOCK // 2
     for slot in range(parts):
         back = dot(attn_grad, w_out[slot, :, : 3 * DH]).astype(BF16)
-        for half in range(halves):
-            part = back[half * BLOCK : (half + 1) * BLOCK]
-            ctx_grad_ref[place_ref[slot], half] = pack(
-                part[:, : 2 * DH], part[:middle, 2 * DH :], part[middle:, 2 * DH :]
-            )
+        ctx_grad_ref[place_ref[slot], 0] = pack(
+            back[:, : 2 * DH], back[:middle, 2 * DH :], back[middle:, 2 * DH :]
+        )
 
 
     @pl.when(step == pl.num_programs(0) - 1)
@@ -482,10 +478,6 @@
                 )
         notes_ref[...] = gathered[...].astype(BF16)
 
-    for which in range(2):
-        for slot in range(parts):
-            leave(which, slot).wait()
-
 
 def width_of(ref):
     return ref.shape[-1]
@@ -498,20 +490,26 @@
     out_cols = pieces[0].shape[2] - 2 * hidden_cols
     room = -(-(8 * width + parts * hidden_cols) // (note_rows * 2 * DH)) * 2 * DH
 
+    def by_rows(columns):
+        return pl.BlockSpec((BLOCK, columns), lambda i: (i, 0))
+
+    def by_part(columns):
+        return pl.BlockSpec((parts, BLOCK, columns), lambda i: (0, i, 0))
+
     def fixed(shape):
         return pl.BlockSpec(shape, lambda i: (0,) * len(shape))
 
-    anywhere = pl.BlockSpec(memory_space=pl.ANY)
+    packed_shape = (parts, halves) + ctxs[0].shape[1:]
+    packed = pl.BlockSpec((parts, 1) + packed_shape[2:], lambda i: (0, i, 0, 0))
     low = jax.ShapeDtypeStruct((part_len, width), BF16)
     wide = jax.ShapeDtypeStruct((parts, part_len, hidden_cols), BF16)
-    packed = (parts, halves) + ctxs[0].shape[1:]
-    given = (rows_in, teacher, cotangent, valid, vecs, inner_bias) + tuple(ctxs)
+    smem = pl.BlockSpec(memory_space=pltpu.SMEM)
     return pl.pallas_call(
         functools.partial(dense_chain, marks, halves, total_tokens),
         out_shape=(
             low,
             jax.ShapeDtypeStruct((part_len, width), F32),
-            jax.ShapeDtypeStruct(packed, BF16),
+            jax.ShapeDtypeStruct(packed_shape, BF16),
             low,
             low,
             low,
@@ -519,33 +517,38 @@
             wide,
             jax.ShapeDtypeStruct((note_rows, room), BF16),
         ),
-        grid=(1,),
-        in_specs=[pl.BlockSpec(memory_space=pltpu.SMEM)]
-        + [fixed(value.shape) for value in given]
-        + [anywhere] * len(pieces),
+        grid=(halves,),
+        in_specs=[
+            smem,
+            by_rows(width),
+            by_rows(width),
+            by_rows(width),
+            by_rows(1),
+            fixed(vecs.shape),
+            fixed(inner_bias.shape),
+        ]
+        + [fixed(ctx.shape) for ctx in ctxs]
+        + [pl.BlockSpec(memory_space=pl.ANY)] * len(pieces),
         out_specs=(
-            fixed(low.shape),
-            fixed(low.shape),
-            fixed(packed),
-            fixed(low.shape),
-            fixed(low.shape),
-            fixed(low.shape),
-            anywhere,
-            anywhere,
+            by_rows(width),
+            by_rows(width),
+            packed,
+            by_rows(width),
+            by_rows(width),
+            by_rows(width),
+            by_part(hidden_cols),
+            by_part(hidden_cols),
             fixed((note_rows, room)),
         ),
         scratch_shapes=[
             pltpu.VMEM((parts, width, out_cols), BF16),
             pltpu.VMEM((parts, width, hidden_cols), BF16),
             pltpu.VMEM((parts, width, hidden_cols), BF16),
-            pltpu.VMEM((parts, part_len, hidden_cols), F32),
-            pltpu.VMEM((parts, part_len, hidden_cols), BF16),
-            pltpu.VMEM((parts, part_len, hidden_cols), BF16),
+            pltpu.VMEM((parts, BLOCK, hidden_cols), F32),
             pltpu.VMEM((8, width), F32),
             pltpu.VMEM((parts, 1, hidden_cols), F32),
             pltpu.VMEM((note_rows, room), F32),
             pltpu.SemaphoreType.DMA((3, parts)),
-            pltpu.SemaphoreType.DMA((2, parts)),
         ],
         compiler_params=pltpu.CompilerParams(
             dimension_semantics=("arbitrary",), vmem_limit_bytes=VMEM_LIMIT
@@ -556,7 +559,7 @@
             transcendentals=2 * part_len * hidden_cols * parts,
         ),
         name="dense_chain",
-    )(place, *given, *pieces)
+    )(place, rows_in, teacher, cotangent, valid, vecs, inner_bias, *ctxs, *pieces)
 
 
 def dense_weights(
@@ -796,6 +799,8 @@
             far, contexts[0], bounds = lax.optimization_barrier((far, contexts[0], bounds))
             weights = lax.all_gather(far, "dp", axis=0, tiled=False)
         context, lse = run_forward((halves, half), lane, bounds, qkv, seg_col, seg_row)
+        if half > 0:
+            context, arrived[0] = lax.optimization_barrier((context, arrived[0]))
         contexts.append(context)
         lses.append(lse)
         arrived.append(exchange(context))

time: 385 us -> 372 us (0.966); the launches traced: 378 us -> 369 us
  starting transfers between devices: 26.4 us -> 43 us
  blocking collectives: 16.3 us -> 0 us
  Pallas kernels: 119 us -> 107 us
  waiting for transfers between devices: 134 us -> 138 us
    all_to_all x1 -> x0, blocking collectives: 16.3 us -> none  [exchange(): return lax.all_to_all(packed_blocks, 'tensor', 0, 0)]
    ppermute x16, starting transfers between devices: 18.8 us -> 28.8 us  [swap(): return lax.ppermute(value, axis, [(i, i ^ bit) for i in range(size)])]
    pallas_call x1, Pallas kernels: 37.3 us -> 29.7 us  [run_backward(): pl.pallas_call(functools.partial(attend_backward, halves, len(qkv)), out_...]
    all_to_all x2 -> x3, starting transfers between devices: 6.96 us -> 13.8 us  [exchange(): return lax.all_to_all(packed_blocks, 'tensor', 0, 0)]
    pallas_call x2, Pallas kernels: 37 us -> 30.9 us  [run_forward(): pl.pallas_call(functools.partial(attend_forward, which), out_shape=(jax.S...]
    ppermute x16, waiting for transfers between devices: 105 us -> 110 us  [swap(): return lax.ppermute(value, axis, [(i, i ^ bit) for i in range(size)])]
    all_to_all x2 -> x3, waiting for transfers between devices: 18.1 us -> 21.1 us  [exchange(): return lax.all_to_all(packed_blocks, 'tensor', 0, 0)]
  transfers between devices with their start and end apart: 23 -> 24, of which waited for: 14 -> 16; matrix products, arithmetic and copies ran while one was open for 15% -> 15% of each run, Pallas kernels for 22% -> 19%
where the time goes in v15:
time: 372 us; the launch traced here: 369 us
  waiting for transfers between devices  138 us (37%)
  Pallas kernels  107 us (29%)
  starting transfers between devices  43 us (12%)
  other arithmetic  22.1 us (6%)
  local copies, waits for them, and re-layouts  20.4 us (5%)
  matrix products  19.6 us (5%)
  between operations  18.8 us (5%)
    ppermute x16, waiting for transfers between devices, swap(): return lax.ppermute(value, axis, [(i, i ^ bit) for i in range(size)])  110 us
    pallas_call x2, Pallas kernels, run_forward(): pl.pallas_call(functools.partial(attend_forward, which), out_shape=(jax.S...  30.9 us
    pallas_call x1, Pallas kernels, run_backward(): pl.pallas_call(functools.partial(attend_backward, halves, len(qkv)), out_...  29.7 us
    ppermute x16, starting transfers between devices, swap(): return lax.ppermute(value, axis, [(i, i ^ bit) for i in range(size)])  28.8 us
    pallas_call x1, Pallas kernels, run_dense(): pl.pallas_call(functools.partial(dense_chain, marks, halves, total_tokens...  26.8 us
    all_to_all x3, waiting for transfers between devices, exchange(): return lax.all_to_all(packed_blocks, 'tensor', 0, 0)  21.1 us
    dot_general x3, matrix products, dot(): lax.dot_general(left_side, right_side, dims, preferred_element_type=F32)  19.6 us
    pallas_call x2, Pallas kernels, run_weights(): pl.pallas_call(functools.partial(dense_weights, tuple((turns for _, turns...  16.2 us
  transfers between devices with their start and end apart: 24, of which 16 were waited for; matrix products, arithmetic and copies ran while one was open for 15% of the time, Pallas kernels for 19%

profile of v15, /device:TPU:0, one launch (start us, length us, event | category | flops | bytes accessed | tf_op | source)
XLA Modules:
  0.0 369.0 jit_solution(3399172782331874419)
XLA Ops:
  13.8 2.6 collective-permute-start.3
  16.7 1.6 collective-permute-start
  18.3 7.8 %collective-permute-done.3 = bf16[192,768]{0,1:T(8,128)(2,1)S(1)} collective-permute-done((bf16[192,768]{0,1:T(8,128)(2,1)S(1)}, bf16[192,768]{0,1:T(8,128)(2,1)S(1)}, u32[]{:S(2)}, u32[]{:S(2)}) %collective-permute-start.3) | collective-permute-done | bytes 294944 | tf_op jit(solution)/shard_map/ppermute | solution.py:689
  26.6 1.8 collective-permute-start.4
  28.5 13.8 %collective-permute-done = bf16[1,96,1792]{2,1,0:T(8,128)(2,1)S(1)} collective-permute-done((bf16[1,96,1792]{2,1,0:T(8,128)(2,1)S(1)}, bf16[1,96,1792]{2,1,0:T(8,128)(2,1)S(1)}, u32[]{:S(2)}, u32[]{:S(2)}) %collective-permute-start) | collective-permute-done | bytes 344096 | tf_op jit(solution)/shard_map/ppermute | solution.py:689
  42.4 1.3 maximum_select_fusion
  43.7 12.1 %collective-permute-done.1 = bf16[2,96,1792]{2,1,0:T(8,128)(2,1)} collective-permute-done((bf16[2,96,1792]{2,1,0:T(8,128)(2,1)S(1)}, bf16[2,96,1792]{2,1,0:T(8,128)(2,1)}, u32[]{:S(2)}, u32[]{:S(2)}) %collective-permute-start.1) | collective-permute-done | bytes 688160 | tf_op jit(solution)/shard_map/ppermute | solution.py:689
  55.7 1.2 pad_maximum_fusion.1
  57.0 1.7 collective-permute-start.5
  60.0 1.4 copy.93.refs_1_
  62.2 22.0 %collective-permute-done.5 = bf16[4,96,1792]{2,1,0:T(8,128)(2,1)S(1)} collective-permute-done((bf16[4,96,1792]{2,1,0:T(8,128)(2,1)S(1)}, bf16[4,96,1792]{2,1,0:T(8,128)(2,1)S(1)}, u32[]{:S(2)}, u32[]{:S(2)}) %collective-permute-start.5) | collective-permute-done | bytes 1376288 | tf_op jit(solution)/shard_map/ppermute | solution.py:689
  84.2 5.0 %collective-permute-start.6 = (bf16[2,96,1792]{2,1,0:T(8,128)(2,1)S(1)}, bf16[2,96,1792]{2,1,0:T(8,128)(2,1)}, u32[]{:S(2)}, u32[]{:S(2)}) collective-permute-start(bf16[2,96,1792]{2,1,0:T(8,128)(2,1)S(1)} %pad_maximum_fusion.2), channel_id=1, source_target_pairs={{0,2},{1,3},{2,0},{3,1},{4,6},{5,7},{6,4},{7,5},{8,10},{9,11},{10,... | collective-permute-start | bytes 2064392 | tf_op jit(solution)/shard_map/ppermute | solution.py:689
  89.2 6.5 %add_convert_fusion.refs_0_ = bf16[2048,768]{1,0:T(8,128)(2,1)} fusion(bf16[2048,768]{1,0:T(8,128)(2,1)} %bitcast.107, bf16[768,768]{0,1:T(8,128)(2,1)} %maximum_select_fusion, f32[768]{0:T(1024)S(1)} %add.115), kind=kOutput, calls=%fused_computation | convolution fusion | flops 2419064832 | bytes 7474176 | tf_op jit(solution)/shard_map/dot_general | solution.py:30
  95.7 15.3 %attend_forward.2 = (bf16[4,384,128]{2,1,0:T(8,128)(2,1)}, f32[3,1,1024]{2,1,0:T(1,128)}) custom-call(s32[1]{0:T(128)} %bitcast.lane_ref, s32[8]{0:T(128)} %get-tuple-element.74.low_ref, s32[8]{0:T(128)} %get-tuple-element.75.count_ref, bf16[2048,768]{1,0:T(8,128)(2,1)} %add_convert_fusion.refs_0_, s32[2048,1]{1,0:T(8,128)} %copy.93.refs_1_, s32[1,2048]{1,0:T(1,128)} %refs_2_.5), custom_call_target="tpu_custom_call" | custom-call | flops 12884901888 | bytes 5242880 | tf_op jit(solution)/shard_map/attend_forward/pallas_call | solution.py:259
  111.0 2.6 collective-permute-done.6
  114.8 4.8 %all-to-all-start = ((bf16[4,384,128]{2,1,0:T(8,128)(2,1)}), bf16[4,384,128]{2,1,0:T(8,128)(2,1)S(1)}, u32[]{:S(2)}, u32[]{:S(2)}) async-start(bf16[4,384,128]{2,1,0:T(8,128)(2,1)} %get-tuple-element.92.refs_4_), calls=%async_computation | async-start | bytes 786432 | tf_op jit(solution)/shard_map/all_to_all | solution.py:794
  119.6 15.5 %attend_forward.3 = (bf16[4,384,128]{2,1,0:T(8,128)(2,1)}, f32[3,1,1024]{2,1,0:T(1,128)}) custom-call(s32[1]{0:T(128)} %bitcast.lane_ref, s32[8]{0:T(128)} %get-tuple-element.74.low_ref, s32[8]{0:T(128)} %get-tuple-element.75.count_ref, bf16[2048,768]{1,0:T(8,128)(2,1)} %add_convert_fusion.refs_0_, s32[2048,1]{1,0:T(8,128)} %copy.93.refs_1_, s32[1,2048]{1,0:T(1,128)} %refs_2_.5), custom_call_target="tpu_custom_call" | custom-call | flops 12884901888 | bytes 5242880 | tf_op jit(solution)/shard_map/attend_forward/pallas_call | solution.py:259
  136.5 3.0 collective-permute-start.7
  139.5 4.8 %all-to-all-start.1 = ((bf16[4,384,128]{2,1,0:T(8,128)(2,1)}), bf16[4,384,128]{2,1,0:T(8,128)(2,1)S(1)}, u32[]{:S(2)}, u32[]{:S(2)}) async-start(bf16[4,384,128]{2,1,0:T(8,128)(2,1)} %get-tuple-element.78.refs_5_), calls=%async_computation.1 | async-start | bytes 786432 | tf_op jit(solution)/shard_map/all_to_all | solution.py:794
  147.2 9.0 %all-to-all-done.1.refs_1_ = bf16[4,384,128]{2,1,0:T(8,128)(2,1)S(1)} async-done(((bf16[4,384,128]{2,1,0:T(8,128)(2,1)}), bf16[4,384,128]{2,1,0:T(8,128)(2,1)S(1)}, u32[]{:S(2)}, u32[]{:S(2)}) %all-to-all-start.1) | async-done | bytes 393248 | tf_op jit(solution)/shard_map/all_to_all | solution.py:794
  156.9 26.8 %dense_chain.1 = (bf16[512,768]{1,0:T(8,128)(2,1)}, f32[512,768]{1,0:T(8,128)}, bf16[4,2,384,128]{3,2,1,0:T(8,128)(2,1)}, bf16[512,768]{1,0:T(8,128)(2,1)}, bf16...) custom-call(s32[5]{0:T(128)} %stack.53.place_ref, ...), custom_call_target="tpu_custom_call" | custom-call | flops 22548578304 | bytes 25165824 | tf_op jit(solution)/shard_map/dense_chain/pallas_call | solution.py:507
  183.8 7.9 %dense_weights.3 = bf16[2,768,1856]{2,1,0:T(8,128)(2,1)} custom-call(s32[5]{0:T(128)} %stack.53.place_ref, bf16[512,768]{1,0:T(8,128)(2,1)} %get-tuple-element.83.first_ref, bf16[512,768]{1,0:T(8,128)(2,1)} %get-tuple-element.84.branch_grad_ref, bf16[512,768]{1,0:T(8,128)(2,1)} %get-tuple-element.85.attn_grad_ref, ...), custom_call_target="tpu_custom_call" | custom-call | flops 2919235584 | bytes 10485760 | tf_op jit(solution)/shard_map/dense_weights/pallas_call | solution.py:607
  191.7 4.2 %all-to-all-start.2 = ((bf16[4,2,384,128]{3,2,1,0:T(8,128)(2,1)}), bf16[4,2,384,128]{3,2,1,0:T(8,128)(2,1)S(1)}, u32[]{:S(2)}, u32[]{:S(2)}) async-start(bf16[4,2,384,128]{3,2,1,0:T(8,128)(2,1)} %get-tuple-element.91), calls=%async_computation.2 | async-start | bytes 1572864 | tf_op jit(solution)/shard_map/all_to_all | solution.py:794
  195.9 8.3 %dense_weights.2 = (bf16[8,96,1856]{2,1,0:T(8,128)(2,1)}, bf16[8,96,1856]{2,1,0:T(8,128)(2,1)}) custom-call(s32[5]{0:T(128)} %stack.53.place_ref, bf16[512,768]{1,0:T(8,128)(2,1)} %get-tuple-element.83.first_ref, bf16[512,768]{1,0:T(8,128)(2,1)} %get-tuple-element.84.branch_grad_ref, bf16[512,768]{1,0:T(8,128)(2,1)} %get-tuple-element.85.attn_grad_ref, ...), custom_call_target="tpu_custom_call" | custom-call | flops 2919235584 | bytes 10485760 | tf_op jit(solution)/shard_map/dense_weights/pallas_call | solution.py:607
  204.3 12.1 %all-to-all-done.2 = bf16[4,2,384,128]{3,2,1,0:T(8,128)(2,1)S(1)} async-done(((bf16[4,2,384,128]{3,2,1,0:T(8,128)(2,1)}), bf16[4,2,384,128]{3,2,1,0:T(8,128)(2,1)S(1)}, u32[]{:S(2)}, u32[]{:S(2)}) %all-to-all-start.2) | async-done | bytes 786464 | tf_op jit(solution)/shard_map/all_to_all | solution.py:794
  217.3 29.7 %attend_backward.1 = (bf16[1,2048,768]{2,1,0:T(8,128)(2,1)}, f32[1,768]{1,0:T(1,128)}) custom-call(s32[1]{0:T(128)} %bitcast.lane_ref, s32[8]{0:T(128)} %get-tuple-element.74.low_ref, s32[8]{0:T(128)} %get-tuple-element.75.count_ref, bf16[2048,768]{1,0:T(8,128)(2,1)} %add_convert_fusion.refs_0_, s32[2048,1]{1,0:T(8,128)} %copy.93.refs_1_, ...), custom_call_target="tpu_custom_call" | custom-call | flops 51539607552 | bytes 10485760 | tf_op jit(solution)/shard_map/attend_backward/pallas_call | solution.py:303
  247.1 6.2 %convolution_convert_fusion = bf16[2048,768]{1,0:T(8,128)(2,1)} fusion(bf16[768,768]{0,1:T(8,128)(2,1)S(1)} %copy-done.5, bf16[1,2048,768]{2,1,0:T(8,128)(2,1)} %get-tuple-element.95), kind=kOutput, calls=%fused_computation.1 | convolution fusion | flops 2417491968 | bytes 7471104 | tf_op jit(solution)/shard_map/dot_general | solution.py:30
  253.6 1.5 copy-done
  255.3 2.6 fusion
  257.9 8.7 %collective-permute-start.9 = (bf16[2,2,96,1856]{3,2,1,0:T(8,128)(2,1)S(1)}, bf16[2,2,96,1856]{3,2,1,0:T(8,128)(2,1)}, u32[]{:S(2)}, u32[]{:S(2)}) collective-permute-start(bf16[2,2,96,1856]{3,2,1,0:T(8,128)(2,1)S(1)} %get-tuple-element.100), channel_id=1, source_target_pairs={{0,8},{4,12},{8,0},{12,4},{16,24},{20,28},{24,16},{28,20},{1,9},{5... | collective-permute-start | bytes 4276232 | tf_op jit(solution)/shard_map/ppermute | solution.py:689
  266.7 7.0 %fusion.16 = f32[768,768]{1,0:T(8,128)} fusion(bf16[2048,768]{1,0:T(8,128)(2,1)} %bitcast.108, bf16[2048,768]{1,0:T(8,128)(2,1)} %bitcast.113), kind=kOutput, calls=%fused_computation.84 | convolution fusion | flops 2415919104 | bytes 8650752 | tf_op jit(solution)/shard_map/dot_general | solution.py:30
  273.6 25.4 %collective-permute-done.9 = bf16[2,2,96,1856]{3,2,1,0:T(8,128)(2,1)} collective-permute-done((bf16[2,2,96,1856]{3,2,1,0:T(8,128)(2,1)S(1)}, bf16[2,2,96,1856]{3,2,1,0:T(8,128)(2,1)}, u32[]{:S(2)}, u32[]{:S(2)}) %collective-permute-start.9) | collective-permute-done | bytes 1425440 | tf_op jit(solution)/shard_map/ppermute | solution.py:689
  299.0 1.7 add_convert_fusion.3
  302.0 3.6 collective-permute-done.11
  305.7 4.7 %collective-permute-done.12 = f32[2,384]{1,0:T(2,128)S(1)} collective-permute-done((f32[2,384]{1,0:T(2,128)S(1)}, f32[2,384]{1,0:T(2,128)S(1)}, u32[]{:S(2)}, u32[]{:S(2)}) %collective-permute-start.12) | collective-permute-done | bytes 3104 | tf_op jit(solution)/shard_map/ppermute | solution.py:689
  311.7 8.4 %collective-permute-done.10 = bf16[1,2,96,1856]{3,2,1,0:T(8,128)(2,1)S(1)} collective-permute-done((bf16[1,2,96,1856]{3,2,1,0:T(8,128)(2,1)S(1)}, bf16[1,2,96,1856]{3,2,1,0:T(8,128)(2,1)S(1)}, u32[]{:S(2)}, u32[]{:S(2)}) %collective-permute-start.10) | collective-permute-done | bytes 712736 | tf_op jit(solution)/shard_map/ppermute | solution.py:689
  320.3 1.7 fusion.6
  322.1 1.4 pad_maximum_fusion
  325.6 1.9 collective-permute-done.13
  327.7 2.1 collective-permute-start.14
  332.5 4.6 %collective-permute-done.14 = bf16[2,96,768]{2,1,0:T(8,128)(2,1)S(1)} collective-permute-done((bf16[2,96,768]{2,1,0:T(8,128)(2,1)S(1)}, bf16[2,96,768]{2,1,0:T(8,128)(2,1)S(1)}, u32[]{:S(2)}, u32[]{:S(2)}) %collective-permute-start.14) | collective-permute-done | bytes 294944 | tf_op jit(solution)/shard_map/ppermute | solution.py:689
  339.6 3.2 collective-permute-done.15
  343.5 1.7 finish_heads.1
  347.3 2.4 add_bitcast_fusion
  349.7 5.8 %reduce-scatter.6.cloned.1.call-done = bf16[1,96,1856]{2,1,0:T(8,128)(2,1)} async-done(((bf16[4,96,1856]{2,1,0:T(8,128)(2,1)}), bf16[1,96,1856]{2,1,0:T(8,128)(2,1)}) %reduce-scatter.6.cloned.1.call-update) | async-done | bytes 356368 | tf_op jit(solution)/shard_map/reduce_scatter | solution.py:878
  355.5 1.9 finish_dense.1
  357.4 1.3 slice_bitcast_fusion
  358.7 2.0 slice_bitcast_fusion.1
  (140 shorter events, 27.6 us)
Async XLA Ops:
  7.2 4.3 %copy-start.11 = (s32[1,512]{1,0:T(1,128)S(1)}, s32[1,512]{1,0:T(1,128)}, u32[]{:S(2)}) copy-start(s32[1,512]{1,0:T(1,128)} %param.22) | copy-start | bytes 6148
  7.2 9.2 %copy-start.9 = (bf16[192,96]{1,0:T(8,128)(2,1)S(1)}, bf16[192,96]{1,0:T(8,128)(2,1)}, u32[]{:S(2)}) copy-start(bf16[192,96]{1,0:T(8,128)(2,1)} %param.28) | copy-start | bytes 110596
  7.2 9.3 %copy-start.8 = (bf16[768,96]{0,1:T(8,128)(2,1)S(1)}, bf16[768,96]{0,1:T(8,128)(2,1)}, u32[]{:S(2)}) copy-start(bf16[768,96]{0,1:T(8,128)(2,1)} %param.30) | copy-start | bytes 442372
  7.2 9.3 %copy-start.7 = (bf16[96,768]{1,0:T(8,128)(2,1)S(1)}, bf16[96,768]{1,0:T(8,128)(2,1)}, u32[]{:S(2)}) copy-start(bf16[96,768]{1,0:T(8,128)(2,1)} %param.29) | copy-start | bytes 442372
  7.2 76.9 %all-gather.5.cloned.1.call-start = ((), (), s32[]{:S(2)}) async-start(), calls=%async_computation.9 | async-start | bytes 3932160 | tf_op jit(solution)/shard_map/all_gather | solution.py:752
  8.0 148.6 %all-gather.7.cloned.1.call-start = ((), (), s32[]{:S(2)}) async-start(), calls=%async_computation.10 | async-start | bytes 6193152 | tf_op jit(solution)/shard_map/all_gather | solution.py:800
  11.0 2.4 collective-permute-start.2
  13.8 12.3 %collective-permute-start.3 = (bf16[192,768]{0,1:T(8,128)(2,1)S(1)}, bf16[192,768]{0,1:T(8,128)(2,1)S(1)}, u32[]{:S(2)}, u32[]{:S(2)}) collective-permute-start(bf16[192,768]{0,1:T(8,128)(2,1)S(1)} %maximum_select_fusion.2), channel_id=1, source_target_pairs={{0,8},{4,12},{8,0},{12,4},{16,24},{20,28},{24,16},{28,20},{1,9},{5... | collective-permute-start | bytes 884744 | tf_op jit(solution)/shard_map/ppermute | solution.py:689
  16.7 25.5 %collective-permute-start = (bf16[1,96,1792]{2,1,0:T(8,128)(2,1)S(1)}, bf16[1,96,1792]{2,1,0:T(8,128)(2,1)S(1)}, u32[]{:S(2)}, u32[]{:S(2)}) collective-permute-start(bf16[1,96,1792]{2,1,0:T(8,128)(2,1)S(1)} %bitcast.82), channel_id=1, source_target_pairs={{0,1},{1,0},{2,3},{3,2},{4,5},{5,4},{6,7},{7,6},{8,9},{9,8},{10,11... | collective-permute-start | bytes 1032200 | tf_op jit(solution)/shard_map/ppermute | solution.py:689
  26.6 15.8 %collective-permute-start.4 = (bf16[384,768]{0,1:T(8,128)(2,1)S(1)}, bf16[384,768]{0,1:T(8,128)(2,1)S(1)}, u32[]{:S(2)}, u32[]{:S(2)}) collective-permute-start(bf16[384,768]{0,1:T(8,128)(2,1)S(1)} %maximum_select_fusion.1), channel_id=1, source_target_pairs={{0,16},{4,20},{8,24},{12,28},{16,0},{20,4},{24,8},{28,12},{1,17},{... | collective-permute-start | bytes 1769480 | tf_op jit(solution)/shard_map/ppermute | solution.py:689
  42.3 13.5 %collective-permute-start.1 = (bf16[2,96,1792]{2,1,0:T(8,128)(2,1)S(1)}, bf16[2,96,1792]{2,1,0:T(8,128)(2,1)}, u32[]{:S(2)}, u32[]{:S(2)}) collective-permute-start(bf16[2,96,1792]{2,1,0:T(8,128)(2,1)S(1)} %pad_maximum_fusion.2), channel_id=1, source_target_pairs={{0,8},{4,12},{8,0},{12,4},{16,24},{20,28},{24,16},{28,20},{1,9},{5... | collective-permute-start | bytes 2064392 | tf_op jit(solution)/shard_map/ppermute | solution.py:689
  43.7 15.0 %copy-start.10 = (s32[1,2048]{1,0:T(1,128)S(1)}, s32[1,2048]{1,0:T(1,128)}, u32[]{:S(2)}) copy-start(s32[1,2048]{1,0:T(1,128)} %refs_2_.5) | copy-start | bytes 24580
  57.0 27.2 %collective-permute-start.5 = (bf16[4,96,1792]{2,1,0:T(8,128)(2,1)S(1)}, bf16[4,96,1792]{2,1,0:T(8,128)(2,1)S(1)}, u32[]{:S(2)}, u32[]{:S(2)}) collective-permute-start(bf16[4,96,1792]{2,1,0:T(8,128)(2,1)S(1)} %pad_maximum_fusion.1), channel_id=1, source_target_pairs={{0,16},{4,20},{8,24},{12,28},{16,0},{20,4},{24,8},{28,12},{1,17},{... | collective-permute-start | bytes 4128776 | tf_op jit(solution)/shard_map/ppermute | solution.py:689
  84.2 29.5 %collective-permute-start.6 = (bf16[2,96,1792]{2,1,0:T(8,128)(2,1)S(1)}, bf16[2,96,1792]{2,1,0:T(8,128)(2,1)}, u32[]{:S(2)}, u32[]{:S(2)}) collective-permute-start(bf16[2,96,1792]{2,1,0:T(8,128)(2,1)S(1)} %pad_maximum_fusion.2), channel_id=1, source_target_pairs={{0,2},{1,3},{2,0},{3,1},{4,6},{5,7},{6,4},{7,5},{8,10},{9,11},{10,... | collective-permute-start | bytes 2064392 | tf_op jit(solution)/shard_map/ppermute | solution.py:689
  114.8 20.4 %all-to-all-start = ((bf16[4,384,128]{2,1,0:T(8,128)(2,1)}), bf16[4,384,128]{2,1,0:T(8,128)(2,1)S(1)}, u32[]{:S(2)}, u32[]{:S(2)}) async-start(bf16[4,384,128]{2,1,0:T(8,128)(2,1)} %get-tuple-element.92.refs_4_), calls=%async_computation | async-start | bytes 786432 | tf_op jit(solution)/shard_map/all_to_all | solution.py:794
  135.2 4.3 %copy-start.3 = (bf16[4,384,128]{2,1,0:T(8,128)(2,1)}, bf16[4,384,128]{2,1,0:T(8,128)(2,1)S(1)}, u32[]{:S(2)}) copy-start(bf16[4,384,128]{2,1,0:T(8,128)(2,1)S(1)} %all-to-all-done.refs_0_) | copy-start | bytes 1179652
  135.2 9.1 %copy-start.14 = (bf16[768]{0:T(1024)(128)(2,1)S(1)}, bf16[768]{0:T(1024)(128)(2,1)}, u32[]{:S(2)}) copy-start(bf16[768]{0:T(1024)(128)(2,1)} %param.33) | copy-start | bytes 4612
  135.2 9.1 %copy-start.15 = (bf16[768]{0:T(1024)(128)(2,1)S(1)}, bf16[768]{0:T(1024)(128)(2,1)}, u32[]{:S(2)}) copy-start(bf16[768]{0:T(1024)(128)(2,1)} %param.35) | copy-start | bytes 4612
  135.2 9.1 %copy-start.16 = (bf16[768]{0:T(1024)(128)(2,1)S(1)}, bf16[768]{0:T(1024)(128)(2,1)}, u32[]{:S(2)}) copy-start(bf16[768]{0:T(1024)(128)(2,1)} %param.36) | copy-start | bytes 4612
  135.2 9.2 %copy-start.17 = (bf16[768]{0:T(1024)(128)(2,1)S(1)}, bf16[768]{0:T(1024)(128)(2,1)}, u32[]{:S(2)}) copy-start(bf16[768]{0:T(1024)(128)(2,1)} %param.37) | copy-start | bytes 4612
  135.2 9.2 %copy-start.18 = (bf16[768]{0:T(1024)(128)(2,1)S(1)}, bf16[768]{0:T(1024)(128)(2,1)}, u32[]{:S(2)}) copy-start(bf16[768]{0:T(1024)(128)(2,1)} %param.38) | copy-start | bytes 4612
  135.2 9.2 %copy-start.19 = (bf16[768]{0:T(1024)(128)(2,1)S(1)}, bf16[768]{0:T(1024)(128)(2,1)}, u32[]{:S(2)}) copy-start(bf16[768]{0:T(1024)(128)(2,1)} %param.39) | copy-start | bytes 4612
  135.3 9.9 %copy-start.12 = (bf16[3072]{0:T(1024)(128)(2,1)S(1)}, bf16[3072]{0:T(1024)(128)(2,1)}, u32[]{:S(2)}) copy-start(bf16[3072]{0:T(1024)(128)(2,1)} %param.34) | copy-start | bytes 18436
  136.5 19.7 %collective-permute-start.7 = (bf16[8,96,1792]{2,1,0:T(8,128)(2,1)}, bf16[8,96,1792]{2,1,0:T(8,128)(2,1)}, u32[]{:S(2)}, u32[]{:S(2)}) collective-permute-start(bf16[8,96,1792]{2,1,0:T(8,128)(2,1)} %constant_dynamic-update-slice_fusion.refs_2_), channel_id=1, source_target_pairs={{0,4},{4,0},{8,12},{12,8},{16,20},{20,16},{24,28},{28,24},{1,5},{5... | collective-permute-start | bytes 8257544 | tf_op jit(solution)/shard_map/ppermute | solution.py:689
  139.5 16.7 %all-to-all-start.1 = ((bf16[4,384,128]{2,1,0:T(8,128)(2,1)}), bf16[4,384,128]{2,1,0:T(8,128)(2,1)S(1)}, u32[]{:S(2)}, u32[]{:S(2)}) async-start(bf16[4,384,128]{2,1,0:T(8,128)(2,1)} %get-tuple-element.78.refs_5_), calls=%async_computation.1 | async-start | bytes 786432 | tf_op jit(solution)/shard_map/all_to_all | solution.py:794
  144.3 176.0 %reduce-scatter.4.cloned.1.call-start = ((), (), s32[]{:S(2)}) async-start(), calls=%async_computation.6 | async-start | bytes 6635520 | tf_op jit(solution)/shard_map/reduce_scatter | solution.py:845
  156.2 0.8 copy-start.4
  191.7 24.7 %all-to-all-start.2 = ((bf16[4,2,384,128]{3,2,1,0:T(8,128)(2,1)}), bf16[4,2,384,128]{3,2,1,0:T(8,128)(2,1)S(1)}, u32[]{:S(2)}, u32[]{:S(2)}) async-start(bf16[4,2,384,128]{3,2,1,0:T(8,128)(2,1)} %get-tuple-element.91), calls=%async_computation.2 | async-start | bytes 1572864 | tf_op jit(solution)/shard_map/all_to_all | solution.py:794
  195.9 151.4 %reduce-scatter.8.cloned.1.call-start = ((), (), s32[]{:S(2)}) async-start(), calls=%async_computation.8 | async-start | bytes 3932160 | tf_op jit(solution)/shard_map/reduce_scatter | solution.py:857
  204.2 51.2 %collective-permute-start.8 = (bf16[4,2,96,1856]{3,2,1,0:T(8,128)(2,1)}, bf16[4,2,96,1856]{3,2,1,0:T(8,128)(2,1)}, u32[]{:S(2)}, u32[]{:S(2)}) collective-permute-start(bf16[4,2,96,1856]{3,2,1,0:T(8,128)(2,1)} %bitcast.109), channel_id=1, source_target_pairs={{0,4},{4,0},{8,12},{12,8},{16,20},{20,16},{24,28},{28,24},{1,5},{5... | collective-permute-start | bytes 8552456 | tf_op jit(solution)/shard_map/ppermute | solution.py:689
  216.4 0.9 copy-start.6
  217.3 29.8 %copy-start.5 = (bf16[768,768]{0,1:T(8,128)(2,1)S(1)}, bf16[768,768]{0,1:T(8,128)(2,1)}, u32[]{:S(2)}) copy-start(bf16[768,768]{0,1:T(8,128)(2,1)} %maximum_select_fusion) | copy-start | bytes 3538948
  253.3 1.8 copy-start
  253.3 102.2 %reduce-scatter.6.cloned.1.call-start = ((), (), s32[]{:S(2)}) async-start(), calls=%async_computation.7 | async-start | bytes 1843200 | tf_op jit(solution)/shard_map/reduce_scatter | solution.py:878
  255.3 11.3 %copy-start.13 = (f32[1,768]{1,0:T(1,128)S(1)}, f32[1,768]{1,0:T(1,128)}, u32[]{:S(2)}) copy-start(f32[1,768]{1,0:T(1,128)} %get-tuple-element.112) | copy-start | bytes 9220
  257.9 41.1 %collective-permute-start.9 = (bf16[2,2,96,1856]{3,2,1,0:T(8,128)(2,1)S(1)}, bf16[2,2,96,1856]{3,2,1,0:T(8,128)(2,1)}, u32[]{:S(2)}, u32[]{:S(2)}) collective-permute-start(bf16[2,2,96,1856]{3,2,1,0:T(8,128)(2,1)S(1)} %get-tuple-element.100), channel_id=1, source_target_pairs={{0,8},{4,12},{8,0},{12,4},{16,24},{20,28},{24,16},{28,20},{1,9},{5... | collective-permute-start | bytes 4276232 | tf_op jit(solution)/shard_map/ppermute | solution.py:689
  300.7 19.4 %collective-permute-start.10 = (bf16[1,2,96,1856]{3,2,1,0:T(8,128)(2,1)S(1)}, bf16[1,2,96,1856]{3,2,1,0:T(8,128)(2,1)S(1)}, u32[]{:S(2)}, u32[]{:S(2)}) collective-permute-start(bf16[1,2,96,1856]{3,2,1,0:T(8,128)(2,1)S(1)} %get-tuple-element.105), channel_id=1, source_target_pairs={{0,16},{4,20},{8,24},{12,28},{16,0},{20,4},{24,8},{28,12},{1,17},{... | collective-permute-start | bytes 2138120 | tf_op jit(solution)/shard_map/ppermute | solution.py:689
  301.9 3.7 collective-permute-start.11
  305.7 4.7 %collective-permute-start.12 = (f32[2,384]{1,0:T(2,128)S(1)}, f32[2,384]{1,0:T(2,128)S(1)}, u32[]{:S(2)}, u32[]{:S(2)}) collective-permute-start(f32[2,384]{1,0:T(2,128)S(1)} %maximum_select_fusion.4), channel_id=1, source_target_pairs={{0,2},{1,3},{2,0},{3,1},{4,6},{5,7},{6,4},{7,5},{8,10},{9,11},{10,... | collective-permute-start | bytes 9224 | tf_op jit(solution)/shard_map/ppermute | solution.py:689
  322.1 2.2 copy-start.1
  325.5 2.1 collective-permute-start.13
  327.7 19.6 %copy-start.2 = (f32[512,768]{1,0:T(8,128)S(1)}, f32[512,768]{1,0:T(8,128)}, u32[]{:S(2)}) copy-start(f32[512,768]{1,0:T(8,128)} %get-tuple-element.109) | copy-start | bytes 4718596
  327.7 9.4 %collective-permute-start.14 = (bf16[2,96,768]{2,1,0:T(8,128)(2,1)S(1)}, bf16[2,96,768]{2,1,0:T(8,128)(2,1)S(1)}, u32[]{:S(2)}, u32[]{:S(2)}) collective-permute-start(bf16[2,96,768]{2,1,0:T(8,128)(2,1)S(1)} %dynamic-slice_bitcast_fusion.1), channel_id=1, source_target_pairs={{0,8},{4,12},{8,0},{12,4},{16,24},{20,28},{24,16},{28,20},{1,9},{5... | collective-permute-start | bytes 884744 | tf_op jit(solution)/shard_map/ppermute | solution.py:689
  337.2 5.5 %collective-permute-start.15 = (bf16[1,96,768]{2,1,0:T(8,128)(2,1)S(1)}, bf16[1,96,768]{2,1,0:T(8,128)(2,1)S(1)}, u32[]{:S(2)}, u32[]{:S(2)}) collective-permute-start(bf16[1,96,768]{2,1,0:T(8,128)(2,1)S(1)} %constant_dynamic-slice_fusion), channel_id=1, source_target_pairs={{0,16},{4,20},{8,24},{12,28},{16,0},{20,4},{24,8},{28,12},{1,17},{... | collective-permute-start | bytes 442376 | tf_op jit(solution)/shard_map/ppermute | solution.py:689
Sparse Core Ops, SparseCore 0:
  9.6 68.1 all-gather.4
  113.8 42.7 all-gather.6
  191.8 63.3 reduce-scatter.3
  257.4 62.0 reduce-scatter.7
  323.6 31.8 reduce-scatter.5

commit v16 on v15

--- a/solution.py
+++ b/solution.py
@@ -281,7 +281,7 @@
             ],
         ),
         compiler_params=pltpu.CompilerParams(
-            dimension_semantics=("arbitrary",), vmem_limit_bytes=VMEM_LIMIT
+            dimension_semantics=("arbitrary",), vmem_limit_bytes=28 << 20
         ),
         cost_estimate=pl.CostEstimate(
             flops=heads * seq_len * seq_len * 2048 * steps // blocks,
@@ -326,7 +326,7 @@
             ],
         ),
         compiler_params=pltpu.CompilerParams(
-            dimension_semantics=("arbitrary",), vmem_limit_bytes=VMEM_LIMIT
+            dimension_semantics=("arbitrary",), vmem_limit_bytes=28 << 20
         ),
         cost_estimate=pl.CostEstimate(
             flops=heads * seq_len * seq_len * 4096,

time: 372 us -> 370 us (level)
  starting transfers between devices: 43 us -> 28.7 us
  waiting for transfers between devices: 138 us -> 145 us
  local copies, waits for them, and re-layouts: 20.4 us -> 26.3 us
    ppermute x16, starting transfers between devices: 28.8 us -> 15.2 us  [swap(): return lax.ppermute(value, axis, [(i, i ^ bit) for i in range(size)])]
    ppermute x16, waiting for transfers between devices: 110 us -> 117 us  [swap(): return lax.ppermute(value, axis, [(i, i ^ bit) for i in range(size)])]
    unnamed x46 -> x48, local copies, waits for them, and re-layouts: 7.76 us -> 11.3 us
  transfers between devices with their start and end apart: 24 -> 24, of which waited for: 16 -> 15; matrix products, arithmetic and copies ran while one was open for 15% -> 15% of each run, Pallas kernels for 19% -> 20%
where the time goes in v16:
time: 370 us; the launch traced here: 368 us
  waiting for transfers between devices  145 us (39%)
  Pallas kernels  110 us (30%)
  starting transfers between devices  28.7 us (8%)
  local copies, waits for them, and re-layouts  26.3 us (7%)
  other arithmetic  22.8 us (6%)
  between operations  18.8 us (5%)
  matrix products  16.3 us (4%)
    ppermute x16, waiting for transfers between devices, swap(): return lax.ppermute(value, axis, [(i, i ^ bit) for i in range(size)])  117 us
    pallas_call x1, Pallas kernels, run_backward(): pl.pallas_call(functools.partial(attend_backward, halves, len(qkv)), out_...  32.7 us
    pallas_call x2, Pallas kernels, run_forward(): pl.pallas_call(functools.partial(attend_forward, which), out_shape=(jax.S...  30.8 us
    pallas_call x1, Pallas kernels, run_dense(): pl.pallas_call(functools.partial(dense_chain, marks, halves, total_tokens...  26.8 us
    all_to_all x3, waiting for transfers between devices, exchange(): return lax.all_to_all(packed_blocks, 'tensor', 0, 0)  20 us
    dot_general x3, matrix products, dot(): lax.dot_general(left_side, right_side, dims, preferred_element_type=F32)  16.3 us
    pallas_call x2, Pallas kernels, run_weights(): pl.pallas_call(functools.partial(dense_weights, tuple((turns for _, turns...  16.2 us
    ppermute x16, starting transfers between devices, swap(): return lax.ppermute(value, axis, [(i, i ^ bit) for i in range(size)])  15.2 us
  transfers between devices with their start and end apart: 24, of which 15 were waited for; matrix products, arithmetic and copies ran while one was open for 15% of the time, Pallas kernels for 20%

profile of v16, /device:TPU:0, one launch (start us, length us, event | category | flops | bytes accessed | tf_op | source)
XLA Modules:
  0.0 368.2 jit_solution(17367213537914433592)
XLA Ops:
  13.8 2.6 collective-permute-start.3
  16.7 1.6 collective-permute-start
  18.3 7.8 %collective-permute-done.3 = bf16[192,768]{0,1:T(8,128)(2,1)S(1)} collective-permute-done((bf16[192,768]{0,1:T(8,128)(2,1)S(1)}, bf16[192,768]{0,1:T(8,128)(2,1)S(1)}, u32[]{:S(2)}, u32[]{:S(2)}) %collective-permute-start.3) | collective-permute-done | bytes 294944 | tf_op jit(solution)/shard_map/ppermute | solution.py:689
  26.6 1.8 collective-permute-start.4
  28.5 13.8 %collective-permute-done = bf16[1,96,1792]{2,1,0:T(8,128)(2,1)S(1)} collective-permute-done((bf16[1,96,1792]{2,1,0:T(8,128)(2,1)S(1)}, bf16[1,96,1792]{2,1,0:T(8,128)(2,1)S(1)}, u32[]{:S(2)}, u32[]{:S(2)}) %collective-permute-start) | collective-permute-done | bytes 344096 | tf_op jit(solution)/shard_map/ppermute | solution.py:689
  42.4 1.3 maximum_select_fusion
  43.7 12.1 %collective-permute-done.1 = bf16[2,96,1792]{2,1,0:T(8,128)(2,1)} collective-permute-done((bf16[2,96,1792]{2,1,0:T(8,128)(2,1)S(1)}, bf16[2,96,1792]{2,1,0:T(8,128)(2,1)}, u32[]{:S(2)}, u32[]{:S(2)}) %collective-permute-start.1) | collective-permute-done | bytes 688160 | tf_op jit(solution)/shard_map/ppermute | solution.py:689
  55.7 1.2 pad_maximum_fusion.1
  57.0 1.7 collective-permute-start.5
  60.7 23.6 %collective-permute-done.5 = bf16[4,96,1792]{2,1,0:T(8,128)(2,1)} collective-permute-done((bf16[4,96,1792]{2,1,0:T(8,128)(2,1)S(1)}, bf16[4,96,1792]{2,1,0:T(8,128)(2,1)}, u32[]{:S(2)}, u32[]{:S(2)}) %collective-permute-start.5) | collective-permute-done | bytes 1376288 | tf_op jit(solution)/shard_map/ppermute | solution.py:689
  84.3 5.0 %collective-permute-start.6 = (bf16[2,96,1792]{2,1,0:T(8,128)(2,1)S(1)}, bf16[2,96,1792]{2,1,0:T(8,128)(2,1)}, u32[]{:S(2)}, u32[]{:S(2)}) collective-permute-start(bf16[2,96,1792]{2,1,0:T(8,128)(2,1)S(1)} %pad_maximum_fusion.2), channel_id=1, source_target_pairs={{0,2},{1,3},{2,0},{3,1},{4,6},{5,7},{6,4},{7,5},{8,10},{9,11},{10,... | collective-permute-start | bytes 2064392 | tf_op jit(solution)/shard_map/ppermute | solution.py:689
  89.3 4.9 %add_convert_fusion.refs_0_ = bf16[2048,768]{1,0:T(8,128)(2,1)S(1)} fusion(bf16[2048,768]{1,0:T(8,128)(2,1)} %bitcast.108, bf16[768,768]{0,1:T(8,128)(2,1)} %maximum_select_fusion, f32[768]{0:T(1024)S(1)} %add.115), kind=kOutput, calls=%fused_computation | convolution fusion | flops 2419064832 | bytes 7474176 | tf_op jit(solution)/shard_map/dot_general | solution.py:30
  94.2 14.4 %attend_forward.2 = (bf16[4,384,128]{2,1,0:T(8,128)(2,1)}, f32[3,1,1024]{2,1,0:T(1,128)S(1)}) custom-call(s32[1]{0:T(128)} %bitcast.lane_ref, s32[8]{0:T(128)S(1)} %get-tuple-element.74.low_ref, s32[8]{0:T(128)S(1)} %get-tuple-element.75.count_ref, bf16[2048,768]{1,0:T(8,128)(2,1)S(1)} %add_convert_fusion.refs_0_, s32[2048,1]{1,0:T(8,128)S(1)} %copy.93.refs_1_, ...), custom_call_target="tpu_custom_call" | custom-call | flops 12884901888 | bytes 5242880 | tf_op jit(solution)/shard_map/attend_forward/pallas_call | solution.py:259
  108.6 5.1 %collective-permute-done.6 = bf16[2,96,1792]{2,1,0:T(8,128)(2,1)} collective-permute-done((bf16[2,96,1792]{2,1,0:T(8,128)(2,1)S(1)}, bf16[2,96,1792]{2,1,0:T(8,128)(2,1)}, u32[]{:S(2)}, u32[]{:S(2)}) %collective-permute-start.6) | collective-permute-done | bytes 688160 | tf_op jit(solution)/shard_map/ppermute | solution.py:689
  114.9 4.8 %all-to-all-start = ((bf16[4,384,128]{2,1,0:T(8,128)(2,1)}), bf16[4,384,128]{2,1,0:T(8,128)(2,1)S(1)}, u32[]{:S(2)}, u32[]{:S(2)}) async-start(bf16[4,384,128]{2,1,0:T(8,128)(2,1)} %get-tuple-element.92.refs_4_), calls=%async_computation | async-start | bytes 786432 | tf_op jit(solution)/shard_map/all_to_all | solution.py:794
  119.7 2.1 copy-done.3
  121.8 16.4 %attend_forward.3 = (bf16[4,384,128]{2,1,0:T(8,128)(2,1)}, f32[3,1,1024]{2,1,0:T(1,128)S(1)}) custom-call(s32[1]{0:T(128)} %bitcast.lane_ref, s32[8]{0:T(128)S(1)} %get-tuple-element.74.low_ref, s32[8]{0:T(128)S(1)} %get-tuple-element.75.count_ref, bf16[2048,768]{1,0:T(8,128)(2,1)S(1)} %copy-done.3, s32[2048,1]{1,0:T(8,128)S(1)} %copy.93.refs_1_, ...), custom_call_target="tpu_custom_call" | custom-call | flops 12884901888 | bytes 5242880 | tf_op jit(solution)/shard_map/attend_forward/pallas_call | solution.py:259
  138.4 2.7 constant_dynamic-update-slice_fusion.refs_2_
  141.9 4.8 %all-to-all-start.1 = ((bf16[4,384,128]{2,1,0:T(8,128)(2,1)}), bf16[4,384,128]{2,1,0:T(8,128)(2,1)S(1)}, u32[]{:S(2)}, u32[]{:S(2)}) async-start(bf16[4,384,128]{2,1,0:T(8,128)(2,1)} %get-tuple-element.78.refs_5_), calls=%async_computation.1 | async-start | bytes 786432 | tf_op jit(solution)/shard_map/all_to_all | solution.py:794
  149.5 9.0 %all-to-all-done.1.refs_1_ = bf16[4,384,128]{2,1,0:T(8,128)(2,1)S(1)} async-done(((bf16[4,384,128]{2,1,0:T(8,128)(2,1)}), bf16[4,384,128]{2,1,0:T(8,128)(2,1)S(1)}, u32[]{:S(2)}, u32[]{:S(2)}) %all-to-all-start.1) | async-done | bytes 393248 | tf_op jit(solution)/shard_map/all_to_all | solution.py:794
  159.3 26.8 %dense_chain.1 = (bf16[512,768]{1,0:T(8,128)(2,1)}, f32[512,768]{1,0:T(8,128)}, bf16[4,2,384,128]{3,2,1,0:T(8,128)(2,1)}, bf16[512,768]{1,0:T(8,128)(2,1)}, bf16...) custom-call(s32[5]{0:T(128)} %stack.53.place_ref, ...), custom_call_target="tpu_custom_call" | custom-call | flops 22548578304 | bytes 25165824 | tf_op jit(solution)/shard_map/dense_chain/pallas_call | solution.py:507
  186.1 7.9 %dense_weights.3 = bf16[2,768,1856]{2,1,0:T(8,128)(2,1)} custom-call(s32[5]{0:T(128)} %stack.53.place_ref, bf16[512,768]{1,0:T(8,128)(2,1)} %get-tuple-element.83.first_ref, bf16[512,768]{1,0:T(8,128)(2,1)} %get-tuple-element.84.branch_grad_ref, bf16[512,768]{1,0:T(8,128)(2,1)} %get-tuple-element.85.attn_grad_ref, ...), custom_call_target="tpu_custom_call" | custom-call | flops 2919235584 | bytes 10485760 | tf_op jit(solution)/shard_map/dense_weights/pallas_call | solution.py:607
  194.0 3.5 all-to-all-start.2
  197.8 8.3 %dense_weights.2 = (bf16[8,96,1856]{2,1,0:T(8,128)(2,1)}, bf16[8,96,1856]{2,1,0:T(8,128)(2,1)}) custom-call(s32[5]{0:T(128)} %stack.53.place_ref, bf16[512,768]{1,0:T(8,128)(2,1)} %get-tuple-element.83.first_ref, bf16[512,768]{1,0:T(8,128)(2,1)} %get-tuple-element.84.branch_grad_ref, bf16[512,768]{1,0:T(8,128)(2,1)} %get-tuple-element.85.attn_grad_ref, ...), custom_call_target="tpu_custom_call" | custom-call | flops 2919235584 | bytes 10485760 | tf_op jit(solution)/shard_map/dense_weights/pallas_call | solution.py:607
  206.2 11.0 %all-to-all-done.2 = bf16[4,2,384,128]{3,2,1,0:T(8,128)(2,1)S(1)} async-done(((bf16[4,2,384,128]{3,2,1,0:T(8,128)(2,1)}), bf16[4,2,384,128]{3,2,1,0:T(8,128)(2,1)S(1)}, u32[]{:S(2)}, u32[]{:S(2)}) %all-to-all-start.2) | async-done | bytes 786464 | tf_op jit(solution)/shard_map/all_to_all | solution.py:794
  217.2 1.9 copy-done.4
  219.1 32.7 %attend_backward.1 = (bf16[1,2048,768]{2,1,0:T(8,128)(2,1)S(1)}, f32[1,768]{1,0:T(1,128)S(1)}) custom-call(s32[1]{0:T(128)} %bitcast.lane_ref, s32[8]{0:T(128)S(1)} %get-tuple-element.74.low_ref, s32[8]{0:T(128)S(1)} %get-tuple-element.75.count_ref, bf16[2048,768]{1,0:T(8,128)(2,1)S(1)} %copy-done.4, s32[2048,1]{1,0:T(8,128)S(1)} %copy.93.refs_1_, ...), custom_call_target="tpu_custom_call" | custom-call | flops 51539607552 | bytes 10485760 | tf_op jit(solution)/shard_map/attend_backward/pallas_call | solution.py:303
  251.8 1.6 copy-done.1
  253.5 4.0 %convolution_convert_fusion = bf16[2048,768]{1,0:T(8,128)(2,1)} fusion(bf16[768,768]{0,1:T(8,128)(2,1)S(1)} %copy-done.9, bf16[1,2048,768]{2,1,0:T(8,128)(2,1)S(1)} %get-tuple-element.95), kind=kOutput, calls=%fused_computation.1 | convolution fusion | flops 2417491968 | bytes 7471104 | tf_op jit(solution)/shard_map/dot_general | solution.py:30
  257.5 2.0 fusion.13
  259.5 3.8 %fusion = (bf16[2,2,96,1856]{3,2,1,0:T(8,128)(2,1)}, bf16[2,2,96,1856]{3,2,1,0:T(8,128)(2,1)S(1)}) fusion(bf16[2,2,96,1856]{3,2,1,0:T(8,128)(2,1)S(1)} %bitcast.84, bf16[4,2,96,1856]{3,2,1,0:T(8,128)(2,1)} %collective-permute-done.8, bf16[2,2,96,1856]{3,2,1,0:T(8,128)(2,1)S(1)} %bitcast.85), kind=kLoop, calls=%fused_computation.3 | loop fusion | flops 5701632 | bytes 8552448 | tf_op jit(solution)/shard_map/convert_element_type | solution.py:711
  263.4 7.5 %fusion.16 = f32[768,768]{1,0:T(8,128)} fusion(bf16[2048,768]{1,0:T(8,128)(2,1)} %bitcast.109, bf16[2048,768]{1,0:T(8,128)(2,1)} %bitcast.83), kind=kOutput, calls=%fused_computation.84 | convolution fusion | flops 2415919104 | bytes 8650752 | tf_op jit(solution)/shard_map/dot_general | solution.py:30
  270.9 27.4 %collective-permute-done.9 = bf16[2,2,96,1856]{3,2,1,0:T(8,128)(2,1)} collective-permute-done((bf16[2,2,96,1856]{3,2,1,0:T(8,128)(2,1)}, bf16[2,2,96,1856]{3,2,1,0:T(8,128)(2,1)}, u32[]{:S(2)}, u32[]{:S(2)}) %collective-permute-start.9) | collective-permute-done | bytes 1425440 | tf_op jit(solution)/shard_map/ppermute | solution.py:689
  298.3 1.7 add_convert_fusion.3
  300.4 4.3 %collective-permute-done.11 = f32[1,384]{1,0:T(1,128)S(1)} collective-permute-done((f32[1,384]{1,0:T(1,128)S(1)}, f32[1,384]{1,0:T(1,128)S(1)}, u32[]{:S(2)}, u32[]{:S(2)}) %collective-permute-start.11) | collective-permute-done | bytes 1568 | tf_op jit(solution)/shard_map/ppermute | solution.py:689
  304.8 4.7 %collective-permute-done.12 = f32[2,384]{1,0:T(2,128)S(1)} collective-permute-done((f32[2,384]{1,0:T(2,128)S(1)}, f32[2,384]{1,0:T(2,128)S(1)}, u32[]{:S(2)}, u32[]{:S(2)}) %collective-permute-start.12) | collective-permute-done | bytes 3104 | tf_op jit(solution)/shard_map/ppermute | solution.py:689
  310.7 7.4 %collective-permute-done.10 = bf16[1,2,96,1856]{3,2,1,0:T(8,128)(2,1)S(1)} collective-permute-done((bf16[1,2,96,1856]{3,2,1,0:T(8,128)(2,1)S(1)}, bf16[1,2,96,1856]{3,2,1,0:T(8,128)(2,1)S(1)}, u32[]{:S(2)}, u32[]{:S(2)}) %collective-permute-start.10) | collective-permute-done | bytes 712736 | tf_op jit(solution)/shard_map/ppermute | solution.py:689
  318.3 1.8 fusion.6
  320.1 1.4 pad_maximum_fusion
  323.6 2.0 collective-permute-done.13
  329.1 5.8 %collective-permute-done.14 = bf16[2,96,768]{2,1,0:T(8,128)(2,1)S(1)} collective-permute-done((bf16[2,96,768]{2,1,0:T(8,128)(2,1)S(1)}, bf16[2,96,768]{2,1,0:T(8,128)(2,1)S(1)}, u32[]{:S(2)}, u32[]{:S(2)}) %collective-permute-start.14) | collective-permute-done | bytes 294944 | tf_op jit(solution)/shard_map/ppermute | solution.py:689
  337.3 2.9 collective-permute-done.15
  340.9 1.7 finish_heads.1
  344.7 2.4 add_bitcast_fusion
  347.2 7.5 %reduce-scatter.6.cloned.1.call-done = bf16[1,96,1856]{2,1,0:T(8,128)(2,1)} async-done(((bf16[4,96,1856]{2,1,0:T(8,128)(2,1)}), bf16[1,96,1856]{2,1,0:T(8,128)(2,1)}) %reduce-scatter.6.cloned.1.call-update) | async-done | bytes 356368 | tf_op jit(solution)/shard_map/reduce_scatter | solution.py:878
  354.7 1.9 finish_dense.1
  356.5 1.3 slice_bitcast_fusion
  357.9 2.0 slice_bitcast_fusion.1
  (142 shorter events, 25.5 us)
Async XLA Ops:
  7.2 4.3 %copy-start.13 = (s32[1,512]{1,0:T(1,128)S(1)}, s32[1,512]{1,0:T(1,128)}, u32[]{:S(2)}) copy-start(s32[1,512]{1,0:T(1,128)} %param.22) | copy-start | bytes 6148
  7.2 9.2 %copy-start.12 = (bf16[192,96]{1,0:T(8,128)(2,1)S(1)}, bf16[192,96]{1,0:T(8,128)(2,1)}, u32[]{:S(2)}) copy-start(bf16[192,96]{1,0:T(8,128)(2,1)} %param.28) | copy-start | bytes 110596
  7.2 9.3 %copy-start.11 = (bf16[768,96]{0,1:T(8,128)(2,1)S(1)}, bf16[768,96]{0,1:T(8,128)(2,1)}, u32[]{:S(2)}) copy-start(bf16[768,96]{0,1:T(8,128)(2,1)} %param.30) | copy-start | bytes 442372
  7.2 9.3 %copy-start.10 = (bf16[96,768]{1,0:T(8,128)(2,1)S(1)}, bf16[96,768]{1,0:T(8,128)(2,1)}, u32[]{:S(2)}) copy-start(bf16[96,768]{1,0:T(8,128)(2,1)} %param.29) | copy-start | bytes 442372
  7.2 77.0 %all-gather.5.cloned.1.call-start = ((), (), s32[]{:S(2)}) async-start(), calls=%async_computation.9 | async-start | bytes 3932160 | tf_op jit(solution)/shard_map/all_gather | solution.py:752
  8.0 150.6 %all-gather.7.cloned.1.call-start = ((), (), s32[]{:S(2)}) async-start(), calls=%async_computation.10 | async-start | bytes 6193152 | tf_op jit(solution)/shard_map/all_gather | solution.py:800
  11.0 2.4 collective-permute-start.2
  13.8 12.3 %collective-permute-start.3 = (bf16[192,768]{0,1:T(8,128)(2,1)S(1)}, bf16[192,768]{0,1:T(8,128)(2,1)S(1)}, u32[]{:S(2)}, u32[]{:S(2)}) collective-permute-start(bf16[192,768]{0,1:T(8,128)(2,1)S(1)} %maximum_select_fusion.2), channel_id=1, source_target_pairs={{0,8},{4,12},{8,0},{12,4},{16,24},{20,28},{24,16},{28,20},{1,9},{5... | collective-permute-start | bytes 884744 | tf_op jit(solution)/shard_map/ppermute | solution.py:689
  16.7 25.6 %collective-permute-start = (bf16[1,96,1792]{2,1,0:T(8,128)(2,1)S(1)}, bf16[1,96,1792]{2,1,0:T(8,128)(2,1)S(1)}, u32[]{:S(2)}, u32[]{:S(2)}) collective-permute-start(bf16[1,96,1792]{2,1,0:T(8,128)(2,1)S(1)} %bitcast.88), channel_id=1, source_target_pairs={{0,1},{1,0},{2,3},{3,2},{4,5},{5,4},{6,7},{7,6},{8,9},{9,8},{10,11... | collective-permute-start | bytes 1032200 | tf_op jit(solution)/shard_map/ppermute | solution.py:689
  26.6 15.8 %collective-permute-start.4 = (bf16[384,768]{0,1:T(8,128)(2,1)S(1)}, bf16[384,768]{0,1:T(8,128)(2,1)S(1)}, u32[]{:S(2)}, u32[]{:S(2)}) collective-permute-start(bf16[384,768]{0,1:T(8,128)(2,1)S(1)} %maximum_select_fusion.1), channel_id=1, source_target_pairs={{0,16},{4,20},{8,24},{12,28},{16,0},{20,4},{24,8},{28,12},{1,17},{... | collective-permute-start | bytes 1769480 | tf_op jit(solution)/shard_map/ppermute | solution.py:689
  42.3 13.5 %collective-permute-start.1 = (bf16[2,96,1792]{2,1,0:T(8,128)(2,1)S(1)}, bf16[2,96,1792]{2,1,0:T(8,128)(2,1)}, u32[]{:S(2)}, u32[]{:S(2)}) collective-permute-start(bf16[2,96,1792]{2,1,0:T(8,128)(2,1)S(1)} %pad_maximum_fusion.2), channel_id=1, source_target_pairs={{0,8},{4,12},{8,0},{12,4},{16,24},{20,28},{24,16},{28,20},{1,9},{5... | collective-permute-start | bytes 2064392 | tf_op jit(solution)/shard_map/ppermute | solution.py:689
  43.7 15.0 %copy-start = (s32[1,2048]{1,0:T(1,128)S(1)}, s32[1,2048]{1,0:T(1,128)}, u32[]{:S(2)}) copy-start(s32[1,2048]{1,0:T(1,128)} %refs_2_.5) | copy-start | bytes 24580
  57.0 27.3 %collective-permute-start.5 = (bf16[4,96,1792]{2,1,0:T(8,128)(2,1)S(1)}, bf16[4,96,1792]{2,1,0:T(8,128)(2,1)}, u32[]{:S(2)}, u32[]{:S(2)}) collective-permute-start(bf16[4,96,1792]{2,1,0:T(8,128)(2,1)S(1)} %pad_maximum_fusion.1), channel_id=1, source_target_pairs={{0,16},{4,20},{8,24},{12,28},{16,0},{20,4},{24,8},{28,12},{1,17},{... | collective-permute-start | bytes 4128776 | tf_op jit(solution)/shard_map/ppermute | solution.py:689
  84.3 29.5 %collective-permute-start.6 = (bf16[2,96,1792]{2,1,0:T(8,128)(2,1)S(1)}, bf16[2,96,1792]{2,1,0:T(8,128)(2,1)}, u32[]{:S(2)}, u32[]{:S(2)}) collective-permute-start(bf16[2,96,1792]{2,1,0:T(8,128)(2,1)S(1)} %pad_maximum_fusion.2), channel_id=1, source_target_pairs={{0,2},{1,3},{2,0},{3,1},{4,6},{5,7},{6,4},{7,5},{8,10},{9,11},{10,... | collective-permute-start | bytes 2064392 | tf_op jit(solution)/shard_map/ppermute | solution.py:689
  94.1 14.5 %copy-start.2 = (bf16[2048,768]{1,0:T(8,128)(2,1)}, bf16[2048,768]{1,0:T(8,128)(2,1)S(1)}, u32[]{:S(2)}) copy-start(bf16[2048,768]{1,0:T(8,128)(2,1)S(1)} %add_convert_fusion.refs_0_) | copy-start | bytes 9437188
  114.9 23.3 %all-to-all-start = ((bf16[4,384,128]{2,1,0:T(8,128)(2,1)}), bf16[4,384,128]{2,1,0:T(8,128)(2,1)S(1)}, u32[]{:S(2)}, u32[]{:S(2)}) async-start(bf16[4,384,128]{2,1,0:T(8,128)(2,1)} %get-tuple-element.92.refs_4_), calls=%async_computation | async-start | bytes 786432 | tf_op jit(solution)/shard_map/all_to_all | solution.py:794
  119.7 2.1 copy-start.3
  138.3 3.6 copy-start.7
  138.3 8.4 %copy-start.15 = (bf16[768]{0:T(1024)(128)(2,1)S(1)}, bf16[768]{0:T(1024)(128)(2,1)}, u32[]{:S(2)}) copy-start(bf16[768]{0:T(1024)(128)(2,1)} %param.33) | copy-start | bytes 4612
  138.3 8.4 %copy-start.16 = (bf16[768]{0:T(1024)(128)(2,1)S(1)}, bf16[768]{0:T(1024)(128)(2,1)}, u32[]{:S(2)}) copy-start(bf16[768]{0:T(1024)(128)(2,1)} %param.35) | copy-start | bytes 4612
  138.3 8.4 %copy-start.17 = (bf16[768]{0:T(1024)(128)(2,1)S(1)}, bf16[768]{0:T(1024)(128)(2,1)}, u32[]{:S(2)}) copy-start(bf16[768]{0:T(1024)(128)(2,1)} %param.36) | copy-start | bytes 4612
  138.3 8.4 %copy-start.18 = (bf16[768]{0:T(1024)(128)(2,1)S(1)}, bf16[768]{0:T(1024)(128)(2,1)}, u32[]{:S(2)}) copy-start(bf16[768]{0:T(1024)(128)(2,1)} %param.37) | copy-start | bytes 4612
  138.3 8.4 %copy-start.19 = (bf16[768]{0:T(1024)(128)(2,1)S(1)}, bf16[768]{0:T(1024)(128)(2,1)}, u32[]{:S(2)}) copy-start(bf16[768]{0:T(1024)(128)(2,1)} %param.38) | copy-start | bytes 4612
  138.3 8.5 %copy-start.20 = (bf16[768]{0:T(1024)(128)(2,1)S(1)}, bf16[768]{0:T(1024)(128)(2,1)}, u32[]{:S(2)}) copy-start(bf16[768]{0:T(1024)(128)(2,1)} %param.39) | copy-start | bytes 4612
  138.3 9.1 %copy-start.14 = (bf16[3072]{0:T(1024)(128)(2,1)S(1)}, bf16[3072]{0:T(1024)(128)(2,1)}, u32[]{:S(2)}) copy-start(bf16[3072]{0:T(1024)(128)(2,1)} %param.34) | copy-start | bytes 18436
  141.0 17.5 %collective-permute-start.7 = (bf16[8,96,1792]{2,1,0:T(8,128)(2,1)}, bf16[8,96,1792]{2,1,0:T(8,128)(2,1)}, u32[]{:S(2)}, u32[]{:S(2)}) collective-permute-start(bf16[8,96,1792]{2,1,0:T(8,128)(2,1)} %constant_dynamic-update-slice_fusion.refs_2_), channel_id=1, source_target_pairs={{0,4},{4,0},{8,12},{12,8},{16,20},{20,16},{24,28},{28,24},{1,5},{5... | collective-permute-start | bytes 8257544 | tf_op jit(solution)/shard_map/ppermute | solution.py:689
  141.9 16.6 %all-to-all-start.1 = ((bf16[4,384,128]{2,1,0:T(8,128)(2,1)}), bf16[4,384,128]{2,1,0:T(8,128)(2,1)S(1)}, u32[]{:S(2)}, u32[]{:S(2)}) async-start(bf16[4,384,128]{2,1,0:T(8,128)(2,1)} %get-tuple-element.78.refs_5_), calls=%async_computation.1 | async-start | bytes 786432 | tf_op jit(solution)/shard_map/all_to_all | solution.py:794
  146.7 171.6 %reduce-scatter.4.cloned.1.call-start = ((), (), s32[]{:S(2)}) async-start(), calls=%async_computation.6 | async-start | bytes 6635520 | tf_op jit(solution)/shard_map/reduce_scatter | solution.py:845
  158.5 0.8 copy-start.8
  194.0 23.1 %all-to-all-start.2 = ((bf16[4,2,384,128]{3,2,1,0:T(8,128)(2,1)}), bf16[4,2,384,128]{3,2,1,0:T(8,128)(2,1)S(1)}, u32[]{:S(2)}, u32[]{:S(2)}) async-start(bf16[4,2,384,128]{3,2,1,0:T(8,128)(2,1)} %get-tuple-element.91), calls=%async_computation.2 | async-start | bytes 1572864 | tf_op jit(solution)/shard_map/all_to_all | solution.py:794
  197.6 147.2 %reduce-scatter.8.cloned.1.call-start = ((), (), s32[]{:S(2)}) async-start(), calls=%async_computation.8 | async-start | bytes 3932160 | tf_op jit(solution)/shard_map/reduce_scatter | solution.py:857
  206.1 53.4 %collective-permute-start.8 = (bf16[4,2,96,1856]{3,2,1,0:T(8,128)(2,1)}, bf16[4,2,96,1856]{3,2,1,0:T(8,128)(2,1)}, u32[]{:S(2)}, u32[]{:S(2)}) collective-permute-start(bf16[4,2,96,1856]{3,2,1,0:T(8,128)(2,1)} %bitcast.110), channel_id=1, source_target_pairs={{0,4},{4,0},{8,12},{12,8},{16,20},{20,16},{24,28},{28,24},{1,5},{5... | collective-permute-start | bytes 8552456 | tf_op jit(solution)/shard_map/ppermute | solution.py:689
  217.2 1.9 copy-start.4
  219.1 34.4 %copy-start.9 = (bf16[768,768]{0,1:T(8,128)(2,1)S(1)}, bf16[768,768]{0,1:T(8,128)(2,1)}, u32[]{:S(2)}) copy-start(bf16[768,768]{0,1:T(8,128)(2,1)} %maximum_select_fusion) | copy-start | bytes 3538948
  251.8 1.6 copy-start.1
  257.5 97.2 %reduce-scatter.6.cloned.1.call-start = ((), (), s32[]{:S(2)}) async-start(), calls=%async_computation.7 | async-start | bytes 1843200 | tf_op jit(solution)/shard_map/reduce_scatter | solution.py:878
  263.3 35.0 %collective-permute-start.9 = (bf16[2,2,96,1856]{3,2,1,0:T(8,128)(2,1)}, bf16[2,2,96,1856]{3,2,1,0:T(8,128)(2,1)}, u32[]{:S(2)}, u32[]{:S(2)}) collective-permute-start(bf16[2,2,96,1856]{3,2,1,0:T(8,128)(2,1)} %get-tuple-element.100), channel_id=1, source_target_pairs={{0,8},{4,12},{8,0},{12,4},{16,24},{20,28},{24,16},{28,20},{1,9},{5... | collective-permute-start | bytes 4276232 | tf_op jit(solution)/shard_map/ppermute | solution.py:689
  300.0 18.1 %collective-permute-start.10 = (bf16[1,2,96,1856]{3,2,1,0:T(8,128)(2,1)S(1)}, bf16[1,2,96,1856]{3,2,1,0:T(8,128)(2,1)S(1)}, u32[]{:S(2)}, u32[]{:S(2)}) collective-permute-start(bf16[1,2,96,1856]{3,2,1,0:T(8,128)(2,1)S(1)} %get-tuple-element.105), channel_id=1, source_target_pairs={{0,16},{4,20},{8,24},{12,28},{16,0},{20,4},{24,8},{28,12},{1,17},{... | collective-permute-start | bytes 2138120 | tf_op jit(solution)/shard_map/ppermute | solution.py:689
  300.4 4.3 %collective-permute-start.11 = (f32[1,384]{1,0:T(1,128)S(1)}, f32[1,384]{1,0:T(1,128)S(1)}, u32[]{:S(2)}, u32[]{:S(2)}) collective-permute-start(f32[1,384]{1,0:T(1,128)S(1)} %pad_maximum_fusion.6), channel_id=1, source_target_pairs={{0,1},{1,0},{2,3},{3,2},{4,5},{5,4},{6,7},{7,6},{8,9},{9,8},{10,11... | collective-permute-start | bytes 4616 | tf_op jit(solution)/shard_map/ppermute | solution.py:689
  304.7 4.7 %collective-permute-start.12 = (f32[2,384]{1,0:T(2,128)S(1)}, f32[2,384]{1,0:T(2,128)S(1)}, u32[]{:S(2)}, u32[]{:S(2)}) collective-permute-start(f32[2,384]{1,0:T(2,128)S(1)} %maximum_select_fusion.4), channel_id=1, source_target_pairs={{0,2},{1,3},{2,0},{3,1},{4,6},{5,7},{6,4},{7,5},{8,10},{9,11},{10,... | collective-permute-start | bytes 9224 | tf_op jit(solution)/shard_map/ppermute | solution.py:689
  320.1 2.2 copy-start.5
  323.5 2.1 collective-permute-start.13
  325.7 19.0 %copy-start.6 = (f32[512,768]{1,0:T(8,128)S(1)}, f32[512,768]{1,0:T(8,128)}, u32[]{:S(2)}) copy-start(f32[512,768]{1,0:T(8,128)} %get-tuple-element.109) | copy-start | bytes 4718596
  325.8 9.1 %collective-permute-start.14 = (bf16[2,96,768]{2,1,0:T(8,128)(2,1)S(1)}, bf16[2,96,768]{2,1,0:T(8,128)(2,1)S(1)}, u32[]{:S(2)}, u32[]{:S(2)}) collective-permute-start(bf16[2,96,768]{2,1,0:T(8,128)(2,1)S(1)} %dynamic-slice_bitcast_fusion.1), channel_id=1, source_target_pairs={{0,8},{4,12},{8,0},{12,4},{16,24},{20,28},{24,16},{28,20},{1,9},{5... | collective-permute-start | bytes 884744 | tf_op jit(solution)/shard_map/ppermute | solution.py:689
  335.0 5.2 %collective-permute-start.15 = (bf16[1,96,768]{2,1,0:T(8,128)(2,1)S(1)}, bf16[1,96,768]{2,1,0:T(8,128)(2,1)S(1)}, u32[]{:S(2)}, u32[]{:S(2)}) collective-permute-start(bf16[1,96,768]{2,1,0:T(8,128)(2,1)S(1)} %constant_dynamic-slice_fusion), channel_id=1, source_target_pairs={{0,16},{4,20},{8,24},{12,28},{16,0},{20,4},{24,8},{28,12},{1,17},{... | collective-permute-start | bytes 442376 | tf_op jit(solution)/shard_map/ppermute | solution.py:689
Sparse Core Ops, SparseCore 0:
  9.6 68.1 all-gather.4
  113.9 42.7 all-gather.6
  194.2 61.9 reduce-scatter.3
  258.3 60.2 reduce-scatter.7
  321.7 32.9 reduce-scatter.5

commit v17 on v16

--- a/solution.py
+++ b/solution.py
@@ -360,10 +360,15 @@
 
     @pl.when(step == 0)
     def _():
-        for group, (start, size, target) in enumerate(groups):
+        order = [(0, slot) for slot in range(parts)]
+        order += [(group, slot) for slot in range(parts) for group in (1, 2)]
+        for group, wanted in order:
+            start, size, target = groups[group]
             for piece, marked in zip(pieces, marks):
                 block = piece.shape[1]
                 for at, (slot, turn, relative) in enumerate(marked):
+                    if slot != wanted:
+                        continue
                     offset = pl.multiple_of((index ^ turn) * block, block) if relative else turn * block
                     pltpu.make_async_copy(
                         piece.at[at, :, pl.ds(start, size)],
@@ -570,24 +575,35 @@
     step = pl.program_id(0)
     slots = whole.shape[0]
 
+    def leave(start, stop):
+        for out, turns in zip(outs, plans):
+            block = out.shape[1]
+            for at, turn in enumerate(turns):
+                offset = 0
+                if block < whole.shape[1]:
+                    offset = pl.multiple_of((place_ref[place_ref.shape[0] - 1] ^ turn) * block, block)
+                pltpu.make_async_copy(
+                    whole.at[step, pl.ds(offset, block), pl.ds(start, stop - start)],
+                    out.at[at * slots + step, :, pl.ds(start, stop - start)],
+                    sems.at[step],
+                ).start()
+
     hidden_cols = act_ref.shape[2]
+    columns = whole.shape[2]
+    in_parts = len(plans) == 1 and outs[0].shape[1] == whole.shape[1]
     whole[step, :, :hidden_cols] = dot(first_ref[...], hidden_grad_ref[0], TN).astype(BF16)
+    if in_parts:
+        leave(0, hidden_cols)
     whole[step, :, hidden_cols : 2 * hidden_cols] = dot(branch_grad_ref[...], act_ref[0], TN).astype(BF16)
+    if in_parts:
+        leave(hidden_cols, 2 * hidden_cols)
     ctx = jnp.concatenate([unpack(ref[0]) for ref in ctx_refs], axis=0)
     plain = 2 * hidden_cols + ctx.shape[1]
     whole[step, :, 2 * hidden_cols : plain] = dot(attn_grad_ref[...], ctx, TN).astype(BF16)
     note_rows, room = notes_ref.shape
     for at in range(whole.shape[1] // note_rows):
         whole[step, at * note_rows : (at + 1) * note_rows, plain : plain + room] = notes_ref[...]
-    for out, turns in zip(outs, plans):
-        block = out.shape[1]
-        for at, turn in enumerate(turns):
-            offset = 0
-            if block < whole.shape[1]:
-                offset = pl.multiple_of((place_ref[place_ref.shape[0] - 1] ^ turn) * block, block)
-            pltpu.make_async_copy(
-                whole.at[step, pl.ds(offset, block), :], out.at[at * slots + step], sems.at[step]
-            ).start()
+    leave(2 * hidden_cols if in_parts else 0, columns)
 
     @pl.when(step == slots - 1)
     def _():

time: 370 us -> 370 us (level)
  starting transfers between devices: 28.7 us -> 37 us
  waiting for transfers between devices: 145 us -> 137 us
    ppermute x16, waiting for transfers between devices: 117 us -> 103 us  [swap(): return lax.ppermute(value, axis, [(i, i ^ bit) for i in range(size)])]
    ppermute x16, starting transfers between devices: 15.2 us -> 23 us  [swap(): return lax.ppermute(value, axis, [(i, i ^ bit) for i in range(size)])]
    reduce_scatter x1, waiting for transfers between devices: 7.48 us -> 11.6 us  [local(): lax.psum_scatter(packed, 'tensor', scatter_dimension=0, tiled=True)[0]]
  transfers between devices with their start and end apart: 24 -> 24, of which waited for: 15 -> 16; matrix products, arithmetic and copies ran while one was open for 15% -> 15% of each run, Pallas kernels for 20% -> 20%
where the time goes in v17:
time: 370 us; the launch traced here: 367 us
  waiting for transfers between devices  137 us (37%)
  Pallas kernels  109 us (29%)
  starting transfers between devices  37 us (10%)
  local copies, waits for them, and re-layouts  26.3 us (7%)
  other arithmetic  22.8 us (6%)
  between operations  18.9 us (5%)
  matrix products  16.4 us (4%)
    ppermute x16, waiting for transfers between devices, swap(): return lax.ppermute(value, axis, [(i, i ^ bit) for i in range(size)])  103 us
    pallas_call x1, Pallas kernels, run_backward(): pl.pallas_call(functools.partial(attend_backward, halves, len(qkv)), out_...  32.6 us
    pallas_call x2, Pallas kernels, run_forward(): pl.pallas_call(functools.partial(attend_forward, which), out_shape=(jax.S...  30.8 us
    pallas_call x1, Pallas kernels, run_dense(): pl.pallas_call(functools.partial(dense_chain, marks, halves, total_tokens...  26.3 us
    ppermute x16, starting transfers between devices, swap(): return lax.ppermute(value, axis, [(i, i ^ bit) for i in range(size)])  23 us
    all_to_all x3, waiting for transfers between devices, exchange(): return lax.all_to_all(packed_blocks, 'tensor', 0, 0)  21.5 us
    dot_general x3, matrix products, dot(): lax.dot_general(left_side, right_side, dims, preferred_element_type=F32)  16.4 us
    pallas_call x2, Pallas kernels, run_weights(): pl.pallas_call(functools.partial(dense_weights, tuple((turns for _, turns...  15.9 us
  transfers between devices with their start and end apart: 24, of which 16 were waited for; matrix products, arithmetic and copies ran while one was open for 15% of the time, Pallas kernels for 20%

profile of v17, /device:TPU:0, one launch (start us, length us, event | category | flops | bytes accessed | tf_op | source)
XLA Modules:
  0.0 367.3 jit_solution(18328849032845605968)
XLA Ops:
  13.8 2.6 collective-permute-start.3
  16.7 1.6 collective-permute-start
  18.3 7.8 %collective-permute-done.3 = bf16[192,768]{0,1:T(8,128)(2,1)S(1)} collective-permute-done((bf16[192,768]{0,1:T(8,128)(2,1)S(1)}, bf16[192,768]{0,1:T(8,128)(2,1)S(1)}, u32[]{:S(2)}, u32[]{:S(2)}) %collective-permute-start.3) | collective-permute-done | bytes 294944 | tf_op jit(solution)/shard_map/ppermute | solution.py:705
  26.6 1.8 collective-permute-start.4
  28.5 13.8 %collective-permute-done = bf16[1,96,1792]{2,1,0:T(8,128)(2,1)S(1)} collective-permute-done((bf16[1,96,1792]{2,1,0:T(8,128)(2,1)S(1)}, bf16[1,96,1792]{2,1,0:T(8,128)(2,1)S(1)}, u32[]{:S(2)}, u32[]{:S(2)}) %collective-permute-start) | collective-permute-done | bytes 344096 | tf_op jit(solution)/shard_map/ppermute | solution.py:705
  43.7 12.1 %collective-permute-done.1 = bf16[2,96,1792]{2,1,0:T(8,128)(2,1)} collective-permute-done((bf16[2,96,1792]{2,1,0:T(8,128)(2,1)S(1)}, bf16[2,96,1792]{2,1,0:T(8,128)(2,1)}, u32[]{:S(2)}, u32[]{:S(2)}) %collective-permute-start.1) | collective-permute-done | bytes 688160 | tf_op jit(solution)/shard_map/ppermute | solution.py:705
  57.0 1.7 collective-permute-start.5
  60.7 23.6 %collective-permute-done.5 = bf16[4,96,1792]{2,1,0:T(8,128)(2,1)} collective-permute-done((bf16[4,96,1792]{2,1,0:T(8,128)(2,1)S(1)}, bf16[4,96,1792]{2,1,0:T(8,128)(2,1)}, u32[]{:S(2)}, u32[]{:S(2)}) %collective-permute-start.5) | collective-permute-done | bytes 1376288 | tf_op jit(solution)/shard_map/ppermute | solution.py:705
  84.3 5.0 %collective-permute-start.6 = (bf16[2,96,1792]{2,1,0:T(8,128)(2,1)S(1)}, bf16[2,96,1792]{2,1,0:T(8,128)(2,1)}, u32[]{:S(2)}, u32[]{:S(2)}) collective-permute-start(bf16[2,96,1792]{2,1,0:T(8,128)(2,1)S(1)} %pad_maximum_fusion.2), channel_id=1, source_target_pairs={{0,2},{1,3},{2,0},{3,1},{4,6},{5,7},{6,4},{7,5},{8,10},{9,11},{10,... | collective-permute-start | bytes 2064392 | tf_op jit(solution)/shard_map/ppermute | solution.py:705
  89.3 4.9 %add_convert_fusion.refs_0_ = bf16[2048,768]{1,0:T(8,128)(2,1)S(1)} fusion(bf16[2048,768]{1,0:T(8,128)(2,1)} %bitcast.108, bf16[768,768]{0,1:T(8,128)(2,1)} %maximum_select_fusion, f32[768]{0:T(1024)S(1)} %add.115), kind=kOutput, calls=%fused_computation | convolution fusion | flops 2419064832 | bytes 7474176 | tf_op jit(solution)/shard_map/dot_general | solution.py:30
  94.2 16.4 %attend_forward.2 = (bf16[4,384,128]{2,1,0:T(8,128)(2,1)}, f32[3,1,1024]{2,1,0:T(1,128)S(1)}) custom-call(s32[1]{0:T(128)} %bitcast.lane_ref, s32[8]{0:T(128)S(1)} %get-tuple-element.74.low_ref, s32[8]{0:T(128)S(1)} %get-tuple-element.75.count_ref, bf16[2048,768]{1,0:T(8,128)(2,1)S(1)} %add_convert_fusion.refs_0_, s32[2048,1]{1,0:T(8,128)S(1)} %copy.93.refs_1_, ...), custom_call_target="tpu_custom_call" | custom-call | flops 12884901888 | bytes 5242880 | tf_op jit(solution)/shard_map/attend_forward/pallas_call | solution.py:259
  110.5 3.2 collective-permute-done.6
  114.9 4.8 %all-to-all-start = ((bf16[4,384,128]{2,1,0:T(8,128)(2,1)}), bf16[4,384,128]{2,1,0:T(8,128)(2,1)S(1)}, u32[]{:S(2)}, u32[]{:S(2)}) async-start(bf16[4,384,128]{2,1,0:T(8,128)(2,1)} %get-tuple-element.92.refs_4_), calls=%async_computation | async-start | bytes 786432 | tf_op jit(solution)/shard_map/all_to_all | solution.py:810
  119.7 2.1 copy-done.3
  121.8 14.5 %attend_forward.3 = (bf16[4,384,128]{2,1,0:T(8,128)(2,1)}, f32[3,1,1024]{2,1,0:T(1,128)S(1)}) custom-call(s32[1]{0:T(128)} %bitcast.lane_ref, s32[8]{0:T(128)S(1)} %get-tuple-element.74.low_ref, s32[8]{0:T(128)S(1)} %get-tuple-element.75.count_ref, bf16[2048,768]{1,0:T(8,128)(2,1)S(1)} %copy-done.3, s32[2048,1]{1,0:T(8,128)S(1)} %copy.93.refs_1_, ...), custom_call_target="tpu_custom_call" | custom-call | flops 12884901888 | bytes 5242880 | tf_op jit(solution)/shard_map/attend_forward/pallas_call | solution.py:259
  136.4 2.7 constant_dynamic-update-slice_fusion.refs_2_
  139.1 5.1 %all-to-all-start.1 = ((bf16[4,384,128]{2,1,0:T(8,128)(2,1)}), bf16[4,384,128]{2,1,0:T(8,128)(2,1)S(1)}, u32[]{:S(2)}, u32[]{:S(2)}) async-start(bf16[4,384,128]{2,1,0:T(8,128)(2,1)} %get-tuple-element.78.refs_5_), calls=%async_computation.1 | async-start | bytes 786432 | tf_op jit(solution)/shard_map/all_to_all | solution.py:810
  147.1 9.5 %all-to-all-done.1.refs_1_ = bf16[4,384,128]{2,1,0:T(8,128)(2,1)S(1)} async-done(((bf16[4,384,128]{2,1,0:T(8,128)(2,1)}), bf16[4,384,128]{2,1,0:T(8,128)(2,1)S(1)}, u32[]{:S(2)}, u32[]{:S(2)}) %all-to-all-start.1) | async-done | bytes 393248 | tf_op jit(solution)/shard_map/all_to_all | solution.py:810
  157.3 26.3 %dense_chain.1 = (bf16[512,768]{1,0:T(8,128)(2,1)}, f32[512,768]{1,0:T(8,128)}, bf16[4,2,384,128]{3,2,1,0:T(8,128)(2,1)}, bf16[512,768]{1,0:T(8,128)(2,1)}, bf16...) custom-call(s32[5]{0:T(128)} %stack.53.place_ref, ...), custom_call_target="tpu_custom_call" | custom-call | flops 22548578304 | bytes 25165824 | tf_op jit(solution)/shard_map/dense_chain/pallas_call | solution.py:512
  183.7 7.6 %dense_weights.3 = bf16[2,768,1856]{2,1,0:T(8,128)(2,1)} custom-call(s32[5]{0:T(128)} %stack.53.place_ref, bf16[512,768]{1,0:T(8,128)(2,1)} %get-tuple-element.83.first_ref, bf16[512,768]{1,0:T(8,128)(2,1)} %get-tuple-element.84.branch_grad_ref, bf16[512,768]{1,0:T(8,128)(2,1)} %get-tuple-element.85.attn_grad_ref, ...), custom_call_target="tpu_custom_call" | custom-call | flops 2919235584 | bytes 10485760 | tf_op jit(solution)/shard_map/dense_weights/pallas_call | solution.py:623
  191.3 3.9 %all-to-all-start.2 = ((bf16[4,2,384,128]{3,2,1,0:T(8,128)(2,1)}), bf16[4,2,384,128]{3,2,1,0:T(8,128)(2,1)S(1)}, u32[]{:S(2)}, u32[]{:S(2)}) async-start(bf16[4,2,384,128]{3,2,1,0:T(8,128)(2,1)} %get-tuple-element.91), calls=%async_computation.2 | async-start | bytes 1572864 | tf_op jit(solution)/shard_map/all_to_all | solution.py:810
  195.2 8.4 %dense_weights.2 = (bf16[8,96,1856]{2,1,0:T(8,128)(2,1)}, bf16[8,96,1856]{2,1,0:T(8,128)(2,1)}) custom-call(s32[5]{0:T(128)} %stack.53.place_ref, bf16[512,768]{1,0:T(8,128)(2,1)} %get-tuple-element.83.first_ref, bf16[512,768]{1,0:T(8,128)(2,1)} %get-tuple-element.84.branch_grad_ref, bf16[512,768]{1,0:T(8,128)(2,1)} %get-tuple-element.85.attn_grad_ref, ...), custom_call_target="tpu_custom_call" | custom-call | flops 2919235584 | bytes 10485760 | tf_op jit(solution)/shard_map/dense_weights/pallas_call | solution.py:623
  203.6 12.1 %all-to-all-done.2 = bf16[4,2,384,128]{3,2,1,0:T(8,128)(2,1)S(1)} async-done(((bf16[4,2,384,128]{3,2,1,0:T(8,128)(2,1)}), bf16[4,2,384,128]{3,2,1,0:T(8,128)(2,1)S(1)}, u32[]{:S(2)}, u32[]{:S(2)}) %all-to-all-start.2) | async-done | bytes 786464 | tf_op jit(solution)/shard_map/all_to_all | solution.py:810
  215.7 1.9 copy-done.4
  217.6 32.6 %attend_backward.1 = (bf16[1,2048,768]{2,1,0:T(8,128)(2,1)S(1)}, f32[1,768]{1,0:T(1,128)S(1)}) custom-call(s32[1]{0:T(128)} %bitcast.lane_ref, s32[8]{0:T(128)S(1)} %get-tuple-element.74.low_ref, s32[8]{0:T(128)S(1)} %get-tuple-element.75.count_ref, bf16[2048,768]{1,0:T(8,128)(2,1)S(1)} %copy-done.4, s32[2048,1]{1,0:T(8,128)S(1)} %copy.93.refs_1_, ...), custom_call_target="tpu_custom_call" | custom-call | flops 51539607552 | bytes 10485760 | tf_op jit(solution)/shard_map/attend_backward/pallas_call | solution.py:303
  250.2 1.6 copy-done.1
  251.8 4.0 %convolution_convert_fusion = bf16[2048,768]{1,0:T(8,128)(2,1)} fusion(bf16[768,768]{0,1:T(8,128)(2,1)S(1)} %copy-done.9, bf16[1,2048,768]{2,1,0:T(8,128)(2,1)S(1)} %get-tuple-element.95), kind=kOutput, calls=%fused_computation.1 | convolution fusion | flops 2417491968 | bytes 7471104 | tf_op jit(solution)/shard_map/dot_general | solution.py:30
  255.8 2.0 fusion.13
  257.9 3.8 %fusion = (bf16[2,2,96,1856]{3,2,1,0:T(8,128)(2,1)}, bf16[2,2,96,1856]{3,2,1,0:T(8,128)(2,1)S(1)}) fusion(bf16[2,2,96,1856]{3,2,1,0:T(8,128)(2,1)S(1)} %bitcast.84, bf16[4,2,96,1856]{3,2,1,0:T(8,128)(2,1)} %collective-permute-done.8, bf16[2,2,96,1856]{3,2,1,0:T(8,128)(2,1)S(1)} %bitcast.85), kind=kLoop, calls=%fused_computation.3 | loop fusion | flops 5701632 | bytes 8552448 | tf_op jit(solution)/shard_map/convert_element_type | solution.py:727
  261.8 7.5 %fusion.16 = f32[768,768]{1,0:T(8,128)} fusion(bf16[2048,768]{1,0:T(8,128)(2,1)} %bitcast.109, bf16[2048,768]{1,0:T(8,128)(2,1)} %bitcast.83), kind=kOutput, calls=%fused_computation.84 | convolution fusion | flops 2415919104 | bytes 8650752 | tf_op jit(solution)/shard_map/dot_general | solution.py:30
  269.3 19.5 %collective-permute-done.9 = bf16[2,2,96,1856]{3,2,1,0:T(8,128)(2,1)} collective-permute-done((bf16[2,2,96,1856]{3,2,1,0:T(8,128)(2,1)}, bf16[2,2,96,1856]{3,2,1,0:T(8,128)(2,1)}, u32[]{:S(2)}, u32[]{:S(2)}) %collective-permute-start.9) | collective-permute-done | bytes 1425440 | tf_op jit(solution)/shard_map/ppermute | solution.py:705
  288.8 1.7 add_convert_fusion.3
  290.5 7.7 %collective-permute-start.10 = (bf16[1,2,96,1856]{3,2,1,0:T(8,128)(2,1)S(1)}, bf16[1,2,96,1856]{3,2,1,0:T(8,128)(2,1)S(1)}, u32[]{:S(2)}, u32[]{:S(2)}) collective-permute-start(bf16[1,2,96,1856]{3,2,1,0:T(8,128)(2,1)S(1)} %get-tuple-element.105), channel_id=1, source_target_pairs={{0,16},{4,20},{8,24},{12,28},{16,0},{20,4},{24,8},{28,12},{1,17},{... | collective-permute-start | bytes 2138120 | tf_op jit(solution)/shard_map/ppermute | solution.py:705
  298.5 5.3 %collective-permute-done.11 = f32[1,384]{1,0:T(1,128)S(1)} collective-permute-done((f32[1,384]{1,0:T(1,128)S(1)}, f32[1,384]{1,0:T(1,128)S(1)}, u32[]{:S(2)}, u32[]{:S(2)}) %collective-permute-start.11) | collective-permute-done | bytes 1568 | tf_op jit(solution)/shard_map/ppermute | solution.py:705
  303.9 4.7 %collective-permute-done.12 = f32[2,384]{1,0:T(2,128)S(1)} collective-permute-done((f32[2,384]{1,0:T(2,128)S(1)}, f32[2,384]{1,0:T(2,128)S(1)}, u32[]{:S(2)}, u32[]{:S(2)}) %collective-permute-start.12) | collective-permute-done | bytes 3104 | tf_op jit(solution)/shard_map/ppermute | solution.py:705
  309.9 3.3 collective-permute-done.10
  313.3 1.7 fusion.6
  315.1 1.4 pad_maximum_fusion
  318.6 2.0 collective-permute-done.13
  323.7 6.2 %collective-permute-done.14 = bf16[2,96,768]{2,1,0:T(8,128)(2,1)S(1)} collective-permute-done((bf16[2,96,768]{2,1,0:T(8,128)(2,1)S(1)}, bf16[2,96,768]{2,1,0:T(8,128)(2,1)S(1)}, u32[]{:S(2)}, u32[]{:S(2)}) %collective-permute-start.14) | collective-permute-done | bytes 294944 | tf_op jit(solution)/shard_map/ppermute | solution.py:705
  330.0 1.8 collective-permute-start.15
  333.8 1.4 collective-permute-done.15
  335.9 1.7 finish_heads.1
  339.8 2.4 add_bitcast_fusion
  342.2 11.6 %reduce-scatter.6.cloned.1.call-done = bf16[1,96,1856]{2,1,0:T(8,128)(2,1)} async-done(((bf16[4,96,1856]{2,1,0:T(8,128)(2,1)}), bf16[1,96,1856]{2,1,0:T(8,128)(2,1)}) %reduce-scatter.6.cloned.1.call-update) | async-done | bytes 356368 | tf_op jit(solution)/shard_map/reduce_scatter | solution.py:894
  353.8 1.9 finish_dense.1
  355.6 1.3 slice_bitcast_fusion
  357.0 2.0 slice_bitcast_fusion.1
  (142 shorter events, 26.1 us)
Async XLA Ops:
  7.2 4.3 %copy-start.13 = (s32[1,512]{1,0:T(1,128)S(1)}, s32[1,512]{1,0:T(1,128)}, u32[]{:S(2)}) copy-start(s32[1,512]{1,0:T(1,128)} %param.22) | copy-start | bytes 6148
  7.2 9.2 %copy-start.12 = (bf16[192,96]{1,0:T(8,128)(2,1)S(1)}, bf16[192,96]{1,0:T(8,128)(2,1)}, u32[]{:S(2)}) copy-start(bf16[192,96]{1,0:T(8,128)(2,1)} %param.28) | copy-start | bytes 110596
  7.2 9.3 %copy-start.11 = (bf16[768,96]{0,1:T(8,128)(2,1)S(1)}, bf16[768,96]{0,1:T(8,128)(2,1)}, u32[]{:S(2)}) copy-start(bf16[768,96]{0,1:T(8,128)(2,1)} %param.30) | copy-start | bytes 442372
  7.2 9.3 %copy-start.10 = (bf16[96,768]{1,0:T(8,128)(2,1)S(1)}, bf16[96,768]{1,0:T(8,128)(2,1)}, u32[]{:S(2)}) copy-start(bf16[96,768]{1,0:T(8,128)(2,1)} %param.29) | copy-start | bytes 442372
  7.2 77.0 %all-gather.5.cloned.1.call-start = ((), (), s32[]{:S(2)}) async-start(), calls=%async_computation.9 | async-start | bytes 3932160 | tf_op jit(solution)/shard_map/all_gather | solution.py:768
  8.0 148.7 %all-gather.7.cloned.1.call-start = ((), (), s32[]{:S(2)}) async-start(), calls=%async_computation.10 | async-start | bytes 6193152 | tf_op jit(solution)/shard_map/all_gather | solution.py:816
  11.0 2.4 collective-permute-start.2
  13.8 12.3 %collective-permute-start.3 = (bf16[192,768]{0,1:T(8,128)(2,1)S(1)}, bf16[192,768]{0,1:T(8,128)(2,1)S(1)}, u32[]{:S(2)}, u32[]{:S(2)}) collective-permute-start(bf16[192,768]{0,1:T(8,128)(2,1)S(1)} %maximum_select_fusion.2), channel_id=1, source_target_pairs={{0,8},{4,12},{8,0},{12,4},{16,24},{20,28},{24,16},{28,20},{1,9},{5... | collective-permute-start | bytes 884744 | tf_op jit(solution)/shard_map/ppermute | solution.py:705
  16.7 25.6 %collective-permute-start = (bf16[1,96,1792]{2,1,0:T(8,128)(2,1)S(1)}, bf16[1,96,1792]{2,1,0:T(8,128)(2,1)S(1)}, u32[]{:S(2)}, u32[]{:S(2)}) collective-permute-start(bf16[1,96,1792]{2,1,0:T(8,128)(2,1)S(1)} %bitcast.88), channel_id=1, source_target_pairs={{0,1},{1,0},{2,3},{3,2},{4,5},{5,4},{6,7},{7,6},{8,9},{9,8},{10,11... | collective-permute-start | bytes 1032200 | tf_op jit(solution)/shard_map/ppermute | solution.py:705
  26.6 15.8 %collective-permute-start.4 = (bf16[384,768]{0,1:T(8,128)(2,1)S(1)}, bf16[384,768]{0,1:T(8,128)(2,1)S(1)}, u32[]{:S(2)}, u32[]{:S(2)}) collective-permute-start(bf16[384,768]{0,1:T(8,128)(2,1)S(1)} %maximum_select_fusion.1), channel_id=1, source_target_pairs={{0,16},{4,20},{8,24},{12,28},{16,0},{20,4},{24,8},{28,12},{1,17},{... | collective-permute-start | bytes 1769480 | tf_op jit(solution)/shard_map/ppermute | solution.py:705
  42.3 13.5 %collective-permute-start.1 = (bf16[2,96,1792]{2,1,0:T(8,128)(2,1)S(1)}, bf16[2,96,1792]{2,1,0:T(8,128)(2,1)}, u32[]{:S(2)}, u32[]{:S(2)}) collective-permute-start(bf16[2,96,1792]{2,1,0:T(8,128)(2,1)S(1)} %pad_maximum_fusion.2), channel_id=1, source_target_pairs={{0,8},{4,12},{8,0},{12,4},{16,24},{20,28},{24,16},{28,20},{1,9},{5... | collective-permute-start | bytes 2064392 | tf_op jit(solution)/shard_map/ppermute | solution.py:705
  43.7 15.0 %copy-start = (s32[1,2048]{1,0:T(1,128)S(1)}, s32[1,2048]{1,0:T(1,128)}, u32[]{:S(2)}) copy-start(s32[1,2048]{1,0:T(1,128)} %refs_2_.5) | copy-start | bytes 24580
  57.0 27.3 %collective-permute-start.5 = (bf16[4,96,1792]{2,1,0:T(8,128)(2,1)S(1)}, bf16[4,96,1792]{2,1,0:T(8,128)(2,1)}, u32[]{:S(2)}, u32[]{:S(2)}) collective-permute-start(bf16[4,96,1792]{2,1,0:T(8,128)(2,1)S(1)} %pad_maximum_fusion.1), channel_id=1, source_target_pairs={{0,16},{4,20},{8,24},{12,28},{16,0},{20,4},{24,8},{28,12},{1,17},{... | collective-permute-start | bytes 4128776 | tf_op jit(solution)/shard_map/ppermute | solution.py:705
  84.3 29.5 %collective-permute-start.6 = (bf16[2,96,1792]{2,1,0:T(8,128)(2,1)S(1)}, bf16[2,96,1792]{2,1,0:T(8,128)(2,1)}, u32[]{:S(2)}, u32[]{:S(2)}) collective-permute-start(bf16[2,96,1792]{2,1,0:T(8,128)(2,1)S(1)} %pad_maximum_fusion.2), channel_id=1, source_target_pairs={{0,2},{1,3},{2,0},{3,1},{4,6},{5,7},{6,4},{7,5},{8,10},{9,11},{10,... | collective-permute-start | bytes 2064392 | tf_op jit(solution)/shard_map/ppermute | solution.py:705
  94.1 16.4 %copy-start.2 = (bf16[2048,768]{1,0:T(8,128)(2,1)}, bf16[2048,768]{1,0:T(8,128)(2,1)S(1)}, u32[]{:S(2)}) copy-start(bf16[2048,768]{1,0:T(8,128)(2,1)S(1)} %add_convert_fusion.refs_0_) | copy-start | bytes 9437188
  114.9 21.4 %all-to-all-start = ((bf16[4,384,128]{2,1,0:T(8,128)(2,1)}), bf16[4,384,128]{2,1,0:T(8,128)(2,1)S(1)}, u32[]{:S(2)}, u32[]{:S(2)}) async-start(bf16[4,384,128]{2,1,0:T(8,128)(2,1)} %get-tuple-element.92.refs_4_), calls=%async_computation | async-start | bytes 786432 | tf_op jit(solution)/shard_map/all_to_all | solution.py:810
  119.7 2.1 copy-start.3
  136.3 2.8 copy-start.7
  136.3 7.9 %copy-start.15 = (bf16[768]{0:T(1024)(128)(2,1)S(1)}, bf16[768]{0:T(1024)(128)(2,1)}, u32[]{:S(2)}) copy-start(bf16[768]{0:T(1024)(128)(2,1)} %param.33) | copy-start | bytes 4612
  136.4 7.9 %copy-start.16 = (bf16[768]{0:T(1024)(128)(2,1)S(1)}, bf16[768]{0:T(1024)(128)(2,1)}, u32[]{:S(2)}) copy-start(bf16[768]{0:T(1024)(128)(2,1)} %param.35) | copy-start | bytes 4612
  136.4 7.9 %copy-start.17 = (bf16[768]{0:T(1024)(128)(2,1)S(1)}, bf16[768]{0:T(1024)(128)(2,1)}, u32[]{:S(2)}) copy-start(bf16[768]{0:T(1024)(128)(2,1)} %param.36) | copy-start | bytes 4612
  136.4 7.9 %copy-start.18 = (bf16[768]{0:T(1024)(128)(2,1)S(1)}, bf16[768]{0:T(1024)(128)(2,1)}, u32[]{:S(2)}) copy-start(bf16[768]{0:T(1024)(128)(2,1)} %param.37) | copy-start | bytes 4612
  136.4 7.9 %copy-start.19 = (bf16[768]{0:T(1024)(128)(2,1)S(1)}, bf16[768]{0:T(1024)(128)(2,1)}, u32[]{:S(2)}) copy-start(bf16[768]{0:T(1024)(128)(2,1)} %param.38) | copy-start | bytes 4612
  136.4 7.9 %copy-start.20 = (bf16[768]{0:T(1024)(128)(2,1)S(1)}, bf16[768]{0:T(1024)(128)(2,1)}, u32[]{:S(2)}) copy-start(bf16[768]{0:T(1024)(128)(2,1)} %param.39) | copy-start | bytes 4612
  136.4 8.6 %copy-start.14 = (bf16[3072]{0:T(1024)(128)(2,1)S(1)}, bf16[3072]{0:T(1024)(128)(2,1)}, u32[]{:S(2)}) copy-start(bf16[3072]{0:T(1024)(128)(2,1)} %param.34) | copy-start | bytes 18436
  139.1 17.4 %collective-permute-start.7 = (bf16[8,96,1792]{2,1,0:T(8,128)(2,1)}, bf16[8,96,1792]{2,1,0:T(8,128)(2,1)}, u32[]{:S(2)}, u32[]{:S(2)}) collective-permute-start(bf16[8,96,1792]{2,1,0:T(8,128)(2,1)} %constant_dynamic-update-slice_fusion.refs_2_), channel_id=1, source_target_pairs={{0,4},{4,0},{8,12},{12,8},{16,20},{20,16},{24,28},{28,24},{1,5},{5... | collective-permute-start | bytes 8257544 | tf_op jit(solution)/shard_map/ppermute | solution.py:705
  139.1 17.4 %all-to-all-start.1 = ((bf16[4,384,128]{2,1,0:T(8,128)(2,1)}), bf16[4,384,128]{2,1,0:T(8,128)(2,1)S(1)}, u32[]{:S(2)}, u32[]{:S(2)}) async-start(bf16[4,384,128]{2,1,0:T(8,128)(2,1)} %get-tuple-element.78.refs_5_), calls=%async_computation.1 | async-start | bytes 786432 | tf_op jit(solution)/shard_map/all_to_all | solution.py:810
  144.2 169.1 %reduce-scatter.4.cloned.1.call-start = ((), (), s32[]{:S(2)}) async-start(), calls=%async_computation.6 | async-start | bytes 6635520 | tf_op jit(solution)/shard_map/reduce_scatter | solution.py:861
  156.6 0.8 copy-start.8
  191.3 24.4 %all-to-all-start.2 = ((bf16[4,2,384,128]{3,2,1,0:T(8,128)(2,1)}), bf16[4,2,384,128]{3,2,1,0:T(8,128)(2,1)S(1)}, u32[]{:S(2)}, u32[]{:S(2)}) async-start(bf16[4,2,384,128]{3,2,1,0:T(8,128)(2,1)} %get-tuple-element.91), calls=%async_computation.2 | async-start | bytes 1572864 | tf_op jit(solution)/shard_map/all_to_all | solution.py:810
  195.2 144.6 %reduce-scatter.8.cloned.1.call-start = ((), (), s32[]{:S(2)}) async-start(), calls=%async_computation.8 | async-start | bytes 3932160 | tf_op jit(solution)/shard_map/reduce_scatter | solution.py:873
  203.5 54.3 %collective-permute-start.8 = (bf16[4,2,96,1856]{3,2,1,0:T(8,128)(2,1)}, bf16[4,2,96,1856]{3,2,1,0:T(8,128)(2,1)}, u32[]{:S(2)}, u32[]{:S(2)}) collective-permute-start(bf16[4,2,96,1856]{3,2,1,0:T(8,128)(2,1)} %bitcast.110), channel_id=1, source_target_pairs={{0,4},{4,0},{8,12},{12,8},{16,20},{20,16},{24,28},{28,24},{1,5},{5... | collective-permute-start | bytes 8552456 | tf_op jit(solution)/shard_map/ppermute | solution.py:705
  215.7 1.9 copy-start.4
  217.6 34.2 %copy-start.9 = (bf16[768,768]{0,1:T(8,128)(2,1)S(1)}, bf16[768,768]{0,1:T(8,128)(2,1)}, u32[]{:S(2)}) copy-start(bf16[768,768]{0,1:T(8,128)(2,1)} %maximum_select_fusion) | copy-start | bytes 3538948
  250.2 1.6 copy-start.1
  255.8 98.0 %reduce-scatter.6.cloned.1.call-start = ((), (), s32[]{:S(2)}) async-start(), calls=%async_computation.7 | async-start | bytes 1843200 | tf_op jit(solution)/shard_map/reduce_scatter | solution.py:894
  261.7 27.1 %collective-permute-start.9 = (bf16[2,2,96,1856]{3,2,1,0:T(8,128)(2,1)}, bf16[2,2,96,1856]{3,2,1,0:T(8,128)(2,1)}, u32[]{:S(2)}, u32[]{:S(2)}) collective-permute-start(bf16[2,2,96,1856]{3,2,1,0:T(8,128)(2,1)} %get-tuple-element.100), channel_id=1, source_target_pairs={{0,8},{4,12},{8,0},{12,4},{16,24},{20,28},{24,16},{28,20},{1,9},{5... | collective-permute-start | bytes 4276232 | tf_op jit(solution)/shard_map/ppermute | solution.py:705
  290.5 22.6 %collective-permute-start.10 = (bf16[1,2,96,1856]{3,2,1,0:T(8,128)(2,1)S(1)}, bf16[1,2,96,1856]{3,2,1,0:T(8,128)(2,1)S(1)}, u32[]{:S(2)}, u32[]{:S(2)}) collective-permute-start(bf16[1,2,96,1856]{3,2,1,0:T(8,128)(2,1)S(1)} %get-tuple-element.105), channel_id=1, source_target_pairs={{0,16},{4,20},{8,24},{12,28},{16,0},{20,4},{24,8},{28,12},{1,17},{... | collective-permute-start | bytes 2138120 | tf_op jit(solution)/shard_map/ppermute | solution.py:705
  298.5 5.3 %collective-permute-start.11 = (f32[1,384]{1,0:T(1,128)S(1)}, f32[1,384]{1,0:T(1,128)S(1)}, u32[]{:S(2)}, u32[]{:S(2)}) collective-permute-start(f32[1,384]{1,0:T(1,128)S(1)} %pad_maximum_fusion.6), channel_id=1, source_target_pairs={{0,1},{1,0},{2,3},{3,2},{4,5},{5,4},{6,7},{7,6},{8,9},{9,8},{10,11... | collective-permute-start | bytes 4616 | tf_op jit(solution)/shard_map/ppermute | solution.py:705
  303.9 4.7 %collective-permute-start.12 = (f32[2,384]{1,0:T(2,128)S(1)}, f32[2,384]{1,0:T(2,128)S(1)}, u32[]{:S(2)}, u32[]{:S(2)}) collective-permute-start(f32[2,384]{1,0:T(2,128)S(1)} %maximum_select_fusion.4), channel_id=1, source_target_pairs={{0,2},{1,3},{2,0},{3,1},{4,6},{5,7},{6,4},{7,5},{8,10},{9,11},{10,... | collective-permute-start | bytes 9224 | tf_op jit(solution)/shard_map/ppermute | solution.py:705
  315.1 2.2 copy-start.5
  318.5 2.1 collective-permute-start.13
  320.7 19.0 %copy-start.6 = (f32[512,768]{1,0:T(8,128)S(1)}, f32[512,768]{1,0:T(8,128)}, u32[]{:S(2)}) copy-start(f32[512,768]{1,0:T(8,128)} %get-tuple-element.109) | copy-start | bytes 4718596
  320.8 9.1 %collective-permute-start.14 = (bf16[2,96,768]{2,1,0:T(8,128)(2,1)S(1)}, bf16[2,96,768]{2,1,0:T(8,128)(2,1)S(1)}, u32[]{:S(2)}, u32[]{:S(2)}) collective-permute-start(bf16[2,96,768]{2,1,0:T(8,128)(2,1)S(1)} %dynamic-slice_bitcast_fusion.1), channel_id=1, source_target_pairs={{0,8},{4,12},{8,0},{12,4},{16,24},{20,28},{24,16},{28,20},{1,9},{5... | collective-permute-start | bytes 884744 | tf_op jit(solution)/shard_map/ppermute | solution.py:705
  330.0 5.2 %collective-permute-start.15 = (bf16[1,96,768]{2,1,0:T(8,128)(2,1)S(1)}, bf16[1,96,768]{2,1,0:T(8,128)(2,1)S(1)}, u32[]{:S(2)}, u32[]{:S(2)}) collective-permute-start(bf16[1,96,768]{2,1,0:T(8,128)(2,1)S(1)} %constant_dynamic-slice_fusion), channel_id=1, source_target_pairs={{0,16},{4,20},{8,24},{12,28},{16,0},{20,4},{24,8},{28,12},{1,17},{... | collective-permute-start | bytes 442376 | tf_op jit(solution)/shard_map/ppermute | solution.py:705
Sparse Core Ops, SparseCore 0:
  9.6 68.1 all-gather.4
  113.9 42.7 all-gather.6
  191.4 63.7 reduce-scatter.3
  257.4 60.3 reduce-scatter.7
  319.9 33.7 reduce-scatter.5

commit v18 on v17

--- a/solution.py
+++ b/solution.py
@@ -281,7 +281,7 @@
             ],
         ),
         compiler_params=pltpu.CompilerParams(
-            dimension_semantics=("arbitrary",), vmem_limit_bytes=28 << 20
+            dimension_semantics=("arbitrary",), vmem_limit_bytes=VMEM_LIMIT if half else 28 << 20
         ),
         cost_estimate=pl.CostEstimate(
             flops=heads * seq_len * seq_len * 2048 * steps // blocks,
@@ -326,7 +326,7 @@
             ],
         ),
         compiler_params=pltpu.CompilerParams(
-            dimension_semantics=("arbitrary",), vmem_limit_bytes=28 << 20
+            dimension_semantics=("arbitrary",), vmem_limit_bytes=VMEM_LIMIT
         ),
         cost_estimate=pl.CostEstimate(
             flops=heads * seq_len * seq_len * 4096,

time: 370 us -> 371 us (level)
  Pallas kernels: 109 us -> 117 us
    pallas_call x1, Pallas kernels: 32.6 us -> 36.9 us  [run_backward(): pl.pallas_call(functools.partial(attend_backward, halves, len(qkv)), out_...]
    ppermute x16, waiting for transfers between devices: 103 us -> 106 us  [swap(): return lax.ppermute(value, axis, [(i, i ^ bit) for i in range(size)])]
    unnamed x48 -> x50, local copies, waits for them, and re-layouts: 11.3 us -> 8.77 us
  transfers between devices with their start and end apart: 24 -> 24, of which waited for: 16 -> 15; matrix products, arithmetic and copies ran while one was open for 15% -> 15% of each run, Pallas kernels for 20% -> 22%
where the time goes in v18:
time: 371 us; the launch traced here: 370 us
  waiting for transfers between devices  135 us (36%)
  Pallas kernels  117 us (32%)
  starting transfers between devices  35.3 us (10%)
  local copies, waits for them, and re-layouts  24.5 us (7%)
  other arithmetic  21.5 us (6%)
  between operations  18.8 us (5%)
  matrix products  18 us (5%)
    ppermute x16, waiting for transfers between devices, swap(): return lax.ppermute(value, axis, [(i, i ^ bit) for i in range(size)])  106 us
    pallas_call x1, Pallas kernels, run_backward(): pl.pallas_call(functools.partial(attend_backward, halves, len(qkv)), out_...  36.9 us
    pallas_call x2, Pallas kernels, run_forward(): pl.pallas_call(functools.partial(attend_forward, which), out_shape=(jax.S...  34.2 us
    pallas_call x1, Pallas kernels, run_dense(): pl.pallas_call(functools.partial(dense_chain, marks, halves, total_tokens...  26.3 us
    ppermute x16, starting transfers between devices, swap(): return lax.ppermute(value, axis, [(i, i ^ bit) for i in range(size)])  21.4 us
    all_to_all x3, waiting for transfers between devices, exchange(): return lax.all_to_all(packed_blocks, 'tensor', 0, 0)  18.1 us
    dot_general x3, matrix products, dot(): lax.dot_general(left_side, right_side, dims, preferred_element_type=F32)  18 us
    pallas_call x2, Pallas kernels, run_weights(): pl.pallas_call(functools.partial(dense_weights, tuple((turns for _, turns...  15.8 us
  transfers between devices with their start and end apart: 24, of which 15 were waited for; matrix products, arithmetic and copies ran while one was open for 15% of the time, Pallas kernels for 22%

profile of v18, /device:TPU:0, one launch (start us, length us, event | category | flops | bytes accessed | tf_op | source)
XLA Modules:
  0.0 370.1 jit_solution(16895101061199854628)
XLA Ops:
  13.8 2.6 collective-permute-start.3
  16.7 1.6 collective-permute-start
  18.3 7.8 %collective-permute-done.3 = bf16[192,768]{0,1:T(8,128)(2,1)S(1)} collective-permute-done((bf16[192,768]{0,1:T(8,128)(2,1)S(1)}, bf16[192,768]{0,1:T(8,128)(2,1)S(1)}, u32[]{:S(2)}, u32[]{:S(2)}) %collective-permute-start.3) | collective-permute-done | bytes 294944 | tf_op jit(solution)/shard_map/ppermute | solution.py:705
  26.6 1.8 collective-permute-start.4
  28.5 13.8 %collective-permute-done = bf16[1,96,1792]{2,1,0:T(8,128)(2,1)S(1)} collective-permute-done((bf16[1,96,1792]{2,1,0:T(8,128)(2,1)S(1)}, bf16[1,96,1792]{2,1,0:T(8,128)(2,1)S(1)}, u32[]{:S(2)}, u32[]{:S(2)}) %collective-permute-start) | collective-permute-done | bytes 344096 | tf_op jit(solution)/shard_map/ppermute | solution.py:705
  42.4 1.3 maximum_select_fusion
  43.7 12.1 %collective-permute-done.1 = bf16[2,96,1792]{2,1,0:T(8,128)(2,1)} collective-permute-done((bf16[2,96,1792]{2,1,0:T(8,128)(2,1)S(1)}, bf16[2,96,1792]{2,1,0:T(8,128)(2,1)}, u32[]{:S(2)}, u32[]{:S(2)}) %collective-permute-start.1) | collective-permute-done | bytes 688160 | tf_op jit(solution)/shard_map/ppermute | solution.py:705
  55.7 1.2 pad_maximum_fusion.1
  57.0 1.7 collective-permute-start.5
  60.7 23.6 %collective-permute-done.5 = bf16[4,96,1792]{2,1,0:T(8,128)(2,1)} collective-permute-done((bf16[4,96,1792]{2,1,0:T(8,128)(2,1)S(1)}, bf16[4,96,1792]{2,1,0:T(8,128)(2,1)}, u32[]{:S(2)}, u32[]{:S(2)}) %collective-permute-start.5) | collective-permute-done | bytes 1376288 | tf_op jit(solution)/shard_map/ppermute | solution.py:705
  84.3 5.0 %collective-permute-start.6 = (bf16[2,96,1792]{2,1,0:T(8,128)(2,1)S(1)}, bf16[2,96,1792]{2,1,0:T(8,128)(2,1)}, u32[]{:S(2)}, u32[]{:S(2)}) collective-permute-start(bf16[2,96,1792]{2,1,0:T(8,128)(2,1)S(1)} %pad_maximum_fusion.2), channel_id=1, source_target_pairs={{0,2},{1,3},{2,0},{3,1},{4,6},{5,7},{6,4},{7,5},{8,10},{9,11},{10,... | collective-permute-start | bytes 2064392 | tf_op jit(solution)/shard_map/ppermute | solution.py:705
  89.3 4.9 %add_convert_fusion.refs_0_ = bf16[2048,768]{1,0:T(8,128)(2,1)S(1)} fusion(bf16[2048,768]{1,0:T(8,128)(2,1)} %bitcast.107, bf16[768,768]{0,1:T(8,128)(2,1)} %maximum_select_fusion, f32[768]{0:T(1024)S(1)} %add.115), kind=kOutput, calls=%fused_computation | convolution fusion | flops 2419064832 | bytes 7474176 | tf_op jit(solution)/shard_map/dot_general | solution.py:30
  94.2 16.4 %attend_forward.2 = (bf16[4,384,128]{2,1,0:T(8,128)(2,1)}, f32[3,1,1024]{2,1,0:T(1,128)S(1)}) custom-call(s32[1]{0:T(128)} %bitcast.lane_ref, s32[8]{0:T(128)S(1)} %get-tuple-element.74.low_ref, s32[8]{0:T(128)S(1)} %get-tuple-element.75.count_ref, bf16[2048,768]{1,0:T(8,128)(2,1)S(1)} %add_convert_fusion.refs_0_, s32[2048,1]{1,0:T(8,128)S(1)} %copy.93.refs_1_, ...), custom_call_target="tpu_custom_call" | custom-call | flops 12884901888 | bytes 5242880 | tf_op jit(solution)/shard_map/attend_forward/pallas_call | solution.py:259
  111.2 2.5 collective-permute-done.6
  115.0 4.8 %all-to-all-start = ((bf16[4,384,128]{2,1,0:T(8,128)(2,1)}), bf16[4,384,128]{2,1,0:T(8,128)(2,1)S(1)}, u32[]{:S(2)}, u32[]{:S(2)}) async-start(bf16[4,384,128]{2,1,0:T(8,128)(2,1)} %get-tuple-element.92.refs_4_), calls=%async_computation | async-start | bytes 786432 | tf_op jit(solution)/shard_map/all_to_all | solution.py:810
  119.8 17.9 %attend_forward.3 = (bf16[4,384,128]{2,1,0:T(8,128)(2,1)}, f32[3,1,1024]{2,1,0:T(1,128)}) custom-call(s32[1]{0:T(128)} %bitcast.lane_ref, s32[8]{0:T(128)} %copy-done.2, s32[8]{0:T(128)} %copy-done.3, bf16[2048,768]{1,0:T(8,128)(2,1)} %copy-done.4, s32[2048,1]{1,0:T(8,128)} %copy-done, s32[1,2048]{1,0:T(1,128)} %refs_2_.5), custom_call_target="tpu_custom_call" | custom-call | flops 12884901888 | bytes 5242880 | tf_op jit(solution)/shard_map/attend_forward/pallas_call | solution.py:259
  137.7 1.9 constant_dynamic-update-slice_fusion.refs_2_
  139.7 5.0 %all-to-all-start.1 = ((bf16[4,384,128]{2,1,0:T(8,128)(2,1)}), bf16[4,384,128]{2,1,0:T(8,128)(2,1)S(1)}, u32[]{:S(2)}, u32[]{:S(2)}) async-start(bf16[4,384,128]{2,1,0:T(8,128)(2,1)} %get-tuple-element.78.refs_5_), calls=%async_computation.1 | async-start | bytes 786432 | tf_op jit(solution)/shard_map/all_to_all | solution.py:810
  150.9 6.1 %all-to-all-done.1.refs_1_ = bf16[4,384,128]{2,1,0:T(8,128)(2,1)S(1)} async-done(((bf16[4,384,128]{2,1,0:T(8,128)(2,1)}), bf16[4,384,128]{2,1,0:T(8,128)(2,1)S(1)}, u32[]{:S(2)}, u32[]{:S(2)}) %all-to-all-start.1) | async-done | bytes 393248 | tf_op jit(solution)/shard_map/all_to_all | solution.py:810
  157.8 26.3 %dense_chain.1 = (bf16[512,768]{1,0:T(8,128)(2,1)}, f32[512,768]{1,0:T(8,128)}, bf16[4,2,384,128]{3,2,1,0:T(8,128)(2,1)}, bf16[512,768]{1,0:T(8,128)(2,1)}, bf16...) custom-call(s32[5]{0:T(128)} %stack.53.place_ref, ...), custom_call_target="tpu_custom_call" | custom-call | flops 22548578304 | bytes 25165824 | tf_op jit(solution)/shard_map/dense_chain/pallas_call | solution.py:512
  184.1 7.6 %dense_weights.3 = bf16[2,768,1856]{2,1,0:T(8,128)(2,1)} custom-call(s32[5]{0:T(128)} %stack.53.place_ref, bf16[512,768]{1,0:T(8,128)(2,1)} %get-tuple-element.83.first_ref, bf16[512,768]{1,0:T(8,128)(2,1)} %get-tuple-element.84.branch_grad_ref, bf16[512,768]{1,0:T(8,128)(2,1)} %get-tuple-element.85.attn_grad_ref, ...), custom_call_target="tpu_custom_call" | custom-call | flops 2919235584 | bytes 10485760 | tf_op jit(solution)/shard_map/dense_weights/pallas_call | solution.py:623
  191.7 3.5 all-to-all-start.2
  195.5 8.2 %dense_weights.2 = (bf16[8,96,1856]{2,1,0:T(8,128)(2,1)}, bf16[8,96,1856]{2,1,0:T(8,128)(2,1)}) custom-call(s32[5]{0:T(128)} %stack.53.place_ref, bf16[512,768]{1,0:T(8,128)(2,1)} %get-tuple-element.83.first_ref, bf16[512,768]{1,0:T(8,128)(2,1)} %get-tuple-element.84.branch_grad_ref, bf16[512,768]{1,0:T(8,128)(2,1)} %get-tuple-element.85.attn_grad_ref, ...), custom_call_target="tpu_custom_call" | custom-call | flops 2919235584 | bytes 10485760 | tf_op jit(solution)/shard_map/dense_weights/pallas_call | solution.py:623
  203.8 11.9 %all-to-all-done.2 = bf16[4,2,384,128]{3,2,1,0:T(8,128)(2,1)S(1)} async-done(((bf16[4,2,384,128]{3,2,1,0:T(8,128)(2,1)}), bf16[4,2,384,128]{3,2,1,0:T(8,128)(2,1)S(1)}, u32[]{:S(2)}, u32[]{:S(2)}) %all-to-all-start.2) | async-done | bytes 786464 | tf_op jit(solution)/shard_map/all_to_all | solution.py:810
  216.6 36.9 %attend_backward.1 = (bf16[1,2048,768]{2,1,0:T(8,128)(2,1)}, f32[1,768]{1,0:T(1,128)}) custom-call(s32[1]{0:T(128)} %bitcast.lane_ref, s32[8]{0:T(128)} %copy-done.2, s32[8]{0:T(128)} %copy-done.3, bf16[2048,768]{1,0:T(8,128)(2,1)} %copy-done.4, s32[2048,1]{1,0:T(8,128)} %copy-done, s32[1,2048]{1,0:T(1,128)} %refs_2_.5, bf16[8,384,128]{2,1,0:T(8,128)(2,1)} %bitcast.94, ...), custom_call_target="tpu_custom_call" | custom-call | flops 51539607552 | bytes 10485760 | tf_op jit(solution)/shard_map/attend_backward/pallas_call | solution.py:303
  253.6 6.2 %convolution_convert_fusion = bf16[2048,768]{1,0:T(8,128)(2,1)} fusion(bf16[768,768]{0,1:T(8,128)(2,1)S(1)} %copy-done.11, bf16[1,2048,768]{2,1,0:T(8,128)(2,1)} %get-tuple-element.95), kind=kOutput, calls=%fused_computation.1 | convolution fusion | flops 2417491968 | bytes 7471104 | tf_op jit(solution)/shard_map/dot_general | solution.py:30
  260.2 1.5 copy-done.6
  261.9 2.6 fusion
  264.5 3.7 %collective-permute-start.9 = (bf16[2,2,96,1856]{3,2,1,0:T(8,128)(2,1)S(1)}, bf16[2,2,96,1856]{3,2,1,0:T(8,128)(2,1)}, u32[]{:S(2)}, u32[]{:S(2)}) collective-permute-start(bf16[2,2,96,1856]{3,2,1,0:T(8,128)(2,1)S(1)} %get-tuple-element.100), channel_id=1, source_target_pairs={{0,8},{4,12},{8,0},{12,4},{16,24},{20,28},{24,16},{28,20},{1,9},{5... | collective-permute-start | bytes 4276232 | tf_op jit(solution)/shard_map/ppermute | solution.py:705
  268.3 6.9 %fusion.16 = f32[768,768]{1,0:T(8,128)} fusion(bf16[2048,768]{1,0:T(8,128)(2,1)} %bitcast.108, bf16[2048,768]{1,0:T(8,128)(2,1)} %bitcast.113), kind=kOutput, calls=%fused_computation.84 | convolution fusion | flops 2415919104 | bytes 8650752 | tf_op jit(solution)/shard_map/dot_general | solution.py:30
  275.2 23.1 %collective-permute-done.9 = bf16[2,2,96,1856]{3,2,1,0:T(8,128)(2,1)} collective-permute-done((bf16[2,2,96,1856]{3,2,1,0:T(8,128)(2,1)S(1)}, bf16[2,2,96,1856]{3,2,1,0:T(8,128)(2,1)}, u32[]{:S(2)}, u32[]{:S(2)}) %collective-permute-start.9) | collective-permute-done | bytes 1425440 | tf_op jit(solution)/shard_map/ppermute | solution.py:705
  298.4 1.7 add_convert_fusion.3
  300.0 1.4 collective-permute-start.10
  301.7 4.9 %collective-permute-done.11 = f32[1,384]{1,0:T(1,128)S(1)} collective-permute-done((f32[1,384]{1,0:T(1,128)S(1)}, f32[1,384]{1,0:T(1,128)S(1)}, u32[]{:S(2)}, u32[]{:S(2)}) %collective-permute-start.11) | collective-permute-done | bytes 1568 | tf_op jit(solution)/shard_map/ppermute | solution.py:705
  306.7 4.7 %collective-permute-done.12 = f32[2,384]{1,0:T(2,128)S(1)} collective-permute-done((f32[2,384]{1,0:T(2,128)S(1)}, f32[2,384]{1,0:T(2,128)S(1)}, u32[]{:S(2)}, u32[]{:S(2)}) %collective-permute-start.12) | collective-permute-done | bytes 3104 | tf_op jit(solution)/shard_map/ppermute | solution.py:705
  312.7 5.1 %collective-permute-done.10 = bf16[1,2,96,1856]{3,2,1,0:T(8,128)(2,1)S(1)} collective-permute-done((bf16[1,2,96,1856]{3,2,1,0:T(8,128)(2,1)S(1)}, bf16[1,2,96,1856]{3,2,1,0:T(8,128)(2,1)S(1)}, u32[]{:S(2)}, u32[]{:S(2)}) %collective-permute-start.10) | collective-permute-done | bytes 712736 | tf_op jit(solution)/shard_map/ppermute | solution.py:705
  318.0 1.7 fusion.6
  319.8 1.4 pad_maximum_fusion
  323.3 2.0 collective-permute-done.13
  329.1 5.5 %collective-permute-done.14 = bf16[2,96,768]{2,1,0:T(8,128)(2,1)S(1)} collective-permute-done((bf16[2,96,768]{2,1,0:T(8,128)(2,1)S(1)}, bf16[2,96,768]{2,1,0:T(8,128)(2,1)S(1)}, u32[]{:S(2)}, u32[]{:S(2)}) %collective-permute-start.14) | collective-permute-done | bytes 294944 | tf_op jit(solution)/shard_map/ppermute | solution.py:705
  334.7 1.8 collective-permute-start.15
  338.5 1.4 collective-permute-done.15
  340.6 1.7 finish_heads.1
  344.5 2.4 add_bitcast_fusion
  346.9 9.7 %reduce-scatter.6.cloned.1.call-done = bf16[1,96,1856]{2,1,0:T(8,128)(2,1)} async-done(((bf16[4,96,1856]{2,1,0:T(8,128)(2,1)}), bf16[1,96,1856]{2,1,0:T(8,128)(2,1)}) %reduce-scatter.6.cloned.1.call-update) | async-done | bytes 356368 | tf_op jit(solution)/shard_map/reduce_scatter | solution.py:894
  356.6 1.9 finish_dense.1
  358.5 1.3 slice_bitcast_fusion
  359.8 2.0 slice_bitcast_fusion.1
  (144 shorter events, 30.1 us)
Async XLA Ops:
  7.2 4.3 %copy-start.18 = (s32[1,512]{1,0:T(1,128)S(1)}, s32[1,512]{1,0:T(1,128)}, u32[]{:S(2)}) copy-start(s32[1,512]{1,0:T(1,128)} %param.22) | copy-start | bytes 6148
  7.2 9.2 %copy-start.17 = (bf16[192,96]{1,0:T(8,128)(2,1)S(1)}, bf16[192,96]{1,0:T(8,128)(2,1)}, u32[]{:S(2)}) copy-start(bf16[192,96]{1,0:T(8,128)(2,1)} %param.28) | copy-start | bytes 110596
  7.2 9.3 %copy-start.16 = (bf16[768,96]{0,1:T(8,128)(2,1)S(1)}, bf16[768,96]{0,1:T(8,128)(2,1)}, u32[]{:S(2)}) copy-start(bf16[768,96]{0,1:T(8,128)(2,1)} %param.30) | copy-start | bytes 442372
  7.2 9.3 %copy-start.15 = (bf16[96,768]{1,0:T(8,128)(2,1)S(1)}, bf16[96,768]{1,0:T(8,128)(2,1)}, u32[]{:S(2)}) copy-start(bf16[96,768]{1,0:T(8,128)(2,1)} %param.29) | copy-start | bytes 442372
  7.2 77.0 %all-gather.5.cloned.1.call-start = ((), (), s32[]{:S(2)}) async-start(), calls=%async_computation.9 | async-start | bytes 3932160 | tf_op jit(solution)/shard_map/all_gather | solution.py:768
  8.0 149.1 %all-gather.7.cloned.1.call-start = ((), (), s32[]{:S(2)}) async-start(), calls=%async_computation.10 | async-start | bytes 6193152 | tf_op jit(solution)/shard_map/all_gather | solution.py:816
  11.0 2.4 collective-permute-start.2
  13.8 12.3 %collective-permute-start.3 = (bf16[192,768]{0,1:T(8,128)(2,1)S(1)}, bf16[192,768]{0,1:T(8,128)(2,1)S(1)}, u32[]{:S(2)}, u32[]{:S(2)}) collective-permute-start(bf16[192,768]{0,1:T(8,128)(2,1)S(1)} %maximum_select_fusion.2), channel_id=1, source_target_pairs={{0,8},{4,12},{8,0},{12,4},{16,24},{20,28},{24,16},{28,20},{1,9},{5... | collective-permute-start | bytes 884744 | tf_op jit(solution)/shard_map/ppermute | solution.py:705
  16.7 25.5 %collective-permute-start = (bf16[1,96,1792]{2,1,0:T(8,128)(2,1)S(1)}, bf16[1,96,1792]{2,1,0:T(8,128)(2,1)S(1)}, u32[]{:S(2)}, u32[]{:S(2)}) collective-permute-start(bf16[1,96,1792]{2,1,0:T(8,128)(2,1)S(1)} %bitcast.86), channel_id=1, source_target_pairs={{0,1},{1,0},{2,3},{3,2},{4,5},{5,4},{6,7},{7,6},{8,9},{9,8},{10,11... | collective-permute-start | bytes 1032200 | tf_op jit(solution)/shard_map/ppermute | solution.py:705
  26.6 15.7 %collective-permute-start.4 = (bf16[384,768]{0,1:T(8,128)(2,1)S(1)}, bf16[384,768]{0,1:T(8,128)(2,1)S(1)}, u32[]{:S(2)}, u32[]{:S(2)}) collective-permute-start(bf16[384,768]{0,1:T(8,128)(2,1)S(1)} %maximum_select_fusion.1), channel_id=1, source_target_pairs={{0,16},{4,20},{8,24},{12,28},{16,0},{20,4},{24,8},{28,12},{1,17},{... | collective-permute-start | bytes 1769480 | tf_op jit(solution)/shard_map/ppermute | solution.py:705
  42.3 13.5 %collective-permute-start.1 = (bf16[2,96,1792]{2,1,0:T(8,128)(2,1)S(1)}, bf16[2,96,1792]{2,1,0:T(8,128)(2,1)}, u32[]{:S(2)}, u32[]{:S(2)}) collective-permute-start(bf16[2,96,1792]{2,1,0:T(8,128)(2,1)S(1)} %pad_maximum_fusion.2), channel_id=1, source_target_pairs={{0,8},{4,12},{8,0},{12,4},{16,24},{20,28},{24,16},{28,20},{1,9},{5... | collective-permute-start | bytes 2064392 | tf_op jit(solution)/shard_map/ppermute | solution.py:705
  43.7 15.0 %copy-start.1 = (s32[1,2048]{1,0:T(1,128)S(1)}, s32[1,2048]{1,0:T(1,128)}, u32[]{:S(2)}) copy-start(s32[1,2048]{1,0:T(1,128)} %refs_2_.5) | copy-start | bytes 24580
  57.0 27.3 %collective-permute-start.5 = (bf16[4,96,1792]{2,1,0:T(8,128)(2,1)S(1)}, bf16[4,96,1792]{2,1,0:T(8,128)(2,1)}, u32[]{:S(2)}, u32[]{:S(2)}) collective-permute-start(bf16[4,96,1792]{2,1,0:T(8,128)(2,1)S(1)} %pad_maximum_fusion.1), channel_id=1, source_target_pairs={{0,16},{4,20},{8,24},{12,28},{16,0},{20,4},{24,8},{28,12},{1,17},{... | collective-permute-start | bytes 4128776 | tf_op jit(solution)/shard_map/ppermute | solution.py:705
  60.4 33.8 %copy-start = (s32[2048,1]{1,0:T(8,128)}, s32[2048,1]{1,0:T(8,128)S(1)}, u32[]{:S(2)}) copy-start(s32[2048,1]{1,0:T(8,128)S(1)} %copy.93.refs_1_) | copy-start | bytes 24580
  60.7 33.5 %copy-start.2 = (s32[8]{0:T(128)}, s32[8]{0:T(128)S(1)}, u32[]{:S(2)}) copy-start(s32[8]{0:T(128)S(1)} %get-tuple-element.74.low_ref) | copy-start | bytes 100
  60.7 33.5 %copy-start.3 = (s32[8]{0:T(128)}, s32[8]{0:T(128)S(1)}, u32[]{:S(2)}) copy-start(s32[8]{0:T(128)S(1)} %get-tuple-element.75.count_ref) | copy-start | bytes 100
  84.3 29.5 %collective-permute-start.6 = (bf16[2,96,1792]{2,1,0:T(8,128)(2,1)S(1)}, bf16[2,96,1792]{2,1,0:T(8,128)(2,1)}, u32[]{:S(2)}, u32[]{:S(2)}) collective-permute-start(bf16[2,96,1792]{2,1,0:T(8,128)(2,1)S(1)} %pad_maximum_fusion.2), channel_id=1, source_target_pairs={{0,2},{1,3},{2,0},{3,1},{4,6},{5,7},{6,4},{7,5},{8,10},{9,11},{10,... | collective-permute-start | bytes 2064392 | tf_op jit(solution)/shard_map/ppermute | solution.py:705
  94.1 16.4 %copy-start.4 = (bf16[2048,768]{1,0:T(8,128)(2,1)}, bf16[2048,768]{1,0:T(8,128)(2,1)S(1)}, u32[]{:S(2)}) copy-start(bf16[2048,768]{1,0:T(8,128)(2,1)S(1)} %add_convert_fusion.refs_0_) | copy-start | bytes 9437188
  110.6 0.6 copy-start.5
  115.0 22.7 %all-to-all-start = ((bf16[4,384,128]{2,1,0:T(8,128)(2,1)}), bf16[4,384,128]{2,1,0:T(8,128)(2,1)S(1)}, u32[]{:S(2)}, u32[]{:S(2)}) async-start(bf16[4,384,128]{2,1,0:T(8,128)(2,1)} %get-tuple-element.92.refs_4_), calls=%async_computation | async-start | bytes 786432 | tf_op jit(solution)/shard_map/all_to_all | solution.py:810
  119.8 17.9 %copy-start.13 = (bf16[8,96,1792]{2,1,0:T(8,128)(2,1)S(1)}, bf16[8,96,1792]{2,1,0:T(8,128)(2,1)}, u32[]{:S(2)}) copy-start(bf16[8,96,1792]{2,1,0:T(8,128)(2,1)} %constant_dynamic-update-slice_fusion.1) | copy-start | bytes 8257540
  137.7 2.0 copy-start.9
  137.7 7.0 %copy-start.21 = (bf16[768]{0:T(1024)(128)(2,1)S(1)}, bf16[768]{0:T(1024)(128)(2,1)}, u32[]{:S(2)}) copy-start(bf16[768]{0:T(1024)(128)(2,1)} %param.33) | copy-start | bytes 4612
  137.7 11.1 %copy-start.19 = (bf16[3072]{0:T(1024)(128)(2,1)S(1)}, bf16[3072]{0:T(1024)(128)(2,1)}, u32[]{:S(2)}) copy-start(bf16[3072]{0:T(1024)(128)(2,1)} %param.34) | copy-start | bytes 18436
  139.6 17.4 %copy-start.14 = (bf16[8,96,1792]{2,1,0:T(8,128)(2,1)}, bf16[8,96,1792]{2,1,0:T(8,128)(2,1)S(1)}, u32[]{:S(2)}) copy-start(bf16[8,96,1792]{2,1,0:T(8,128)(2,1)S(1)} %constant_dynamic-update-slice_fusion.refs_2_) | copy-start | bytes 8257540
  139.6 17.4 %collective-permute-start.7 = (bf16[8,96,1792]{2,1,0:T(8,128)(2,1)S(1)}, bf16[8,96,1792]{2,1,0:T(8,128)(2,1)}, u32[]{:S(2)}, u32[]{:S(2)}) collective-permute-start(bf16[8,96,1792]{2,1,0:T(8,128)(2,1)S(1)} %constant_dynamic-update-slice_fusion.refs_2_), channel_id=1, source_target_pairs={{0,4},{4,0},{8,12},{12,8},{16,20},{20,16},{24,28},{28,24},{1,5},{5... | collective-permute-start | bytes 8257544 | tf_op jit(solution)/shard_map/ppermute | solution.py:705
  139.7 17.3 %all-to-all-start.1 = ((bf16[4,384,128]{2,1,0:T(8,128)(2,1)}), bf16[4,384,128]{2,1,0:T(8,128)(2,1)S(1)}, u32[]{:S(2)}, u32[]{:S(2)}) async-start(bf16[4,384,128]{2,1,0:T(8,128)(2,1)} %get-tuple-element.78.refs_5_), calls=%async_computation.1 | async-start | bytes 786432 | tf_op jit(solution)/shard_map/all_to_all | solution.py:810
  144.7 173.3 %reduce-scatter.4.cloned.1.call-start = ((), (), s32[]{:S(2)}) async-start(), calls=%async_computation.6 | async-start | bytes 6635520 | tf_op jit(solution)/shard_map/reduce_scatter | solution.py:861
  157.0 0.8 copy-start.10
  191.7 24.0 %all-to-all-start.2 = ((bf16[4,2,384,128]{3,2,1,0:T(8,128)(2,1)}), bf16[4,2,384,128]{3,2,1,0:T(8,128)(2,1)S(1)}, u32[]{:S(2)}, u32[]{:S(2)}) async-start(bf16[4,2,384,128]{3,2,1,0:T(8,128)(2,1)} %get-tuple-element.91), calls=%async_computation.2 | async-start | bytes 1572864 | tf_op jit(solution)/shard_map/all_to_all | solution.py:810
  195.2 149.2 %reduce-scatter.8.cloned.1.call-start = ((), (), s32[]{:S(2)}) async-start(), calls=%async_computation.8 | async-start | bytes 3932160 | tf_op jit(solution)/shard_map/reduce_scatter | solution.py:873
  203.7 58.2 %collective-permute-start.8 = (bf16[4,2,96,1856]{3,2,1,0:T(8,128)(2,1)}, bf16[4,2,96,1856]{3,2,1,0:T(8,128)(2,1)}, u32[]{:S(2)}, u32[]{:S(2)}) collective-permute-start(bf16[4,2,96,1856]{3,2,1,0:T(8,128)(2,1)} %bitcast.109), channel_id=1, source_target_pairs={{0,4},{4,0},{8,12},{12,8},{16,20},{20,16},{24,28},{28,24},{1,5},{5... | collective-permute-start | bytes 8552456 | tf_op jit(solution)/shard_map/ppermute | solution.py:705
  215.7 0.9 copy-start.12
  216.6 37.0 %copy-start.11 = (bf16[768,768]{0,1:T(8,128)(2,1)S(1)}, bf16[768,768]{0,1:T(8,128)(2,1)}, u32[]{:S(2)}) copy-start(bf16[768,768]{0,1:T(8,128)(2,1)} %maximum_select_fusion) | copy-start | bytes 3538948
  259.8 1.8 copy-start.6
  259.8 96.7 %reduce-scatter.6.cloned.1.call-start = ((), (), s32[]{:S(2)}) async-start(), calls=%async_computation.7 | async-start | bytes 1843200 | tf_op jit(solution)/shard_map/reduce_scatter | solution.py:894
  261.9 6.3 %copy-start.20 = (f32[1,768]{1,0:T(1,128)S(1)}, f32[1,768]{1,0:T(1,128)}, u32[]{:S(2)}) copy-start(f32[1,768]{1,0:T(1,128)} %get-tuple-element.112) | copy-start | bytes 9220
  264.5 33.9 %collective-permute-start.9 = (bf16[2,2,96,1856]{3,2,1,0:T(8,128)(2,1)S(1)}, bf16[2,2,96,1856]{3,2,1,0:T(8,128)(2,1)}, u32[]{:S(2)}, u32[]{:S(2)}) collective-permute-start(bf16[2,2,96,1856]{3,2,1,0:T(8,128)(2,1)S(1)} %get-tuple-element.100), channel_id=1, source_target_pairs={{0,8},{4,12},{8,0},{12,4},{16,24},{20,28},{24,16},{28,20},{1,9},{5... | collective-permute-start | bytes 4276232 | tf_op jit(solution)/shard_map/ppermute | solution.py:705
  300.0 17.8 %collective-permute-start.10 = (bf16[1,2,96,1856]{3,2,1,0:T(8,128)(2,1)S(1)}, bf16[1,2,96,1856]{3,2,1,0:T(8,128)(2,1)S(1)}, u32[]{:S(2)}, u32[]{:S(2)}) collective-permute-start(bf16[1,2,96,1856]{3,2,1,0:T(8,128)(2,1)S(1)} %get-tuple-element.105), channel_id=1, source_target_pairs={{0,16},{4,20},{8,24},{12,28},{16,0},{20,4},{24,8},{28,12},{1,17},{... | collective-permute-start | bytes 2138120 | tf_op jit(solution)/shard_map/ppermute | solution.py:705
  301.7 4.9 %collective-permute-start.11 = (f32[1,384]{1,0:T(1,128)S(1)}, f32[1,384]{1,0:T(1,128)S(1)}, u32[]{:S(2)}, u32[]{:S(2)}) collective-permute-start(f32[1,384]{1,0:T(1,128)S(1)} %pad_maximum_fusion.6), channel_id=1, source_target_pairs={{0,1},{1,0},{2,3},{3,2},{4,5},{5,4},{6,7},{7,6},{8,9},{9,8},{10,11... | collective-permute-start | bytes 4616 | tf_op jit(solution)/shard_map/ppermute | solution.py:705
  306.7 4.7 %collective-permute-start.12 = (f32[2,384]{1,0:T(2,128)S(1)}, f32[2,384]{1,0:T(2,128)S(1)}, u32[]{:S(2)}, u32[]{:S(2)}) collective-permute-start(f32[2,384]{1,0:T(2,128)S(1)} %maximum_select_fusion.4), channel_id=1, source_target_pairs={{0,2},{1,3},{2,0},{3,1},{4,6},{5,7},{6,4},{7,5},{8,10},{9,11},{10,... | collective-permute-start | bytes 9224 | tf_op jit(solution)/shard_map/ppermute | solution.py:705
  319.8 2.2 copy-start.7
  323.2 2.1 collective-permute-start.13
  325.4 19.0 %copy-start.8 = (f32[512,768]{1,0:T(8,128)S(1)}, f32[512,768]{1,0:T(8,128)}, u32[]{:S(2)}) copy-start(f32[512,768]{1,0:T(8,128)} %get-tuple-element.109) | copy-start | bytes 4718596
  325.5 9.1 %collective-permute-start.14 = (bf16[2,96,768]{2,1,0:T(8,128)(2,1)S(1)}, bf16[2,96,768]{2,1,0:T(8,128)(2,1)S(1)}, u32[]{:S(2)}, u32[]{:S(2)}) collective-permute-start(bf16[2,96,768]{2,1,0:T(8,128)(2,1)S(1)} %dynamic-slice_bitcast_fusion.1), channel_id=1, source_target_pairs={{0,8},{4,12},{8,0},{12,4},{16,24},{20,28},{24,16},{28,20},{1,9},{5... | collective-permute-start | bytes 884744 | tf_op jit(solution)/shard_map/ppermute | solution.py:705
  334.7 5.2 %collective-permute-start.15 = (bf16[1,96,768]{2,1,0:T(8,128)(2,1)S(1)}, bf16[1,96,768]{2,1,0:T(8,128)(2,1)S(1)}, u32[]{:S(2)}, u32[]{:S(2)}) collective-permute-start(bf16[1,96,768]{2,1,0:T(8,128)(2,1)S(1)} %constant_dynamic-slice_fusion), channel_id=1, source_target_pairs={{0,16},{4,20},{8,24},{12,28},{16,0},{20,4},{24,8},{28,12},{1,17},{... | collective-permute-start | bytes 442376 | tf_op jit(solution)/shard_map/ppermute | solution.py:705
Sparse Core Ops, SparseCore 0:
  9.6 68.1 all-gather.4
  113.9 42.7 all-gather.6
  191.8 62.9 reduce-scatter.3
  260.0 60.5 reduce-scatter.7
  322.7 33.7 reduce-scatter.5

commit v19 on v18

--- a/solution.py
+++ b/solution.py
@@ -326,7 +326,7 @@
             ],
         ),
         compiler_params=pltpu.CompilerParams(
-            dimension_semantics=("arbitrary",), vmem_limit_bytes=VMEM_LIMIT
+            dimension_semantics=("arbitrary",), vmem_limit_bytes=28 << 20
         ),
         cost_estimate=pl.CostEstimate(
             flops=heads * seq_len * seq_len * 4096,

time: 371 us -> 367 us (0.989)
  starting transfers between devices: 35.3 us -> 31.4 us
    ppermute x16, waiting for transfers between devices: 106 us -> 111 us  [swap(): return lax.ppermute(value, axis, [(i, i ^ bit) for i in range(size)])]
    ppermute x16, starting transfers between devices: 21.4 us -> 17.5 us  [swap(): return lax.ppermute(value, axis, [(i, i ^ bit) for i in range(size)])]
    unnamed x50 -> x58, local copies, waits for them, and re-layouts: 8.77 us -> 11 us
where the time goes in v19:
time: 367 us; the launch traced here: 365 us
  waiting for transfers between devices  134 us (37%)
  Pallas kernels  114 us (31%)
  starting transfers between devices  31.4 us (9%)
  local copies, waits for them, and re-layouts  27.3 us (7%)
  other arithmetic  24.3 us (7%)
  between operations  18.9 us (5%)
  matrix products  14.9 us (4%)
    ppermute x16, waiting for transfers between devices, swap(): return lax.ppermute(value, axis, [(i, i ^ bit) for i in range(size)])  111 us
    pallas_call x2, Pallas kernels, run_forward(): pl.pallas_call(functools.partial(attend_forward, which), out_shape=(jax.S...  34.9 us
    pallas_call x1, Pallas kernels, run_backward(): pl.pallas_call(functools.partial(attend_backward, halves, len(qkv)), out_...  33.2 us
    pallas_call x1, Pallas kernels, run_dense(): pl.pallas_call(functools.partial(dense_chain, marks, halves, total_tokens...  26.3 us
    ppermute x16, starting transfers between devices, swap(): return lax.ppermute(value, axis, [(i, i ^ bit) for i in range(size)])  17.5 us
    pallas_call x2, Pallas kernels, run_weights(): pl.pallas_call(functools.partial(dense_weights, tuple((turns for _, turns...  16.4 us
    all_to_all x3, waiting for transfers between devices, exchange(): return lax.all_to_all(packed_blocks, 'tensor', 0, 0)  15.5 us
    dot_general x3, matrix products, dot(): lax.dot_general(left_side, right_side, dims, preferred_element_type=F32)  14.9 us
  transfers between devices with their start and end apart: 24, of which 15 were waited for; matrix products, arithmetic and copies ran while one was open for 15% of the time, Pallas kernels for 22%

profile of v19, /device:TPU:0, one launch (start us, length us, event | category | flops | bytes accessed | tf_op | source)
XLA Modules:
  0.0 365.3 jit_solution(11410594082939075494)
XLA Ops:
  13.8 2.6 collective-permute-start.3
  16.7 1.6 collective-permute-start
  18.3 7.8 %collective-permute-done.3 = bf16[192,768]{0,1:T(8,128)(2,1)S(1)} collective-permute-done((bf16[192,768]{0,1:T(8,128)(2,1)S(1)}, bf16[192,768]{0,1:T(8,128)(2,1)S(1)}, u32[]{:S(2)}, u32[]{:S(2)}) %collective-permute-start.3) | collective-permute-done | bytes 294944 | tf_op jit(solution)/shard_map/ppermute | solution.py:705
  26.6 1.8 collective-permute-start.4
  28.5 13.8 %collective-permute-done = bf16[1,96,1792]{2,1,0:T(8,128)(2,1)S(1)} collective-permute-done((bf16[1,96,1792]{2,1,0:T(8,128)(2,1)S(1)}, bf16[1,96,1792]{2,1,0:T(8,128)(2,1)S(1)}, u32[]{:S(2)}, u32[]{:S(2)}) %collective-permute-start) | collective-permute-done | bytes 344096 | tf_op jit(solution)/shard_map/ppermute | solution.py:705
  43.7 12.1 %collective-permute-done.1 = bf16[2,96,1792]{2,1,0:T(8,128)(2,1)} collective-permute-done((bf16[2,96,1792]{2,1,0:T(8,128)(2,1)S(1)}, bf16[2,96,1792]{2,1,0:T(8,128)(2,1)}, u32[]{:S(2)}, u32[]{:S(2)}) %collective-permute-start.1) | collective-permute-done | bytes 688160 | tf_op jit(solution)/shard_map/ppermute | solution.py:705
  57.0 1.7 collective-permute-start.5
  60.7 23.6 %collective-permute-done.5 = bf16[4,96,1792]{2,1,0:T(8,128)(2,1)} collective-permute-done((bf16[4,96,1792]{2,1,0:T(8,128)(2,1)S(1)}, bf16[4,96,1792]{2,1,0:T(8,128)(2,1)}, u32[]{:S(2)}, u32[]{:S(2)}) %collective-permute-start.5) | collective-permute-done | bytes 1376288 | tf_op jit(solution)/shard_map/ppermute | solution.py:705
  84.3 5.0 %collective-permute-start.6 = (bf16[2,96,1792]{2,1,0:T(8,128)(2,1)S(1)}, bf16[2,96,1792]{2,1,0:T(8,128)(2,1)}, u32[]{:S(2)}, u32[]{:S(2)}) collective-permute-start(bf16[2,96,1792]{2,1,0:T(8,128)(2,1)S(1)} %pad_maximum_fusion.2), channel_id=1, source_target_pairs={{0,2},{1,3},{2,0},{3,1},{4,6},{5,7},{6,4},{7,5},{8,10},{9,11},{10,... | collective-permute-start | bytes 2064392 | tf_op jit(solution)/shard_map/ppermute | solution.py:705
  89.3 4.9 %add_convert_fusion.refs_0_ = bf16[2048,768]{1,0:T(8,128)(2,1)S(1)} fusion(bf16[2048,768]{1,0:T(8,128)(2,1)} %bitcast.108, bf16[768,768]{0,1:T(8,128)(2,1)} %maximum_select_fusion, f32[768]{0:T(1024)S(1)} %add.115), kind=kOutput, calls=%fused_computation | convolution fusion | flops 2419064832 | bytes 7474176 | tf_op jit(solution)/shard_map/dot_general | solution.py:30
  94.2 15.1 %attend_forward.2 = (bf16[4,384,128]{2,1,0:T(8,128)(2,1)}, f32[3,1,1024]{2,1,0:T(1,128)S(1)}) custom-call(s32[1]{0:T(128)} %bitcast.lane_ref, s32[8]{0:T(128)S(1)} %get-tuple-element.74.low_ref, s32[8]{0:T(128)S(1)} %get-tuple-element.75.count_ref, bf16[2048,768]{1,0:T(8,128)(2,1)S(1)} %add_convert_fusion.refs_0_, s32[2048,1]{1,0:T(8,128)S(1)} %copy.93.refs_1_, ...), custom_call_target="tpu_custom_call" | custom-call | flops 12884901888 | bytes 5242880 | tf_op jit(solution)/shard_map/attend_forward/pallas_call | solution.py:259
  109.3 4.4 %collective-permute-done.6 = bf16[2,96,1792]{2,1,0:T(8,128)(2,1)} collective-permute-done((bf16[2,96,1792]{2,1,0:T(8,128)(2,1)S(1)}, bf16[2,96,1792]{2,1,0:T(8,128)(2,1)}, u32[]{:S(2)}, u32[]{:S(2)}) %collective-permute-start.6) | collective-permute-done | bytes 688160 | tf_op jit(solution)/shard_map/ppermute | solution.py:705
  115.0 4.8 %all-to-all-start = ((bf16[4,384,128]{2,1,0:T(8,128)(2,1)}), bf16[4,384,128]{2,1,0:T(8,128)(2,1)S(1)}, u32[]{:S(2)}, u32[]{:S(2)}) async-start(bf16[4,384,128]{2,1,0:T(8,128)(2,1)} %get-tuple-element.92.refs_4_), calls=%async_computation | async-start | bytes 786432 | tf_op jit(solution)/shard_map/all_to_all | solution.py:810
  119.8 19.8 %attend_forward.3 = (bf16[4,384,128]{2,1,0:T(8,128)(2,1)}, f32[3,1,1024]{2,1,0:T(1,128)}) custom-call(s32[1]{0:T(128)} %bitcast.lane_ref, s32[8]{0:T(128)} %copy-done.4, s32[8]{0:T(128)} %copy-done.6, bf16[2048,768]{1,0:T(8,128)(2,1)} %copy-done.10, s32[2048,1]{1,0:T(8,128)} %copy-done, s32[1,2048]{1,0:T(1,128)} %refs_2_.5), custom_call_target="tpu_custom_call" | custom-call | flops 12884901888 | bytes 5242880 | tf_op jit(solution)/shard_map/attend_forward/pallas_call | solution.py:259
  139.6 1.6 constant_dynamic-update-slice_fusion.refs_2_
  141.3 5.1 %all-to-all-start.1 = ((bf16[4,384,128]{2,1,0:T(8,128)(2,1)}), bf16[4,384,128]{2,1,0:T(8,128)(2,1)S(1)}, u32[]{:S(2)}, u32[]{:S(2)}) async-start(bf16[4,384,128]{2,1,0:T(8,128)(2,1)} %get-tuple-element.78.refs_5_), calls=%async_computation.1 | async-start | bytes 786432 | tf_op jit(solution)/shard_map/all_to_all | solution.py:810
  151.2 1.3 reshape.172
  153.9 4.8 %all-to-all-done.1.refs_1_ = bf16[4,384,128]{2,1,0:T(8,128)(2,1)S(1)} async-done(((bf16[4,384,128]{2,1,0:T(8,128)(2,1)}), bf16[4,384,128]{2,1,0:T(8,128)(2,1)S(1)}, u32[]{:S(2)}, u32[]{:S(2)}) %all-to-all-start.1) | async-done | bytes 393248 | tf_op jit(solution)/shard_map/all_to_all | solution.py:810
  159.5 26.3 %dense_chain.1 = (bf16[512,768]{1,0:T(8,128)(2,1)}, f32[512,768]{1,0:T(8,128)}, bf16[4,2,384,128]{3,2,1,0:T(8,128)(2,1)}, bf16[512,768]{1,0:T(8,128)(2,1)}, bf16...) custom-call(s32[5]{0:T(128)} %stack.53.place_ref, ...), custom_call_target="tpu_custom_call" | custom-call | flops 22548578304 | bytes 25165824 | tf_op jit(solution)/shard_map/dense_chain/pallas_call | solution.py:512
  185.8 7.6 %dense_weights.3 = bf16[2,768,1856]{2,1,0:T(8,128)(2,1)} custom-call(s32[5]{0:T(128)} %stack.53.place_ref, bf16[512,768]{1,0:T(8,128)(2,1)} %get-tuple-element.83.first_ref, bf16[512,768]{1,0:T(8,128)(2,1)} %get-tuple-element.84.branch_grad_ref, bf16[512,768]{1,0:T(8,128)(2,1)} %get-tuple-element.85.attn_grad_ref, ...), custom_call_target="tpu_custom_call" | custom-call | flops 2919235584 | bytes 10485760 | tf_op jit(solution)/shard_map/dense_weights/pallas_call | solution.py:623
  193.4 3.5 all-to-all-start.2
  197.3 8.8 %dense_weights.2 = (bf16[8,96,1856]{2,1,0:T(8,128)(2,1)}, bf16[8,96,1856]{2,1,0:T(8,128)(2,1)}) custom-call(s32[5]{0:T(128)} %stack.53.place_ref, bf16[512,768]{1,0:T(8,128)(2,1)} %get-tuple-element.83.first_ref, bf16[512,768]{1,0:T(8,128)(2,1)} %get-tuple-element.84.branch_grad_ref, bf16[512,768]{1,0:T(8,128)(2,1)} %get-tuple-element.85.attn_grad_ref, ...), custom_call_target="tpu_custom_call" | custom-call | flops 2919235584 | bytes 10485760 | tf_op jit(solution)/shard_map/dense_weights/pallas_call | solution.py:623
  206.1 10.7 %all-to-all-done.2 = bf16[4,2,384,128]{3,2,1,0:T(8,128)(2,1)S(1)} async-done(((bf16[4,2,384,128]{3,2,1,0:T(8,128)(2,1)}), bf16[4,2,384,128]{3,2,1,0:T(8,128)(2,1)S(1)}, u32[]{:S(2)}, u32[]{:S(2)}) %all-to-all-start.2) | async-done | bytes 786464 | tf_op jit(solution)/shard_map/all_to_all | solution.py:810
  216.9 1.9 copy-done.11
  218.8 33.2 %attend_backward.1 = (bf16[1,2048,768]{2,1,0:T(8,128)(2,1)S(1)}, f32[1,768]{1,0:T(1,128)S(1)}) custom-call(s32[1]{0:T(128)} %bitcast.lane_ref, s32[8]{0:T(128)S(1)} %copy-done.5, s32[8]{0:T(128)S(1)} %copy-done.7, bf16[2048,768]{1,0:T(8,128)(2,1)S(1)} %copy-done.11, s32[2048,1]{1,0:T(8,128)S(1)} %copy-done.1, s32[1,2048]{1,0:T(1,128)S(1)} %copy-done.3, ...), custom_call_target="tpu_custom_call" | custom-call | flops 51539607552 | bytes 10485760 | tf_op jit(solution)/shard_map/attend_backward/pallas_call | solution.py:303
  252.0 1.6 copy-done.8
  253.7 4.0 %convolution_convert_fusion = bf16[2048,768]{1,0:T(8,128)(2,1)} fusion(bf16[768,768]{0,1:T(8,128)(2,1)S(1)} %copy-done.19, bf16[1,2048,768]{2,1,0:T(8,128)(2,1)S(1)} %get-tuple-element.95), kind=kOutput, calls=%fused_computation.1 | convolution fusion | flops 2417491968 | bytes 7471104 | tf_op jit(solution)/shard_map/dot_general | solution.py:30
  257.7 1.8 copy-done.14
  259.7 4.6 %fusion = (bf16[2,2,96,1856]{3,2,1,0:T(8,128)(2,1)}, bf16[2,2,96,1856]{3,2,1,0:T(8,128)(2,1)}) fusion(bf16[2,2,96,1856]{3,2,1,0:T(8,128)(2,1)S(1)} %bitcast.84, bf16[4,2,96,1856]{3,2,1,0:T(8,128)(2,1)} %collective-permute-done.8, bf16[2,2,96,1856]{3,2,1,0:T(8,128)(2,1)S(1)} %bitcast.85), kind=kLoop, calls=%fused_computation.3 | loop fusion | flops 5701632 | bytes 8552448 | tf_op jit(solution)/shard_map/convert_element_type | solution.py:727
  264.4 6.1 %fusion.16 = f32[768,768]{1,0:T(8,128)} fusion(bf16[2048,768]{1,0:T(8,128)(2,1)} %bitcast.109, bf16[2048,768]{1,0:T(8,128)(2,1)S(1)} %bitcast.83), kind=kOutput, calls=%fused_computation.84 | convolution fusion | flops 2415919104 | bytes 8650752 | tf_op jit(solution)/shard_map/dot_general | solution.py:30
  270.5 26.1 %collective-permute-done.9 = bf16[2,2,96,1856]{3,2,1,0:T(8,128)(2,1)} collective-permute-done((bf16[2,2,96,1856]{3,2,1,0:T(8,128)(2,1)}, bf16[2,2,96,1856]{3,2,1,0:T(8,128)(2,1)}, u32[]{:S(2)}, u32[]{:S(2)}) %collective-permute-start.9) | collective-permute-done | bytes 1425440 | tf_op jit(solution)/shard_map/ppermute | solution.py:705
  296.6 1.7 add_convert_fusion.3
  298.3 2.1 collective-permute-start.10
  300.7 5.4 %collective-permute-done.11 = f32[1,384]{1,0:T(1,128)S(1)} collective-permute-done((f32[1,384]{1,0:T(1,128)S(1)}, f32[1,384]{1,0:T(1,128)S(1)}, u32[]{:S(2)}, u32[]{:S(2)}) %collective-permute-start.11) | collective-permute-done | bytes 1568 | tf_op jit(solution)/shard_map/ppermute | solution.py:705
  306.2 4.7 %collective-permute-done.12 = f32[2,384]{1,0:T(2,128)S(1)} collective-permute-done((f32[2,384]{1,0:T(2,128)S(1)}, f32[2,384]{1,0:T(2,128)S(1)}, u32[]{:S(2)}, u32[]{:S(2)}) %collective-permute-start.12) | collective-permute-done | bytes 3104 | tf_op jit(solution)/shard_map/ppermute | solution.py:705
  312.2 3.7 %collective-permute-done.10 = bf16[1,2,96,1856]{3,2,1,0:T(8,128)(2,1)S(1)} collective-permute-done((bf16[1,2,96,1856]{3,2,1,0:T(8,128)(2,1)S(1)}, bf16[1,2,96,1856]{3,2,1,0:T(8,128)(2,1)S(1)}, u32[]{:S(2)}, u32[]{:S(2)}) %collective-permute-start.10) | collective-permute-done | bytes 712736 | tf_op jit(solution)/shard_map/ppermute | solution.py:705
  316.1 1.7 fusion.6
  317.9 1.4 pad_maximum_fusion
  321.4 2.0 collective-permute-done.13
  326.5 6.1 %collective-permute-done.14 = bf16[2,96,768]{2,1,0:T(8,128)(2,1)S(1)} collective-permute-done((bf16[2,96,768]{2,1,0:T(8,128)(2,1)S(1)}, bf16[2,96,768]{2,1,0:T(8,128)(2,1)S(1)}, u32[]{:S(2)}, u32[]{:S(2)}) %collective-permute-start.14) | collective-permute-done | bytes 294944 | tf_op jit(solution)/shard_map/ppermute | solution.py:705
  332.8 1.8 collective-permute-start.15
  336.6 1.4 collective-permute-done.15
  338.7 1.7 finish_heads.1
  342.5 2.4 add_bitcast_fusion
  344.9 6.9 %reduce-scatter.6.cloned.1.call-done = bf16[1,96,1856]{2,1,0:T(8,128)(2,1)} async-done(((bf16[4,96,1856]{2,1,0:T(8,128)(2,1)}), bf16[1,96,1856]{2,1,0:T(8,128)(2,1)}) %reduce-scatter.6.cloned.1.call-update) | async-done | bytes 356368 | tf_op jit(solution)/shard_map/reduce_scatter | solution.py:894
  351.8 1.9 finish_dense.1
  353.7 1.3 slice_bitcast_fusion
  355.0 2.0 slice_bitcast_fusion.1
  (152 shorter events, 30.2 us)
Async XLA Ops:
  7.2 4.3 %copy-start.25 = (s32[1,512]{1,0:T(1,128)S(1)}, s32[1,512]{1,0:T(1,128)}, u32[]{:S(2)}) copy-start(s32[1,512]{1,0:T(1,128)} %param.22) | copy-start | bytes 6148
  7.2 9.2 %copy-start.24 = (bf16[192,96]{1,0:T(8,128)(2,1)S(1)}, bf16[192,96]{1,0:T(8,128)(2,1)}, u32[]{:S(2)}) copy-start(bf16[192,96]{1,0:T(8,128)(2,1)} %param.28) | copy-start | bytes 110596
  7.2 9.3 %copy-start.23 = (bf16[768,96]{0,1:T(8,128)(2,1)S(1)}, bf16[768,96]{0,1:T(8,128)(2,1)}, u32[]{:S(2)}) copy-start(bf16[768,96]{0,1:T(8,128)(2,1)} %param.30) | copy-start | bytes 442372
  7.2 9.3 %copy-start.22 = (bf16[96,768]{1,0:T(8,128)(2,1)S(1)}, bf16[96,768]{1,0:T(8,128)(2,1)}, u32[]{:S(2)}) copy-start(bf16[96,768]{1,0:T(8,128)(2,1)} %param.29) | copy-start | bytes 442372
  7.2 77.0 %all-gather.5.cloned.1.call-start = ((), (), s32[]{:S(2)}) async-start(), calls=%async_computation.9 | async-start | bytes 3932160 | tf_op jit(solution)/shard_map/all_gather | solution.py:768
  8.0 150.8 %all-gather.7.cloned.1.call-start = ((), (), s32[]{:S(2)}) async-start(), calls=%async_computation.10 | async-start | bytes 6193152 | tf_op jit(solution)/shard_map/all_gather | solution.py:816
  11.0 2.4 collective-permute-start.2
  13.8 12.3 %collective-permute-start.3 = (bf16[192,768]{0,1:T(8,128)(2,1)S(1)}, bf16[192,768]{0,1:T(8,128)(2,1)S(1)}, u32[]{:S(2)}, u32[]{:S(2)}) collective-permute-start(bf16[192,768]{0,1:T(8,128)(2,1)S(1)} %maximum_select_fusion.2), channel_id=1, source_target_pairs={{0,8},{4,12},{8,0},{12,4},{16,24},{20,28},{24,16},{28,20},{1,9},{5... | collective-permute-start | bytes 884744 | tf_op jit(solution)/shard_map/ppermute | solution.py:705
  16.7 25.5 %collective-permute-start = (bf16[1,96,1792]{2,1,0:T(8,128)(2,1)S(1)}, bf16[1,96,1792]{2,1,0:T(8,128)(2,1)S(1)}, u32[]{:S(2)}, u32[]{:S(2)}) collective-permute-start(bf16[1,96,1792]{2,1,0:T(8,128)(2,1)S(1)} %bitcast.88), channel_id=1, source_target_pairs={{0,1},{1,0},{2,3},{3,2},{4,5},{5,4},{6,7},{7,6},{8,9},{9,8},{10,11... | collective-permute-start | bytes 1032200 | tf_op jit(solution)/shard_map/ppermute | solution.py:705
  26.6 15.7 %collective-permute-start.4 = (bf16[384,768]{0,1:T(8,128)(2,1)S(1)}, bf16[384,768]{0,1:T(8,128)(2,1)S(1)}, u32[]{:S(2)}, u32[]{:S(2)}) collective-permute-start(bf16[384,768]{0,1:T(8,128)(2,1)S(1)} %maximum_select_fusion.1), channel_id=1, source_target_pairs={{0,16},{4,20},{8,24},{12,28},{16,0},{20,4},{24,8},{28,12},{1,17},{... | collective-permute-start | bytes 1769480 | tf_op jit(solution)/shard_map/ppermute | solution.py:705
  42.3 13.5 %collective-permute-start.1 = (bf16[2,96,1792]{2,1,0:T(8,128)(2,1)S(1)}, bf16[2,96,1792]{2,1,0:T(8,128)(2,1)}, u32[]{:S(2)}, u32[]{:S(2)}) collective-permute-start(bf16[2,96,1792]{2,1,0:T(8,128)(2,1)S(1)} %pad_maximum_fusion.2), channel_id=1, source_target_pairs={{0,8},{4,12},{8,0},{12,4},{16,24},{20,28},{24,16},{28,20},{1,9},{5... | collective-permute-start | bytes 2064392 | tf_op jit(solution)/shard_map/ppermute | solution.py:705
  43.7 15.0 %copy-start.2 = (s32[1,2048]{1,0:T(1,128)S(1)}, s32[1,2048]{1,0:T(1,128)}, u32[]{:S(2)}) copy-start(s32[1,2048]{1,0:T(1,128)} %refs_2_.5) | copy-start | bytes 24580
  57.0 27.3 %collective-permute-start.5 = (bf16[4,96,1792]{2,1,0:T(8,128)(2,1)S(1)}, bf16[4,96,1792]{2,1,0:T(8,128)(2,1)}, u32[]{:S(2)}, u32[]{:S(2)}) collective-permute-start(bf16[4,96,1792]{2,1,0:T(8,128)(2,1)S(1)} %pad_maximum_fusion.1), channel_id=1, source_target_pairs={{0,16},{4,20},{8,24},{12,28},{16,0},{20,4},{24,8},{28,12},{1,17},{... | collective-permute-start | bytes 4128776 | tf_op jit(solution)/shard_map/ppermute | solution.py:705
  60.4 33.8 %copy-start = (s32[2048,1]{1,0:T(8,128)}, s32[2048,1]{1,0:T(8,128)S(1)}, u32[]{:S(2)}) copy-start(s32[2048,1]{1,0:T(8,128)S(1)} %copy.93.refs_1_) | copy-start | bytes 24580
  60.7 33.5 %copy-start.4 = (s32[8]{0:T(128)}, s32[8]{0:T(128)S(1)}, u32[]{:S(2)}) copy-start(s32[8]{0:T(128)S(1)} %get-tuple-element.74.low_ref) | copy-start | bytes 100
  60.7 33.5 %copy-start.6 = (s32[8]{0:T(128)}, s32[8]{0:T(128)S(1)}, u32[]{:S(2)}) copy-start(s32[8]{0:T(128)S(1)} %get-tuple-element.75.count_ref) | copy-start | bytes 100
  84.3 29.5 %collective-permute-start.6 = (bf16[2,96,1792]{2,1,0:T(8,128)(2,1)S(1)}, bf16[2,96,1792]{2,1,0:T(8,128)(2,1)}, u32[]{:S(2)}, u32[]{:S(2)}) collective-permute-start(bf16[2,96,1792]{2,1,0:T(8,128)(2,1)S(1)} %pad_maximum_fusion.2), channel_id=1, source_target_pairs={{0,2},{1,3},{2,0},{3,1},{4,6},{5,7},{6,4},{7,5},{8,10},{9,11},{10,... | collective-permute-start | bytes 2064392 | tf_op jit(solution)/shard_map/ppermute | solution.py:705
  94.1 15.2 %copy-start.10 = (bf16[2048,768]{1,0:T(8,128)(2,1)}, bf16[2048,768]{1,0:T(8,128)(2,1)S(1)}, u32[]{:S(2)}) copy-start(bf16[2048,768]{1,0:T(8,128)(2,1)S(1)} %add_convert_fusion.refs_0_) | copy-start | bytes 9437188
  115.0 24.6 %all-to-all-start = ((bf16[4,384,128]{2,1,0:T(8,128)(2,1)}), bf16[4,384,128]{2,1,0:T(8,128)(2,1)S(1)}, u32[]{:S(2)}, u32[]{:S(2)}) async-start(bf16[4,384,128]{2,1,0:T(8,128)(2,1)} %get-tuple-element.92.refs_4_), calls=%async_computation | async-start | bytes 786432 | tf_op jit(solution)/shard_map/all_to_all | solution.py:810
  119.8 19.8 %copy-start.20 = (bf16[8,96,1792]{2,1,0:T(8,128)(2,1)S(1)}, bf16[8,96,1792]{2,1,0:T(8,128)(2,1)}, u32[]{:S(2)}) copy-start(bf16[8,96,1792]{2,1,0:T(8,128)(2,1)} %constant_dynamic-update-slice_fusion.1) | copy-start | bytes 8257540
  139.6 1.7 copy-start.17
  141.2 17.6 %copy-start.21 = (bf16[8,96,1792]{2,1,0:T(8,128)(2,1)}, bf16[8,96,1792]{2,1,0:T(8,128)(2,1)S(1)}, u32[]{:S(2)}) copy-start(bf16[8,96,1792]{2,1,0:T(8,128)(2,1)S(1)} %constant_dynamic-update-slice_fusion.refs_2_) | copy-start | bytes 8257540
  141.2 17.5 %collective-permute-start.7 = (bf16[8,96,1792]{2,1,0:T(8,128)(2,1)S(1)}, bf16[8,96,1792]{2,1,0:T(8,128)(2,1)}, u32[]{:S(2)}, u32[]{:S(2)}) collective-permute-start(bf16[8,96,1792]{2,1,0:T(8,128)(2,1)S(1)} %constant_dynamic-update-slice_fusion.refs_2_), channel_id=1, source_target_pairs={{0,4},{4,0},{8,12},{12,8},{16,20},{20,16},{24,28},{28,24},{1,5},{5... | collective-permute-start | bytes 8257544 | tf_op jit(solution)/shard_map/ppermute | solution.py:705
  141.3 17.5 %all-to-all-start.1 = ((bf16[4,384,128]{2,1,0:T(8,128)(2,1)}), bf16[4,384,128]{2,1,0:T(8,128)(2,1)S(1)}, u32[]{:S(2)}, u32[]{:S(2)}) async-start(bf16[4,384,128]{2,1,0:T(8,128)(2,1)} %get-tuple-element.78.refs_5_), calls=%async_computation.1 | async-start | bytes 786432 | tf_op jit(solution)/shard_map/all_to_all | solution.py:810
  146.4 169.7 %reduce-scatter.4.cloned.1.call-start = ((), (), s32[]{:S(2)}) async-start(), calls=%async_computation.6 | async-start | bytes 6635520 | tf_op jit(solution)/shard_map/reduce_scatter | solution.py:861
  193.4 23.4 %all-to-all-start.2 = ((bf16[4,2,384,128]{3,2,1,0:T(8,128)(2,1)}), bf16[4,2,384,128]{3,2,1,0:T(8,128)(2,1)S(1)}, u32[]{:S(2)}, u32[]{:S(2)}) async-start(bf16[4,2,384,128]{3,2,1,0:T(8,128)(2,1)} %get-tuple-element.91), calls=%async_computation.2 | async-start | bytes 1572864 | tf_op jit(solution)/shard_map/all_to_all | solution.py:810
  196.9 19.9 %copy-start.1 = (s32[2048,1]{1,0:T(8,128)S(1)}, s32[2048,1]{1,0:T(8,128)}, u32[]{:S(2)}) copy-start(s32[2048,1]{1,0:T(8,128)} %copy-done) | copy-start | bytes 24580
  196.9 19.9 %copy-start.3 = (s32[1,2048]{1,0:T(1,128)S(1)}, s32[1,2048]{1,0:T(1,128)}, u32[]{:S(2)}) copy-start(s32[1,2048]{1,0:T(1,128)} %refs_2_.5) | copy-start | bytes 24580
  197.0 19.9 %copy-start.5 = (s32[8]{0:T(128)S(1)}, s32[8]{0:T(128)}, u32[]{:S(2)}) copy-start(s32[8]{0:T(128)} %copy-done.4) | copy-start | bytes 100
  197.0 19.9 %copy-start.7 = (s32[8]{0:T(128)S(1)}, s32[8]{0:T(128)}, u32[]{:S(2)}) copy-start(s32[8]{0:T(128)} %copy-done.6) | copy-start | bytes 100
  197.0 19.9 %copy-start.12 = (f32[3,1,1024]{2,1,0:T(1,128)S(1)}, f32[3,1,1024]{2,1,0:T(1,128)}, u32[]{:S(2)}) copy-start(f32[3,1,1024]{2,1,0:T(1,128)} %get-tuple-element.94.refs_7_) | copy-start | bytes 36868
  197.0 145.5 %reduce-scatter.8.cloned.1.call-start = ((), (), s32[]{:S(2)}) async-start(), calls=%async_computation.8 | async-start | bytes 3932160 | tf_op jit(solution)/shard_map/reduce_scatter | solution.py:873
  206.1 53.6 %collective-permute-start.8 = (bf16[4,2,96,1856]{3,2,1,0:T(8,128)(2,1)}, bf16[4,2,96,1856]{3,2,1,0:T(8,128)(2,1)}, u32[]{:S(2)}, u32[]{:S(2)}) collective-permute-start(bf16[4,2,96,1856]{3,2,1,0:T(8,128)(2,1)} %bitcast.110), channel_id=1, source_target_pairs={{0,4},{4,0},{8,12},{12,8},{16,20},{20,16},{24,28},{28,24},{1,5},{5... | collective-permute-start | bytes 8552456 | tf_op jit(solution)/shard_map/ppermute | solution.py:705
  216.9 1.9 copy-start.11
  218.8 34.9 %copy-start.19 = (bf16[768,768]{0,1:T(8,128)(2,1)S(1)}, bf16[768,768]{0,1:T(8,128)(2,1)}, u32[]{:S(2)}) copy-start(bf16[768,768]{0,1:T(8,128)(2,1)} %maximum_select_fusion) | copy-start | bytes 3538948
  257.6 1.8 copy-start.14
  257.6 94.2 %reduce-scatter.6.cloned.1.call-start = ((), (), s32[]{:S(2)}) async-start(), calls=%async_computation.7 | async-start | bytes 1843200 | tf_op jit(solution)/shard_map/reduce_scatter | solution.py:894
  259.7 4.7 %copy-start.9 = (bf16[1,2048,768]{2,1,0:T(8,128)(2,1)S(1)}, bf16[1,2048,768]{2,1,0:T(8,128)(2,1)}, u32[]{:S(2)}) copy-start(bf16[1,2048,768]{2,1,0:T(8,128)(2,1)} %copy-done.8) | copy-start | bytes 9437188
  264.3 32.3 %collective-permute-start.9 = (bf16[2,2,96,1856]{3,2,1,0:T(8,128)(2,1)}, bf16[2,2,96,1856]{3,2,1,0:T(8,128)(2,1)}, u32[]{:S(2)}, u32[]{:S(2)}) collective-permute-start(bf16[2,2,96,1856]{3,2,1,0:T(8,128)(2,1)} %get-tuple-element.100), channel_id=1, source_target_pairs={{0,8},{4,12},{8,0},{12,4},{16,24},{20,28},{24,16},{28,20},{1,9},{5... | collective-permute-start | bytes 4276232 | tf_op jit(solution)/shard_map/ppermute | solution.py:705
  264.4 32.2 %copy-start.13 = (bf16[2,2,96,1856]{3,2,1,0:T(8,128)(2,1)S(1)}, bf16[2,2,96,1856]{3,2,1,0:T(8,128)(2,1)}, u32[]{:S(2)}) copy-start(bf16[2,2,96,1856]{3,2,1,0:T(8,128)(2,1)} %get-tuple-element.99) | copy-start | bytes 4276228
  298.3 17.6 %collective-permute-start.10 = (bf16[1,2,96,1856]{3,2,1,0:T(8,128)(2,1)S(1)}, bf16[1,2,96,1856]{3,2,1,0:T(8,128)(2,1)S(1)}, u32[]{:S(2)}, u32[]{:S(2)}) collective-permute-start(bf16[1,2,96,1856]{3,2,1,0:T(8,128)(2,1)S(1)} %get-tuple-element.105), channel_id=1, source_target_pairs={{0,16},{4,20},{8,24},{12,28},{16,0},{20,4},{24,8},{28,12},{1,17},{... | collective-permute-start | bytes 2138120 | tf_op jit(solution)/shard_map/ppermute | solution.py:705
  300.7 5.4 %collective-permute-start.11 = (f32[1,384]{1,0:T(1,128)S(1)}, f32[1,384]{1,0:T(1,128)S(1)}, u32[]{:S(2)}, u32[]{:S(2)}) collective-permute-start(f32[1,384]{1,0:T(1,128)S(1)} %pad_maximum_fusion.6), channel_id=1, source_target_pairs={{0,1},{1,0},{2,3},{3,2},{4,5},{5,4},{6,7},{7,6},{8,9},{9,8},{10,11... | collective-permute-start | bytes 4616 | tf_op jit(solution)/shard_map/ppermute | solution.py:705
  306.2 4.7 %collective-permute-start.12 = (f32[2,384]{1,0:T(2,128)S(1)}, f32[2,384]{1,0:T(2,128)S(1)}, u32[]{:S(2)}, u32[]{:S(2)}) collective-permute-start(f32[2,384]{1,0:T(2,128)S(1)} %maximum_select_fusion.4), channel_id=1, source_target_pairs={{0,2},{1,3},{2,0},{3,1},{4,6},{5,7},{6,4},{7,5},{8,10},{9,11},{10,... | collective-permute-start | bytes 9224 | tf_op jit(solution)/shard_map/ppermute | solution.py:705
  317.9 2.2 copy-start.15
  321.3 2.1 collective-permute-start.13
  323.5 19.0 %copy-start.16 = (f32[512,768]{1,0:T(8,128)S(1)}, f32[512,768]{1,0:T(8,128)}, u32[]{:S(2)}) copy-start(f32[512,768]{1,0:T(8,128)} %get-tuple-element.109) | copy-start | bytes 4718596
  323.5 9.1 %collective-permute-start.14 = (bf16[2,96,768]{2,1,0:T(8,128)(2,1)S(1)}, bf16[2,96,768]{2,1,0:T(8,128)(2,1)S(1)}, u32[]{:S(2)}, u32[]{:S(2)}) collective-permute-start(bf16[2,96,768]{2,1,0:T(8,128)(2,1)S(1)} %dynamic-slice_bitcast_fusion.1), channel_id=1, source_target_pairs={{0,8},{4,12},{8,0},{12,4},{16,24},{20,28},{24,16},{28,20},{1,9},{5... | collective-permute-start | bytes 884744 | tf_op jit(solution)/shard_map/ppermute | solution.py:705
  332.8 5.2 %collective-permute-start.15 = (bf16[1,96,768]{2,1,0:T(8,128)(2,1)S(1)}, bf16[1,96,768]{2,1,0:T(8,128)(2,1)S(1)}, u32[]{:S(2)}, u32[]{:S(2)}) collective-permute-start(bf16[1,96,768]{2,1,0:T(8,128)(2,1)S(1)} %constant_dynamic-slice_fusion), channel_id=1, source_target_pairs={{0,16},{4,20},{8,24},{12,28},{16,0},{20,4},{24,8},{28,12},{1,17},{... | collective-permute-start | bytes 442376 | tf_op jit(solution)/shard_map/ppermute | solution.py:705
  (2 other events, 2.4 us)
Sparse Core Ops, SparseCore 0:
  9.6 68.1 all-gather.4
  113.9 42.7 all-gather.6
  193.5 58.6 reduce-scatter.3
  257.8 58.0 reduce-scatter.7
  319.4 32.3 reduce-scatter.5
